TPU v7x, 256 devices: a whole 4x4x8 slice. The times are simulated.
256 devices in a mesh: row: 16 (over x, z_lo, core), col: 16 (over z_hi, y).
Axes of the slice: x: 4, y: 4, z: 8 (z_hi: 4, z_lo: 2; z = z_hi * 2 + z_lo), core: 2. Of those that a mesh axis runs over, the one named last changes fastest.
Arguments:
- iterate: bfloat16 [4096, 8192], P('row', 'col'), may hold values from -0.5 to 0.5, as said below
Outputs:
- update: float32 [4096, 8192], P('row', 'col')
Inputs may be any that keep to these rules, and one draw needn't show every extreme that they name: One iterate of the orthogonalization.
All inputs are finite; a program needn't handle non-finite values.
Results may differ from a plain program's by a relative error of at most 0.0041.
Values may be sent and summed in bfloat16 or wider, within the bound.
No kernel may reach another device: no remote copies, remote signals or barrier semaphores. Data moves between devices by JAX's collectives and lax.ppermute only.
A program may use at most 64 MiB of HBM per device.

v0:
```python
import math

import jax
import jax.numpy as jnp
from jax import lax
from jax.sharding import PartitionSpec as P

COLS = 8192


coef_a = 3.4445
coef_b = -4.775
coef_c = 2.0315


def per_device(iterate):
    cols_x = lax.all_gather(iterate, "row", axis=0, tiled=True)
    mirrored = lax.psum_scatter(
        lax.dot_general(
            cols_x, iterate, (((1,), (1,)), ((), ())), preferred_element_type=jnp.float32
        ),
        "col",
        scatter_dimension=0,
        tiled=True,
    )
    gram_block = mirrored.T.astype(jnp.bfloat16)
    gram_cols = lax.all_gather(gram_block, "row", axis=0, tiled=True)
    lower = gram_cols
    square = jnp.dot(
        lax.all_gather(gram_block, "col", axis=1, tiled=True),
        lower,
        preferred_element_type=jnp.float32,
    )
    poly = (coef_b * gram_block.astype(jnp.float32) + coef_c * square).astype(jnp.bfloat16)
    lower = cols_x
    mixed = jnp.dot(
        lax.all_gather(poly, "col", axis=1, tiled=True), lower, preferred_element_type=jnp.float32
    )
    return math.sqrt(COLS) * (coef_a * iterate.astype(jnp.float32) + mixed)


def solution(mesh):
    placed = (P("row", "col"),)
    return jax.shard_map(
        per_device, mesh=mesh, in_specs=placed, out_specs=P("row", "col"), check_vma=False
    )
```

profile of v0, /device:TPU:1, one launch (start us, length us, event | category | flops | bytes accessed | tf_op | source)
XLA Modules:
  0.0 328.1 jit_solution(15729585336127097783)
XLA Ops:
  6.5 0.0 all-gather.5.cloned.1.call-start
  6.5 0.7 all-gather.5.cloned.1.call-update
  7.3 0.0 reduce-scatter.2.cloned.1.call-start
  7.3 46.2 %all-gather.5.cloned.1.call-done = bf16[4096,512]{1,0:T(8,128)(2,1)} async-done(((bf16[256,512]{1,0:T(8,128)(2,1)}), bf16[4096,512]{1,0:T(8,128)(2,1)}) %all-gather.5.cloned.1.call-update) | async-done | bytes 4194320 | tf_op jit(solution)/shard_map/all_gather | solution.py:17
  53.5 5.5 %fusion.3 = f32[4096,256]{1,0:T(8,128)} fusion(bf16[4096,512]{1,0:T(8,128)(2,1)} %all-gather.5.cloned.1.call-done, bf16[256,512]{1,0:T(8,128)(2,1)} %param.1), kind=kOutput, calls=%fused_computation.6 | convolution fusion | flops 1073741824 | bytes 8650752 | tf_op jit(solution)/shard_map/dot_general | solution.py:19
  59.0 0.0 reduce-scatter.2.cloned.1.call-update
  59.0 0.0 all-gather.7.cloned.1.call-start
  59.0 94.7 %reduce-scatter.2.cloned.1.call-done = f32[256,256]{1,0:T(8,128)} async-done(((f32[4096,256]{1,0:T(8,128)}), f32[256,256]{1,0:T(8,128)}) %reduce-scatter.2.cloned.1.call-update) | async-done | bytes 262160 | tf_op jit(solution)/shard_map/reduce_scatter | solution.py:18
  153.7 1.6 convert_bitcast_fusion
  155.4 0.0 all-gather.7.cloned.1.call-update
  155.4 0.0 all-gather.9.cloned.1.call-start
  155.4 0.5 all-gather.9.cloned.1.call-update
  156.0 0.0 copy-start
  156.0 0.0 all-gather.11.cloned.1.call-start
  156.0 57.9 %all-gather.7.cloned.1.call-done = bf16[256,4096]{0,1:T(8,128)(2,1)} async-done(((bf16[256,256]{0,1:T(8,128)(2,1)}), bf16[256,4096]{0,1:T(8,128)(2,1)}) %all-gather.7.cloned.1.call-update) | async-done | bytes 2097168 | tf_op jit(solution)/shard_map/all_gather | solution.py:30
  214.0 40.3 %all-gather.9.cloned.1.call-done = bf16[4096,256]{0,1:T(8,128)(2,1)} async-done(((bf16[256,256]{0,1:T(8,128)(2,1)}), bf16[4096,256]{0,1:T(8,128)(2,1)}) %all-gather.9.cloned.1.call-update) | async-done | bytes 2097168 | tf_op jit(solution)/shard_map/all_gather | solution.py:27
  254.3 3.6 %fusion.2 = bf16[256,256]{0,1:T(8,128)(2,1)} fusion(bf16[4096,256]{0,1:T(8,128)(2,1)} %all-gather.9.cloned.1.call-done, bf16[256,4096]{0,1:T(8,128)(2,1)} %all-gather.7.cloned.1.call-done, bf16[256,256]{0,1:T(8,128)(2,1)} %convert_bitcast_fusion), kind=kOutput, calls=%fused_computation.4 | convolution fusion | flops 537198592 | bytes 4456448 | tf_op jit(solution)/shard_map/dot_general | solution.py:29
  257.9 0.0 all-gather.11.cloned.1.call-update
  257.9 58.8 %all-gather.11.cloned.1.call-done = bf16[256,4096]{0,1:T(8,128)(2,1)} async-done(((bf16[256,256]{0,1:T(8,128)(2,1)}), bf16[256,4096]{0,1:T(8,128)(2,1)}) %all-gather.11.cloned.1.call-update) | async-done | bytes 2097168 | tf_op jit(solution)/shard_map/all_gather | solution.py:37
  316.7 0.0 copy-done
  316.7 4.9 %fusion = f32[256,512]{1,0:T(8,128)} fusion(bf16[256,4096]{0,1:T(8,128)(2,1)} %all-gather.11.cloned.1.call-done, bf16[4096,512]{1,0:T(8,128)(2,1)} %all-gather.5.cloned.1.call-done, bf16[256,512]{1,0:T(8,128)(2,1)S(1)} %copy-done), kind=kOutput, calls=%fused_computation.1 | convolution fusion | flops 1074266112 | bytes 7077888 | tf_op jit(solution)/shard_map/dot_general | solution.py:36
Async XLA Ops:
  6.5 47.0 %all-gather.5.cloned.1.call-start = ((), (), s32[]{:S(2)}) async-start(), calls=%async_computation.1 | async-start | bytes 4456448 | tf_op jit(solution)/shard_map/all_gather | solution.py:17
  7.3 146.5 %reduce-scatter.2.cloned.1.call-start = ((), (), s32[]{:S(2)}) async-start(), calls=%async_computation.2 | async-start | bytes 4456448 | tf_op jit(solution)/shard_map/reduce_scatter | solution.py:18
  59.0 155.0 %all-gather.7.cloned.1.call-start = ((), (), s32[]{:S(2)}) async-start(), calls=%async_computation.3 | async-start | bytes 2228224 | tf_op jit(solution)/shard_map/all_gather | solution.py:30
  155.4 98.9 %all-gather.9.cloned.1.call-start = ((), (), s32[]{:S(2)}) async-start(), calls=%async_computation.4 | async-start | bytes 2228224 | tf_op jit(solution)/shard_map/all_gather | solution.py:27
  156.0 160.7 %copy-start = (bf16[256,512]{1,0:T(8,128)(2,1)S(1)}, bf16[256,512]{1,0:T(8,128)(2,1)}, u32[]{:S(2)}) copy-start(bf16[256,512]{1,0:T(8,128)(2,1)} %param.1) | copy-start | bytes 786436
  156.0 160.7 %all-gather.11.cloned.1.call-start = ((), (), s32[]{:S(2)}) async-start(), calls=%async_computation.5 | async-start | bytes 2228224 | tf_op jit(solution)/shard_map/all_gather | solution.py:37
Sparse Core Ops, SparseCore 0:
  9.2 44.2 all-gather.4
  59.1 94.5 reduce-scatter.1
  156.5 57.4 all-gather.6
  215.7 38.5 all-gather.8
  258.0 58.6 all-gather.10
where the time goes:
time: 328 us
  waiting for transfers between devices  299 us (91%)
  matrix products  13.9 us (4%)
  between operations  13.1 us (4%)
    reduce_scatter x1, waiting for transfers between devices, per_device(): lax.psum_scatter(lax.dot_general(cols_x, iterate, (((1,), (1,)), ((), ())...  94.7 us
    all_gather x1, waiting for transfers between devices, per_device(): lax.all_gather(poly, 'col', axis=1, tiled=True)  58.8 us
    all_gather x1, waiting for transfers between devices, per_device(): lax.all_gather(gram_block, 'col', axis=1, tiled=True)  57.9 us
    all_gather x1, waiting for transfers between devices, per_device(): cols_x = lax.all_gather(iterate, 'row', axis=0, tiled=True)  46.2 us
    all_gather x1, waiting for transfers between devices, per_device(): gram_cols = lax.all_gather(gram_block, 'row', axis=0, tiled=True)  40.3 us
  transfers between devices with their start and end apart: 5, of which 5 were waited for; matrix products, arithmetic and copies ran while one was open for 0% of the time, Pallas kernels for 0%

commit v1 on v0

v1 whole, which is shorter than its diff:
```python
import math

import jax
import jax.numpy as jnp
from jax import lax
from jax.sharding import Mesh
from jax.sharding import PartitionSpec as P

COLS = 8192

coef_a = 3.4445
coef_b = -4.775
coef_c = 2.0315

CHIPS = ("x", "zl")
ROW = ("x", "zl", "core")
COL = ("zh", "y")


def gather(block, axes, n):
    copies = jnp.broadcast_to(block[None], (n, *block.shape))
    got = lax.all_to_all(copies, axes, 0, 0)
    return got.reshape(n * block.shape[0], *block.shape[1:])


def scatter_sum(part, axes, n):
    pieces = part.reshape(n, part.shape[0] // n, *part.shape[1:])
    got = lax.all_to_all(pieces, axes, 0, 0)
    return jnp.sum(got.astype(jnp.float32), axis=0).astype(jnp.bfloat16)


def matmul(a, b, dims):
    return lax.dot_general(a, b, (dims, ((), ())), preferred_element_type=jnp.float32)


def core_sum(part, core):
    half = part.shape[0] // 2
    mine = lax.dynamic_slice_in_dim(part, core * half, half, 0)
    other = lax.dynamic_slice_in_dim(part, (1 - core) * half, half, 0)
    return mine + lax.ppermute(other, "core", [(0, 1), (1, 0)])


def per_device(iterate):
    core = lax.axis_index("core")
    own = lax.all_gather(iterate, "core", axis=0, tiled=True)
    panel = gather(iterate, CHIPS, 8)
    gram = matmul(panel, own, ((1,), (1,))).astype(jnp.bfloat16)
    gram = scatter_sum(gram, "y", 4)
    gram = scatter_sum(gram, "zh", 4)
    gram = gather(gram, "zh", 4)
    gram = gather(gram, "y", 4)
    inner = core_sum(matmul(gram, panel, ((0,), (0,))), core)
    mine = iterate.astype(jnp.float32)
    inner = (coef_b * mine + coef_c * inner).astype(jnp.bfloat16)
    panel = gather(inner, CHIPS, 8)
    mixed = core_sum(matmul(gram, panel, ((0,), (0,))), core)
    return math.sqrt(COLS) * (coef_a * mine + mixed)


def solution(mesh):
    fine = Mesh(mesh.devices.reshape(4, 2, 2, 4, 4), (*ROW, *COL))
    placed = P(ROW, COL)
    return jax.shard_map(
        per_device, mesh=fine, in_specs=(placed,), out_specs=placed, check_vma=False
    )
```

time: 328 us -> 176 us (0.54)
  waiting for transfers between devices: 299 us -> 48.6 us
  blocking collectives: 0 us -> 97.3 us
  starting transfers between devices: 0.16 us -> 16.6 us
  between operations: 13.1 us -> 0.07 us
  matrix products: 13.9 us -> 5.41 us
  local copies, waits for them, and re-layouts: 0.01 us -> 5.08 us
    all_gather x4 -> x0, waiting for transfers between devices: 203 us -> none  [the longest x1 58.8 us: per_device(): lax.all_gather(poly, 'col', axis=1, tiled=True)]
    reduce_scatter x1 -> x0, waiting for transfers between devices: 94.7 us -> none  [per_device(): lax.psum_scatter(lax.dot_general(cols_x, iterate, (((1,), (1,)), ((), ())...]
    all_to_all x0 -> x4, blocking collectives: none -> 94.5 us  [the longest x2 47.4 us: gather(): got = lax.all_to_all(copies, axes, 0, 0)]
    all_to_all x0 -> x2, waiting for transfers between devices: none -> 45.2 us  [gather(): got = lax.all_to_all(copies, axes, 0, 0)]
    all_to_all x0 -> x2, starting transfers between devices: none -> 9.94 us  [gather(): got = lax.all_to_all(copies, axes, 0, 0)]
    dot_general x3, matrix products: 13.9 us -> 5.41 us  [matmul(): lax.dot_general(a, b, (dims, ((), ())), preferred_element_type=jnp.float32)]
    ppermute x0 -> x2, starting transfers between devices: none -> 6.62 us  [core_sum(): return mine + lax.ppermute(other, 'core', [(0, 1), (1, 0)])]
    broadcast_in_dim x0 -> x4, local copies, waits for them, and re-layouts: none -> 4.15 us  [gather(): copies = jnp.broadcast_to(block[None], (n, *block.shape))]
  transfers between devices with their start and end apart: 5 -> 4, of which waited for: 5 -> 4; matrix products, arithmetic and copies ran while one was open for 0% -> 0% of each run, Pallas kernels for 0% -> 0%
where the time goes in v1:
time: 176 us
  blocking collectives  97.3 us (55%)
  waiting for transfers between devices  48.6 us (28%)
  starting transfers between devices  16.6 us (9%)
  matrix products  5.41 us (3%)
  local copies, waits for them, and re-layouts  5.08 us (3%)
  other arithmetic  2.82 us (2%)
    all_to_all x2, blocking collectives, gather(): got = lax.all_to_all(copies, axes, 0, 0)  47.4 us
    all_to_all x2, blocking collectives, scatter_sum(): got = lax.all_to_all(pieces, axes, 0, 0)  47.1 us
    all_to_all x2, waiting for transfers between devices, gather(): got = lax.all_to_all(copies, axes, 0, 0)  45.2 us
    all_to_all x2, starting transfers between devices, gather(): got = lax.all_to_all(copies, axes, 0, 0)  9.94 us
    ppermute x2, starting transfers between devices, core_sum(): return mine + lax.ppermute(other, 'core', [(0, 1), (1, 0)])  6.62 us
    dot_general x3, matrix products, matmul(): lax.dot_general(a, b, (dims, ((), ())), preferred_element_type=jnp.float32)  5.41 us
    broadcast_in_dim x4, local copies, waits for them, and re-layouts, gather(): copies = jnp.broadcast_to(block[None], (n, *block.shape))  4.15 us
  transfers between devices with their start and end apart: 4, of which 4 were waited for; matrix products, arithmetic and copies ran while one was open for 0% of the time, Pallas kernels for 0%

profile of v1, /device:TPU:1, one launch (start us, length us, event | category | flops | bytes accessed | tf_op | source)
XLA Modules:
  0.0 175.9 jit_solution(12735367094263790227)
XLA Ops:
  0.0 2.5 %broadcast_in_dim.10 = bf16[8,256,512]{2,1,0:T(8,128)(2,1)} broadcast(bf16[256,512]{1,0:T(8,128)(2,1)} %param.1), dimensions={1,2} | broadcast | bytes 2359296 | tf_op jit(solution)/shard_map/broadcast_in_dim | solution.py:21
  2.5 0.0 copy-start
  2.5 6.3 %all-to-all-start = ((bf16[8,256,512]{2,1,0:T(8,128)(2,1)}), bf16[8,256,512]{2,1,0:T(8,128)(2,1)S(1)}, u32[]{:S(2)}, u32[]{:S(2)}) async-start(bf16[8,256,512]{2,1,0:T(8,128)(2,1)} %broadcast_in_dim.10), calls=%async_computation | async-start | bytes 4194304 | tf_op jit(solution)/shard_map/all_to_all | solution.py:22
  8.8 0.0 copy-done
  8.8 2.8 %all_gather.3 = bf16[512,512]{1,0:T(8,128)(2,1)S(1)} all-gather(bf16[256,512]{1,0:T(8,128)(2,1)S(1)} %copy-done), channel_id=1, replica_groups=mesh['x'=4,'zl'=2,'core'=2,'zh'=4,'y'=4] {'core'}, dimensions={0}, use_global_device_ids=true | all-gather | bytes 786432 | tf_op jit(solution)/shard_map/all_gather | solution.py:45
  11.6 23.3 %all-to-all-done = bf16[8,256,512]{2,1,0:T(8,128)(2,1)S(1)} async-done(((bf16[8,256,512]{2,1,0:T(8,128)(2,1)}), bf16[8,256,512]{2,1,0:T(8,128)(2,1)S(1)}, u32[]{:S(2)}, u32[]{:S(2)}) %all-to-all-start) | async-done | bytes 2097184 | tf_op jit(solution)/shard_map/all_to_all | solution.py:22
  34.9 0.0 copy-start.1
  34.9 1.3 convolution_convert_fusion
  36.2 0.0 copy-done.1
  36.2 27.9 %all_to_all.30 = bf16[4,512,512]{2,1,0:T(8,128)(2,1)S(1)} all-to-all(bf16[4,512,512]{2,1,0:T(8,128)(2,1)S(1)} %bitcast.18), channel_id=1, replica_groups=mesh['x'=4,'zl'=2,'core'=2,'zh'=4,'y'=4] {'y'}, dimensions={0} | all-to-all | bytes 4194304 | tf_op jit(solution)/shard_map/all_to_all | solution.py:28
  64.1 0.6 reduce_sum.24
  64.8 19.2 %all_to_all.31 = bf16[4,128,512]{2,1,0:T(8,128)(2,1)S(1)} all-to-all(bf16[4,128,512]{2,1,0:T(8,128)(2,1)S(1)} %bitcast.19), channel_id=1, replica_groups=mesh['x'=4,'zl'=2,'core'=2,'zh'=4,'y'=4] {'zh'}, dimensions={0} | all-to-all | bytes 1048576 | tf_op jit(solution)/shard_map/all_to_all | solution.py:28
  84.0 0.1 reduce_sum.25
  84.1 18.3 %all_to_all.32 = bf16[4,128,512]{2,1,0:T(8,128)(2,1)S(1)} all-to-all(bf16[4,128,512]{2,1,0:T(8,128)(2,1)S(1)} %broadcast_in_dim.11), channel_id=1, replica_groups=mesh['x'=4,'zl'=2,'core'=2,'zh'=4,'y'=4] {'zh'}, dimensions={0} | all-to-all | bytes 1048576 | tf_op jit(solution)/shard_map/all_to_all | solution.py:22
  102.4 1.5 broadcast_in_dim.13
  103.9 3.6 %all-to-all-start.4 = ((bf16[4,512,512]{2,1,0:T(8,128)(2,1)}), bf16[4,512,512]{2,1,0:T(8,128)(2,1)S(1)}, u32[]{:S(2)}, u32[]{:S(2)}) async-start(bf16[4,512,512]{2,1,0:T(8,128)(2,1)} %broadcast_in_dim.13), calls=%async_computation.4 | async-start | bytes 4194304 | tf_op jit(solution)/shard_map/all_to_all | solution.py:22
  107.5 21.9 %all-to-all-done.4 = bf16[4,512,512]{2,1,0:T(8,128)(2,1)S(1)} async-done(((bf16[4,512,512]{2,1,0:T(8,128)(2,1)}), bf16[4,512,512]{2,1,0:T(8,128)(2,1)S(1)}, u32[]{:S(2)}, u32[]{:S(2)}) %all-to-all-start.4) | async-done | bytes 2097184 | tf_op jit(solution)/shard_map/all_to_all | solution.py:22
  129.4 2.9 %fusion.4 = f32[512,512]{1,0:T(8,128)S(1)} fusion(bf16[2048,512]{1,0:T(8,128)(2,1)S(1)} %bitcast.13, bf16[2048,512]{1,0:T(8,128)(2,1)} %bitcast.16), kind=kOutput, calls=%fused_computation.9 | convolution fusion | flops 1073741824 | bytes 5242880 | tf_op jit(solution)/shard_map/dot_general | solution.py:33
  132.2 0.8 constant_dynamic-slice_fusion.1
  133.1 5.3 %collective-permute-start = (f32[256,512]{1,0:T(8,128)}, f32[256,512]{1,0:T(8,128)}, u32[]{:S(2)}, u32[]{:S(2)}) collective-permute-start(f32[256,512]{1,0:T(8,128)} %constant_dynamic-slice_fusion.1), channel_id=1, source_target_pairs={{0,16},{16,0},{1,17},{17,1},{2,18},{18,2},{3,19},{19,3},{4,20},{20... | collective-permute-start | bytes 1572872 | tf_op jit(solution)/shard_map/ppermute | solution.py:40
  138.4 1.9 %collective-permute-done = f32[256,512]{1,0:T(8,128)} collective-permute-done((f32[256,512]{1,0:T(8,128)}, f32[256,512]{1,0:T(8,128)}, u32[]{:S(2)}, u32[]{:S(2)}) %collective-permute-start) | collective-permute-done | bytes 524320 | tf_op jit(solution)/shard_map/ppermute | solution.py:40
  140.3 1.2 fusion.3
  141.5 0.2 broadcast_in_dim.14
  141.7 29.1 %all_to_all.33 = bf16[8,256,512]{2,1,0:T(8,128)(2,1)S(1)} all-to-all(bf16[8,256,512]{2,1,0:T(8,128)(2,1)S(1)} %broadcast_in_dim.14), channel_id=1, replica_groups=mesh['x'=4,'zl'=2,'core'=2,'zh'=4,'y'=4] {'x','zl'}, dimensions={0} | all-to-all | bytes 4194304 | tf_op jit(solution)/shard_map/all_to_all | solution.py:22
  170.8 1.3 fusion.5
  172.1 1.3 collective-permute-start.1
  173.4 1.5 collective-permute-done.1
  174.9 0.9 fusion.1
  (2 shorter events, 0.1 us)
Async XLA Ops:
  2.5 6.3 %copy-start = (bf16[256,512]{1,0:T(8,128)(2,1)S(1)}, bf16[256,512]{1,0:T(8,128)(2,1)}, u32[]{:S(2)}) copy-start(bf16[256,512]{1,0:T(8,128)(2,1)} %param.1) | copy-start | bytes 786436
  2.5 32.4 %all-to-all-start = ((bf16[8,256,512]{2,1,0:T(8,128)(2,1)}), bf16[8,256,512]{2,1,0:T(8,128)(2,1)S(1)}, u32[]{:S(2)}, u32[]{:S(2)}) async-start(bf16[8,256,512]{2,1,0:T(8,128)(2,1)} %broadcast_in_dim.10), calls=%async_computation | async-start | bytes 4194304 | tf_op jit(solution)/shard_map/all_to_all | solution.py:22
  34.9 1.3 copy-start.1
  103.9 25.5 %all-to-all-start.4 = ((bf16[4,512,512]{2,1,0:T(8,128)(2,1)}), bf16[4,512,512]{2,1,0:T(8,128)(2,1)S(1)}, u32[]{:S(2)}, u32[]{:S(2)}) async-start(bf16[4,512,512]{2,1,0:T(8,128)(2,1)} %broadcast_in_dim.13), calls=%async_computation.4 | async-start | bytes 4194304 | tf_op jit(solution)/shard_map/all_to_all | solution.py:22
  133.1 7.2 %collective-permute-start = (f32[256,512]{1,0:T(8,128)}, f32[256,512]{1,0:T(8,128)}, u32[]{:S(2)}, u32[]{:S(2)}) collective-permute-start(f32[256,512]{1,0:T(8,128)} %constant_dynamic-slice_fusion.1), channel_id=1, source_target_pairs={{0,16},{16,0},{1,17},{17,1},{2,18},{18,2},{3,19},{19,3},{4,20},{20... | collective-permute-start | bytes 1572872 | tf_op jit(solution)/shard_map/ppermute | solution.py:40
  172.1 2.8 %collective-permute-start.1 = (f32[256,512]{1,0:T(8,128)S(1)}, f32[256,512]{1,0:T(8,128)S(1)}, u32[]{:S(2)}, u32[]{:S(2)}) collective-permute-start(f32[256,512]{1,0:T(8,128)S(1)} %constant_dynamic-slice_fusion), channel_id=1, source_target_pairs={{0,16},{16,0},{1,17},{17,1},{2,18},{18,2},{3,19},{19,3},{4,20},{20... | collective-permute-start | bytes 1572872 | tf_op jit(solution)/shard_map/ppermute | solution.py:40

commit v2 on v1

v2 whole, which is shorter than its diff:
```python
import functools
import math

import jax
import jax.numpy as jnp
from jax import lax
from jax.experimental import pallas as pl
from jax.experimental.pallas import tpu as pltpu
from jax.sharding import Mesh
from jax.sharding import PartitionSpec as P

COLS = 8192

coef_a = 3.4445
coef_b = -4.775
coef_c = 2.0315

ROW = ("x", "zl", "core")
COL = ("zh", "y")
BF, F32 = jnp.bfloat16, jnp.float32
ANY = pl.BlockSpec(memory_space=pl.ANY)
VMEM = pl.BlockSpec(memory_space=pltpu.VMEM)


def fetch(axis, k):
    return [((i + k) % 4, i) for i in range(4)]


def swap(array, axis):
    return lax.ppermute(array, axis, [(0, 1), (1, 0)])


def around(array, axis):
    return [array] + [lax.ppermute(array, axis, fetch(axis, k)) for k in (1, 3, 2)]


def panel_copies(blocks, panel, sems):
    y = lax.axis_index("y")
    copies = []
    for n, j in enumerate((0, 1, 3, 2)):
        slot = lax.rem(j - y + 4, 4)
        copies.append(pltpu.make_async_copy(blocks[n], panel.at[slot], sems.at[n]))
    return copies


def gram_kernel(mine, other, b0, b1, b3, b2, o0, o1, o2, o3, own, panel, sems):
    core, zh = lax.axis_index("core"), lax.axis_index("zh")
    copies = panel_copies((b0, b1, b3, b2), panel, sems)
    for n, (ref, half) in enumerate(((mine, core), (other, 1 - core))):
        for i in range(2):
            place = lax.rem(half * 2 + i - zh + 4, 4)
            rows = pl.ds(pl.multiple_of(place * 128, 128), 128)
            copies.append(
                pltpu.make_async_copy(ref.at[pl.ds(i * 128, 128)], own.at[rows], sems.at[4 + 2 * n + i])
            )
    for copy in copies:
        copy.start()
    for copy in copies:
        copy.wait()
    for p, out in enumerate((o0, o1, o2, o3)):
        out[...] = lax.dot_general(
            own[...], panel[p], (((1,), (1,)), ((), ())), preferred_element_type=F32
        ).astype(BF)


def gram_pieces(mine, other, blocks):
    return pl.pallas_call(
        gram_kernel,
        out_shape=[jax.ShapeDtypeStruct((512, 256), BF)] * 4,
        in_specs=[ANY] * 6,
        out_specs=[VMEM] * 4,
        scratch_shapes=[
            pltpu.VMEM((512, 512), BF),
            pltpu.VMEM((4, 256, 512), BF),
            pltpu.SemaphoreType.DMA((8,)),
        ],
        cost_estimate=pl.CostEstimate(flops=2**29, bytes_accessed=5 * 2**19, transcendentals=0),
        name="gram",
    )(mine, other, *blocks)


def sum_kernel(a, b, c, d, o0, o1, o2, o3):
    for k, out in enumerate((o0, o1, o2, o3)):
        rows = pl.ds(k * 128, 128)
        total = (a[rows].astype(F32) + b[rows].astype(F32)) + (c[rows].astype(F32) + d[rows].astype(F32))
        out[...] = total.astype(BF)


def sum_pieces(pieces):
    return pl.pallas_call(
        sum_kernel,
        out_shape=[jax.ShapeDtypeStruct((128, 256), BF)] * 4,
        in_specs=[VMEM] * 4,
        out_specs=[VMEM] * 4,
        cost_estimate=pl.CostEstimate(flops=2**19, bytes_accessed=5 * 2**18, transcendentals=0),
        name="sum_y",
    )(*pieces)


def apply_kernel(*refs):
    gram, blocks = refs[:8], refs[8:16]
    mine, other, panel, total, sems = refs[16:]
    core, zh, y = lax.axis_index("core"), lax.axis_index("zh"), lax.axis_index("y")
    copies = panel_copies(blocks[:4], panel.at[0], sems.at[0])
    copies += panel_copies(blocks[4:], panel.at[1], sems.at[1])
    for copy in copies:
        copy.start()
    for copy in copies:
        copy.wait()
    for k in range(4):
        rows = pl.ds(k * 128, 128)
        acc = jnp.zeros((128, 512), F32)
        for s in range(2):
            for n, p in enumerate((0, 1, 3, 2)):
                acc += jnp.dot(gram[4 * s + n][rows], panel[s, p], preferred_element_type=F32)
        place = lax.rem(zh + k, 4)
        total[pl.ds(pl.multiple_of(place * 128, 128), 128)] = acc
    mine[...] = total[pl.ds(pl.multiple_of(core * 256, 256), 256)]
    other[...] = total[pl.ds(pl.multiple_of((1 - core) * 256, 256), 256)]


def apply(gram, blocks):
    mine, other = pl.pallas_call(
        apply_kernel,
        out_shape=[jax.ShapeDtypeStruct((256, 512), F32)] * 2,
        in_specs=[VMEM] * 8 + [ANY] * 8,
        out_specs=[VMEM] * 2,
        scratch_shapes=[
            pltpu.VMEM((2, 4, 256, 512), BF),
            pltpu.VMEM((512, 512), F32),
            pltpu.SemaphoreType.DMA((2, 4)),
        ],
        cost_estimate=pl.CostEstimate(flops=2**30, bytes_accessed=5 * 2**20, transcendentals=0),
        name="apply",
    )(*gram, *blocks)
    return mine + swap(other, "core")


def gather(block):
    partner = swap(block, "zl")
    return around(block, "x"), around(partner, "x")


def to_y(pieces):
    moved = [lax.ppermute(pieces[p], "y", [(i, (i + p) % 4) for i in range(4)]) for p in (1, 3, 2)]
    return [pieces[0], *moved]


def to_zh(pieces):
    moved = [lax.ppermute(pieces[p], "zh", [(i, (i + p) % 4) for i in range(4)]) for p in (1, 3, 2)]
    return sum(piece.astype(F32) for piece in [pieces[0], *moved]).astype(BF)


def from_zh(block):
    got = around(block, "zh")
    return jnp.concatenate([got[0], got[1], got[3], got[2]], axis=0)


def per_device(iterate):
    other = swap(iterate, "core")
    streams = gather(iterate)
    gram = []
    for blocks in streams:
        pieces = to_y(gram_pieces(iterate, other, blocks))
        block = from_zh(to_zh(sum_pieces(pieces)))
        gram += around(block, "y")
    inner = apply(gram, [*streams[0], *streams[1]])
    streams = gather(inner.astype(BF))
    mixed = apply(gram, [*streams[0], *streams[1]])
    mine = iterate.astype(F32)
    return math.sqrt(COLS) * (coef_a * mine + (coef_b * inner + coef_c * mixed))


def solution(mesh):
    fine = Mesh(mesh.devices.reshape(4, 2, 2, 4, 4), (*ROW, *COL))
    placed = P(ROW, COL)
    return jax.shard_map(
        per_device, mesh=fine, in_specs=(placed,), out_specs=placed, check_vma=False
    )
```

time: 176 us -> 157 us (0.89)
  blocking collectives: 97.3 us -> 0 us
  starting transfers between devices: 16.6 us -> 66.7 us
  Pallas kernels: 0 us -> 20.6 us
  waiting for transfers between devices: 48.6 us -> 58.8 us
  matrix products: 5.41 us -> 0 us
  local copies, waits for them, and re-layouts: 5.08 us -> 7.11 us
    all_to_all x4 -> x0, blocking collectives: 94.5 us -> none  [the longest x2 47.4 us: gather(): got = lax.all_to_all(copies, axes, 0, 0)]
    ppermute x2 -> x41, starting transfers between devices: 6.62 us -> 66.7 us  [the longest x24 33.1 us: around(): lax.ppermute(array, axis, fetch(axis, k))]
    ppermute x2 -> x41, waiting for transfers between devices: 3.42 us -> 58.8 us  [the longest x24 33.2 us: around(): lax.ppermute(array, axis, fetch(axis, k))]
    all_to_all x2 -> x0, waiting for transfers between devices: 45.2 us -> none  [gather(): got = lax.all_to_all(copies, axes, 0, 0)]
    pallas_call x0 -> x6, Pallas kernels: none -> 20.6 us  [the longest x2 10.8 us: apply(): pl.pallas_call(apply_kernel, out_shape=[jax.ShapeDtypeStruct((256, 512),...]
    all_to_all x2 -> x0, starting transfers between devices: 9.94 us -> none  [gather(): got = lax.all_to_all(copies, axes, 0, 0)]
    unnamed x4 -> x68, local copies, waits for them, and re-layouts: 0.05 us -> 7.11 us
    dot_general x3 -> x0, matrix products: 5.41 us -> none  [matmul(): lax.dot_general(a, b, (dims, ((), ())), preferred_element_type=jnp.float32)]
  transfers between devices with their start and end apart: 4 -> 41, of which waited for: 4 -> 18; matrix products, arithmetic and copies ran while one was open for 0% -> 0% of each run, Pallas kernels for 0% -> 6%
where the time goes in v2:
time: 157 us
  starting transfers between devices  66.7 us (42%)
  waiting for transfers between devices  58.8 us (37%)
  Pallas kernels  20.6 us (13%)
  local copies, waits for them, and re-layouts  7.11 us (5%)
  other arithmetic  3.32 us (2%)
    ppermute x24, waiting for transfers between devices, around(): lax.ppermute(array, axis, fetch(axis, k))  33.2 us
    ppermute x24, starting transfers between devices, around(): lax.ppermute(array, axis, fetch(axis, k))  33.1 us
    ppermute x6, starting transfers between devices, to_zh(): lax.ppermute(pieces[p], 'zh', [(i, (i + p) % 4) for i in range(4)])  15.3 us
    ppermute x6, waiting for transfers between devices, to_y(): lax.ppermute(pieces[p], 'y', [(i, (i + p) % 4) for i in range(4)])  12.6 us
    pallas_call x2, Pallas kernels, apply(): pl.pallas_call(apply_kernel, out_shape=[jax.ShapeDtypeStruct((256, 512),...  10.8 us
    ppermute x5, starting transfers between devices, swap(): return lax.ppermute(array, axis, [(0, 1), (1, 0)])  10.1 us
    ppermute x6, starting transfers between devices, to_y(): lax.ppermute(pieces[p], 'y', [(i, (i + p) % 4) for i in range(4)])  8.13 us
    ppermute x5, waiting for transfers between devices, swap(): return lax.ppermute(array, axis, [(0, 1), (1, 0)])  7.45 us
  transfers between devices with their start and end apart: 41, of which 18 were waited for; matrix products, arithmetic and copies ran while one was open for 0% of the time, Pallas kernels for 6%

profile of v2, /device:TPU:1, one launch (start us, length us, event | category | flops | bytes accessed | tf_op | source)
XLA Modules:
  0.0 156.9 jit_solution(763154711609601227)
XLA Ops:
  0.0 3.6 %collective-permute-start.3 = (bf16[256,512]{1,0:T(8,128)(2,1)}, bf16[256,512]{1,0:T(8,128)(2,1)S(1)}, u32[]{:S(2)}, u32[]{:S(2)}) collective-permute-start(bf16[256,512]{1,0:T(8,128)(2,1)} %refs_8_.1), channel_id=1, source_target_pairs={{128,0},{192,64},{0,128},{64,192},{129,1},{193,65},{1,129},{65,193... | collective-permute-start | bytes 786440 | tf_op jit(solution)/shard_map/ppermute | solution.py:34
  3.9 2.4 %collective-permute-start.1 = (bf16[256,512]{1,0:T(8,128)(2,1)}, bf16[256,512]{1,0:T(8,128)(2,1)S(1)}, u32[]{:S(2)}, u32[]{:S(2)}) collective-permute-start(bf16[256,512]{1,0:T(8,128)(2,1)} %refs_8_.1), channel_id=1, source_target_pairs={{64,0},{128,64},{192,128},{0,192},{65,1},{129,65},{193,129},{1,193... | collective-permute-start | bytes 786440 | tf_op jit(solution)/shard_map/ppermute | solution.py:34
  6.3 1.5 collective-permute-start
  7.8 1.6 %collective-permute-start.16 = (bf16[256,512]{1,0:T(8,128)(2,1)}, bf16[256,512]{1,0:T(8,128)(2,1)S(1)}, u32[]{:S(2)}, u32[]{:S(2)}) collective-permute-start(bf16[256,512]{1,0:T(8,128)(2,1)} %refs_8_.1), channel_id=1, source_target_pairs={{0,32},{32,0},{1,33},{33,1},{2,34},{34,2},{3,35},{35,3},{4,36},{36... | collective-permute-start | bytes 786440 | tf_op jit(solution)/shard_map/ppermute | solution.py:30
  9.4 6.0 %collective-permute-done.2.b3.refs_10_ = bf16[256,512]{1,0:T(8,128)(2,1)S(1)} collective-permute-done((bf16[256,512]{1,0:T(8,128)(2,1)}, bf16[256,512]{1,0:T(8,128)(2,1)S(1)}, u32[]{:S(2)}, u32[]{:S(2)}) %collective-permute-start.2) | collective-permute-done | bytes 262176 | tf_op jit(solution)/shard_map/ppermute | solution.py:34
  15.6 0.6 copy-done.12
  16.3 0.7 copy-done.33
  17.0 3.0 %gram.2 = (bf16[512,256]{1,0:T(8,128)(2,1)}, bf16[512,256]{1,0:T(8,128)(2,1)}, bf16[512,256]{1,0:T(8,128)(2,1)}, bf16[512,256]{1,0:T(8,128)(2,1)}) custom-call(bf16[256,512]{1,0:T(8,128)(2,1)} %refs_8_.1, bf16[256,512]{1,0:T(8,128)(2,1)} %copy-done.33, bf16[256,512]{1,0:T(8,128)(2,1)} %refs_8_.1, bf16[256,512]{1,0:T(8,128)(2,1)} %copy-done.13, ...), custom_call_target="tpu_custom_call" | custom-call | flops 536870912 | bytes 2621440 | tf_op jit(solution)/shard_map/gram/pallas_call | solution.py:67
  19.9 2.3 %collective-permute-start.4 = (bf16[512,256]{1,0:T(8,128)(2,1)}, bf16[512,256]{1,0:T(8,128)(2,1)S(1)}, u32[]{:S(2)}, u32[]{:S(2)}) collective-permute-start(bf16[512,256]{1,0:T(8,128)(2,1)} %get-tuple-element.26), channel_id=1, source_target_pairs={{0,1},{1,2},{2,3},{3,0},{4,5},{5,6},{6,7},{7,4},{8,9},{9,10},{10,1... | collective-permute-start | bytes 786440 | tf_op jit(solution)/shard_map/ppermute | solution.py:145
  22.2 1.5 collective-permute-start.5
  23.8 1.6 collective-permute-start.6
  25.3 1.1 collective-permute-start.19
  26.4 1.9 %collective-permute-start.18 = (bf16[256,512]{1,0:T(8,128)(2,1)S(1)}, bf16[256,512]{1,0:T(8,128)(2,1)S(1)}, u32[]{:S(2)}, u32[]{:S(2)}) collective-permute-start(bf16[256,512]{1,0:T(8,128)(2,1)S(1)} %collective-permute-done.16.b0.refs_12_), channel_id=1, source_target_pairs={{192,0},{0,64},{64,128},{128,192},{193,1},{1,65},{65,129},{129,193... | collective-permute-start | bytes 786440 | tf_op jit(solution)/shard_map/ppermute | solution.py:34
  28.3 1.5 collective-permute-done.4.b
  29.8 2.4 %collective-permute-start.17 = (bf16[256,512]{1,0:T(8,128)(2,1)S(1)}, bf16[256,512]{1,0:T(8,128)(2,1)S(1)}, u32[]{:S(2)}, u32[]{:S(2)}) collective-permute-start(bf16[256,512]{1,0:T(8,128)(2,1)S(1)} %collective-permute-done.16.b0.refs_12_), channel_id=1, source_target_pairs={{64,0},{128,64},{192,128},{0,192},{65,1},{129,65},{193,129},{1,193... | collective-permute-start | bytes 786440 | tf_op jit(solution)/shard_map/ppermute | solution.py:34
  32.3 4.3 %collective-permute-done.6.d = bf16[512,256]{1,0:T(8,128)(2,1)S(1)} collective-permute-done((bf16[512,256]{1,0:T(8,128)(2,1)}, bf16[512,256]{1,0:T(8,128)(2,1)S(1)}, u32[]{:S(2)}, u32[]{:S(2)}) %collective-permute-start.6) | collective-permute-done | bytes 262176 | tf_op jit(solution)/shard_map/ppermute | solution.py:145
  36.5 0.7 copy-done.30
  37.3 1.9 %sum_y.2 = (bf16[128,256]{1,0:T(8,128)(2,1)}, bf16[128,256]{1,0:T(8,128)(2,1)}, bf16[128,256]{1,0:T(8,128)(2,1)}, bf16[128,256]{1,0:T(8,128)(2,1)}) custom-call(bf16[512,256]{1,0:T(8,128)(2,1)} %get-tuple-element.25.a, bf16[512,256]{1,0:T(8,128)(2,1)} %copy-done.28, bf16[512,256]{1,0:T(8,128)(2,1)} %copy-done.29, bf16[512,256]{1,0:T(8,128)(2,1)} %copy-done.30), custom_call_target="tpu_custom_call" | custom-call | flops 524288 | bytes 1310720 | tf_op jit(solution)/shard_map/sum_y/pallas_call | solution.py:90
  39.2 3.0 %collective-permute-start.7 = (bf16[128,256]{1,0:T(8,128)(2,1)}, bf16[128,256]{1,0:T(8,128)(2,1)S(1)}, u32[]{:S(2)}, u32[]{:S(2)}) collective-permute-start(bf16[128,256]{1,0:T(8,128)(2,1)} %get-tuple-element.30), channel_id=1, source_target_pairs={{0,4},{4,8},{8,12},{12,0},{1,5},{5,9},{9,13},{13,1},{2,6},{6,10},{... | collective-permute-start | bytes 196616 | tf_op jit(solution)/shard_map/ppermute | solution.py:150
  42.2 3.1 %collective-permute-start.8 = (bf16[128,256]{1,0:T(8,128)(2,1)}, bf16[128,256]{1,0:T(8,128)(2,1)S(1)}, u32[]{:S(2)}, u32[]{:S(2)}) collective-permute-start(bf16[128,256]{1,0:T(8,128)(2,1)} %get-tuple-element.31), channel_id=1, source_target_pairs={{0,12},{4,0},{8,4},{12,8},{1,13},{5,1},{9,5},{13,9},{2,14},{6,2},{... | collective-permute-start | bytes 196616 | tf_op jit(solution)/shard_map/ppermute | solution.py:150
  45.3 4.4 %collective-permute-start.9 = (bf16[128,256]{1,0:T(8,128)(2,1)}, bf16[128,256]{1,0:T(8,128)(2,1)S(1)}, u32[]{:S(2)}, u32[]{:S(2)}) collective-permute-start(bf16[128,256]{1,0:T(8,128)(2,1)} %get-tuple-element.32), channel_id=1, source_target_pairs={{0,8},{4,12},{8,0},{12,4},{1,9},{5,13},{9,1},{13,5},{2,10},{6,14},... | collective-permute-start | bytes 196616 | tf_op jit(solution)/shard_map/ppermute | solution.py:150
  49.7 0.7 copy-done.16
  50.4 0.7 copy-done.17
  51.1 3.0 %gram.3 = (bf16[512,256]{1,0:T(8,128)(2,1)}, bf16[512,256]{1,0:T(8,128)(2,1)}, bf16[512,256]{1,0:T(8,128)(2,1)}, bf16[512,256]{1,0:T(8,128)(2,1)}) custom-call(bf16[256,512]{1,0:T(8,128)(2,1)} %refs_8_.1, bf16[256,512]{1,0:T(8,128)(2,1)} %copy-done.33, bf16[256,512]{1,0:T(8,128)(2,1)} %copy-done.14, bf16[256,512]{1,0:T(8,128)(2,1)} %copy-done.17, ...), custom_call_target="tpu_custom_call" | custom-call | flops 536870912 | bytes 2621440 | tf_op jit(solution)/shard_map/gram/pallas_call | solution.py:67
  54.1 0.6 collective-permute-start.20
  54.7 2.1 %collective-permute-start.21 = (bf16[512,256]{1,0:T(8,128)(2,1)}, bf16[512,256]{1,0:T(8,128)(2,1)S(1)}, u32[]{:S(2)}, u32[]{:S(2)}) collective-permute-start(bf16[512,256]{1,0:T(8,128)(2,1)} %get-tuple-element.35), channel_id=1, source_target_pairs={{0,3},{1,0},{2,1},{3,2},{4,7},{5,4},{6,5},{7,6},{8,11},{9,8},{10,9... | collective-permute-start | bytes 786440 | tf_op jit(solution)/shard_map/ppermute | solution.py:145
  57.0 2.2 %collective-permute-start.11 = (bf16[128,256]{1,0:T(8,128)(2,1)S(1)}, bf16[128,256]{1,0:T(8,128)(2,1)S(1)}, u32[]{:S(2)}, u32[]{:S(2)}) collective-permute-start(bf16[128,256]{1,0:T(8,128)(2,1)S(1)} %add_convert_fusion.2), channel_id=1, source_target_pairs={{8,0},{12,4},{0,8},{4,12},{9,1},{13,5},{1,9},{5,13},{10,2},{14,6},... | collective-permute-start | bytes 196616 | tf_op jit(solution)/shard_map/ppermute | solution.py:34
  59.2 2.0 %collective-permute-done.20.b = bf16[512,256]{1,0:T(8,128)(2,1)S(1)} collective-permute-done((bf16[512,256]{1,0:T(8,128)(2,1)}, bf16[512,256]{1,0:T(8,128)(2,1)S(1)}, u32[]{:S(2)}, u32[]{:S(2)}) %collective-permute-start.20) | collective-permute-done | bytes 262176 | tf_op jit(solution)/shard_map/ppermute | solution.py:145
  61.7 1.6 %collective-permute-done.21.c = bf16[512,256]{1,0:T(8,128)(2,1)S(1)} collective-permute-done((bf16[512,256]{1,0:T(8,128)(2,1)}, bf16[512,256]{1,0:T(8,128)(2,1)S(1)}, u32[]{:S(2)}, u32[]{:S(2)}) %collective-permute-start.21) | collective-permute-done | bytes 262176 | tf_op jit(solution)/shard_map/ppermute | solution.py:145
  63.3 3.3 %collective-permute-done.22.d = bf16[512,256]{1,0:T(8,128)(2,1)S(1)} collective-permute-done((bf16[512,256]{1,0:T(8,128)(2,1)}, bf16[512,256]{1,0:T(8,128)(2,1)S(1)}, u32[]{:S(2)}, u32[]{:S(2)}) %collective-permute-start.22) | collective-permute-done | bytes 262176 | tf_op jit(solution)/shard_map/ppermute | solution.py:145
  66.6 0.7 copy-done.27
  67.3 1.9 %sum_y.3 = (bf16[128,256]{1,0:T(8,128)(2,1)}, bf16[128,256]{1,0:T(8,128)(2,1)}, bf16[128,256]{1,0:T(8,128)(2,1)}, bf16[128,256]{1,0:T(8,128)(2,1)}) custom-call(bf16[512,256]{1,0:T(8,128)(2,1)} %get-tuple-element.33.a, bf16[512,256]{1,0:T(8,128)(2,1)} %copy-done.25, bf16[512,256]{1,0:T(8,128)(2,1)} %copy-done.26, bf16[512,256]{1,0:T(8,128)(2,1)} %copy-done.27), custom_call_target="tpu_custom_call" | custom-call | flops 524288 | bytes 1310720 | tf_op jit(solution)/shard_map/sum_y/pallas_call | solution.py:90
  69.3 3.6 %collective-permute-start.24 = (bf16[128,256]{1,0:T(8,128)(2,1)}, bf16[128,256]{1,0:T(8,128)(2,1)S(1)}, u32[]{:S(2)}, u32[]{:S(2)}) collective-permute-start(bf16[128,256]{1,0:T(8,128)(2,1)} %get-tuple-element.39), channel_id=1, source_target_pairs={{0,12},{4,0},{8,4},{12,8},{1,13},{5,1},{9,5},{13,9},{2,14},{6,2},{... | collective-permute-start | bytes 196616 | tf_op jit(solution)/shard_map/ppermute | solution.py:150
  72.8 1.3 collective-permute-start.25
  74.2 1.2 collective-permute-start.15
  75.4 5.4 %collective-permute-done.25 = bf16[128,256]{1,0:T(8,128)(2,1)S(1)} collective-permute-done((bf16[128,256]{1,0:T(8,128)(2,1)}, bf16[128,256]{1,0:T(8,128)(2,1)S(1)}, u32[]{:S(2)}, u32[]{:S(2)}) %collective-permute-start.25) | collective-permute-done | bytes 65568 | tf_op jit(solution)/shard_map/ppermute | solution.py:150
  81.0 3.2 %collective-permute-start.27 = (bf16[128,256]{1,0:T(8,128)(2,1)S(1)}, bf16[128,256]{1,0:T(8,128)(2,1)S(1)}, u32[]{:S(2)}, u32[]{:S(2)}) collective-permute-start(bf16[128,256]{1,0:T(8,128)(2,1)S(1)} %add_convert_fusion.1), channel_id=1, source_target_pairs={{8,0},{12,4},{0,8},{4,12},{9,1},{13,5},{1,9},{5,13},{10,2},{14,6},... | collective-permute-start | bytes 196616 | tf_op jit(solution)/shard_map/ppermute | solution.py:34
  84.2 1.6 %collective-permute-start.26 = (bf16[128,256]{1,0:T(8,128)(2,1)S(1)}, bf16[128,256]{1,0:T(8,128)(2,1)S(1)}, u32[]{:S(2)}, u32[]{:S(2)}) collective-permute-start(bf16[128,256]{1,0:T(8,128)(2,1)S(1)} %add_convert_fusion.1), channel_id=1, source_target_pairs={{4,0},{8,4},{12,8},{0,12},{5,1},{9,5},{13,9},{1,13},{6,2},{10,6},{... | collective-permute-start | bytes 196616 | tf_op jit(solution)/shard_map/ppermute | solution.py:34
  85.8 0.7 collective-permute-done.28
  86.5 2.0 %collective-permute-start.13 = (bf16[512,256]{1,0:T(8,128)(2,1)S(1)}, bf16[512,256]{1,0:T(8,128)(2,1)S(1)}, u32[]{:S(2)}, u32[]{:S(2)}) collective-permute-start(bf16[512,256]{1,0:T(8,128)(2,1)S(1)} %pad_maximum_fusion.refs_0_), channel_id=1, source_target_pairs={{1,0},{2,1},{3,2},{0,3},{5,4},{6,5},{7,6},{4,7},{9,8},{10,9},{11,1... | collective-permute-start | bytes 786440 | tf_op jit(solution)/shard_map/ppermute | solution.py:34
  88.5 1.9 %collective-permute-done.26 = bf16[128,256]{1,0:T(8,128)(2,1)S(1)} collective-permute-done((bf16[128,256]{1,0:T(8,128)(2,1)S(1)}, bf16[128,256]{1,0:T(8,128)(2,1)S(1)}, u32[]{:S(2)}, u32[]{:S(2)}) %collective-permute-start.26) | collective-permute-done | bytes 65568 | tf_op jit(solution)/shard_map/ppermute | solution.py:34
  90.5 0.9 collective-permute-start.30
  91.5 1.8 %collective-permute-start.29 = (bf16[512,256]{1,0:T(8,128)(2,1)S(1)}, bf16[512,256]{1,0:T(8,128)(2,1)S(1)}, u32[]{:S(2)}, u32[]{:S(2)}) collective-permute-start(bf16[512,256]{1,0:T(8,128)(2,1)S(1)} %pad_maximum_fusion.1.refs_4_), channel_id=1, source_target_pairs={{1,0},{2,1},{3,2},{0,3},{5,4},{6,5},{7,6},{4,7},{9,8},{10,9},{11,1... | collective-permute-start | bytes 786440 | tf_op jit(solution)/shard_map/ppermute | solution.py:34
  93.3 5.0 %collective-permute-done.31.refs_7_ = bf16[512,256]{1,0:T(8,128)(2,1)S(1)} collective-permute-done((bf16[512,256]{1,0:T(8,128)(2,1)S(1)}, bf16[512,256]{1,0:T(8,128)(2,1)S(1)}, u32[]{:S(2)}, u32[]{:S(2)}) %collective-permute-start.31) | collective-permute-done | bytes 262176 | tf_op jit(solution)/shard_map/ppermute | solution.py:34
  98.3 4.4 %collective-permute-done.30.refs_6_ = bf16[512,256]{1,0:T(8,128)(2,1)S(1)} collective-permute-done((bf16[512,256]{1,0:T(8,128)(2,1)S(1)}, bf16[512,256]{1,0:T(8,128)(2,1)S(1)}, u32[]{:S(2)}, u32[]{:S(2)}) %collective-permute-start.30) | collective-permute-done | bytes 262176 | tf_op jit(solution)/shard_map/ppermute | solution.py:34
  102.8 0.7 copy-done.7
  103.5 0.7 copy-done.8
  104.2 5.4 %apply.2 = (f32[256,512]{1,0:T(8,128)}, f32[256,512]{1,0:T(8,128)}) custom-call(bf16[512,256]{1,0:T(8,128)(2,1)} %copy-done, bf16[512,256]{1,0:T(8,128)(2,1)} %copy-done.5, bf16[512,256]{1,0:T(8,128)(2,1)} %copy-done.4, bf16[512,256]{1,0:T(8,128)(2,1)} %copy-done.3, bf16[512,256]{1,0:T(8,128)(2,1)} %copy-done.1, bf16[512,256]{1,0:T(8,128)(2,1)} %copy-done.8, ...), custom_call_target="tpu_custom_call" | custom-call | flops 1073741824 | bytes 5242880 | tf_op jit(solution)/shard_map/apply/pallas_call | solution.py:123
  109.6 6.3 %collective-permute-start.32 = (f32[256,512]{1,0:T(8,128)}, f32[256,512]{1,0:T(8,128)S(1)}, u32[]{:S(2)}, u32[]{:S(2)}) collective-permute-start(f32[256,512]{1,0:T(8,128)} %get-tuple-element.42), channel_id=1, source_target_pairs={{0,16},{16,0},{1,17},{17,1},{2,18},{18,2},{3,19},{19,3},{4,20},{20... | collective-permute-start | bytes 1572872 | tf_op jit(solution)/shard_map/ppermute | solution.py:30
  115.9 1.7 %collective-permute-done.32 = f32[256,512]{1,0:T(8,128)S(1)} collective-permute-done((f32[256,512]{1,0:T(8,128)}, f32[256,512]{1,0:T(8,128)S(1)}, u32[]{:S(2)}, u32[]{:S(2)}) %collective-permute-start.32) | collective-permute-done | bytes 524320 | tf_op jit(solution)/shard_map/ppermute | solution.py:30
  117.6 1.1 add_convert_fusion.refs_8_
  119.0 3.4 %collective-permute-start.34 = (bf16[256,512]{1,0:T(8,128)(2,1)S(1)}, bf16[256,512]{1,0:T(8,128)(2,1)S(1)}, u32[]{:S(2)}, u32[]{:S(2)}) collective-permute-start(bf16[256,512]{1,0:T(8,128)(2,1)S(1)} %add_convert_fusion.refs_8_), channel_id=1, source_target_pairs={{192,0},{0,64},{64,128},{128,192},{193,1},{1,65},{65,129},{129,193... | collective-permute-start | bytes 786440 | tf_op jit(solution)/shard_map/ppermute | solution.py:34
  122.4 3.9 %collective-permute-done.36.refs_12_ = bf16[256,512]{1,0:T(8,128)(2,1)S(1)} collective-permute-done((bf16[256,512]{1,0:T(8,128)(2,1)S(1)}, bf16[256,512]{1,0:T(8,128)(2,1)S(1)}, u32[]{:S(2)}, u32[]{:S(2)}) %collective-permute-start.36) | collective-permute-done | bytes 262176 | tf_op jit(solution)/shard_map/ppermute | solution.py:30
  126.4 2.3 %collective-permute-start.38 = (bf16[256,512]{1,0:T(8,128)(2,1)S(1)}, bf16[256,512]{1,0:T(8,128)(2,1)S(1)}, u32[]{:S(2)}, u32[]{:S(2)}) collective-permute-start(bf16[256,512]{1,0:T(8,128)(2,1)S(1)} %collective-permute-done.36.refs_12_), channel_id=1, source_target_pairs={{192,0},{0,64},{64,128},{128,192},{193,1},{1,65},{65,129},{129,193... | collective-permute-start | bytes 786440 | tf_op jit(solution)/shard_map/ppermute | solution.py:34
  128.7 1.8 %collective-permute-start.37 = (bf16[256,512]{1,0:T(8,128)(2,1)S(1)}, bf16[256,512]{1,0:T(8,128)(2,1)S(1)}, u32[]{:S(2)}, u32[]{:S(2)}) collective-permute-start(bf16[256,512]{1,0:T(8,128)(2,1)S(1)} %collective-permute-done.36.refs_12_), channel_id=1, source_target_pairs={{64,0},{128,64},{192,128},{0,192},{65,1},{129,65},{193,129},{1,193... | collective-permute-start | bytes 786440 | tf_op jit(solution)/shard_map/ppermute | solution.py:34
  130.5 4.6 %collective-permute-done.34.refs_10_ = bf16[256,512]{1,0:T(8,128)(2,1)S(1)} collective-permute-done((bf16[256,512]{1,0:T(8,128)(2,1)S(1)}, bf16[256,512]{1,0:T(8,128)(2,1)S(1)}, u32[]{:S(2)}, u32[]{:S(2)}) %collective-permute-start.34) | collective-permute-done | bytes 262176 | tf_op jit(solution)/shard_map/ppermute | solution.py:34
  135.1 4.1 %collective-permute-done.39.refs_15_ = bf16[256,512]{1,0:T(8,128)(2,1)S(1)} collective-permute-done((bf16[256,512]{1,0:T(8,128)(2,1)S(1)}, bf16[256,512]{1,0:T(8,128)(2,1)S(1)}, u32[]{:S(2)}, u32[]{:S(2)}) %collective-permute-start.39) | collective-permute-done | bytes 262176 | tf_op jit(solution)/shard_map/ppermute | solution.py:34
  139.2 6.4 %collective-permute-done.38.refs_14_ = bf16[256,512]{1,0:T(8,128)(2,1)S(1)} collective-permute-done((bf16[256,512]{1,0:T(8,128)(2,1)S(1)}, bf16[256,512]{1,0:T(8,128)(2,1)S(1)}, u32[]{:S(2)}, u32[]{:S(2)}) %collective-permute-start.38) | collective-permute-done | bytes 262176 | tf_op jit(solution)/shard_map/ppermute | solution.py:34
  145.6 0.7 copy-done.23
  146.3 0.7 copy-done.24
  147.0 5.4 %apply.3 = (f32[256,512]{1,0:T(8,128)}, f32[256,512]{1,0:T(8,128)}) custom-call(bf16[512,256]{1,0:T(8,128)(2,1)} %copy-done, bf16[512,256]{1,0:T(8,128)(2,1)} %copy-done.5, bf16[512,256]{1,0:T(8,128)(2,1)} %copy-done.4, bf16[512,256]{1,0:T(8,128)(2,1)} %copy-done.3, bf16[512,256]{1,0:T(8,128)(2,1)} %copy-done.1, bf16[512,256]{1,0:T(8,128)(2,1)} %copy-done.8, ...), custom_call_target="tpu_custom_call" | custom-call | flops 1073741824 | bytes 5242880 | tf_op jit(solution)/shard_map/apply/pallas_call | solution.py:123
  152.4 0.6 collective-permute-start.40
  153.0 1.7 %collective-permute-done.40 = f32[256,512]{1,0:T(8,128)S(1)} collective-permute-done((f32[256,512]{1,0:T(8,128)}, f32[256,512]{1,0:T(8,128)S(1)}, u32[]{:S(2)}, u32[]{:S(2)}) %collective-permute-start.40) | collective-permute-done | bytes 524320 | tf_op jit(solution)/shard_map/ppermute | solution.py:30
  154.8 2.1 %add_multiply_fusion = f32[256,512]{1,0:T(8,128)} fusion(f32[256,512]{1,0:T(8,128)} %get-tuple-element.43, f32[256,512]{1,0:T(8,128)S(1)} %collective-permute-done.40, bf16[256,512]{1,0:T(8,128)(2,1)S(1)} %copy-done.10, f32[256,512]{1,0:T(8,128)S(1)} %copy-done.2, f32[256,512]{1,0:T(8,128)S(1)} %collective-permute-done.32), kind=kLoop, calls=%fused_computation | loop fusion | flops 1179648 | bytes 2883584 | tf_op jit(solution)/shard_map/mul | solution.py:171
  (98 shorter events, 2.0 us)
Async XLA Ops:
  0.0 9.4 %collective-permute-start.3 = (bf16[256,512]{1,0:T(8,128)(2,1)}, bf16[256,512]{1,0:T(8,128)(2,1)S(1)}, u32[]{:S(2)}, u32[]{:S(2)}) collective-permute-start(bf16[256,512]{1,0:T(8,128)(2,1)} %refs_8_.1), channel_id=1, source_target_pairs={{128,0},{192,64},{0,128},{64,192},{129,1},{193,65},{1,129},{65,193... | collective-permute-start | bytes 786440 | tf_op jit(solution)/shard_map/ppermute | solution.py:34
  3.6 11.8 %collective-permute-start.2 = (bf16[256,512]{1,0:T(8,128)(2,1)}, bf16[256,512]{1,0:T(8,128)(2,1)S(1)}, u32[]{:S(2)}, u32[]{:S(2)}) collective-permute-start(bf16[256,512]{1,0:T(8,128)(2,1)} %refs_8_.1), channel_id=1, source_target_pairs={{192,0},{0,64},{64,128},{128,192},{193,1},{1,65},{65,129},{129,193... | collective-permute-start | bytes 786440 | tf_op jit(solution)/shard_map/ppermute | solution.py:34
  3.9 11.7 %collective-permute-start.1 = (bf16[256,512]{1,0:T(8,128)(2,1)}, bf16[256,512]{1,0:T(8,128)(2,1)S(1)}, u32[]{:S(2)}, u32[]{:S(2)}) collective-permute-start(bf16[256,512]{1,0:T(8,128)(2,1)} %refs_8_.1), channel_id=1, source_target_pairs={{64,0},{128,64},{192,128},{0,192},{65,1},{129,65},{193,129},{1,193... | collective-permute-start | bytes 786440 | tf_op jit(solution)/shard_map/ppermute | solution.py:34
  6.3 9.3 %collective-permute-start = (bf16[256,512]{1,0:T(8,128)(2,1)}, bf16[256,512]{1,0:T(8,128)(2,1)S(1)}, u32[]{:S(2)}, u32[]{:S(2)}) collective-permute-start(bf16[256,512]{1,0:T(8,128)(2,1)} %refs_8_.1), channel_id=1, source_target_pairs={{0,16},{16,0},{1,17},{17,1},{2,18},{18,2},{3,19},{19,3},{4,20},{20... | collective-permute-start | bytes 786440 | tf_op jit(solution)/shard_map/ppermute | solution.py:30
  7.8 17.5 %collective-permute-start.16 = (bf16[256,512]{1,0:T(8,128)(2,1)}, bf16[256,512]{1,0:T(8,128)(2,1)S(1)}, u32[]{:S(2)}, u32[]{:S(2)}) collective-permute-start(bf16[256,512]{1,0:T(8,128)(2,1)} %refs_8_.1), channel_id=1, source_target_pairs={{0,32},{32,0},{1,33},{33,1},{2,34},{34,2},{3,35},{35,3},{4,36},{36... | collective-permute-start | bytes 786440 | tf_op jit(solution)/shard_map/ppermute | solution.py:30
  9.4 6.2 %copy-start.11 = (bf16[256,512]{1,0:T(8,128)(2,1)}, bf16[256,512]{1,0:T(8,128)(2,1)S(1)}, u32[]{:S(2)}) copy-start(bf16[256,512]{1,0:T(8,128)(2,1)S(1)} %collective-permute-done.3.b2.refs_11_) | copy-start | bytes 786436
  19.9 9.9 %collective-permute-start.4 = (bf16[512,256]{1,0:T(8,128)(2,1)}, bf16[512,256]{1,0:T(8,128)(2,1)S(1)}, u32[]{:S(2)}, u32[]{:S(2)}) collective-permute-start(bf16[512,256]{1,0:T(8,128)(2,1)} %get-tuple-element.26), channel_id=1, source_target_pairs={{0,1},{1,2},{2,3},{3,0},{4,5},{5,6},{6,7},{7,4},{8,9},{9,10},{10,1... | collective-permute-start | bytes 786440 | tf_op jit(solution)/shard_map/ppermute | solution.py:145
  22.2 10.0 %collective-permute-start.5 = (bf16[512,256]{1,0:T(8,128)(2,1)}, bf16[512,256]{1,0:T(8,128)(2,1)S(1)}, u32[]{:S(2)}, u32[]{:S(2)}) collective-permute-start(bf16[512,256]{1,0:T(8,128)(2,1)} %get-tuple-element.27), channel_id=1, source_target_pairs={{0,3},{1,0},{2,1},{3,2},{4,7},{5,4},{6,5},{7,6},{8,11},{9,8},{10,9... | collective-permute-start | bytes 786440 | tf_op jit(solution)/shard_map/ppermute | solution.py:145
  23.8 12.8 %collective-permute-start.6 = (bf16[512,256]{1,0:T(8,128)(2,1)}, bf16[512,256]{1,0:T(8,128)(2,1)S(1)}, u32[]{:S(2)}, u32[]{:S(2)}) collective-permute-start(bf16[512,256]{1,0:T(8,128)(2,1)} %get-tuple-element.28), channel_id=1, source_target_pairs={{0,2},{1,3},{2,0},{3,1},{4,6},{5,7},{6,4},{7,5},{8,10},{9,11},{10,... | collective-permute-start | bytes 786440 | tf_op jit(solution)/shard_map/ppermute | solution.py:145
  25.3 13.9 %copy-start.14 = (bf16[256,512]{1,0:T(8,128)(2,1)}, bf16[256,512]{1,0:T(8,128)(2,1)S(1)}, u32[]{:S(2)}) copy-start(bf16[256,512]{1,0:T(8,128)(2,1)S(1)} %collective-permute-done.16.b0.refs_12_) | copy-start | bytes 786436
  25.3 20.0 %collective-permute-start.19 = (bf16[256,512]{1,0:T(8,128)(2,1)S(1)}, bf16[256,512]{1,0:T(8,128)(2,1)S(1)}, u32[]{:S(2)}, u32[]{:S(2)}) collective-permute-start(bf16[256,512]{1,0:T(8,128)(2,1)S(1)} %collective-permute-done.16.b0.refs_12_), channel_id=1, source_target_pairs={{128,0},{192,64},{0,128},{64,192},{129,1},{193,65},{1,129},{65,193... | collective-permute-start | bytes 786440 | tf_op jit(solution)/shard_map/ppermute | solution.py:34
  26.4 23.3 %collective-permute-start.18 = (bf16[256,512]{1,0:T(8,128)(2,1)S(1)}, bf16[256,512]{1,0:T(8,128)(2,1)S(1)}, u32[]{:S(2)}, u32[]{:S(2)}) collective-permute-start(bf16[256,512]{1,0:T(8,128)(2,1)S(1)} %collective-permute-done.16.b0.refs_12_), channel_id=1, source_target_pairs={{192,0},{0,64},{64,128},{128,192},{193,1},{1,65},{65,129},{129,193... | collective-permute-start | bytes 786440 | tf_op jit(solution)/shard_map/ppermute | solution.py:34
  29.8 6.7 %copy-start.28 = (bf16[512,256]{1,0:T(8,128)(2,1)}, bf16[512,256]{1,0:T(8,128)(2,1)S(1)}, u32[]{:S(2)}) copy-start(bf16[512,256]{1,0:T(8,128)(2,1)S(1)} %collective-permute-done.4.b) | copy-start | bytes 786436
  29.8 19.9 %collective-permute-start.17 = (bf16[256,512]{1,0:T(8,128)(2,1)S(1)}, bf16[256,512]{1,0:T(8,128)(2,1)S(1)}, u32[]{:S(2)}, u32[]{:S(2)}) collective-permute-start(bf16[256,512]{1,0:T(8,128)(2,1)S(1)} %collective-permute-done.16.b0.refs_12_), channel_id=1, source_target_pairs={{64,0},{128,64},{192,128},{0,192},{65,1},{129,65},{193,129},{1,193... | collective-permute-start | bytes 786440 | tf_op jit(solution)/shard_map/ppermute | solution.py:34
  32.3 4.3 %copy-start.29 = (bf16[512,256]{1,0:T(8,128)(2,1)}, bf16[512,256]{1,0:T(8,128)(2,1)S(1)}, u32[]{:S(2)}) copy-start(bf16[512,256]{1,0:T(8,128)(2,1)S(1)} %collective-permute-done.5.c) | copy-start | bytes 786436
  39.2 17.7 %collective-permute-start.7 = (bf16[128,256]{1,0:T(8,128)(2,1)}, bf16[128,256]{1,0:T(8,128)(2,1)S(1)}, u32[]{:S(2)}, u32[]{:S(2)}) collective-permute-start(bf16[128,256]{1,0:T(8,128)(2,1)} %get-tuple-element.30), channel_id=1, source_target_pairs={{0,4},{4,8},{8,12},{12,0},{1,5},{5,9},{9,13},{13,1},{2,6},{6,10},{... | collective-permute-start | bytes 196616 | tf_op jit(solution)/shard_map/ppermute | solution.py:150
  42.2 14.7 %collective-permute-start.8 = (bf16[128,256]{1,0:T(8,128)(2,1)}, bf16[128,256]{1,0:T(8,128)(2,1)S(1)}, u32[]{:S(2)}, u32[]{:S(2)}) collective-permute-start(bf16[128,256]{1,0:T(8,128)(2,1)} %get-tuple-element.31), channel_id=1, source_target_pairs={{0,12},{4,0},{8,4},{12,8},{1,13},{5,1},{9,5},{13,9},{2,14},{6,2},{... | collective-permute-start | bytes 196616 | tf_op jit(solution)/shard_map/ppermute | solution.py:150
  45.3 4.4 %copy-start.15 = (bf16[256,512]{1,0:T(8,128)(2,1)}, bf16[256,512]{1,0:T(8,128)(2,1)S(1)}, u32[]{:S(2)}) copy-start(bf16[256,512]{1,0:T(8,128)(2,1)S(1)} %collective-permute-done.19.b2.refs_15_) | copy-start | bytes 786436
  45.3 11.6 %copy-start.31 = (bf16[128,256]{1,0:T(8,128)(2,1)S(1)}, bf16[128,256]{1,0:T(8,128)(2,1)}, u32[]{:S(2)}) copy-start(bf16[128,256]{1,0:T(8,128)(2,1)} %get-tuple-element.29) | copy-start | bytes 196612
  45.3 11.6 %collective-permute-start.9 = (bf16[128,256]{1,0:T(8,128)(2,1)}, bf16[128,256]{1,0:T(8,128)(2,1)S(1)}, u32[]{:S(2)}, u32[]{:S(2)}) collective-permute-start(bf16[128,256]{1,0:T(8,128)(2,1)} %get-tuple-element.32), channel_id=1, source_target_pairs={{0,8},{4,12},{8,0},{12,4},{1,9},{5,13},{9,1},{13,5},{2,10},{6,14},... | collective-permute-start | bytes 196616 | tf_op jit(solution)/shard_map/ppermute | solution.py:150
  54.1 7.1 %collective-permute-start.20 = (bf16[512,256]{1,0:T(8,128)(2,1)}, bf16[512,256]{1,0:T(8,128)(2,1)S(1)}, u32[]{:S(2)}, u32[]{:S(2)}) collective-permute-start(bf16[512,256]{1,0:T(8,128)(2,1)} %get-tuple-element.34), channel_id=1, source_target_pairs={{0,1},{1,2},{2,3},{3,0},{4,5},{5,6},{6,7},{7,4},{8,9},{9,10},{10,1... | collective-permute-start | bytes 786440 | tf_op jit(solution)/shard_map/ppermute | solution.py:145
  54.7 8.6 %collective-permute-start.21 = (bf16[512,256]{1,0:T(8,128)(2,1)}, bf16[512,256]{1,0:T(8,128)(2,1)S(1)}, u32[]{:S(2)}, u32[]{:S(2)}) collective-permute-start(bf16[512,256]{1,0:T(8,128)(2,1)} %get-tuple-element.35), channel_id=1, source_target_pairs={{0,3},{1,0},{2,1},{3,2},{4,7},{5,4},{6,5},{7,6},{8,11},{9,8},{10,9... | collective-permute-start | bytes 786440 | tf_op jit(solution)/shard_map/ppermute | solution.py:145
  56.9 9.7 %collective-permute-start.22 = (bf16[512,256]{1,0:T(8,128)(2,1)}, bf16[512,256]{1,0:T(8,128)(2,1)S(1)}, u32[]{:S(2)}, u32[]{:S(2)}) collective-permute-start(bf16[512,256]{1,0:T(8,128)(2,1)} %get-tuple-element.36), channel_id=1, source_target_pairs={{0,2},{1,3},{2,0},{3,1},{4,6},{5,7},{6,4},{7,5},{8,10},{9,11},{10,... | collective-permute-start | bytes 786440 | tf_op jit(solution)/shard_map/ppermute | solution.py:145
  56.9 15.9 %collective-permute-start.12 = (bf16[128,256]{1,0:T(8,128)(2,1)S(1)}, bf16[128,256]{1,0:T(8,128)(2,1)S(1)}, u32[]{:S(2)}, u32[]{:S(2)}) collective-permute-start(bf16[128,256]{1,0:T(8,128)(2,1)S(1)} %add_convert_fusion.2), channel_id=1, source_target_pairs={{12,0},{0,4},{4,8},{8,12},{13,1},{1,5},{5,9},{9,13},{14,2},{2,6},{... | collective-permute-start | bytes 196616 | tf_op jit(solution)/shard_map/ppermute | solution.py:34
  57.0 17.1 %collective-permute-start.11 = (bf16[128,256]{1,0:T(8,128)(2,1)S(1)}, bf16[128,256]{1,0:T(8,128)(2,1)S(1)}, u32[]{:S(2)}, u32[]{:S(2)}) collective-permute-start(bf16[128,256]{1,0:T(8,128)(2,1)S(1)} %add_convert_fusion.2), channel_id=1, source_target_pairs={{8,0},{12,4},{0,8},{4,12},{9,1},{13,5},{1,9},{5,13},{10,2},{14,6},... | collective-permute-start | bytes 196616 | tf_op jit(solution)/shard_map/ppermute | solution.py:34
  61.2 5.4 %copy-start.25 = (bf16[512,256]{1,0:T(8,128)(2,1)}, bf16[512,256]{1,0:T(8,128)(2,1)S(1)}, u32[]{:S(2)}) copy-start(bf16[512,256]{1,0:T(8,128)(2,1)S(1)} %collective-permute-done.20.b) | copy-start | bytes 786436
  61.2 13.0 %collective-permute-start.10 = (bf16[128,256]{1,0:T(8,128)(2,1)S(1)}, bf16[128,256]{1,0:T(8,128)(2,1)S(1)}, u32[]{:S(2)}, u32[]{:S(2)}) collective-permute-start(bf16[128,256]{1,0:T(8,128)(2,1)S(1)} %add_convert_fusion.2), channel_id=1, source_target_pairs={{4,0},{8,4},{12,8},{0,12},{5,1},{9,5},{13,9},{1,13},{6,2},{10,6},{... | collective-permute-start | bytes 196616 | tf_op jit(solution)/shard_map/ppermute | solution.py:34
  63.3 3.3 %copy-start.26 = (bf16[512,256]{1,0:T(8,128)(2,1)}, bf16[512,256]{1,0:T(8,128)(2,1)S(1)}, u32[]{:S(2)}) copy-start(bf16[512,256]{1,0:T(8,128)(2,1)S(1)} %collective-permute-done.21.c) | copy-start | bytes 786436
  69.3 6.1 %collective-permute-start.23 = (bf16[128,256]{1,0:T(8,128)(2,1)}, bf16[128,256]{1,0:T(8,128)(2,1)S(1)}, u32[]{:S(2)}, u32[]{:S(2)}) collective-permute-start(bf16[128,256]{1,0:T(8,128)(2,1)} %get-tuple-element.38), channel_id=1, source_target_pairs={{0,4},{4,8},{8,12},{12,0},{1,5},{5,9},{9,13},{13,1},{2,6},{6,10},{... | collective-permute-start | bytes 196616 | tf_op jit(solution)/shard_map/ppermute | solution.py:150
  69.3 6.1 %collective-permute-start.24 = (bf16[128,256]{1,0:T(8,128)(2,1)}, bf16[128,256]{1,0:T(8,128)(2,1)S(1)}, u32[]{:S(2)}, u32[]{:S(2)}) collective-permute-start(bf16[128,256]{1,0:T(8,128)(2,1)} %get-tuple-element.39), channel_id=1, source_target_pairs={{0,12},{4,0},{8,4},{12,8},{1,13},{5,1},{9,5},{13,9},{2,14},{6,2},{... | collective-permute-start | bytes 196616 | tf_op jit(solution)/shard_map/ppermute | solution.py:150
  72.8 8.0 %copy-start.32 = (bf16[128,256]{1,0:T(8,128)(2,1)S(1)}, bf16[128,256]{1,0:T(8,128)(2,1)}, u32[]{:S(2)}) copy-start(bf16[128,256]{1,0:T(8,128)(2,1)} %get-tuple-element.37) | copy-start | bytes 196612
  72.8 8.0 %collective-permute-start.25 = (bf16[128,256]{1,0:T(8,128)(2,1)}, bf16[128,256]{1,0:T(8,128)(2,1)S(1)}, u32[]{:S(2)}, u32[]{:S(2)}) collective-permute-start(bf16[128,256]{1,0:T(8,128)(2,1)} %get-tuple-element.40), channel_id=1, source_target_pairs={{0,8},{4,12},{8,0},{12,4},{1,9},{5,13},{9,1},{13,5},{2,10},{6,14},... | collective-permute-start | bytes 196616 | tf_op jit(solution)/shard_map/ppermute | solution.py:150
  74.2 16.2 %copy-start = (bf16[512,256]{1,0:T(8,128)(2,1)}, bf16[512,256]{1,0:T(8,128)(2,1)S(1)}, u32[]{:S(2)}) copy-start(bf16[512,256]{1,0:T(8,128)(2,1)S(1)} %pad_maximum_fusion.refs_0_) | copy-start | bytes 786436
  74.2 17.3 %collective-permute-start.15 = (bf16[512,256]{1,0:T(8,128)(2,1)S(1)}, bf16[512,256]{1,0:T(8,128)(2,1)S(1)}, u32[]{:S(2)}, u32[]{:S(2)}) collective-permute-start(bf16[512,256]{1,0:T(8,128)(2,1)S(1)} %pad_maximum_fusion.refs_0_), channel_id=1, source_target_pairs={{2,0},{3,1},{0,2},{1,3},{6,4},{7,5},{4,6},{5,7},{10,8},{11,9},{8,1... | collective-permute-start | bytes 786440 | tf_op jit(solution)/shard_map/ppermute | solution.py:34
  80.9 5.6 %collective-permute-start.28 = (bf16[128,256]{1,0:T(8,128)(2,1)S(1)}, bf16[128,256]{1,0:T(8,128)(2,1)S(1)}, u32[]{:S(2)}, u32[]{:S(2)}) collective-permute-start(bf16[128,256]{1,0:T(8,128)(2,1)S(1)} %add_convert_fusion.1), channel_id=1, source_target_pairs={{12,0},{0,4},{4,8},{8,12},{13,1},{1,5},{5,9},{9,13},{14,2},{2,6},{... | collective-permute-start | bytes 196616 | tf_op jit(solution)/shard_map/ppermute | solution.py:34
  81.0 7.5 %collective-permute-start.27 = (bf16[128,256]{1,0:T(8,128)(2,1)S(1)}, bf16[128,256]{1,0:T(8,128)(2,1)S(1)}, u32[]{:S(2)}, u32[]{:S(2)}) collective-permute-start(bf16[128,256]{1,0:T(8,128)(2,1)S(1)} %add_convert_fusion.1), channel_id=1, source_target_pairs={{8,0},{12,4},{0,8},{4,12},{9,1},{13,5},{1,9},{5,13},{10,2},{14,6},... | collective-permute-start | bytes 196616 | tf_op jit(solution)/shard_map/ppermute | solution.py:34
  84.2 6.2 %collective-permute-start.26 = (bf16[128,256]{1,0:T(8,128)(2,1)S(1)}, bf16[128,256]{1,0:T(8,128)(2,1)S(1)}, u32[]{:S(2)}, u32[]{:S(2)}) collective-permute-start(bf16[128,256]{1,0:T(8,128)(2,1)S(1)} %add_convert_fusion.1), channel_id=1, source_target_pairs={{4,0},{8,4},{12,8},{0,12},{5,1},{9,5},{13,9},{1,13},{6,2},{10,6},{... | collective-permute-start | bytes 196616 | tf_op jit(solution)/shard_map/ppermute | solution.py:34
  85.8 7.5 %collective-permute-start.14 = (bf16[512,256]{1,0:T(8,128)(2,1)S(1)}, bf16[512,256]{1,0:T(8,128)(2,1)S(1)}, u32[]{:S(2)}, u32[]{:S(2)}) collective-permute-start(bf16[512,256]{1,0:T(8,128)(2,1)S(1)} %pad_maximum_fusion.refs_0_), channel_id=1, source_target_pairs={{3,0},{0,1},{1,2},{2,3},{7,4},{4,5},{5,6},{6,7},{11,8},{8,9},{9,10... | collective-permute-start | bytes 786440 | tf_op jit(solution)/shard_map/ppermute | solution.py:34
  86.5 6.8 %collective-permute-start.13 = (bf16[512,256]{1,0:T(8,128)(2,1)S(1)}, bf16[512,256]{1,0:T(8,128)(2,1)S(1)}, u32[]{:S(2)}, u32[]{:S(2)}) collective-permute-start(bf16[512,256]{1,0:T(8,128)(2,1)S(1)} %pad_maximum_fusion.refs_0_), channel_id=1, source_target_pairs={{1,0},{2,1},{3,2},{0,3},{5,4},{6,5},{7,6},{4,7},{9,8},{10,9},{11,1... | collective-permute-start | bytes 786440 | tf_op jit(solution)/shard_map/ppermute | solution.py:34
  90.4 12.3 %copy-start.1 = (bf16[512,256]{1,0:T(8,128)(2,1)}, bf16[512,256]{1,0:T(8,128)(2,1)S(1)}, u32[]{:S(2)}) copy-start(bf16[512,256]{1,0:T(8,128)(2,1)S(1)} %pad_maximum_fusion.1.refs_4_) | copy-start | bytes 786436
  90.4 7.9 %collective-permute-start.31 = (bf16[512,256]{1,0:T(8,128)(2,1)S(1)}, bf16[512,256]{1,0:T(8,128)(2,1)S(1)}, u32[]{:S(2)}, u32[]{:S(2)}) collective-permute-start(bf16[512,256]{1,0:T(8,128)(2,1)S(1)} %pad_maximum_fusion.1.refs_4_), channel_id=1, source_target_pairs={{2,0},{3,1},{0,2},{1,3},{6,4},{7,5},{4,6},{5,7},{10,8},{11,9},{8,1... | collective-permute-start | bytes 786440 | tf_op jit(solution)/shard_map/ppermute | solution.py:34
  90.5 12.2 %collective-permute-start.30 = (bf16[512,256]{1,0:T(8,128)(2,1)S(1)}, bf16[512,256]{1,0:T(8,128)(2,1)S(1)}, u32[]{:S(2)}, u32[]{:S(2)}) collective-permute-start(bf16[512,256]{1,0:T(8,128)(2,1)S(1)} %pad_maximum_fusion.1.refs_4_), channel_id=1, source_target_pairs={{3,0},{0,1},{1,2},{2,3},{7,4},{4,5},{5,6},{6,7},{11,8},{8,9},{9,10... | collective-permute-start | bytes 786440 | tf_op jit(solution)/shard_map/ppermute | solution.py:34
  91.5 11.3 %copy-start.3 = (bf16[512,256]{1,0:T(8,128)(2,1)}, bf16[512,256]{1,0:T(8,128)(2,1)S(1)}, u32[]{:S(2)}) copy-start(bf16[512,256]{1,0:T(8,128)(2,1)S(1)} %collective-permute-done.15.refs_3_) | copy-start | bytes 786436
  91.5 11.3 %collective-permute-start.29 = (bf16[512,256]{1,0:T(8,128)(2,1)S(1)}, bf16[512,256]{1,0:T(8,128)(2,1)S(1)}, u32[]{:S(2)}, u32[]{:S(2)}) collective-permute-start(bf16[512,256]{1,0:T(8,128)(2,1)S(1)} %pad_maximum_fusion.1.refs_4_), channel_id=1, source_target_pairs={{1,0},{2,1},{3,2},{0,3},{5,4},{6,5},{7,6},{4,7},{9,8},{10,9},{11,1... | collective-permute-start | bytes 786440 | tf_op jit(solution)/shard_map/ppermute | solution.py:34
  93.3 9.5 %copy-start.4 = (bf16[512,256]{1,0:T(8,128)(2,1)}, bf16[512,256]{1,0:T(8,128)(2,1)S(1)}, u32[]{:S(2)}) copy-start(bf16[512,256]{1,0:T(8,128)(2,1)S(1)} %collective-permute-done.14.refs_2_) | copy-start | bytes 786436
  93.3 9.5 %copy-start.5 = (bf16[512,256]{1,0:T(8,128)(2,1)}, bf16[512,256]{1,0:T(8,128)(2,1)S(1)}, u32[]{:S(2)}) copy-start(bf16[512,256]{1,0:T(8,128)(2,1)S(1)} %collective-permute-done.13.refs_1_) | copy-start | bytes 786436
  98.3 4.5 %copy-start.6 = (bf16[512,256]{1,0:T(8,128)(2,1)}, bf16[512,256]{1,0:T(8,128)(2,1)S(1)}, u32[]{:S(2)}) copy-start(bf16[512,256]{1,0:T(8,128)(2,1)S(1)} %collective-permute-done.31.refs_7_) | copy-start | bytes 786436
  109.6 8.0 %collective-permute-start.32 = (f32[256,512]{1,0:T(8,128)}, f32[256,512]{1,0:T(8,128)S(1)}, u32[]{:S(2)}, u32[]{:S(2)}) collective-permute-start(f32[256,512]{1,0:T(8,128)} %get-tuple-element.42), channel_id=1, source_target_pairs={{0,16},{16,0},{1,17},{17,1},{2,18},{18,2},{3,19},{19,3},{4,20},{20... | collective-permute-start | bytes 1572872 | tf_op jit(solution)/shard_map/ppermute | solution.py:30
  118.8 26.8 %copy-start.9 = (bf16[256,512]{1,0:T(8,128)(2,1)}, bf16[256,512]{1,0:T(8,128)(2,1)S(1)}, u32[]{:S(2)}) copy-start(bf16[256,512]{1,0:T(8,128)(2,1)S(1)} %add_convert_fusion.refs_8_) | copy-start | bytes 786436
  118.8 36.0 %copy-start.2 = (f32[256,512]{1,0:T(8,128)S(1)}, f32[256,512]{1,0:T(8,128)}, u32[]{:S(2)}) copy-start(f32[256,512]{1,0:T(8,128)} %get-tuple-element.41) | copy-start | bytes 1572868
  118.8 36.0 %copy-start.10 = (bf16[256,512]{1,0:T(8,128)(2,1)S(1)}, bf16[256,512]{1,0:T(8,128)(2,1)}, u32[]{:S(2)}) copy-start(bf16[256,512]{1,0:T(8,128)(2,1)} %refs_8_.1) | copy-start | bytes 786436
  118.8 7.6 %collective-permute-start.36 = (bf16[256,512]{1,0:T(8,128)(2,1)S(1)}, bf16[256,512]{1,0:T(8,128)(2,1)S(1)}, u32[]{:S(2)}, u32[]{:S(2)}) collective-permute-start(bf16[256,512]{1,0:T(8,128)(2,1)S(1)} %add_convert_fusion.refs_8_), channel_id=1, source_target_pairs={{0,32},{32,0},{1,33},{33,1},{2,34},{34,2},{3,35},{35,3},{4,36},{36... | collective-permute-start | bytes 786440 | tf_op jit(solution)/shard_map/ppermute | solution.py:30
  118.9 9.8 %collective-permute-start.35 = (bf16[256,512]{1,0:T(8,128)(2,1)S(1)}, bf16[256,512]{1,0:T(8,128)(2,1)S(1)}, u32[]{:S(2)}, u32[]{:S(2)}) collective-permute-start(bf16[256,512]{1,0:T(8,128)(2,1)S(1)} %add_convert_fusion.refs_8_), channel_id=1, source_target_pairs={{128,0},{192,64},{0,128},{64,192},{129,1},{193,65},{1,129},{65,193... | collective-permute-start | bytes 786440 | tf_op jit(solution)/shard_map/ppermute | solution.py:34
  119.0 16.1 %collective-permute-start.34 = (bf16[256,512]{1,0:T(8,128)(2,1)S(1)}, bf16[256,512]{1,0:T(8,128)(2,1)S(1)}, u32[]{:S(2)}, u32[]{:S(2)}) collective-permute-start(bf16[256,512]{1,0:T(8,128)(2,1)S(1)} %add_convert_fusion.refs_8_), channel_id=1, source_target_pairs={{192,0},{0,64},{64,128},{128,192},{193,1},{1,65},{65,129},{129,193... | collective-permute-start | bytes 786440 | tf_op jit(solution)/shard_map/ppermute | solution.py:34
  122.3 12.8 %collective-permute-start.33 = (bf16[256,512]{1,0:T(8,128)(2,1)S(1)}, bf16[256,512]{1,0:T(8,128)(2,1)S(1)}, u32[]{:S(2)}, u32[]{:S(2)}) collective-permute-start(bf16[256,512]{1,0:T(8,128)(2,1)S(1)} %add_convert_fusion.refs_8_), channel_id=1, source_target_pairs={{64,0},{128,64},{192,128},{0,192},{65,1},{129,65},{193,129},{1,193... | collective-permute-start | bytes 786440 | tf_op jit(solution)/shard_map/ppermute | solution.py:34
  126.4 19.2 %copy-start.18 = (bf16[256,512]{1,0:T(8,128)(2,1)}, bf16[256,512]{1,0:T(8,128)(2,1)S(1)}, u32[]{:S(2)}) copy-start(bf16[256,512]{1,0:T(8,128)(2,1)S(1)} %collective-permute-done.36.refs_12_) | copy-start | bytes 786436
  126.4 12.8 %collective-permute-start.39 = (bf16[256,512]{1,0:T(8,128)(2,1)S(1)}, bf16[256,512]{1,0:T(8,128)(2,1)S(1)}, u32[]{:S(2)}, u32[]{:S(2)}) collective-permute-start(bf16[256,512]{1,0:T(8,128)(2,1)S(1)} %collective-permute-done.36.refs_12_), channel_id=1, source_target_pairs={{128,0},{192,64},{0,128},{64,192},{129,1},{193,65},{1,129},{65,193... | collective-permute-start | bytes 786440 | tf_op jit(solution)/shard_map/ppermute | solution.py:34
  126.4 19.2 %collective-permute-start.38 = (bf16[256,512]{1,0:T(8,128)(2,1)S(1)}, bf16[256,512]{1,0:T(8,128)(2,1)S(1)}, u32[]{:S(2)}, u32[]{:S(2)}) collective-permute-start(bf16[256,512]{1,0:T(8,128)(2,1)S(1)} %collective-permute-done.36.refs_12_), channel_id=1, source_target_pairs={{192,0},{0,64},{64,128},{128,192},{193,1},{1,65},{65,129},{129,193... | collective-permute-start | bytes 786440 | tf_op jit(solution)/shard_map/ppermute | solution.py:34
  128.7 16.8 %copy-start.19 = (bf16[256,512]{1,0:T(8,128)(2,1)}, bf16[256,512]{1,0:T(8,128)(2,1)S(1)}, u32[]{:S(2)}) copy-start(bf16[256,512]{1,0:T(8,128)(2,1)S(1)} %collective-permute-done.35.refs_11_) | copy-start | bytes 786436
  128.7 16.8 %collective-permute-start.37 = (bf16[256,512]{1,0:T(8,128)(2,1)S(1)}, bf16[256,512]{1,0:T(8,128)(2,1)S(1)}, u32[]{:S(2)}, u32[]{:S(2)}) collective-permute-start(bf16[256,512]{1,0:T(8,128)(2,1)S(1)} %collective-permute-done.36.refs_12_), channel_id=1, source_target_pairs={{64,0},{128,64},{192,128},{0,192},{65,1},{129,65},{193,129},{1,193... | collective-permute-start | bytes 786440 | tf_op jit(solution)/shard_map/ppermute | solution.py:34
  135.1 10.5 %copy-start.20 = (bf16[256,512]{1,0:T(8,128)(2,1)}, bf16[256,512]{1,0:T(8,128)(2,1)S(1)}, u32[]{:S(2)}) copy-start(bf16[256,512]{1,0:T(8,128)(2,1)S(1)} %collective-permute-done.34.refs_10_) | copy-start | bytes 786436
  135.1 10.5 %copy-start.21 = (bf16[256,512]{1,0:T(8,128)(2,1)}, bf16[256,512]{1,0:T(8,128)(2,1)S(1)}, u32[]{:S(2)}) copy-start(bf16[256,512]{1,0:T(8,128)(2,1)S(1)} %collective-permute-done.33.refs_9_) | copy-start | bytes 786436
  139.2 6.4 %copy-start.22 = (bf16[256,512]{1,0:T(8,128)(2,1)}, bf16[256,512]{1,0:T(8,128)(2,1)S(1)}, u32[]{:S(2)}) copy-start(bf16[256,512]{1,0:T(8,128)(2,1)S(1)} %collective-permute-done.39.refs_15_) | copy-start | bytes 786436
  152.4 2.3 %collective-permute-start.40 = (f32[256,512]{1,0:T(8,128)}, f32[256,512]{1,0:T(8,128)S(1)}, u32[]{:S(2)}, u32[]{:S(2)}) collective-permute-start(f32[256,512]{1,0:T(8,128)} %get-tuple-element.44), channel_id=1, source_target_pairs={{0,16},{16,0},{1,17},{17,1},{2,18},{18,2},{3,19},{19,3},{4,20},{20... | collective-permute-start | bytes 1572872 | tf_op jit(solution)/shard_map/ppermute | solution.py:30
  (11 other events, 7.9 us)

commit v3 on v1

v3 whole, which is shorter than its diff:
```python
import math

import jax
import jax.numpy as jnp
from jax import lax
from jax.sharding import Mesh
from jax.sharding import PartitionSpec as P

COLS = 8192

coef_a = 3.4445
coef_b = -4.775
coef_c = 2.0315

ROW = ("x", "zl", "core")
COL = ("zh", "y")
BF, F32 = jnp.bfloat16, jnp.float32


def swap(array, axis):
    return lax.ppermute(array, axis, [(0, 1), (1, 0)])


def send(array, axis, k):
    return lax.ppermute(array, axis, [(i, (i + k) % 4) for i in range(4)]) if k else array


def around(array, axis):
    got = {k: send(array, axis, (4 - k) % 4) for k in (0, 1, 3, 2)}
    return [got[k] for k in range(4)]


def scatter_sum(pieces, axis):
    got = [send(pieces[k], axis, k).astype(F32) for k in (0, 1, 3, 2)]
    return ((got[0] + got[1]) + (got[2] + got[3])).astype(BF)


def chunks(array):
    return jnp.split(array, 4, axis=0)


def window(parts, first, count):
    rows = parts[0].shape[0]
    ring = jnp.concatenate([*parts, *parts[: count - 1]], axis=0)
    return lax.dynamic_slice_in_dim(ring, first * rows, count * rows, 0)


def matmul(a, b, dims):
    return lax.dot_general(a, b, (dims, ((), ())), preferred_element_type=F32)


def panels_of(block):
    partner = swap(block, "zl")
    return [jnp.concatenate(around(b, "x"), axis=0) for b in (block, partner)]


def apply(gram, panels):
    other = sum(matmul(g[1], panel, ((1,), (0,))) for g, panel in zip(gram, panels))
    mine = sum(matmul(g[0], panel, ((1,), (0,))) for g, panel in zip(gram, panels))
    return mine + swap(other, "core")


def per_device(iterate):
    core, y, zh = (lax.axis_index(a) for a in ("core", "y", "zh"))
    other = swap(iterate, "core")
    panels = panels_of(iterate)
    halves = [*jnp.split(iterate, 2), *jnp.split(other, 2)]
    own = window(halves, lax.rem(y - 2 * core + 4, 4), 4)
    own = [window(chunks(rows), zh, 4) for rows in chunks(own)]
    gram = []
    for panel in panels:
        pieces = [matmul(rows, panel, ((1,), (1,))).astype(BF) for rows in own]
        part = scatter_sum(pieces, "y")
        part = scatter_sum(chunks(part), "zh")
        rows = window(around(part, "zh"), lax.rem(4 - zh, 4), 4)
        ring = around(rows, "y")
        first = lax.rem(2 * core - y + 4, 4)
        gram.append((window(ring, first, 2), window(ring, lax.rem(first + 2, 4), 2)))
    inner = apply(gram, panels)
    mixed = apply(gram, panels_of(inner.astype(BF)))
    mine = iterate.astype(F32)
    return math.sqrt(COLS) * (coef_a * mine + (coef_b * inner + coef_c * mixed))


def solution(mesh):
    fine = Mesh(mesh.devices.reshape(4, 2, 2, 4, 4), (*ROW, *COL))
    placed = P(ROW, COL)
    return jax.shard_map(
        per_device, mesh=fine, in_specs=(placed,), out_specs=placed, check_vma=False
    )
```

time: 176 us -> 153 us (0.87)
  blocking collectives: 97.3 us -> 0 us
  starting transfers between devices: 16.6 us -> 75.5 us
  waiting for transfers between devices: 48.6 us -> 56.4 us
  matrix products: 5.41 us -> 12.1 us
    all_to_all x4 -> x0, blocking collectives: 94.5 us -> none  [the longest x2 47.4 us: gather(): got = lax.all_to_all(copies, axes, 0, 0)]
    ppermute x2 -> x41, starting transfers between devices: 6.62 us -> 75.5 us  [the longest x36 59.6 us: send(): lax.ppermute(array, axis, [(i, (i + k) % 4) for i in range(4)])]
    ppermute x2 -> x41, waiting for transfers between devices: 3.42 us -> 56.4 us  [the longest x36 52.9 us: send(): lax.ppermute(array, axis, [(i, (i + k) % 4) for i in range(4)])]
    all_to_all x2 -> x0, waiting for transfers between devices: 45.2 us -> none  [gather(): got = lax.all_to_all(copies, axes, 0, 0)]
    all_to_all x2 -> x0, starting transfers between devices: 9.94 us -> none  [gather(): got = lax.all_to_all(copies, axes, 0, 0)]
    dot_general x3 -> x16, matrix products: 5.41 us -> 12.1 us  [matmul(): return lax.dot_general(a, b, (dims, ((), ())), preferred_element_type=F32)]
    broadcast_in_dim x4 -> x0, local copies, waits for them, and re-layouts: 4.15 us -> none  [gather(): copies = jnp.broadcast_to(block[None], (n, *block.shape))]
    unnamed x4 -> x35, local copies, waits for them, and re-layouts: 0.05 us -> 3.7 us
  transfers between devices with their start and end apart: 4 -> 41, of which waited for: 4 -> 17; matrix products, arithmetic and copies ran while one was open for 0% -> 9% of each run, Pallas kernels for 0% -> 0%
where the time goes in v3:
time: 153 us
  starting transfers between devices  75.5 us (49%)
  waiting for transfers between devices  56.4 us (37%)
  matrix products  12.1 us (8%)
  local copies, waits for them, and re-layouts  5.57 us (4%)
  other arithmetic  3.01 us (2%)
    ppermute x36, starting transfers between devices, send(): lax.ppermute(array, axis, [(i, (i + k) % 4) for i in range(4)])  59.6 us
    ppermute x36, waiting for transfers between devices, send(): lax.ppermute(array, axis, [(i, (i + k) % 4) for i in range(4)])  52.9 us
    ppermute x5, starting transfers between devices, swap(): return lax.ppermute(array, axis, [(0, 1), (1, 0)])  16 us
    dot_general x16, matrix products, matmul(): return lax.dot_general(a, b, (dims, ((), ())), preferred_element_type=F32)  12.1 us
    unnamed x35, local copies, waits for them, and re-layouts  3.7 us
    ppermute x5, waiting for transfers between devices, swap(): return lax.ppermute(array, axis, [(0, 1), (1, 0)])  3.49 us
  transfers between devices with their start and end apart: 41, of which 17 were waited for; matrix products, arithmetic and copies ran while one was open for 9% of the time, Pallas kernels for 0%

profile of v3, /device:TPU:1, one launch (start us, length us, event | category | flops | bytes accessed | tf_op | source)
XLA Modules:
  0.0 153.1 jit_solution(16375622569648444463)
XLA Ops:
  0.0 3.2 %collective-permute-start = (bf16[256,512]{1,0:T(8,128)(2,1)}, bf16[256,512]{1,0:T(8,128)(2,1)S(1)}, u32[]{:S(2)}, u32[]{:S(2)}) collective-permute-start(bf16[256,512]{1,0:T(8,128)(2,1)} %param.1), channel_id=1, source_target_pairs={{0,16},{16,0},{1,17},{17,1},{2,18},{18,2},{3,19},{19,3},{4,20},{20... | collective-permute-start | bytes 786440 | tf_op jit(solution)/shard_map/ppermute | solution.py:21
  3.2 0.7 collective-permute-start.1
  4.0 0.7 collective-permute-start.3
  4.7 1.0 collective-permute-start.2
  5.7 1.6 %collective-permute-start.16 = (bf16[256,512]{1,0:T(8,128)(2,1)}, bf16[256,512]{1,0:T(8,128)(2,1)S(1)}, u32[]{:S(2)}, u32[]{:S(2)}) collective-permute-start(bf16[256,512]{1,0:T(8,128)(2,1)} %param.1), channel_id=1, source_target_pairs={{0,32},{32,0},{1,33},{33,1},{2,34},{34,2},{3,35},{35,3},{4,36},{36... | collective-permute-start | bytes 786440 | tf_op jit(solution)/shard_map/ppermute | solution.py:21
  7.4 1.0 constant_dynamic-update-slice_fusion.3
  8.4 2.1 %fusion.13 = bf16[512,512]{1,0:T(8,128)(2,1)S(1)} fusion(s32[]{:T(128)S(6)} %select_n.10, bf16[256,512]{1,0:T(8,128)(2,1)} %param.1, bf16[256,512]{1,0:T(8,128)(2,1)S(1)} %collective-permute-done, bf16[128,512]{1,0:T(8,128)(2,1)S(1)} %split.83), kind=kLoop, calls=%fused_computation.30 | loop fusion | flops 2097152 | bytes 1179652 | tf_op jit(solution)/shard_map/concatenate | solution.py:44
  10.4 0.9 collective-permute-done.1
  11.4 6.3 %collective-permute-done.2 = bf16[256,512]{1,0:T(8,128)(2,1)S(1)} collective-permute-done((bf16[256,512]{1,0:T(8,128)(2,1)}, bf16[256,512]{1,0:T(8,128)(2,1)S(1)}, u32[]{:S(2)}, u32[]{:S(2)}) %collective-permute-start.2) | collective-permute-done | bytes 262176 | tf_op jit(solution)/shard_map/ppermute | solution.py:25
  17.8 0.8 collective-permute-done.3
  18.7 0.5 convolution_convert_fusion.6
  19.1 1.4 collective-permute-start.4
  21.0 1.5 %collective-permute-start.5 = (bf16[128,1024]{1,0:T(8,128)(2,1)S(1)}, bf16[128,1024]{1,0:T(8,128)(2,1)S(1)}, u32[]{:S(2)}, u32[]{:S(2)}) collective-permute-start(bf16[128,1024]{1,0:T(8,128)(2,1)S(1)} %convolution_convert_fusion.5), channel_id=1, source_target_pairs={{0,3},{1,0},{2,1},{3,2},{4,7},{5,4},{6,5},{7,6},{8,11},{9,8},{10,9... | collective-permute-start | bytes 786440 | tf_op jit(solution)/shard_map/ppermute | solution.py:25
  22.5 1.0 collective-permute-start.18
  24.3 1.3 collective-permute-start.19
  25.6 9.6 %collective-permute-done.17 = bf16[256,512]{1,0:T(8,128)(2,1)S(1)} collective-permute-done((bf16[256,512]{1,0:T(8,128)(2,1)S(1)}, bf16[256,512]{1,0:T(8,128)(2,1)S(1)}, u32[]{:S(2)}, u32[]{:S(2)}) %collective-permute-start.17) | collective-permute-done | bytes 262176 | tf_op jit(solution)/shard_map/ppermute | solution.py:25
  35.2 1.3 collective-permute-start.6
  36.6 1.2 collective-permute-done.19
  37.8 0.5 convolution_convert_fusion
  38.3 4.6 %collective-permute-done.6 = bf16[128,1024]{1,0:T(8,128)(2,1)S(1)} collective-permute-done((bf16[128,1024]{1,0:T(8,128)(2,1)S(1)}, bf16[128,1024]{1,0:T(8,128)(2,1)S(1)}, u32[]{:S(2)}, u32[]{:S(2)}) %collective-permute-start.6) | collective-permute-done | bytes 262176 | tf_op jit(solution)/shard_map/ppermute | solution.py:25
  43.0 0.5 fusion.6
  43.5 2.8 %collective-permute-start.7 = (bf16[32,1024]{1,0:T(8,128)(2,1)S(1)}, bf16[32,1024]{1,0:T(8,128)(2,1)S(1)}, u32[]{:S(2)}, u32[]{:S(2)}) collective-permute-start(bf16[32,1024]{1,0:T(8,128)(2,1)S(1)} %get-tuple-element.24), channel_id=1, source_target_pairs={{0,4},{4,8},{8,12},{12,0},{1,5},{5,9},{9,13},{13,1},{2,6},{6,10},{... | collective-permute-start | bytes 196616 | tf_op jit(solution)/shard_map/ppermute | solution.py:25
  46.3 5.1 %collective-permute-start.9 = (bf16[32,1024]{1,0:T(8,128)(2,1)S(1)}, bf16[32,1024]{1,0:T(8,128)(2,1)S(1)}, u32[]{:S(2)}, u32[]{:S(2)}) collective-permute-start(bf16[32,1024]{1,0:T(8,128)(2,1)S(1)} %get-tuple-element.25), channel_id=1, source_target_pairs={{0,8},{4,12},{8,0},{12,4},{1,9},{5,13},{9,1},{13,5},{2,10},{6,14},... | collective-permute-start | bytes 196616 | tf_op jit(solution)/shard_map/ppermute | solution.py:25
  51.4 2.4 %collective-permute-start.8 = (bf16[32,1024]{1,0:T(8,128)(2,1)S(1)}, bf16[32,1024]{1,0:T(8,128)(2,1)S(1)}, u32[]{:S(2)}, u32[]{:S(2)}) collective-permute-start(bf16[32,1024]{1,0:T(8,128)(2,1)S(1)} %get-tuple-element.26), channel_id=1, source_target_pairs={{0,12},{4,0},{8,4},{12,8},{1,13},{5,1},{9,5},{13,9},{2,14},{6,2},{... | collective-permute-start | bytes 196616 | tf_op jit(solution)/shard_map/ppermute | solution.py:25
  54.3 1.9 %collective-permute-done.8 = bf16[32,1024]{1,0:T(8,128)(2,1)S(1)} collective-permute-done((bf16[32,1024]{1,0:T(8,128)(2,1)S(1)}, bf16[32,1024]{1,0:T(8,128)(2,1)S(1)}, u32[]{:S(2)}, u32[]{:S(2)}) %collective-permute-start.8) | collective-permute-done | bytes 65568 | tf_op jit(solution)/shard_map/ppermute | solution.py:25
  56.2 5.0 %collective-permute-start.10 = (bf16[32,1024]{1,0:T(8,128)(2,1)S(1)}, bf16[32,1024]{1,0:T(8,128)(2,1)S(1)}, u32[]{:S(2)}, u32[]{:S(2)}) collective-permute-start(bf16[32,1024]{1,0:T(8,128)(2,1)S(1)} %get-tuple-element.12), channel_id=1, source_target_pairs={{0,12},{4,0},{8,4},{12,8},{1,13},{5,1},{9,5},{13,9},{2,14},{6,2},{... | collective-permute-start | bytes 196616 | tf_op jit(solution)/shard_map/ppermute | solution.py:25
  61.8 2.7 %collective-permute-start.21 = (bf16[128,1024]{1,0:T(8,128)(2,1)S(1)}, bf16[128,1024]{1,0:T(8,128)(2,1)S(1)}, u32[]{:S(2)}, u32[]{:S(2)}) collective-permute-start(bf16[128,1024]{1,0:T(8,128)(2,1)S(1)} %convolution_convert_fusion.1), channel_id=1, source_target_pairs={{0,3},{1,0},{2,1},{3,2},{4,7},{5,4},{6,5},{7,6},{8,11},{9,8},{10,9... | collective-permute-start | bytes 786440 | tf_op jit(solution)/shard_map/ppermute | solution.py:25
  64.9 2.1 %collective-permute-start.11 = (bf16[32,1024]{1,0:T(8,128)(2,1)S(1)}, bf16[32,1024]{1,0:T(8,128)(2,1)S(1)}, u32[]{:S(2)}, u32[]{:S(2)}) collective-permute-start(bf16[32,1024]{1,0:T(8,128)(2,1)S(1)} %get-tuple-element.12), channel_id=1, source_target_pairs={{0,8},{4,12},{8,0},{12,4},{1,9},{5,13},{9,1},{13,5},{2,10},{6,14},... | collective-permute-start | bytes 196616 | tf_op jit(solution)/shard_map/ppermute | solution.py:25
  67.0 5.4 %collective-permute-done.11 = bf16[32,1024]{1,0:T(8,128)(2,1)S(1)} collective-permute-done((bf16[32,1024]{1,0:T(8,128)(2,1)S(1)}, bf16[32,1024]{1,0:T(8,128)(2,1)S(1)}, u32[]{:S(2)}, u32[]{:S(2)}) %collective-permute-start.11) | collective-permute-done | bytes 65568 | tf_op jit(solution)/shard_map/ppermute | solution.py:25
  72.5 1.8 %collective-permute-done.22 = bf16[128,1024]{1,0:T(8,128)(2,1)S(1)} collective-permute-done((bf16[128,1024]{1,0:T(8,128)(2,1)S(1)}, bf16[128,1024]{1,0:T(8,128)(2,1)S(1)}, u32[]{:S(2)}, u32[]{:S(2)}) %collective-permute-start.22) | collective-permute-done | bytes 262176 | tf_op jit(solution)/shard_map/ppermute | solution.py:25
  74.3 0.5 fusion.10
  74.8 0.7 fusion.52
  75.5 4.2 %collective-permute-start.25 = (bf16[32,1024]{1,0:T(8,128)(2,1)}, bf16[32,1024]{1,0:T(8,128)(2,1)S(1)}, u32[]{:S(2)}, u32[]{:S(2)}) collective-permute-start(bf16[32,1024]{1,0:T(8,128)(2,1)} %get-tuple-element.22), channel_id=1, source_target_pairs={{0,8},{4,12},{8,0},{12,4},{1,9},{5,13},{9,1},{13,5},{2,10},{6,14},... | collective-permute-start | bytes 196616 | tf_op jit(solution)/shard_map/ppermute | solution.py:25
  79.8 0.8 constant_dynamic-update-slice_fusion.15
  80.5 0.7 collective-permute-start.13
  81.3 0.7 collective-permute-start.15
  82.0 2.5 %collective-permute-start.14 = (bf16[128,1024]{1,0:T(8,128)(2,1)}, bf16[128,1024]{1,0:T(8,128)(2,1)S(1)}, u32[]{:S(2)}, u32[]{:S(2)}) collective-permute-start(bf16[128,1024]{1,0:T(8,128)(2,1)} %get-tuple-element.10), channel_id=1, source_target_pairs={{0,2},{1,3},{2,0},{3,1},{4,6},{5,7},{6,4},{7,5},{8,10},{9,11},{10,... | collective-permute-start | bytes 786440 | tf_op jit(solution)/shard_map/ppermute | solution.py:25
  84.5 0.9 constant_dynamic-update-slice_fusion.26
  85.4 2.4 %collective-permute-start.28 = (bf16[32,1024]{1,0:T(8,128)(2,1)S(1)}, bf16[32,1024]{1,0:T(8,128)(2,1)S(1)}, u32[]{:S(2)}, u32[]{:S(2)}) collective-permute-start(bf16[32,1024]{1,0:T(8,128)(2,1)S(1)} %get-tuple-element.8), channel_id=1, source_target_pairs={{0,4},{4,8},{8,12},{12,0},{1,5},{5,9},{9,13},{13,1},{2,6},{6,10},{... | collective-permute-start | bytes 196616 | tf_op jit(solution)/shard_map/ppermute | solution.py:25
  87.9 1.9 %collective-permute-start.27 = (bf16[32,1024]{1,0:T(8,128)(2,1)S(1)}, bf16[32,1024]{1,0:T(8,128)(2,1)S(1)}, u32[]{:S(2)}, u32[]{:S(2)}) collective-permute-start(bf16[32,1024]{1,0:T(8,128)(2,1)S(1)} %get-tuple-element.8), channel_id=1, source_target_pairs={{0,8},{4,12},{8,0},{12,4},{1,9},{5,13},{9,1},{13,5},{2,10},{6,14},... | collective-permute-start | bytes 196616 | tf_op jit(solution)/shard_map/ppermute | solution.py:25
  89.8 2.7 %collective-permute-start.26 = (bf16[32,1024]{1,0:T(8,128)(2,1)S(1)}, bf16[32,1024]{1,0:T(8,128)(2,1)S(1)}, u32[]{:S(2)}, u32[]{:S(2)}) collective-permute-start(bf16[32,1024]{1,0:T(8,128)(2,1)S(1)} %get-tuple-element.8), channel_id=1, source_target_pairs={{0,12},{4,0},{8,4},{12,8},{1,13},{5,1},{9,5},{13,9},{2,14},{6,2},{... | collective-permute-start | bytes 196616 | tf_op jit(solution)/shard_map/ppermute | solution.py:25
  92.4 1.0 constant_dynamic-update-slice_fusion.14
  93.5 1.0 constant_dynamic-update-slice_fusion.11
  94.9 0.6 copy-done.1
  95.6 1.6 %collective-permute-start.31 = (bf16[128,1024]{1,0:T(8,128)(2,1)S(1)}, bf16[128,1024]{1,0:T(8,128)(2,1)S(1)}, u32[]{:S(2)}, u32[]{:S(2)}) collective-permute-start(bf16[128,1024]{1,0:T(8,128)(2,1)S(1)} %get-tuple-element.6), channel_id=1, source_target_pairs={{0,1},{1,2},{2,3},{3,0},{4,5},{5,6},{6,7},{7,4},{8,9},{9,10},{10,1... | collective-permute-start | bytes 786440 | tf_op jit(solution)/shard_map/ppermute | solution.py:25
  97.2 1.2 collective-permute-start.30
  98.4 1.4 collective-permute-start.29
  99.8 1.5 fusion.18
  101.3 4.5 %collective-permute-done.29 = bf16[128,1024]{1,0:T(8,128)(2,1)S(1)} collective-permute-done((bf16[128,1024]{1,0:T(8,128)(2,1)S(1)}, bf16[128,1024]{1,0:T(8,128)(2,1)S(1)}, u32[]{:S(2)}, u32[]{:S(2)}) %collective-permute-start.29) | collective-permute-done | bytes 262176 | tf_op jit(solution)/shard_map/ppermute | solution.py:25
  105.9 1.2 convolution_add_fusion.2
  107.1 9.4 %collective-permute-start.32 = (f32[256,512]{1,0:T(8,128)}, f32[256,512]{1,0:T(8,128)}, u32[]{:S(2)}, u32[]{:S(2)}) collective-permute-start(f32[256,512]{1,0:T(8,128)} %convolution_add_fusion.2), channel_id=1, source_target_pairs={{0,16},{16,0},{1,17},{17,1},{2,18},{18,2},{3,19},{19,3},{4,20},{20... | collective-permute-start | bytes 1572872 | tf_op jit(solution)/shard_map/ppermute | solution.py:21
  116.5 1.5 fusion.26
  118.4 1.5 fusion.54
  120.0 2.7 %collective-permute-start.35 = (bf16[256,512]{1,0:T(8,128)(2,1)S(1)}, bf16[256,512]{1,0:T(8,128)(2,1)S(1)}, u32[]{:S(2)}, u32[]{:S(2)}) collective-permute-start(bf16[256,512]{1,0:T(8,128)(2,1)S(1)} %get-tuple-element.27), channel_id=1, source_target_pairs={{0,64},{64,128},{128,192},{192,0},{1,65},{65,129},{129,193},{193,1... | collective-permute-start | bytes 786440 | tf_op jit(solution)/shard_map/ppermute | solution.py:25
  122.7 2.8 %collective-permute-start.34 = (bf16[256,512]{1,0:T(8,128)(2,1)S(1)}, bf16[256,512]{1,0:T(8,128)(2,1)S(1)}, u32[]{:S(2)}, u32[]{:S(2)}) collective-permute-start(bf16[256,512]{1,0:T(8,128)(2,1)S(1)} %get-tuple-element.27), channel_id=1, source_target_pairs={{0,128},{64,192},{128,0},{192,64},{1,129},{65,193},{129,1},{193,65... | collective-permute-start | bytes 786440 | tf_op jit(solution)/shard_map/ppermute | solution.py:25
  125.5 2.0 %collective-permute-done.36 = bf16[256,512]{1,0:T(8,128)(2,1)S(1)} collective-permute-done((bf16[256,512]{1,0:T(8,128)(2,1)S(1)}, bf16[256,512]{1,0:T(8,128)(2,1)S(1)}, u32[]{:S(2)}, u32[]{:S(2)}) %collective-permute-start.36) | collective-permute-done | bytes 262176 | tf_op jit(solution)/shard_map/ppermute | solution.py:21
  127.5 3.6 %collective-permute-start.37 = (bf16[256,512]{1,0:T(8,128)(2,1)S(1)}, bf16[256,512]{1,0:T(8,128)(2,1)S(1)}, u32[]{:S(2)}, u32[]{:S(2)}) collective-permute-start(bf16[256,512]{1,0:T(8,128)(2,1)S(1)} %collective-permute-done.36), channel_id=1, source_target_pairs={{0,192},{64,0},{128,64},{192,128},{1,193},{65,1},{129,65},{193,129... | collective-permute-start | bytes 786440 | tf_op jit(solution)/shard_map/ppermute | solution.py:25
  131.1 1.2 collective-permute-start.38
  132.3 4.6 %collective-permute-done.34 = bf16[256,512]{1,0:T(8,128)(2,1)S(1)} collective-permute-done((bf16[256,512]{1,0:T(8,128)(2,1)S(1)}, bf16[256,512]{1,0:T(8,128)(2,1)S(1)}, u32[]{:S(2)}, u32[]{:S(2)}) %collective-permute-start.34) | collective-permute-done | bytes 262176 | tf_op jit(solution)/shard_map/ppermute | solution.py:25
  137.4 5.0 %collective-permute-done.37 = bf16[256,512]{1,0:T(8,128)(2,1)S(1)} collective-permute-done((bf16[256,512]{1,0:T(8,128)(2,1)S(1)}, bf16[256,512]{1,0:T(8,128)(2,1)S(1)}, u32[]{:S(2)}, u32[]{:S(2)}) %collective-permute-start.37) | collective-permute-done | bytes 262176 | tf_op jit(solution)/shard_map/ppermute | solution.py:25
  142.4 5.7 %collective-permute-done.38 = bf16[256,512]{1,0:T(8,128)(2,1)S(1)} collective-permute-done((bf16[256,512]{1,0:T(8,128)(2,1)S(1)}, bf16[256,512]{1,0:T(8,128)(2,1)S(1)}, u32[]{:S(2)}, u32[]{:S(2)}) %collective-permute-start.38) | collective-permute-done | bytes 262176 | tf_op jit(solution)/shard_map/ppermute | solution.py:25
  148.7 1.6 %collective-permute-start.40 = (f32[256,512]{1,0:T(8,128)S(1)}, f32[256,512]{1,0:T(8,128)S(1)}, u32[]{:S(2)}, u32[]{:S(2)}) collective-permute-start(f32[256,512]{1,0:T(8,128)S(1)} %convolution_add_fusion), channel_id=1, source_target_pairs={{0,16},{16,0},{1,17},{17,1},{2,18},{18,2},{3,19},{19,3},{4,20},{20... | collective-permute-start | bytes 1572872 | tf_op jit(solution)/shard_map/ppermute | solution.py:21
  150.7 1.1 collective-permute-done.40
  151.8 1.3 add_multiply_fusion
  (84 shorter events, 5.4 us)
Async XLA Ops:
  0.0 8.4 %collective-permute-start = (bf16[256,512]{1,0:T(8,128)(2,1)}, bf16[256,512]{1,0:T(8,128)(2,1)S(1)}, u32[]{:S(2)}, u32[]{:S(2)}) collective-permute-start(bf16[256,512]{1,0:T(8,128)(2,1)} %param.1), channel_id=1, source_target_pairs={{0,16},{16,0},{1,17},{17,1},{2,18},{18,2},{3,19},{19,3},{4,20},{20... | collective-permute-start | bytes 786440 | tf_op jit(solution)/shard_map/ppermute | solution.py:21
  3.2 8.1 %collective-permute-start.1 = (bf16[256,512]{1,0:T(8,128)(2,1)}, bf16[256,512]{1,0:T(8,128)(2,1)S(1)}, u32[]{:S(2)}, u32[]{:S(2)}) collective-permute-start(bf16[256,512]{1,0:T(8,128)(2,1)} %param.1), channel_id=1, source_target_pairs={{0,192},{64,0},{128,64},{192,128},{1,193},{65,1},{129,65},{193,129... | collective-permute-start | bytes 786440 | tf_op jit(solution)/shard_map/ppermute | solution.py:25
  4.0 14.7 %collective-permute-start.3 = (bf16[256,512]{1,0:T(8,128)(2,1)}, bf16[256,512]{1,0:T(8,128)(2,1)S(1)}, u32[]{:S(2)}, u32[]{:S(2)}) collective-permute-start(bf16[256,512]{1,0:T(8,128)(2,1)} %param.1), channel_id=1, source_target_pairs={{0,64},{64,128},{128,192},{192,0},{1,65},{65,129},{129,193},{193,1... | collective-permute-start | bytes 786440 | tf_op jit(solution)/shard_map/ppermute | solution.py:25
  4.7 13.0 %collective-permute-start.2 = (bf16[256,512]{1,0:T(8,128)(2,1)}, bf16[256,512]{1,0:T(8,128)(2,1)S(1)}, u32[]{:S(2)}, u32[]{:S(2)}) collective-permute-start(bf16[256,512]{1,0:T(8,128)(2,1)} %param.1), channel_id=1, source_target_pairs={{0,128},{64,192},{128,0},{192,64},{1,129},{65,193},{129,1},{193,65... | collective-permute-start | bytes 786440 | tf_op jit(solution)/shard_map/ppermute | solution.py:25
  5.7 16.8 %collective-permute-start.16 = (bf16[256,512]{1,0:T(8,128)(2,1)}, bf16[256,512]{1,0:T(8,128)(2,1)S(1)}, u32[]{:S(2)}, u32[]{:S(2)}) collective-permute-start(bf16[256,512]{1,0:T(8,128)(2,1)} %param.1), channel_id=1, source_target_pairs={{0,32},{32,0},{1,33},{33,1},{2,34},{34,2},{3,35},{35,3},{4,36},{36... | collective-permute-start | bytes 786440 | tf_op jit(solution)/shard_map/ppermute | solution.py:21
  19.1 19.2 %collective-permute-start.4 = (bf16[128,1024]{1,0:T(8,128)(2,1)S(1)}, bf16[128,1024]{1,0:T(8,128)(2,1)S(1)}, u32[]{:S(2)}, u32[]{:S(2)}) collective-permute-start(bf16[128,1024]{1,0:T(8,128)(2,1)S(1)} %convolution_convert_fusion.6), channel_id=1, source_target_pairs={{0,1},{1,2},{2,3},{3,0},{4,5},{5,6},{6,7},{7,4},{8,9},{9,10},{10,1... | collective-permute-start | bytes 786440 | tf_op jit(solution)/shard_map/ppermute | solution.py:25
  21.0 17.3 %collective-permute-start.5 = (bf16[128,1024]{1,0:T(8,128)(2,1)S(1)}, bf16[128,1024]{1,0:T(8,128)(2,1)S(1)}, u32[]{:S(2)}, u32[]{:S(2)}) collective-permute-start(bf16[128,1024]{1,0:T(8,128)(2,1)S(1)} %convolution_convert_fusion.5), channel_id=1, source_target_pairs={{0,3},{1,0},{2,1},{3,2},{4,7},{5,4},{6,5},{7,6},{8,11},{9,8},{10,9... | collective-permute-start | bytes 786440 | tf_op jit(solution)/shard_map/ppermute | solution.py:25
  22.5 14.1 %collective-permute-start.18 = (bf16[256,512]{1,0:T(8,128)(2,1)S(1)}, bf16[256,512]{1,0:T(8,128)(2,1)S(1)}, u32[]{:S(2)}, u32[]{:S(2)}) collective-permute-start(bf16[256,512]{1,0:T(8,128)(2,1)S(1)} %collective-permute-done.16), channel_id=1, source_target_pairs={{0,128},{64,192},{128,0},{192,64},{1,129},{65,193},{129,1},{193,65... | collective-permute-start | bytes 786440 | tf_op jit(solution)/shard_map/ppermute | solution.py:25
  23.6 11.7 %collective-permute-start.17 = (bf16[256,512]{1,0:T(8,128)(2,1)S(1)}, bf16[256,512]{1,0:T(8,128)(2,1)S(1)}, u32[]{:S(2)}, u32[]{:S(2)}) collective-permute-start(bf16[256,512]{1,0:T(8,128)(2,1)S(1)} %collective-permute-done.16), channel_id=1, source_target_pairs={{0,192},{64,0},{128,64},{192,128},{1,193},{65,1},{129,65},{193,129... | collective-permute-start | bytes 786440 | tf_op jit(solution)/shard_map/ppermute | solution.py:25
  24.3 13.6 %collective-permute-start.19 = (bf16[256,512]{1,0:T(8,128)(2,1)S(1)}, bf16[256,512]{1,0:T(8,128)(2,1)S(1)}, u32[]{:S(2)}, u32[]{:S(2)}) collective-permute-start(bf16[256,512]{1,0:T(8,128)(2,1)S(1)} %collective-permute-done.16), channel_id=1, source_target_pairs={{0,64},{64,128},{128,192},{192,0},{1,65},{65,129},{129,193},{193,1... | collective-permute-start | bytes 786440 | tf_op jit(solution)/shard_map/ppermute | solution.py:25
  35.2 7.7 %collective-permute-start.6 = (bf16[128,1024]{1,0:T(8,128)(2,1)S(1)}, bf16[128,1024]{1,0:T(8,128)(2,1)S(1)}, u32[]{:S(2)}, u32[]{:S(2)}) collective-permute-start(bf16[128,1024]{1,0:T(8,128)(2,1)S(1)} %convolution_convert_fusion.4), channel_id=1, source_target_pairs={{0,2},{1,3},{2,0},{3,1},{4,6},{5,7},{6,4},{7,5},{8,10},{9,11},{10,... | collective-permute-start | bytes 786440 | tf_op jit(solution)/shard_map/ppermute | solution.py:25
  43.5 10.8 %collective-permute-start.7 = (bf16[32,1024]{1,0:T(8,128)(2,1)S(1)}, bf16[32,1024]{1,0:T(8,128)(2,1)S(1)}, u32[]{:S(2)}, u32[]{:S(2)}) collective-permute-start(bf16[32,1024]{1,0:T(8,128)(2,1)S(1)} %get-tuple-element.24), channel_id=1, source_target_pairs={{0,4},{4,8},{8,12},{12,0},{1,5},{5,9},{9,13},{13,1},{2,6},{6,10},{... | collective-permute-start | bytes 196616 | tf_op jit(solution)/shard_map/ppermute | solution.py:25
  46.3 8.0 %collective-permute-start.9 = (bf16[32,1024]{1,0:T(8,128)(2,1)S(1)}, bf16[32,1024]{1,0:T(8,128)(2,1)S(1)}, u32[]{:S(2)}, u32[]{:S(2)}) collective-permute-start(bf16[32,1024]{1,0:T(8,128)(2,1)S(1)} %get-tuple-element.25), channel_id=1, source_target_pairs={{0,8},{4,12},{8,0},{12,4},{1,9},{5,13},{9,1},{13,5},{2,10},{6,14},... | collective-permute-start | bytes 196616 | tf_op jit(solution)/shard_map/ppermute | solution.py:25
  51.4 4.8 %collective-permute-start.8 = (bf16[32,1024]{1,0:T(8,128)(2,1)S(1)}, bf16[32,1024]{1,0:T(8,128)(2,1)S(1)}, u32[]{:S(2)}, u32[]{:S(2)}) collective-permute-start(bf16[32,1024]{1,0:T(8,128)(2,1)S(1)} %get-tuple-element.26), channel_id=1, source_target_pairs={{0,12},{4,0},{8,4},{12,8},{1,13},{5,1},{9,5},{13,9},{2,14},{6,2},{... | collective-permute-start | bytes 196616 | tf_op jit(solution)/shard_map/ppermute | solution.py:25
  56.2 8.7 %collective-permute-start.10 = (bf16[32,1024]{1,0:T(8,128)(2,1)S(1)}, bf16[32,1024]{1,0:T(8,128)(2,1)S(1)}, u32[]{:S(2)}, u32[]{:S(2)}) collective-permute-start(bf16[32,1024]{1,0:T(8,128)(2,1)S(1)} %get-tuple-element.12), channel_id=1, source_target_pairs={{0,12},{4,0},{8,4},{12,8},{1,13},{5,1},{9,5},{13,9},{2,14},{6,2},{... | collective-permute-start | bytes 196616 | tf_op jit(solution)/shard_map/ppermute | solution.py:25
  61.7 10.8 %collective-permute-start.20 = (bf16[128,1024]{1,0:T(8,128)(2,1)S(1)}, bf16[128,1024]{1,0:T(8,128)(2,1)S(1)}, u32[]{:S(2)}, u32[]{:S(2)}) collective-permute-start(bf16[128,1024]{1,0:T(8,128)(2,1)S(1)} %convolution_convert_fusion.2), channel_id=1, source_target_pairs={{0,1},{1,2},{2,3},{3,0},{4,5},{5,6},{6,7},{7,4},{8,9},{9,10},{10,1... | collective-permute-start | bytes 786440 | tf_op jit(solution)/shard_map/ppermute | solution.py:25
  61.8 10.7 %collective-permute-start.21 = (bf16[128,1024]{1,0:T(8,128)(2,1)S(1)}, bf16[128,1024]{1,0:T(8,128)(2,1)S(1)}, u32[]{:S(2)}, u32[]{:S(2)}) collective-permute-start(bf16[128,1024]{1,0:T(8,128)(2,1)S(1)} %convolution_convert_fusion.1), channel_id=1, source_target_pairs={{0,3},{1,0},{2,1},{3,2},{4,7},{5,4},{6,5},{7,6},{8,11},{9,8},{10,9... | collective-permute-start | bytes 786440 | tf_op jit(solution)/shard_map/ppermute | solution.py:25
  64.5 9.8 %collective-permute-start.22 = (bf16[128,1024]{1,0:T(8,128)(2,1)S(1)}, bf16[128,1024]{1,0:T(8,128)(2,1)S(1)}, u32[]{:S(2)}, u32[]{:S(2)}) collective-permute-start(bf16[128,1024]{1,0:T(8,128)(2,1)S(1)} %convolution_convert_fusion), channel_id=1, source_target_pairs={{0,2},{1,3},{2,0},{3,1},{4,6},{5,7},{6,4},{7,5},{8,10},{9,11},{10,... | collective-permute-start | bytes 786440 | tf_op jit(solution)/shard_map/ppermute | solution.py:25
  64.9 7.5 %collective-permute-start.12 = (bf16[32,1024]{1,0:T(8,128)(2,1)S(1)}, bf16[32,1024]{1,0:T(8,128)(2,1)S(1)}, u32[]{:S(2)}, u32[]{:S(2)}) collective-permute-start(bf16[32,1024]{1,0:T(8,128)(2,1)S(1)} %get-tuple-element.12), channel_id=1, source_target_pairs={{0,4},{4,8},{8,12},{12,0},{1,5},{5,9},{9,13},{13,1},{2,6},{6,10},{... | collective-permute-start | bytes 196616 | tf_op jit(solution)/shard_map/ppermute | solution.py:25
  64.9 7.5 %collective-permute-start.11 = (bf16[32,1024]{1,0:T(8,128)(2,1)S(1)}, bf16[32,1024]{1,0:T(8,128)(2,1)S(1)}, u32[]{:S(2)}, u32[]{:S(2)}) collective-permute-start(bf16[32,1024]{1,0:T(8,128)(2,1)S(1)} %get-tuple-element.12), channel_id=1, source_target_pairs={{0,8},{4,12},{8,0},{12,4},{1,9},{5,13},{9,1},{13,5},{2,10},{6,14},... | collective-permute-start | bytes 196616 | tf_op jit(solution)/shard_map/ppermute | solution.py:25
  74.8 4.9 %copy-start.3 = (bf16[128,1024]{1,0:T(8,128)(2,1)}, bf16[128,1024]{1,0:T(8,128)(2,1)S(1)}, u32[]{:S(2)}) copy-start(bf16[128,1024]{1,0:T(8,128)(2,1)S(1)} %fusion.10) | copy-start | bytes 786436
  75.5 6.5 %collective-permute-start.23 = (bf16[32,1024]{1,0:T(8,128)(2,1)}, bf16[32,1024]{1,0:T(8,128)(2,1)S(1)}, u32[]{:S(2)}, u32[]{:S(2)}) collective-permute-start(bf16[32,1024]{1,0:T(8,128)(2,1)} %get-tuple-element.21), channel_id=1, source_target_pairs={{0,4},{4,8},{8,12},{12,0},{1,5},{5,9},{9,13},{13,1},{2,6},{6,10},{... | collective-permute-start | bytes 196616 | tf_op jit(solution)/shard_map/ppermute | solution.py:25
  75.5 9.0 %collective-permute-start.25 = (bf16[32,1024]{1,0:T(8,128)(2,1)}, bf16[32,1024]{1,0:T(8,128)(2,1)S(1)}, u32[]{:S(2)}, u32[]{:S(2)}) collective-permute-start(bf16[32,1024]{1,0:T(8,128)(2,1)} %get-tuple-element.22), channel_id=1, source_target_pairs={{0,8},{4,12},{8,0},{12,4},{1,9},{5,13},{9,1},{13,5},{2,10},{6,14},... | collective-permute-start | bytes 196616 | tf_op jit(solution)/shard_map/ppermute | solution.py:25
  79.8 4.8 %collective-permute-start.24 = (bf16[32,1024]{1,0:T(8,128)(2,1)}, bf16[32,1024]{1,0:T(8,128)(2,1)}, u32[]{:S(2)}, u32[]{:S(2)}) collective-permute-start(bf16[32,1024]{1,0:T(8,128)(2,1)} %get-tuple-element.23), channel_id=1, source_target_pairs={{0,12},{4,0},{8,4},{12,8},{1,13},{5,1},{9,5},{13,9},{2,14},{6,2},{... | collective-permute-start | bytes 196616 | tf_op jit(solution)/shard_map/ppermute | solution.py:25
  80.5 9.2 %collective-permute-start.13 = (bf16[128,1024]{1,0:T(8,128)(2,1)}, bf16[128,1024]{1,0:T(8,128)(2,1)}, u32[]{:S(2)}, u32[]{:S(2)}) collective-permute-start(bf16[128,1024]{1,0:T(8,128)(2,1)} %get-tuple-element.10), channel_id=1, source_target_pairs={{0,3},{1,0},{2,1},{3,2},{4,7},{5,4},{6,5},{7,6},{8,11},{9,8},{10,9... | collective-permute-start | bytes 786440 | tf_op jit(solution)/shard_map/ppermute | solution.py:25
  81.3 12.2 %collective-permute-start.15 = (bf16[128,1024]{1,0:T(8,128)(2,1)}, bf16[128,1024]{1,0:T(8,128)(2,1)S(1)}, u32[]{:S(2)}, u32[]{:S(2)}) collective-permute-start(bf16[128,1024]{1,0:T(8,128)(2,1)} %get-tuple-element.10), channel_id=1, source_target_pairs={{0,1},{1,2},{2,3},{3,0},{4,5},{5,6},{6,7},{7,4},{8,9},{9,10},{10,1... | collective-permute-start | bytes 786440 | tf_op jit(solution)/shard_map/ppermute | solution.py:25
  82.0 11.4 %collective-permute-start.14 = (bf16[128,1024]{1,0:T(8,128)(2,1)}, bf16[128,1024]{1,0:T(8,128)(2,1)S(1)}, u32[]{:S(2)}, u32[]{:S(2)}) collective-permute-start(bf16[128,1024]{1,0:T(8,128)(2,1)} %get-tuple-element.10), channel_id=1, source_target_pairs={{0,2},{1,3},{2,0},{3,1},{4,6},{5,7},{6,4},{7,5},{8,10},{9,11},{10,... | collective-permute-start | bytes 786440 | tf_op jit(solution)/shard_map/ppermute | solution.py:25
  85.4 9.5 %collective-permute-start.28 = (bf16[32,1024]{1,0:T(8,128)(2,1)S(1)}, bf16[32,1024]{1,0:T(8,128)(2,1)S(1)}, u32[]{:S(2)}, u32[]{:S(2)}) collective-permute-start(bf16[32,1024]{1,0:T(8,128)(2,1)S(1)} %get-tuple-element.8), channel_id=1, source_target_pairs={{0,4},{4,8},{8,12},{12,0},{1,5},{5,9},{9,13},{13,1},{2,6},{6,10},{... | collective-permute-start | bytes 196616 | tf_op jit(solution)/shard_map/ppermute | solution.py:25
  87.9 7.0 %collective-permute-start.27 = (bf16[32,1024]{1,0:T(8,128)(2,1)S(1)}, bf16[32,1024]{1,0:T(8,128)(2,1)S(1)}, u32[]{:S(2)}, u32[]{:S(2)}) collective-permute-start(bf16[32,1024]{1,0:T(8,128)(2,1)S(1)} %get-tuple-element.8), channel_id=1, source_target_pairs={{0,8},{4,12},{8,0},{12,4},{1,9},{5,13},{9,1},{13,5},{2,10},{6,14},... | collective-permute-start | bytes 196616 | tf_op jit(solution)/shard_map/ppermute | solution.py:25
  89.8 4.7 %collective-permute-start.26 = (bf16[32,1024]{1,0:T(8,128)(2,1)S(1)}, bf16[32,1024]{1,0:T(8,128)(2,1)S(1)}, u32[]{:S(2)}, u32[]{:S(2)}) collective-permute-start(bf16[32,1024]{1,0:T(8,128)(2,1)S(1)} %get-tuple-element.8), channel_id=1, source_target_pairs={{0,12},{4,0},{8,4},{12,8},{1,13},{5,1},{9,5},{13,9},{2,14},{6,2},{... | collective-permute-start | bytes 196616 | tf_op jit(solution)/shard_map/ppermute | solution.py:25
  94.5 1.1 copy-start.1
  95.6 10.2 %collective-permute-start.31 = (bf16[128,1024]{1,0:T(8,128)(2,1)S(1)}, bf16[128,1024]{1,0:T(8,128)(2,1)S(1)}, u32[]{:S(2)}, u32[]{:S(2)}) collective-permute-start(bf16[128,1024]{1,0:T(8,128)(2,1)S(1)} %get-tuple-element.6), channel_id=1, source_target_pairs={{0,1},{1,2},{2,3},{3,0},{4,5},{5,6},{6,7},{7,4},{8,9},{9,10},{10,1... | collective-permute-start | bytes 786440 | tf_op jit(solution)/shard_map/ppermute | solution.py:25
  97.2 8.6 %collective-permute-start.30 = (bf16[128,1024]{1,0:T(8,128)(2,1)S(1)}, bf16[128,1024]{1,0:T(8,128)(2,1)S(1)}, u32[]{:S(2)}, u32[]{:S(2)}) collective-permute-start(bf16[128,1024]{1,0:T(8,128)(2,1)S(1)} %get-tuple-element.6), channel_id=1, source_target_pairs={{0,2},{1,3},{2,0},{3,1},{4,6},{5,7},{6,4},{7,5},{8,10},{9,11},{10,... | collective-permute-start | bytes 786440 | tf_op jit(solution)/shard_map/ppermute | solution.py:25
  98.4 7.3 %collective-permute-start.29 = (bf16[128,1024]{1,0:T(8,128)(2,1)S(1)}, bf16[128,1024]{1,0:T(8,128)(2,1)S(1)}, u32[]{:S(2)}, u32[]{:S(2)}) collective-permute-start(bf16[128,1024]{1,0:T(8,128)(2,1)S(1)} %get-tuple-element.6), channel_id=1, source_target_pairs={{0,3},{1,0},{2,1},{3,2},{4,7},{5,4},{6,5},{7,6},{8,11},{9,8},{10,9... | collective-permute-start | bytes 786440 | tf_op jit(solution)/shard_map/ppermute | solution.py:25
  107.1 11.3 %collective-permute-start.32 = (f32[256,512]{1,0:T(8,128)}, f32[256,512]{1,0:T(8,128)}, u32[]{:S(2)}, u32[]{:S(2)}) collective-permute-start(f32[256,512]{1,0:T(8,128)} %convolution_add_fusion.2), channel_id=1, source_target_pairs={{0,16},{16,0},{1,17},{17,1},{2,18},{18,2},{3,19},{19,3},{4,20},{20... | collective-permute-start | bytes 1572872 | tf_op jit(solution)/shard_map/ppermute | solution.py:21
  118.0 18.9 %copy-start.2 = (bf16[640,1024]{1,0:T(8,128)(2,1)S(1)}, bf16[640,1024]{1,0:T(8,128)(2,1)}, u32[]{:S(2)}) copy-start(bf16[640,1024]{1,0:T(8,128)(2,1)} %copy-done.1) | copy-start | bytes 3932164
  119.9 7.6 %collective-permute-start.36 = (bf16[256,512]{1,0:T(8,128)(2,1)S(1)}, bf16[256,512]{1,0:T(8,128)(2,1)S(1)}, u32[]{:S(2)}, u32[]{:S(2)}) collective-permute-start(bf16[256,512]{1,0:T(8,128)(2,1)S(1)} %get-tuple-element.27), channel_id=1, source_target_pairs={{0,32},{32,0},{1,33},{33,1},{2,34},{34,2},{3,35},{35,3},{4,36},{36... | collective-permute-start | bytes 786440 | tf_op jit(solution)/shard_map/ppermute | solution.py:21
  120.0 11.1 %collective-permute-start.35 = (bf16[256,512]{1,0:T(8,128)(2,1)S(1)}, bf16[256,512]{1,0:T(8,128)(2,1)S(1)}, u32[]{:S(2)}, u32[]{:S(2)}) collective-permute-start(bf16[256,512]{1,0:T(8,128)(2,1)S(1)} %get-tuple-element.27), channel_id=1, source_target_pairs={{0,64},{64,128},{128,192},{192,0},{1,65},{65,129},{129,193},{193,1... | collective-permute-start | bytes 786440 | tf_op jit(solution)/shard_map/ppermute | solution.py:25
  122.7 14.2 %collective-permute-start.34 = (bf16[256,512]{1,0:T(8,128)(2,1)S(1)}, bf16[256,512]{1,0:T(8,128)(2,1)S(1)}, u32[]{:S(2)}, u32[]{:S(2)}) collective-permute-start(bf16[256,512]{1,0:T(8,128)(2,1)S(1)} %get-tuple-element.27), channel_id=1, source_target_pairs={{0,128},{64,192},{128,0},{192,64},{1,129},{65,193},{129,1},{193,65... | collective-permute-start | bytes 786440 | tf_op jit(solution)/shard_map/ppermute | solution.py:25
  125.5 11.4 %collective-permute-start.33 = (bf16[256,512]{1,0:T(8,128)(2,1)S(1)}, bf16[256,512]{1,0:T(8,128)(2,1)S(1)}, u32[]{:S(2)}, u32[]{:S(2)}) collective-permute-start(bf16[256,512]{1,0:T(8,128)(2,1)S(1)} %get-tuple-element.27), channel_id=1, source_target_pairs={{0,192},{64,0},{128,64},{192,128},{1,193},{65,1},{129,65},{193,129... | collective-permute-start | bytes 786440 | tf_op jit(solution)/shard_map/ppermute | solution.py:25
  127.5 14.9 %collective-permute-start.37 = (bf16[256,512]{1,0:T(8,128)(2,1)S(1)}, bf16[256,512]{1,0:T(8,128)(2,1)S(1)}, u32[]{:S(2)}, u32[]{:S(2)}) collective-permute-start(bf16[256,512]{1,0:T(8,128)(2,1)S(1)} %collective-permute-done.36), channel_id=1, source_target_pairs={{0,192},{64,0},{128,64},{192,128},{1,193},{65,1},{129,65},{193,129... | collective-permute-start | bytes 786440 | tf_op jit(solution)/shard_map/ppermute | solution.py:25
  131.1 17.1 %collective-permute-start.39 = (bf16[256,512]{1,0:T(8,128)(2,1)S(1)}, bf16[256,512]{1,0:T(8,128)(2,1)S(1)}, u32[]{:S(2)}, u32[]{:S(2)}) collective-permute-start(bf16[256,512]{1,0:T(8,128)(2,1)S(1)} %collective-permute-done.36), channel_id=1, source_target_pairs={{0,64},{64,128},{128,192},{192,0},{1,65},{65,129},{129,193},{193,1... | collective-permute-start | bytes 786440 | tf_op jit(solution)/shard_map/ppermute | solution.py:25
  131.1 17.0 %collective-permute-start.38 = (bf16[256,512]{1,0:T(8,128)(2,1)S(1)}, bf16[256,512]{1,0:T(8,128)(2,1)S(1)}, u32[]{:S(2)}, u32[]{:S(2)}) collective-permute-start(bf16[256,512]{1,0:T(8,128)(2,1)S(1)} %collective-permute-done.36), channel_id=1, source_target_pairs={{0,128},{64,192},{128,0},{192,64},{1,129},{65,193},{129,1},{193,65... | collective-permute-start | bytes 786440 | tf_op jit(solution)/shard_map/ppermute | solution.py:25
  148.7 3.2 %copy-start = (bf16[256,512]{1,0:T(8,128)(2,1)S(1)}, bf16[256,512]{1,0:T(8,128)(2,1)}, u32[]{:S(2)}) copy-start(bf16[256,512]{1,0:T(8,128)(2,1)} %param.1) | copy-start | bytes 786436
  148.7 3.1 %collective-permute-start.40 = (f32[256,512]{1,0:T(8,128)S(1)}, f32[256,512]{1,0:T(8,128)S(1)}, u32[]{:S(2)}, u32[]{:S(2)}) collective-permute-start(f32[256,512]{1,0:T(8,128)S(1)} %convolution_add_fusion), channel_id=1, source_target_pairs={{0,16},{16,0},{1,17},{17,1},{2,18},{18,2},{3,19},{19,3},{4,20},{20... | collective-permute-start | bytes 1572872 | tf_op jit(solution)/shard_map/ppermute | solution.py:21

commit v4 on v3

--- a/solution.py
+++ b/solution.py
@@ -30,9 +30,17 @@
     return [got[k] for k in range(4)]
 
 
+def add(got):
+    got = [g.astype(F32) for g in got]
+    return ((got[0] + got[1]) + (got[2] + got[3])).astype(BF)
+
+
 def scatter_sum(pieces, axis):
-    got = [send(pieces[k], axis, k).astype(F32) for k in (0, 1, 3, 2)]
-    return ((got[0] + got[1]) + (got[2] + got[3])).astype(BF)
+    return add([send(pieces[k], axis, k) for k in range(4)])
+
+
+def exchange(pieces, axis):
+    return lax.all_to_all(pieces, axis, 0, 0)
 
 
 def chunks(array):
@@ -54,30 +62,29 @@
     return [jnp.concatenate(around(b, "x"), axis=0) for b in (block, partner)]
 
 
-def apply(gram, panels):
-    other = sum(matmul(g[1], panel, ((1,), (0,))) for g, panel in zip(gram, panels))
-    mine = sum(matmul(g[0], panel, ((1,), (0,))) for g, panel in zip(gram, panels))
+def apply(core, gram, panels):
+    product = sum(matmul(g, panel, ((1,), (0,))) for g, panel in zip(gram, panels))
+    mine = lax.dynamic_slice_in_dim(product, core * 256, 256, 0)
+    other = lax.dynamic_slice_in_dim(product, (1 - core) * 256, 256, 0)
     return mine + swap(other, "core")
 
 
 def per_device(iterate):
-    core, y, zh = (lax.axis_index(a) for a in ("core", "y", "zh"))
+    core, zh = lax.axis_index("core"), lax.axis_index("zh")
     other = swap(iterate, "core")
     panels = panels_of(iterate)
-    halves = [*jnp.split(iterate, 2), *jnp.split(other, 2)]
-    own = window(halves, lax.rem(y - 2 * core + 4, 4), 4)
-    own = [window(chunks(rows), zh, 4) for rows in chunks(own)]
+    own = window([iterate, other, iterate, other], core, 2)
+    own = jnp.concatenate([window(chunks(rows), zh, 4) for rows in chunks(own)], axis=0)
     gram = []
     for panel in panels:
-        pieces = [matmul(rows, panel, ((1,), (1,))).astype(BF) for rows in own]
-        part = scatter_sum(pieces, "y")
+        pieces = matmul(own, panel, ((1,), (1,))).astype(BF)
+        part = add(exchange(pieces.reshape(4, 128, 1024), "y"))
         part = scatter_sum(chunks(part), "zh")
         rows = window(around(part, "zh"), lax.rem(4 - zh, 4), 4)
-        ring = around(rows, "y")
-        first = lax.rem(2 * core - y + 4, 4)
-        gram.append((window(ring, first, 2), window(ring, lax.rem(first + 2, 4), 2)))
-    inner = apply(gram, panels)
-    mixed = apply(gram, panels_of(inner.astype(BF)))
+        copies = jnp.broadcast_to(rows[None], (4, 128, 1024))
+        gram.append(exchange(copies, "y").reshape(512, 1024))
+    inner = apply(core, gram, panels)
+    mixed = apply(core, gram, panels_of(inner.astype(BF)))
     mine = iterate.astype(F32)
     return math.sqrt(COLS) * (coef_a * mine + (coef_b * inner + coef_c * mixed))
 

time: 153 us -> 157 us (1.026)
  waiting for transfers between devices: 56.4 us -> 79.6 us
  starting transfers between devices: 75.5 us -> 60.6 us
  matrix products: 12.1 us -> 9.73 us
    ppermute x36 -> x24, starting transfers between devices: 59.6 us -> 32.8 us  [send(): lax.ppermute(array, axis, [(i, (i + k) % 4) for i in range(4)])]
    all_to_all x0 -> x4, starting transfers between devices: none -> 15.4 us  [exchange(): return lax.all_to_all(pieces, axis, 0, 0)]
    all_to_all x0 -> x4, waiting for transfers between devices: none -> 12.4 us  [exchange(): return lax.all_to_all(pieces, axis, 0, 0)]
    ppermute x36 -> x24, waiting for transfers between devices: 52.9 us -> 59.4 us  [send(): lax.ppermute(array, axis, [(i, (i + k) % 4) for i in range(4)])]
    ppermute x5, waiting for transfers between devices: 3.49 us -> 7.71 us  [swap(): return lax.ppermute(array, axis, [(0, 1), (1, 0)])]
    ppermute x5, starting transfers between devices: 16 us -> 12.5 us  [swap(): return lax.ppermute(array, axis, [(0, 1), (1, 0)])]
    broadcast_in_dim x0 -> x2, local copies, waits for them, and re-layouts: none -> 2.37 us  [per_device(): copies = jnp.broadcast_to(rows[None], (4, 128, 1024))]
    dot_general x16 -> x6, matrix products: 12.1 us -> 9.73 us  [matmul(): return lax.dot_general(a, b, (dims, ((), ())), preferred_element_type=F32)]
  transfers between devices with their start and end apart: 41 -> 33, of which waited for: 17 -> 25; matrix products, arithmetic and copies ran while one was open for 9% -> 7% of each run, Pallas kernels for 0% -> 0%
where the time goes in v4:
time: 157 us
  waiting for transfers between devices  79.6 us (51%)
  starting transfers between devices  60.6 us (39%)
  matrix products  9.73 us (6%)
  local copies, waits for them, and re-layouts  4.88 us (3%)
  other arithmetic  1.86 us (1%)
    ppermute x24, waiting for transfers between devices, send(): lax.ppermute(array, axis, [(i, (i + k) % 4) for i in range(4)])  59.4 us
    ppermute x24, starting transfers between devices, send(): lax.ppermute(array, axis, [(i, (i + k) % 4) for i in range(4)])  32.8 us
    all_to_all x4, starting transfers between devices, exchange(): return lax.all_to_all(pieces, axis, 0, 0)  15.4 us
    ppermute x5, starting transfers between devices, swap(): return lax.ppermute(array, axis, [(0, 1), (1, 0)])  12.5 us
    all_to_all x4, waiting for transfers between devices, exchange(): return lax.all_to_all(pieces, axis, 0, 0)  12.4 us
    dot_general x6, matrix products, matmul(): return lax.dot_general(a, b, (dims, ((), ())), preferred_element_type=F32)  9.73 us
    ppermute x5, waiting for transfers between devices, swap(): return lax.ppermute(array, axis, [(0, 1), (1, 0)])  7.71 us
  transfers between devices with their start and end apart: 33, of which 25 were waited for; matrix products, arithmetic and copies ran while one was open for 7% of the time, Pallas kernels for 0%

profile of v4, /device:TPU:1, one launch (start us, length us, event | category | flops | bytes accessed | tf_op | source)
XLA Modules:
  0.0 157.0 jit_solution(11339956350632303335)
XLA Ops:
  0.0 3.2 %collective-permute-start = (bf16[256,512]{1,0:T(8,128)(2,1)}, bf16[256,512]{1,0:T(8,128)(2,1)S(1)}, u32[]{:S(2)}, u32[]{:S(2)}) collective-permute-start(bf16[256,512]{1,0:T(8,128)(2,1)} %param.1), channel_id=1, source_target_pairs={{0,16},{16,0},{1,17},{17,1},{2,18},{18,2},{3,19},{19,3},{4,20},{20... | collective-permute-start | bytes 786440 | tf_op jit(solution)/shard_map/ppermute | solution.py:21
  3.2 2.4 %collective-permute-start.1 = (bf16[256,512]{1,0:T(8,128)(2,1)}, bf16[256,512]{1,0:T(8,128)(2,1)S(1)}, u32[]{:S(2)}, u32[]{:S(2)}) collective-permute-start(bf16[256,512]{1,0:T(8,128)(2,1)} %param.1), channel_id=1, source_target_pairs={{0,192},{64,0},{128,64},{192,128},{1,193},{65,1},{129,65},{193,129... | collective-permute-start | bytes 786440 | tf_op jit(solution)/shard_map/ppermute | solution.py:25
  5.6 0.5 collective-permute-start.2
  6.2 0.6 collective-permute-start.3
  6.8 1.0 constant_dynamic-update-slice_fusion.4
  7.8 1.0 constant_dynamic-update-slice_fusion.2
  9.3 2.6 %collective-permute-done.1 = bf16[256,512]{1,0:T(8,128)(2,1)S(1)} collective-permute-done((bf16[256,512]{1,0:T(8,128)(2,1)}, bf16[256,512]{1,0:T(8,128)(2,1)S(1)}, u32[]{:S(2)}, u32[]{:S(2)}) %collective-permute-start.1) | collective-permute-done | bytes 262176 | tf_op jit(solution)/shard_map/ppermute | solution.py:25
  11.9 2.8 %collective-permute-done.2 = bf16[256,512]{1,0:T(8,128)(2,1)S(1)} collective-permute-done((bf16[256,512]{1,0:T(8,128)(2,1)}, bf16[256,512]{1,0:T(8,128)(2,1)S(1)}, u32[]{:S(2)}, u32[]{:S(2)}) %collective-permute-start.2) | collective-permute-done | bytes 262176 | tf_op jit(solution)/shard_map/ppermute | solution.py:25
  14.6 6.6 %collective-permute-done.3 = bf16[256,512]{1,0:T(8,128)(2,1)S(1)} collective-permute-done((bf16[256,512]{1,0:T(8,128)(2,1)}, bf16[256,512]{1,0:T(8,128)(2,1)S(1)}, u32[]{:S(2)}, u32[]{:S(2)}) %collective-permute-start.3) | collective-permute-done | bytes 262176 | tf_op jit(solution)/shard_map/ppermute | solution.py:25
  21.2 1.7 %convolution_convert_fusion.1 = bf16[512,1024]{1,0:T(8,128)(2,1)} fusion(bf16[1024,512]{1,0:T(8,128)(2,1)S(1)} %constant_dynamic-update-slice_fusion.5, bf16[128,512]{1,0:T(8,128)(2,1)S(1)} %get-tuple-element.25, bf16[128,512]{1,0:T(8,128)(2,1)S(1)} %get-tuple-element.26, bf16[128,512]{1,0:T(8,128)(2,1)S(1)} %get-tuple-element.27, ...), kind=kOutput, calls=%fused_computation.1 | convolution fusion | flops 539492352 | bytes 2621440 | tf_op jit(solution)/shard_map/dot_general | solution.py:57
  23.0 4.2 %all-to-all-start = ((bf16[4,128,1024]{2,1,0:T(8,128)(2,1)}), bf16[4,128,1024]{2,1,0:T(8,128)(2,1)S(1)}, u32[]{:S(2)}, u32[]{:S(2)}) async-start(bf16[4,128,1024]{2,1,0:T(8,128)(2,1)} %bitcast), calls=%async_computation | async-start | bytes 2097152 | tf_op jit(solution)/shard_map/all_to_all | solution.py:43
  27.2 0.6 collective-permute-start.12
  27.8 0.9 collective-permute-start.13
  28.7 5.6 %collective-permute-done.11 = bf16[256,512]{1,0:T(8,128)(2,1)S(1)} collective-permute-done((bf16[256,512]{1,0:T(8,128)(2,1)S(1)}, bf16[256,512]{1,0:T(8,128)(2,1)S(1)}, u32[]{:S(2)}, u32[]{:S(2)}) %collective-permute-start.11) | collective-permute-done | bytes 262176 | tf_op jit(solution)/shard_map/ppermute | solution.py:25
  34.3 1.1 collective-permute-done.12
  35.3 7.3 %collective-permute-done.13 = bf16[256,512]{1,0:T(8,128)(2,1)S(1)} collective-permute-done((bf16[256,512]{1,0:T(8,128)(2,1)S(1)}, bf16[256,512]{1,0:T(8,128)(2,1)S(1)}, u32[]{:S(2)}, u32[]{:S(2)}) %collective-permute-start.13) | collective-permute-done | bytes 262176 | tf_op jit(solution)/shard_map/ppermute | solution.py:25
  42.8 3.1 %collective-permute-start.4 = (bf16[32,1024]{1,0:T(8,128)(2,1)S(1)}, bf16[32,1024]{1,0:T(8,128)(2,1)S(1)}, u32[]{:S(2)}, u32[]{:S(2)}) collective-permute-start(bf16[32,1024]{1,0:T(8,128)(2,1)S(1)} %get-tuple-element.20), channel_id=1, source_target_pairs={{0,4},{4,8},{8,12},{12,0},{1,5},{5,9},{9,13},{13,1},{2,6},{6,10},{... | collective-permute-start | bytes 196616 | tf_op jit(solution)/shard_map/ppermute | solution.py:25
  45.9 4.2 %collective-permute-start.5 = (bf16[32,1024]{1,0:T(8,128)(2,1)S(1)}, bf16[32,1024]{1,0:T(8,128)(2,1)S(1)}, u32[]{:S(2)}, u32[]{:S(2)}) collective-permute-start(bf16[32,1024]{1,0:T(8,128)(2,1)S(1)} %get-tuple-element.22), channel_id=1, source_target_pairs={{0,8},{4,12},{8,0},{12,4},{1,9},{5,13},{9,1},{13,5},{2,10},{6,14},... | collective-permute-start | bytes 196616 | tf_op jit(solution)/shard_map/ppermute | solution.py:25
  50.1 2.4 %collective-permute-start.6 = (bf16[32,1024]{1,0:T(8,128)(2,1)S(1)}, bf16[32,1024]{1,0:T(8,128)(2,1)S(1)}, u32[]{:S(2)}, u32[]{:S(2)}) collective-permute-start(bf16[32,1024]{1,0:T(8,128)(2,1)S(1)} %get-tuple-element.21), channel_id=1, source_target_pairs={{0,12},{4,0},{8,4},{12,8},{1,13},{5,1},{9,5},{13,9},{2,14},{6,2},{... | collective-permute-start | bytes 196616 | tf_op jit(solution)/shard_map/ppermute | solution.py:25
  52.5 1.7 %convolution_convert_fusion = bf16[512,1024]{1,0:T(8,128)(2,1)} fusion(bf16[1024,512]{1,0:T(8,128)(2,1)S(1)} %constant_dynamic-update-slice_fusion.16, bf16[128,512]{1,0:T(8,128)(2,1)S(1)} %get-tuple-element.25, bf16[128,512]{1,0:T(8,128)(2,1)S(1)} %get-tuple-element.26, bf16[128,512]{1,0:T(8,128)(2,1)S(1)} %get-tuple-element.27, ...), kind=kOutput, calls=%fused_computation | convolution fusion | flops 539492352 | bytes 2621440 | tf_op jit(solution)/shard_map/dot_general | solution.py:57
  54.2 4.1 %all-to-all-start.2 = ((bf16[4,128,1024]{2,1,0:T(8,128)(2,1)}), bf16[4,128,1024]{2,1,0:T(8,128)(2,1)S(1)}, u32[]{:S(2)}, u32[]{:S(2)}) async-start(bf16[4,128,1024]{2,1,0:T(8,128)(2,1)} %bitcast.40), calls=%async_computation.2 | async-start | bytes 2097152 | tf_op jit(solution)/shard_map/all_to_all | solution.py:43
  58.5 1.1 collective-permute-start.7
  59.6 2.2 %collective-permute-start.8 = (bf16[32,1024]{1,0:T(8,128)(2,1)S(1)}, bf16[32,1024]{1,0:T(8,128)(2,1)S(1)}, u32[]{:S(2)}, u32[]{:S(2)}) collective-permute-start(bf16[32,1024]{1,0:T(8,128)(2,1)S(1)} %get-tuple-element.8), channel_id=1, source_target_pairs={{0,8},{4,12},{8,0},{12,4},{1,9},{5,13},{9,1},{13,5},{2,10},{6,14},... | collective-permute-start | bytes 196616 | tf_op jit(solution)/shard_map/ppermute | solution.py:25
  61.8 0.9 collective-permute-start.9
  62.7 0.6 collective-permute-done.7
  63.2 3.5 %collective-permute-done.8 = bf16[32,1024]{1,0:T(8,128)(2,1)S(1)} collective-permute-done((bf16[32,1024]{1,0:T(8,128)(2,1)S(1)}, bf16[32,1024]{1,0:T(8,128)(2,1)S(1)}, u32[]{:S(2)}, u32[]{:S(2)}) %collective-permute-start.8) | collective-permute-done | bytes 65568 | tf_op jit(solution)/shard_map/ppermute | solution.py:25
  66.7 0.7 collective-permute-done.9
  67.4 4.5 %all-to-all-done.2 = bf16[4,128,1024]{2,1,0:T(8,128)(2,1)S(1)} async-done(((bf16[4,128,1024]{2,1,0:T(8,128)(2,1)}), bf16[4,128,1024]{2,1,0:T(8,128)(2,1)S(1)}, u32[]{:S(2)}, u32[]{:S(2)}) %all-to-all-start.2) | async-done | bytes 1048608 | tf_op jit(solution)/shard_map/all_to_all | solution.py:43
  72.1 0.3 collective-permute-start.14
  72.4 2.4 %collective-permute-start.15 = (bf16[32,1024]{1,0:T(8,128)(2,1)S(1)}, bf16[32,1024]{1,0:T(8,128)(2,1)S(1)}, u32[]{:S(2)}, u32[]{:S(2)}) collective-permute-start(bf16[32,1024]{1,0:T(8,128)(2,1)S(1)} %get-tuple-element.19), channel_id=1, source_target_pairs={{0,8},{4,12},{8,0},{12,4},{1,9},{5,13},{9,1},{13,5},{2,10},{6,14},... | collective-permute-start | bytes 196616 | tf_op jit(solution)/shard_map/ppermute | solution.py:25
  74.7 2.5 %collective-permute-start.16 = (bf16[32,1024]{1,0:T(8,128)(2,1)S(1)}, bf16[32,1024]{1,0:T(8,128)(2,1)S(1)}, u32[]{:S(2)}, u32[]{:S(2)}) collective-permute-start(bf16[32,1024]{1,0:T(8,128)(2,1)S(1)} %get-tuple-element.18), channel_id=1, source_target_pairs={{0,12},{4,0},{8,4},{12,8},{1,13},{5,1},{9,5},{13,9},{2,14},{6,2},{... | collective-permute-start | bytes 196616 | tf_op jit(solution)/shard_map/ppermute | solution.py:25
  77.2 0.5 collective-permute-done.14
  77.7 2.2 %collective-permute-done.15 = bf16[32,1024]{1,0:T(8,128)(2,1)S(1)} collective-permute-done((bf16[32,1024]{1,0:T(8,128)(2,1)S(1)}, bf16[32,1024]{1,0:T(8,128)(2,1)S(1)}, u32[]{:S(2)}, u32[]{:S(2)}) %collective-permute-start.15) | collective-permute-done | bytes 65568 | tf_op jit(solution)/shard_map/ppermute | solution.py:25
  79.9 2.2 %collective-permute-done.16 = bf16[32,1024]{1,0:T(8,128)(2,1)S(1)} collective-permute-done((bf16[32,1024]{1,0:T(8,128)(2,1)S(1)}, bf16[32,1024]{1,0:T(8,128)(2,1)S(1)}, u32[]{:S(2)}, u32[]{:S(2)}) %collective-permute-start.16) | collective-permute-done | bytes 65568 | tf_op jit(solution)/shard_map/ppermute | solution.py:25
  82.1 1.7 %collective-permute-start.17 = (bf16[32,1024]{1,0:T(8,128)(2,1)S(1)}, bf16[32,1024]{1,0:T(8,128)(2,1)S(1)}, u32[]{:S(2)}, u32[]{:S(2)}) collective-permute-start(bf16[32,1024]{1,0:T(8,128)(2,1)S(1)} %get-tuple-element.6), channel_id=1, source_target_pairs={{0,12},{4,0},{8,4},{12,8},{1,13},{5,1},{9,5},{13,9},{2,14},{6,2},{... | collective-permute-start | bytes 196616 | tf_op jit(solution)/shard_map/ppermute | solution.py:25
  83.8 1.1 broadcast_in_dim.4
  85.0 3.5 %all-to-all-start.1 = ((bf16[4,128,1024]{2,1,0:T(8,128)(2,1)}), bf16[4,128,1024]{2,1,0:T(8,128)(2,1)S(1)}, u32[]{:S(2)}, u32[]{:S(2)}) async-start(bf16[4,128,1024]{2,1,0:T(8,128)(2,1)} %broadcast_in_dim.4), calls=%async_computation.1 | async-start | bytes 2097152 | tf_op jit(solution)/shard_map/all_to_all | solution.py:43
  88.5 3.7 %collective-permute-start.18 = (bf16[32,1024]{1,0:T(8,128)(2,1)S(1)}, bf16[32,1024]{1,0:T(8,128)(2,1)S(1)}, u32[]{:S(2)}, u32[]{:S(2)}) collective-permute-start(bf16[32,1024]{1,0:T(8,128)(2,1)S(1)} %get-tuple-element.6), channel_id=1, source_target_pairs={{0,8},{4,12},{8,0},{12,4},{1,9},{5,13},{9,1},{13,5},{2,10},{6,14},... | collective-permute-start | bytes 196616 | tf_op jit(solution)/shard_map/ppermute | solution.py:25
  92.2 4.2 %collective-permute-done.18 = bf16[32,1024]{1,0:T(8,128)(2,1)S(1)} collective-permute-done((bf16[32,1024]{1,0:T(8,128)(2,1)S(1)}, bf16[32,1024]{1,0:T(8,128)(2,1)S(1)}, u32[]{:S(2)}, u32[]{:S(2)}) %collective-permute-start.18) | collective-permute-done | bytes 65568 | tf_op jit(solution)/shard_map/ppermute | solution.py:25
  96.4 2.1 %collective-permute-done.19 = bf16[32,1024]{1,0:T(8,128)(2,1)S(1)} collective-permute-done((bf16[32,1024]{1,0:T(8,128)(2,1)S(1)}, bf16[32,1024]{1,0:T(8,128)(2,1)S(1)}, u32[]{:S(2)}, u32[]{:S(2)}) %collective-permute-start.19) | collective-permute-done | bytes 65568 | tf_op jit(solution)/shard_map/ppermute | solution.py:25
  98.6 1.0 all-to-all-done.1
  99.6 1.2 broadcast_in_dim.5
  100.8 3.5 %all-to-all-start.3 = ((bf16[4,128,1024]{2,1,0:T(8,128)(2,1)}), bf16[4,128,1024]{2,1,0:T(8,128)(2,1)S(1)}, u32[]{:S(2)}, u32[]{:S(2)}) async-start(bf16[4,128,1024]{2,1,0:T(8,128)(2,1)} %broadcast_in_dim.5), calls=%async_computation.3 | async-start | bytes 2097152 | tf_op jit(solution)/shard_map/all_to_all | solution.py:43
  104.4 2.9 %fusion.30 = f32[512,512]{1,0:T(8,128)} fusion(bf16[512,1024]{1,0:T(8,128)(2,1)S(1)} %bitcast.38, bf16[1024,512]{1,0:T(8,128)(2,1)} %copy-done.3), kind=kOutput, calls=%fused_computation.94 | convolution fusion | flops 536870912 | bytes 3145728 | tf_op jit(solution)/shard_map/dot_general | solution.py:57
  107.3 6.9 %all-to-all-done.3 = bf16[4,128,1024]{2,1,0:T(8,128)(2,1)S(1)} async-done(((bf16[4,128,1024]{2,1,0:T(8,128)(2,1)}), bf16[4,128,1024]{2,1,0:T(8,128)(2,1)S(1)}, u32[]{:S(2)}, u32[]{:S(2)}) %all-to-all-start.3) | async-done | bytes 1048608 | tf_op jit(solution)/shard_map/all_to_all | solution.py:43
  114.2 1.9 %convolution_add_fusion.1 = f32[512,512]{1,0:T(8,128)S(1)} fusion(f32[512,512]{1,0:T(8,128)} %fusion.30, bf16[512,1024]{1,0:T(8,128)(2,1)S(1)} %bitcast.36, bf16[1024,512]{1,0:T(8,128)(2,1)S(1)} %constant_dynamic-update-slice_fusion.16), kind=kOutput, calls=%fused_computation.3 | convolution fusion | flops 537133056 | bytes 4194304 | tf_op jit(solution)/shard_map/dot_general | solution.py:57
  116.2 6.2 %collective-permute-start.20 = (f32[256,512]{1,0:T(8,128)S(1)}, f32[256,512]{1,0:T(8,128)S(1)}, u32[]{:S(2)}, u32[]{:S(2)}) collective-permute-start(f32[256,512]{1,0:T(8,128)S(1)} %constant_dynamic-slice_fusion.6), channel_id=1, source_target_pairs={{0,16},{16,0},{1,17},{17,1},{2,18},{18,2},{3,19},{19,3},{4,20},{20... | collective-permute-start | bytes 1572872 | tf_op jit(solution)/shard_map/ppermute | solution.py:21
  122.4 1.5 collective-permute-done.20
  124.1 2.4 %collective-permute-start.24 = (bf16[256,512]{1,0:T(8,128)(2,1)S(1)}, bf16[256,512]{1,0:T(8,128)(2,1)S(1)}, u32[]{:S(2)}, u32[]{:S(2)}) collective-permute-start(bf16[256,512]{1,0:T(8,128)(2,1)S(1)} %fusion.15), channel_id=1, source_target_pairs={{0,32},{32,0},{1,33},{33,1},{2,34},{34,2},{3,35},{35,3},{4,36},{36... | collective-permute-start | bytes 786440 | tf_op jit(solution)/shard_map/ppermute | solution.py:21
  126.5 0.9 collective-permute-start.22
  127.3 0.9 collective-permute-start.23
  128.2 4.6 %collective-permute-done.24 = bf16[256,512]{1,0:T(8,128)(2,1)S(1)} collective-permute-done((bf16[256,512]{1,0:T(8,128)(2,1)S(1)}, bf16[256,512]{1,0:T(8,128)(2,1)S(1)}, u32[]{:S(2)}, u32[]{:S(2)}) %collective-permute-start.24) | collective-permute-done | bytes 262176 | tf_op jit(solution)/shard_map/ppermute | solution.py:21
  132.8 0.9 collective-permute-start.26
  133.7 0.9 collective-permute-start.27
  134.6 0.6 collective-permute-done.22
  135.2 7.6 %collective-permute-done.23 = bf16[256,512]{1,0:T(8,128)(2,1)S(1)} collective-permute-done((bf16[256,512]{1,0:T(8,128)(2,1)S(1)}, bf16[256,512]{1,0:T(8,128)(2,1)S(1)}, u32[]{:S(2)}, u32[]{:S(2)}) %collective-permute-start.23) | collective-permute-done | bytes 262176 | tf_op jit(solution)/shard_map/ppermute | solution.py:25
  142.8 0.7 fusion
  143.5 1.4 collective-permute-done.25
  144.9 1.6 collective-permute-done.26
  146.5 6.6 %collective-permute-done.27 = bf16[256,512]{1,0:T(8,128)(2,1)S(1)} collective-permute-done((bf16[256,512]{1,0:T(8,128)(2,1)S(1)}, bf16[256,512]{1,0:T(8,128)(2,1)S(1)}, u32[]{:S(2)}, u32[]{:S(2)}) %collective-permute-start.27) | collective-permute-done | bytes 262176 | tf_op jit(solution)/shard_map/ppermute | solution.py:25
  153.0 0.7 convolution_add_fusion
  153.8 0.6 collective-permute-start.28
  154.4 1.5 collective-permute-done.28
  155.9 1.1 add_multiply_fusion
  (58 shorter events, 1.4 us)
Async XLA Ops:
  0.0 8.8 %copy-start = (bf16[256,512]{1,0:T(8,128)(2,1)S(1)}, bf16[256,512]{1,0:T(8,128)(2,1)}, u32[]{:S(2)}) copy-start(bf16[256,512]{1,0:T(8,128)(2,1)} %param.1) | copy-start | bytes 786436
  0.0 7.8 %collective-permute-start = (bf16[256,512]{1,0:T(8,128)(2,1)}, bf16[256,512]{1,0:T(8,128)(2,1)S(1)}, u32[]{:S(2)}, u32[]{:S(2)}) collective-permute-start(bf16[256,512]{1,0:T(8,128)(2,1)} %param.1), channel_id=1, source_target_pairs={{0,16},{16,0},{1,17},{17,1},{2,18},{18,2},{3,19},{19,3},{4,20},{20... | collective-permute-start | bytes 786440 | tf_op jit(solution)/shard_map/ppermute | solution.py:21
  3.2 23.9 %collective-permute-start.10 = (bf16[256,512]{1,0:T(8,128)(2,1)}, bf16[256,512]{1,0:T(8,128)(2,1)S(1)}, u32[]{:S(2)}, u32[]{:S(2)}) collective-permute-start(bf16[256,512]{1,0:T(8,128)(2,1)} %param.1), channel_id=1, source_target_pairs={{0,32},{32,0},{1,33},{33,1},{2,34},{34,2},{3,35},{35,3},{4,36},{36... | collective-permute-start | bytes 786440 | tf_op jit(solution)/shard_map/ppermute | solution.py:21
  3.2 8.6 %collective-permute-start.1 = (bf16[256,512]{1,0:T(8,128)(2,1)}, bf16[256,512]{1,0:T(8,128)(2,1)S(1)}, u32[]{:S(2)}, u32[]{:S(2)}) collective-permute-start(bf16[256,512]{1,0:T(8,128)(2,1)} %param.1), channel_id=1, source_target_pairs={{0,192},{64,0},{128,64},{192,128},{1,193},{65,1},{129,65},{193,129... | collective-permute-start | bytes 786440 | tf_op jit(solution)/shard_map/ppermute | solution.py:25
  5.6 9.0 %collective-permute-start.2 = (bf16[256,512]{1,0:T(8,128)(2,1)}, bf16[256,512]{1,0:T(8,128)(2,1)S(1)}, u32[]{:S(2)}, u32[]{:S(2)}) collective-permute-start(bf16[256,512]{1,0:T(8,128)(2,1)} %param.1), channel_id=1, source_target_pairs={{0,128},{64,192},{128,0},{192,64},{1,129},{65,193},{129,1},{193,65... | collective-permute-start | bytes 786440 | tf_op jit(solution)/shard_map/ppermute | solution.py:25
  6.2 15.0 %collective-permute-start.3 = (bf16[256,512]{1,0:T(8,128)(2,1)}, bf16[256,512]{1,0:T(8,128)(2,1)S(1)}, u32[]{:S(2)}, u32[]{:S(2)}) collective-permute-start(bf16[256,512]{1,0:T(8,128)(2,1)} %param.1), channel_id=1, source_target_pairs={{0,64},{64,128},{128,192},{192,0},{1,65},{65,129},{129,193},{193,1... | collective-permute-start | bytes 786440 | tf_op jit(solution)/shard_map/ppermute | solution.py:25
  21.2 1.8 %copy-start.3 = (bf16[1024,512]{1,0:T(8,128)(2,1)}, bf16[1024,512]{1,0:T(8,128)(2,1)S(1)}, u32[]{:S(2)}) copy-start(bf16[1024,512]{1,0:T(8,128)(2,1)S(1)} %constant_dynamic-update-slice_fusion.5) | copy-start | bytes 3145732
  23.0 19.7 %all-to-all-start = ((bf16[4,128,1024]{2,1,0:T(8,128)(2,1)}), bf16[4,128,1024]{2,1,0:T(8,128)(2,1)S(1)}, u32[]{:S(2)}, u32[]{:S(2)}) async-start(bf16[4,128,1024]{2,1,0:T(8,128)(2,1)} %bitcast), calls=%async_computation | async-start | bytes 2097152 | tf_op jit(solution)/shard_map/all_to_all | solution.py:43
  27.2 7.1 %collective-permute-start.11 = (bf16[256,512]{1,0:T(8,128)(2,1)S(1)}, bf16[256,512]{1,0:T(8,128)(2,1)S(1)}, u32[]{:S(2)}, u32[]{:S(2)}) collective-permute-start(bf16[256,512]{1,0:T(8,128)(2,1)S(1)} %collective-permute-done.10), channel_id=1, source_target_pairs={{0,192},{64,0},{128,64},{192,128},{1,193},{65,1},{129,65},{193,129... | collective-permute-start | bytes 786440 | tf_op jit(solution)/shard_map/ppermute | solution.py:25
  27.2 8.1 %collective-permute-start.12 = (bf16[256,512]{1,0:T(8,128)(2,1)S(1)}, bf16[256,512]{1,0:T(8,128)(2,1)S(1)}, u32[]{:S(2)}, u32[]{:S(2)}) collective-permute-start(bf16[256,512]{1,0:T(8,128)(2,1)S(1)} %collective-permute-done.10), channel_id=1, source_target_pairs={{0,128},{64,192},{128,0},{192,64},{1,129},{65,193},{129,1},{193,65... | collective-permute-start | bytes 786440 | tf_op jit(solution)/shard_map/ppermute | solution.py:25
  27.8 14.8 %collective-permute-start.13 = (bf16[256,512]{1,0:T(8,128)(2,1)S(1)}, bf16[256,512]{1,0:T(8,128)(2,1)S(1)}, u32[]{:S(2)}, u32[]{:S(2)}) collective-permute-start(bf16[256,512]{1,0:T(8,128)(2,1)S(1)} %collective-permute-done.10), channel_id=1, source_target_pairs={{0,64},{64,128},{128,192},{192,0},{1,65},{65,129},{129,193},{193,1... | collective-permute-start | bytes 786440 | tf_op jit(solution)/shard_map/ppermute | solution.py:25
  42.8 15.6 %collective-permute-start.4 = (bf16[32,1024]{1,0:T(8,128)(2,1)S(1)}, bf16[32,1024]{1,0:T(8,128)(2,1)S(1)}, u32[]{:S(2)}, u32[]{:S(2)}) collective-permute-start(bf16[32,1024]{1,0:T(8,128)(2,1)S(1)} %get-tuple-element.20), channel_id=1, source_target_pairs={{0,4},{4,8},{8,12},{12,0},{1,5},{5,9},{9,13},{13,1},{2,6},{6,10},{... | collective-permute-start | bytes 196616 | tf_op jit(solution)/shard_map/ppermute | solution.py:25
  45.9 12.5 %collective-permute-start.5 = (bf16[32,1024]{1,0:T(8,128)(2,1)S(1)}, bf16[32,1024]{1,0:T(8,128)(2,1)S(1)}, u32[]{:S(2)}, u32[]{:S(2)}) collective-permute-start(bf16[32,1024]{1,0:T(8,128)(2,1)S(1)} %get-tuple-element.22), channel_id=1, source_target_pairs={{0,8},{4,12},{8,0},{12,4},{1,9},{5,13},{9,1},{13,5},{2,10},{6,14},... | collective-permute-start | bytes 196616 | tf_op jit(solution)/shard_map/ppermute | solution.py:25
  50.1 8.3 %collective-permute-start.6 = (bf16[32,1024]{1,0:T(8,128)(2,1)S(1)}, bf16[32,1024]{1,0:T(8,128)(2,1)S(1)}, u32[]{:S(2)}, u32[]{:S(2)}) collective-permute-start(bf16[32,1024]{1,0:T(8,128)(2,1)S(1)} %get-tuple-element.21), channel_id=1, source_target_pairs={{0,12},{4,0},{8,4},{12,8},{1,13},{5,1},{9,5},{13,9},{2,14},{6,2},{... | collective-permute-start | bytes 196616 | tf_op jit(solution)/shard_map/ppermute | solution.py:25
  54.2 17.7 %all-to-all-start.2 = ((bf16[4,128,1024]{2,1,0:T(8,128)(2,1)}), bf16[4,128,1024]{2,1,0:T(8,128)(2,1)S(1)}, u32[]{:S(2)}, u32[]{:S(2)}) async-start(bf16[4,128,1024]{2,1,0:T(8,128)(2,1)} %bitcast.40), calls=%async_computation.2 | async-start | bytes 2097152 | tf_op jit(solution)/shard_map/all_to_all | solution.py:43
  58.5 4.8 %collective-permute-start.7 = (bf16[32,1024]{1,0:T(8,128)(2,1)S(1)}, bf16[32,1024]{1,0:T(8,128)(2,1)S(1)}, u32[]{:S(2)}, u32[]{:S(2)}) collective-permute-start(bf16[32,1024]{1,0:T(8,128)(2,1)S(1)} %get-tuple-element.8), channel_id=1, source_target_pairs={{0,12},{4,0},{8,4},{12,8},{1,13},{5,1},{9,5},{13,9},{2,14},{6,2},{... | collective-permute-start | bytes 196616 | tf_op jit(solution)/shard_map/ppermute | solution.py:25
  59.6 7.1 %collective-permute-start.8 = (bf16[32,1024]{1,0:T(8,128)(2,1)S(1)}, bf16[32,1024]{1,0:T(8,128)(2,1)S(1)}, u32[]{:S(2)}, u32[]{:S(2)}) collective-permute-start(bf16[32,1024]{1,0:T(8,128)(2,1)S(1)} %get-tuple-element.8), channel_id=1, source_target_pairs={{0,8},{4,12},{8,0},{12,4},{1,9},{5,13},{9,1},{13,5},{2,10},{6,14},... | collective-permute-start | bytes 196616 | tf_op jit(solution)/shard_map/ppermute | solution.py:25
  61.8 5.6 %collective-permute-start.9 = (bf16[32,1024]{1,0:T(8,128)(2,1)S(1)}, bf16[32,1024]{1,0:T(8,128)(2,1)S(1)}, u32[]{:S(2)}, u32[]{:S(2)}) collective-permute-start(bf16[32,1024]{1,0:T(8,128)(2,1)S(1)} %get-tuple-element.8), channel_id=1, source_target_pairs={{0,4},{4,8},{8,12},{12,0},{1,5},{5,9},{9,13},{13,1},{2,6},{6,10},{... | collective-permute-start | bytes 196616 | tf_op jit(solution)/shard_map/ppermute | solution.py:25
  72.1 5.6 %collective-permute-start.14 = (bf16[32,1024]{1,0:T(8,128)(2,1)S(1)}, bf16[32,1024]{1,0:T(8,128)(2,1)S(1)}, u32[]{:S(2)}, u32[]{:S(2)}) collective-permute-start(bf16[32,1024]{1,0:T(8,128)(2,1)S(1)} %get-tuple-element.17), channel_id=1, source_target_pairs={{0,4},{4,8},{8,12},{12,0},{1,5},{5,9},{9,13},{13,1},{2,6},{6,10},{... | collective-permute-start | bytes 196616 | tf_op jit(solution)/shard_map/ppermute | solution.py:25
  72.4 7.5 %collective-permute-start.15 = (bf16[32,1024]{1,0:T(8,128)(2,1)S(1)}, bf16[32,1024]{1,0:T(8,128)(2,1)S(1)}, u32[]{:S(2)}, u32[]{:S(2)}) collective-permute-start(bf16[32,1024]{1,0:T(8,128)(2,1)S(1)} %get-tuple-element.19), channel_id=1, source_target_pairs={{0,8},{4,12},{8,0},{12,4},{1,9},{5,13},{9,1},{13,5},{2,10},{6,14},... | collective-permute-start | bytes 196616 | tf_op jit(solution)/shard_map/ppermute | solution.py:25
  74.7 7.3 %collective-permute-start.16 = (bf16[32,1024]{1,0:T(8,128)(2,1)S(1)}, bf16[32,1024]{1,0:T(8,128)(2,1)S(1)}, u32[]{:S(2)}, u32[]{:S(2)}) collective-permute-start(bf16[32,1024]{1,0:T(8,128)(2,1)S(1)} %get-tuple-element.18), channel_id=1, source_target_pairs={{0,12},{4,0},{8,4},{12,8},{1,13},{5,1},{9,5},{13,9},{2,14},{6,2},{... | collective-permute-start | bytes 196616 | tf_op jit(solution)/shard_map/ppermute | solution.py:25
  82.1 10.0 %collective-permute-start.17 = (bf16[32,1024]{1,0:T(8,128)(2,1)S(1)}, bf16[32,1024]{1,0:T(8,128)(2,1)S(1)}, u32[]{:S(2)}, u32[]{:S(2)}) collective-permute-start(bf16[32,1024]{1,0:T(8,128)(2,1)S(1)} %get-tuple-element.6), channel_id=1, source_target_pairs={{0,12},{4,0},{8,4},{12,8},{1,13},{5,1},{9,5},{13,9},{2,14},{6,2},{... | collective-permute-start | bytes 196616 | tf_op jit(solution)/shard_map/ppermute | solution.py:25
  85.0 14.6 %all-to-all-start.1 = ((bf16[4,128,1024]{2,1,0:T(8,128)(2,1)}), bf16[4,128,1024]{2,1,0:T(8,128)(2,1)S(1)}, u32[]{:S(2)}, u32[]{:S(2)}) async-start(bf16[4,128,1024]{2,1,0:T(8,128)(2,1)} %broadcast_in_dim.4), calls=%async_computation.1 | async-start | bytes 2097152 | tf_op jit(solution)/shard_map/all_to_all | solution.py:43
  88.5 7.9 %collective-permute-start.18 = (bf16[32,1024]{1,0:T(8,128)(2,1)S(1)}, bf16[32,1024]{1,0:T(8,128)(2,1)S(1)}, u32[]{:S(2)}, u32[]{:S(2)}) collective-permute-start(bf16[32,1024]{1,0:T(8,128)(2,1)S(1)} %get-tuple-element.6), channel_id=1, source_target_pairs={{0,8},{4,12},{8,0},{12,4},{1,9},{5,13},{9,1},{13,5},{2,10},{6,14},... | collective-permute-start | bytes 196616 | tf_op jit(solution)/shard_map/ppermute | solution.py:25
  92.2 6.3 %collective-permute-start.19 = (bf16[32,1024]{1,0:T(8,128)(2,1)S(1)}, bf16[32,1024]{1,0:T(8,128)(2,1)S(1)}, u32[]{:S(2)}, u32[]{:S(2)}) collective-permute-start(bf16[32,1024]{1,0:T(8,128)(2,1)S(1)} %get-tuple-element.6), channel_id=1, source_target_pairs={{0,4},{4,8},{8,12},{12,0},{1,5},{5,9},{9,13},{13,1},{2,6},{6,10},{... | collective-permute-start | bytes 196616 | tf_op jit(solution)/shard_map/ppermute | solution.py:25
  99.6 4.8 %copy-start.1 = (bf16[4,128,1024]{2,1,0:T(8,128)(2,1)}, bf16[4,128,1024]{2,1,0:T(8,128)(2,1)S(1)}, u32[]{:S(2)}) copy-start(bf16[4,128,1024]{2,1,0:T(8,128)(2,1)S(1)} %all-to-all-done.1) | copy-start | bytes 3145732
  100.8 13.4 %all-to-all-start.3 = ((bf16[4,128,1024]{2,1,0:T(8,128)(2,1)}), bf16[4,128,1024]{2,1,0:T(8,128)(2,1)S(1)}, u32[]{:S(2)}, u32[]{:S(2)}) async-start(bf16[4,128,1024]{2,1,0:T(8,128)(2,1)} %broadcast_in_dim.5), calls=%async_computation.3 | async-start | bytes 2097152 | tf_op jit(solution)/shard_map/all_to_all | solution.py:43
  116.2 7.8 %collective-permute-start.20 = (f32[256,512]{1,0:T(8,128)S(1)}, f32[256,512]{1,0:T(8,128)S(1)}, u32[]{:S(2)}, u32[]{:S(2)}) collective-permute-start(f32[256,512]{1,0:T(8,128)S(1)} %constant_dynamic-slice_fusion.6), channel_id=1, source_target_pairs={{0,16},{16,0},{1,17},{17,1},{2,18},{18,2},{3,19},{19,3},{4,20},{20... | collective-permute-start | bytes 1572872 | tf_op jit(solution)/shard_map/ppermute | solution.py:21
  122.4 20.4 %copy-start.2 = (bf16[4,128,1024]{2,1,0:T(8,128)(2,1)S(1)}, bf16[4,128,1024]{2,1,0:T(8,128)(2,1)}, u32[]{:S(2)}) copy-start(bf16[4,128,1024]{2,1,0:T(8,128)(2,1)} %copy-done.1) | copy-start | bytes 3145732
  124.1 8.8 %collective-permute-start.24 = (bf16[256,512]{1,0:T(8,128)(2,1)S(1)}, bf16[256,512]{1,0:T(8,128)(2,1)S(1)}, u32[]{:S(2)}, u32[]{:S(2)}) collective-permute-start(bf16[256,512]{1,0:T(8,128)(2,1)S(1)} %fusion.15), channel_id=1, source_target_pairs={{0,32},{32,0},{1,33},{33,1},{2,34},{34,2},{3,35},{35,3},{4,36},{36... | collective-permute-start | bytes 786440 | tf_op jit(solution)/shard_map/ppermute | solution.py:21
  126.5 7.3 %collective-permute-start.21 = (bf16[256,512]{1,0:T(8,128)(2,1)S(1)}, bf16[256,512]{1,0:T(8,128)(2,1)S(1)}, u32[]{:S(2)}, u32[]{:S(2)}) collective-permute-start(bf16[256,512]{1,0:T(8,128)(2,1)S(1)} %fusion.15), channel_id=1, source_target_pairs={{0,192},{64,0},{128,64},{192,128},{1,193},{65,1},{129,65},{193,129... | collective-permute-start | bytes 786440 | tf_op jit(solution)/shard_map/ppermute | solution.py:25
  126.5 8.7 %collective-permute-start.22 = (bf16[256,512]{1,0:T(8,128)(2,1)S(1)}, bf16[256,512]{1,0:T(8,128)(2,1)S(1)}, u32[]{:S(2)}, u32[]{:S(2)}) collective-permute-start(bf16[256,512]{1,0:T(8,128)(2,1)S(1)} %fusion.15), channel_id=1, source_target_pairs={{0,128},{64,192},{128,0},{192,64},{1,129},{65,193},{129,1},{193,65... | collective-permute-start | bytes 786440 | tf_op jit(solution)/shard_map/ppermute | solution.py:25
  127.3 15.4 %collective-permute-start.23 = (bf16[256,512]{1,0:T(8,128)(2,1)S(1)}, bf16[256,512]{1,0:T(8,128)(2,1)S(1)}, u32[]{:S(2)}, u32[]{:S(2)}) collective-permute-start(bf16[256,512]{1,0:T(8,128)(2,1)S(1)} %fusion.15), channel_id=1, source_target_pairs={{0,64},{64,128},{128,192},{192,0},{1,65},{65,129},{129,193},{193,1... | collective-permute-start | bytes 786440 | tf_op jit(solution)/shard_map/ppermute | solution.py:25
  132.8 12.1 %collective-permute-start.25 = (bf16[256,512]{1,0:T(8,128)(2,1)S(1)}, bf16[256,512]{1,0:T(8,128)(2,1)S(1)}, u32[]{:S(2)}, u32[]{:S(2)}) collective-permute-start(bf16[256,512]{1,0:T(8,128)(2,1)S(1)} %collective-permute-done.24), channel_id=1, source_target_pairs={{0,192},{64,0},{128,64},{192,128},{1,193},{65,1},{129,65},{193,129... | collective-permute-start | bytes 786440 | tf_op jit(solution)/shard_map/ppermute | solution.py:25
  132.8 13.6 %collective-permute-start.26 = (bf16[256,512]{1,0:T(8,128)(2,1)S(1)}, bf16[256,512]{1,0:T(8,128)(2,1)S(1)}, u32[]{:S(2)}, u32[]{:S(2)}) collective-permute-start(bf16[256,512]{1,0:T(8,128)(2,1)S(1)} %collective-permute-done.24), channel_id=1, source_target_pairs={{0,128},{64,192},{128,0},{192,64},{1,129},{65,193},{129,1},{193,65... | collective-permute-start | bytes 786440 | tf_op jit(solution)/shard_map/ppermute | solution.py:25
  133.7 19.3 %collective-permute-start.27 = (bf16[256,512]{1,0:T(8,128)(2,1)S(1)}, bf16[256,512]{1,0:T(8,128)(2,1)S(1)}, u32[]{:S(2)}, u32[]{:S(2)}) collective-permute-start(bf16[256,512]{1,0:T(8,128)(2,1)S(1)} %collective-permute-done.24), channel_id=1, source_target_pairs={{0,64},{64,128},{128,192},{192,0},{1,65},{65,129},{129,193},{193,1... | collective-permute-start | bytes 786440 | tf_op jit(solution)/shard_map/ppermute | solution.py:25
  153.8 2.1 %collective-permute-start.28 = (f32[256,512]{1,0:T(8,128)S(1)}, f32[256,512]{1,0:T(8,128)S(1)}, u32[]{:S(2)}, u32[]{:S(2)}) collective-permute-start(f32[256,512]{1,0:T(8,128)S(1)} %constant_dynamic-slice_fusion.5), channel_id=1, source_target_pairs={{0,16},{16,0},{1,17},{17,1},{2,18},{18,2},{3,19},{19,3},{4,20},{20... | collective-permute-start | bytes 1572872 | tf_op jit(solution)/shard_map/ppermute | solution.py:21

commit v5 on v4

--- a/solution.py
+++ b/solution.py
@@ -28,15 +28,6 @@
 def around(array, axis):
     got = {k: send(array, axis, (4 - k) % 4) for k in (0, 1, 3, 2)}
     return [got[k] for k in range(4)]
-
-
-def add(got):
-    got = [g.astype(F32) for g in got]
-    return ((got[0] + got[1]) + (got[2] + got[3])).astype(BF)
-
-
-def scatter_sum(pieces, axis):
-    return add([send(pieces[k], axis, k) for k in range(4)])
 
 
 def exchange(pieces, axis):
@@ -74,12 +65,11 @@
     other = swap(iterate, "core")
     panels = panels_of(iterate)
     own = window([iterate, other, iterate, other], core, 2)
-    own = jnp.concatenate([window(chunks(rows), zh, 4) for rows in chunks(own)], axis=0)
     gram = []
     for panel in panels:
         pieces = matmul(own, panel, ((1,), (1,))).astype(BF)
-        part = add(exchange(pieces.reshape(4, 128, 1024), "y"))
-        part = scatter_sum(chunks(part), "zh")
+        part = exchange(pieces.reshape(16, 32, 1024), ("y", "zh")).astype(F32)
+        part = jnp.sum(part, axis=0).astype(BF)
         rows = window(around(part, "zh"), lax.rem(4 - zh, 4), 4)
         copies = jnp.broadcast_to(rows[None], (4, 128, 1024))
         gram.append(exchange(copies, "y").reshape(512, 1024))

time: 157 us -> 195 us (1.24)
  waiting for transfers between devices: 79.6 us -> 119 us
  starting transfers between devices: 60.6 us -> 58.6 us
    ppermute x5, waiting for transfers between devices: 7.71 us -> 36.2 us  [swap(): return lax.ppermute(array, axis, [(0, 1), (1, 0)])]
    ppermute x24 -> x18, waiting for transfers between devices: 59.4 us -> 72.7 us  [send(): lax.ppermute(array, axis, [(i, (i + k) % 4) for i in range(4)])]
    all_to_all x4, starting transfers between devices: 15.4 us -> 27.8 us  [exchange(): return lax.all_to_all(pieces, axis, 0, 0)]
    ppermute x24 -> x18, starting transfers between devices: 32.8 us -> 20.8 us  [send(): lax.ppermute(array, axis, [(i, (i + k) % 4) for i in range(4)])]
    all_to_all x4, waiting for transfers between devices: 12.4 us -> 9.55 us  [exchange(): return lax.all_to_all(pieces, axis, 0, 0)]
    ppermute x5, starting transfers between devices: 12.5 us -> 10 us  [swap(): return lax.ppermute(array, axis, [(0, 1), (1, 0)])]
  transfers between devices with their start and end apart: 33 -> 27, of which waited for: 25 -> 20; matrix products, arithmetic and copies ran while one was open for 7% -> 5% of each run, Pallas kernels for 0% -> 0%
where the time goes in v5:
time: 195 us
  waiting for transfers between devices  119 us (61%)
  starting transfers between devices  58.6 us (30%)
  matrix products  10.7 us (5%)
  local copies, waits for them, and re-layouts  4.78 us (2%)
    ppermute x18, waiting for transfers between devices, send(): lax.ppermute(array, axis, [(i, (i + k) % 4) for i in range(4)])  72.7 us
    ppermute x5, waiting for transfers between devices, swap(): return lax.ppermute(array, axis, [(0, 1), (1, 0)])  36.2 us
    all_to_all x4, starting transfers between devices, exchange(): return lax.all_to_all(pieces, axis, 0, 0)  27.8 us
    ppermute x18, starting transfers between devices, send(): lax.ppermute(array, axis, [(i, (i + k) % 4) for i in range(4)])  20.8 us
    dot_general x6, matrix products, matmul(): return lax.dot_general(a, b, (dims, ((), ())), preferred_element_type=F32)  10.7 us
    ppermute x5, starting transfers between devices, swap(): return lax.ppermute(array, axis, [(0, 1), (1, 0)])  10 us
    all_to_all x4, waiting for transfers between devices, exchange(): return lax.all_to_all(pieces, axis, 0, 0)  9.55 us
  transfers between devices with their start and end apart: 27, of which 20 were waited for; matrix products, arithmetic and copies ran while one was open for 5% of the time, Pallas kernels for 0%

profile of v5, /device:TPU:1, one launch (start us, length us, event | category | flops | bytes accessed | tf_op | source)
XLA Modules:
  0.0 194.5 jit_solution(13278796803611122430)
XLA Ops:
  0.0 3.2 %collective-permute-start = (bf16[256,512]{1,0:T(8,128)(2,1)}, bf16[256,512]{1,0:T(8,128)(2,1)S(1)}, u32[]{:S(2)}, u32[]{:S(2)}) collective-permute-start(bf16[256,512]{1,0:T(8,128)(2,1)} %param.1), channel_id=1, source_target_pairs={{0,16},{16,0},{1,17},{17,1},{2,18},{18,2},{3,19},{19,3},{4,20},{20... | collective-permute-start | bytes 786440 | tf_op jit(solution)/shard_map/ppermute | solution.py:21
  3.2 0.7 collective-permute-start.1
  4.0 0.5 collective-permute-start.2
  4.5 0.6 collective-permute-start.3
  5.1 1.0 constant_dynamic-update-slice_fusion.4
  6.1 0.0 collective-permute-done
  6.2 1.0 constant_dynamic-update-slice_fusion.2
  7.2 4.2 %collective-permute-done.1 = bf16[256,512]{1,0:T(8,128)(2,1)S(1)} collective-permute-done((bf16[256,512]{1,0:T(8,128)(2,1)}, bf16[256,512]{1,0:T(8,128)(2,1)S(1)}, u32[]{:S(2)}, u32[]{:S(2)}) %collective-permute-start.1) | collective-permute-done | bytes 262176 | tf_op jit(solution)/shard_map/ppermute | solution.py:25
  11.4 1.9 collective-permute-done.2
  13.3 6.2 %collective-permute-done.3 = bf16[256,512]{1,0:T(8,128)(2,1)S(1)} collective-permute-done((bf16[256,512]{1,0:T(8,128)(2,1)}, bf16[256,512]{1,0:T(8,128)(2,1)S(1)}, u32[]{:S(2)}, u32[]{:S(2)}) %collective-permute-start.3) | collective-permute-done | bytes 262176 | tf_op jit(solution)/shard_map/ppermute | solution.py:25
  19.6 1.7 convolution_convert_fusion.1
  21.3 10.9 %all-to-all-start = ((bf16[16,32,1024]{2,1,0:T(8,128)(2,1)}), bf16[16,32,1024]{2,1,0:T(8,128)(2,1)S(1)}, u32[]{:S(2)}, u32[]{:S(2)}) async-start(bf16[16,32,1024]{2,1,0:T(8,128)(2,1)} %bitcast), calls=%async_computation | async-start | bytes 2097152 | tf_op jit(solution)/shard_map/all_to_all | solution.py:34
  32.2 0.8 collective-permute-start.7
  33.1 28.5 %collective-permute-done.7 = bf16[256,512]{1,0:T(8,128)(2,1)S(1)} collective-permute-done((bf16[256,512]{1,0:T(8,128)(2,1)S(1)}, bf16[256,512]{1,0:T(8,128)(2,1)S(1)}, u32[]{:S(2)}, u32[]{:S(2)}) %collective-permute-start.7) | collective-permute-done | bytes 262176 | tf_op jit(solution)/shard_map/ppermute | solution.py:21
  61.5 0.0 collective-permute-start.8
  61.5 0.5 collective-permute-start.9
  62.0 0.9 collective-permute-start.10
  63.0 5.0 %collective-permute-done.8 = bf16[256,512]{1,0:T(8,128)(2,1)S(1)} collective-permute-done((bf16[256,512]{1,0:T(8,128)(2,1)S(1)}, bf16[256,512]{1,0:T(8,128)(2,1)S(1)}, u32[]{:S(2)}, u32[]{:S(2)}) %collective-permute-start.8) | collective-permute-done | bytes 262176 | tf_op jit(solution)/shard_map/ppermute | solution.py:25
  68.0 1.5 collective-permute-done.9
  69.5 7.3 %collective-permute-done.10 = bf16[256,512]{1,0:T(8,128)(2,1)S(1)} collective-permute-done((bf16[256,512]{1,0:T(8,128)(2,1)S(1)}, bf16[256,512]{1,0:T(8,128)(2,1)S(1)}, u32[]{:S(2)}, u32[]{:S(2)}) %collective-permute-start.10) | collective-permute-done | bytes 262176 | tf_op jit(solution)/shard_map/ppermute | solution.py:25
  76.9 2.8 %convolution_convert_fusion = bf16[512,1024]{1,0:T(8,128)(2,1)} fusion(bf16[1024,512]{1,0:T(8,128)(2,1)S(1)} %constant_dynamic-update-slice_fusion.16, bf16[1280,512]{1,0:T(8,128)(2,1)} %copy-done.4, s32[]{:T(128)S(6)} %select_n.15), kind=kOutput, calls=%fused_computation | convolution fusion | flops 537395200 | bytes 2621444 | tf_op jit(solution)/shard_map/dot_general | solution.py:48
  79.7 8.5 %all-to-all-start.2 = ((bf16[16,32,1024]{2,1,0:T(8,128)(2,1)}), bf16[16,32,1024]{2,1,0:T(8,128)(2,1)S(1)}, u32[]{:S(2)}, u32[]{:S(2)}) async-start(bf16[16,32,1024]{2,1,0:T(8,128)(2,1)} %bitcast.16), calls=%async_computation.2 | async-start | bytes 2097152 | tf_op jit(solution)/shard_map/all_to_all | solution.py:34
  88.2 0.2 reduce_sum.24
  88.4 3.5 %collective-permute-start.4 = (bf16[32,1024]{1,0:T(8,128)(2,1)S(1)}, bf16[32,1024]{1,0:T(8,128)(2,1)S(1)}, u32[]{:S(2)}, u32[]{:S(2)}) collective-permute-start(bf16[32,1024]{1,0:T(8,128)(2,1)S(1)} %reduce_sum.24), channel_id=1, source_target_pairs={{0,12},{4,0},{8,4},{12,8},{1,13},{5,1},{9,5},{13,9},{2,14},{6,2},{... | collective-permute-start | bytes 196616 | tf_op jit(solution)/shard_map/ppermute | solution.py:25
  91.9 2.1 %collective-permute-start.5 = (bf16[32,1024]{1,0:T(8,128)(2,1)S(1)}, bf16[32,1024]{1,0:T(8,128)(2,1)S(1)}, u32[]{:S(2)}, u32[]{:S(2)}) collective-permute-start(bf16[32,1024]{1,0:T(8,128)(2,1)S(1)} %reduce_sum.24), channel_id=1, source_target_pairs={{0,8},{4,12},{8,0},{12,4},{1,9},{5,13},{9,1},{13,5},{2,10},{6,14},... | collective-permute-start | bytes 196616 | tf_op jit(solution)/shard_map/ppermute | solution.py:25
  94.0 2.1 %collective-permute-start.6 = (bf16[32,1024]{1,0:T(8,128)(2,1)S(1)}, bf16[32,1024]{1,0:T(8,128)(2,1)S(1)}, u32[]{:S(2)}, u32[]{:S(2)}) collective-permute-start(bf16[32,1024]{1,0:T(8,128)(2,1)S(1)} %reduce_sum.24), channel_id=1, source_target_pairs={{0,4},{4,8},{8,12},{12,0},{1,5},{5,9},{9,13},{13,1},{2,6},{6,10},{... | collective-permute-start | bytes 196616 | tf_op jit(solution)/shard_map/ppermute | solution.py:25
  96.1 21.7 %collective-permute-done.4 = bf16[32,1024]{1,0:T(8,128)(2,1)S(1)} collective-permute-done((bf16[32,1024]{1,0:T(8,128)(2,1)S(1)}, bf16[32,1024]{1,0:T(8,128)(2,1)S(1)}, u32[]{:S(2)}, u32[]{:S(2)}) %collective-permute-start.4) | collective-permute-done | bytes 65568 | tf_op jit(solution)/shard_map/ppermute | solution.py:25
  117.8 0.0 collective-permute-done.6
  117.9 1.1 broadcast_in_dim.4
  119.0 3.5 %all-to-all-start.1 = ((bf16[4,128,1024]{2,1,0:T(8,128)(2,1)}), bf16[4,128,1024]{2,1,0:T(8,128)(2,1)S(1)}, u32[]{:S(2)}, u32[]{:S(2)}) async-start(bf16[4,128,1024]{2,1,0:T(8,128)(2,1)} %broadcast_in_dim.4), calls=%async_computation.1 | async-start | bytes 2097152 | tf_op jit(solution)/shard_map/all_to_all | solution.py:34
  122.6 0.2 reduce_sum.25
  122.8 3.0 %collective-permute-start.11 = (bf16[32,1024]{1,0:T(8,128)(2,1)S(1)}, bf16[32,1024]{1,0:T(8,128)(2,1)S(1)}, u32[]{:S(2)}, u32[]{:S(2)}) collective-permute-start(bf16[32,1024]{1,0:T(8,128)(2,1)S(1)} %reduce_sum.25), channel_id=1, source_target_pairs={{0,12},{4,0},{8,4},{12,8},{1,13},{5,1},{9,5},{13,9},{2,14},{6,2},{... | collective-permute-start | bytes 196616 | tf_op jit(solution)/shard_map/ppermute | solution.py:25
  125.7 3.7 %collective-permute-start.12 = (bf16[32,1024]{1,0:T(8,128)(2,1)S(1)}, bf16[32,1024]{1,0:T(8,128)(2,1)S(1)}, u32[]{:S(2)}, u32[]{:S(2)}) collective-permute-start(bf16[32,1024]{1,0:T(8,128)(2,1)S(1)} %reduce_sum.25), channel_id=1, source_target_pairs={{0,8},{4,12},{8,0},{12,4},{1,9},{5,13},{9,1},{13,5},{2,10},{6,14},... | collective-permute-start | bytes 196616 | tf_op jit(solution)/shard_map/ppermute | solution.py:25
  129.4 0.7 collective-permute-start.13
  130.1 0.0 collective-permute-done.11
  130.1 2.6 %collective-permute-done.12 = bf16[32,1024]{1,0:T(8,128)(2,1)S(1)} collective-permute-done((bf16[32,1024]{1,0:T(8,128)(2,1)S(1)}, bf16[32,1024]{1,0:T(8,128)(2,1)S(1)}, u32[]{:S(2)}, u32[]{:S(2)}) %collective-permute-start.12) | collective-permute-done | bytes 65568 | tf_op jit(solution)/shard_map/ppermute | solution.py:25
  132.8 3.6 %collective-permute-done.13 = bf16[32,1024]{1,0:T(8,128)(2,1)S(1)} collective-permute-done((bf16[32,1024]{1,0:T(8,128)(2,1)S(1)}, bf16[32,1024]{1,0:T(8,128)(2,1)S(1)}, u32[]{:S(2)}, u32[]{:S(2)}) %collective-permute-start.13) | collective-permute-done | bytes 65568 | tf_op jit(solution)/shard_map/ppermute | solution.py:25
  136.5 1.2 broadcast_in_dim.5
  137.7 4.8 %all-to-all-start.3 = ((bf16[4,128,1024]{2,1,0:T(8,128)(2,1)}), bf16[4,128,1024]{2,1,0:T(8,128)(2,1)S(1)}, u32[]{:S(2)}, u32[]{:S(2)}) async-start(bf16[4,128,1024]{2,1,0:T(8,128)(2,1)} %broadcast_in_dim.5), calls=%async_computation.3 | async-start | bytes 2097152 | tf_op jit(solution)/shard_map/all_to_all | solution.py:34
  142.5 2.9 %fusion.22 = f32[512,512]{1,0:T(8,128)} fusion(bf16[512,1024]{1,0:T(8,128)(2,1)S(1)} %bitcast.14, bf16[1024,512]{1,0:T(8,128)(2,1)} %copy-done.3), kind=kOutput, calls=%fused_computation.59 | convolution fusion | flops 536870912 | bytes 3145728 | tf_op jit(solution)/shard_map/dot_general | solution.py:48
  145.4 9.5 %all-to-all-done.3 = bf16[4,128,1024]{2,1,0:T(8,128)(2,1)S(1)} async-done(((bf16[4,128,1024]{2,1,0:T(8,128)(2,1)}), bf16[4,128,1024]{2,1,0:T(8,128)(2,1)S(1)}, u32[]{:S(2)}, u32[]{:S(2)}) %all-to-all-start.3) | async-done | bytes 1048608 | tf_op jit(solution)/shard_map/all_to_all | solution.py:34
  155.0 1.9 convolution_add_fusion.1
  157.0 3.7 %collective-permute-start.14 = (f32[256,512]{1,0:T(8,128)S(1)}, f32[256,512]{1,0:T(8,128)S(1)}, u32[]{:S(2)}, u32[]{:S(2)}) collective-permute-start(f32[256,512]{1,0:T(8,128)S(1)} %constant_dynamic-slice_fusion.1), channel_id=1, source_target_pairs={{0,16},{16,0},{1,17},{17,1},{2,18},{18,2},{3,19},{19,3},{4,20},{20... | collective-permute-start | bytes 1572872 | tf_op jit(solution)/shard_map/ppermute | solution.py:21
  160.7 1.5 collective-permute-done.14
  162.2 0.1 fusion.17
  162.3 1.7 collective-permute-start.18
  164.0 0.0 collective-permute-start.15
  164.0 0.5 collective-permute-start.16
  164.5 0.9 collective-permute-start.17
  165.4 4.7 %collective-permute-done.18 = bf16[256,512]{1,0:T(8,128)(2,1)S(1)} collective-permute-done((bf16[256,512]{1,0:T(8,128)(2,1)S(1)}, bf16[256,512]{1,0:T(8,128)(2,1)S(1)}, u32[]{:S(2)}, u32[]{:S(2)}) %collective-permute-start.18) | collective-permute-done | bytes 262176 | tf_op jit(solution)/shard_map/ppermute | solution.py:21
  170.1 0.5 collective-permute-start.19
  170.6 0.0 collective-permute-start.20
  170.6 0.5 collective-permute-done.15
  171.2 0.5 collective-permute-start.21
  171.6 1.1 collective-permute-done.16
  172.7 7.6 %collective-permute-done.17 = bf16[256,512]{1,0:T(8,128)(2,1)S(1)} collective-permute-done((bf16[256,512]{1,0:T(8,128)(2,1)S(1)}, bf16[256,512]{1,0:T(8,128)(2,1)S(1)}, u32[]{:S(2)}, u32[]{:S(2)}) %collective-permute-start.17) | collective-permute-done | bytes 262176 | tf_op jit(solution)/shard_map/ppermute | solution.py:25
  180.3 0.7 fusion
  181.0 1.4 collective-permute-done.19
  182.4 1.6 collective-permute-done.20
  184.0 6.6 %collective-permute-done.21 = bf16[256,512]{1,0:T(8,128)(2,1)S(1)} collective-permute-done((bf16[256,512]{1,0:T(8,128)(2,1)S(1)}, bf16[256,512]{1,0:T(8,128)(2,1)S(1)}, u32[]{:S(2)}, u32[]{:S(2)}) %collective-permute-start.21) | collective-permute-done | bytes 262176 | tf_op jit(solution)/shard_map/ppermute | solution.py:25
  190.5 0.7 convolution_add_fusion
  191.3 0.6 collective-permute-start.22
  191.9 1.5 collective-permute-done.22
  193.4 1.1 add_multiply_fusion
  (42 shorter events, 0.5 us)
Async XLA Ops:
  0.0 7.2 %copy-start = (bf16[256,512]{1,0:T(8,128)(2,1)S(1)}, bf16[256,512]{1,0:T(8,128)(2,1)}, u32[]{:S(2)}) copy-start(bf16[256,512]{1,0:T(8,128)(2,1)} %param.1) | copy-start | bytes 786436
  0.0 6.1 %collective-permute-start = (bf16[256,512]{1,0:T(8,128)(2,1)}, bf16[256,512]{1,0:T(8,128)(2,1)S(1)}, u32[]{:S(2)}, u32[]{:S(2)}) collective-permute-start(bf16[256,512]{1,0:T(8,128)(2,1)} %param.1), channel_id=1, source_target_pairs={{0,16},{16,0},{1,17},{17,1},{2,18},{18,2},{3,19},{19,3},{4,20},{20... | collective-permute-start | bytes 786440 | tf_op jit(solution)/shard_map/ppermute | solution.py:21
  3.2 8.1 %collective-permute-start.1 = (bf16[256,512]{1,0:T(8,128)(2,1)}, bf16[256,512]{1,0:T(8,128)(2,1)S(1)}, u32[]{:S(2)}, u32[]{:S(2)}) collective-permute-start(bf16[256,512]{1,0:T(8,128)(2,1)} %param.1), channel_id=1, source_target_pairs={{0,192},{64,0},{128,64},{192,128},{1,193},{65,1},{129,65},{193,129... | collective-permute-start | bytes 786440 | tf_op jit(solution)/shard_map/ppermute | solution.py:25
  4.0 9.3 %collective-permute-start.2 = (bf16[256,512]{1,0:T(8,128)(2,1)}, bf16[256,512]{1,0:T(8,128)(2,1)S(1)}, u32[]{:S(2)}, u32[]{:S(2)}) collective-permute-start(bf16[256,512]{1,0:T(8,128)(2,1)} %param.1), channel_id=1, source_target_pairs={{0,128},{64,192},{128,0},{192,64},{1,129},{65,193},{129,1},{193,65... | collective-permute-start | bytes 786440 | tf_op jit(solution)/shard_map/ppermute | solution.py:25
  4.5 15.0 %collective-permute-start.3 = (bf16[256,512]{1,0:T(8,128)(2,1)}, bf16[256,512]{1,0:T(8,128)(2,1)S(1)}, u32[]{:S(2)}, u32[]{:S(2)}) collective-permute-start(bf16[256,512]{1,0:T(8,128)(2,1)} %param.1), channel_id=1, source_target_pairs={{0,64},{64,128},{128,192},{192,0},{1,65},{65,129},{129,193},{193,1... | collective-permute-start | bytes 786440 | tf_op jit(solution)/shard_map/ppermute | solution.py:25
  7.2 14.1 %copy-start.4 = (bf16[1280,512]{1,0:T(8,128)(2,1)}, bf16[1280,512]{1,0:T(8,128)(2,1)S(1)}, u32[]{:S(2)}) copy-start(bf16[1280,512]{1,0:T(8,128)(2,1)S(1)} %get-tuple-element.5) | copy-start | bytes 3932164
  19.6 1.7 copy-start.3
  21.3 58.3 %all-to-all-start = ((bf16[16,32,1024]{2,1,0:T(8,128)(2,1)}), bf16[16,32,1024]{2,1,0:T(8,128)(2,1)S(1)}, u32[]{:S(2)}, u32[]{:S(2)}) async-start(bf16[16,32,1024]{2,1,0:T(8,128)(2,1)} %bitcast), calls=%async_computation | async-start | bytes 2097152 | tf_op jit(solution)/shard_map/all_to_all | solution.py:34
  32.2 29.3 %collective-permute-start.7 = (bf16[256,512]{1,0:T(8,128)(2,1)S(1)}, bf16[256,512]{1,0:T(8,128)(2,1)S(1)}, u32[]{:S(2)}, u32[]{:S(2)}) collective-permute-start(bf16[256,512]{1,0:T(8,128)(2,1)S(1)} %copy-done), channel_id=1, source_target_pairs={{0,32},{32,0},{1,33},{33,1},{2,34},{34,2},{3,35},{35,3},{4,36},{36... | collective-permute-start | bytes 786440 | tf_op jit(solution)/shard_map/ppermute | solution.py:21
  61.5 6.5 %collective-permute-start.8 = (bf16[256,512]{1,0:T(8,128)(2,1)S(1)}, bf16[256,512]{1,0:T(8,128)(2,1)S(1)}, u32[]{:S(2)}, u32[]{:S(2)}) collective-permute-start(bf16[256,512]{1,0:T(8,128)(2,1)S(1)} %collective-permute-done.7), channel_id=1, source_target_pairs={{0,192},{64,0},{128,64},{192,128},{1,193},{65,1},{129,65},{193,129... | collective-permute-start | bytes 786440 | tf_op jit(solution)/shard_map/ppermute | solution.py:25
  61.5 8.0 %collective-permute-start.9 = (bf16[256,512]{1,0:T(8,128)(2,1)S(1)}, bf16[256,512]{1,0:T(8,128)(2,1)S(1)}, u32[]{:S(2)}, u32[]{:S(2)}) collective-permute-start(bf16[256,512]{1,0:T(8,128)(2,1)S(1)} %collective-permute-done.7), channel_id=1, source_target_pairs={{0,128},{64,192},{128,0},{192,64},{1,129},{65,193},{129,1},{193,65... | collective-permute-start | bytes 786440 | tf_op jit(solution)/shard_map/ppermute | solution.py:25
  62.0 14.8 %collective-permute-start.10 = (bf16[256,512]{1,0:T(8,128)(2,1)S(1)}, bf16[256,512]{1,0:T(8,128)(2,1)S(1)}, u32[]{:S(2)}, u32[]{:S(2)}) collective-permute-start(bf16[256,512]{1,0:T(8,128)(2,1)S(1)} %collective-permute-done.7), channel_id=1, source_target_pairs={{0,64},{64,128},{128,192},{192,0},{1,65},{65,129},{129,193},{193,1... | collective-permute-start | bytes 786440 | tf_op jit(solution)/shard_map/ppermute | solution.py:25
  79.7 38.3 %all-to-all-start.2 = ((bf16[16,32,1024]{2,1,0:T(8,128)(2,1)}), bf16[16,32,1024]{2,1,0:T(8,128)(2,1)S(1)}, u32[]{:S(2)}, u32[]{:S(2)}) async-start(bf16[16,32,1024]{2,1,0:T(8,128)(2,1)} %bitcast.16), calls=%async_computation.2 | async-start | bytes 2097152 | tf_op jit(solution)/shard_map/all_to_all | solution.py:34
  88.4 29.4 %collective-permute-start.4 = (bf16[32,1024]{1,0:T(8,128)(2,1)S(1)}, bf16[32,1024]{1,0:T(8,128)(2,1)S(1)}, u32[]{:S(2)}, u32[]{:S(2)}) collective-permute-start(bf16[32,1024]{1,0:T(8,128)(2,1)S(1)} %reduce_sum.24), channel_id=1, source_target_pairs={{0,12},{4,0},{8,4},{12,8},{1,13},{5,1},{9,5},{13,9},{2,14},{6,2},{... | collective-permute-start | bytes 196616 | tf_op jit(solution)/shard_map/ppermute | solution.py:25
  91.9 25.8 %collective-permute-start.5 = (bf16[32,1024]{1,0:T(8,128)(2,1)S(1)}, bf16[32,1024]{1,0:T(8,128)(2,1)S(1)}, u32[]{:S(2)}, u32[]{:S(2)}) collective-permute-start(bf16[32,1024]{1,0:T(8,128)(2,1)S(1)} %reduce_sum.24), channel_id=1, source_target_pairs={{0,8},{4,12},{8,0},{12,4},{1,9},{5,13},{9,1},{13,5},{2,10},{6,14},... | collective-permute-start | bytes 196616 | tf_op jit(solution)/shard_map/ppermute | solution.py:25
  94.0 23.8 %collective-permute-start.6 = (bf16[32,1024]{1,0:T(8,128)(2,1)S(1)}, bf16[32,1024]{1,0:T(8,128)(2,1)S(1)}, u32[]{:S(2)}, u32[]{:S(2)}) collective-permute-start(bf16[32,1024]{1,0:T(8,128)(2,1)S(1)} %reduce_sum.24), channel_id=1, source_target_pairs={{0,4},{4,8},{8,12},{12,0},{1,5},{5,9},{9,13},{13,1},{2,6},{6,10},{... | collective-permute-start | bytes 196616 | tf_op jit(solution)/shard_map/ppermute | solution.py:25
  119.0 17.4 %all-to-all-start.1 = ((bf16[4,128,1024]{2,1,0:T(8,128)(2,1)}), bf16[4,128,1024]{2,1,0:T(8,128)(2,1)S(1)}, u32[]{:S(2)}, u32[]{:S(2)}) async-start(bf16[4,128,1024]{2,1,0:T(8,128)(2,1)} %broadcast_in_dim.4), calls=%async_computation.1 | async-start | bytes 2097152 | tf_op jit(solution)/shard_map/all_to_all | solution.py:34
  122.8 7.4 %collective-permute-start.11 = (bf16[32,1024]{1,0:T(8,128)(2,1)S(1)}, bf16[32,1024]{1,0:T(8,128)(2,1)S(1)}, u32[]{:S(2)}, u32[]{:S(2)}) collective-permute-start(bf16[32,1024]{1,0:T(8,128)(2,1)S(1)} %reduce_sum.25), channel_id=1, source_target_pairs={{0,12},{4,0},{8,4},{12,8},{1,13},{5,1},{9,5},{13,9},{2,14},{6,2},{... | collective-permute-start | bytes 196616 | tf_op jit(solution)/shard_map/ppermute | solution.py:25
  125.7 7.0 %collective-permute-start.12 = (bf16[32,1024]{1,0:T(8,128)(2,1)S(1)}, bf16[32,1024]{1,0:T(8,128)(2,1)S(1)}, u32[]{:S(2)}, u32[]{:S(2)}) collective-permute-start(bf16[32,1024]{1,0:T(8,128)(2,1)S(1)} %reduce_sum.25), channel_id=1, source_target_pairs={{0,8},{4,12},{8,0},{12,4},{1,9},{5,13},{9,1},{13,5},{2,10},{6,14},... | collective-permute-start | bytes 196616 | tf_op jit(solution)/shard_map/ppermute | solution.py:25
  129.4 7.0 %collective-permute-start.13 = (bf16[32,1024]{1,0:T(8,128)(2,1)S(1)}, bf16[32,1024]{1,0:T(8,128)(2,1)S(1)}, u32[]{:S(2)}, u32[]{:S(2)}) collective-permute-start(bf16[32,1024]{1,0:T(8,128)(2,1)S(1)} %reduce_sum.25), channel_id=1, source_target_pairs={{0,4},{4,8},{8,12},{12,0},{1,5},{5,9},{9,13},{13,1},{2,6},{6,10},{... | collective-permute-start | bytes 196616 | tf_op jit(solution)/shard_map/ppermute | solution.py:25
  136.5 6.1 %copy-start.1 = (bf16[4,128,1024]{2,1,0:T(8,128)(2,1)}, bf16[4,128,1024]{2,1,0:T(8,128)(2,1)S(1)}, u32[]{:S(2)}) copy-start(bf16[4,128,1024]{2,1,0:T(8,128)(2,1)S(1)} %all-to-all-done.1) | copy-start | bytes 3145732
  137.7 17.3 %all-to-all-start.3 = ((bf16[4,128,1024]{2,1,0:T(8,128)(2,1)}), bf16[4,128,1024]{2,1,0:T(8,128)(2,1)S(1)}, u32[]{:S(2)}, u32[]{:S(2)}) async-start(bf16[4,128,1024]{2,1,0:T(8,128)(2,1)} %broadcast_in_dim.5), calls=%async_computation.3 | async-start | bytes 2097152 | tf_op jit(solution)/shard_map/all_to_all | solution.py:34
  157.0 5.2 %collective-permute-start.14 = (f32[256,512]{1,0:T(8,128)S(1)}, f32[256,512]{1,0:T(8,128)S(1)}, u32[]{:S(2)}, u32[]{:S(2)}) collective-permute-start(f32[256,512]{1,0:T(8,128)S(1)} %constant_dynamic-slice_fusion.1), channel_id=1, source_target_pairs={{0,16},{16,0},{1,17},{17,1},{2,18},{18,2},{3,19},{19,3},{4,20},{20... | collective-permute-start | bytes 1572872 | tf_op jit(solution)/shard_map/ppermute | solution.py:21
  160.7 19.6 %copy-start.2 = (bf16[4,128,1024]{2,1,0:T(8,128)(2,1)S(1)}, bf16[4,128,1024]{2,1,0:T(8,128)(2,1)}, u32[]{:S(2)}) copy-start(bf16[4,128,1024]{2,1,0:T(8,128)(2,1)} %copy-done.1) | copy-start | bytes 3145732
  162.3 7.9 %collective-permute-start.18 = (bf16[256,512]{1,0:T(8,128)(2,1)S(1)}, bf16[256,512]{1,0:T(8,128)(2,1)S(1)}, u32[]{:S(2)}, u32[]{:S(2)}) collective-permute-start(bf16[256,512]{1,0:T(8,128)(2,1)S(1)} %fusion.17), channel_id=1, source_target_pairs={{0,32},{32,0},{1,33},{33,1},{2,34},{34,2},{3,35},{35,3},{4,36},{36... | collective-permute-start | bytes 786440 | tf_op jit(solution)/shard_map/ppermute | solution.py:21
  164.0 7.2 %collective-permute-start.15 = (bf16[256,512]{1,0:T(8,128)(2,1)S(1)}, bf16[256,512]{1,0:T(8,128)(2,1)S(1)}, u32[]{:S(2)}, u32[]{:S(2)}) collective-permute-start(bf16[256,512]{1,0:T(8,128)(2,1)S(1)} %fusion.17), channel_id=1, source_target_pairs={{0,192},{64,0},{128,64},{192,128},{1,193},{65,1},{129,65},{193,129... | collective-permute-start | bytes 786440 | tf_op jit(solution)/shard_map/ppermute | solution.py:25
  164.0 8.7 %collective-permute-start.16 = (bf16[256,512]{1,0:T(8,128)(2,1)S(1)}, bf16[256,512]{1,0:T(8,128)(2,1)S(1)}, u32[]{:S(2)}, u32[]{:S(2)}) collective-permute-start(bf16[256,512]{1,0:T(8,128)(2,1)S(1)} %fusion.17), channel_id=1, source_target_pairs={{0,128},{64,192},{128,0},{192,64},{1,129},{65,193},{129,1},{193,65... | collective-permute-start | bytes 786440 | tf_op jit(solution)/shard_map/ppermute | solution.py:25
  164.5 15.8 %collective-permute-start.17 = (bf16[256,512]{1,0:T(8,128)(2,1)S(1)}, bf16[256,512]{1,0:T(8,128)(2,1)S(1)}, u32[]{:S(2)}, u32[]{:S(2)}) collective-permute-start(bf16[256,512]{1,0:T(8,128)(2,1)S(1)} %fusion.17), channel_id=1, source_target_pairs={{0,64},{64,128},{128,192},{192,0},{1,65},{65,129},{129,193},{193,1... | collective-permute-start | bytes 786440 | tf_op jit(solution)/shard_map/ppermute | solution.py:25
  170.1 12.3 %collective-permute-start.19 = (bf16[256,512]{1,0:T(8,128)(2,1)S(1)}, bf16[256,512]{1,0:T(8,128)(2,1)S(1)}, u32[]{:S(2)}, u32[]{:S(2)}) collective-permute-start(bf16[256,512]{1,0:T(8,128)(2,1)S(1)} %collective-permute-done.18), channel_id=1, source_target_pairs={{0,192},{64,0},{128,64},{192,128},{1,193},{65,1},{129,65},{193,129... | collective-permute-start | bytes 786440 | tf_op jit(solution)/shard_map/ppermute | solution.py:25
  170.6 13.3 %collective-permute-start.20 = (bf16[256,512]{1,0:T(8,128)(2,1)S(1)}, bf16[256,512]{1,0:T(8,128)(2,1)S(1)}, u32[]{:S(2)}, u32[]{:S(2)}) collective-permute-start(bf16[256,512]{1,0:T(8,128)(2,1)S(1)} %collective-permute-done.18), channel_id=1, source_target_pairs={{0,128},{64,192},{128,0},{192,64},{1,129},{65,193},{129,1},{193,65... | collective-permute-start | bytes 786440 | tf_op jit(solution)/shard_map/ppermute | solution.py:25
  171.2 19.4 %collective-permute-start.21 = (bf16[256,512]{1,0:T(8,128)(2,1)S(1)}, bf16[256,512]{1,0:T(8,128)(2,1)S(1)}, u32[]{:S(2)}, u32[]{:S(2)}) collective-permute-start(bf16[256,512]{1,0:T(8,128)(2,1)S(1)} %collective-permute-done.18), channel_id=1, source_target_pairs={{0,64},{64,128},{128,192},{192,0},{1,65},{65,129},{129,193},{193,1... | collective-permute-start | bytes 786440 | tf_op jit(solution)/shard_map/ppermute | solution.py:25
  191.3 2.1 %collective-permute-start.22 = (f32[256,512]{1,0:T(8,128)S(1)}, f32[256,512]{1,0:T(8,128)S(1)}, u32[]{:S(2)}, u32[]{:S(2)}) collective-permute-start(f32[256,512]{1,0:T(8,128)S(1)} %constant_dynamic-slice_fusion), channel_id=1, source_target_pairs={{0,16},{16,0},{1,17},{17,1},{2,18},{18,2},{3,19},{19,3},{4,20},{20... | collective-permute-start | bytes 1572872 | tf_op jit(solution)/shard_map/ppermute | solution.py:21

commit v6 on v5

--- a/solution.py
+++ b/solution.py
@@ -50,7 +50,9 @@
 
 def panels_of(block):
     partner = swap(block, "zl")
-    return [jnp.concatenate(around(b, "x"), axis=0) for b in (block, partner)]
+    panel = jnp.concatenate(around(block, "x"), axis=0)
+    panel, partner = lax.optimization_barrier((panel, partner))
+    return [panel, jnp.concatenate(around(partner, "x"), axis=0)]
 
 
 def apply(core, gram, panels):
@@ -65,10 +67,11 @@
     other = swap(iterate, "core")
     panels = panels_of(iterate)
     own = window([iterate, other, iterate, other], core, 2)
+    own = own.reshape(4, 4, 32, 512).swapaxes(0, 1).reshape(512, 512)
     gram = []
     for panel in panels:
         pieces = matmul(own, panel, ((1,), (1,))).astype(BF)
-        part = exchange(pieces.reshape(16, 32, 1024), ("y", "zh")).astype(F32)
+        part = exchange(pieces.reshape(16, 32, 1024), COL).astype(F32)
         part = jnp.sum(part, axis=0).astype(BF)
         rows = window(around(part, "zh"), lax.rem(4 - zh, 4), 4)
         copies = jnp.broadcast_to(rows[None], (4, 128, 1024))

time: 195 us -> 186 us (0.954)
  waiting for transfers between devices: 119 us -> 91.6 us
  starting transfers between devices: 58.6 us -> 72.6 us
    ppermute x5, waiting for transfers between devices: 36.2 us -> 3.08 us  [swap(): return lax.ppermute(array, axis, [(0, 1), (1, 0)])]
    all_to_all x4, waiting for transfers between devices: 9.55 us -> 35.7 us  [exchange(): return lax.all_to_all(pieces, axis, 0, 0)]
    ppermute x18, waiting for transfers between devices: 72.7 us -> 52.8 us  [send(): lax.ppermute(array, axis, [(i, (i + k) % 4) for i in range(4)])]
    ppermute x18, starting transfers between devices: 20.8 us -> 35.4 us  [send(): lax.ppermute(array, axis, [(i, (i + k) % 4) for i in range(4)])]
    all_to_all x4, starting transfers between devices: 27.8 us -> 25.8 us  [exchange(): return lax.all_to_all(pieces, axis, 0, 0)]
  transfers between devices with their start and end apart: 27 -> 27, of which waited for: 20 -> 15; matrix products, arithmetic and copies ran while one was open for 5% -> 7% of each run, Pallas kernels for 0% -> 0%
where the time goes in v6:
time: 186 us; the launch traced here: 185 us
  waiting for transfers between devices  91.6 us (49%)
  starting transfers between devices  72.6 us (39%)
  matrix products  10.9 us (6%)
  local copies, waits for them, and re-layouts  6.61 us (4%)
  other arithmetic  2.63 us (1%)
    ppermute x18, waiting for transfers between devices, send(): lax.ppermute(array, axis, [(i, (i + k) % 4) for i in range(4)])  52.8 us
    all_to_all x4, waiting for transfers between devices, exchange(): return lax.all_to_all(pieces, axis, 0, 0)  35.7 us
    ppermute x18, starting transfers between devices, send(): lax.ppermute(array, axis, [(i, (i + k) % 4) for i in range(4)])  35.4 us
    all_to_all x4, starting transfers between devices, exchange(): return lax.all_to_all(pieces, axis, 0, 0)  25.8 us
    ppermute x5, starting transfers between devices, swap(): return lax.ppermute(array, axis, [(0, 1), (1, 0)])  11.4 us
    dot_general x6, matrix products, matmul(): return lax.dot_general(a, b, (dims, ((), ())), preferred_element_type=F32)  10.9 us
  transfers between devices with their start and end apart: 27, of which 15 were waited for; matrix products, arithmetic and copies ran while one was open for 7% of the time, Pallas kernels for 0%

profile of v6, /device:TPU:1, one launch (start us, length us, event | category | flops | bytes accessed | tf_op | source)
XLA Modules:
  0.0 184.7 jit_solution(10569132413772977368)
XLA Ops:
  0.0 2.0 %collective-permute-start.3 = (bf16[256,512]{1,0:T(8,128)(2,1)}, bf16[256,512]{1,0:T(8,128)(2,1)S(1)}, u32[]{:S(2)}, u32[]{:S(2)}) collective-permute-start(bf16[256,512]{1,0:T(8,128)(2,1)} %param.1), channel_id=1, source_target_pairs={{0,64},{64,128},{128,192},{192,0},{1,65},{65,129},{129,193},{193,1... | collective-permute-start | bytes 786440 | tf_op jit(solution)/shard_map/ppermute | solution.py:25
  2.0 2.5 %collective-permute-start.2 = (bf16[256,512]{1,0:T(8,128)(2,1)}, bf16[256,512]{1,0:T(8,128)(2,1)S(1)}, u32[]{:S(2)}, u32[]{:S(2)}) collective-permute-start(bf16[256,512]{1,0:T(8,128)(2,1)} %param.1), channel_id=1, source_target_pairs={{0,128},{64,192},{128,0},{192,64},{1,129},{65,193},{129,1},{193,65... | collective-permute-start | bytes 786440 | tf_op jit(solution)/shard_map/ppermute | solution.py:25
  4.5 1.2 collective-permute-start.1
  5.6 1.6 collective-permute-start.4
  7.3 1.8 collective-permute-start
  9.1 1.0 constant_dynamic-update-slice_fusion.4
  10.1 0.0 copy-start
  10.1 6.0 %collective-permute-done.2 = bf16[256,512]{1,0:T(8,128)(2,1)S(1)} collective-permute-done((bf16[256,512]{1,0:T(8,128)(2,1)}, bf16[256,512]{1,0:T(8,128)(2,1)S(1)}, u32[]{:S(2)}, u32[]{:S(2)}) %collective-permute-start.2) | collective-permute-done | bytes 262176 | tf_op jit(solution)/shard_map/ppermute | solution.py:25
  16.0 0.0 collective-permute-done.1
  16.0 1.0 pad_maximum_fusion
  17.3 1.8 convolution_convert_fusion.1
  19.0 10.9 %all-to-all-start = ((bf16[16,32,1024]{2,1,0:T(8,128)(2,1)}), bf16[16,32,1024]{2,1,0:T(8,128)(2,1)S(1)}, u32[]{:S(2)}, u32[]{:S(2)}) async-start(bf16[16,32,1024]{2,1,0:T(8,128)(2,1)} %bitcast.3), calls=%async_computation | async-start | bytes 2097152 | tf_op jit(solution)/shard_map/all_to_all | solution.py:34
  30.0 3.1 %collective-permute-start.8 = (bf16[256,512]{1,0:T(8,128)(2,1)S(1)}, bf16[256,512]{1,0:T(8,128)(2,1)S(1)}, u32[]{:S(2)}, u32[]{:S(2)}) collective-permute-start(bf16[256,512]{1,0:T(8,128)(2,1)S(1)} %collective-permute-done.4), channel_id=1, source_target_pairs={{0,192},{64,0},{128,64},{192,128},{1,193},{65,1},{129,65},{193,129... | collective-permute-start | bytes 786440 | tf_op jit(solution)/shard_map/ppermute | solution.py:25
  33.1 0.1 collective-permute-start.9
  33.2 0.6 collective-permute-start.10
  33.8 0.7 constant_dynamic-update-slice_fusion.15
  34.5 8.9 %collective-permute-done.8 = bf16[256,512]{1,0:T(8,128)(2,1)S(1)} collective-permute-done((bf16[256,512]{1,0:T(8,128)(2,1)S(1)}, bf16[256,512]{1,0:T(8,128)(2,1)S(1)}, u32[]{:S(2)}, u32[]{:S(2)}) %collective-permute-start.8) | collective-permute-done | bytes 262176 | tf_op jit(solution)/shard_map/ppermute | solution.py:25
  43.4 0.7 constant_dynamic-update-slice_fusion.14
  44.2 0.0 collective-permute-done.9
  44.2 0.7 constant_dynamic-update-slice_fusion.13
  44.9 3.2 %collective-permute-done.10 = bf16[256,512]{1,0:T(8,128)(2,1)S(1)} collective-permute-done((bf16[256,512]{1,0:T(8,128)(2,1)S(1)}, bf16[256,512]{1,0:T(8,128)(2,1)S(1)}, u32[]{:S(2)}, u32[]{:S(2)}) %collective-permute-start.10) | collective-permute-done | bytes 262176 | tf_op jit(solution)/shard_map/ppermute | solution.py:25
  48.1 0.7 constant_dynamic-update-slice_fusion.12
  48.8 2.9 %convolution_convert_fusion = bf16[512,1024]{1,0:T(8,128)(2,1)} fusion(bf16[512,512]{1,0:T(8,128)(2,1)S(1)} %bitcast.26, bf16[1024,512]{1,0:T(8,128)(2,1)} %constant_dynamic-update-slice_fusion.12), kind=kOutput, calls=%fused_computation | convolution fusion | flops 537395200 | bytes 2621440 | tf_op jit(solution)/shard_map/dot_general | solution.py:48
  51.7 2.9 %all-to-all-done = bf16[16,32,1024]{2,1,0:T(8,128)(2,1)S(1)} async-done(((bf16[16,32,1024]{2,1,0:T(8,128)(2,1)}), bf16[16,32,1024]{2,1,0:T(8,128)(2,1)S(1)}, u32[]{:S(2)}, u32[]{:S(2)}) %all-to-all-start) | async-done | bytes 1048608 | tf_op jit(solution)/shard_map/all_to_all | solution.py:34
  54.6 7.7 %all-to-all-start.2 = ((bf16[16,32,1024]{2,1,0:T(8,128)(2,1)}), bf16[16,32,1024]{2,1,0:T(8,128)(2,1)S(1)}, u32[]{:S(2)}, u32[]{:S(2)}) async-start(bf16[16,32,1024]{2,1,0:T(8,128)(2,1)} %bitcast.24), calls=%async_computation.2 | async-start | bytes 2097152 | tf_op jit(solution)/shard_map/all_to_all | solution.py:34
  62.3 0.2 reduce_sum.24
  62.5 2.3 %collective-permute-start.7 = (bf16[32,1024]{1,0:T(8,128)(2,1)S(1)}, bf16[32,1024]{1,0:T(8,128)(2,1)S(1)}, u32[]{:S(2)}, u32[]{:S(2)}) collective-permute-start(bf16[32,1024]{1,0:T(8,128)(2,1)S(1)} %reduce_sum.24), channel_id=1, source_target_pairs={{0,4},{4,8},{8,12},{12,0},{1,5},{5,9},{9,13},{13,1},{2,6},{6,10},{... | collective-permute-start | bytes 196616 | tf_op jit(solution)/shard_map/ppermute | solution.py:25
  64.9 3.3 %collective-permute-start.6 = (bf16[32,1024]{1,0:T(8,128)(2,1)S(1)}, bf16[32,1024]{1,0:T(8,128)(2,1)S(1)}, u32[]{:S(2)}, u32[]{:S(2)}) collective-permute-start(bf16[32,1024]{1,0:T(8,128)(2,1)S(1)} %reduce_sum.24), channel_id=1, source_target_pairs={{0,8},{4,12},{8,0},{12,4},{1,9},{5,13},{9,1},{13,5},{2,10},{6,14},... | collective-permute-start | bytes 196616 | tf_op jit(solution)/shard_map/ppermute | solution.py:25
  68.1 3.3 %collective-permute-start.5 = (bf16[32,1024]{1,0:T(8,128)(2,1)S(1)}, bf16[32,1024]{1,0:T(8,128)(2,1)S(1)}, u32[]{:S(2)}, u32[]{:S(2)}) collective-permute-start(bf16[32,1024]{1,0:T(8,128)(2,1)S(1)} %reduce_sum.24), channel_id=1, source_target_pairs={{0,12},{4,0},{8,4},{12,8},{1,13},{5,1},{9,5},{13,9},{2,14},{6,2},{... | collective-permute-start | bytes 196616 | tf_op jit(solution)/shard_map/ppermute | solution.py:25
  71.4 11.5 %all-to-all-done.2 = bf16[16,32,1024]{2,1,0:T(8,128)(2,1)S(1)} async-done(((bf16[16,32,1024]{2,1,0:T(8,128)(2,1)}), bf16[16,32,1024]{2,1,0:T(8,128)(2,1)S(1)}, u32[]{:S(2)}, u32[]{:S(2)}) %all-to-all-start.2) | async-done | bytes 1048608 | tf_op jit(solution)/shard_map/all_to_all | solution.py:34
  82.9 0.2 reduce_sum.25
  83.1 0.1 collective-permute-start.13
  83.2 3.6 %collective-permute-start.11 = (bf16[32,1024]{1,0:T(8,128)(2,1)S(1)}, bf16[32,1024]{1,0:T(8,128)(2,1)S(1)}, u32[]{:S(2)}, u32[]{:S(2)}) collective-permute-start(bf16[32,1024]{1,0:T(8,128)(2,1)S(1)} %reduce_sum.25), channel_id=1, source_target_pairs={{0,12},{4,0},{8,4},{12,8},{1,13},{5,1},{9,5},{13,9},{2,14},{6,2},{... | collective-permute-start | bytes 196616 | tf_op jit(solution)/shard_map/ppermute | solution.py:25
  86.8 9.4 %collective-permute-done.11 = bf16[32,1024]{1,0:T(8,128)(2,1)S(1)} collective-permute-done((bf16[32,1024]{1,0:T(8,128)(2,1)S(1)}, bf16[32,1024]{1,0:T(8,128)(2,1)S(1)}, u32[]{:S(2)}, u32[]{:S(2)}) %collective-permute-start.11) | collective-permute-done | bytes 65568 | tf_op jit(solution)/shard_map/ppermute | solution.py:25
  96.2 2.0 %collective-permute-start.12 = (bf16[32,1024]{1,0:T(8,128)(2,1)S(1)}, bf16[32,1024]{1,0:T(8,128)(2,1)S(1)}, u32[]{:S(2)}, u32[]{:S(2)}) collective-permute-start(bf16[32,1024]{1,0:T(8,128)(2,1)S(1)} %reduce_sum.25), channel_id=1, source_target_pairs={{0,8},{4,12},{8,0},{12,4},{1,9},{5,13},{9,1},{13,5},{2,10},{6,14},... | collective-permute-start | bytes 196616 | tf_op jit(solution)/shard_map/ppermute | solution.py:25
  98.2 6.1 %collective-permute-done.12 = bf16[32,1024]{1,0:T(8,128)(2,1)S(1)} collective-permute-done((bf16[32,1024]{1,0:T(8,128)(2,1)S(1)}, bf16[32,1024]{1,0:T(8,128)(2,1)S(1)}, u32[]{:S(2)}, u32[]{:S(2)}) %collective-permute-start.12) | collective-permute-done | bytes 65568 | tf_op jit(solution)/shard_map/ppermute | solution.py:25
  104.3 1.1 broadcast_in_dim.5
  105.5 3.7 %all-to-all-start.3 = ((bf16[4,128,1024]{2,1,0:T(8,128)(2,1)}), bf16[4,128,1024]{2,1,0:T(8,128)(2,1)S(1)}, u32[]{:S(2)}, u32[]{:S(2)}) async-start(bf16[4,128,1024]{2,1,0:T(8,128)(2,1)} %broadcast_in_dim.5), calls=%async_computation.3 | async-start | bytes 2097152 | tf_op jit(solution)/shard_map/all_to_all | solution.py:34
  109.3 12.5 %all-to-all-done.3 = bf16[4,128,1024]{2,1,0:T(8,128)(2,1)S(1)} async-done(((bf16[4,128,1024]{2,1,0:T(8,128)(2,1)}), bf16[4,128,1024]{2,1,0:T(8,128)(2,1)S(1)}, u32[]{:S(2)}, u32[]{:S(2)}) %all-to-all-start.3) | async-done | bytes 1048608 | tf_op jit(solution)/shard_map/all_to_all | solution.py:34
  121.9 1.2 broadcast_in_dim.4
  123.1 3.5 %all-to-all-start.1 = ((bf16[4,128,1024]{2,1,0:T(8,128)(2,1)}), bf16[4,128,1024]{2,1,0:T(8,128)(2,1)S(1)}, u32[]{:S(2)}, u32[]{:S(2)}) async-start(bf16[4,128,1024]{2,1,0:T(8,128)(2,1)} %broadcast_in_dim.4), calls=%async_computation.1 | async-start | bytes 2097152 | tf_op jit(solution)/shard_map/all_to_all | solution.py:34
  126.6 2.9 %fusion.10 = f32[512,512]{1,0:T(8,128)} fusion(bf16[512,1024]{1,0:T(8,128)(2,1)S(1)} %bitcast.22, bf16[1024,512]{1,0:T(8,128)(2,1)} %constant_dynamic-update-slice_fusion.12), kind=kOutput, calls=%fused_computation.46 | convolution fusion | flops 536870912 | bytes 3145728 | tf_op jit(solution)/shard_map/dot_general | solution.py:48
  129.5 8.8 %all-to-all-done.1 = bf16[4,128,1024]{2,1,0:T(8,128)(2,1)S(1)} async-done(((bf16[4,128,1024]{2,1,0:T(8,128)(2,1)}), bf16[4,128,1024]{2,1,0:T(8,128)(2,1)S(1)}, u32[]{:S(2)}, u32[]{:S(2)}) %all-to-all-start.1) | async-done | bytes 1048608 | tf_op jit(solution)/shard_map/all_to_all | solution.py:34
  138.3 1.9 %convolution_add_fusion.1 = f32[512,512]{1,0:T(8,128)S(1)} fusion(f32[512,512]{1,0:T(8,128)} %fusion.10, bf16[512,1024]{1,0:T(8,128)(2,1)S(1)} %bitcast.19, bf16[1024,512]{1,0:T(8,128)(2,1)S(1)} %pad_maximum_fusion), kind=kOutput, calls=%fused_computation.3 | convolution fusion | flops 537133056 | bytes 4194304 | tf_op jit(solution)/shard_map/dot_general | solution.py:48
  140.3 4.4 %collective-permute-start.14 = (f32[256,512]{1,0:T(8,128)S(1)}, f32[256,512]{1,0:T(8,128)S(1)}, u32[]{:S(2)}, u32[]{:S(2)}) collective-permute-start(f32[256,512]{1,0:T(8,128)S(1)} %constant_dynamic-slice_fusion.1), channel_id=1, source_target_pairs={{0,16},{16,0},{1,17},{17,1},{2,18},{18,2},{3,19},{19,3},{4,20},{20... | collective-permute-start | bytes 1572872 | tf_op jit(solution)/shard_map/ppermute | solution.py:21
  144.7 1.5 collective-permute-done.14
  146.2 0.1 fusion.8
  146.3 4.4 %collective-permute-start.17 = (bf16[256,512]{1,0:T(8,128)(2,1)S(1)}, bf16[256,512]{1,0:T(8,128)(2,1)S(1)}, u32[]{:S(2)}, u32[]{:S(2)}) collective-permute-start(bf16[256,512]{1,0:T(8,128)(2,1)S(1)} %fusion.8), channel_id=1, source_target_pairs={{0,64},{64,128},{128,192},{192,0},{1,65},{65,129},{129,193},{193,1... | collective-permute-start | bytes 786440 | tf_op jit(solution)/shard_map/ppermute | solution.py:25
  150.7 1.3 collective-permute-start.16
  152.0 1.2 collective-permute-start.15
  153.2 2.1 %collective-permute-start.18 = (bf16[256,512]{1,0:T(8,128)(2,1)S(1)}, bf16[256,512]{1,0:T(8,128)(2,1)S(1)}, u32[]{:S(2)}, u32[]{:S(2)}) collective-permute-start(bf16[256,512]{1,0:T(8,128)(2,1)S(1)} %fusion.8), channel_id=1, source_target_pairs={{0,32},{32,0},{1,33},{33,1},{2,34},{34,2},{3,35},{35,3},{4,36},{36... | collective-permute-start | bytes 786440 | tf_op jit(solution)/shard_map/ppermute | solution.py:21
  155.3 1.9 %collective-permute-done.17 = bf16[256,512]{1,0:T(8,128)(2,1)S(1)} collective-permute-done((bf16[256,512]{1,0:T(8,128)(2,1)S(1)}, bf16[256,512]{1,0:T(8,128)(2,1)S(1)}, u32[]{:S(2)}, u32[]{:S(2)}) %collective-permute-start.17) | collective-permute-done | bytes 262176 | tf_op jit(solution)/shard_map/ppermute | solution.py:25
  157.2 6.5 %collective-permute-done.16 = bf16[256,512]{1,0:T(8,128)(2,1)S(1)} collective-permute-done((bf16[256,512]{1,0:T(8,128)(2,1)S(1)}, bf16[256,512]{1,0:T(8,128)(2,1)S(1)}, u32[]{:S(2)}, u32[]{:S(2)}) %collective-permute-start.16) | collective-permute-done | bytes 262176 | tf_op jit(solution)/shard_map/ppermute | solution.py:25
  163.7 0.1 pad_maximum_fusion.1
  163.8 1.7 collective-permute-start.21
  165.5 2.2 %collective-permute-start.20 = (bf16[256,512]{1,0:T(8,128)(2,1)S(1)}, bf16[256,512]{1,0:T(8,128)(2,1)S(1)}, u32[]{:S(2)}, u32[]{:S(2)}) collective-permute-start(bf16[256,512]{1,0:T(8,128)(2,1)S(1)} %collective-permute-done.18), channel_id=1, source_target_pairs={{0,128},{64,192},{128,0},{192,64},{1,129},{65,193},{129,1},{193,65... | collective-permute-start | bytes 786440 | tf_op jit(solution)/shard_map/ppermute | solution.py:25
  167.6 0.7 collective-permute-start.19
  168.3 3.3 %collective-permute-done.21 = bf16[256,512]{1,0:T(8,128)(2,1)S(1)} collective-permute-done((bf16[256,512]{1,0:T(8,128)(2,1)S(1)}, bf16[256,512]{1,0:T(8,128)(2,1)S(1)}, u32[]{:S(2)}, u32[]{:S(2)}) %collective-permute-start.21) | collective-permute-done | bytes 262176 | tf_op jit(solution)/shard_map/ppermute | solution.py:25
  171.7 7.5 %collective-permute-done.20 = bf16[256,512]{1,0:T(8,128)(2,1)S(1)} collective-permute-done((bf16[256,512]{1,0:T(8,128)(2,1)S(1)}, bf16[256,512]{1,0:T(8,128)(2,1)S(1)}, u32[]{:S(2)}, u32[]{:S(2)}) %collective-permute-start.20) | collective-permute-done | bytes 262176 | tf_op jit(solution)/shard_map/ppermute | solution.py:25
  179.2 0.7 fusion
  179.9 0.7 convolution_add_fusion
  180.7 1.4 collective-permute-start.22
  182.1 1.5 collective-permute-done.22
  183.6 1.1 add_multiply_fusion
  (39 shorter events, 0.4 us)
Async XLA Ops:
  0.0 10.1 %collective-permute-start.3 = (bf16[256,512]{1,0:T(8,128)(2,1)}, bf16[256,512]{1,0:T(8,128)(2,1)S(1)}, u32[]{:S(2)}, u32[]{:S(2)}) collective-permute-start(bf16[256,512]{1,0:T(8,128)(2,1)} %param.1), channel_id=1, source_target_pairs={{0,64},{64,128},{128,192},{192,0},{1,65},{65,129},{129,193},{193,1... | collective-permute-start | bytes 786440 | tf_op jit(solution)/shard_map/ppermute | solution.py:25
  2.0 14.0 %collective-permute-start.2 = (bf16[256,512]{1,0:T(8,128)(2,1)}, bf16[256,512]{1,0:T(8,128)(2,1)S(1)}, u32[]{:S(2)}, u32[]{:S(2)}) collective-permute-start(bf16[256,512]{1,0:T(8,128)(2,1)} %param.1), channel_id=1, source_target_pairs={{0,128},{64,192},{128,0},{192,64},{1,129},{65,193},{129,1},{193,65... | collective-permute-start | bytes 786440 | tf_op jit(solution)/shard_map/ppermute | solution.py:25
  4.5 11.5 %collective-permute-start.1 = (bf16[256,512]{1,0:T(8,128)(2,1)}, bf16[256,512]{1,0:T(8,128)(2,1)S(1)}, u32[]{:S(2)}, u32[]{:S(2)}) collective-permute-start(bf16[256,512]{1,0:T(8,128)(2,1)} %param.1), channel_id=1, source_target_pairs={{0,192},{64,0},{128,64},{192,128},{1,193},{65,1},{129,65},{193,129... | collective-permute-start | bytes 786440 | tf_op jit(solution)/shard_map/ppermute | solution.py:25
  5.6 11.4 %collective-permute-start.4 = (bf16[256,512]{1,0:T(8,128)(2,1)}, bf16[256,512]{1,0:T(8,128)(2,1)S(1)}, u32[]{:S(2)}, u32[]{:S(2)}) collective-permute-start(bf16[256,512]{1,0:T(8,128)(2,1)} %param.1), channel_id=1, source_target_pairs={{0,32},{32,0},{1,33},{33,1},{2,34},{34,2},{3,35},{35,3},{4,36},{36... | collective-permute-start | bytes 786440 | tf_op jit(solution)/shard_map/ppermute | solution.py:21
  7.3 9.8 %collective-permute-start = (bf16[256,512]{1,0:T(8,128)(2,1)}, bf16[256,512]{1,0:T(8,128)(2,1)S(1)}, u32[]{:S(2)}, u32[]{:S(2)}) collective-permute-start(bf16[256,512]{1,0:T(8,128)(2,1)} %param.1), channel_id=1, source_target_pairs={{0,16},{16,0},{1,17},{17,1},{2,18},{18,2},{3,19},{19,3},{4,20},{20... | collective-permute-start | bytes 786440 | tf_op jit(solution)/shard_map/ppermute | solution.py:21
  10.1 7.1 %copy-start = (bf16[256,512]{1,0:T(8,128)(2,1)S(1)}, bf16[256,512]{1,0:T(8,128)(2,1)}, u32[]{:S(2)}) copy-start(bf16[256,512]{1,0:T(8,128)(2,1)} %param.1) | copy-start | bytes 786436
  19.0 35.6 %all-to-all-start = ((bf16[16,32,1024]{2,1,0:T(8,128)(2,1)}), bf16[16,32,1024]{2,1,0:T(8,128)(2,1)S(1)}, u32[]{:S(2)}, u32[]{:S(2)}) async-start(bf16[16,32,1024]{2,1,0:T(8,128)(2,1)} %bitcast.3), calls=%async_computation | async-start | bytes 2097152 | tf_op jit(solution)/shard_map/all_to_all | solution.py:34
  30.0 13.4 %collective-permute-start.8 = (bf16[256,512]{1,0:T(8,128)(2,1)S(1)}, bf16[256,512]{1,0:T(8,128)(2,1)S(1)}, u32[]{:S(2)}, u32[]{:S(2)}) collective-permute-start(bf16[256,512]{1,0:T(8,128)(2,1)S(1)} %collective-permute-done.4), channel_id=1, source_target_pairs={{0,192},{64,0},{128,64},{192,128},{1,193},{65,1},{129,65},{193,129... | collective-permute-start | bytes 786440 | tf_op jit(solution)/shard_map/ppermute | solution.py:25
  33.1 11.1 %collective-permute-start.9 = (bf16[256,512]{1,0:T(8,128)(2,1)S(1)}, bf16[256,512]{1,0:T(8,128)(2,1)S(1)}, u32[]{:S(2)}, u32[]{:S(2)}) collective-permute-start(bf16[256,512]{1,0:T(8,128)(2,1)S(1)} %collective-permute-done.4), channel_id=1, source_target_pairs={{0,128},{64,192},{128,0},{192,64},{1,129},{65,193},{129,1},{193,65... | collective-permute-start | bytes 786440 | tf_op jit(solution)/shard_map/ppermute | solution.py:25
  33.2 14.9 %collective-permute-start.10 = (bf16[256,512]{1,0:T(8,128)(2,1)S(1)}, bf16[256,512]{1,0:T(8,128)(2,1)S(1)}, u32[]{:S(2)}, u32[]{:S(2)}) collective-permute-start(bf16[256,512]{1,0:T(8,128)(2,1)S(1)} %collective-permute-done.4), channel_id=1, source_target_pairs={{0,64},{64,128},{128,192},{192,0},{1,65},{65,129},{129,193},{193,1... | collective-permute-start | bytes 786440 | tf_op jit(solution)/shard_map/ppermute | solution.py:25
  54.6 28.3 %all-to-all-start.2 = ((bf16[16,32,1024]{2,1,0:T(8,128)(2,1)}), bf16[16,32,1024]{2,1,0:T(8,128)(2,1)S(1)}, u32[]{:S(2)}, u32[]{:S(2)}) async-start(bf16[16,32,1024]{2,1,0:T(8,128)(2,1)} %bitcast.24), calls=%async_computation.2 | async-start | bytes 2097152 | tf_op jit(solution)/shard_map/all_to_all | solution.py:34
  62.5 46.7 %collective-permute-start.7 = (bf16[32,1024]{1,0:T(8,128)(2,1)S(1)}, bf16[32,1024]{1,0:T(8,128)(2,1)S(1)}, u32[]{:S(2)}, u32[]{:S(2)}) collective-permute-start(bf16[32,1024]{1,0:T(8,128)(2,1)S(1)} %reduce_sum.24), channel_id=1, source_target_pairs={{0,4},{4,8},{8,12},{12,0},{1,5},{5,9},{9,13},{13,1},{2,6},{6,10},{... | collective-permute-start | bytes 196616 | tf_op jit(solution)/shard_map/ppermute | solution.py:25
  64.9 44.4 %collective-permute-start.6 = (bf16[32,1024]{1,0:T(8,128)(2,1)S(1)}, bf16[32,1024]{1,0:T(8,128)(2,1)S(1)}, u32[]{:S(2)}, u32[]{:S(2)}) collective-permute-start(bf16[32,1024]{1,0:T(8,128)(2,1)S(1)} %reduce_sum.24), channel_id=1, source_target_pairs={{0,8},{4,12},{8,0},{12,4},{1,9},{5,13},{9,1},{13,5},{2,10},{6,14},... | collective-permute-start | bytes 196616 | tf_op jit(solution)/shard_map/ppermute | solution.py:25
  68.1 41.0 %collective-permute-start.5 = (bf16[32,1024]{1,0:T(8,128)(2,1)S(1)}, bf16[32,1024]{1,0:T(8,128)(2,1)S(1)}, u32[]{:S(2)}, u32[]{:S(2)}) collective-permute-start(bf16[32,1024]{1,0:T(8,128)(2,1)S(1)} %reduce_sum.24), channel_id=1, source_target_pairs={{0,12},{4,0},{8,4},{12,8},{1,13},{5,1},{9,5},{13,9},{2,14},{6,2},{... | collective-permute-start | bytes 196616 | tf_op jit(solution)/shard_map/ppermute | solution.py:25
  83.1 21.1 %collective-permute-start.13 = (bf16[32,1024]{1,0:T(8,128)(2,1)S(1)}, bf16[32,1024]{1,0:T(8,128)(2,1)S(1)}, u32[]{:S(2)}, u32[]{:S(2)}) collective-permute-start(bf16[32,1024]{1,0:T(8,128)(2,1)S(1)} %reduce_sum.25), channel_id=1, source_target_pairs={{0,4},{4,8},{8,12},{12,0},{1,5},{5,9},{9,13},{13,1},{2,6},{6,10},{... | collective-permute-start | bytes 196616 | tf_op jit(solution)/shard_map/ppermute | solution.py:25
  83.2 13.0 %collective-permute-start.11 = (bf16[32,1024]{1,0:T(8,128)(2,1)S(1)}, bf16[32,1024]{1,0:T(8,128)(2,1)S(1)}, u32[]{:S(2)}, u32[]{:S(2)}) collective-permute-start(bf16[32,1024]{1,0:T(8,128)(2,1)S(1)} %reduce_sum.25), channel_id=1, source_target_pairs={{0,12},{4,0},{8,4},{12,8},{1,13},{5,1},{9,5},{13,9},{2,14},{6,2},{... | collective-permute-start | bytes 196616 | tf_op jit(solution)/shard_map/ppermute | solution.py:25
  96.2 8.0 %collective-permute-start.12 = (bf16[32,1024]{1,0:T(8,128)(2,1)S(1)}, bf16[32,1024]{1,0:T(8,128)(2,1)S(1)}, u32[]{:S(2)}, u32[]{:S(2)}) collective-permute-start(bf16[32,1024]{1,0:T(8,128)(2,1)S(1)} %reduce_sum.25), channel_id=1, source_target_pairs={{0,8},{4,12},{8,0},{12,4},{1,9},{5,13},{9,1},{13,5},{2,10},{6,14},... | collective-permute-start | bytes 196616 | tf_op jit(solution)/shard_map/ppermute | solution.py:25
  105.5 16.4 %all-to-all-start.3 = ((bf16[4,128,1024]{2,1,0:T(8,128)(2,1)}), bf16[4,128,1024]{2,1,0:T(8,128)(2,1)S(1)}, u32[]{:S(2)}, u32[]{:S(2)}) async-start(bf16[4,128,1024]{2,1,0:T(8,128)(2,1)} %broadcast_in_dim.5), calls=%async_computation.3 | async-start | bytes 2097152 | tf_op jit(solution)/shard_map/all_to_all | solution.py:34
  121.9 4.7 %copy-start.1 = (bf16[4,128,1024]{2,1,0:T(8,128)(2,1)}, bf16[4,128,1024]{2,1,0:T(8,128)(2,1)S(1)}, u32[]{:S(2)}) copy-start(bf16[4,128,1024]{2,1,0:T(8,128)(2,1)S(1)} %all-to-all-done.3) | copy-start | bytes 3145732
  123.1 15.2 %all-to-all-start.1 = ((bf16[4,128,1024]{2,1,0:T(8,128)(2,1)}), bf16[4,128,1024]{2,1,0:T(8,128)(2,1)S(1)}, u32[]{:S(2)}, u32[]{:S(2)}) async-start(bf16[4,128,1024]{2,1,0:T(8,128)(2,1)} %broadcast_in_dim.4), calls=%async_computation.1 | async-start | bytes 2097152 | tf_op jit(solution)/shard_map/all_to_all | solution.py:34
  140.3 6.0 %collective-permute-start.14 = (f32[256,512]{1,0:T(8,128)S(1)}, f32[256,512]{1,0:T(8,128)S(1)}, u32[]{:S(2)}, u32[]{:S(2)}) collective-permute-start(f32[256,512]{1,0:T(8,128)S(1)} %constant_dynamic-slice_fusion.1), channel_id=1, source_target_pairs={{0,16},{16,0},{1,17},{17,1},{2,18},{18,2},{3,19},{19,3},{4,20},{20... | collective-permute-start | bytes 1572872 | tf_op jit(solution)/shard_map/ppermute | solution.py:21
  146.3 32.8 %copy-start.2 = (bf16[4,128,1024]{2,1,0:T(8,128)(2,1)S(1)}, bf16[4,128,1024]{2,1,0:T(8,128)(2,1)}, u32[]{:S(2)}) copy-start(bf16[4,128,1024]{2,1,0:T(8,128)(2,1)} %copy-done.1) | copy-start | bytes 3145732
  146.3 10.9 %collective-permute-start.17 = (bf16[256,512]{1,0:T(8,128)(2,1)S(1)}, bf16[256,512]{1,0:T(8,128)(2,1)S(1)}, u32[]{:S(2)}, u32[]{:S(2)}) collective-permute-start(bf16[256,512]{1,0:T(8,128)(2,1)S(1)} %fusion.8), channel_id=1, source_target_pairs={{0,64},{64,128},{128,192},{192,0},{1,65},{65,129},{129,193},{193,1... | collective-permute-start | bytes 786440 | tf_op jit(solution)/shard_map/ppermute | solution.py:25
  150.7 13.0 %collective-permute-start.16 = (bf16[256,512]{1,0:T(8,128)(2,1)S(1)}, bf16[256,512]{1,0:T(8,128)(2,1)S(1)}, u32[]{:S(2)}, u32[]{:S(2)}) collective-permute-start(bf16[256,512]{1,0:T(8,128)(2,1)S(1)} %fusion.8), channel_id=1, source_target_pairs={{0,128},{64,192},{128,0},{192,64},{1,129},{65,193},{129,1},{193,65... | collective-permute-start | bytes 786440 | tf_op jit(solution)/shard_map/ppermute | solution.py:25
  152.0 11.7 %collective-permute-start.15 = (bf16[256,512]{1,0:T(8,128)(2,1)S(1)}, bf16[256,512]{1,0:T(8,128)(2,1)S(1)}, u32[]{:S(2)}, u32[]{:S(2)}) collective-permute-start(bf16[256,512]{1,0:T(8,128)(2,1)S(1)} %fusion.8), channel_id=1, source_target_pairs={{0,192},{64,0},{128,64},{192,128},{1,193},{65,1},{129,65},{193,129... | collective-permute-start | bytes 786440 | tf_op jit(solution)/shard_map/ppermute | solution.py:25
  153.2 10.6 %collective-permute-start.18 = (bf16[256,512]{1,0:T(8,128)(2,1)S(1)}, bf16[256,512]{1,0:T(8,128)(2,1)S(1)}, u32[]{:S(2)}, u32[]{:S(2)}) collective-permute-start(bf16[256,512]{1,0:T(8,128)(2,1)S(1)} %fusion.8), channel_id=1, source_target_pairs={{0,32},{32,0},{1,33},{33,1},{2,34},{34,2},{3,35},{35,3},{4,36},{36... | collective-permute-start | bytes 786440 | tf_op jit(solution)/shard_map/ppermute | solution.py:21
  163.8 7.9 %collective-permute-start.21 = (bf16[256,512]{1,0:T(8,128)(2,1)S(1)}, bf16[256,512]{1,0:T(8,128)(2,1)S(1)}, u32[]{:S(2)}, u32[]{:S(2)}) collective-permute-start(bf16[256,512]{1,0:T(8,128)(2,1)S(1)} %collective-permute-done.18), channel_id=1, source_target_pairs={{0,64},{64,128},{128,192},{192,0},{1,65},{65,129},{129,193},{193,1... | collective-permute-start | bytes 786440 | tf_op jit(solution)/shard_map/ppermute | solution.py:25
  165.5 13.7 %collective-permute-start.20 = (bf16[256,512]{1,0:T(8,128)(2,1)S(1)}, bf16[256,512]{1,0:T(8,128)(2,1)S(1)}, u32[]{:S(2)}, u32[]{:S(2)}) collective-permute-start(bf16[256,512]{1,0:T(8,128)(2,1)S(1)} %collective-permute-done.18), channel_id=1, source_target_pairs={{0,128},{64,192},{128,0},{192,64},{1,129},{65,193},{129,1},{193,65... | collective-permute-start | bytes 786440 | tf_op jit(solution)/shard_map/ppermute | solution.py:25
  167.6 11.5 %collective-permute-start.19 = (bf16[256,512]{1,0:T(8,128)(2,1)S(1)}, bf16[256,512]{1,0:T(8,128)(2,1)S(1)}, u32[]{:S(2)}, u32[]{:S(2)}) collective-permute-start(bf16[256,512]{1,0:T(8,128)(2,1)S(1)} %collective-permute-done.18), channel_id=1, source_target_pairs={{0,192},{64,0},{128,64},{192,128},{1,193},{65,1},{129,65},{193,129... | collective-permute-start | bytes 786440 | tf_op jit(solution)/shard_map/ppermute | solution.py:25
  180.7 3.0 %collective-permute-start.22 = (f32[256,512]{1,0:T(8,128)S(1)}, f32[256,512]{1,0:T(8,128)S(1)}, u32[]{:S(2)}, u32[]{:S(2)}) collective-permute-start(f32[256,512]{1,0:T(8,128)S(1)} %constant_dynamic-slice_fusion), channel_id=1, source_target_pairs={{0,16},{16,0},{1,17},{17,1},{2,18},{18,2},{3,19},{19,3},{4,20},{20... | collective-permute-start | bytes 1572872 | tf_op jit(solution)/shard_map/ppermute | solution.py:21

commit v7 on v3

v7 whole, which is shorter than its diff:
```python
import math

import jax
import jax.numpy as jnp
from jax import lax
from jax.sharding import Mesh
from jax.sharding import PartitionSpec as P

COLS = 8192

coef_a = 3.4445
coef_b = -4.775
coef_c = 2.0315

ROW = ("x", "zl", "core")
COL = ("zh", "y")
BF, F32 = jnp.bfloat16, jnp.float32


def swap(array, axis):
    return lax.ppermute(array, axis, [(0, 1), (1, 0)])


def send(array, axis, k):
    return lax.ppermute(array, axis, [(i, (i + k) % 4) for i in range(4)]) if k else array


def fetch(array, axis, k):
    return send(array, axis, (4 - k) % 4)


def scatter_sum(pieces, axis):
    got = [send(pieces[k], axis, k).astype(F32) for k in (0, 1, 3, 2)]
    return ((got[0] + got[1]) + (got[2] + got[3])).astype(BF)


def around(array, axis):
    return [array] + [fetch(array, axis, k) for k in (1, 2, 3)]


def around_ring(array, axis):
    half = array.shape[0] // 2
    after, before = fetch(array, axis, 1), fetch(array, axis, 3)
    far = [fetch(after[:half], axis, 1), fetch(before[half:], axis, 3)]
    return [array, after, jnp.concatenate(far, axis=0), before]


def chunks(array):
    return jnp.split(array, 4, axis=0)


def window(parts, first, count):
    rows = parts[0].shape[0]
    ring = jnp.concatenate([*parts, *parts[: count - 1]], axis=0)
    return lax.dynamic_slice_in_dim(ring, first * rows, count * rows, 0)


def matmul(a, b, dims):
    return lax.dot_general(a, b, (dims, ((), ())), preferred_element_type=F32)


def panel_of(block):
    partner = swap(block, "zl")
    mine = around(block, "x")
    theirs = [partner, fetch(partner, "x", 1), swap(mine[2], "zl"), fetch(partner, "x", 3)]
    return jnp.concatenate([*mine, *theirs], axis=0)


def apply(gram, panel):
    other = swap(matmul(gram[1], panel, ((1,), (0,))), "core")
    return matmul(gram[0], panel, ((1,), (0,))) + other


def per_device(iterate):
    core, y, zh = (lax.axis_index(a) for a in ("core", "y", "zh"))
    other = swap(iterate, "core")
    panel = panel_of(iterate)
    halves = [*jnp.split(iterate, 2), *jnp.split(other, 2)]
    own = window(halves, lax.rem(y - 2 * core + 4, 4), 4)
    own = [window(chunks(rows), zh, 4) for rows in chunks(own)]
    pieces = [matmul(rows, panel, ((1,), (1,))).astype(BF) for rows in own]
    part = scatter_sum(pieces, "y")
    part = scatter_sum(chunks(part), "zh")
    rows = window(around(part, "zh"), lax.rem(4 - zh, 4), 4)
    ring = around_ring(rows, "y")
    first = lax.rem(2 * core - y + 4, 4)
    gram = window(ring, first, 2), window(ring, lax.rem(first + 2, 4), 2)
    inner = apply(gram, panel)
    mixed = apply(gram, panel_of(inner.astype(BF)))
    mine = iterate.astype(F32)
    return math.sqrt(COLS) * (coef_a * mine + (coef_b * inner + coef_c * mixed))


def solution(mesh):
    fine = Mesh(mesh.devices.reshape(4, 2, 2, 4, 4), (*ROW, *COL))
    placed = P(ROW, COL)
    return jax.shard_map(
        per_device, mesh=fine, in_specs=(placed,), out_specs=placed, check_vma=False
    )
```

time: 153 us -> 152 us (level)
  starting transfers between devices: 75.5 us -> 57.7 us
  waiting for transfers between devices: 56.4 us -> 73.6 us
  local copies, waits for them, and re-layouts: 5.57 us -> 8.89 us
  matrix products: 12.1 us -> 9.36 us
    ppermute x36 -> x23, starting transfers between devices: 59.6 us -> 37.3 us  [send(): lax.ppermute(array, axis, [(i, (i + k) % 4) for i in range(4)])]
    ppermute x36 -> x23, waiting for transfers between devices: 52.9 us -> 69.1 us  [send(): lax.ppermute(array, axis, [(i, (i + k) % 4) for i in range(4)])]
    ppermute x5 -> x7, starting transfers between devices: 16 us -> 20.4 us  [swap(): return lax.ppermute(array, axis, [(0, 1), (1, 0)])]
    unnamed x35 -> x29, local copies, waits for them, and re-layouts: 3.7 us -> 7.16 us
    dot_general x16 -> x8, matrix products: 12.1 us -> 9.36 us  [matmul(): return lax.dot_general(a, b, (dims, ((), ())), preferred_element_type=F32)]
    ppermute x5 -> x7, waiting for transfers between devices: 3.49 us -> 4.47 us  [swap(): return lax.ppermute(array, axis, [(0, 1), (1, 0)])]
  transfers between devices with their start and end apart: 41 -> 30, of which waited for: 17 -> 23; matrix products, arithmetic and copies ran while one was open for 9% -> 5% of each run, Pallas kernels for 0% -> 0%
where the time goes in v7:
time: 152 us
  waiting for transfers between devices  73.6 us (48%)
  starting transfers between devices  57.7 us (38%)
  matrix products  9.36 us (6%)
  local copies, waits for them, and re-layouts  8.89 us (6%)
  other arithmetic  2.13 us (1%)
    ppermute x23, waiting for transfers between devices, send(): lax.ppermute(array, axis, [(i, (i + k) % 4) for i in range(4)])  69.1 us
    ppermute x23, starting transfers between devices, send(): lax.ppermute(array, axis, [(i, (i + k) % 4) for i in range(4)])  37.3 us
    ppermute x7, starting transfers between devices, swap(): return lax.ppermute(array, axis, [(0, 1), (1, 0)])  20.4 us
    dot_general x8, matrix products, matmul(): return lax.dot_general(a, b, (dims, ((), ())), preferred_element_type=F32)  9.36 us
    unnamed x29, local copies, waits for them, and re-layouts  7.16 us
    ppermute x7, waiting for transfers between devices, swap(): return lax.ppermute(array, axis, [(0, 1), (1, 0)])  4.47 us
  transfers between devices with their start and end apart: 30, of which 23 were waited for; matrix products, arithmetic and copies ran while one was open for 5% of the time, Pallas kernels for 0%

profile of v7, /device:TPU:1, one launch (start us, length us, event | category | flops | bytes accessed | tf_op | source)
XLA Modules:
  0.0 152.0 jit_solution(5188326440085129908)
XLA Ops:
  0.0 3.2 %collective-permute-start = (bf16[256,512]{1,0:T(8,128)(2,1)}, bf16[256,512]{1,0:T(8,128)(2,1)S(1)}, u32[]{:S(2)}, u32[]{:S(2)}) collective-permute-start(bf16[256,512]{1,0:T(8,128)(2,1)} %param.1), channel_id=1, source_target_pairs={{0,16},{16,0},{1,17},{17,1},{2,18},{18,2},{3,19},{19,3},{4,20},{20... | collective-permute-start | bytes 786440 | tf_op jit(solution)/shard_map/ppermute | solution.py:21
  3.2 2.6 %collective-permute-start.2 = (bf16[256,512]{1,0:T(8,128)(2,1)}, bf16[256,512]{1,0:T(8,128)(2,1)S(1)}, u32[]{:S(2)}, u32[]{:S(2)}) collective-permute-start(bf16[256,512]{1,0:T(8,128)(2,1)} %param.1), channel_id=1, source_target_pairs={{0,128},{64,192},{128,0},{192,64},{1,129},{65,193},{129,1},{193,65... | collective-permute-start | bytes 786440 | tf_op jit(solution)/shard_map/ppermute | solution.py:25
  5.9 0.9 collective-permute-start.1
  6.7 0.6 collective-permute-start.3
  7.4 1.0 constant_dynamic-update-slice_fusion.7
  8.4 2.1 %fusion.13 = bf16[512,512]{1,0:T(8,128)(2,1)S(1)} fusion(s32[]{:T(128)S(6)} %select_n.18, bf16[256,512]{1,0:T(8,128)(2,1)} %param.1, bf16[256,512]{1,0:T(8,128)(2,1)S(1)} %collective-permute-done, bf16[128,512]{1,0:T(8,128)(2,1)S(1)} %split.67), kind=kLoop, calls=%fused_computation.23 | loop fusion | flops 2097152 | bytes 1179652 | tf_op jit(solution)/shard_map/concatenate | solution.py:54
  10.5 0.9 collective-permute-done.4
  11.4 1.3 collective-permute-start.5
  12.9 1.2 collective-permute-start.6
  14.1 4.1 %collective-permute-done.1 = bf16[256,512]{1,0:T(8,128)(2,1)S(1)} collective-permute-done((bf16[256,512]{1,0:T(8,128)(2,1)}, bf16[256,512]{1,0:T(8,128)(2,1)S(1)}, u32[]{:S(2)}, u32[]{:S(2)}) %collective-permute-start.1) | collective-permute-done | bytes 262176 | tf_op jit(solution)/shard_map/ppermute | solution.py:25
  18.3 0.5 collective-permute-done.3
  18.9 5.0 %collective-permute-done.5 = bf16[256,512]{1,0:T(8,128)(2,1)S(1)} collective-permute-done((bf16[256,512]{1,0:T(8,128)(2,1)S(1)}, bf16[256,512]{1,0:T(8,128)(2,1)S(1)}, u32[]{:S(2)}, u32[]{:S(2)}) %collective-permute-start.5) | collective-permute-done | bytes 262176 | tf_op jit(solution)/shard_map/ppermute | solution.py:25
  23.9 0.5 collective-permute-done.7
  24.4 0.8 convolution_convert_fusion.2
  25.3 1.3 collective-permute-start.8
  26.5 0.8 convolution_convert_fusion.1
  27.3 1.6 %collective-permute-start.9 = (bf16[128,2048]{1,0:T(8,128)(2,1)S(1)}, bf16[128,2048]{1,0:T(8,128)(2,1)S(1)}, u32[]{:S(2)}, u32[]{:S(2)}) collective-permute-start(bf16[128,2048]{1,0:T(8,128)(2,1)S(1)} %convolution_convert_fusion.1), channel_id=1, source_target_pairs={{0,3},{1,0},{2,1},{3,2},{4,7},{5,4},{6,5},{7,6},{8,11},{9,8},{10,9... | collective-permute-start | bytes 1572872 | tf_op jit(solution)/shard_map/ppermute | solution.py:25
  28.9 0.8 convolution_convert_fusion
  29.7 1.7 %collective-permute-start.10 = (bf16[128,2048]{1,0:T(8,128)(2,1)S(1)}, bf16[128,2048]{1,0:T(8,128)(2,1)S(1)}, u32[]{:S(2)}, u32[]{:S(2)}) collective-permute-start(bf16[128,2048]{1,0:T(8,128)(2,1)S(1)} %convolution_convert_fusion), channel_id=1, source_target_pairs={{0,2},{1,3},{2,0},{3,1},{4,6},{5,7},{6,4},{7,5},{8,10},{9,11},{10,... | collective-permute-start | bytes 1572872 | tf_op jit(solution)/shard_map/ppermute | solution.py:25
  31.4 8.0 %collective-permute-done.8 = bf16[128,2048]{1,0:T(8,128)(2,1)S(1)} collective-permute-done((bf16[128,2048]{1,0:T(8,128)(2,1)S(1)}, bf16[128,2048]{1,0:T(8,128)(2,1)S(1)}, u32[]{:S(2)}, u32[]{:S(2)}) %collective-permute-start.8) | collective-permute-done | bytes 524320 | tf_op jit(solution)/shard_map/ppermute | solution.py:25
  39.4 0.4 collective-permute-done.9
  39.9 11.8 %collective-permute-done.10 = bf16[128,2048]{1,0:T(8,128)(2,1)S(1)} collective-permute-done((bf16[128,2048]{1,0:T(8,128)(2,1)S(1)}, bf16[128,2048]{1,0:T(8,128)(2,1)S(1)}, u32[]{:S(2)}, u32[]{:S(2)}) %collective-permute-start.10) | collective-permute-done | bytes 524320 | tf_op jit(solution)/shard_map/ppermute | solution.py:25
  51.7 0.8 fusion.3
  52.6 3.1 %collective-permute-start.11 = (bf16[32,2048]{1,0:T(8,128)(2,1)S(1)}, bf16[32,2048]{1,0:T(8,128)(2,1)S(1)}, u32[]{:S(2)}, u32[]{:S(2)}) collective-permute-start(bf16[32,2048]{1,0:T(8,128)(2,1)S(1)} %get-tuple-element.11), channel_id=1, source_target_pairs={{0,4},{4,8},{8,12},{12,0},{1,5},{5,9},{9,13},{13,1},{2,6},{6,10},{... | collective-permute-start | bytes 393224 | tf_op jit(solution)/shard_map/ppermute | solution.py:25
  55.6 2.4 %collective-permute-start.12 = (bf16[32,2048]{1,0:T(8,128)(2,1)S(1)}, bf16[32,2048]{1,0:T(8,128)(2,1)S(1)}, u32[]{:S(2)}, u32[]{:S(2)}) collective-permute-start(bf16[32,2048]{1,0:T(8,128)(2,1)S(1)} %get-tuple-element.13), channel_id=1, source_target_pairs={{0,12},{4,0},{8,4},{12,8},{1,13},{5,1},{9,5},{13,9},{2,14},{6,2},{... | collective-permute-start | bytes 393224 | tf_op jit(solution)/shard_map/ppermute | solution.py:25
  58.0 4.2 %collective-permute-start.13 = (bf16[32,2048]{1,0:T(8,128)(2,1)S(1)}, bf16[32,2048]{1,0:T(8,128)(2,1)S(1)}, u32[]{:S(2)}, u32[]{:S(2)}) collective-permute-start(bf16[32,2048]{1,0:T(8,128)(2,1)S(1)} %get-tuple-element.12), channel_id=1, source_target_pairs={{0,8},{4,12},{8,0},{12,4},{1,9},{5,13},{9,1},{13,5},{2,10},{6,14},... | collective-permute-start | bytes 393224 | tf_op jit(solution)/shard_map/ppermute | solution.py:25
  62.2 3.1 %collective-permute-done.12 = bf16[32,2048]{1,0:T(8,128)(2,1)S(1)} collective-permute-done((bf16[32,2048]{1,0:T(8,128)(2,1)S(1)}, bf16[32,2048]{1,0:T(8,128)(2,1)S(1)}, u32[]{:S(2)}, u32[]{:S(2)}) %collective-permute-start.12) | collective-permute-done | bytes 131104 | tf_op jit(solution)/shard_map/ppermute | solution.py:25
  65.3 5.6 %collective-permute-done.13 = bf16[32,2048]{1,0:T(8,128)(2,1)S(1)} collective-permute-done((bf16[32,2048]{1,0:T(8,128)(2,1)S(1)}, bf16[32,2048]{1,0:T(8,128)(2,1)S(1)}, u32[]{:S(2)}, u32[]{:S(2)}) %collective-permute-start.13) | collective-permute-done | bytes 131104 | tf_op jit(solution)/shard_map/ppermute | solution.py:25
  71.1 2.1 %collective-permute-start.15 = (bf16[32,2048]{1,0:T(8,128)(2,1)S(1)}, bf16[32,2048]{1,0:T(8,128)(2,1)S(1)}, u32[]{:S(2)}, u32[]{:S(2)}) collective-permute-start(bf16[32,2048]{1,0:T(8,128)(2,1)S(1)} %get-tuple-element.10), channel_id=1, source_target_pairs={{0,8},{4,12},{8,0},{12,4},{1,9},{5,13},{9,1},{13,5},{2,10},{6,14},... | collective-permute-start | bytes 393224 | tf_op jit(solution)/shard_map/ppermute | solution.py:25
  73.2 2.3 %collective-permute-start.16 = (bf16[32,2048]{1,0:T(8,128)(2,1)S(1)}, bf16[32,2048]{1,0:T(8,128)(2,1)S(1)}, u32[]{:S(2)}, u32[]{:S(2)}) collective-permute-start(bf16[32,2048]{1,0:T(8,128)(2,1)S(1)} %get-tuple-element.10), channel_id=1, source_target_pairs={{0,4},{4,8},{8,12},{12,0},{1,5},{5,9},{9,13},{13,1},{2,6},{6,10},{... | collective-permute-start | bytes 393224 | tf_op jit(solution)/shard_map/ppermute | solution.py:25
  75.5 0.4 collective-permute-done.14
  75.9 3.1 %collective-permute-done.15 = bf16[32,2048]{1,0:T(8,128)(2,1)S(1)} collective-permute-done((bf16[32,2048]{1,0:T(8,128)(2,1)S(1)}, bf16[32,2048]{1,0:T(8,128)(2,1)S(1)}, u32[]{:S(2)}, u32[]{:S(2)}) %collective-permute-start.15) | collective-permute-done | bytes 131104 | tf_op jit(solution)/shard_map/ppermute | solution.py:25
  79.0 5.2 %collective-permute-done.16 = bf16[32,2048]{1,0:T(8,128)(2,1)S(1)} collective-permute-done((bf16[32,2048]{1,0:T(8,128)(2,1)S(1)}, bf16[32,2048]{1,0:T(8,128)(2,1)S(1)}, u32[]{:S(2)}, u32[]{:S(2)}) %collective-permute-start.16) | collective-permute-done | bytes 131104 | tf_op jit(solution)/shard_map/ppermute | solution.py:25
  84.3 0.9 constant_dynamic-update-slice_fusion.20
  85.2 1.5 collective-permute-start.19
  86.7 8.6 %collective-permute-done.17 = bf16[128,2048]{1,0:T(8,128)(2,1)S(1)} collective-permute-done((bf16[128,2048]{1,0:T(8,128)(2,1)S(1)}, bf16[128,2048]{1,0:T(8,128)(2,1)S(1)}, u32[]{:S(2)}, u32[]{:S(2)}) %collective-permute-start.17) | collective-permute-done | bytes 524320 | tf_op jit(solution)/shard_map/ppermute | solution.py:25
  95.3 0.8 copy-done.2
  96.1 0.7 slice.35
  96.8 1.5 %collective-permute-start.20 = (bf16[64,2048]{1,0:T(8,128)(2,1)S(1)}, bf16[64,2048]{1,0:T(8,128)(2,1)S(1)}, u32[]{:S(2)}, u32[]{:S(2)}) collective-permute-start(bf16[64,2048]{1,0:T(8,128)(2,1)S(1)} %slice.36), channel_id=1, source_target_pairs={{0,1},{1,2},{2,3},{3,0},{4,5},{5,6},{6,7},{7,4},{8,9},{9,10},{10,1... | collective-permute-start | bytes 786440 | tf_op jit(solution)/shard_map/ppermute | solution.py:25
  98.4 1.9 %constant_dynamic-update-slice_fusion.19 = bf16[640,2048]{1,0:T(8,128)(2,1)} fusion(bf16[640,2048]{1,0:T(8,128)(2,1)} %get-tuple-element.7, bf16[128,2048]{1,0:T(8,128)(2,1)} %copy-done.2), kind=kLoop, calls=%fused_computation.57 | loop fusion | bytes 1048576
  100.3 2.0 %collective-permute-done.18 = bf16[64,2048]{1,0:T(8,128)(2,1)S(1)} collective-permute-done((bf16[64,2048]{1,0:T(8,128)(2,1)}, bf16[64,2048]{1,0:T(8,128)(2,1)S(1)}, u32[]{:S(2)}, u32[]{:S(2)}) %collective-permute-start.18) | collective-permute-done | bytes 262176 | tf_op jit(solution)/shard_map/ppermute | solution.py:25
  102.2 0.7 constant_dynamic-update-slice_fusion.18
  102.9 0.4 collective-permute-done.20
  103.3 0.7 constant_dynamic-update-slice_fusion.17
  104.1 0.8 constant_dynamic-update-slice_fusion.16
  104.9 0.8 constant_dynamic-update-slice_fusion.15
  105.7 1.9 %fusion.7 = f32[256,512]{1,0:T(8,128)S(1)} fusion(bf16[2048,512]{1,0:T(8,128)(2,1)S(1)} %constant_dynamic-update-slice_fusion, bf16[640,2048]{1,0:T(8,128)(2,1)} %constant_dynamic-update-slice_fusion.15, s32[]{:T(128)S(6)} %select_n.22), kind=kOutput, calls=%fused_computation.13 | convolution fusion | flops 536870912 | bytes 3670020 | tf_op jit(solution)/shard_map/dot_general | solution.py:59
  107.7 7.0 %collective-permute-start.21 = (f32[256,512]{1,0:T(8,128)S(1)}, f32[256,512]{1,0:T(8,128)S(1)}, u32[]{:S(2)}, u32[]{:S(2)}) collective-permute-start(f32[256,512]{1,0:T(8,128)S(1)} %fusion.7), channel_id=1, source_target_pairs={{0,16},{16,0},{1,17},{17,1},{2,18},{18,2},{3,19},{19,3},{4,20},{20... | collective-permute-start | bytes 1572872 | tf_op jit(solution)/shard_map/ppermute | solution.py:21
  114.6 1.5 %collective-permute-done.21 = f32[256,512]{1,0:T(8,128)S(1)} collective-permute-done((f32[256,512]{1,0:T(8,128)S(1)}, f32[256,512]{1,0:T(8,128)S(1)}, u32[]{:S(2)}, u32[]{:S(2)}) %collective-permute-start.21) | collective-permute-done | bytes 524320 | tf_op jit(solution)/shard_map/ppermute | solution.py:21
  116.2 1.9 %constant_dynamic-update-slice_fusion.28 = (bf16[2048,512]{1,0:T(8,128)(2,1)S(1)}, bf16[256,512]{1,0:T(8,128)(2,1)S(1)}, f32[256,512]{1,0:T(8,128)S(1)}) fusion(f32[256,512]{1,0:T(8,128)S(1)} %collective-permute-done.21, bf16[2048,512]{1,0:T(8,128)(2,1)S(1)} %constant_dynamic-update-slice_fusion, ...), kind=kOutput, calls=%fused_computation.66 | convolution fusion | flops 537133056 | bytes 4718596 | tf_op jit(solution)/shard_map/dot_general | solution.py:59
  118.1 6.4 %collective-permute-start.25 = (bf16[256,512]{1,0:T(8,128)(2,1)S(1)}, bf16[256,512]{1,0:T(8,128)(2,1)S(1)}, u32[]{:S(2)}, u32[]{:S(2)}) collective-permute-start(bf16[256,512]{1,0:T(8,128)(2,1)S(1)} %get-tuple-element.6), channel_id=1, source_target_pairs={{0,32},{32,0},{1,33},{33,1},{2,34},{34,2},{3,35},{35,3},{4,36},{36... | collective-permute-start | bytes 786440 | tf_op jit(solution)/shard_map/ppermute | solution.py:21
  124.6 4.4 %collective-permute-start.23 = (bf16[256,512]{1,0:T(8,128)(2,1)S(1)}, bf16[256,512]{1,0:T(8,128)(2,1)S(1)}, u32[]{:S(2)}, u32[]{:S(2)}) collective-permute-start(bf16[256,512]{1,0:T(8,128)(2,1)S(1)} %get-tuple-element.6), channel_id=1, source_target_pairs={{0,128},{64,192},{128,0},{192,64},{1,129},{65,193},{129,1},{193,65... | collective-permute-start | bytes 786440 | tf_op jit(solution)/shard_map/ppermute | solution.py:25
  129.0 1.1 collective-permute-start.22
  130.0 0.4 collective-permute-start.24
  130.4 0.5 collective-permute-done.25
  131.0 4.2 %collective-permute-start.26 = (bf16[256,512]{1,0:T(8,128)(2,1)S(1)}, bf16[256,512]{1,0:T(8,128)(2,1)S(1)}, u32[]{:S(2)}, u32[]{:S(2)}) collective-permute-start(bf16[256,512]{1,0:T(8,128)(2,1)S(1)} %collective-permute-done.25), channel_id=1, source_target_pairs={{0,192},{64,0},{128,64},{192,128},{1,193},{65,1},{129,65},{193,129... | collective-permute-start | bytes 786440 | tf_op jit(solution)/shard_map/ppermute | solution.py:25
  135.2 1.1 collective-permute-start.27
  136.3 4.4 %collective-permute-done.22 = bf16[256,512]{1,0:T(8,128)(2,1)S(1)} collective-permute-done((bf16[256,512]{1,0:T(8,128)(2,1)S(1)}, bf16[256,512]{1,0:T(8,128)(2,1)S(1)}, u32[]{:S(2)}, u32[]{:S(2)}) %collective-permute-start.22) | collective-permute-done | bytes 262176 | tf_op jit(solution)/shard_map/ppermute | solution.py:25
  140.8 0.3 collective-permute-done.24
  141.2 5.2 %collective-permute-done.26 = bf16[256,512]{1,0:T(8,128)(2,1)S(1)} collective-permute-done((bf16[256,512]{1,0:T(8,128)(2,1)S(1)}, bf16[256,512]{1,0:T(8,128)(2,1)S(1)}, u32[]{:S(2)}, u32[]{:S(2)}) %collective-permute-start.26) | collective-permute-done | bytes 262176 | tf_op jit(solution)/shard_map/ppermute | solution.py:25
  146.8 0.7 fusion.5
  147.5 1.4 collective-permute-start.29
  148.8 1.5 %collective-permute-done.29 = f32[256,512]{1,0:T(8,128)S(1)} collective-permute-done((f32[256,512]{1,0:T(8,128)S(1)}, f32[256,512]{1,0:T(8,128)S(1)}, u32[]{:S(2)}, u32[]{:S(2)}) %collective-permute-start.29) | collective-permute-done | bytes 524320 | tf_op jit(solution)/shard_map/ppermute | solution.py:21
  150.4 1.6 %add_multiply_fusion = f32[256,512]{1,0:T(8,128)} fusion(f32[256,512]{1,0:T(8,128)S(1)} %get-tuple-element.22, bf16[256,512]{1,0:T(8,128)(2,1)S(1)} %copy-done.1, f32[256,512]{1,0:T(8,128)S(1)} %collective-permute-done.29, bf16[2048,512]{1,0:T(8,128)(2,1)S(1)} %constant_dynamic-update-slice_fusion.21, bf16[640,2048]{1,0:T(8,128)(2,1)S(1)} %copy-done, ...), kind=kOutput, calls=%fused_computation.24 | convolution fusion | flops 537919488 | bytes 4980740 | tf_op jit(solution)/shard_map/dot_general | solution.py:59
  (45 shorter events, 1.1 us)
Async XLA Ops:
  0.0 8.4 %collective-permute-start = (bf16[256,512]{1,0:T(8,128)(2,1)}, bf16[256,512]{1,0:T(8,128)(2,1)S(1)}, u32[]{:S(2)}, u32[]{:S(2)}) collective-permute-start(bf16[256,512]{1,0:T(8,128)(2,1)} %param.1), channel_id=1, source_target_pairs={{0,16},{16,0},{1,17},{17,1},{2,18},{18,2},{3,19},{19,3},{4,20},{20... | collective-permute-start | bytes 786440 | tf_op jit(solution)/shard_map/ppermute | solution.py:21
  3.2 8.1 %collective-permute-start.4 = (bf16[256,512]{1,0:T(8,128)(2,1)}, bf16[256,512]{1,0:T(8,128)(2,1)S(1)}, u32[]{:S(2)}, u32[]{:S(2)}) collective-permute-start(bf16[256,512]{1,0:T(8,128)(2,1)} %param.1), channel_id=1, source_target_pairs={{0,32},{32,0},{1,33},{33,1},{2,34},{34,2},{3,35},{35,3},{4,36},{36... | collective-permute-start | bytes 786440 | tf_op jit(solution)/shard_map/ppermute | solution.py:21
  3.2 9.6 %collective-permute-start.2 = (bf16[256,512]{1,0:T(8,128)(2,1)}, bf16[256,512]{1,0:T(8,128)(2,1)S(1)}, u32[]{:S(2)}, u32[]{:S(2)}) collective-permute-start(bf16[256,512]{1,0:T(8,128)(2,1)} %param.1), channel_id=1, source_target_pairs={{0,128},{64,192},{128,0},{192,64},{1,129},{65,193},{129,1},{193,65... | collective-permute-start | bytes 786440 | tf_op jit(solution)/shard_map/ppermute | solution.py:25
  5.9 12.3 %collective-permute-start.1 = (bf16[256,512]{1,0:T(8,128)(2,1)}, bf16[256,512]{1,0:T(8,128)(2,1)S(1)}, u32[]{:S(2)}, u32[]{:S(2)}) collective-permute-start(bf16[256,512]{1,0:T(8,128)(2,1)} %param.1), channel_id=1, source_target_pairs={{0,192},{64,0},{128,64},{192,128},{1,193},{65,1},{129,65},{193,129... | collective-permute-start | bytes 786440 | tf_op jit(solution)/shard_map/ppermute | solution.py:25
  6.7 12.1 %collective-permute-start.3 = (bf16[256,512]{1,0:T(8,128)(2,1)}, bf16[256,512]{1,0:T(8,128)(2,1)S(1)}, u32[]{:S(2)}, u32[]{:S(2)}) collective-permute-start(bf16[256,512]{1,0:T(8,128)(2,1)} %param.1), channel_id=1, source_target_pairs={{0,64},{64,128},{128,192},{192,0},{1,65},{65,129},{129,193},{193,1... | collective-permute-start | bytes 786440 | tf_op jit(solution)/shard_map/ppermute | solution.py:25
  11.4 12.5 %collective-permute-start.5 = (bf16[256,512]{1,0:T(8,128)(2,1)S(1)}, bf16[256,512]{1,0:T(8,128)(2,1)S(1)}, u32[]{:S(2)}, u32[]{:S(2)}) collective-permute-start(bf16[256,512]{1,0:T(8,128)(2,1)S(1)} %collective-permute-done.4), channel_id=1, source_target_pairs={{0,192},{64,0},{128,64},{192,128},{1,193},{65,1},{129,65},{193,129... | collective-permute-start | bytes 786440 | tf_op jit(solution)/shard_map/ppermute | solution.py:25
  12.7 11.7 %collective-permute-start.7 = (bf16[256,512]{1,0:T(8,128)(2,1)S(1)}, bf16[256,512]{1,0:T(8,128)(2,1)S(1)}, u32[]{:S(2)}, u32[]{:S(2)}) collective-permute-start(bf16[256,512]{1,0:T(8,128)(2,1)S(1)} %collective-permute-done.4), channel_id=1, source_target_pairs={{0,64},{64,128},{128,192},{192,0},{1,65},{65,129},{129,193},{193,1... | collective-permute-start | bytes 786440 | tf_op jit(solution)/shard_map/ppermute | solution.py:25
  12.9 11.0 %collective-permute-start.6 = (bf16[256,512]{1,0:T(8,128)(2,1)S(1)}, bf16[256,512]{1,0:T(8,128)(2,1)S(1)}, u32[]{:S(2)}, u32[]{:S(2)}) collective-permute-start(bf16[256,512]{1,0:T(8,128)(2,1)S(1)} %collective-permute-done.2), channel_id=1, source_target_pairs={{0,32},{32,0},{1,33},{33,1},{2,34},{34,2},{3,35},{35,3},{4,36},{36... | collective-permute-start | bytes 786440 | tf_op jit(solution)/shard_map/ppermute | solution.py:21
  25.3 14.2 %collective-permute-start.8 = (bf16[128,2048]{1,0:T(8,128)(2,1)S(1)}, bf16[128,2048]{1,0:T(8,128)(2,1)S(1)}, u32[]{:S(2)}, u32[]{:S(2)}) collective-permute-start(bf16[128,2048]{1,0:T(8,128)(2,1)S(1)} %convolution_convert_fusion.2), channel_id=1, source_target_pairs={{0,1},{1,2},{2,3},{3,0},{4,5},{5,6},{6,7},{7,4},{8,9},{9,10},{10,1... | collective-permute-start | bytes 1572872 | tf_op jit(solution)/shard_map/ppermute | solution.py:25
  27.3 12.5 %collective-permute-start.9 = (bf16[128,2048]{1,0:T(8,128)(2,1)S(1)}, bf16[128,2048]{1,0:T(8,128)(2,1)S(1)}, u32[]{:S(2)}, u32[]{:S(2)}) collective-permute-start(bf16[128,2048]{1,0:T(8,128)(2,1)S(1)} %convolution_convert_fusion.1), channel_id=1, source_target_pairs={{0,3},{1,0},{2,1},{3,2},{4,7},{5,4},{6,5},{7,6},{8,11},{9,8},{10,9... | collective-permute-start | bytes 1572872 | tf_op jit(solution)/shard_map/ppermute | solution.py:25
  29.7 22.0 %collective-permute-start.10 = (bf16[128,2048]{1,0:T(8,128)(2,1)S(1)}, bf16[128,2048]{1,0:T(8,128)(2,1)S(1)}, u32[]{:S(2)}, u32[]{:S(2)}) collective-permute-start(bf16[128,2048]{1,0:T(8,128)(2,1)S(1)} %convolution_convert_fusion), channel_id=1, source_target_pairs={{0,2},{1,3},{2,0},{3,1},{4,6},{5,7},{6,4},{7,5},{8,10},{9,11},{10,... | collective-permute-start | bytes 1572872 | tf_op jit(solution)/shard_map/ppermute | solution.py:25
  52.6 9.7 %collective-permute-start.11 = (bf16[32,2048]{1,0:T(8,128)(2,1)S(1)}, bf16[32,2048]{1,0:T(8,128)(2,1)S(1)}, u32[]{:S(2)}, u32[]{:S(2)}) collective-permute-start(bf16[32,2048]{1,0:T(8,128)(2,1)S(1)} %get-tuple-element.11), channel_id=1, source_target_pairs={{0,4},{4,8},{8,12},{12,0},{1,5},{5,9},{9,13},{13,1},{2,6},{6,10},{... | collective-permute-start | bytes 393224 | tf_op jit(solution)/shard_map/ppermute | solution.py:25
  55.6 9.7 %collective-permute-start.12 = (bf16[32,2048]{1,0:T(8,128)(2,1)S(1)}, bf16[32,2048]{1,0:T(8,128)(2,1)S(1)}, u32[]{:S(2)}, u32[]{:S(2)}) collective-permute-start(bf16[32,2048]{1,0:T(8,128)(2,1)S(1)} %get-tuple-element.13), channel_id=1, source_target_pairs={{0,12},{4,0},{8,4},{12,8},{1,13},{5,1},{9,5},{13,9},{2,14},{6,2},{... | collective-permute-start | bytes 393224 | tf_op jit(solution)/shard_map/ppermute | solution.py:25
  58.0 12.9 %collective-permute-start.13 = (bf16[32,2048]{1,0:T(8,128)(2,1)S(1)}, bf16[32,2048]{1,0:T(8,128)(2,1)S(1)}, u32[]{:S(2)}, u32[]{:S(2)}) collective-permute-start(bf16[32,2048]{1,0:T(8,128)(2,1)S(1)} %get-tuple-element.12), channel_id=1, source_target_pairs={{0,8},{4,12},{8,0},{12,4},{1,9},{5,13},{9,1},{13,5},{2,10},{6,14},... | collective-permute-start | bytes 393224 | tf_op jit(solution)/shard_map/ppermute | solution.py:25
  71.0 4.9 %collective-permute-start.14 = (bf16[32,2048]{1,0:T(8,128)(2,1)S(1)}, bf16[32,2048]{1,0:T(8,128)(2,1)S(1)}, u32[]{:S(2)}, u32[]{:S(2)}) collective-permute-start(bf16[32,2048]{1,0:T(8,128)(2,1)S(1)} %get-tuple-element.10), channel_id=1, source_target_pairs={{0,12},{4,0},{8,4},{12,8},{1,13},{5,1},{9,5},{13,9},{2,14},{6,2},{... | collective-permute-start | bytes 393224 | tf_op jit(solution)/shard_map/ppermute | solution.py:25
  71.1 7.9 %collective-permute-start.15 = (bf16[32,2048]{1,0:T(8,128)(2,1)S(1)}, bf16[32,2048]{1,0:T(8,128)(2,1)S(1)}, u32[]{:S(2)}, u32[]{:S(2)}) collective-permute-start(bf16[32,2048]{1,0:T(8,128)(2,1)S(1)} %get-tuple-element.10), channel_id=1, source_target_pairs={{0,8},{4,12},{8,0},{12,4},{1,9},{5,13},{9,1},{13,5},{2,10},{6,14},... | collective-permute-start | bytes 393224 | tf_op jit(solution)/shard_map/ppermute | solution.py:25
  73.2 11.0 %collective-permute-start.16 = (bf16[32,2048]{1,0:T(8,128)(2,1)S(1)}, bf16[32,2048]{1,0:T(8,128)(2,1)S(1)}, u32[]{:S(2)}, u32[]{:S(2)}) collective-permute-start(bf16[32,2048]{1,0:T(8,128)(2,1)S(1)} %get-tuple-element.10), channel_id=1, source_target_pairs={{0,4},{4,8},{8,12},{12,0},{1,5},{5,9},{9,13},{13,1},{2,6},{6,10},{... | collective-permute-start | bytes 393224 | tf_op jit(solution)/shard_map/ppermute | solution.py:25
  85.2 10.1 %collective-permute-start.17 = (bf16[128,2048]{1,0:T(8,128)(2,1)S(1)}, bf16[128,2048]{1,0:T(8,128)(2,1)S(1)}, u32[]{:S(2)}, u32[]{:S(2)}) collective-permute-start(bf16[128,2048]{1,0:T(8,128)(2,1)S(1)} %get-tuple-element.8), channel_id=1, source_target_pairs={{0,3},{1,0},{2,1},{3,2},{4,7},{5,4},{6,5},{7,6},{8,11},{9,8},{10,9... | collective-permute-start | bytes 1572872 | tf_op jit(solution)/shard_map/ppermute | solution.py:25
  85.2 11.6 %collective-permute-start.19 = (bf16[128,2048]{1,0:T(8,128)(2,1)S(1)}, bf16[128,2048]{1,0:T(8,128)(2,1)S(1)}, u32[]{:S(2)}, u32[]{:S(2)}) collective-permute-start(bf16[128,2048]{1,0:T(8,128)(2,1)S(1)} %get-tuple-element.8), channel_id=1, source_target_pairs={{0,1},{1,2},{2,3},{3,0},{4,5},{5,6},{6,7},{7,4},{8,9},{9,10},{10,1... | collective-permute-start | bytes 1572872 | tf_op jit(solution)/shard_map/ppermute | solution.py:25
  95.3 0.8 copy-start.2
  96.8 5.4 %collective-permute-start.18 = (bf16[64,2048]{1,0:T(8,128)(2,1)}, bf16[64,2048]{1,0:T(8,128)(2,1)S(1)}, u32[]{:S(2)}, u32[]{:S(2)}) collective-permute-start(bf16[64,2048]{1,0:T(8,128)(2,1)} %slice.35), channel_id=1, source_target_pairs={{0,3},{1,0},{2,1},{3,2},{4,7},{5,4},{6,5},{7,6},{8,11},{9,8},{10,9... | collective-permute-start | bytes 786440 | tf_op jit(solution)/shard_map/ppermute | solution.py:25
  96.8 6.5 %collective-permute-start.20 = (bf16[64,2048]{1,0:T(8,128)(2,1)S(1)}, bf16[64,2048]{1,0:T(8,128)(2,1)S(1)}, u32[]{:S(2)}, u32[]{:S(2)}) collective-permute-start(bf16[64,2048]{1,0:T(8,128)(2,1)S(1)} %slice.36), channel_id=1, source_target_pairs={{0,1},{1,2},{2,3},{3,0},{4,5},{5,6},{6,7},{7,4},{8,9},{9,10},{10,1... | collective-permute-start | bytes 786440 | tf_op jit(solution)/shard_map/ppermute | solution.py:25
  107.7 8.5 %collective-permute-start.21 = (f32[256,512]{1,0:T(8,128)S(1)}, f32[256,512]{1,0:T(8,128)S(1)}, u32[]{:S(2)}, u32[]{:S(2)}) collective-permute-start(f32[256,512]{1,0:T(8,128)S(1)} %fusion.7), channel_id=1, source_target_pairs={{0,16},{16,0},{1,17},{17,1},{2,18},{18,2},{3,19},{19,3},{4,20},{20... | collective-permute-start | bytes 1572872 | tf_op jit(solution)/shard_map/ppermute | solution.py:21
  118.1 28.7 %copy-start = (bf16[640,2048]{1,0:T(8,128)(2,1)S(1)}, bf16[640,2048]{1,0:T(8,128)(2,1)}, u32[]{:S(2)}) copy-start(bf16[640,2048]{1,0:T(8,128)(2,1)} %constant_dynamic-update-slice_fusion.15) | copy-start | bytes 7864324
  118.1 12.8 %collective-permute-start.25 = (bf16[256,512]{1,0:T(8,128)(2,1)S(1)}, bf16[256,512]{1,0:T(8,128)(2,1)S(1)}, u32[]{:S(2)}, u32[]{:S(2)}) collective-permute-start(bf16[256,512]{1,0:T(8,128)(2,1)S(1)} %get-tuple-element.6), channel_id=1, source_target_pairs={{0,32},{32,0},{1,33},{33,1},{2,34},{34,2},{3,35},{35,3},{4,36},{36... | collective-permute-start | bytes 786440 | tf_op jit(solution)/shard_map/ppermute | solution.py:21
  124.6 10.6 %collective-permute-start.23 = (bf16[256,512]{1,0:T(8,128)(2,1)S(1)}, bf16[256,512]{1,0:T(8,128)(2,1)S(1)}, u32[]{:S(2)}, u32[]{:S(2)}) collective-permute-start(bf16[256,512]{1,0:T(8,128)(2,1)S(1)} %get-tuple-element.6), channel_id=1, source_target_pairs={{0,128},{64,192},{128,0},{192,64},{1,129},{65,193},{129,1},{193,65... | collective-permute-start | bytes 786440 | tf_op jit(solution)/shard_map/ppermute | solution.py:25
  129.0 11.8 %collective-permute-start.22 = (bf16[256,512]{1,0:T(8,128)(2,1)S(1)}, bf16[256,512]{1,0:T(8,128)(2,1)S(1)}, u32[]{:S(2)}, u32[]{:S(2)}) collective-permute-start(bf16[256,512]{1,0:T(8,128)(2,1)S(1)} %get-tuple-element.6), channel_id=1, source_target_pairs={{0,192},{64,0},{128,64},{192,128},{1,193},{65,1},{129,65},{193,129... | collective-permute-start | bytes 786440 | tf_op jit(solution)/shard_map/ppermute | solution.py:25
  130.0 11.1 %collective-permute-start.24 = (bf16[256,512]{1,0:T(8,128)(2,1)S(1)}, bf16[256,512]{1,0:T(8,128)(2,1)S(1)}, u32[]{:S(2)}, u32[]{:S(2)}) collective-permute-start(bf16[256,512]{1,0:T(8,128)(2,1)S(1)} %get-tuple-element.6), channel_id=1, source_target_pairs={{0,64},{64,128},{128,192},{192,0},{1,65},{65,129},{129,193},{193,1... | collective-permute-start | bytes 786440 | tf_op jit(solution)/shard_map/ppermute | solution.py:25
  131.0 15.5 %collective-permute-start.26 = (bf16[256,512]{1,0:T(8,128)(2,1)S(1)}, bf16[256,512]{1,0:T(8,128)(2,1)S(1)}, u32[]{:S(2)}, u32[]{:S(2)}) collective-permute-start(bf16[256,512]{1,0:T(8,128)(2,1)S(1)} %collective-permute-done.25), channel_id=1, source_target_pairs={{0,192},{64,0},{128,64},{192,128},{1,193},{65,1},{129,65},{193,129... | collective-permute-start | bytes 786440 | tf_op jit(solution)/shard_map/ppermute | solution.py:25
  135.2 11.6 %collective-permute-start.28 = (bf16[256,512]{1,0:T(8,128)(2,1)S(1)}, bf16[256,512]{1,0:T(8,128)(2,1)S(1)}, u32[]{:S(2)}, u32[]{:S(2)}) collective-permute-start(bf16[256,512]{1,0:T(8,128)(2,1)S(1)} %collective-permute-done.25), channel_id=1, source_target_pairs={{0,64},{64,128},{128,192},{192,0},{1,65},{65,129},{129,193},{193,1... | collective-permute-start | bytes 786440 | tf_op jit(solution)/shard_map/ppermute | solution.py:25
  135.2 11.2 %collective-permute-start.27 = (bf16[256,512]{1,0:T(8,128)(2,1)S(1)}, bf16[256,512]{1,0:T(8,128)(2,1)S(1)}, u32[]{:S(2)}, u32[]{:S(2)}) collective-permute-start(bf16[256,512]{1,0:T(8,128)(2,1)S(1)} %collective-permute-done.23), channel_id=1, source_target_pairs={{0,32},{32,0},{1,33},{33,1},{2,34},{34,2},{3,35},{35,3},{4,36},{36... | collective-permute-start | bytes 786440 | tf_op jit(solution)/shard_map/ppermute | solution.py:21
  146.5 3.9 %copy-start.1 = (bf16[256,512]{1,0:T(8,128)(2,1)S(1)}, bf16[256,512]{1,0:T(8,128)(2,1)}, u32[]{:S(2)}) copy-start(bf16[256,512]{1,0:T(8,128)(2,1)} %param.1) | copy-start | bytes 786436
  147.5 2.9 %collective-permute-start.29 = (f32[256,512]{1,0:T(8,128)S(1)}, f32[256,512]{1,0:T(8,128)S(1)}, u32[]{:S(2)}, u32[]{:S(2)}) collective-permute-start(f32[256,512]{1,0:T(8,128)S(1)} %fusion.5), channel_id=1, source_target_pairs={{0,16},{16,0},{1,17},{17,1},{2,18},{18,2},{3,19},{19,3},{4,20},{20... | collective-permute-start | bytes 1572872 | tf_op jit(solution)/shard_map/ppermute | solution.py:21

commit v8 on v7

v8 whole, which is shorter than its diff:
```python
import math

import jax
import jax.numpy as jnp
from jax import lax
from jax.sharding import Mesh
from jax.sharding import PartitionSpec as P

COLS = 8192

coef_a = 3.4445
coef_b = -4.775
coef_c = 2.0315

ROW = ("x", "zl", "core")
COL = ("zh", "y")
BF, F32 = jnp.bfloat16, jnp.float32


def swap(array, axis):
    return lax.ppermute(array, axis, [(0, 1), (1, 0)])


def send(array, axis, k):
    return lax.ppermute(array, axis, [(i, (i + k) % 4) for i in range(4)]) if k else array


def fetch(array, axis, k):
    return send(array, axis, (4 - k) % 4)


def scatter_sum(pieces, axis):
    got = [send(pieces[k], axis, k).astype(F32) for k in (0, 1, 3, 2)]
    return ((got[0] + got[1]) + (got[2] + got[3])).astype(BF)


def around(array, axis):
    return [array] + [fetch(array, axis, k) for k in (1, 2, 3)]


def chunks(array):
    return jnp.split(array, 4, axis=0)


def window(parts, first, count):
    rows = parts[0].shape[0]
    ring = jnp.concatenate([*parts, *parts[: count - 1]], axis=0)
    return lax.dynamic_slice_in_dim(ring, first * rows, count * rows, 0)


def matmul(a, b, dims):
    return lax.dot_general(a, b, (dims, ((), ())), preferred_element_type=F32)


def spread(block):
    partner = swap(block, "zl")
    return partner, around(block, "x")


def spread_more(partner, mine):
    return [partner, fetch(partner, "x", 1), swap(mine[2], "zl"), fetch(partner, "x", 3)]


def panel_of(blocks):
    count = blocks[0].shape[0] // 64
    panel = jnp.concatenate([b.reshape(count, 1, 64, 512) for b in blocks], axis=1)
    return panel.reshape(count * 512, 512)


def core_sum(products):
    mine = jnp.concatenate([m for m, _ in products], axis=0)
    other = jnp.concatenate([o for _, o in products], axis=0)
    return mine + swap(other, "core")


def per_device(iterate):
    y, zh = lax.axis_index("y"), lax.axis_index("zh")
    back = lax.rem(4 - y, 4)
    other = swap(iterate, "core")
    partner, blocks = spread(iterate)
    panel = panel_of([*blocks, *spread_more(partner, blocks)])

    own = zip(chunks(window(chunks(iterate), y, 4)), chunks(window(chunks(other), y, 4)))
    own = [window(chunks(jnp.concatenate(rows, axis=0)), zh, 4) for rows in own]
    pieces = [matmul(rows, panel, ((1,), (1,))).astype(BF) for rows in own]
    part = scatter_sum(pieces, "y")
    part = scatter_sum(chunks(part), "zh")
    near = window(around(part, "zh"), lax.rem(4 - zh, 4), 4)
    after, before = fetch(near, "y", 1), fetch(near, "y", 3)
    far = fetch(after[:64], "y", 1), fetch(before[64:], "y", 3)

    def product(rows):
        return matmul(rows, panel, ((1,), (0,)))

    first = core_sum([(m[:64], m[64:]) for m in map(product, (near, after, before))])
    partner, blocks = spread(first.astype(BF))
    partner, *blocks, far_0, far_1 = lax.optimization_barrier((partner, *blocks, *far))
    far = far_0, far_1
    second = core_sum([(product(far[0]), product(far[1]))])
    sent = second.astype(BF)
    panel_1 = panel_of([*blocks, *spread_more(partner, blocks)])
    partner, blocks = spread(sent)
    panel_2 = panel_of([*blocks, *spread_more(partner, blocks)])

    gram = [(near[:64], near[64:]), (after[:64], after[64:]), far, (before[:64], before[64:])]
    inner = window([first[:64], first[64:128], second, first[128:]], back, 4)
    mixed = []
    for rows in zip(*gram):
        rows = window(rows, back, 4)
        c = [lax.dynamic_slice_in_dim(rows, lax.rem(y + p, 4) * 512, 512, 1) for p in range(4)]
        near_3 = jnp.concatenate([c[0], c[1], c[3]], axis=1)
        mixed.append(matmul(near_3, panel_1, ((1,), (0,))) + matmul(c[2], panel_2, ((1,), (0,))))
    mixed = mixed[0] + swap(mixed[1], "core")
    mine = iterate.astype(F32)
    return math.sqrt(COLS) * (coef_a * mine + (coef_b * inner + coef_c * mixed))


def solution(mesh):
    fine = Mesh(mesh.devices.reshape(4, 2, 2, 4, 4), (*ROW, *COL))
    placed = P(ROW, COL)
    return jax.shard_map(
        per_device, mesh=fine, in_specs=(placed,), out_specs=placed, check_vma=False
    )
```

time: 152 us -> 160 us (1.053)
  waiting for transfers between devices: 73.6 us -> 82.1 us
  starting transfers between devices: 57.7 us -> 54.7 us
    ppermute x23 -> x28, waiting for transfers between devices: 69.1 us -> 73.9 us  [send(): lax.ppermute(array, axis, [(i, (i + k) % 4) for i in range(4)])]
    ppermute x7 -> x10, waiting for transfers between devices: 4.47 us -> 8.15 us  [swap(): return lax.ppermute(array, axis, [(0, 1), (1, 0)])]
    ppermute x7 -> x10, starting transfers between devices: 20.4 us -> 18.1 us  [swap(): return lax.ppermute(array, axis, [(0, 1), (1, 0)])]
    dot_general x8 -> x13, matrix products: 9.36 us -> 8.69 us  [matmul(): return lax.dot_general(a, b, (dims, ((), ())), preferred_element_type=F32)]
    ppermute x23 -> x28, starting transfers between devices: 37.3 us -> 36.7 us  [send(): lax.ppermute(array, axis, [(i, (i + k) % 4) for i in range(4)])]
    unnamed x29 -> x46, local copies, waits for them, and re-layouts: 7.16 us -> 6.88 us
  transfers between devices with their start and end apart: 30 -> 38, of which waited for: 23 -> 24; matrix products, arithmetic and copies ran while one was open for 5% -> 10% of each run, Pallas kernels for 0% -> 0%
where the time goes in v8:
time: 160 us
  waiting for transfers between devices  82.1 us (51%)
  starting transfers between devices  54.7 us (34%)
  local copies, waits for them, and re-layouts  10.4 us (6%)
  matrix products  8.69 us (5%)
  other arithmetic  3.43 us (2%)
    ppermute x28, waiting for transfers between devices, send(): lax.ppermute(array, axis, [(i, (i + k) % 4) for i in range(4)])  73.9 us
    ppermute x28, starting transfers between devices, send(): lax.ppermute(array, axis, [(i, (i + k) % 4) for i in range(4)])  36.7 us
    ppermute x10, starting transfers between devices, swap(): return lax.ppermute(array, axis, [(0, 1), (1, 0)])  18.1 us
    dot_general x13, matrix products, matmul(): return lax.dot_general(a, b, (dims, ((), ())), preferred_element_type=F32)  8.69 us
    ppermute x10, waiting for transfers between devices, swap(): return lax.ppermute(array, axis, [(0, 1), (1, 0)])  8.15 us
    unnamed x46, local copies, waits for them, and re-layouts  6.88 us
  transfers between devices with their start and end apart: 38, of which 24 were waited for; matrix products, arithmetic and copies ran while one was open for 10% of the time, Pallas kernels for 0%

profile of v8, /device:TPU:1, one launch (start us, length us, event | category | flops | bytes accessed | tf_op | source)
XLA Modules:
  0.0 159.9 jit_solution(15215301366782092107)
XLA Ops:
  0.0 3.3 %collective-permute-start.1 = (bf16[256,512]{1,0:T(8,128)(2,1)}, bf16[256,512]{1,0:T(8,128)(2,1)}, u32[]{:S(2)}, u32[]{:S(2)}) collective-permute-start(bf16[256,512]{1,0:T(8,128)(2,1)} %param.1), channel_id=1, source_target_pairs={{0,192},{64,0},{128,64},{192,128},{1,193},{65,1},{129,65},{193,129... | collective-permute-start | bytes 786440 | tf_op jit(solution)/shard_map/ppermute | solution.py:25
  4.4 1.6 %collective-permute-start.4 = (bf16[256,512]{1,0:T(8,128)(2,1)}, bf16[256,512]{1,0:T(8,128)(2,1)S(1)}, u32[]{:S(2)}, u32[]{:S(2)}) collective-permute-start(bf16[256,512]{1,0:T(8,128)(2,1)} %param.1), channel_id=1, source_target_pairs={{0,32},{32,0},{1,33},{33,1},{2,34},{34,2},{3,35},{35,3},{4,36},{36... | collective-permute-start | bytes 786440 | tf_op jit(solution)/shard_map/ppermute | solution.py:21
  6.1 1.8 %collective-permute-start = (bf16[256,512]{1,0:T(8,128)(2,1)}, bf16[256,512]{1,0:T(8,128)(2,1)S(1)}, u32[]{:S(2)}, u32[]{:S(2)}) collective-permute-start(bf16[256,512]{1,0:T(8,128)(2,1)} %param.1), channel_id=1, source_target_pairs={{0,16},{16,0},{1,17},{17,1},{2,18},{18,2},{3,19},{19,3},{4,20},{20... | collective-permute-start | bytes 786440 | tf_op jit(solution)/shard_map/ppermute | solution.py:21
  7.9 0.9 split.72
  8.8 1.0 constant_dynamic-update-slice_fusion.7
  9.8 1.1 fusion.19
  11.4 2.1 %collective-permute-start.5 = (bf16[256,512]{1,0:T(8,128)(2,1)S(1)}, bf16[256,512]{1,0:T(8,128)(2,1)S(1)}, u32[]{:S(2)}, u32[]{:S(2)}) collective-permute-start(bf16[256,512]{1,0:T(8,128)(2,1)S(1)} %collective-permute-done.4), channel_id=1, source_target_pairs={{0,192},{64,0},{128,64},{192,128},{1,193},{65,1},{129,65},{193,129... | collective-permute-start | bytes 786440 | tf_op jit(solution)/shard_map/ppermute | solution.py:25
  13.5 1.0 constant_dynamic-update-slice_fusion.6
  14.5 1.3 collective-permute-start.6
  15.8 3.1 %collective-permute-done.3 = bf16[256,512]{1,0:T(8,128)(2,1)} collective-permute-done((bf16[256,512]{1,0:T(8,128)(2,1)}, bf16[256,512]{1,0:T(8,128)(2,1)}, u32[]{:S(2)}, u32[]{:S(2)}) %collective-permute-start.3) | collective-permute-done | bytes 262176 | tf_op jit(solution)/shard_map/ppermute | solution.py:25
  19.0 1.0 constant_dynamic-update-slice_fusion.4
  20.2 7.8 %collective-permute-done.7 = bf16[256,512]{1,0:T(8,128)(2,1)S(1)} collective-permute-done((bf16[256,512]{1,0:T(8,128)(2,1)S(1)}, bf16[256,512]{1,0:T(8,128)(2,1)S(1)}, u32[]{:S(2)}, u32[]{:S(2)}) %collective-permute-start.7) | collective-permute-done | bytes 262176 | tf_op jit(solution)/shard_map/ppermute | solution.py:25
  28.0 0.9 convolution_convert_fusion
  28.9 3.0 %collective-permute-start.10 = (bf16[128,2048]{1,0:T(8,128)(2,1)S(1)}, bf16[128,2048]{1,0:T(8,128)(2,1)S(1)}, u32[]{:S(2)}, u32[]{:S(2)}) collective-permute-start(bf16[128,2048]{1,0:T(8,128)(2,1)S(1)} %convolution_convert_fusion), channel_id=1, source_target_pairs={{0,2},{1,3},{2,0},{3,1},{4,6},{5,7},{6,4},{7,5},{8,10},{9,11},{10,... | collective-permute-start | bytes 1572872 | tf_op jit(solution)/shard_map/ppermute | solution.py:25
  31.9 0.9 convolution_convert_fusion.1
  32.8 0.9 collective-permute-start.9
  33.7 0.9 convolution_convert_fusion.2
  34.6 0.8 collective-permute-start.8
  35.4 6.6 %collective-permute-done.10 = bf16[128,2048]{1,0:T(8,128)(2,1)S(1)} collective-permute-done((bf16[128,2048]{1,0:T(8,128)(2,1)S(1)}, bf16[128,2048]{1,0:T(8,128)(2,1)S(1)}, u32[]{:S(2)}, u32[]{:S(2)}) %collective-permute-start.10) | collective-permute-done | bytes 524320 | tf_op jit(solution)/shard_map/ppermute | solution.py:25
  41.9 12.9 %collective-permute-done.9 = bf16[128,2048]{1,0:T(8,128)(2,1)S(1)} collective-permute-done((bf16[128,2048]{1,0:T(8,128)(2,1)S(1)}, bf16[128,2048]{1,0:T(8,128)(2,1)S(1)}, u32[]{:S(2)}, u32[]{:S(2)}) %collective-permute-start.9) | collective-permute-done | bytes 524320 | tf_op jit(solution)/shard_map/ppermute | solution.py:25
  54.9 0.7 collective-permute-done.8
  55.6 1.0 fusion.3
  56.6 7.7 %collective-permute-start.13 = (bf16[32,2048]{1,0:T(8,128)(2,1)S(1)}, bf16[32,2048]{1,0:T(8,128)(2,1)S(1)}, u32[]{:S(2)}, u32[]{:S(2)}) collective-permute-start(bf16[32,2048]{1,0:T(8,128)(2,1)S(1)} %get-tuple-element.38), channel_id=1, source_target_pairs={{0,8},{4,12},{8,0},{12,4},{1,9},{5,13},{9,1},{13,5},{2,10},{6,14},... | collective-permute-start | bytes 393224 | tf_op jit(solution)/shard_map/ppermute | solution.py:25
  64.2 2.4 %collective-permute-start.11 = (bf16[32,2048]{1,0:T(8,128)(2,1)S(1)}, bf16[32,2048]{1,0:T(8,128)(2,1)S(1)}, u32[]{:S(2)}, u32[]{:S(2)}) collective-permute-start(bf16[32,2048]{1,0:T(8,128)(2,1)S(1)} %get-tuple-element.37), channel_id=1, source_target_pairs={{0,4},{4,8},{8,12},{12,0},{1,5},{5,9},{9,13},{13,1},{2,6},{6,10},{... | collective-permute-start | bytes 393224 | tf_op jit(solution)/shard_map/ppermute | solution.py:25
  67.2 9.9 %collective-permute-done.12 = bf16[32,2048]{1,0:T(8,128)(2,1)S(1)} collective-permute-done((bf16[32,2048]{1,0:T(8,128)(2,1)S(1)}, bf16[32,2048]{1,0:T(8,128)(2,1)S(1)}, u32[]{:S(2)}, u32[]{:S(2)}) %collective-permute-start.12) | collective-permute-done | bytes 131104 | tf_op jit(solution)/shard_map/ppermute | solution.py:25
  77.2 2.4 %collective-permute-start.14 = (bf16[32,2048]{1,0:T(8,128)(2,1)S(1)}, bf16[32,2048]{1,0:T(8,128)(2,1)S(1)}, u32[]{:S(2)}, u32[]{:S(2)}) collective-permute-start(bf16[32,2048]{1,0:T(8,128)(2,1)S(1)} %get-tuple-element.24), channel_id=1, source_target_pairs={{0,12},{4,0},{8,4},{12,8},{1,13},{5,1},{9,5},{13,9},{2,14},{6,2},{... | collective-permute-start | bytes 393224 | tf_op jit(solution)/shard_map/ppermute | solution.py:25
  79.6 1.2 collective-permute-start.15
  80.8 1.0 collective-permute-start.16
  81.8 5.4 %collective-permute-done.14 = bf16[32,2048]{1,0:T(8,128)(2,1)S(1)} collective-permute-done((bf16[32,2048]{1,0:T(8,128)(2,1)S(1)}, bf16[32,2048]{1,0:T(8,128)(2,1)S(1)}, u32[]{:S(2)}, u32[]{:S(2)}) %collective-permute-start.14) | collective-permute-done | bytes 131104 | tf_op jit(solution)/shard_map/ppermute | solution.py:25
  87.2 3.2 %collective-permute-done.15 = bf16[32,2048]{1,0:T(8,128)(2,1)S(1)} collective-permute-done((bf16[32,2048]{1,0:T(8,128)(2,1)S(1)}, bf16[32,2048]{1,0:T(8,128)(2,1)S(1)}, u32[]{:S(2)}, u32[]{:S(2)}) %collective-permute-start.15) | collective-permute-done | bytes 131104 | tf_op jit(solution)/shard_map/ppermute | solution.py:25
  90.5 3.0 %collective-permute-done.16 = bf16[32,2048]{1,0:T(8,128)(2,1)S(1)} collective-permute-done((bf16[32,2048]{1,0:T(8,128)(2,1)S(1)}, bf16[32,2048]{1,0:T(8,128)(2,1)S(1)}, u32[]{:S(2)}, u32[]{:S(2)}) %collective-permute-start.16) | collective-permute-done | bytes 131104 | tf_op jit(solution)/shard_map/ppermute | solution.py:25
  93.6 0.9 copy-done.1
  94.6 1.4 collective-permute-start.18
  95.9 1.6 collective-permute-start.17
  97.5 1.7 %dynamic-slice_dynamic-update-slice_fusion.2 = bf16[448,2048]{1,0:T(8,128)(2,1)} fusion(bf16[224,2048]{1,0:T(8,128)(2,1)} %copy-done.1, s32[]{:T(128)S(6)} %select_n.46), kind=kLoop, calls=%fused_computation.44 | loop fusion | bytes 524292
  99.6 8.6 %collective-permute-done.18 = bf16[128,2048]{1,0:T(8,128)(2,1)S(1)} collective-permute-done((bf16[128,2048]{1,0:T(8,128)(2,1)S(1)}, bf16[128,2048]{1,0:T(8,128)(2,1)S(1)}, u32[]{:S(2)}, u32[]{:S(2)}) %collective-permute-start.18) | collective-permute-done | bytes 524320 | tf_op jit(solution)/shard_map/ppermute | solution.py:25
  108.7 0.7 fusion.54
  109.8 0.7 fusion.53
  110.4 0.8 pad_maximum_fusion
  111.2 2.1 %collective-permute-start.19 = (f32[192,512]{1,0:T(8,128)}, f32[192,512]{1,0:T(8,128)}, u32[]{:S(2)}, u32[]{:S(2)}) collective-permute-start(f32[192,512]{1,0:T(8,128)} %pad_maximum_fusion), channel_id=1, source_target_pairs={{0,16},{16,0},{1,17},{17,1},{2,18},{18,2},{3,19},{19,3},{4,20},{20... | collective-permute-start | bytes 1179656 | tf_op jit(solution)/shard_map/ppermute | solution.py:21
  113.3 0.8 constant_dynamic-update-slice_fusion.20
  114.1 1.6 %collective-permute-start.24 = (bf16[64,2048]{1,0:T(8,128)(2,1)}, bf16[64,2048]{1,0:T(8,128)(2,1)S(1)}, u32[]{:S(2)}, u32[]{:S(2)}) collective-permute-start(bf16[64,2048]{1,0:T(8,128)(2,1)} %get-tuple-element.36), channel_id=1, source_target_pairs={{0,3},{1,0},{2,1},{3,2},{4,7},{5,4},{6,5},{7,6},{8,11},{9,8},{10,9... | collective-permute-start | bytes 786440 | tf_op jit(solution)/shard_map/ppermute | solution.py:25
  115.9 1.1 fusion.48
  117.1 4.2 %collective-permute-start.20 = (bf16[192,512]{1,0:T(8,128)(2,1)S(1)}, bf16[192,512]{1,0:T(8,128)(2,1)S(1)}, u32[]{:S(2)}, u32[]{:S(2)}) collective-permute-start(bf16[192,512]{1,0:T(8,128)(2,1)S(1)} %get-tuple-element.14), channel_id=1, source_target_pairs={{0,32},{32,0},{1,33},{33,1},{2,34},{34,2},{3,35},{35,3},{4,36},{36... | collective-permute-start | bytes 589832 | tf_op jit(solution)/shard_map/ppermute | solution.py:21
  121.5 0.8 collective-permute-done.24
  122.8 1.9 %collective-permute-done.25 = bf16[64,2048]{1,0:T(8,128)(2,1)S(1)} collective-permute-done((bf16[64,2048]{1,0:T(8,128)(2,1)S(1)}, bf16[64,2048]{1,0:T(8,128)(2,1)S(1)}, u32[]{:S(2)}, u32[]{:S(2)}) %collective-permute-start.25) | collective-permute-done | bytes 262176 | tf_op jit(solution)/shard_map/ppermute | solution.py:25
  124.7 1.6 collective-permute-done.20
  126.3 0.8 collective-permute-done.21
  127.1 1.6 collective-permute-done.22
  128.6 5.2 %collective-permute-done.23 = bf16[192,512]{1,0:T(8,128)(2,1)S(1)} collective-permute-done((bf16[192,512]{1,0:T(8,128)(2,1)S(1)}, bf16[192,512]{1,0:T(8,128)(2,1)S(1)}, u32[]{:S(2)}, u32[]{:S(2)}) %collective-permute-start.23) | collective-permute-done | bytes 196640 | tf_op jit(solution)/shard_map/ppermute | solution.py:25
  133.8 1.5 collective-permute-start.29
  135.8 1.4 collective-permute-start.26
  137.2 0.9 collective-permute-start.28
  140.0 1.5 collective-permute-start.30
  142.3 1.5 collective-permute-done.28
  143.8 0.8 collective-permute-start.33
  145.2 2.0 %collective-permute-done.33 = bf16[64,512]{1,0:T(8,128)(2,1)S(1)} collective-permute-done((bf16[64,512]{1,0:T(8,128)(2,1)S(1)}, bf16[64,512]{1,0:T(8,128)(2,1)S(1)}, u32[]{:S(2)}, u32[]{:S(2)}) %collective-permute-start.33) | collective-permute-done | bytes 65568 | tf_op jit(solution)/shard_map/ppermute | solution.py:21
  147.2 1.8 %collective-permute-start.34 = (bf16[64,512]{1,0:T(8,128)(2,1)S(1)}, bf16[64,512]{1,0:T(8,128)(2,1)S(1)}, u32[]{:S(2)}, u32[]{:S(2)}) collective-permute-start(bf16[64,512]{1,0:T(8,128)(2,1)S(1)} %collective-permute-done.33), channel_id=1, source_target_pairs={{0,192},{64,0},{128,64},{192,128},{1,193},{65,1},{129,65},{193,129... | collective-permute-start | bytes 196616 | tf_op jit(solution)/shard_map/ppermute | solution.py:25
  149.5 0.8 collective-permute-done.34
  150.3 2.1 %collective-permute-done.35 = bf16[64,512]{1,0:T(8,128)(2,1)S(1)} collective-permute-done((bf16[64,512]{1,0:T(8,128)(2,1)S(1)}, bf16[64,512]{1,0:T(8,128)(2,1)S(1)}, u32[]{:S(2)}, u32[]{:S(2)}) %collective-permute-start.35) | collective-permute-done | bytes 65568 | tf_op jit(solution)/shard_map/ppermute | solution.py:21
  152.4 0.9 collective-permute-done.36
  153.7 3.5 %collective-permute-start.37 = (f32[256,512]{1,0:T(8,128)S(1)}, f32[256,512]{1,0:T(8,128)S(1)}, u32[]{:S(2)}, u32[]{:S(2)}) collective-permute-start(f32[256,512]{1,0:T(8,128)S(1)} %convolution_add_fusion), channel_id=1, source_target_pairs={{0,16},{16,0},{1,17},{17,1},{2,18},{18,2},{3,19},{19,3},{4,20},{20... | collective-permute-start | bytes 1572872 | tf_op jit(solution)/shard_map/ppermute | solution.py:21
  157.8 0.9 collective-permute-done.37
  158.7 1.2 add_multiply_fusion
  (97 shorter events, 9.9 us)
Async XLA Ops:
  0.0 13.5 %collective-permute-start.1 = (bf16[256,512]{1,0:T(8,128)(2,1)}, bf16[256,512]{1,0:T(8,128)(2,1)}, u32[]{:S(2)}, u32[]{:S(2)}) collective-permute-start(bf16[256,512]{1,0:T(8,128)(2,1)} %param.1), channel_id=1, source_target_pairs={{0,192},{64,0},{128,64},{192,128},{1,193},{65,1},{129,65},{193,129... | collective-permute-start | bytes 786440 | tf_op jit(solution)/shard_map/ppermute | solution.py:25
  3.3 11.2 %collective-permute-start.2 = (bf16[256,512]{1,0:T(8,128)(2,1)}, bf16[256,512]{1,0:T(8,128)(2,1)S(1)}, u32[]{:S(2)}, u32[]{:S(2)}) collective-permute-start(bf16[256,512]{1,0:T(8,128)(2,1)} %param.1), channel_id=1, source_target_pairs={{0,128},{64,192},{128,0},{192,64},{1,129},{65,193},{129,1},{193,65... | collective-permute-start | bytes 786440 | tf_op jit(solution)/shard_map/ppermute | solution.py:25
  3.8 15.1 %collective-permute-start.3 = (bf16[256,512]{1,0:T(8,128)(2,1)}, bf16[256,512]{1,0:T(8,128)(2,1)}, u32[]{:S(2)}, u32[]{:S(2)}) collective-permute-start(bf16[256,512]{1,0:T(8,128)(2,1)} %param.1), channel_id=1, source_target_pairs={{0,64},{64,128},{128,192},{192,0},{1,65},{65,129},{129,193},{193,1... | collective-permute-start | bytes 786440 | tf_op jit(solution)/shard_map/ppermute | solution.py:25
  4.4 7.0 %collective-permute-start.4 = (bf16[256,512]{1,0:T(8,128)(2,1)}, bf16[256,512]{1,0:T(8,128)(2,1)S(1)}, u32[]{:S(2)}, u32[]{:S(2)}) collective-permute-start(bf16[256,512]{1,0:T(8,128)(2,1)} %param.1), channel_id=1, source_target_pairs={{0,32},{32,0},{1,33},{33,1},{2,34},{34,2},{3,35},{35,3},{4,36},{36... | collective-permute-start | bytes 786440 | tf_op jit(solution)/shard_map/ppermute | solution.py:21
  6.1 4.9 %collective-permute-start = (bf16[256,512]{1,0:T(8,128)(2,1)}, bf16[256,512]{1,0:T(8,128)(2,1)S(1)}, u32[]{:S(2)}, u32[]{:S(2)}) collective-permute-start(bf16[256,512]{1,0:T(8,128)(2,1)} %param.1), channel_id=1, source_target_pairs={{0,16},{16,0},{1,17},{17,1},{2,18},{18,2},{3,19},{19,3},{4,20},{20... | collective-permute-start | bytes 786440 | tf_op jit(solution)/shard_map/ppermute | solution.py:21
  11.4 8.6 %collective-permute-start.5 = (bf16[256,512]{1,0:T(8,128)(2,1)S(1)}, bf16[256,512]{1,0:T(8,128)(2,1)S(1)}, u32[]{:S(2)}, u32[]{:S(2)}) collective-permute-start(bf16[256,512]{1,0:T(8,128)(2,1)S(1)} %collective-permute-done.4), channel_id=1, source_target_pairs={{0,192},{64,0},{128,64},{192,128},{1,193},{65,1},{129,65},{193,129... | collective-permute-start | bytes 786440 | tf_op jit(solution)/shard_map/ppermute | solution.py:25
  14.5 5.6 %collective-permute-start.6 = (bf16[256,512]{1,0:T(8,128)(2,1)S(1)}, bf16[256,512]{1,0:T(8,128)(2,1)S(1)}, u32[]{:S(2)}, u32[]{:S(2)}) collective-permute-start(bf16[256,512]{1,0:T(8,128)(2,1)S(1)} %collective-permute-done.2), channel_id=1, source_target_pairs={{0,32},{32,0},{1,33},{33,1},{2,34},{34,2},{3,35},{35,3},{4,36},{36... | collective-permute-start | bytes 786440 | tf_op jit(solution)/shard_map/ppermute | solution.py:21
  19.9 8.0 %collective-permute-start.7 = (bf16[256,512]{1,0:T(8,128)(2,1)S(1)}, bf16[256,512]{1,0:T(8,128)(2,1)S(1)}, u32[]{:S(2)}, u32[]{:S(2)}) collective-permute-start(bf16[256,512]{1,0:T(8,128)(2,1)S(1)} %collective-permute-done.4), channel_id=1, source_target_pairs={{0,64},{64,128},{128,192},{192,0},{1,65},{65,129},{129,193},{193,1... | collective-permute-start | bytes 786440 | tf_op jit(solution)/shard_map/ppermute | solution.py:25
  28.9 13.0 %collective-permute-start.10 = (bf16[128,2048]{1,0:T(8,128)(2,1)S(1)}, bf16[128,2048]{1,0:T(8,128)(2,1)S(1)}, u32[]{:S(2)}, u32[]{:S(2)}) collective-permute-start(bf16[128,2048]{1,0:T(8,128)(2,1)S(1)} %convolution_convert_fusion), channel_id=1, source_target_pairs={{0,2},{1,3},{2,0},{3,1},{4,6},{5,7},{6,4},{7,5},{8,10},{9,11},{10,... | collective-permute-start | bytes 1572872 | tf_op jit(solution)/shard_map/ppermute | solution.py:25
  32.8 22.1 %collective-permute-start.9 = (bf16[128,2048]{1,0:T(8,128)(2,1)S(1)}, bf16[128,2048]{1,0:T(8,128)(2,1)S(1)}, u32[]{:S(2)}, u32[]{:S(2)}) collective-permute-start(bf16[128,2048]{1,0:T(8,128)(2,1)S(1)} %convolution_convert_fusion.1), channel_id=1, source_target_pairs={{0,3},{1,0},{2,1},{3,2},{4,7},{5,4},{6,5},{7,6},{8,11},{9,8},{10,9... | collective-permute-start | bytes 1572872 | tf_op jit(solution)/shard_map/ppermute | solution.py:25
  34.6 21.0 %collective-permute-start.8 = (bf16[128,2048]{1,0:T(8,128)(2,1)S(1)}, bf16[128,2048]{1,0:T(8,128)(2,1)S(1)}, u32[]{:S(2)}, u32[]{:S(2)}) collective-permute-start(bf16[128,2048]{1,0:T(8,128)(2,1)S(1)} %convolution_convert_fusion.2), channel_id=1, source_target_pairs={{0,1},{1,2},{2,3},{3,0},{4,5},{5,6},{6,7},{7,4},{8,9},{9,10},{10,1... | collective-permute-start | bytes 1572872 | tf_op jit(solution)/shard_map/ppermute | solution.py:25
  56.6 10.7 %collective-permute-start.13 = (bf16[32,2048]{1,0:T(8,128)(2,1)S(1)}, bf16[32,2048]{1,0:T(8,128)(2,1)S(1)}, u32[]{:S(2)}, u32[]{:S(2)}) collective-permute-start(bf16[32,2048]{1,0:T(8,128)(2,1)S(1)} %get-tuple-element.38), channel_id=1, source_target_pairs={{0,8},{4,12},{8,0},{12,4},{1,9},{5,13},{9,1},{13,5},{2,10},{6,14},... | collective-permute-start | bytes 393224 | tf_op jit(solution)/shard_map/ppermute | solution.py:25
  64.2 12.9 %collective-permute-start.12 = (bf16[32,2048]{1,0:T(8,128)(2,1)S(1)}, bf16[32,2048]{1,0:T(8,128)(2,1)S(1)}, u32[]{:S(2)}, u32[]{:S(2)}) collective-permute-start(bf16[32,2048]{1,0:T(8,128)(2,1)S(1)} %get-tuple-element.39), channel_id=1, source_target_pairs={{0,12},{4,0},{8,4},{12,8},{1,13},{5,1},{9,5},{13,9},{2,14},{6,2},{... | collective-permute-start | bytes 393224 | tf_op jit(solution)/shard_map/ppermute | solution.py:25
  64.2 12.9 %collective-permute-start.11 = (bf16[32,2048]{1,0:T(8,128)(2,1)S(1)}, bf16[32,2048]{1,0:T(8,128)(2,1)S(1)}, u32[]{:S(2)}, u32[]{:S(2)}) collective-permute-start(bf16[32,2048]{1,0:T(8,128)(2,1)S(1)} %get-tuple-element.37), channel_id=1, source_target_pairs={{0,4},{4,8},{8,12},{12,0},{1,5},{5,9},{9,13},{13,1},{2,6},{6,10},{... | collective-permute-start | bytes 393224 | tf_op jit(solution)/shard_map/ppermute | solution.py:25
  77.2 10.0 %collective-permute-start.14 = (bf16[32,2048]{1,0:T(8,128)(2,1)S(1)}, bf16[32,2048]{1,0:T(8,128)(2,1)S(1)}, u32[]{:S(2)}, u32[]{:S(2)}) collective-permute-start(bf16[32,2048]{1,0:T(8,128)(2,1)S(1)} %get-tuple-element.24), channel_id=1, source_target_pairs={{0,12},{4,0},{8,4},{12,8},{1,13},{5,1},{9,5},{13,9},{2,14},{6,2},{... | collective-permute-start | bytes 393224 | tf_op jit(solution)/shard_map/ppermute | solution.py:25
  79.6 10.8 %collective-permute-start.15 = (bf16[32,2048]{1,0:T(8,128)(2,1)S(1)}, bf16[32,2048]{1,0:T(8,128)(2,1)S(1)}, u32[]{:S(2)}, u32[]{:S(2)}) collective-permute-start(bf16[32,2048]{1,0:T(8,128)(2,1)S(1)} %get-tuple-element.24), channel_id=1, source_target_pairs={{0,8},{4,12},{8,0},{12,4},{1,9},{5,13},{9,1},{13,5},{2,10},{6,14},... | collective-permute-start | bytes 393224 | tf_op jit(solution)/shard_map/ppermute | solution.py:25
  80.8 12.7 %collective-permute-start.16 = (bf16[32,2048]{1,0:T(8,128)(2,1)S(1)}, bf16[32,2048]{1,0:T(8,128)(2,1)S(1)}, u32[]{:S(2)}, u32[]{:S(2)}) collective-permute-start(bf16[32,2048]{1,0:T(8,128)(2,1)S(1)} %get-tuple-element.24), channel_id=1, source_target_pairs={{0,4},{4,8},{8,12},{12,0},{1,5},{5,9},{9,13},{13,1},{2,6},{6,10},{... | collective-permute-start | bytes 393224 | tf_op jit(solution)/shard_map/ppermute | solution.py:25
  93.6 0.9 copy-start.1
  94.6 13.6 %collective-permute-start.18 = (bf16[128,2048]{1,0:T(8,128)(2,1)S(1)}, bf16[128,2048]{1,0:T(8,128)(2,1)S(1)}, u32[]{:S(2)}, u32[]{:S(2)}) collective-permute-start(bf16[128,2048]{1,0:T(8,128)(2,1)S(1)} %constant_dynamic-slice_fusion), channel_id=1, source_target_pairs={{0,1},{1,2},{2,3},{3,0},{4,5},{5,6},{6,7},{7,4},{8,9},{9,10},{10,1... | collective-permute-start | bytes 1572872 | tf_op jit(solution)/shard_map/ppermute | solution.py:25
  95.9 13.4 %collective-permute-start.17 = (bf16[128,2048]{1,0:T(8,128)(2,1)S(1)}, bf16[128,2048]{1,0:T(8,128)(2,1)S(1)}, u32[]{:S(2)}, u32[]{:S(2)}) collective-permute-start(bf16[128,2048]{1,0:T(8,128)(2,1)S(1)} %constant_dynamic-slice_fusion), channel_id=1, source_target_pairs={{0,3},{1,0},{2,1},{3,2},{4,7},{5,4},{6,5},{7,6},{8,11},{9,8},{10,9... | collective-permute-start | bytes 1572872 | tf_op jit(solution)/shard_map/ppermute | solution.py:25
  111.2 4.7 %collective-permute-start.19 = (f32[192,512]{1,0:T(8,128)}, f32[192,512]{1,0:T(8,128)}, u32[]{:S(2)}, u32[]{:S(2)}) collective-permute-start(f32[192,512]{1,0:T(8,128)} %pad_maximum_fusion), channel_id=1, source_target_pairs={{0,16},{16,0},{1,17},{17,1},{2,18},{18,2},{3,19},{19,3},{4,20},{20... | collective-permute-start | bytes 1179656 | tf_op jit(solution)/shard_map/ppermute | solution.py:21
  114.1 8.1 %collective-permute-start.24 = (bf16[64,2048]{1,0:T(8,128)(2,1)}, bf16[64,2048]{1,0:T(8,128)(2,1)S(1)}, u32[]{:S(2)}, u32[]{:S(2)}) collective-permute-start(bf16[64,2048]{1,0:T(8,128)(2,1)} %get-tuple-element.36), channel_id=1, source_target_pairs={{0,3},{1,0},{2,1},{3,2},{4,7},{5,4},{6,5},{7,6},{8,11},{9,8},{10,9... | collective-permute-start | bytes 786440 | tf_op jit(solution)/shard_map/ppermute | solution.py:25
  115.8 8.9 %collective-permute-start.25 = (bf16[64,2048]{1,0:T(8,128)(2,1)S(1)}, bf16[64,2048]{1,0:T(8,128)(2,1)S(1)}, u32[]{:S(2)}, u32[]{:S(2)}) collective-permute-start(bf16[64,2048]{1,0:T(8,128)(2,1)S(1)} %slice.101), channel_id=1, source_target_pairs={{0,1},{1,2},{2,3},{3,0},{4,5},{5,6},{6,7},{7,4},{8,9},{9,10},{10,1... | collective-permute-start | bytes 786440 | tf_op jit(solution)/shard_map/ppermute | solution.py:25
  117.1 21.0 %copy-start.3 = (bf16[448,2048]{1,0:T(8,128)(2,1)S(1)}, bf16[448,2048]{1,0:T(8,128)(2,1)}, u32[]{:S(2)}) copy-start(bf16[448,2048]{1,0:T(8,128)(2,1)} %get-tuple-element.35) | copy-start | bytes 5505028
  117.1 9.2 %collective-permute-start.20 = (bf16[192,512]{1,0:T(8,128)(2,1)S(1)}, bf16[192,512]{1,0:T(8,128)(2,1)S(1)}, u32[]{:S(2)}, u32[]{:S(2)}) collective-permute-start(bf16[192,512]{1,0:T(8,128)(2,1)S(1)} %get-tuple-element.14), channel_id=1, source_target_pairs={{0,32},{32,0},{1,33},{33,1},{2,34},{34,2},{3,35},{35,3},{4,36},{36... | collective-permute-start | bytes 589832 | tf_op jit(solution)/shard_map/ppermute | solution.py:21
  121.3 5.8 %collective-permute-start.21 = (bf16[192,512]{1,0:T(8,128)(2,1)S(1)}, bf16[192,512]{1,0:T(8,128)(2,1)S(1)}, u32[]{:S(2)}, u32[]{:S(2)}) collective-permute-start(bf16[192,512]{1,0:T(8,128)(2,1)S(1)} %get-tuple-element.14), channel_id=1, source_target_pairs={{0,192},{64,0},{128,64},{192,128},{1,193},{65,1},{129,65},{193,129... | collective-permute-start | bytes 589832 | tf_op jit(solution)/shard_map/ppermute | solution.py:25
  121.3 7.3 %collective-permute-start.22 = (bf16[192,512]{1,0:T(8,128)(2,1)S(1)}, bf16[192,512]{1,0:T(8,128)(2,1)S(1)}, u32[]{:S(2)}, u32[]{:S(2)}) collective-permute-start(bf16[192,512]{1,0:T(8,128)(2,1)S(1)} %get-tuple-element.14), channel_id=1, source_target_pairs={{0,128},{64,192},{128,0},{192,64},{1,129},{65,193},{129,1},{193,65... | collective-permute-start | bytes 589832 | tf_op jit(solution)/shard_map/ppermute | solution.py:25
  122.3 11.5 %collective-permute-start.23 = (bf16[192,512]{1,0:T(8,128)(2,1)S(1)}, bf16[192,512]{1,0:T(8,128)(2,1)S(1)}, u32[]{:S(2)}, u32[]{:S(2)}) collective-permute-start(bf16[192,512]{1,0:T(8,128)(2,1)S(1)} %get-tuple-element.14), channel_id=1, source_target_pairs={{0,64},{64,128},{128,192},{192,0},{1,65},{65,129},{129,193},{193,1... | collective-permute-start | bytes 589832 | tf_op jit(solution)/shard_map/ppermute | solution.py:25
  122.8 15.3 %copy-start.2 = (bf16[224,2048]{1,0:T(8,128)(2,1)S(1)}, bf16[224,2048]{1,0:T(8,128)(2,1)}, u32[]{:S(2)}) copy-start(bf16[224,2048]{1,0:T(8,128)(2,1)} %copy-done.1) | copy-start | bytes 2752516
  133.8 7.8 %collective-permute-start.27 = (bf16[192,512]{1,0:T(8,128)(2,1)S(1)}, bf16[192,512]{1,0:T(8,128)(2,1)S(1)}, u32[]{:S(2)}, u32[]{:S(2)}) collective-permute-start(bf16[192,512]{1,0:T(8,128)(2,1)S(1)} %collective-permute-done.20), channel_id=1, source_target_pairs={{0,192},{64,0},{128,64},{192,128},{1,193},{65,1},{129,65},{193,129... | collective-permute-start | bytes 589832 | tf_op jit(solution)/shard_map/ppermute | solution.py:25
  133.8 10.8 %collective-permute-start.29 = (bf16[192,512]{1,0:T(8,128)(2,1)S(1)}, bf16[192,512]{1,0:T(8,128)(2,1)S(1)}, u32[]{:S(2)}, u32[]{:S(2)}) collective-permute-start(bf16[192,512]{1,0:T(8,128)(2,1)S(1)} %collective-permute-done.20), channel_id=1, source_target_pairs={{0,64},{64,128},{128,192},{192,0},{1,65},{65,129},{129,193},{193,1... | collective-permute-start | bytes 589832 | tf_op jit(solution)/shard_map/ppermute | solution.py:25
  135.8 3.7 %collective-permute-start.26 = (f32[64,512]{1,0:T(8,128)S(1)}, f32[64,512]{1,0:T(8,128)S(1)}, u32[]{:S(2)}, u32[]{:S(2)}) collective-permute-start(f32[64,512]{1,0:T(8,128)S(1)} %fusion.61), channel_id=1, source_target_pairs={{0,16},{16,0},{1,17},{17,1},{2,18},{18,2},{3,19},{19,3},{4,20},{20... | collective-permute-start | bytes 393224 | tf_op jit(solution)/shard_map/ppermute | solution.py:21
  137.2 6.6 %collective-permute-start.28 = (bf16[192,512]{1,0:T(8,128)(2,1)S(1)}, bf16[192,512]{1,0:T(8,128)(2,1)S(1)}, u32[]{:S(2)}, u32[]{:S(2)}) collective-permute-start(bf16[192,512]{1,0:T(8,128)(2,1)S(1)} %collective-permute-done.22), channel_id=1, source_target_pairs={{0,32},{32,0},{1,33},{33,1},{2,34},{34,2},{3,35},{35,3},{4,36},{36... | collective-permute-start | bytes 589832 | tf_op jit(solution)/shard_map/ppermute | solution.py:21
  140.0 9.4 %collective-permute-start.30 = (bf16[64,512]{1,0:T(8,128)(2,1)S(1)}, bf16[64,512]{1,0:T(8,128)(2,1)S(1)}, u32[]{:S(2)}, u32[]{:S(2)}) collective-permute-start(bf16[64,512]{1,0:T(8,128)(2,1)S(1)} %get-tuple-element.20), channel_id=1, source_target_pairs={{0,192},{64,0},{128,64},{192,128},{1,193},{65,1},{129,65},{193,129... | collective-permute-start | bytes 196616 | tf_op jit(solution)/shard_map/ppermute | solution.py:25
  141.5 7.5 %collective-permute-start.31 = (bf16[64,512]{1,0:T(8,128)(2,1)S(1)}, bf16[64,512]{1,0:T(8,128)(2,1)S(1)}, u32[]{:S(2)}, u32[]{:S(2)}) collective-permute-start(bf16[64,512]{1,0:T(8,128)(2,1)S(1)} %get-tuple-element.20), channel_id=1, source_target_pairs={{0,128},{64,192},{128,0},{192,64},{1,129},{65,193},{129,1},{193,65... | collective-permute-start | bytes 196616 | tf_op jit(solution)/shard_map/ppermute | solution.py:25
  141.6 7.8 %collective-permute-start.32 = (bf16[64,512]{1,0:T(8,128)(2,1)S(1)}, bf16[64,512]{1,0:T(8,128)(2,1)S(1)}, u32[]{:S(2)}, u32[]{:S(2)}) collective-permute-start(bf16[64,512]{1,0:T(8,128)(2,1)S(1)} %get-tuple-element.20), channel_id=1, source_target_pairs={{0,64},{64,128},{128,192},{192,0},{1,65},{65,129},{129,193},{193,1... | collective-permute-start | bytes 196616 | tf_op jit(solution)/shard_map/ppermute | solution.py:25
  143.8 3.4 %collective-permute-start.33 = (bf16[64,512]{1,0:T(8,128)(2,1)S(1)}, bf16[64,512]{1,0:T(8,128)(2,1)S(1)}, u32[]{:S(2)}, u32[]{:S(2)}) collective-permute-start(bf16[64,512]{1,0:T(8,128)(2,1)S(1)} %get-tuple-element.20), channel_id=1, source_target_pairs={{0,32},{32,0},{1,33},{33,1},{2,34},{34,2},{3,35},{35,3},{4,36},{36... | collective-permute-start | bytes 196616 | tf_op jit(solution)/shard_map/ppermute | solution.py:21
  147.2 3.1 %collective-permute-start.34 = (bf16[64,512]{1,0:T(8,128)(2,1)S(1)}, bf16[64,512]{1,0:T(8,128)(2,1)S(1)}, u32[]{:S(2)}, u32[]{:S(2)}) collective-permute-start(bf16[64,512]{1,0:T(8,128)(2,1)S(1)} %collective-permute-done.33), channel_id=1, source_target_pairs={{0,192},{64,0},{128,64},{192,128},{1,193},{65,1},{129,65},{193,129... | collective-permute-start | bytes 196616 | tf_op jit(solution)/shard_map/ppermute | solution.py:25
  149.0 4.3 %collective-permute-start.36 = (bf16[64,512]{1,0:T(8,128)(2,1)S(1)}, bf16[64,512]{1,0:T(8,128)(2,1)S(1)}, u32[]{:S(2)}, u32[]{:S(2)}) collective-permute-start(bf16[64,512]{1,0:T(8,128)(2,1)S(1)} %collective-permute-done.33), channel_id=1, source_target_pairs={{0,64},{64,128},{128,192},{192,0},{1,65},{65,129},{129,193},{193,1... | collective-permute-start | bytes 196616 | tf_op jit(solution)/shard_map/ppermute | solution.py:25
  149.0 3.4 %collective-permute-start.35 = (bf16[64,512]{1,0:T(8,128)(2,1)S(1)}, bf16[64,512]{1,0:T(8,128)(2,1)S(1)}, u32[]{:S(2)}, u32[]{:S(2)}) collective-permute-start(bf16[64,512]{1,0:T(8,128)(2,1)S(1)} %collective-permute-done.31), channel_id=1, source_target_pairs={{0,32},{32,0},{1,33},{33,1},{2,34},{34,2},{3,35},{35,3},{4,36},{36... | collective-permute-start | bytes 196616 | tf_op jit(solution)/shard_map/ppermute | solution.py:21
  153.7 5.0 %collective-permute-start.37 = (f32[256,512]{1,0:T(8,128)S(1)}, f32[256,512]{1,0:T(8,128)S(1)}, u32[]{:S(2)}, u32[]{:S(2)}) collective-permute-start(f32[256,512]{1,0:T(8,128)S(1)} %convolution_add_fusion), channel_id=1, source_target_pairs={{0,16},{16,0},{1,17},{17,1},{2,18},{18,2},{3,19},{19,3},{4,20},{20... | collective-permute-start | bytes 1572872 | tf_op jit(solution)/shard_map/ppermute | solution.py:21
  157.2 1.5 copy-start

commit v9 on v8

v9 whole, which is shorter than its diff:
```python
import math

import jax
import jax.numpy as jnp
from jax import lax
from jax.sharding import Mesh
from jax.sharding import PartitionSpec as P

COLS = 8192

coef_a = 3.4445
coef_b = -4.775
coef_c = 2.0315

ROW = ("x", "zl", "core")
COL = ("zh", "y")
BF, F32 = jnp.bfloat16, jnp.float32


def swap(array, axis):
    return lax.ppermute(array, axis, [(0, 1), (1, 0)])


def send(array, axis, k):
    return lax.ppermute(array, axis, [(i, (i + k) % 4) for i in range(4)]) if k else array


def fetch(array, axis, k):
    return send(array, axis, (4 - k) % 4)


def add(got):
    got = [g.astype(F32) for g in got]
    return ((got[0] + got[1]) + (got[2] + got[3])).astype(BF)


def scatter(pieces, axis):
    return [send(pieces[k], axis, k) for k in (0, 1, 3, 2)]


def around(array, axis):
    return [array] + [fetch(array, axis, k) for k in (1, 2, 3)]


def chunks(array):
    return jnp.split(array, 4, axis=0)


def window(parts, first, count):
    rows = parts[0].shape[0]
    ring = jnp.concatenate([*parts, *parts[: count - 1]], axis=0)
    return lax.dynamic_slice_in_dim(ring, first * rows, count * rows, 0)


def matmul(a, b, dims):
    return lax.dot_general(a, b, (dims, ((), ())), preferred_element_type=F32)


def panels_of(block):
    partner = swap(block, "zl")
    mine = around(block, "x")
    theirs = [partner, fetch(partner, "x", 1), swap(mine[2], "zl"), fetch(partner, "x", 3)]
    panels = [jnp.concatenate([b.reshape(4, 1, 64, 512) for b in four], axis=1) for four in (mine, theirs)]
    return [panel.reshape(1024, 512) for panel in panels]


def core_sum(products):
    mine = jnp.concatenate([m for m, _ in products], axis=0)
    other = jnp.concatenate([o for _, o in products], axis=0)
    return mine + swap(other, "core")


def per_device(iterate):
    y, zh = lax.axis_index("y"), lax.axis_index("zh")
    other = swap(iterate, "core")
    panels = panels_of(iterate)

    own = [jnp.concatenate(rows, axis=0) for rows in zip(chunks(iterate), chunks(other))]
    own = [window(chunks(rows), zh, 4) for rows in own]
    pieces = matmul(jnp.concatenate(own, axis=0), panels[0], ((1,), (1,))).astype(BF)
    first = add(lax.all_to_all(pieces.reshape(4, 128, 1024), "y", 0, 0))
    own = chunks(window(own, y, 4))
    pieces = [matmul(rows, panels[1], ((1,), (1,))).astype(BF) for rows in own]
    second = add(scatter(pieces, "y"))
    part = jnp.concatenate([first, second], axis=1)
    part = add(scatter(chunks(part), "zh"))
    near = lax.all_gather(part, "zh", axis=0, tiled=True)
    after, before = fetch(near, "y", 1), fetch(near, "y", 3)
    far = fetch(after[:64], "y", 1), fetch(before[64:], "y", 3)

    panel = jnp.concatenate(panels, axis=0)

    def product(rows):
        return matmul(rows, panel, ((1,), (0,)))

    first = core_sum([(m[:64], m[64:]) for m in map(product, (near, after, before))])
    second = core_sum([(product(far[0]), product(far[1]))])
    inner = [first[:64], first[64:128], second, first[128:]]
    panels = panels_of(jnp.concatenate(inner, axis=0).astype(BF))

    back = lax.rem(4 - y, 4)
    gram = [(near[:64], near[64:]), (after[:64], after[64:]), far, (before[:64], before[64:])]
    mixed = []
    for rows in zip(*gram):
        rows = window(rows, back, 4)
        halves = jnp.split(rows, 2, axis=1)
        halves = [lax.dynamic_slice_in_dim(jnp.concatenate([h, h[:, :768]], axis=1), y * 256, 1024, 1) for h in halves]
        mixed.append(sum(matmul(h, panel, ((1,), (0,))) for h, panel in zip(halves, panels)))
    mixed = mixed[0] + swap(mixed[1], "core")
    mine = iterate.astype(F32)
    inner = window(inner, back, 4)
    return math.sqrt(COLS) * (coef_a * mine + (coef_b * inner + coef_c * mixed))


def solution(mesh):
    fine = Mesh(mesh.devices.reshape(4, 2, 2, 4, 4), (*ROW, *COL))
    placed = P(ROW, COL)
    return jax.shard_map(
        per_device, mesh=fine, in_specs=(placed,), out_specs=placed, check_vma=False
    )
```

time: 160 us -> 151 us (0.944)
  waiting for transfers between devices: 82.1 us -> 64.9 us
  blocking collectives: 0 us -> 12 us
  local copies, waits for them, and re-layouts: 10.4 us -> 1.92 us
  starting transfers between devices: 54.7 us -> 58.9 us
    ppermute x28 -> x20, waiting for transfers between devices: 73.9 us -> 61.3 us  [send(): lax.ppermute(array, axis, [(i, (i + k) % 4) for i in range(4)])]
    all_gather x0 -> x1, blocking collectives: none -> 12 us  [per_device(): near = lax.all_gather(part, 'zh', axis=0, tiled=True)]
    ppermute x10 -> x8, starting transfers between devices: 18.1 us -> 26.8 us  [swap(): return lax.ppermute(array, axis, [(0, 1), (1, 0)])]
    ppermute x28 -> x20, starting transfers between devices: 36.7 us -> 28.6 us  [send(): lax.ppermute(array, axis, [(i, (i + k) % 4) for i in range(4)])]
    unnamed x46 -> x27, local copies, waits for them, and re-layouts: 6.88 us -> 0.46 us
    ppermute x10 -> x8, waiting for transfers between devices: 8.15 us -> 3.63 us  [swap(): return lax.ppermute(array, axis, [(0, 1), (1, 0)])]
    all_to_all x0 -> x1, starting transfers between devices: none -> 3.53 us  [per_device(): first = add(lax.all_to_all(pieces.reshape(4, 128, 1024), 'y', 0, 0))]
    dot_general x13 -> x14, matrix products: 8.69 us -> 8.59 us  [matmul(): return lax.dot_general(a, b, (dims, ((), ())), preferred_element_type=F32)]
  transfers between devices with their start and end apart: 38 -> 29, of which waited for: 24 -> 18; matrix products, arithmetic and copies ran while one was open for 10% -> 7% of each run, Pallas kernels for 0% -> 0%
where the time goes in v9:
time: 151 us
  waiting for transfers between devices  64.9 us (43%)
  starting transfers between devices  58.9 us (39%)
  blocking collectives  12 us (8%)
  matrix products  8.59 us (6%)
  other arithmetic  4.12 us (3%)
  local copies, waits for them, and re-layouts  1.92 us (1%)
    ppermute x20, waiting for transfers between devices, send(): lax.ppermute(array, axis, [(i, (i + k) % 4) for i in range(4)])  61.3 us
    ppermute x20, starting transfers between devices, send(): lax.ppermute(array, axis, [(i, (i + k) % 4) for i in range(4)])  28.6 us
    ppermute x8, starting transfers between devices, swap(): return lax.ppermute(array, axis, [(0, 1), (1, 0)])  26.8 us
    all_gather x1, blocking collectives, per_device(): near = lax.all_gather(part, 'zh', axis=0, tiled=True)  12 us
    dot_general x14, matrix products, matmul(): return lax.dot_general(a, b, (dims, ((), ())), preferred_element_type=F32)  8.59 us
    ppermute x8, waiting for transfers between devices, swap(): return lax.ppermute(array, axis, [(0, 1), (1, 0)])  3.63 us
    all_to_all x1, starting transfers between devices, per_device(): first = add(lax.all_to_all(pieces.reshape(4, 128, 1024), 'y', 0, 0))  3.53 us
  transfers between devices with their start and end apart: 29, of which 18 were waited for; matrix products, arithmetic and copies ran while one was open for 7% of the time, Pallas kernels for 0%

profile of v9, /device:TPU:1, one launch (start us, length us, event | category | flops | bytes accessed | tf_op | source)
XLA Modules:
  0.0 151.0 jit_solution(1984230834820628654)
XLA Ops:
  0.0 3.2 %collective-permute-start = (bf16[256,512]{1,0:T(8,128)(2,1)}, bf16[256,512]{1,0:T(8,128)(2,1)S(1)}, u32[]{:S(2)}, u32[]{:S(2)}) collective-permute-start(bf16[256,512]{1,0:T(8,128)(2,1)} %param.1), channel_id=1, source_target_pairs={{0,16},{16,0},{1,17},{17,1},{2,18},{18,2},{3,19},{19,3},{4,20},{20... | collective-permute-start | bytes 786440 | tf_op jit(solution)/shard_map/ppermute | solution.py:21
  3.2 2.7 %collective-permute-start.2 = (bf16[256,512]{1,0:T(8,128)(2,1)}, bf16[256,512]{1,0:T(8,128)(2,1)S(1)}, u32[]{:S(2)}, u32[]{:S(2)}) collective-permute-start(bf16[256,512]{1,0:T(8,128)(2,1)} %param.1), channel_id=1, source_target_pairs={{0,128},{64,192},{128,0},{192,64},{1,129},{65,193},{129,1},{193,65... | collective-permute-start | bytes 786440 | tf_op jit(solution)/shard_map/ppermute | solution.py:25
  5.9 0.9 collective-permute-start.1
  6.8 0.6 collective-permute-start.3
  7.4 1.0 fusion.74
  8.4 0.3 constant_dynamic-update-slice_fusion.6
  8.7 0.3 constant_dynamic-update-slice_fusion.5
  9.6 3.0 %collective-permute-done.2 = bf16[256,512]{1,0:T(8,128)(2,1)S(1)} collective-permute-done((bf16[256,512]{1,0:T(8,128)(2,1)}, bf16[256,512]{1,0:T(8,128)(2,1)S(1)}, u32[]{:S(2)}, u32[]{:S(2)}) %collective-permute-start.2) | collective-permute-done | bytes 262176 | tf_op jit(solution)/shard_map/ppermute | solution.py:25
  12.6 5.5 %collective-permute-done.1 = bf16[256,512]{1,0:T(8,128)(2,1)S(1)} collective-permute-done((bf16[256,512]{1,0:T(8,128)(2,1)}, bf16[256,512]{1,0:T(8,128)(2,1)S(1)}, u32[]{:S(2)}, u32[]{:S(2)}) %collective-permute-start.1) | collective-permute-done | bytes 262176 | tf_op jit(solution)/shard_map/ppermute | solution.py:25
  18.2 0.6 collective-permute-done.3
  19.0 1.7 %convolution_convert_fusion = bf16[512,1024]{1,0:T(8,128)(2,1)} fusion(bf16[1024,512]{1,0:T(8,128)(2,1)S(1)} %bitcast.65, bf16[128,512]{1,0:T(8,128)(2,1)S(1)} %get-tuple-element.6, bf16[128,512]{1,0:T(8,128)(2,1)S(1)} %get-tuple-element.8, bf16[128,512]{1,0:T(8,128)(2,1)S(1)} %get-tuple-element.10, bf16[128,512]{1,0:T(8,128)(2,1)S(1)} %get-tuple-element.12), kind=kOutput, calls=%fused_computation.1 | convolution fusion | flops 539492352 | bytes 2621440 | tf_op jit(solution)/shard_map/dot_general | solution.py:56
  20.7 1.1 collective-permute-start.7
  21.8 1.5 %collective-permute-start.5 = (bf16[256,512]{1,0:T(8,128)(2,1)S(1)}, bf16[256,512]{1,0:T(8,128)(2,1)}, u32[]{:S(2)}, u32[]{:S(2)}) collective-permute-start(bf16[256,512]{1,0:T(8,128)(2,1)S(1)} %collective-permute-done.4), channel_id=1, source_target_pairs={{0,192},{64,0},{128,64},{192,128},{1,193},{65,1},{129,65},{193,129... | collective-permute-start | bytes 786440 | tf_op jit(solution)/shard_map/ppermute | solution.py:25
  23.4 1.5 collective-permute-start.6
  24.9 3.5 %all-to-all-start = ((bf16[4,128,1024]{2,1,0:T(8,128)(2,1)}), bf16[4,128,1024]{2,1,0:T(8,128)(2,1)S(1)}, u32[]{:S(2)}, u32[]{:S(2)}) async-start(bf16[4,128,1024]{2,1,0:T(8,128)(2,1)} %bitcast.5), calls=%async_computation | async-start | bytes 2097152 | tf_op jit(solution)/shard_map/all_to_all | solution.py:81
  28.4 0.8 collective-permute-done.7
  29.2 0.9 collective-permute-done.6
  30.2 1.2 pad_maximum_fusion.2
  31.5 0.5 convolution_convert_fusion.3
  32.0 1.2 collective-permute-start.8
  33.2 0.5 convolution_convert_fusion.2
  33.7 1.6 %collective-permute-start.9 = (bf16[128,1024]{1,0:T(8,128)(2,1)S(1)}, bf16[128,1024]{1,0:T(8,128)(2,1)S(1)}, u32[]{:S(2)}, u32[]{:S(2)}) collective-permute-start(bf16[128,1024]{1,0:T(8,128)(2,1)S(1)} %convolution_convert_fusion.2), channel_id=1, source_target_pairs={{0,3},{1,0},{2,1},{3,2},{4,7},{5,4},{6,5},{7,6},{8,11},{9,8},{10,9... | collective-permute-start | bytes 786440 | tf_op jit(solution)/shard_map/ppermute | solution.py:25
  35.3 0.5 convolution_convert_fusion.1
  35.8 1.6 %collective-permute-start.10 = (bf16[128,1024]{1,0:T(8,128)(2,1)S(1)}, bf16[128,1024]{1,0:T(8,128)(2,1)S(1)}, u32[]{:S(2)}, u32[]{:S(2)}) collective-permute-start(bf16[128,1024]{1,0:T(8,128)(2,1)S(1)} %convolution_convert_fusion.1), channel_id=1, source_target_pairs={{0,2},{1,3},{2,0},{3,1},{4,6},{5,7},{6,4},{7,5},{8,10},{9,11},{10,... | collective-permute-start | bytes 786440 | tf_op jit(solution)/shard_map/ppermute | solution.py:25
  37.4 10.1 %collective-permute-done.8 = bf16[128,1024]{1,0:T(8,128)(2,1)S(1)} collective-permute-done((bf16[128,1024]{1,0:T(8,128)(2,1)S(1)}, bf16[128,1024]{1,0:T(8,128)(2,1)S(1)}, u32[]{:S(2)}, u32[]{:S(2)}) %collective-permute-start.8) | collective-permute-done | bytes 262176 | tf_op jit(solution)/shard_map/ppermute | solution.py:25
  47.5 6.0 %collective-permute-done.10 = bf16[128,1024]{1,0:T(8,128)(2,1)S(1)} collective-permute-done((bf16[128,1024]{1,0:T(8,128)(2,1)S(1)}, bf16[128,1024]{1,0:T(8,128)(2,1)S(1)}, u32[]{:S(2)}, u32[]{:S(2)}) %collective-permute-start.10) | collective-permute-done | bytes 262176 | tf_op jit(solution)/shard_map/ppermute | solution.py:25
  53.4 0.5 fusion.5
  54.2 1.8 %collective-permute-start.11 = (bf16[32,2048]{1,0:T(8,128)(2,1)S(1)}, bf16[32,2048]{1,0:T(8,128)(2,1)S(1)}, u32[]{:S(2)}, u32[]{:S(2)}) collective-permute-start(bf16[32,2048]{1,0:T(8,128)(2,1)S(1)} %get-tuple-element.29), channel_id=1, source_target_pairs={{0,4},{4,8},{8,12},{12,0},{1,5},{5,9},{9,13},{13,1},{2,6},{6,10},{... | collective-permute-start | bytes 393224 | tf_op jit(solution)/shard_map/ppermute | solution.py:25
  56.0 3.1 %collective-permute-start.12 = (bf16[32,2048]{1,0:T(8,128)(2,1)S(1)}, bf16[32,2048]{1,0:T(8,128)(2,1)S(1)}, u32[]{:S(2)}, u32[]{:S(2)}) collective-permute-start(bf16[32,2048]{1,0:T(8,128)(2,1)S(1)} %get-tuple-element.31), channel_id=1, source_target_pairs={{0,12},{4,0},{8,4},{12,8},{1,13},{5,1},{9,5},{13,9},{2,14},{6,2},{... | collective-permute-start | bytes 393224 | tf_op jit(solution)/shard_map/ppermute | solution.py:25
  59.1 4.2 %collective-permute-start.13 = (bf16[32,2048]{1,0:T(8,128)(2,1)S(1)}, bf16[32,2048]{1,0:T(8,128)(2,1)}, u32[]{:S(2)}, u32[]{:S(2)}) collective-permute-start(bf16[32,2048]{1,0:T(8,128)(2,1)S(1)} %get-tuple-element.30), channel_id=1, source_target_pairs={{0,8},{4,12},{8,0},{12,4},{1,9},{5,13},{9,1},{13,5},{2,10},{6,14},... | collective-permute-start | bytes 393224 | tf_op jit(solution)/shard_map/ppermute | solution.py:25
  63.3 0.8 collective-permute-done.12
  64.1 6.5 %collective-permute-done.13 = bf16[32,2048]{1,0:T(8,128)(2,1)} collective-permute-done((bf16[32,2048]{1,0:T(8,128)(2,1)S(1)}, bf16[32,2048]{1,0:T(8,128)(2,1)}, u32[]{:S(2)}, u32[]{:S(2)}) %collective-permute-start.13) | collective-permute-done | bytes 131104 | tf_op jit(solution)/shard_map/ppermute | solution.py:25
  70.5 1.0 add_convert_fusion.1
  71.5 12.0 %all_gather.3 = bf16[128,2048]{1,0:T(8,128)(2,1)S(1)} all-gather(bf16[32,2048]{1,0:T(8,128)(2,1)S(1)} %add_convert_fusion.1), channel_id=1, replica_groups=mesh['x'=4,'zl'=2,'core'=2,'zh'=4,'y'=4] {'zh'}, dimensions={0}, use_global_device_ids=true | all-gather | bytes 655360 | tf_op jit(solution)/shard_map/all_gather | solution.py:87
  83.5 1.4 collective-permute-start.14
  85.0 0.4 fusion.61
  85.5 6.1 %collective-permute-done.14 = bf16[128,2048]{1,0:T(8,128)(2,1)S(1)} collective-permute-done((bf16[128,2048]{1,0:T(8,128)(2,1)S(1)}, bf16[128,2048]{1,0:T(8,128)(2,1)S(1)}, u32[]{:S(2)}, u32[]{:S(2)}) %collective-permute-start.14) | collective-permute-done | bytes 524320 | tf_op jit(solution)/shard_map/ppermute | solution.py:25
  91.6 2.7 %collective-permute-start.17 = (bf16[64,2048]{1,0:T(8,128)(2,1)S(1)}, bf16[64,2048]{1,0:T(8,128)(2,1)S(1)}, u32[]{:S(2)}, u32[]{:S(2)}) collective-permute-start(bf16[64,2048]{1,0:T(8,128)(2,1)S(1)} %get-tuple-element.28), channel_id=1, source_target_pairs={{0,3},{1,0},{2,1},{3,2},{4,7},{5,4},{6,5},{7,6},{8,11},{9,8},{10,9... | collective-permute-start | bytes 786440 | tf_op jit(solution)/shard_map/ppermute | solution.py:25
  94.3 0.4 fusion.60
  94.8 0.5 fusion.59
  95.3 11.6 %collective-permute-start.16 = (f32[192,512]{1,0:T(8,128)S(1)}, f32[192,512]{1,0:T(8,128)S(1)}, u32[]{:S(2)}, u32[]{:S(2)}) collective-permute-start(f32[192,512]{1,0:T(8,128)S(1)} %pad_maximum_fusion.5), channel_id=1, source_target_pairs={{0,16},{16,0},{1,17},{17,1},{2,18},{18,2},{3,19},{19,3},{4,20},{20... | collective-permute-start | bytes 1179656 | tf_op jit(solution)/shard_map/ppermute | solution.py:21
  107.4 0.9 collective-permute-done.16
  108.4 5.2 %collective-permute-done.18 = bf16[64,2048]{1,0:T(8,128)(2,1)S(1)} collective-permute-done((bf16[64,2048]{1,0:T(8,128)(2,1)S(1)}, bf16[64,2048]{1,0:T(8,128)(2,1)S(1)}, u32[]{:S(2)}, u32[]{:S(2)}) %collective-permute-start.18) | collective-permute-done | bytes 262176 | tf_op jit(solution)/shard_map/ppermute | solution.py:25
  113.5 0.5 fusion.58
  114.0 4.5 %collective-permute-start.19 = (f32[64,512]{1,0:T(8,128)S(1)}, f32[64,512]{1,0:T(8,128)S(1)}, u32[]{:S(2)}, u32[]{:S(2)}) collective-permute-start(f32[64,512]{1,0:T(8,128)S(1)} %fusion.58), channel_id=1, source_target_pairs={{0,16},{16,0},{1,17},{17,1},{2,18},{18,2},{3,19},{19,3},{4,20},{20... | collective-permute-start | bytes 393224 | tf_op jit(solution)/shard_map/ppermute | solution.py:21
  118.7 0.8 collective-permute-done.19
  119.5 0.5 constant_dynamic-update-slice_fusion.10
  120.0 0.9 collective-permute-start.20
  120.9 1.1 collective-permute-start.21
  122.0 0.4 collective-permute-start.22
  122.5 1.9 %collective-permute-start.23 = (bf16[256,512]{1,0:T(8,128)(2,1)S(1)}, bf16[256,512]{1,0:T(8,128)(2,1)S(1)}, u32[]{:S(2)}, u32[]{:S(2)}) collective-permute-start(bf16[256,512]{1,0:T(8,128)(2,1)S(1)} %maximum_convert_fusion), channel_id=1, source_target_pairs={{0,32},{32,0},{1,33},{33,1},{2,34},{34,2},{3,35},{35,3},{4,36},{36... | collective-permute-start | bytes 786440 | tf_op jit(solution)/shard_map/ppermute | solution.py:21
  124.3 5.3 %collective-permute-done.21 = bf16[256,512]{1,0:T(8,128)(2,1)S(1)} collective-permute-done((bf16[256,512]{1,0:T(8,128)(2,1)S(1)}, bf16[256,512]{1,0:T(8,128)(2,1)S(1)}, u32[]{:S(2)}, u32[]{:S(2)}) %collective-permute-start.21) | collective-permute-done | bytes 262176 | tf_op jit(solution)/shard_map/ppermute | solution.py:25
  129.6 1.4 collective-permute-start.25
  131.1 5.1 %collective-permute-done.22 = bf16[256,512]{1,0:T(8,128)(2,1)S(1)} collective-permute-done((bf16[256,512]{1,0:T(8,128)(2,1)S(1)}, bf16[256,512]{1,0:T(8,128)(2,1)S(1)}, u32[]{:S(2)}, u32[]{:S(2)}) %collective-permute-start.22) | collective-permute-done | bytes 262176 | tf_op jit(solution)/shard_map/ppermute | solution.py:25
  136.4 1.1 collective-permute-start.24
  137.5 0.4 collective-permute-start.26
  137.9 0.4 fusion.9
  138.4 5.5 %collective-permute-done.24 = bf16[256,512]{1,0:T(8,128)(2,1)S(1)} collective-permute-done((bf16[256,512]{1,0:T(8,128)(2,1)S(1)}, bf16[256,512]{1,0:T(8,128)(2,1)S(1)}, u32[]{:S(2)}, u32[]{:S(2)}) %collective-permute-start.24) | collective-permute-done | bytes 262176 | tf_op jit(solution)/shard_map/ppermute | solution.py:25
  143.8 0.9 collective-permute-done.26
  144.9 0.4 convolution_add_fusion
  145.4 2.8 %collective-permute-start.27 = (f32[256,512]{1,0:T(8,128)S(1)}, f32[256,512]{1,0:T(8,128)S(1)}, u32[]{:S(2)}, u32[]{:S(2)}) collective-permute-start(f32[256,512]{1,0:T(8,128)S(1)} %convolution_add_fusion), channel_id=1, source_target_pairs={{0,16},{16,0},{1,17},{17,1},{2,18},{18,2},{3,19},{19,3},{4,20},{20... | collective-permute-start | bytes 1572872 | tf_op jit(solution)/shard_map/ppermute | solution.py:21
  148.2 0.4 fusion.14
  148.6 1.0 collective-permute-done.27
  149.7 1.3 add_multiply_fusion
  (66 shorter events, 2.4 us)
Async XLA Ops:
  0.0 18.8 %copy-start = (bf16[256,512]{1,0:T(8,128)(2,1)S(1)}, bf16[256,512]{1,0:T(8,128)(2,1)}, u32[]{:S(2)}) copy-start(bf16[256,512]{1,0:T(8,128)(2,1)} %param.1) | copy-start | bytes 786436
  0.0 8.3 %collective-permute-start = (bf16[256,512]{1,0:T(8,128)(2,1)}, bf16[256,512]{1,0:T(8,128)(2,1)S(1)}, u32[]{:S(2)}, u32[]{:S(2)}) collective-permute-start(bf16[256,512]{1,0:T(8,128)(2,1)} %param.1), channel_id=1, source_target_pairs={{0,16},{16,0},{1,17},{17,1},{2,18},{18,2},{3,19},{19,3},{4,20},{20... | collective-permute-start | bytes 786440 | tf_op jit(solution)/shard_map/ppermute | solution.py:21
  3.2 17.5 %collective-permute-start.4 = (bf16[256,512]{1,0:T(8,128)(2,1)}, bf16[256,512]{1,0:T(8,128)(2,1)S(1)}, u32[]{:S(2)}, u32[]{:S(2)}) collective-permute-start(bf16[256,512]{1,0:T(8,128)(2,1)} %param.1), channel_id=1, source_target_pairs={{0,32},{32,0},{1,33},{33,1},{2,34},{34,2},{3,35},{35,3},{4,36},{36... | collective-permute-start | bytes 786440 | tf_op jit(solution)/shard_map/ppermute | solution.py:21
  3.2 9.4 %collective-permute-start.2 = (bf16[256,512]{1,0:T(8,128)(2,1)}, bf16[256,512]{1,0:T(8,128)(2,1)S(1)}, u32[]{:S(2)}, u32[]{:S(2)}) collective-permute-start(bf16[256,512]{1,0:T(8,128)(2,1)} %param.1), channel_id=1, source_target_pairs={{0,128},{64,192},{128,0},{192,64},{1,129},{65,193},{129,1},{193,65... | collective-permute-start | bytes 786440 | tf_op jit(solution)/shard_map/ppermute | solution.py:25
  5.9 12.3 %collective-permute-start.1 = (bf16[256,512]{1,0:T(8,128)(2,1)}, bf16[256,512]{1,0:T(8,128)(2,1)S(1)}, u32[]{:S(2)}, u32[]{:S(2)}) collective-permute-start(bf16[256,512]{1,0:T(8,128)(2,1)} %param.1), channel_id=1, source_target_pairs={{0,192},{64,0},{128,64},{192,128},{1,193},{65,1},{129,65},{193,129... | collective-permute-start | bytes 786440 | tf_op jit(solution)/shard_map/ppermute | solution.py:25
  6.8 12.0 %collective-permute-start.3 = (bf16[256,512]{1,0:T(8,128)(2,1)}, bf16[256,512]{1,0:T(8,128)(2,1)S(1)}, u32[]{:S(2)}, u32[]{:S(2)}) collective-permute-start(bf16[256,512]{1,0:T(8,128)(2,1)} %param.1), channel_id=1, source_target_pairs={{0,64},{64,128},{128,192},{192,0},{1,65},{65,129},{129,193},{193,1... | collective-permute-start | bytes 786440 | tf_op jit(solution)/shard_map/ppermute | solution.py:25
  18.9 1.8 %copy-start.1 = (bf16[4,4,64,512]{3,2,1,0:T(8,128)(2,1)}, bf16[4,4,64,512]{3,2,1,0:T(8,128)(2,1)S(1)}, u32[]{:S(2)}) copy-start(bf16[4,4,64,512]{3,2,1,0:T(8,128)(2,1)S(1)} %pad_maximum_fusion.1) | copy-start | bytes 3145732
  20.7 8.5 %collective-permute-start.7 = (bf16[256,512]{1,0:T(8,128)(2,1)S(1)}, bf16[256,512]{1,0:T(8,128)(2,1)S(1)}, u32[]{:S(2)}, u32[]{:S(2)}) collective-permute-start(bf16[256,512]{1,0:T(8,128)(2,1)S(1)} %collective-permute-done.4), channel_id=1, source_target_pairs={{0,64},{64,128},{128,192},{192,0},{1,65},{65,129},{129,193},{193,1... | collective-permute-start | bytes 786440 | tf_op jit(solution)/shard_map/ppermute | solution.py:25
  21.8 7.4 %collective-permute-start.5 = (bf16[256,512]{1,0:T(8,128)(2,1)S(1)}, bf16[256,512]{1,0:T(8,128)(2,1)}, u32[]{:S(2)}, u32[]{:S(2)}) collective-permute-start(bf16[256,512]{1,0:T(8,128)(2,1)S(1)} %collective-permute-done.4), channel_id=1, source_target_pairs={{0,192},{64,0},{128,64},{192,128},{1,193},{65,1},{129,65},{193,129... | collective-permute-start | bytes 786440 | tf_op jit(solution)/shard_map/ppermute | solution.py:25
  23.4 6.8 %collective-permute-start.6 = (bf16[256,512]{1,0:T(8,128)(2,1)S(1)}, bf16[256,512]{1,0:T(8,128)(2,1)}, u32[]{:S(2)}, u32[]{:S(2)}) collective-permute-start(bf16[256,512]{1,0:T(8,128)(2,1)S(1)} %collective-permute-done.2), channel_id=1, source_target_pairs={{0,32},{32,0},{1,33},{33,1},{2,34},{34,2},{3,35},{35,3},{4,36},{36... | collective-permute-start | bytes 786440 | tf_op jit(solution)/shard_map/ppermute | solution.py:21
  24.9 29.1 %all-to-all-start = ((bf16[4,128,1024]{2,1,0:T(8,128)(2,1)}), bf16[4,128,1024]{2,1,0:T(8,128)(2,1)S(1)}, u32[]{:S(2)}, u32[]{:S(2)}) async-start(bf16[4,128,1024]{2,1,0:T(8,128)(2,1)} %bitcast.5), calls=%async_computation | async-start | bytes 2097152 | tf_op jit(solution)/shard_map/all_to_all | solution.py:81
  28.4 1.8 %copy-start.4 = (bf16[896,512]{1,0:T(8,128)(2,1)}, bf16[896,512]{1,0:T(8,128)(2,1)S(1)}, u32[]{:S(2)}) copy-start(bf16[896,512]{1,0:T(8,128)(2,1)S(1)} %constant_dynamic-update-slice_fusion) | copy-start | bytes 2752516
  30.2 1.3 copy-start.5
  32.0 15.5 %collective-permute-start.8 = (bf16[128,1024]{1,0:T(8,128)(2,1)S(1)}, bf16[128,1024]{1,0:T(8,128)(2,1)S(1)}, u32[]{:S(2)}, u32[]{:S(2)}) collective-permute-start(bf16[128,1024]{1,0:T(8,128)(2,1)S(1)} %convolution_convert_fusion.3), channel_id=1, source_target_pairs={{0,1},{1,2},{2,3},{3,0},{4,5},{5,6},{6,7},{7,4},{8,9},{9,10},{10,1... | collective-permute-start | bytes 786440 | tf_op jit(solution)/shard_map/ppermute | solution.py:25
  33.7 13.8 %collective-permute-start.9 = (bf16[128,1024]{1,0:T(8,128)(2,1)S(1)}, bf16[128,1024]{1,0:T(8,128)(2,1)S(1)}, u32[]{:S(2)}, u32[]{:S(2)}) collective-permute-start(bf16[128,1024]{1,0:T(8,128)(2,1)S(1)} %convolution_convert_fusion.2), channel_id=1, source_target_pairs={{0,3},{1,0},{2,1},{3,2},{4,7},{5,4},{6,5},{7,6},{8,11},{9,8},{10,9... | collective-permute-start | bytes 786440 | tf_op jit(solution)/shard_map/ppermute | solution.py:25
  35.8 17.6 %collective-permute-start.10 = (bf16[128,1024]{1,0:T(8,128)(2,1)S(1)}, bf16[128,1024]{1,0:T(8,128)(2,1)S(1)}, u32[]{:S(2)}, u32[]{:S(2)}) collective-permute-start(bf16[128,1024]{1,0:T(8,128)(2,1)S(1)} %convolution_convert_fusion.1), channel_id=1, source_target_pairs={{0,2},{1,3},{2,0},{3,1},{4,6},{5,7},{6,4},{7,5},{8,10},{9,11},{10,... | collective-permute-start | bytes 786440 | tf_op jit(solution)/shard_map/ppermute | solution.py:25
  54.1 30.9 %copy-start.2 = (bf16[4,4,64,512]{3,2,1,0:T(8,128)(2,1)S(1)}, bf16[4,4,64,512]{3,2,1,0:T(8,128)(2,1)}, u32[]{:S(2)}) copy-start(bf16[4,4,64,512]{3,2,1,0:T(8,128)(2,1)} %copy-done.1) | copy-start | bytes 3145732
  54.2 9.1 %collective-permute-start.11 = (bf16[32,2048]{1,0:T(8,128)(2,1)S(1)}, bf16[32,2048]{1,0:T(8,128)(2,1)S(1)}, u32[]{:S(2)}, u32[]{:S(2)}) collective-permute-start(bf16[32,2048]{1,0:T(8,128)(2,1)S(1)} %get-tuple-element.29), channel_id=1, source_target_pairs={{0,4},{4,8},{8,12},{12,0},{1,5},{5,9},{9,13},{13,1},{2,6},{6,10},{... | collective-permute-start | bytes 393224 | tf_op jit(solution)/shard_map/ppermute | solution.py:25
  56.0 8.1 %collective-permute-start.12 = (bf16[32,2048]{1,0:T(8,128)(2,1)S(1)}, bf16[32,2048]{1,0:T(8,128)(2,1)S(1)}, u32[]{:S(2)}, u32[]{:S(2)}) collective-permute-start(bf16[32,2048]{1,0:T(8,128)(2,1)S(1)} %get-tuple-element.31), channel_id=1, source_target_pairs={{0,12},{4,0},{8,4},{12,8},{1,13},{5,1},{9,5},{13,9},{2,14},{6,2},{... | collective-permute-start | bytes 393224 | tf_op jit(solution)/shard_map/ppermute | solution.py:25
  59.1 11.5 %collective-permute-start.13 = (bf16[32,2048]{1,0:T(8,128)(2,1)S(1)}, bf16[32,2048]{1,0:T(8,128)(2,1)}, u32[]{:S(2)}, u32[]{:S(2)}) collective-permute-start(bf16[32,2048]{1,0:T(8,128)(2,1)S(1)} %get-tuple-element.30), channel_id=1, source_target_pairs={{0,8},{4,12},{8,0},{12,4},{1,9},{5,13},{9,1},{13,5},{2,10},{6,14},... | collective-permute-start | bytes 393224 | tf_op jit(solution)/shard_map/ppermute | solution.py:25
  83.5 8.0 %collective-permute-start.14 = (bf16[128,2048]{1,0:T(8,128)(2,1)S(1)}, bf16[128,2048]{1,0:T(8,128)(2,1)S(1)}, u32[]{:S(2)}, u32[]{:S(2)}) collective-permute-start(bf16[128,2048]{1,0:T(8,128)(2,1)S(1)} %all_gather.3), channel_id=1, source_target_pairs={{0,3},{1,0},{2,1},{3,2},{4,7},{5,4},{6,5},{7,6},{8,11},{9,8},{10,9... | collective-permute-start | bytes 1572872 | tf_op jit(solution)/shard_map/ppermute | solution.py:25
  84.9 9.9 %collective-permute-start.15 = (bf16[128,2048]{1,0:T(8,128)(2,1)S(1)}, bf16[128,2048]{1,0:T(8,128)(2,1)S(1)}, u32[]{:S(2)}, u32[]{:S(2)}) collective-permute-start(bf16[128,2048]{1,0:T(8,128)(2,1)S(1)} %all_gather.3), channel_id=1, source_target_pairs={{0,1},{1,2},{2,3},{3,0},{4,5},{5,6},{6,7},{7,4},{8,9},{9,10},{10,1... | collective-permute-start | bytes 1572872 | tf_op jit(solution)/shard_map/ppermute | solution.py:25
  91.6 15.3 %collective-permute-start.17 = (bf16[64,2048]{1,0:T(8,128)(2,1)S(1)}, bf16[64,2048]{1,0:T(8,128)(2,1)S(1)}, u32[]{:S(2)}, u32[]{:S(2)}) collective-permute-start(bf16[64,2048]{1,0:T(8,128)(2,1)S(1)} %get-tuple-element.28), channel_id=1, source_target_pairs={{0,3},{1,0},{2,1},{3,2},{4,7},{5,4},{6,5},{7,6},{8,11},{9,8},{10,9... | collective-permute-start | bytes 786440 | tf_op jit(solution)/shard_map/ppermute | solution.py:25
  95.3 12.9 %collective-permute-start.16 = (f32[192,512]{1,0:T(8,128)S(1)}, f32[192,512]{1,0:T(8,128)S(1)}, u32[]{:S(2)}, u32[]{:S(2)}) collective-permute-start(f32[192,512]{1,0:T(8,128)S(1)} %pad_maximum_fusion.5), channel_id=1, source_target_pairs={{0,16},{16,0},{1,17},{17,1},{2,18},{18,2},{3,19},{19,3},{4,20},{20... | collective-permute-start | bytes 1179656 | tf_op jit(solution)/shard_map/ppermute | solution.py:21
  107.0 6.5 %collective-permute-start.18 = (bf16[64,2048]{1,0:T(8,128)(2,1)S(1)}, bf16[64,2048]{1,0:T(8,128)(2,1)S(1)}, u32[]{:S(2)}, u32[]{:S(2)}) collective-permute-start(bf16[64,2048]{1,0:T(8,128)(2,1)S(1)} %get-tuple-element.26), channel_id=1, source_target_pairs={{0,1},{1,2},{2,3},{3,0},{4,5},{5,6},{6,7},{7,4},{8,9},{9,10},{10,1... | collective-permute-start | bytes 786440 | tf_op jit(solution)/shard_map/ppermute | solution.py:25
  107.3 6.3 %copy-start.3 = (bf16[4,4,64,512]{3,2,1,0:T(8,128)(2,1)S(1)}, bf16[4,4,64,512]{3,2,1,0:T(8,128)(2,1)}, u32[]{:S(2)}) copy-start(bf16[4,4,64,512]{3,2,1,0:T(8,128)(2,1)} %copy-done.1) | copy-start | bytes 3145732
  114.0 5.5 %collective-permute-start.19 = (f32[64,512]{1,0:T(8,128)S(1)}, f32[64,512]{1,0:T(8,128)S(1)}, u32[]{:S(2)}, u32[]{:S(2)}) collective-permute-start(f32[64,512]{1,0:T(8,128)S(1)} %fusion.58), channel_id=1, source_target_pairs={{0,16},{16,0},{1,17},{17,1},{2,18},{18,2},{3,19},{19,3},{4,20},{20... | collective-permute-start | bytes 393224 | tf_op jit(solution)/shard_map/ppermute | solution.py:21
  120.0 11.1 %collective-permute-start.20 = (bf16[256,512]{1,0:T(8,128)(2,1)S(1)}, bf16[256,512]{1,0:T(8,128)(2,1)S(1)}, u32[]{:S(2)}, u32[]{:S(2)}) collective-permute-start(bf16[256,512]{1,0:T(8,128)(2,1)S(1)} %maximum_convert_fusion), channel_id=1, source_target_pairs={{0,192},{64,0},{128,64},{192,128},{1,193},{65,1},{129,65},{193,129... | collective-permute-start | bytes 786440 | tf_op jit(solution)/shard_map/ppermute | solution.py:25
  120.9 8.8 %collective-permute-start.21 = (bf16[256,512]{1,0:T(8,128)(2,1)S(1)}, bf16[256,512]{1,0:T(8,128)(2,1)S(1)}, u32[]{:S(2)}, u32[]{:S(2)}) collective-permute-start(bf16[256,512]{1,0:T(8,128)(2,1)S(1)} %maximum_convert_fusion), channel_id=1, source_target_pairs={{0,128},{64,192},{128,0},{192,64},{1,129},{65,193},{129,1},{193,65... | collective-permute-start | bytes 786440 | tf_op jit(solution)/shard_map/ppermute | solution.py:25
  122.0 14.3 %collective-permute-start.22 = (bf16[256,512]{1,0:T(8,128)(2,1)S(1)}, bf16[256,512]{1,0:T(8,128)(2,1)S(1)}, u32[]{:S(2)}, u32[]{:S(2)}) collective-permute-start(bf16[256,512]{1,0:T(8,128)(2,1)S(1)} %maximum_convert_fusion), channel_id=1, source_target_pairs={{0,64},{64,128},{128,192},{192,0},{1,65},{65,129},{129,193},{193,1... | collective-permute-start | bytes 786440 | tf_op jit(solution)/shard_map/ppermute | solution.py:25
  122.5 13.9 %collective-permute-start.23 = (bf16[256,512]{1,0:T(8,128)(2,1)S(1)}, bf16[256,512]{1,0:T(8,128)(2,1)S(1)}, u32[]{:S(2)}, u32[]{:S(2)}) collective-permute-start(bf16[256,512]{1,0:T(8,128)(2,1)S(1)} %maximum_convert_fusion), channel_id=1, source_target_pairs={{0,32},{32,0},{1,33},{33,1},{2,34},{34,2},{3,35},{35,3},{4,36},{36... | collective-permute-start | bytes 786440 | tf_op jit(solution)/shard_map/ppermute | solution.py:21
  129.6 14.2 %collective-permute-start.25 = (bf16[256,512]{1,0:T(8,128)(2,1)S(1)}, bf16[256,512]{1,0:T(8,128)(2,1)S(1)}, u32[]{:S(2)}, u32[]{:S(2)}) collective-permute-start(bf16[256,512]{1,0:T(8,128)(2,1)S(1)} %collective-permute-done.21), channel_id=1, source_target_pairs={{0,32},{32,0},{1,33},{33,1},{2,34},{34,2},{3,35},{35,3},{4,36},{36... | collective-permute-start | bytes 786440 | tf_op jit(solution)/shard_map/ppermute | solution.py:21
  136.4 7.5 %collective-permute-start.24 = (bf16[256,512]{1,0:T(8,128)(2,1)S(1)}, bf16[256,512]{1,0:T(8,128)(2,1)S(1)}, u32[]{:S(2)}, u32[]{:S(2)}) collective-permute-start(bf16[256,512]{1,0:T(8,128)(2,1)S(1)} %collective-permute-done.23), channel_id=1, source_target_pairs={{0,192},{64,0},{128,64},{192,128},{1,193},{65,1},{129,65},{193,129... | collective-permute-start | bytes 786440 | tf_op jit(solution)/shard_map/ppermute | solution.py:25
  137.5 7.3 %collective-permute-start.26 = (bf16[256,512]{1,0:T(8,128)(2,1)S(1)}, bf16[256,512]{1,0:T(8,128)(2,1)S(1)}, u32[]{:S(2)}, u32[]{:S(2)}) collective-permute-start(bf16[256,512]{1,0:T(8,128)(2,1)S(1)} %collective-permute-done.23), channel_id=1, source_target_pairs={{0,64},{64,128},{128,192},{192,0},{1,65},{65,129},{129,193},{193,1... | collective-permute-start | bytes 786440 | tf_op jit(solution)/shard_map/ppermute | solution.py:25
  145.4 4.3 %collective-permute-start.27 = (f32[256,512]{1,0:T(8,128)S(1)}, f32[256,512]{1,0:T(8,128)S(1)}, u32[]{:S(2)}, u32[]{:S(2)}) collective-permute-start(f32[256,512]{1,0:T(8,128)S(1)} %convolution_add_fusion), channel_id=1, source_target_pairs={{0,16},{16,0},{1,17},{17,1},{2,18},{18,2},{3,19},{19,3},{4,20},{20... | collective-permute-start | bytes 1572872 | tf_op jit(solution)/shard_map/ppermute | solution.py:21

commit v10 on v9

--- a/solution.py
+++ b/solution.py
@@ -60,7 +60,8 @@
     partner = swap(block, "zl")
     mine = around(block, "x")
     theirs = [partner, fetch(partner, "x", 1), swap(mine[2], "zl"), fetch(partner, "x", 3)]
-    panels = [jnp.concatenate([b.reshape(4, 1, 64, 512) for b in four], axis=1) for four in (mine, theirs)]
+    blocks = lax.optimization_barrier([*mine, *theirs])
+    panels = [jnp.concatenate([b.reshape(4, 1, 64, 512) for b in four], axis=1) for four in (blocks[:4], blocks[4:])]
     return [panel.reshape(1024, 512) for panel in panels]
 
 
@@ -75,20 +76,17 @@
     other = swap(iterate, "core")
     panels = panels_of(iterate)
 
-    own = [jnp.concatenate(rows, axis=0) for rows in zip(chunks(iterate), chunks(other))]
-    own = [window(chunks(rows), zh, 4) for rows in own]
-    pieces = matmul(jnp.concatenate(own, axis=0), panels[0], ((1,), (1,))).astype(BF)
-    first = add(lax.all_to_all(pieces.reshape(4, 128, 1024), "y", 0, 0))
-    own = chunks(window(own, y, 4))
-    pieces = [matmul(rows, panels[1], ((1,), (1,))).astype(BF) for rows in own]
-    second = add(scatter(pieces, "y"))
-    part = jnp.concatenate([first, second], axis=1)
+    panel = jnp.concatenate(panels, axis=0)
+
+    own = zip(chunks(window(chunks(iterate), y, 4)), chunks(window(chunks(other), y, 4)))
+    own = [window(chunks(jnp.concatenate(rows, axis=0)), zh, 4) for rows in own]
+    pieces = [matmul(rows, panel, ((1,), (1,))).astype(BF) for rows in own]
+    part = add(scatter(pieces, "y"))
     part = add(scatter(chunks(part), "zh"))
     near = lax.all_gather(part, "zh", axis=0, tiled=True)
     after, before = fetch(near, "y", 1), fetch(near, "y", 3)
-    far = fetch(after[:64], "y", 1), fetch(before[64:], "y", 3)
-
-    panel = jnp.concatenate(panels, axis=0)
+    sent = lax.optimization_barrier((after[:64], before[64:]))
+    far = lax.optimization_barrier((fetch(sent[0], "y", 1), fetch(sent[1], "y", 3)))
 
     def product(rows):
         return matmul(rows, panel, ((1,), (0,)))

time: 151 us -> 143 us (0.947)
  waiting for transfers between devices: 64.9 us -> 57.8 us
  other arithmetic: 4.12 us -> 2.45 us
    ppermute x20, starting transfers between devices: 28.6 us -> 36.1 us  [send(): lax.ppermute(array, axis, [(i, (i + k) % 4) for i in range(4)])]
    ppermute x20, waiting for transfers between devices: 61.3 us -> 56.1 us  [send(): lax.ppermute(array, axis, [(i, (i + k) % 4) for i in range(4)])]
    ppermute x8, starting transfers between devices: 26.8 us -> 23.1 us  [swap(): return lax.ppermute(array, axis, [(0, 1), (1, 0)])]
    all_to_all x1 -> x0, starting transfers between devices: 3.53 us -> none  [per_device(): first = add(lax.all_to_all(pieces.reshape(4, 128, 1024), 'y', 0, 0))]
    ppermute x8, waiting for transfers between devices: 3.63 us -> 1.73 us  [swap(): return lax.ppermute(array, axis, [(0, 1), (1, 0)])]
    dot_general x14 -> x13, matrix products: 8.59 us -> 8.59 us  [matmul(): return lax.dot_general(a, b, (dims, ((), ())), preferred_element_type=F32)]
  transfers between devices with their start and end apart: 29 -> 28, of which waited for: 18 -> 17; matrix products, arithmetic and copies ran while one was open for 7% -> 6% of each run, Pallas kernels for 0% -> 0%
where the time goes in v10:
time: 143 us
  starting transfers between devices  59.2 us (41%)
  waiting for transfers between devices  57.8 us (40%)
  blocking collectives  11.9 us (8%)
  matrix products  8.59 us (6%)
  local copies, waits for them, and re-layouts  2.48 us (2%)
  other arithmetic  2.45 us (2%)
    ppermute x20, waiting for transfers between devices, send(): lax.ppermute(array, axis, [(i, (i + k) % 4) for i in range(4)])  56.1 us
    ppermute x20, starting transfers between devices, send(): lax.ppermute(array, axis, [(i, (i + k) % 4) for i in range(4)])  36.1 us
    ppermute x8, starting transfers between devices, swap(): return lax.ppermute(array, axis, [(0, 1), (1, 0)])  23.1 us
    all_gather x1, blocking collectives, per_device(): near = lax.all_gather(part, 'zh', axis=0, tiled=True)  11.9 us
    dot_general x13, matrix products, matmul(): return lax.dot_general(a, b, (dims, ((), ())), preferred_element_type=F32)  8.59 us
  transfers between devices with their start and end apart: 28, of which 17 were waited for; matrix products, arithmetic and copies ran while one was open for 6% of the time, Pallas kernels for 0%

profile of v10, /device:TPU:1, one launch (start us, length us, event | category | flops | bytes accessed | tf_op | source)
XLA Modules:
  0.0 142.8 jit_solution(8083458554992417003)
XLA Ops:
  0.0 2.5 %collective-permute-start.4 = (bf16[256,512]{1,0:T(8,128)(2,1)}, bf16[256,512]{1,0:T(8,128)(2,1)S(1)}, u32[]{:S(2)}, u32[]{:S(2)}) collective-permute-start(bf16[256,512]{1,0:T(8,128)(2,1)} %param.1), channel_id=1, source_target_pairs={{0,32},{32,0},{1,33},{33,1},{2,34},{34,2},{3,35},{35,3},{4,36},{36... | collective-permute-start | bytes 786440 | tf_op jit(solution)/shard_map/ppermute | solution.py:21
  2.5 2.7 %collective-permute-start.2 = (bf16[256,512]{1,0:T(8,128)(2,1)}, bf16[256,512]{1,0:T(8,128)(2,1)S(1)}, u32[]{:S(2)}, u32[]{:S(2)}) collective-permute-start(bf16[256,512]{1,0:T(8,128)(2,1)} %param.1), channel_id=1, source_target_pairs={{0,128},{64,192},{128,0},{192,64},{1,129},{65,193},{129,1},{193,65... | collective-permute-start | bytes 786440 | tf_op jit(solution)/shard_map/ppermute | solution.py:25
  5.2 0.9 collective-permute-start.1
  6.1 0.6 collective-permute-start.3
  6.7 1.8 %collective-permute-start = (bf16[256,512]{1,0:T(8,128)(2,1)}, bf16[256,512]{1,0:T(8,128)(2,1)S(1)}, u32[]{:S(2)}, u32[]{:S(2)}) collective-permute-start(bf16[256,512]{1,0:T(8,128)(2,1)} %param.1), channel_id=1, source_target_pairs={{0,16},{16,0},{1,17},{17,1},{2,18},{18,2},{3,19},{19,3},{4,20},{20... | collective-permute-start | bytes 786440 | tf_op jit(solution)/shard_map/ppermute | solution.py:21
  8.5 0.9 split.84
  9.4 1.1 fusion.14
  10.6 2.1 %collective-permute-start.5 = (bf16[256,512]{1,0:T(8,128)(2,1)S(1)}, bf16[256,512]{1,0:T(8,128)(2,1)S(1)}, u32[]{:S(2)}, u32[]{:S(2)}) collective-permute-start(bf16[256,512]{1,0:T(8,128)(2,1)S(1)} %collective-permute-done.4), channel_id=1, source_target_pairs={{0,192},{64,0},{128,64},{192,128},{1,193},{65,1},{129,65},{193,129... | collective-permute-start | bytes 786440 | tf_op jit(solution)/shard_map/ppermute | solution.py:25
  12.8 0.1 collective-permute-start.6
  12.9 0.3 fusion.13
  13.2 4.0 %collective-permute-done.1 = bf16[256,512]{1,0:T(8,128)(2,1)S(1)} collective-permute-done((bf16[256,512]{1,0:T(8,128)(2,1)}, bf16[256,512]{1,0:T(8,128)(2,1)S(1)}, u32[]{:S(2)}, u32[]{:S(2)}) %collective-permute-start.1) | collective-permute-done | bytes 262176 | tf_op jit(solution)/shard_map/ppermute | solution.py:25
  17.2 0.3 collective-permute-done.3
  17.5 5.2 %collective-permute-done.5 = bf16[256,512]{1,0:T(8,128)(2,1)S(1)} collective-permute-done((bf16[256,512]{1,0:T(8,128)(2,1)S(1)}, bf16[256,512]{1,0:T(8,128)(2,1)S(1)}, u32[]{:S(2)}, u32[]{:S(2)}) %collective-permute-start.5) | collective-permute-done | bytes 262176 | tf_op jit(solution)/shard_map/ppermute | solution.py:25
  22.7 0.4 collective-permute-done.7
  23.1 0.1 pad_maximum_fusion.1
  23.3 0.1 pad_maximum_fusion.2
  23.4 0.9 convolution_convert_fusion.2
  24.3 1.4 collective-permute-start.8
  25.7 0.9 convolution_convert_fusion.1
  26.6 1.5 %collective-permute-start.9 = (bf16[128,2048]{1,0:T(8,128)(2,1)S(1)}, bf16[128,2048]{1,0:T(8,128)(2,1)S(1)}, u32[]{:S(2)}, u32[]{:S(2)}) collective-permute-start(bf16[128,2048]{1,0:T(8,128)(2,1)S(1)} %convolution_convert_fusion.1), channel_id=1, source_target_pairs={{0,3},{1,0},{2,1},{3,2},{4,7},{5,4},{6,5},{7,6},{8,11},{9,8},{10,9... | collective-permute-start | bytes 1572872 | tf_op jit(solution)/shard_map/ppermute | solution.py:25
  28.1 0.9 convolution_convert_fusion
  29.1 1.7 %collective-permute-start.10 = (bf16[128,2048]{1,0:T(8,128)(2,1)S(1)}, bf16[128,2048]{1,0:T(8,128)(2,1)S(1)}, u32[]{:S(2)}, u32[]{:S(2)}) collective-permute-start(bf16[128,2048]{1,0:T(8,128)(2,1)S(1)} %convolution_convert_fusion), channel_id=1, source_target_pairs={{0,2},{1,3},{2,0},{3,1},{4,6},{5,7},{6,4},{7,5},{8,10},{9,11},{10,... | collective-permute-start | bytes 1572872 | tf_op jit(solution)/shard_map/ppermute | solution.py:25
  30.8 0.9 fusion
  31.7 6.3 %collective-permute-done.8 = bf16[128,2048]{1,0:T(8,128)(2,1)S(1)} collective-permute-done((bf16[128,2048]{1,0:T(8,128)(2,1)S(1)}, bf16[128,2048]{1,0:T(8,128)(2,1)S(1)}, u32[]{:S(2)}, u32[]{:S(2)}) %collective-permute-start.8) | collective-permute-done | bytes 524320 | tf_op jit(solution)/shard_map/ppermute | solution.py:25
  38.0 0.7 collective-permute-done.9
  38.7 11.7 %collective-permute-done.10 = bf16[128,2048]{1,0:T(8,128)(2,1)S(1)} collective-permute-done((bf16[128,2048]{1,0:T(8,128)(2,1)S(1)}, bf16[128,2048]{1,0:T(8,128)(2,1)S(1)}, u32[]{:S(2)}, u32[]{:S(2)}) %collective-permute-start.10) | collective-permute-done | bytes 524320 | tf_op jit(solution)/shard_map/ppermute | solution.py:25
  50.3 0.3 add_convert_fusion
  50.6 0.7 fusion.57
  51.3 3.0 %collective-permute-start.11 = (bf16[32,2048]{1,0:T(8,128)(2,1)}, bf16[32,2048]{1,0:T(8,128)(2,1)S(1)}, u32[]{:S(2)}, u32[]{:S(2)}) collective-permute-start(bf16[32,2048]{1,0:T(8,128)(2,1)} %get-tuple-element.59), channel_id=1, source_target_pairs={{0,4},{4,8},{8,12},{12,0},{1,5},{5,9},{9,13},{13,1},{2,6},{6,10},{... | collective-permute-start | bytes 393224 | tf_op jit(solution)/shard_map/ppermute | solution.py:25
  54.3 2.1 %collective-permute-start.12 = (bf16[32,2048]{1,0:T(8,128)(2,1)S(1)}, bf16[32,2048]{1,0:T(8,128)(2,1)S(1)}, u32[]{:S(2)}, u32[]{:S(2)}) collective-permute-start(bf16[32,2048]{1,0:T(8,128)(2,1)S(1)} %get-tuple-element.61), channel_id=1, source_target_pairs={{0,12},{4,0},{8,4},{12,8},{1,13},{5,1},{9,5},{13,9},{2,14},{6,2},{... | collective-permute-start | bytes 393224 | tf_op jit(solution)/shard_map/ppermute | solution.py:25
  56.5 4.5 %collective-permute-start.13 = (bf16[32,2048]{1,0:T(8,128)(2,1)S(1)}, bf16[32,2048]{1,0:T(8,128)(2,1)S(1)}, u32[]{:S(2)}, u32[]{:S(2)}) collective-permute-start(bf16[32,2048]{1,0:T(8,128)(2,1)S(1)} %get-tuple-element.60), channel_id=1, source_target_pairs={{0,8},{4,12},{8,0},{12,4},{1,9},{5,13},{9,1},{13,5},{2,10},{6,14},... | collective-permute-start | bytes 393224 | tf_op jit(solution)/shard_map/ppermute | solution.py:25
  60.9 0.9 collective-permute-done.12
  61.9 6.7 %collective-permute-done.13 = bf16[32,2048]{1,0:T(8,128)(2,1)S(1)} collective-permute-done((bf16[32,2048]{1,0:T(8,128)(2,1)S(1)}, bf16[32,2048]{1,0:T(8,128)(2,1)S(1)}, u32[]{:S(2)}, u32[]{:S(2)}) %collective-permute-start.13) | collective-permute-done | bytes 131104 | tf_op jit(solution)/shard_map/ppermute | solution.py:25
  68.6 11.9 %all_gather.3 = bf16[128,2048]{1,0:T(8,128)(2,1)S(1)} all-gather(bf16[32,2048]{1,0:T(8,128)(2,1)S(1)} %add_convert_fusion.1), channel_id=1, replica_groups=mesh['x'=4,'zl'=2,'core'=2,'zh'=4,'y'=4] {'zh'}, dimensions={0}, use_global_device_ids=true | all-gather | bytes 655360 | tf_op jit(solution)/shard_map/all_gather | solution.py:86
  80.5 2.3 %collective-permute-start.14 = (bf16[128,2048]{1,0:T(8,128)(2,1)S(1)}, bf16[128,2048]{1,0:T(8,128)(2,1)S(1)}, u32[]{:S(2)}, u32[]{:S(2)}) collective-permute-start(bf16[128,2048]{1,0:T(8,128)(2,1)S(1)} %all_gather.3), channel_id=1, source_target_pairs={{0,3},{1,0},{2,1},{3,2},{4,7},{5,4},{6,5},{7,6},{8,11},{9,8},{10,9... | collective-permute-start | bytes 1572872 | tf_op jit(solution)/shard_map/ppermute | solution.py:25
  82.8 0.4 fusion.52
  83.3 8.7 %collective-permute-done.15 = bf16[128,2048]{1,0:T(8,128)(2,1)S(1)} collective-permute-done((bf16[128,2048]{1,0:T(8,128)(2,1)S(1)}, bf16[128,2048]{1,0:T(8,128)(2,1)S(1)}, u32[]{:S(2)}, u32[]{:S(2)}) %collective-permute-start.15) | collective-permute-done | bytes 524320 | tf_op jit(solution)/shard_map/ppermute | solution.py:25
  92.2 1.5 %collective-permute-start.18 = (bf16[64,2048]{1,0:T(8,128)(2,1)S(1)}, bf16[64,2048]{1,0:T(8,128)(2,1)S(1)}, u32[]{:S(2)}, u32[]{:S(2)}) collective-permute-start(bf16[64,2048]{1,0:T(8,128)(2,1)S(1)} %slice.122), channel_id=1, source_target_pairs={{0,1},{1,2},{2,3},{3,0},{4,5},{5,6},{6,7},{7,4},{8,9},{9,10},{10,1... | collective-permute-start | bytes 786440 | tf_op jit(solution)/shard_map/ppermute | solution.py:25
  93.6 0.4 fusion.51
  94.1 0.4 fusion.50
  94.6 11.1 %collective-permute-start.16 = (f32[192,512]{1,0:T(8,128)S(1)}, f32[192,512]{1,0:T(8,128)S(1)}, u32[]{:S(2)}, u32[]{:S(2)}) collective-permute-start(f32[192,512]{1,0:T(8,128)S(1)} %pad_maximum_fusion.5), channel_id=1, source_target_pairs={{0,16},{16,0},{1,17},{17,1},{2,18},{18,2},{3,19},{19,3},{4,20},{20... | collective-permute-start | bytes 1179656 | tf_op jit(solution)/shard_map/ppermute | solution.py:21
  105.8 0.5 fusion.49
  106.4 4.6 %collective-permute-start.19 = (f32[64,512]{1,0:T(8,128)S(1)}, f32[64,512]{1,0:T(8,128)S(1)}, u32[]{:S(2)}, u32[]{:S(2)}) collective-permute-start(f32[64,512]{1,0:T(8,128)S(1)} %fusion.49), channel_id=1, source_target_pairs={{0,16},{16,0},{1,17},{17,1},{2,18},{18,2},{3,19},{19,3},{4,20},{20... | collective-permute-start | bytes 393224 | tf_op jit(solution)/shard_map/ppermute | solution.py:21
  111.2 0.1 fusion.54
  111.4 0.7 collective-permute-done.19
  112.1 0.5 fusion.64
  112.6 1.4 %collective-permute-start.23 = (bf16[256,512]{1,0:T(8,128)(2,1)S(1)}, bf16[256,512]{1,0:T(8,128)(2,1)S(1)}, u32[]{:S(2)}, u32[]{:S(2)}) collective-permute-start(bf16[256,512]{1,0:T(8,128)(2,1)S(1)} %pad_maximum_fusion.6), channel_id=1, source_target_pairs={{0,32},{32,0},{1,33},{33,1},{2,34},{34,2},{3,35},{35,3},{4,36},{36... | collective-permute-start | bytes 786440 | tf_op jit(solution)/shard_map/ppermute | solution.py:21
  114.0 6.1 %collective-permute-start.21 = (bf16[256,512]{1,0:T(8,128)(2,1)S(1)}, bf16[256,512]{1,0:T(8,128)(2,1)S(1)}, u32[]{:S(2)}, u32[]{:S(2)}) collective-permute-start(bf16[256,512]{1,0:T(8,128)(2,1)S(1)} %pad_maximum_fusion.6), channel_id=1, source_target_pairs={{0,128},{64,192},{128,0},{192,64},{1,129},{65,193},{129,1},{193,65... | collective-permute-start | bytes 786440 | tf_op jit(solution)/shard_map/ppermute | solution.py:25
  120.4 1.5 %collective-permute-start.22 = (bf16[256,512]{1,0:T(8,128)(2,1)S(1)}, bf16[256,512]{1,0:T(8,128)(2,1)S(1)}, u32[]{:S(2)}, u32[]{:S(2)}) collective-permute-start(bf16[256,512]{1,0:T(8,128)(2,1)S(1)} %pad_maximum_fusion.6), channel_id=1, source_target_pairs={{0,64},{64,128},{128,192},{192,0},{1,65},{65,129},{129,193},{193,1... | collective-permute-start | bytes 786440 | tf_op jit(solution)/shard_map/ppermute | solution.py:25
  121.8 4.1 %collective-permute-start.24 = (bf16[256,512]{1,0:T(8,128)(2,1)S(1)}, bf16[256,512]{1,0:T(8,128)(2,1)S(1)}, u32[]{:S(2)}, u32[]{:S(2)}) collective-permute-start(bf16[256,512]{1,0:T(8,128)(2,1)S(1)} %collective-permute-done.23), channel_id=1, source_target_pairs={{0,192},{64,0},{128,64},{192,128},{1,193},{65,1},{129,65},{193,129... | collective-permute-start | bytes 786440 | tf_op jit(solution)/shard_map/ppermute | solution.py:25
  125.9 0.3 collective-permute-done.21
  126.2 0.9 collective-permute-start.25
  127.2 4.4 %collective-permute-done.20 = bf16[256,512]{1,0:T(8,128)(2,1)S(1)} collective-permute-done((bf16[256,512]{1,0:T(8,128)(2,1)S(1)}, bf16[256,512]{1,0:T(8,128)(2,1)S(1)}, u32[]{:S(2)}, u32[]{:S(2)}) %collective-permute-start.20) | collective-permute-done | bytes 262176 | tf_op jit(solution)/shard_map/ppermute | solution.py:25
  131.5 0.9 collective-permute-done.22
  132.5 4.7 %collective-permute-done.24 = bf16[256,512]{1,0:T(8,128)(2,1)S(1)} collective-permute-done((bf16[256,512]{1,0:T(8,128)(2,1)S(1)}, bf16[256,512]{1,0:T(8,128)(2,1)S(1)}, u32[]{:S(2)}, u32[]{:S(2)}) %collective-permute-start.24) | collective-permute-done | bytes 262176 | tf_op jit(solution)/shard_map/ppermute | solution.py:25
  137.2 0.9 collective-permute-done.26
  138.1 0.1 pad_maximum_fusion.3
  138.2 0.1 pad_maximum_fusion.4
  138.4 0.4 fusion.6
  138.8 0.5 convolution_add_fusion
  139.3 0.7 collective-permute-start.27
  140.0 0.4 fusion.11
  140.4 1.0 collective-permute-done.27
  141.5 1.3 add_multiply_fusion
  (50 shorter events, 1.1 us)
Async XLA Ops:
  0.0 23.1 %copy-start = (bf16[256,512]{1,0:T(8,128)(2,1)S(1)}, bf16[256,512]{1,0:T(8,128)(2,1)}, u32[]{:S(2)}) copy-start(bf16[256,512]{1,0:T(8,128)(2,1)} %param.1) | copy-start | bytes 786436
  0.0 10.6 %collective-permute-start.4 = (bf16[256,512]{1,0:T(8,128)(2,1)}, bf16[256,512]{1,0:T(8,128)(2,1)S(1)}, u32[]{:S(2)}, u32[]{:S(2)}) collective-permute-start(bf16[256,512]{1,0:T(8,128)(2,1)} %param.1), channel_id=1, source_target_pairs={{0,32},{32,0},{1,33},{33,1},{2,34},{34,2},{3,35},{35,3},{4,36},{36... | collective-permute-start | bytes 786440 | tf_op jit(solution)/shard_map/ppermute | solution.py:21
  2.5 10.3 %collective-permute-start.2 = (bf16[256,512]{1,0:T(8,128)(2,1)}, bf16[256,512]{1,0:T(8,128)(2,1)S(1)}, u32[]{:S(2)}, u32[]{:S(2)}) collective-permute-start(bf16[256,512]{1,0:T(8,128)(2,1)} %param.1), channel_id=1, source_target_pairs={{0,128},{64,192},{128,0},{192,64},{1,129},{65,193},{129,1},{193,65... | collective-permute-start | bytes 786440 | tf_op jit(solution)/shard_map/ppermute | solution.py:25
  5.2 12.0 %collective-permute-start.1 = (bf16[256,512]{1,0:T(8,128)(2,1)}, bf16[256,512]{1,0:T(8,128)(2,1)S(1)}, u32[]{:S(2)}, u32[]{:S(2)}) collective-permute-start(bf16[256,512]{1,0:T(8,128)(2,1)} %param.1), channel_id=1, source_target_pairs={{0,192},{64,0},{128,64},{192,128},{1,193},{65,1},{129,65},{193,129... | collective-permute-start | bytes 786440 | tf_op jit(solution)/shard_map/ppermute | solution.py:25
  6.1 11.4 %collective-permute-start.3 = (bf16[256,512]{1,0:T(8,128)(2,1)}, bf16[256,512]{1,0:T(8,128)(2,1)S(1)}, u32[]{:S(2)}, u32[]{:S(2)}) collective-permute-start(bf16[256,512]{1,0:T(8,128)(2,1)} %param.1), channel_id=1, source_target_pairs={{0,64},{64,128},{128,192},{192,0},{1,65},{65,129},{129,193},{193,1... | collective-permute-start | bytes 786440 | tf_op jit(solution)/shard_map/ppermute | solution.py:25
  6.7 6.1 %collective-permute-start = (bf16[256,512]{1,0:T(8,128)(2,1)}, bf16[256,512]{1,0:T(8,128)(2,1)S(1)}, u32[]{:S(2)}, u32[]{:S(2)}) collective-permute-start(bf16[256,512]{1,0:T(8,128)(2,1)} %param.1), channel_id=1, source_target_pairs={{0,16},{16,0},{1,17},{17,1},{2,18},{18,2},{3,19},{19,3},{4,20},{20... | collective-permute-start | bytes 786440 | tf_op jit(solution)/shard_map/ppermute | solution.py:21
  10.6 12.1 %collective-permute-start.5 = (bf16[256,512]{1,0:T(8,128)(2,1)S(1)}, bf16[256,512]{1,0:T(8,128)(2,1)S(1)}, u32[]{:S(2)}, u32[]{:S(2)}) collective-permute-start(bf16[256,512]{1,0:T(8,128)(2,1)S(1)} %collective-permute-done.4), channel_id=1, source_target_pairs={{0,192},{64,0},{128,64},{192,128},{1,193},{65,1},{129,65},{193,129... | collective-permute-start | bytes 786440 | tf_op jit(solution)/shard_map/ppermute | solution.py:25
  12.8 10.4 %collective-permute-start.7 = (bf16[256,512]{1,0:T(8,128)(2,1)S(1)}, bf16[256,512]{1,0:T(8,128)(2,1)S(1)}, u32[]{:S(2)}, u32[]{:S(2)}) collective-permute-start(bf16[256,512]{1,0:T(8,128)(2,1)S(1)} %collective-permute-done.4), channel_id=1, source_target_pairs={{0,64},{64,128},{128,192},{192,0},{1,65},{65,129},{129,193},{193,1... | collective-permute-start | bytes 786440 | tf_op jit(solution)/shard_map/ppermute | solution.py:25
  12.8 10.3 %collective-permute-start.6 = (bf16[256,512]{1,0:T(8,128)(2,1)S(1)}, bf16[256,512]{1,0:T(8,128)(2,1)S(1)}, u32[]{:S(2)}, u32[]{:S(2)}) collective-permute-start(bf16[256,512]{1,0:T(8,128)(2,1)S(1)} %collective-permute-done.2), channel_id=1, source_target_pairs={{0,32},{32,0},{1,33},{33,1},{2,34},{34,2},{3,35},{35,3},{4,36},{36... | collective-permute-start | bytes 786440 | tf_op jit(solution)/shard_map/ppermute | solution.py:21
  24.3 13.7 %collective-permute-start.8 = (bf16[128,2048]{1,0:T(8,128)(2,1)S(1)}, bf16[128,2048]{1,0:T(8,128)(2,1)S(1)}, u32[]{:S(2)}, u32[]{:S(2)}) collective-permute-start(bf16[128,2048]{1,0:T(8,128)(2,1)S(1)} %convolution_convert_fusion.2), channel_id=1, source_target_pairs={{0,1},{1,2},{2,3},{3,0},{4,5},{5,6},{6,7},{7,4},{8,9},{9,10},{10,1... | collective-permute-start | bytes 1572872 | tf_op jit(solution)/shard_map/ppermute | solution.py:25
  26.6 12.0 %collective-permute-start.9 = (bf16[128,2048]{1,0:T(8,128)(2,1)S(1)}, bf16[128,2048]{1,0:T(8,128)(2,1)S(1)}, u32[]{:S(2)}, u32[]{:S(2)}) collective-permute-start(bf16[128,2048]{1,0:T(8,128)(2,1)S(1)} %convolution_convert_fusion.1), channel_id=1, source_target_pairs={{0,3},{1,0},{2,1},{3,2},{4,7},{5,4},{6,5},{7,6},{8,11},{9,8},{10,9... | collective-permute-start | bytes 1572872 | tf_op jit(solution)/shard_map/ppermute | solution.py:25
  29.1 21.3 %collective-permute-start.10 = (bf16[128,2048]{1,0:T(8,128)(2,1)S(1)}, bf16[128,2048]{1,0:T(8,128)(2,1)S(1)}, u32[]{:S(2)}, u32[]{:S(2)}) collective-permute-start(bf16[128,2048]{1,0:T(8,128)(2,1)S(1)} %convolution_convert_fusion), channel_id=1, source_target_pairs={{0,2},{1,3},{2,0},{3,1},{4,6},{5,7},{6,4},{7,5},{8,10},{9,11},{10,... | collective-permute-start | bytes 1572872 | tf_op jit(solution)/shard_map/ppermute | solution.py:25
  51.3 9.6 %collective-permute-start.11 = (bf16[32,2048]{1,0:T(8,128)(2,1)}, bf16[32,2048]{1,0:T(8,128)(2,1)S(1)}, u32[]{:S(2)}, u32[]{:S(2)}) collective-permute-start(bf16[32,2048]{1,0:T(8,128)(2,1)} %get-tuple-element.59), channel_id=1, source_target_pairs={{0,4},{4,8},{8,12},{12,0},{1,5},{5,9},{9,13},{13,1},{2,6},{6,10},{... | collective-permute-start | bytes 393224 | tf_op jit(solution)/shard_map/ppermute | solution.py:25
  54.3 7.5 %collective-permute-start.12 = (bf16[32,2048]{1,0:T(8,128)(2,1)S(1)}, bf16[32,2048]{1,0:T(8,128)(2,1)S(1)}, u32[]{:S(2)}, u32[]{:S(2)}) collective-permute-start(bf16[32,2048]{1,0:T(8,128)(2,1)S(1)} %get-tuple-element.61), channel_id=1, source_target_pairs={{0,12},{4,0},{8,4},{12,8},{1,13},{5,1},{9,5},{13,9},{2,14},{6,2},{... | collective-permute-start | bytes 393224 | tf_op jit(solution)/shard_map/ppermute | solution.py:25
  56.5 12.1 %collective-permute-start.13 = (bf16[32,2048]{1,0:T(8,128)(2,1)S(1)}, bf16[32,2048]{1,0:T(8,128)(2,1)S(1)}, u32[]{:S(2)}, u32[]{:S(2)}) collective-permute-start(bf16[32,2048]{1,0:T(8,128)(2,1)S(1)} %get-tuple-element.60), channel_id=1, source_target_pairs={{0,8},{4,12},{8,0},{12,4},{1,9},{5,13},{9,1},{13,5},{2,10},{6,14},... | collective-permute-start | bytes 393224 | tf_op jit(solution)/shard_map/ppermute | solution.py:25
  80.5 11.5 %collective-permute-start.14 = (bf16[128,2048]{1,0:T(8,128)(2,1)S(1)}, bf16[128,2048]{1,0:T(8,128)(2,1)S(1)}, u32[]{:S(2)}, u32[]{:S(2)}) collective-permute-start(bf16[128,2048]{1,0:T(8,128)(2,1)S(1)} %all_gather.3), channel_id=1, source_target_pairs={{0,3},{1,0},{2,1},{3,2},{4,7},{5,4},{6,5},{7,6},{8,11},{9,8},{10,9... | collective-permute-start | bytes 1572872 | tf_op jit(solution)/shard_map/ppermute | solution.py:25
  82.8 9.2 %collective-permute-start.15 = (bf16[128,2048]{1,0:T(8,128)(2,1)S(1)}, bf16[128,2048]{1,0:T(8,128)(2,1)S(1)}, u32[]{:S(2)}, u32[]{:S(2)}) collective-permute-start(bf16[128,2048]{1,0:T(8,128)(2,1)S(1)} %all_gather.3), channel_id=1, source_target_pairs={{0,1},{1,2},{2,3},{3,0},{4,5},{5,6},{6,7},{7,4},{8,9},{9,10},{10,1... | collective-permute-start | bytes 1572872 | tf_op jit(solution)/shard_map/ppermute | solution.py:25
  92.1 13.6 %collective-permute-start.17 = (bf16[64,2048]{1,0:T(8,128)(2,1)S(1)}, bf16[64,2048]{1,0:T(8,128)(2,1)S(1)}, u32[]{:S(2)}, u32[]{:S(2)}) collective-permute-start(bf16[64,2048]{1,0:T(8,128)(2,1)S(1)} %get-tuple-element.33), channel_id=1, source_target_pairs={{0,3},{1,0},{2,1},{3,2},{4,7},{5,4},{6,5},{7,6},{8,11},{9,8},{10,9... | collective-permute-start | bytes 786440 | tf_op jit(solution)/shard_map/ppermute | solution.py:25
  92.2 13.6 %collective-permute-start.18 = (bf16[64,2048]{1,0:T(8,128)(2,1)S(1)}, bf16[64,2048]{1,0:T(8,128)(2,1)S(1)}, u32[]{:S(2)}, u32[]{:S(2)}) collective-permute-start(bf16[64,2048]{1,0:T(8,128)(2,1)S(1)} %slice.122), channel_id=1, source_target_pairs={{0,1},{1,2},{2,3},{3,0},{4,5},{5,6},{6,7},{7,4},{8,9},{9,10},{10,1... | collective-permute-start | bytes 786440 | tf_op jit(solution)/shard_map/ppermute | solution.py:25
  94.6 16.6 %collective-permute-start.16 = (f32[192,512]{1,0:T(8,128)S(1)}, f32[192,512]{1,0:T(8,128)S(1)}, u32[]{:S(2)}, u32[]{:S(2)}) collective-permute-start(f32[192,512]{1,0:T(8,128)S(1)} %pad_maximum_fusion.5), channel_id=1, source_target_pairs={{0,16},{16,0},{1,17},{17,1},{2,18},{18,2},{3,19},{19,3},{4,20},{20... | collective-permute-start | bytes 1179656 | tf_op jit(solution)/shard_map/ppermute | solution.py:21
  106.4 5.6 %collective-permute-start.19 = (f32[64,512]{1,0:T(8,128)S(1)}, f32[64,512]{1,0:T(8,128)S(1)}, u32[]{:S(2)}, u32[]{:S(2)}) collective-permute-start(f32[64,512]{1,0:T(8,128)S(1)} %fusion.49), channel_id=1, source_target_pairs={{0,16},{16,0},{1,17},{17,1},{2,18},{18,2},{3,19},{19,3},{4,20},{20... | collective-permute-start | bytes 393224 | tf_op jit(solution)/shard_map/ppermute | solution.py:21
  112.6 9.2 %collective-permute-start.23 = (bf16[256,512]{1,0:T(8,128)(2,1)S(1)}, bf16[256,512]{1,0:T(8,128)(2,1)S(1)}, u32[]{:S(2)}, u32[]{:S(2)}) collective-permute-start(bf16[256,512]{1,0:T(8,128)(2,1)S(1)} %pad_maximum_fusion.6), channel_id=1, source_target_pairs={{0,32},{32,0},{1,33},{33,1},{2,34},{34,2},{3,35},{35,3},{4,36},{36... | collective-permute-start | bytes 786440 | tf_op jit(solution)/shard_map/ppermute | solution.py:21
  114.0 12.2 %collective-permute-start.21 = (bf16[256,512]{1,0:T(8,128)(2,1)S(1)}, bf16[256,512]{1,0:T(8,128)(2,1)S(1)}, u32[]{:S(2)}, u32[]{:S(2)}) collective-permute-start(bf16[256,512]{1,0:T(8,128)(2,1)S(1)} %pad_maximum_fusion.6), channel_id=1, source_target_pairs={{0,128},{64,192},{128,0},{192,64},{1,129},{65,193},{129,1},{193,65... | collective-permute-start | bytes 786440 | tf_op jit(solution)/shard_map/ppermute | solution.py:25
  120.3 11.3 %collective-permute-start.20 = (bf16[256,512]{1,0:T(8,128)(2,1)S(1)}, bf16[256,512]{1,0:T(8,128)(2,1)S(1)}, u32[]{:S(2)}, u32[]{:S(2)}) collective-permute-start(bf16[256,512]{1,0:T(8,128)(2,1)S(1)} %pad_maximum_fusion.6), channel_id=1, source_target_pairs={{0,192},{64,0},{128,64},{192,128},{1,193},{65,1},{129,65},{193,129... | collective-permute-start | bytes 786440 | tf_op jit(solution)/shard_map/ppermute | solution.py:25
  120.4 12.1 %collective-permute-start.22 = (bf16[256,512]{1,0:T(8,128)(2,1)S(1)}, bf16[256,512]{1,0:T(8,128)(2,1)S(1)}, u32[]{:S(2)}, u32[]{:S(2)}) collective-permute-start(bf16[256,512]{1,0:T(8,128)(2,1)S(1)} %pad_maximum_fusion.6), channel_id=1, source_target_pairs={{0,64},{64,128},{128,192},{192,0},{1,65},{65,129},{129,193},{193,1... | collective-permute-start | bytes 786440 | tf_op jit(solution)/shard_map/ppermute | solution.py:25
  121.8 15.3 %collective-permute-start.24 = (bf16[256,512]{1,0:T(8,128)(2,1)S(1)}, bf16[256,512]{1,0:T(8,128)(2,1)S(1)}, u32[]{:S(2)}, u32[]{:S(2)}) collective-permute-start(bf16[256,512]{1,0:T(8,128)(2,1)S(1)} %collective-permute-done.23), channel_id=1, source_target_pairs={{0,192},{64,0},{128,64},{192,128},{1,193},{65,1},{129,65},{193,129... | collective-permute-start | bytes 786440 | tf_op jit(solution)/shard_map/ppermute | solution.py:25
  125.9 12.2 %collective-permute-start.26 = (bf16[256,512]{1,0:T(8,128)(2,1)S(1)}, bf16[256,512]{1,0:T(8,128)(2,1)S(1)}, u32[]{:S(2)}, u32[]{:S(2)}) collective-permute-start(bf16[256,512]{1,0:T(8,128)(2,1)S(1)} %collective-permute-done.23), channel_id=1, source_target_pairs={{0,64},{64,128},{128,192},{192,0},{1,65},{65,129},{129,193},{193,1... | collective-permute-start | bytes 786440 | tf_op jit(solution)/shard_map/ppermute | solution.py:25
  126.2 10.9 %collective-permute-start.25 = (bf16[256,512]{1,0:T(8,128)(2,1)S(1)}, bf16[256,512]{1,0:T(8,128)(2,1)S(1)}, u32[]{:S(2)}, u32[]{:S(2)}) collective-permute-start(bf16[256,512]{1,0:T(8,128)(2,1)S(1)} %collective-permute-done.21), channel_id=1, source_target_pairs={{0,32},{32,0},{1,33},{33,1},{2,34},{34,2},{3,35},{35,3},{4,36},{36... | collective-permute-start | bytes 786440 | tf_op jit(solution)/shard_map/ppermute | solution.py:21
  139.3 2.2 %collective-permute-start.27 = (f32[256,512]{1,0:T(8,128)S(1)}, f32[256,512]{1,0:T(8,128)S(1)}, u32[]{:S(2)}, u32[]{:S(2)}) collective-permute-start(f32[256,512]{1,0:T(8,128)S(1)} %convolution_add_fusion), channel_id=1, source_target_pairs={{0,16},{16,0},{1,17},{17,1},{2,18},{18,2},{3,19},{19,3},{4,20},{20... | collective-permute-start | bytes 1572872 | tf_op jit(solution)/shard_map/ppermute | solution.py:21

commit v11 on v10

--- a/solution.py
+++ b/solution.py
@@ -38,10 +38,6 @@
     return [send(pieces[k], axis, k) for k in (0, 1, 3, 2)]
 
 
-def around(array, axis):
-    return [array] + [fetch(array, axis, k) for k in (1, 2, 3)]
-
-
 def chunks(array):
     return jnp.split(array, 4, axis=0)
 
@@ -57,11 +53,14 @@
 
 
 def panels_of(block):
+    far = fetch(block, "x", 2)
     partner = swap(block, "zl")
-    mine = around(block, "x")
-    theirs = [partner, fetch(partner, "x", 1), swap(mine[2], "zl"), fetch(partner, "x", 3)]
-    blocks = lax.optimization_barrier([*mine, *theirs])
-    panels = [jnp.concatenate([b.reshape(4, 1, 64, 512) for b in four], axis=1) for four in (blocks[:4], blocks[4:])]
+    pair = jnp.concatenate([block, partner], axis=0)
+    after, before = fetch(pair, "x", 1), fetch(pair, "x", 3)
+    blocks = lax.optimization_barrier([pair, after, before, far, swap(far, "zl")])
+    mine = [blocks[0][:256], blocks[1][:256], blocks[3], blocks[2][:256]]
+    theirs = [blocks[0][256:], blocks[1][256:], blocks[4], blocks[2][256:]]
+    panels = [jnp.concatenate([b.reshape(4, 1, 64, 512) for b in four], axis=1) for four in (mine, theirs)]
     return [panel.reshape(1024, 512) for panel in panels]
 
 

time: 143 us -> 142 us (level)
  starting transfers between devices: 59.2 us -> 52.2 us
  blocking collectives: 11.9 us -> 16.3 us
  waiting for transfers between devices: 57.8 us -> 60.2 us
    ppermute x8, waiting for transfers between devices: 1.73 us -> 15.4 us  [swap(): return lax.ppermute(array, axis, [(0, 1), (1, 0)])]
    ppermute x20 -> x16, waiting for transfers between devices: 56.1 us -> 44.8 us  [send(): lax.ppermute(array, axis, [(i, (i + k) % 4) for i in range(4)])]
    ppermute x20 -> x16, starting transfers between devices: 36.1 us -> 26.4 us  [send(): lax.ppermute(array, axis, [(i, (i + k) % 4) for i in range(4)])]
    all_gather x1, blocking collectives: 11.9 us -> 16.3 us  [per_device(): near = lax.all_gather(part, 'zh', axis=0, tiled=True)]
    ppermute x8, starting transfers between devices: 23.1 us -> 25.7 us  [swap(): return lax.ppermute(array, axis, [(0, 1), (1, 0)])]
  transfers between devices with their start and end apart: 28 -> 24, of which waited for: 17 -> 15; matrix products, arithmetic and copies ran while one was open for 6% -> 6% of each run, Pallas kernels for 0% -> 0%
where the time goes in v11:
time: 142 us
  waiting for transfers between devices  60.2 us (42%)
  starting transfers between devices  52.2 us (37%)
  blocking collectives  16.3 us (11%)
  matrix products  8.59 us (6%)
  other arithmetic  2.57 us (2%)
  local copies, waits for them, and re-layouts  2.04 us (1%)
    ppermute x16, waiting for transfers between devices, send(): lax.ppermute(array, axis, [(i, (i + k) % 4) for i in range(4)])  44.8 us
    ppermute x16, starting transfers between devices, send(): lax.ppermute(array, axis, [(i, (i + k) % 4) for i in range(4)])  26.4 us
    ppermute x8, starting transfers between devices, swap(): return lax.ppermute(array, axis, [(0, 1), (1, 0)])  25.7 us
    all_gather x1, blocking collectives, per_device(): near = lax.all_gather(part, 'zh', axis=0, tiled=True)  16.3 us
    ppermute x8, waiting for transfers between devices, swap(): return lax.ppermute(array, axis, [(0, 1), (1, 0)])  15.4 us
    dot_general x13, matrix products, matmul(): return lax.dot_general(a, b, (dims, ((), ())), preferred_element_type=F32)  8.59 us
  transfers between devices with their start and end apart: 24, of which 15 were waited for; matrix products, arithmetic and copies ran while one was open for 6% of the time, Pallas kernels for 0%

profile of v11, /device:TPU:1, one launch (start us, length us, event | category | flops | bytes accessed | tf_op | source)
XLA Modules:
  0.0 142.4 jit_solution(18391212973773078981)
XLA Ops:
  0.0 2.5 %collective-permute-start.1 = (bf16[256,512]{1,0:T(8,128)(2,1)}, bf16[256,512]{1,0:T(8,128)(2,1)S(1)}, u32[]{:S(2)}, u32[]{:S(2)}) collective-permute-start(bf16[256,512]{1,0:T(8,128)(2,1)} %param.1), channel_id=1, source_target_pairs={{0,32},{32,0},{1,33},{33,1},{2,34},{34,2},{3,35},{35,3},{4,36},{36... | collective-permute-start | bytes 786440 | tf_op jit(solution)/shard_map/ppermute | solution.py:21
  2.5 2.7 %collective-permute-start.4 = (bf16[256,512]{1,0:T(8,128)(2,1)}, bf16[256,512]{1,0:T(8,128)(2,1)S(1)}, u32[]{:S(2)}, u32[]{:S(2)}) collective-permute-start(bf16[256,512]{1,0:T(8,128)(2,1)} %param.1), channel_id=1, source_target_pairs={{0,128},{64,192},{128,0},{192,64},{1,129},{65,193},{129,1},{193,65... | collective-permute-start | bytes 786440 | tf_op jit(solution)/shard_map/ppermute | solution.py:25
  5.2 1.2 collective-permute-start
  6.4 0.9 split.84
  7.4 1.2 constant_dynamic-update-slice_fusion.1
  8.7 2.5 %collective-permute-start.2 = (bf16[512,512]{1,0:T(8,128)(2,1)S(1)}, bf16[512,512]{1,0:T(8,128)(2,1)S(1)}, u32[]{:S(2)}, u32[]{:S(2)}) collective-permute-start(bf16[512,512]{1,0:T(8,128)(2,1)S(1)} %constant_dynamic-update-slice_fusion), channel_id=1, source_target_pairs={{0,192},{64,0},{128,64},{192,128},{1,193},{65,1},{129,65},{193,129... | collective-permute-start | bytes 1572872 | tf_op jit(solution)/shard_map/ppermute | solution.py:25
  11.2 1.3 collective-permute-start.5
  12.5 0.3 fusion.13
  12.8 4.4 %collective-permute-done.5 = bf16[256,512]{1,0:T(8,128)(2,1)S(1)} collective-permute-done((bf16[256,512]{1,0:T(8,128)(2,1)S(1)}, bf16[256,512]{1,0:T(8,128)(2,1)S(1)}, u32[]{:S(2)}, u32[]{:S(2)}) %collective-permute-start.5) | collective-permute-done | bytes 262176 | tf_op jit(solution)/shard_map/ppermute | solution.py:21
  17.2 5.5 %collective-permute-done.2 = bf16[512,512]{1,0:T(8,128)(2,1)S(1)} collective-permute-done((bf16[512,512]{1,0:T(8,128)(2,1)S(1)}, bf16[512,512]{1,0:T(8,128)(2,1)S(1)}, u32[]{:S(2)}, u32[]{:S(2)}) %collective-permute-start.2) | collective-permute-done | bytes 524320 | tf_op jit(solution)/shard_map/ppermute | solution.py:25
  22.8 1.4 collective-permute-done.3
  24.2 0.1 fusion.61
  24.3 0.1 pad_maximum_fusion.1
  24.4 0.1 pad_maximum_fusion.2
  24.6 0.9 convolution_convert_fusion.2
  25.5 1.4 collective-permute-start.6
  26.8 0.9 convolution_convert_fusion.1
  27.8 1.5 %collective-permute-start.7 = (bf16[128,2048]{1,0:T(8,128)(2,1)S(1)}, bf16[128,2048]{1,0:T(8,128)(2,1)S(1)}, u32[]{:S(2)}, u32[]{:S(2)}) collective-permute-start(bf16[128,2048]{1,0:T(8,128)(2,1)S(1)} %convolution_convert_fusion.1), channel_id=1, source_target_pairs={{0,3},{1,0},{2,1},{3,2},{4,7},{5,4},{6,5},{7,6},{8,11},{9,8},{10,9... | collective-permute-start | bytes 1572872 | tf_op jit(solution)/shard_map/ppermute | solution.py:25
  29.3 0.9 convolution_convert_fusion
  30.2 1.7 %collective-permute-start.8 = (bf16[128,2048]{1,0:T(8,128)(2,1)S(1)}, bf16[128,2048]{1,0:T(8,128)(2,1)S(1)}, u32[]{:S(2)}, u32[]{:S(2)}) collective-permute-start(bf16[128,2048]{1,0:T(8,128)(2,1)S(1)} %convolution_convert_fusion), channel_id=1, source_target_pairs={{0,2},{1,3},{2,0},{3,1},{4,6},{5,7},{6,4},{7,5},{8,10},{9,11},{10,... | collective-permute-start | bytes 1572872 | tf_op jit(solution)/shard_map/ppermute | solution.py:25
  31.9 0.9 fusion
  32.8 4.9 %collective-permute-done.6 = bf16[128,2048]{1,0:T(8,128)(2,1)S(1)} collective-permute-done((bf16[128,2048]{1,0:T(8,128)(2,1)S(1)}, bf16[128,2048]{1,0:T(8,128)(2,1)S(1)}, u32[]{:S(2)}, u32[]{:S(2)}) %collective-permute-start.6) | collective-permute-done | bytes 524320 | tf_op jit(solution)/shard_map/ppermute | solution.py:25
  37.7 0.7 collective-permute-done.7
  38.4 11.7 %collective-permute-done.8 = bf16[128,2048]{1,0:T(8,128)(2,1)S(1)} collective-permute-done((bf16[128,2048]{1,0:T(8,128)(2,1)S(1)}, bf16[128,2048]{1,0:T(8,128)(2,1)S(1)}, u32[]{:S(2)}, u32[]{:S(2)}) %collective-permute-start.8) | collective-permute-done | bytes 524320 | tf_op jit(solution)/shard_map/ppermute | solution.py:25
  50.1 0.3 add_convert_fusion
  50.4 5.4 %collective-permute-start.10 = (bf16[32,2048]{1,0:T(8,128)(2,1)S(1)}, bf16[32,2048]{1,0:T(8,128)(2,1)S(1)}, u32[]{:S(2)}, u32[]{:S(2)}) collective-permute-start(bf16[32,2048]{1,0:T(8,128)(2,1)S(1)} %get-tuple-element.55), channel_id=1, source_target_pairs={{0,12},{4,0},{8,4},{12,8},{1,13},{5,1},{9,5},{13,9},{2,14},{6,2},{... | collective-permute-start | bytes 393224 | tf_op jit(solution)/shard_map/ppermute | solution.py:25
  55.8 1.0 collective-permute-start.11
  56.8 2.2 %collective-permute-start.9 = (bf16[32,2048]{1,0:T(8,128)(2,1)S(1)}, bf16[32,2048]{1,0:T(8,128)(2,1)S(1)}, u32[]{:S(2)}, u32[]{:S(2)}) collective-permute-start(bf16[32,2048]{1,0:T(8,128)(2,1)S(1)} %get-tuple-element.53), channel_id=1, source_target_pairs={{0,4},{4,8},{8,12},{12,0},{1,5},{5,9},{9,13},{13,1},{2,6},{6,10},{... | collective-permute-start | bytes 393224 | tf_op jit(solution)/shard_map/ppermute | solution.py:25
  59.1 5.9 %collective-permute-done.11 = bf16[32,2048]{1,0:T(8,128)(2,1)S(1)} collective-permute-done((bf16[32,2048]{1,0:T(8,128)(2,1)S(1)}, bf16[32,2048]{1,0:T(8,128)(2,1)S(1)}, u32[]{:S(2)}, u32[]{:S(2)}) %collective-permute-start.11) | collective-permute-done | bytes 131104 | tf_op jit(solution)/shard_map/ppermute | solution.py:25
  64.9 0.8 collective-permute-done.9
  65.7 0.1 add_convert_fusion.1
  65.8 16.3 %all_gather.3 = bf16[128,2048]{1,0:T(8,128)(2,1)S(1)} all-gather(bf16[32,2048]{1,0:T(8,128)(2,1)S(1)} %add_convert_fusion.1), channel_id=1, replica_groups=mesh['x'=4,'zl'=2,'core'=2,'zh'=4,'y'=4] {'zh'}, dimensions={0}, use_global_device_ids=true | all-gather | bytes 655360 | tf_op jit(solution)/shard_map/all_gather | solution.py:85
  82.1 1.5 %collective-permute-start.13 = (bf16[128,2048]{1,0:T(8,128)(2,1)S(1)}, bf16[128,2048]{1,0:T(8,128)(2,1)S(1)}, u32[]{:S(2)}, u32[]{:S(2)}) collective-permute-start(bf16[128,2048]{1,0:T(8,128)(2,1)S(1)} %all_gather.3), channel_id=1, source_target_pairs={{0,1},{1,2},{2,3},{3,0},{4,5},{5,6},{6,7},{7,4},{8,9},{9,10},{10,1... | collective-permute-start | bytes 1572872 | tf_op jit(solution)/shard_map/ppermute | solution.py:25
  83.5 0.4 fusion.52
  84.0 7.3 %collective-permute-done.13 = bf16[128,2048]{1,0:T(8,128)(2,1)S(1)} collective-permute-done((bf16[128,2048]{1,0:T(8,128)(2,1)S(1)}, bf16[128,2048]{1,0:T(8,128)(2,1)S(1)}, u32[]{:S(2)}, u32[]{:S(2)}) %collective-permute-start.13) | collective-permute-done | bytes 524320 | tf_op jit(solution)/shard_map/ppermute | solution.py:25
  91.4 0.5 collective-permute-start.15
  91.9 1.0 collective-permute-start.16
  92.9 0.4 fusion.51
  93.4 0.4 fusion.50
  93.9 11.9 %collective-permute-start.14 = (f32[192,512]{1,0:T(8,128)S(1)}, f32[192,512]{1,0:T(8,128)S(1)}, u32[]{:S(2)}, u32[]{:S(2)}) collective-permute-start(f32[192,512]{1,0:T(8,128)S(1)} %pad_maximum_fusion.6), channel_id=1, source_target_pairs={{0,16},{16,0},{1,17},{17,1},{2,18},{18,2},{3,19},{19,3},{4,20},{20... | collective-permute-start | bytes 1179656 | tf_op jit(solution)/shard_map/ppermute | solution.py:21
  106.0 0.5 fusion.49
  106.5 4.9 %collective-permute-start.17 = (f32[64,512]{1,0:T(8,128)S(1)}, f32[64,512]{1,0:T(8,128)S(1)}, u32[]{:S(2)}, u32[]{:S(2)}) collective-permute-start(f32[64,512]{1,0:T(8,128)S(1)} %fusion.49), channel_id=1, source_target_pairs={{0,16},{16,0},{1,17},{17,1},{2,18},{18,2},{3,19},{19,3},{4,20},{20... | collective-permute-start | bytes 393224 | tf_op jit(solution)/shard_map/ppermute | solution.py:21
  111.6 0.7 collective-permute-done.17
  112.3 0.5 fusion.70
  112.9 0.6 collective-permute-start.18
  113.5 0.1 fusion.54
  113.6 3.0 %collective-permute-start.21 = (bf16[256,512]{1,0:T(8,128)(2,1)S(1)}, bf16[256,512]{1,0:T(8,128)(2,1)S(1)}, u32[]{:S(2)}, u32[]{:S(2)}) collective-permute-start(bf16[256,512]{1,0:T(8,128)(2,1)S(1)} %pad_maximum_fusion.7), channel_id=1, source_target_pairs={{0,128},{64,192},{128,0},{192,64},{1,129},{65,193},{129,1},{193,65... | collective-permute-start | bytes 786440 | tf_op jit(solution)/shard_map/ppermute | solution.py:25
  116.6 3.9 %collective-permute-done.18 = bf16[256,512]{1,0:T(8,128)(2,1)S(1)} collective-permute-done((bf16[256,512]{1,0:T(8,128)(2,1)S(1)}, bf16[256,512]{1,0:T(8,128)(2,1)S(1)}, u32[]{:S(2)}, u32[]{:S(2)}) %collective-permute-start.18) | collective-permute-done | bytes 262176 | tf_op jit(solution)/shard_map/ppermute | solution.py:21
  120.5 2.0 %collective-permute-start.19 = (bf16[512,512]{1,0:T(8,128)(2,1)S(1)}, bf16[512,512]{1,0:T(8,128)(2,1)S(1)}, u32[]{:S(2)}, u32[]{:S(2)}) collective-permute-start(bf16[512,512]{1,0:T(8,128)(2,1)S(1)} %pad_maximum_fusion.5), channel_id=1, source_target_pairs={{0,192},{64,0},{128,64},{192,128},{1,193},{65,1},{129,65},{193,129... | collective-permute-start | bytes 1572872 | tf_op jit(solution)/shard_map/ppermute | solution.py:25
  122.5 0.1 fusion.53
  122.6 0.1 fusion.56
  122.7 1.2 collective-permute-start.22
  123.9 0.1 fusion.55
  124.0 5.3 %collective-permute-done.22 = bf16[256,512]{1,0:T(8,128)(2,1)S(1)} collective-permute-done((bf16[256,512]{1,0:T(8,128)(2,1)S(1)}, bf16[256,512]{1,0:T(8,128)(2,1)S(1)}, u32[]{:S(2)}, u32[]{:S(2)}) %collective-permute-start.22) | collective-permute-done | bytes 262176 | tf_op jit(solution)/shard_map/ppermute | solution.py:21
  129.3 4.2 %collective-permute-done.19 = bf16[512,512]{1,0:T(8,128)(2,1)S(1)} collective-permute-done((bf16[512,512]{1,0:T(8,128)(2,1)S(1)}, bf16[512,512]{1,0:T(8,128)(2,1)S(1)}, u32[]{:S(2)}, u32[]{:S(2)}) %collective-permute-start.19) | collective-permute-done | bytes 524320 | tf_op jit(solution)/shard_map/ppermute | solution.py:25
  133.5 2.5 %collective-permute-done.20 = bf16[512,512]{1,0:T(8,128)(2,1)S(1)} collective-permute-done((bf16[512,512]{1,0:T(8,128)(2,1)S(1)}, bf16[512,512]{1,0:T(8,128)(2,1)S(1)}, u32[]{:S(2)}, u32[]{:S(2)}) %collective-permute-start.20) | collective-permute-done | bytes 524320 | tf_op jit(solution)/shard_map/ppermute | solution.py:25
  136.1 0.1 pad_maximum_fusion.3
  136.3 0.1 pad_maximum_fusion.4
  136.4 0.5 fusion.6
  136.9 0.4 convolution_add_fusion
  137.3 2.2 %collective-permute-start.23 = (f32[256,512]{1,0:T(8,128)S(1)}, f32[256,512]{1,0:T(8,128)S(1)}, u32[]{:S(2)}, u32[]{:S(2)}) collective-permute-start(f32[256,512]{1,0:T(8,128)S(1)} %convolution_add_fusion), channel_id=1, source_target_pairs={{0,16},{16,0},{1,17},{17,1},{2,18},{18,2},{3,19},{19,3},{4,20},{20... | collective-permute-start | bytes 1572872 | tf_op jit(solution)/shard_map/ppermute | solution.py:21
  139.5 0.4 fusion.11
  140.0 1.0 collective-permute-done.23
  141.0 1.3 add_multiply_fusion
  (50 shorter events, 0.9 us)
Async XLA Ops:
  0.0 8.7 %collective-permute-start.1 = (bf16[256,512]{1,0:T(8,128)(2,1)}, bf16[256,512]{1,0:T(8,128)(2,1)S(1)}, u32[]{:S(2)}, u32[]{:S(2)}) collective-permute-start(bf16[256,512]{1,0:T(8,128)(2,1)} %param.1), channel_id=1, source_target_pairs={{0,32},{32,0},{1,33},{33,1},{2,34},{34,2},{3,35},{35,3},{4,36},{36... | collective-permute-start | bytes 786440 | tf_op jit(solution)/shard_map/ppermute | solution.py:21
  2.5 8.7 %collective-permute-start.4 = (bf16[256,512]{1,0:T(8,128)(2,1)}, bf16[256,512]{1,0:T(8,128)(2,1)S(1)}, u32[]{:S(2)}, u32[]{:S(2)}) collective-permute-start(bf16[256,512]{1,0:T(8,128)(2,1)} %param.1), channel_id=1, source_target_pairs={{0,128},{64,192},{128,0},{192,64},{1,129},{65,193},{129,1},{193,65... | collective-permute-start | bytes 786440 | tf_op jit(solution)/shard_map/ppermute | solution.py:25
  5.2 7.2 %collective-permute-start = (bf16[256,512]{1,0:T(8,128)(2,1)}, bf16[256,512]{1,0:T(8,128)(2,1)S(1)}, u32[]{:S(2)}, u32[]{:S(2)}) collective-permute-start(bf16[256,512]{1,0:T(8,128)(2,1)} %param.1), channel_id=1, source_target_pairs={{0,16},{16,0},{1,17},{17,1},{2,18},{18,2},{3,19},{19,3},{4,20},{20... | collective-permute-start | bytes 786440 | tf_op jit(solution)/shard_map/ppermute | solution.py:21
  8.7 14.1 %collective-permute-start.2 = (bf16[512,512]{1,0:T(8,128)(2,1)S(1)}, bf16[512,512]{1,0:T(8,128)(2,1)S(1)}, u32[]{:S(2)}, u32[]{:S(2)}) collective-permute-start(bf16[512,512]{1,0:T(8,128)(2,1)S(1)} %constant_dynamic-update-slice_fusion), channel_id=1, source_target_pairs={{0,192},{64,0},{128,64},{192,128},{1,193},{65,1},{129,65},{193,129... | collective-permute-start | bytes 1572872 | tf_op jit(solution)/shard_map/ppermute | solution.py:25
  11.2 13.0 %collective-permute-start.3 = (bf16[512,512]{1,0:T(8,128)(2,1)S(1)}, bf16[512,512]{1,0:T(8,128)(2,1)S(1)}, u32[]{:S(2)}, u32[]{:S(2)}) collective-permute-start(bf16[512,512]{1,0:T(8,128)(2,1)S(1)} %constant_dynamic-update-slice_fusion), channel_id=1, source_target_pairs={{0,64},{64,128},{128,192},{192,0},{1,65},{65,129},{129,193},{193,1... | collective-permute-start | bytes 1572872 | tf_op jit(solution)/shard_map/ppermute | solution.py:25
  11.2 6.1 %collective-permute-start.5 = (bf16[256,512]{1,0:T(8,128)(2,1)S(1)}, bf16[256,512]{1,0:T(8,128)(2,1)S(1)}, u32[]{:S(2)}, u32[]{:S(2)}) collective-permute-start(bf16[256,512]{1,0:T(8,128)(2,1)S(1)} %collective-permute-done.4), channel_id=1, source_target_pairs={{0,32},{32,0},{1,33},{33,1},{2,34},{34,2},{3,35},{35,3},{4,36},{36... | collective-permute-start | bytes 786440 | tf_op jit(solution)/shard_map/ppermute | solution.py:21
  25.5 12.3 %collective-permute-start.6 = (bf16[128,2048]{1,0:T(8,128)(2,1)S(1)}, bf16[128,2048]{1,0:T(8,128)(2,1)S(1)}, u32[]{:S(2)}, u32[]{:S(2)}) collective-permute-start(bf16[128,2048]{1,0:T(8,128)(2,1)S(1)} %convolution_convert_fusion.2), channel_id=1, source_target_pairs={{0,1},{1,2},{2,3},{3,0},{4,5},{5,6},{6,7},{7,4},{8,9},{9,10},{10,1... | collective-permute-start | bytes 1572872 | tf_op jit(solution)/shard_map/ppermute | solution.py:25
  27.8 10.7 %collective-permute-start.7 = (bf16[128,2048]{1,0:T(8,128)(2,1)S(1)}, bf16[128,2048]{1,0:T(8,128)(2,1)S(1)}, u32[]{:S(2)}, u32[]{:S(2)}) collective-permute-start(bf16[128,2048]{1,0:T(8,128)(2,1)S(1)} %convolution_convert_fusion.1), channel_id=1, source_target_pairs={{0,3},{1,0},{2,1},{3,2},{4,7},{5,4},{6,5},{7,6},{8,11},{9,8},{10,9... | collective-permute-start | bytes 1572872 | tf_op jit(solution)/shard_map/ppermute | solution.py:25
  30.2 19.9 %collective-permute-start.8 = (bf16[128,2048]{1,0:T(8,128)(2,1)S(1)}, bf16[128,2048]{1,0:T(8,128)(2,1)S(1)}, u32[]{:S(2)}, u32[]{:S(2)}) collective-permute-start(bf16[128,2048]{1,0:T(8,128)(2,1)S(1)} %convolution_convert_fusion), channel_id=1, source_target_pairs={{0,2},{1,3},{2,0},{3,1},{4,6},{5,7},{6,4},{7,5},{8,10},{9,11},{10,... | collective-permute-start | bytes 1572872 | tf_op jit(solution)/shard_map/ppermute | solution.py:25
  50.4 8.6 %collective-permute-start.10 = (bf16[32,2048]{1,0:T(8,128)(2,1)S(1)}, bf16[32,2048]{1,0:T(8,128)(2,1)S(1)}, u32[]{:S(2)}, u32[]{:S(2)}) collective-permute-start(bf16[32,2048]{1,0:T(8,128)(2,1)S(1)} %get-tuple-element.55), channel_id=1, source_target_pairs={{0,12},{4,0},{8,4},{12,8},{1,13},{5,1},{9,5},{13,9},{2,14},{6,2},{... | collective-permute-start | bytes 393224 | tf_op jit(solution)/shard_map/ppermute | solution.py:25
  55.8 9.1 %collective-permute-start.11 = (bf16[32,2048]{1,0:T(8,128)(2,1)S(1)}, bf16[32,2048]{1,0:T(8,128)(2,1)S(1)}, u32[]{:S(2)}, u32[]{:S(2)}) collective-permute-start(bf16[32,2048]{1,0:T(8,128)(2,1)S(1)} %get-tuple-element.54), channel_id=1, source_target_pairs={{0,8},{4,12},{8,0},{12,4},{1,9},{5,13},{9,1},{13,5},{2,10},{6,14},... | collective-permute-start | bytes 393224 | tf_op jit(solution)/shard_map/ppermute | solution.py:25
  56.8 8.9 %collective-permute-start.9 = (bf16[32,2048]{1,0:T(8,128)(2,1)S(1)}, bf16[32,2048]{1,0:T(8,128)(2,1)S(1)}, u32[]{:S(2)}, u32[]{:S(2)}) collective-permute-start(bf16[32,2048]{1,0:T(8,128)(2,1)S(1)} %get-tuple-element.53), channel_id=1, source_target_pairs={{0,4},{4,8},{8,12},{12,0},{1,5},{5,9},{9,13},{13,1},{2,6},{6,10},{... | collective-permute-start | bytes 393224 | tf_op jit(solution)/shard_map/ppermute | solution.py:25
  82.1 9.3 %collective-permute-start.12 = (bf16[128,2048]{1,0:T(8,128)(2,1)S(1)}, bf16[128,2048]{1,0:T(8,128)(2,1)S(1)}, u32[]{:S(2)}, u32[]{:S(2)}) collective-permute-start(bf16[128,2048]{1,0:T(8,128)(2,1)S(1)} %all_gather.3), channel_id=1, source_target_pairs={{0,3},{1,0},{2,1},{3,2},{4,7},{5,4},{6,5},{7,6},{8,11},{9,8},{10,9... | collective-permute-start | bytes 1572872 | tf_op jit(solution)/shard_map/ppermute | solution.py:25
  82.1 9.2 %collective-permute-start.13 = (bf16[128,2048]{1,0:T(8,128)(2,1)S(1)}, bf16[128,2048]{1,0:T(8,128)(2,1)S(1)}, u32[]{:S(2)}, u32[]{:S(2)}) collective-permute-start(bf16[128,2048]{1,0:T(8,128)(2,1)S(1)} %all_gather.3), channel_id=1, source_target_pairs={{0,1},{1,2},{2,3},{3,0},{4,5},{5,6},{6,7},{7,4},{8,9},{9,10},{10,1... | collective-permute-start | bytes 1572872 | tf_op jit(solution)/shard_map/ppermute | solution.py:25
  91.4 14.4 %collective-permute-start.15 = (bf16[64,2048]{1,0:T(8,128)(2,1)S(1)}, bf16[64,2048]{1,0:T(8,128)(2,1)S(1)}, u32[]{:S(2)}, u32[]{:S(2)}) collective-permute-start(bf16[64,2048]{1,0:T(8,128)(2,1)S(1)} %get-tuple-element.24), channel_id=1, source_target_pairs={{0,3},{1,0},{2,1},{3,2},{4,7},{5,4},{6,5},{7,6},{8,11},{9,8},{10,9... | collective-permute-start | bytes 786440 | tf_op jit(solution)/shard_map/ppermute | solution.py:25
  91.9 13.9 %collective-permute-start.16 = (bf16[64,2048]{1,0:T(8,128)(2,1)S(1)}, bf16[64,2048]{1,0:T(8,128)(2,1)S(1)}, u32[]{:S(2)}, u32[]{:S(2)}) collective-permute-start(bf16[64,2048]{1,0:T(8,128)(2,1)S(1)} %slice.170), channel_id=1, source_target_pairs={{0,1},{1,2},{2,3},{3,0},{4,5},{5,6},{6,7},{7,4},{8,9},{9,10},{10,1... | collective-permute-start | bytes 786440 | tf_op jit(solution)/shard_map/ppermute | solution.py:25
  93.9 17.5 %collective-permute-start.14 = (f32[192,512]{1,0:T(8,128)S(1)}, f32[192,512]{1,0:T(8,128)S(1)}, u32[]{:S(2)}, u32[]{:S(2)}) collective-permute-start(f32[192,512]{1,0:T(8,128)S(1)} %pad_maximum_fusion.6), channel_id=1, source_target_pairs={{0,16},{16,0},{1,17},{17,1},{2,18},{18,2},{3,19},{19,3},{4,20},{20... | collective-permute-start | bytes 1179656 | tf_op jit(solution)/shard_map/ppermute | solution.py:21
  106.5 5.9 %collective-permute-start.17 = (f32[64,512]{1,0:T(8,128)S(1)}, f32[64,512]{1,0:T(8,128)S(1)}, u32[]{:S(2)}, u32[]{:S(2)}) collective-permute-start(f32[64,512]{1,0:T(8,128)S(1)} %fusion.49), channel_id=1, source_target_pairs={{0,16},{16,0},{1,17},{17,1},{2,18},{18,2},{3,19},{19,3},{4,20},{20... | collective-permute-start | bytes 393224 | tf_op jit(solution)/shard_map/ppermute | solution.py:21
  112.9 7.6 %collective-permute-start.18 = (bf16[256,512]{1,0:T(8,128)(2,1)S(1)}, bf16[256,512]{1,0:T(8,128)(2,1)S(1)}, u32[]{:S(2)}, u32[]{:S(2)}) collective-permute-start(bf16[256,512]{1,0:T(8,128)(2,1)S(1)} %pad_maximum_fusion.7), channel_id=1, source_target_pairs={{0,32},{32,0},{1,33},{33,1},{2,34},{34,2},{3,35},{35,3},{4,36},{36... | collective-permute-start | bytes 786440 | tf_op jit(solution)/shard_map/ppermute | solution.py:21
  113.6 9.1 %collective-permute-start.21 = (bf16[256,512]{1,0:T(8,128)(2,1)S(1)}, bf16[256,512]{1,0:T(8,128)(2,1)S(1)}, u32[]{:S(2)}, u32[]{:S(2)}) collective-permute-start(bf16[256,512]{1,0:T(8,128)(2,1)S(1)} %pad_maximum_fusion.7), channel_id=1, source_target_pairs={{0,128},{64,192},{128,0},{192,64},{1,129},{65,193},{129,1},{193,65... | collective-permute-start | bytes 786440 | tf_op jit(solution)/shard_map/ppermute | solution.py:25
  120.5 13.0 %collective-permute-start.19 = (bf16[512,512]{1,0:T(8,128)(2,1)S(1)}, bf16[512,512]{1,0:T(8,128)(2,1)S(1)}, u32[]{:S(2)}, u32[]{:S(2)}) collective-permute-start(bf16[512,512]{1,0:T(8,128)(2,1)S(1)} %pad_maximum_fusion.5), channel_id=1, source_target_pairs={{0,192},{64,0},{128,64},{192,128},{1,193},{65,1},{129,65},{193,129... | collective-permute-start | bytes 1572872 | tf_op jit(solution)/shard_map/ppermute | solution.py:25
  122.5 13.5 %collective-permute-start.20 = (bf16[512,512]{1,0:T(8,128)(2,1)S(1)}, bf16[512,512]{1,0:T(8,128)(2,1)S(1)}, u32[]{:S(2)}, u32[]{:S(2)}) collective-permute-start(bf16[512,512]{1,0:T(8,128)(2,1)S(1)} %pad_maximum_fusion.5), channel_id=1, source_target_pairs={{0,64},{64,128},{128,192},{192,0},{1,65},{65,129},{129,193},{193,1... | collective-permute-start | bytes 1572872 | tf_op jit(solution)/shard_map/ppermute | solution.py:25
  122.7 6.6 %collective-permute-start.22 = (bf16[256,512]{1,0:T(8,128)(2,1)S(1)}, bf16[256,512]{1,0:T(8,128)(2,1)S(1)}, u32[]{:S(2)}, u32[]{:S(2)}) collective-permute-start(bf16[256,512]{1,0:T(8,128)(2,1)S(1)} %collective-permute-done.21), channel_id=1, source_target_pairs={{0,32},{32,0},{1,33},{33,1},{2,34},{34,2},{3,35},{35,3},{4,36},{36... | collective-permute-start | bytes 786440 | tf_op jit(solution)/shard_map/ppermute | solution.py:21
  137.3 3.7 %copy-start = (bf16[256,512]{1,0:T(8,128)(2,1)S(1)}, bf16[256,512]{1,0:T(8,128)(2,1)}, u32[]{:S(2)}) copy-start(bf16[256,512]{1,0:T(8,128)(2,1)} %param.1) | copy-start | bytes 786436
  137.3 3.7 %collective-permute-start.23 = (f32[256,512]{1,0:T(8,128)S(1)}, f32[256,512]{1,0:T(8,128)S(1)}, u32[]{:S(2)}, u32[]{:S(2)}) collective-permute-start(f32[256,512]{1,0:T(8,128)S(1)} %convolution_add_fusion), channel_id=1, source_target_pairs={{0,16},{16,0},{1,17},{17,1},{2,18},{18,2},{3,19},{19,3},{4,20},{20... | collective-permute-start | bytes 1572872 | tf_op jit(solution)/shard_map/ppermute | solution.py:21

commit v12 on v11

--- a/solution.py
+++ b/solution.py
@@ -3,6 +3,8 @@
 import jax
 import jax.numpy as jnp
 from jax import lax
+from jax.experimental import pallas as pl
+from jax.experimental.pallas import tpu as pltpu
 from jax.sharding import Mesh
 from jax.sharding import PartitionSpec as P
 
@@ -52,16 +54,29 @@
     return lax.dot_general(a, b, (dims, ((), ())), preferred_element_type=F32)
 
 
-def panels_of(block):
+def blocks_of(block):
     far = fetch(block, "x", 2)
     partner = swap(block, "zl")
     pair = jnp.concatenate([block, partner], axis=0)
-    after, before = fetch(pair, "x", 1), fetch(pair, "x", 3)
-    blocks = lax.optimization_barrier([pair, after, before, far, swap(far, "zl")])
-    mine = [blocks[0][:256], blocks[1][:256], blocks[3], blocks[2][:256]]
-    theirs = [blocks[0][256:], blocks[1][256:], blocks[4], blocks[2][256:]]
-    panels = [jnp.concatenate([b.reshape(4, 1, 64, 512) for b in four], axis=1) for four in (mine, theirs)]
-    return [panel.reshape(1024, 512) for panel in panels]
+    return [pair, far], [fetch(pair, "x", 1), fetch(pair, "x", 3), swap(far, "zl")]
+
+
+def gram_kernel(own, pair, far, out):
+    for q in range(4):
+        rows = own[pl.ds(q * 128, 128)]
+        out[q, :, :512] = matmul(rows, pair[...], ((1,), (1,))).astype(BF)
+        out[q, :, 512:] = matmul(rows, far[...], ((1,), (1,))).astype(BF)
+
+
+def first_pieces(own, pair, far):
+    return pl.pallas_call(
+        gram_kernel,
+        out_shape=jax.ShapeDtypeStruct((4, 128, 768), BF),
+        in_specs=[pl.BlockSpec(memory_space=pltpu.VMEM)] * 3,
+        out_specs=pl.BlockSpec(memory_space=pltpu.VMEM),
+        cost_estimate=pl.CostEstimate(flops=2**35, bytes_accessed=2**21, transcendentals=0),
+        name="gram",
+    )(own, pair, far)
 
 
 def core_sum(products):
@@ -72,15 +87,19 @@
 
 def per_device(iterate):
     y, zh = lax.axis_index("y"), lax.axis_index("zh")
+    back = lax.rem(4 - y, 4)
     other = swap(iterate, "core")
-    panels = panels_of(iterate)
+    early, late = blocks_of(iterate)
 
-    panel = jnp.concatenate(panels, axis=0)
-
-    own = zip(chunks(window(chunks(iterate), y, 4)), chunks(window(chunks(other), y, 4)))
-    own = [window(chunks(jnp.concatenate(rows, axis=0)), zh, 4) for rows in own]
-    pieces = [matmul(rows, panel, ((1,), (1,))).astype(BF) for rows in own]
-    part = add(scatter(pieces, "y"))
+    own = [jnp.concatenate(rows, axis=0) for rows in zip(chunks(iterate), chunks(other))]
+    own = [window(chunks(rows), zh, 4) for rows in own]
+    pieces = first_pieces(jnp.concatenate(own, axis=0), *early)
+    first = add(lax.all_to_all(pieces, "y", 0, 0))
+    panel = jnp.concatenate(late, axis=0)
+    pieces = [matmul(rows, panel, ((1,), (1,))).astype(BF) for rows in chunks(window(own, y, 4))]
+    second = add(scatter(pieces, "y"))
+    part = jnp.concatenate([first, second], axis=1)
+    panel = jnp.concatenate([*early, *late], axis=0)
     part = add(scatter(chunks(part), "zh"))
     near = lax.all_gather(part, "zh", axis=0, tiled=True)
     after, before = fetch(near, "y", 1), fetch(near, "y", 3)
@@ -92,20 +111,19 @@
 
     first = core_sum([(m[:64], m[64:]) for m in map(product, (near, after, before))])
     second = core_sum([(product(far[0]), product(far[1]))])
-    inner = [first[:64], first[64:128], second, first[128:]]
-    panels = panels_of(jnp.concatenate(inner, axis=0).astype(BF))
+    inner = window([first[:64], first[64:128], second, first[128:]], back, 4)
 
-    back = lax.rem(4 - y, 4)
+    early, late = blocks_of(inner.astype(BF))
+    blocks = lax.optimization_barrier([*early, *late])
+    panels = jnp.concatenate(blocks[:2], axis=0), jnp.concatenate(blocks[2:], axis=0)
     gram = [(near[:64], near[64:]), (after[:64], after[64:]), far, (before[:64], before[64:])]
     mixed = []
     for rows in zip(*gram):
         rows = window(rows, back, 4)
-        halves = jnp.split(rows, 2, axis=1)
-        halves = [lax.dynamic_slice_in_dim(jnp.concatenate([h, h[:, :768]], axis=1), y * 256, 1024, 1) for h in halves]
+        halves = rows[:, :768], rows[:, 768:]
         mixed.append(sum(matmul(h, panel, ((1,), (0,))) for h, panel in zip(halves, panels)))
     mixed = mixed[0] + swap(mixed[1], "core")
     mine = iterate.astype(F32)
-    inner = window(inner, back, 4)
     return math.sqrt(COLS) * (coef_a * mine + (coef_b * inner + coef_c * mixed))
 
 

time: 142 us -> 148 us (1.042)
  waiting for transfers between devices: 60.2 us -> 46.5 us
  local copies, waits for them, and re-layouts: 2.04 us -> 8.92 us
  matrix products: 8.59 us -> 13.2 us
  Pallas kernels: 0 us -> 3.29 us
  starting transfers between devices: 52.2 us -> 54.5 us
  other arithmetic: 2.57 us -> 4.48 us
    ppermute x16, waiting for transfers between devices: 44.8 us -> 29.7 us  [send(): lax.ppermute(array, axis, [(i, (i + k) % 4) for i in range(4)])]
    unnamed x15 -> x35, local copies, waits for them, and re-layouts: 0.32 us -> 7.04 us
    dot_general x13, matrix products: 8.59 us -> 13.2 us  [matmul(): return lax.dot_general(a, b, (dims, ((), ())), preferred_element_type=F32)]
    all_to_all x0 -> x1, starting transfers between devices: none -> 4.18 us  [per_device(): first = add(lax.all_to_all(pieces, 'y', 0, 0))]
    pallas_call x0 -> x1, Pallas kernels: none -> 3.29 us  [first_pieces(): pl.pallas_call(gram_kernel, out_shape=jax.ShapeDtypeStruct((4, 128, 768),...]
    ppermute x8, starting transfers between devices: 25.7 us -> 23.7 us  [swap(): return lax.ppermute(array, axis, [(0, 1), (1, 0)])]
    convert_element_type x2, other arithmetic: 0.38 us -> 2.27 us  [add(): return (got[0] + got[1] + (got[2] + got[3])).astype(BF)]
  transfers between devices with their start and end apart: 24 -> 25, of which waited for: 15 -> 14; matrix products, arithmetic and copies ran while one was open for 6% -> 14% of each run, Pallas kernels for 0% -> 2%
where the time goes in v12:
time: 148 us; the launch traced here: 147 us
  starting transfers between devices  54.5 us (37%)
  waiting for transfers between devices  46.5 us (31%)
  blocking collectives  15.7 us (11%)
  matrix products  13.2 us (9%)
  local copies, waits for them, and re-layouts  8.92 us (6%)
  other arithmetic  4.48 us (3%)
  Pallas kernels  3.29 us (2%)
    ppermute x16, waiting for transfers between devices, send(): lax.ppermute(array, axis, [(i, (i + k) % 4) for i in range(4)])  29.7 us
    ppermute x16, starting transfers between devices, send(): lax.ppermute(array, axis, [(i, (i + k) % 4) for i in range(4)])  26.6 us
    ppermute x8, starting transfers between devices, swap(): return lax.ppermute(array, axis, [(0, 1), (1, 0)])  23.7 us
    ppermute x8, waiting for transfers between devices, swap(): return lax.ppermute(array, axis, [(0, 1), (1, 0)])  16.7 us
    all_gather x1, blocking collectives, per_device(): near = lax.all_gather(part, 'zh', axis=0, tiled=True)  15.7 us
    dot_general x13, matrix products, matmul(): return lax.dot_general(a, b, (dims, ((), ())), preferred_element_type=F32)  13.2 us
    unnamed x35, local copies, waits for them, and re-layouts  7.04 us
    all_to_all x1, starting transfers between devices, per_device(): first = add(lax.all_to_all(pieces, 'y', 0, 0))  4.18 us
  transfers between devices with their start and end apart: 25, of which 14 were waited for; matrix products, arithmetic and copies ran while one was open for 14% of the time, Pallas kernels for 2%

profile of v12, /device:TPU:1, one launch (start us, length us, event | category | flops | bytes accessed | tf_op | source)
XLA Modules:
  0.0 147.1 jit_solution(3122729342711300930)
XLA Ops:
  0.0 3.2 %collective-permute-start = (bf16[256,512]{1,0:T(8,128)(2,1)}, bf16[256,512]{1,0:T(8,128)(2,1)S(1)}, u32[]{:S(2)}, u32[]{:S(2)}) collective-permute-start(bf16[256,512]{1,0:T(8,128)(2,1)} %param.1), channel_id=1, source_target_pairs={{0,16},{16,0},{1,17},{17,1},{2,18},{18,2},{3,19},{19,3},{4,20},{20... | collective-permute-start | bytes 786440 | tf_op jit(solution)/shard_map/ppermute | solution.py:23
  3.2 2.6 %collective-permute-start.2 = (bf16[256,512]{1,0:T(8,128)(2,1)}, bf16[256,512]{1,0:T(8,128)(2,1)}, u32[]{:S(2)}, u32[]{:S(2)}) collective-permute-start(bf16[256,512]{1,0:T(8,128)(2,1)} %param.1), channel_id=1, source_target_pairs={{0,128},{64,192},{128,0},{192,64},{1,129},{65,193},{129,1},{193,65... | collective-permute-start | bytes 786440 | tf_op jit(solution)/shard_map/ppermute | solution.py:27
  5.9 1.6 %fusion.48 = (bf16[64,512]{1,0:T(8,128)(2,1)S(1)}, bf16[64,512]{1,0:T(8,128)(2,1)S(1)}, bf16[64,512]{1,0:T(8,128)(2,1)}, bf16[64,512]{1,0:T(8,128)(2,1)}) fusion(bf16[256,512]{1,0:T(8,128)(2,1)} %param.1), kind=kLoop, calls=%fused_computation.122 | loop fusion | bytes 524288 | tf_op jit(solution)/shard_map/split | solution.py:44
  7.5 1.7 %constant_dynamic-update-slice_fusion.17 = (bf16[2048,512]{1,0:T(8,128)(2,1)S(1)}, bf16[512,512]{1,0:T(8,128)(2,1)}) fusion(bf16[256,512]{1,0:T(8,128)(2,1)} %param.1), kind=kLoop, calls=%fused_computation.97 | loop fusion | bytes 786432
  9.2 2.3 %collective-permute-done.1 = bf16[256,512]{1,0:T(8,128)(2,1)S(1)} collective-permute-done((bf16[256,512]{1,0:T(8,128)(2,1)}, bf16[256,512]{1,0:T(8,128)(2,1)S(1)}, u32[]{:S(2)}, u32[]{:S(2)}) %collective-permute-start.1) | collective-permute-done | bytes 262176 | tf_op jit(solution)/shard_map/ppermute | solution.py:23
  11.5 0.7 constant_dynamic-update-slice_fusion.16
  12.2 1.0 collective-permute-start.3
  13.3 0.5 collective-permute-start.4
  13.8 0.3 constant_dynamic-update-slice_fusion.8
  14.1 0.3 constant_dynamic-update-slice_fusion.7
  14.4 0.3 constant_dynamic-update-slice_fusion.6
  14.7 0.3 constant_dynamic-update-slice_fusion.5
  15.0 0.8 pad_maximum_fusion.own
  15.9 3.3 %gram.1 = bf16[4,128,768]{2,1,0:T(8,128)(2,1)} custom-call(bf16[512,512]{1,0:T(8,128)(2,1)} %pad_maximum_fusion.own, bf16[512,512]{1,0:T(8,128)(2,1)} %get-tuple-element.53.pair, bf16[256,512]{1,0:T(8,128)(2,1)} %collective-permute-done.2.far), custom_call_target="tpu_custom_call" | custom-call | flops 34359738368 | bytes 2097152 | tf_op jit(solution)/shard_map/gram/pallas_call | solution.py:72
  19.1 4.2 %all-to-all-start = ((bf16[4,128,768]{2,1,0:T(8,128)(2,1)}), bf16[4,128,768]{2,1,0:T(8,128)(2,1)}, u32[]{:S(2)}, u32[]{:S(2)}) async-start(bf16[4,128,768]{2,1,0:T(8,128)(2,1)} %gram.1), calls=%async_computation | async-start | bytes 1572864 | tf_op jit(solution)/shard_map/all_to_all | solution.py:97
  23.3 1.0 collective-permute-start.5
  24.4 1.2 constant_dynamic-update-slice_fusion.15
  25.6 1.1 constant_dynamic-update-slice_fusion.14
  26.7 0.6 collective-permute-done.4
  27.4 1.1 constant_dynamic-update-slice_fusion.13
  28.5 1.8 %collective-permute-done.5 = bf16[256,512]{1,0:T(8,128)(2,1)S(1)} collective-permute-done((bf16[256,512]{1,0:T(8,128)(2,1)}, bf16[256,512]{1,0:T(8,128)(2,1)S(1)}, u32[]{:S(2)}, u32[]{:S(2)}) %collective-permute-start.5) | collective-permute-done | bytes 262176 | tf_op jit(solution)/shard_map/ppermute | solution.py:23
  30.4 2.2 %convolution_convert_fusion.2 = bf16[128,1280]{1,0:T(8,128)(2,1)} fusion(bf16[1280,512]{1,0:T(8,128)(2,1)S(1)} %get-tuple-element.51, bf16[896,512]{1,0:T(8,128)(2,1)} %copy-done.3, s32[]{:T(128)S(6)} %add.84), kind=kOutput, calls=%fused_computation.2 | convolution fusion | flops 167936000 | bytes 1769476 | tf_op jit(solution)/shard_map/dot_general | solution.py:54
  32.5 1.1 collective-permute-start.6
  33.7 2.2 %convolution_convert_fusion.1 = bf16[128,1280]{1,0:T(8,128)(2,1)} fusion(bf16[1280,512]{1,0:T(8,128)(2,1)S(1)} %get-tuple-element.51, bf16[896,512]{1,0:T(8,128)(2,1)} %copy-done.3, s32[]{:T(128)S(6)} %add.85), kind=kOutput, calls=%fused_computation.1 | convolution fusion | flops 167936000 | bytes 1769476 | tf_op jit(solution)/shard_map/dot_general | solution.py:54
  35.8 1.5 %collective-permute-start.7 = (bf16[128,1280]{1,0:T(8,128)(2,1)}, bf16[128,1280]{1,0:T(8,128)(2,1)}, u32[]{:S(2)}, u32[]{:S(2)}) collective-permute-start(bf16[128,1280]{1,0:T(8,128)(2,1)} %convolution_convert_fusion.1), channel_id=1, source_target_pairs={{0,3},{1,0},{2,1},{3,2},{4,7},{5,4},{6,5},{7,6},{8,11},{9,8},{10,9... | collective-permute-start | bytes 983048 | tf_op jit(solution)/shard_map/ppermute | solution.py:27
  37.4 2.2 %convolution_convert_fusion = bf16[128,1280]{1,0:T(8,128)(2,1)} fusion(bf16[1280,512]{1,0:T(8,128)(2,1)S(1)} %get-tuple-element.51, bf16[896,512]{1,0:T(8,128)(2,1)} %copy-done.3, s32[]{:T(128)S(6)} %add.86), kind=kOutput, calls=%fused_computation | convolution fusion | flops 167936000 | bytes 1769476 | tf_op jit(solution)/shard_map/dot_general | solution.py:54
  39.6 1.4 collective-permute-start.8
  41.0 1.3 fusion.14
  42.3 0.4 collective-permute-done.7
  42.7 6.3 %collective-permute-done.8 = bf16[128,1280]{1,0:T(8,128)(2,1)} collective-permute-done((bf16[128,1280]{1,0:T(8,128)(2,1)}, bf16[128,1280]{1,0:T(8,128)(2,1)}, u32[]{:S(2)}, u32[]{:S(2)}) %collective-permute-start.8) | collective-permute-done | bytes 327712 | tf_op jit(solution)/shard_map/ppermute | solution.py:27
  49.1 1.8 %fusion.3 = bf16[128,1280]{1,0:T(8,128)(2,1)S(1)} fusion(bf16[1280,512]{1,0:T(8,128)(2,1)S(1)} %get-tuple-element.51, bf16[128,1280]{1,0:T(8,128)(2,1)} %collective-permute-done.8, bf16[128,1280]{1,0:T(8,128)(2,1)} %collective-permute-done.7, bf16[128,1280]{1,0:T(8,128)(2,1)} %collective-permute-done.6, bf16[896,512]{1,0:T(8,128)(2,1)} %copy-done.3, ...), kind=kOutput, calls=%fused_computation.7 | convolution fusion | flops 169246720 | bytes 2752516 | tf_op jit(solution)/shard_map/dot_general | solution.py:54
  50.9 0.7 copy-done
  51.6 5.9 %collective-permute-start.10 = (bf16[32,2048]{1,0:T(8,128)(2,1)S(1)}, bf16[32,2048]{1,0:T(8,128)(2,1)S(1)}, u32[]{:S(2)}, u32[]{:S(2)}) collective-permute-start(bf16[32,2048]{1,0:T(8,128)(2,1)S(1)} %get-tuple-element.43), channel_id=1, source_target_pairs={{0,12},{4,0},{8,4},{12,8},{1,13},{5,1},{9,5},{13,9},{2,14},{6,2},{... | collective-permute-start | bytes 393224 | tf_op jit(solution)/shard_map/ppermute | solution.py:27
  57.5 1.0 collective-permute-start.11
  58.5 2.3 %collective-permute-start.9 = (bf16[32,2048]{1,0:T(8,128)(2,1)S(1)}, bf16[32,2048]{1,0:T(8,128)(2,1)S(1)}, u32[]{:S(2)}, u32[]{:S(2)}) collective-permute-start(bf16[32,2048]{1,0:T(8,128)(2,1)S(1)} %get-tuple-element.41), channel_id=1, source_target_pairs={{0,4},{4,8},{8,12},{12,0},{1,5},{5,9},{9,13},{13,1},{2,6},{6,10},{... | collective-permute-start | bytes 393224 | tf_op jit(solution)/shard_map/ppermute | solution.py:27
  60.7 5.9 %collective-permute-done.11 = bf16[32,2048]{1,0:T(8,128)(2,1)S(1)} collective-permute-done((bf16[32,2048]{1,0:T(8,128)(2,1)S(1)}, bf16[32,2048]{1,0:T(8,128)(2,1)S(1)}, u32[]{:S(2)}, u32[]{:S(2)}) %collective-permute-start.11) | collective-permute-done | bytes 131104 | tf_op jit(solution)/shard_map/ppermute | solution.py:27
  66.6 0.9 collective-permute-done.9
  67.5 1.0 add_convert_fusion.1
  68.5 15.7 %all_gather.3 = bf16[128,2048]{1,0:T(8,128)(2,1)S(1)} all-gather(bf16[32,2048]{1,0:T(8,128)(2,1)S(1)} %add_convert_fusion.1), channel_id=1, replica_groups=mesh['x'=4,'zl'=2,'core'=2,'zh'=4,'y'=4] {'zh'}, dimensions={0}, use_global_device_ids=true | all-gather | bytes 655360 | tf_op jit(solution)/shard_map/all_gather | solution.py:104
  84.2 2.8 %collective-permute-start.12 = (bf16[128,2048]{1,0:T(8,128)(2,1)S(1)}, bf16[128,2048]{1,0:T(8,128)(2,1)S(1)}, u32[]{:S(2)}, u32[]{:S(2)}) collective-permute-start(bf16[128,2048]{1,0:T(8,128)(2,1)S(1)} %all_gather.3), channel_id=1, source_target_pairs={{0,3},{1,0},{2,1},{3,2},{4,7},{5,4},{6,5},{7,6},{8,11},{9,8},{10,9... | collective-permute-start | bytes 1572872 | tf_op jit(solution)/shard_map/ppermute | solution.py:27
  86.9 0.4 fusion.50
  87.5 8.7 %collective-permute-done.13 = bf16[128,2048]{1,0:T(8,128)(2,1)S(1)} collective-permute-done((bf16[128,2048]{1,0:T(8,128)(2,1)S(1)}, bf16[128,2048]{1,0:T(8,128)(2,1)S(1)}, u32[]{:S(2)}, u32[]{:S(2)}) %collective-permute-start.13) | collective-permute-done | bytes 524320 | tf_op jit(solution)/shard_map/ppermute | solution.py:27
  96.4 1.5 collective-permute-start.16
  97.8 0.4 fusion.51
  98.3 0.4 fusion.52
  98.8 11.4 %collective-permute-start.14 = (f32[192,512]{1,0:T(8,128)S(1)}, f32[192,512]{1,0:T(8,128)S(1)}, u32[]{:S(2)}, u32[]{:S(2)}) collective-permute-start(f32[192,512]{1,0:T(8,128)S(1)} %pad_maximum_fusion.2), channel_id=1, source_target_pairs={{0,16},{16,0},{1,17},{17,1},{2,18},{18,2},{3,19},{19,3},{4,20},{20... | collective-permute-start | bytes 1179656 | tf_op jit(solution)/shard_map/ppermute | solution.py:23
  110.3 0.5 fusion.53
  110.8 4.6 %collective-permute-start.17 = (f32[64,512]{1,0:T(8,128)S(1)}, f32[64,512]{1,0:T(8,128)S(1)}, u32[]{:S(2)}, u32[]{:S(2)}) collective-permute-start(f32[64,512]{1,0:T(8,128)S(1)} %fusion.53), channel_id=1, source_target_pairs={{0,16},{16,0},{1,17},{17,1},{2,18},{18,2},{3,19},{19,3},{4,20},{20... | collective-permute-start | bytes 393224 | tf_op jit(solution)/shard_map/ppermute | solution.py:23
  115.6 0.8 collective-permute-done.17
  116.4 0.5 constant_dynamic-update-slice_fusion.19
  117.0 0.5 collective-permute-start.18
  117.5 2.1 %collective-permute-start.19 = (bf16[256,512]{1,0:T(8,128)(2,1)S(1)}, bf16[256,512]{1,0:T(8,128)(2,1)S(1)}, u32[]{:S(2)}, u32[]{:S(2)}) collective-permute-start(bf16[256,512]{1,0:T(8,128)(2,1)S(1)} %dynamic-slice_convert_fusion), channel_id=1, source_target_pairs={{0,128},{64,192},{128,0},{192,64},{1,129},{65,193},{129,1},{193,65... | collective-permute-start | bytes 786440 | tf_op jit(solution)/shard_map/ppermute | solution.py:27
  119.6 5.0 %collective-permute-done.18 = bf16[256,512]{1,0:T(8,128)(2,1)S(1)} collective-permute-done((bf16[256,512]{1,0:T(8,128)(2,1)S(1)}, bf16[256,512]{1,0:T(8,128)(2,1)S(1)}, u32[]{:S(2)}, u32[]{:S(2)}) %collective-permute-start.18) | collective-permute-done | bytes 262176 | tf_op jit(solution)/shard_map/ppermute | solution.py:23
  124.7 2.9 %collective-permute-start.20 = (bf16[512,512]{1,0:T(8,128)(2,1)S(1)}, bf16[512,512]{1,0:T(8,128)(2,1)S(1)}, u32[]{:S(2)}, u32[]{:S(2)}) collective-permute-start(bf16[512,512]{1,0:T(8,128)(2,1)S(1)} %pad_maximum_fusion.1), channel_id=1, source_target_pairs={{0,192},{64,0},{128,64},{192,128},{1,193},{65,1},{129,65},{193,129... | collective-permute-start | bytes 1572872 | tf_op jit(solution)/shard_map/ppermute | solution.py:27
  127.6 0.5 collective-permute-start.22
  128.1 5.8 %collective-permute-done.22 = bf16[256,512]{1,0:T(8,128)(2,1)S(1)} collective-permute-done((bf16[256,512]{1,0:T(8,128)(2,1)S(1)}, bf16[256,512]{1,0:T(8,128)(2,1)S(1)}, u32[]{:S(2)}, u32[]{:S(2)}) %collective-permute-start.22) | collective-permute-done | bytes 262176 | tf_op jit(solution)/shard_map/ppermute | solution.py:23
  133.9 3.8 %collective-permute-done.20 = bf16[512,512]{1,0:T(8,128)(2,1)S(1)} collective-permute-done((bf16[512,512]{1,0:T(8,128)(2,1)S(1)}, bf16[512,512]{1,0:T(8,128)(2,1)S(1)}, u32[]{:S(2)}, u32[]{:S(2)}) %collective-permute-start.20) | collective-permute-done | bytes 524320 | tf_op jit(solution)/shard_map/ppermute | solution.py:27
  137.7 3.0 %collective-permute-done.21 = bf16[512,512]{1,0:T(8,128)(2,1)S(1)} collective-permute-done((bf16[512,512]{1,0:T(8,128)(2,1)S(1)}, bf16[512,512]{1,0:T(8,128)(2,1)S(1)}, u32[]{:S(2)}, u32[]{:S(2)}) %collective-permute-start.21) | collective-permute-done | bytes 524320 | tf_op jit(solution)/shard_map/ppermute | solution.py:27
  140.9 0.5 fusion.6
  141.4 0.4 convolution_add_fusion
  141.8 2.5 %collective-permute-start.23 = (f32[256,512]{1,0:T(8,128)S(1)}, f32[256,512]{1,0:T(8,128)S(1)}, u32[]{:S(2)}, u32[]{:S(2)}) collective-permute-start(f32[256,512]{1,0:T(8,128)S(1)} %convolution_add_fusion), channel_id=1, source_target_pairs={{0,16},{16,0},{1,17},{17,1},{2,18},{18,2},{3,19},{19,3},{4,20},{20... | collective-permute-start | bytes 1572872 | tf_op jit(solution)/shard_map/ppermute | solution.py:23
  144.3 0.5 fusion.8
  144.8 1.0 collective-permute-done.23
  145.8 1.2 add_multiply_fusion
  (61 shorter events, 1.0 us)
Async XLA Ops:
  0.0 13.7 %collective-permute-start = (bf16[256,512]{1,0:T(8,128)(2,1)}, bf16[256,512]{1,0:T(8,128)(2,1)S(1)}, u32[]{:S(2)}, u32[]{:S(2)}) collective-permute-start(bf16[256,512]{1,0:T(8,128)(2,1)} %param.1), channel_id=1, source_target_pairs={{0,16},{16,0},{1,17},{17,1},{2,18},{18,2},{3,19},{19,3},{4,20},{20... | collective-permute-start | bytes 786440 | tf_op jit(solution)/shard_map/ppermute | solution.py:23
  3.2 8.3 %collective-permute-start.1 = (bf16[256,512]{1,0:T(8,128)(2,1)}, bf16[256,512]{1,0:T(8,128)(2,1)S(1)}, u32[]{:S(2)}, u32[]{:S(2)}) collective-permute-start(bf16[256,512]{1,0:T(8,128)(2,1)} %param.1), channel_id=1, source_target_pairs={{0,32},{32,0},{1,33},{33,1},{2,34},{34,2},{3,35},{35,3},{4,36},{36... | collective-permute-start | bytes 786440 | tf_op jit(solution)/shard_map/ppermute | solution.py:23
  3.2 12.6 %collective-permute-start.2 = (bf16[256,512]{1,0:T(8,128)(2,1)}, bf16[256,512]{1,0:T(8,128)(2,1)}, u32[]{:S(2)}, u32[]{:S(2)}) collective-permute-start(bf16[256,512]{1,0:T(8,128)(2,1)} %param.1), channel_id=1, source_target_pairs={{0,128},{64,192},{128,0},{192,64},{1,129},{65,193},{129,1},{193,65... | collective-permute-start | bytes 786440 | tf_op jit(solution)/shard_map/ppermute | solution.py:27
  7.5 6.3 %copy-start.5 = (bf16[64,512]{1,0:T(8,128)(2,1)S(1)}, bf16[64,512]{1,0:T(8,128)(2,1)}, u32[]{:S(2)}) copy-start(bf16[64,512]{1,0:T(8,128)(2,1)} %get-tuple-element.63) | copy-start | bytes 196612
  7.5 6.6 %copy-start.4 = (bf16[64,512]{1,0:T(8,128)(2,1)S(1)}, bf16[64,512]{1,0:T(8,128)(2,1)}, u32[]{:S(2)}) copy-start(bf16[64,512]{1,0:T(8,128)(2,1)} %get-tuple-element.62) | copy-start | bytes 196612
  12.2 13.3 %collective-permute-start.3 = (bf16[512,512]{1,0:T(8,128)(2,1)}, bf16[512,512]{1,0:T(8,128)(2,1)}, u32[]{:S(2)}, u32[]{:S(2)}) collective-permute-start(bf16[512,512]{1,0:T(8,128)(2,1)} %get-tuple-element.53.pair), channel_id=1, source_target_pairs={{0,192},{64,0},{128,64},{192,128},{1,193},{65,1},{129,65},{193,129... | collective-permute-start | bytes 1572872 | tf_op jit(solution)/shard_map/ppermute | solution.py:27
  13.3 14.1 %collective-permute-start.4 = (bf16[512,512]{1,0:T(8,128)(2,1)}, bf16[512,512]{1,0:T(8,128)(2,1)}, u32[]{:S(2)}, u32[]{:S(2)}) collective-permute-start(bf16[512,512]{1,0:T(8,128)(2,1)} %get-tuple-element.53.pair), channel_id=1, source_target_pairs={{0,64},{64,128},{128,192},{192,0},{1,65},{65,129},{129,193},{193,1... | collective-permute-start | bytes 1572872 | tf_op jit(solution)/shard_map/ppermute | solution.py:27
  19.1 21.9 %all-to-all-start = ((bf16[4,128,768]{2,1,0:T(8,128)(2,1)}), bf16[4,128,768]{2,1,0:T(8,128)(2,1)}, u32[]{:S(2)}, u32[]{:S(2)}) async-start(bf16[4,128,768]{2,1,0:T(8,128)(2,1)} %gram.1), calls=%async_computation | async-start | bytes 1572864 | tf_op jit(solution)/shard_map/all_to_all | solution.py:97
  23.3 7.0 %collective-permute-start.5 = (bf16[256,512]{1,0:T(8,128)(2,1)}, bf16[256,512]{1,0:T(8,128)(2,1)S(1)}, u32[]{:S(2)}, u32[]{:S(2)}) collective-permute-start(bf16[256,512]{1,0:T(8,128)(2,1)} %collective-permute-done.2.far), channel_id=1, source_target_pairs={{0,32},{32,0},{1,33},{33,1},{2,34},{34,2},{3,35},{35,3},{4,36},{36... | collective-permute-start | bytes 786440 | tf_op jit(solution)/shard_map/ppermute | solution.py:23
  24.4 1.2 copy-start.3
  32.5 9.8 %collective-permute-start.6 = (bf16[128,1280]{1,0:T(8,128)(2,1)}, bf16[128,1280]{1,0:T(8,128)(2,1)}, u32[]{:S(2)}, u32[]{:S(2)}) collective-permute-start(bf16[128,1280]{1,0:T(8,128)(2,1)} %convolution_convert_fusion.2), channel_id=1, source_target_pairs={{0,1},{1,2},{2,3},{3,0},{4,5},{5,6},{6,7},{7,4},{8,9},{9,10},{10,1... | collective-permute-start | bytes 983048 | tf_op jit(solution)/shard_map/ppermute | solution.py:27
  35.8 6.9 %collective-permute-start.7 = (bf16[128,1280]{1,0:T(8,128)(2,1)}, bf16[128,1280]{1,0:T(8,128)(2,1)}, u32[]{:S(2)}, u32[]{:S(2)}) collective-permute-start(bf16[128,1280]{1,0:T(8,128)(2,1)} %convolution_convert_fusion.1), channel_id=1, source_target_pairs={{0,3},{1,0},{2,1},{3,2},{4,7},{5,4},{6,5},{7,6},{8,11},{9,8},{10,9... | collective-permute-start | bytes 983048 | tf_op jit(solution)/shard_map/ppermute | solution.py:27
  39.6 9.5 %collective-permute-start.8 = (bf16[128,1280]{1,0:T(8,128)(2,1)}, bf16[128,1280]{1,0:T(8,128)(2,1)}, u32[]{:S(2)}, u32[]{:S(2)}) collective-permute-start(bf16[128,1280]{1,0:T(8,128)(2,1)} %convolution_convert_fusion), channel_id=1, source_target_pairs={{0,2},{1,3},{2,0},{3,1},{4,6},{5,7},{6,4},{7,5},{8,10},{9,11},{10,... | collective-permute-start | bytes 983048 | tf_op jit(solution)/shard_map/ppermute | solution.py:27
  42.3 9.3 %copy-start.2 = (bf16[128,768]{1,0:T(8,128)(2,1)}, bf16[128,768]{1,0:T(8,128)(2,1)S(1)}, u32[]{:S(2)}) copy-start(bf16[128,768]{1,0:T(8,128)(2,1)S(1)} %fusion.14) | copy-start | bytes 589828
  50.9 0.7 copy-start
  51.6 9.1 %collective-permute-start.10 = (bf16[32,2048]{1,0:T(8,128)(2,1)S(1)}, bf16[32,2048]{1,0:T(8,128)(2,1)S(1)}, u32[]{:S(2)}, u32[]{:S(2)}) collective-permute-start(bf16[32,2048]{1,0:T(8,128)(2,1)S(1)} %get-tuple-element.43), channel_id=1, source_target_pairs={{0,12},{4,0},{8,4},{12,8},{1,13},{5,1},{9,5},{13,9},{2,14},{6,2},{... | collective-permute-start | bytes 393224 | tf_op jit(solution)/shard_map/ppermute | solution.py:27
  57.5 9.1 %collective-permute-start.11 = (bf16[32,2048]{1,0:T(8,128)(2,1)S(1)}, bf16[32,2048]{1,0:T(8,128)(2,1)S(1)}, u32[]{:S(2)}, u32[]{:S(2)}) collective-permute-start(bf16[32,2048]{1,0:T(8,128)(2,1)S(1)} %get-tuple-element.42), channel_id=1, source_target_pairs={{0,8},{4,12},{8,0},{12,4},{1,9},{5,13},{9,1},{13,5},{2,10},{6,14},... | collective-permute-start | bytes 393224 | tf_op jit(solution)/shard_map/ppermute | solution.py:27
  58.5 9.1 %collective-permute-start.9 = (bf16[32,2048]{1,0:T(8,128)(2,1)S(1)}, bf16[32,2048]{1,0:T(8,128)(2,1)S(1)}, u32[]{:S(2)}, u32[]{:S(2)}) collective-permute-start(bf16[32,2048]{1,0:T(8,128)(2,1)S(1)} %get-tuple-element.41), channel_id=1, source_target_pairs={{0,4},{4,8},{8,12},{12,0},{1,5},{5,9},{9,13},{13,1},{2,6},{6,10},{... | collective-permute-start | bytes 393224 | tf_op jit(solution)/shard_map/ppermute | solution.py:27
  84.2 12.0 %collective-permute-start.12 = (bf16[128,2048]{1,0:T(8,128)(2,1)S(1)}, bf16[128,2048]{1,0:T(8,128)(2,1)S(1)}, u32[]{:S(2)}, u32[]{:S(2)}) collective-permute-start(bf16[128,2048]{1,0:T(8,128)(2,1)S(1)} %all_gather.3), channel_id=1, source_target_pairs={{0,3},{1,0},{2,1},{3,2},{4,7},{5,4},{6,5},{7,6},{8,11},{9,8},{10,9... | collective-permute-start | bytes 1572872 | tf_op jit(solution)/shard_map/ppermute | solution.py:27
  86.9 9.2 %collective-permute-start.13 = (bf16[128,2048]{1,0:T(8,128)(2,1)S(1)}, bf16[128,2048]{1,0:T(8,128)(2,1)S(1)}, u32[]{:S(2)}, u32[]{:S(2)}) collective-permute-start(bf16[128,2048]{1,0:T(8,128)(2,1)S(1)} %all_gather.3), channel_id=1, source_target_pairs={{0,1},{1,2},{2,3},{3,0},{4,5},{5,6},{6,7},{7,4},{8,9},{9,10},{10,1... | collective-permute-start | bytes 1572872 | tf_op jit(solution)/shard_map/ppermute | solution.py:27
  96.3 13.9 %collective-permute-start.15 = (bf16[64,2048]{1,0:T(8,128)(2,1)S(1)}, bf16[64,2048]{1,0:T(8,128)(2,1)S(1)}, u32[]{:S(2)}, u32[]{:S(2)}) collective-permute-start(bf16[64,2048]{1,0:T(8,128)(2,1)S(1)} %get-tuple-element.14), channel_id=1, source_target_pairs={{0,3},{1,0},{2,1},{3,2},{4,7},{5,4},{6,5},{7,6},{8,11},{9,8},{10,9... | collective-permute-start | bytes 786440 | tf_op jit(solution)/shard_map/ppermute | solution.py:27
  96.4 13.8 %collective-permute-start.16 = (bf16[64,2048]{1,0:T(8,128)(2,1)S(1)}, bf16[64,2048]{1,0:T(8,128)(2,1)S(1)}, u32[]{:S(2)}, u32[]{:S(2)}) collective-permute-start(bf16[64,2048]{1,0:T(8,128)(2,1)S(1)} %slice.113), channel_id=1, source_target_pairs={{0,1},{1,2},{2,3},{3,0},{4,5},{5,6},{6,7},{7,4},{8,9},{9,10},{10,1... | collective-permute-start | bytes 786440 | tf_op jit(solution)/shard_map/ppermute | solution.py:27
  98.8 16.7 %collective-permute-start.14 = (f32[192,512]{1,0:T(8,128)S(1)}, f32[192,512]{1,0:T(8,128)S(1)}, u32[]{:S(2)}, u32[]{:S(2)}) collective-permute-start(f32[192,512]{1,0:T(8,128)S(1)} %pad_maximum_fusion.2), channel_id=1, source_target_pairs={{0,16},{16,0},{1,17},{17,1},{2,18},{18,2},{3,19},{19,3},{4,20},{20... | collective-permute-start | bytes 1179656 | tf_op jit(solution)/shard_map/ppermute | solution.py:23
  110.8 5.6 %collective-permute-start.17 = (f32[64,512]{1,0:T(8,128)S(1)}, f32[64,512]{1,0:T(8,128)S(1)}, u32[]{:S(2)}, u32[]{:S(2)}) collective-permute-start(f32[64,512]{1,0:T(8,128)S(1)} %fusion.53), channel_id=1, source_target_pairs={{0,16},{16,0},{1,17},{17,1},{2,18},{18,2},{3,19},{19,3},{4,20},{20... | collective-permute-start | bytes 393224 | tf_op jit(solution)/shard_map/ppermute | solution.py:23
  117.0 7.6 %collective-permute-start.18 = (bf16[256,512]{1,0:T(8,128)(2,1)S(1)}, bf16[256,512]{1,0:T(8,128)(2,1)S(1)}, u32[]{:S(2)}, u32[]{:S(2)}) collective-permute-start(bf16[256,512]{1,0:T(8,128)(2,1)S(1)} %dynamic-slice_convert_fusion), channel_id=1, source_target_pairs={{0,32},{32,0},{1,33},{33,1},{2,34},{34,2},{3,35},{35,3},{4,36},{36... | collective-permute-start | bytes 786440 | tf_op jit(solution)/shard_map/ppermute | solution.py:23
  117.5 10.1 %collective-permute-start.19 = (bf16[256,512]{1,0:T(8,128)(2,1)S(1)}, bf16[256,512]{1,0:T(8,128)(2,1)S(1)}, u32[]{:S(2)}, u32[]{:S(2)}) collective-permute-start(bf16[256,512]{1,0:T(8,128)(2,1)S(1)} %dynamic-slice_convert_fusion), channel_id=1, source_target_pairs={{0,128},{64,192},{128,0},{192,64},{1,129},{65,193},{129,1},{193,65... | collective-permute-start | bytes 786440 | tf_op jit(solution)/shard_map/ppermute | solution.py:27
  124.7 13.1 %collective-permute-start.20 = (bf16[512,512]{1,0:T(8,128)(2,1)S(1)}, bf16[512,512]{1,0:T(8,128)(2,1)S(1)}, u32[]{:S(2)}, u32[]{:S(2)}) collective-permute-start(bf16[512,512]{1,0:T(8,128)(2,1)S(1)} %pad_maximum_fusion.1), channel_id=1, source_target_pairs={{0,192},{64,0},{128,64},{192,128},{1,193},{65,1},{129,65},{193,129... | collective-permute-start | bytes 1572872 | tf_op jit(solution)/shard_map/ppermute | solution.py:27
  127.6 13.2 %collective-permute-start.21 = (bf16[512,512]{1,0:T(8,128)(2,1)S(1)}, bf16[512,512]{1,0:T(8,128)(2,1)S(1)}, u32[]{:S(2)}, u32[]{:S(2)}) collective-permute-start(bf16[512,512]{1,0:T(8,128)(2,1)S(1)} %pad_maximum_fusion.1), channel_id=1, source_target_pairs={{0,64},{64,128},{128,192},{192,0},{1,65},{65,129},{129,193},{193,1... | collective-permute-start | bytes 1572872 | tf_op jit(solution)/shard_map/ppermute | solution.py:27
  127.6 6.3 %collective-permute-start.22 = (bf16[256,512]{1,0:T(8,128)(2,1)S(1)}, bf16[256,512]{1,0:T(8,128)(2,1)S(1)}, u32[]{:S(2)}, u32[]{:S(2)}) collective-permute-start(bf16[256,512]{1,0:T(8,128)(2,1)S(1)} %collective-permute-done.19), channel_id=1, source_target_pairs={{0,32},{32,0},{1,33},{33,1},{2,34},{34,2},{3,35},{35,3},{4,36},{36... | collective-permute-start | bytes 786440 | tf_op jit(solution)/shard_map/ppermute | solution.py:23
  141.8 4.0 %copy-start.1 = (bf16[256,512]{1,0:T(8,128)(2,1)S(1)}, bf16[256,512]{1,0:T(8,128)(2,1)}, u32[]{:S(2)}) copy-start(bf16[256,512]{1,0:T(8,128)(2,1)} %param.1) | copy-start | bytes 786436
  141.8 4.0 %collective-permute-start.23 = (f32[256,512]{1,0:T(8,128)S(1)}, f32[256,512]{1,0:T(8,128)S(1)}, u32[]{:S(2)}, u32[]{:S(2)}) collective-permute-start(f32[256,512]{1,0:T(8,128)S(1)} %convolution_add_fusion), channel_id=1, source_target_pairs={{0,16},{16,0},{1,17},{17,1},{2,18},{18,2},{3,19},{19,3},{4,20},{20... | collective-permute-start | bytes 1572872 | tf_op jit(solution)/shard_map/ppermute | solution.py:23

commit v13 on v12

--- a/solution.py
+++ b/solution.py
@@ -3,8 +3,6 @@
 import jax
 import jax.numpy as jnp
 from jax import lax
-from jax.experimental import pallas as pl
-from jax.experimental.pallas import tpu as pltpu
 from jax.sharding import Mesh
 from jax.sharding import PartitionSpec as P
 
@@ -58,25 +56,7 @@
     far = fetch(block, "x", 2)
     partner = swap(block, "zl")
     pair = jnp.concatenate([block, partner], axis=0)
-    return [pair, far], [fetch(pair, "x", 1), fetch(pair, "x", 3), swap(far, "zl")]
-
-
-def gram_kernel(own, pair, far, out):
-    for q in range(4):
-        rows = own[pl.ds(q * 128, 128)]
-        out[q, :, :512] = matmul(rows, pair[...], ((1,), (1,))).astype(BF)
-        out[q, :, 512:] = matmul(rows, far[...], ((1,), (1,))).astype(BF)
-
-
-def first_pieces(own, pair, far):
-    return pl.pallas_call(
-        gram_kernel,
-        out_shape=jax.ShapeDtypeStruct((4, 128, 768), BF),
-        in_specs=[pl.BlockSpec(memory_space=pltpu.VMEM)] * 3,
-        out_specs=pl.BlockSpec(memory_space=pltpu.VMEM),
-        cost_estimate=pl.CostEstimate(flops=2**35, bytes_accessed=2**21, transcendentals=0),
-        name="gram",
-    )(own, pair, far)
+    return pair, [far, fetch(pair, "x", 1), fetch(pair, "x", 3), swap(far, "zl")]
 
 
 def core_sum(products):
@@ -89,17 +69,17 @@
     y, zh = lax.axis_index("y"), lax.axis_index("zh")
     back = lax.rem(4 - y, 4)
     other = swap(iterate, "core")
-    early, late = blocks_of(iterate)
+    pair, late = blocks_of(iterate)
 
     own = [jnp.concatenate(rows, axis=0) for rows in zip(chunks(iterate), chunks(other))]
     own = [window(chunks(rows), zh, 4) for rows in own]
-    pieces = first_pieces(jnp.concatenate(own, axis=0), *early)
-    first = add(lax.all_to_all(pieces, "y", 0, 0))
-    panel = jnp.concatenate(late, axis=0)
+    pieces = matmul(jnp.concatenate(own, axis=0), pair, ((1,), (1,))).astype(BF)
+    first = add(lax.all_to_all(pieces.reshape(4, 128, 512), "y", 0, 0))
+    panel = lax.optimization_barrier(jnp.concatenate(late, axis=0))
     pieces = [matmul(rows, panel, ((1,), (1,))).astype(BF) for rows in chunks(window(own, y, 4))]
     second = add(scatter(pieces, "y"))
     part = jnp.concatenate([first, second], axis=1)
-    panel = jnp.concatenate([*early, *late], axis=0)
+    panel = jnp.concatenate([pair, panel], axis=0)
     part = add(scatter(chunks(part), "zh"))
     near = lax.all_gather(part, "zh", axis=0, tiled=True)
     after, before = fetch(near, "y", 1), fetch(near, "y", 3)
@@ -113,14 +93,14 @@
     second = core_sum([(product(far[0]), product(far[1]))])
     inner = window([first[:64], first[64:128], second, first[128:]], back, 4)
 
-    early, late = blocks_of(inner.astype(BF))
-    blocks = lax.optimization_barrier([*early, *late])
-    panels = jnp.concatenate(blocks[:2], axis=0), jnp.concatenate(blocks[2:], axis=0)
+    pair, late = blocks_of(inner.astype(BF))
+    pair, *late = lax.optimization_barrier([pair, *late])
+    panels = pair, jnp.concatenate(late, axis=0)
     gram = [(near[:64], near[64:]), (after[:64], after[64:]), far, (before[:64], before[64:])]
     mixed = []
     for rows in zip(*gram):
         rows = window(rows, back, 4)
-        halves = rows[:, :768], rows[:, 768:]
+        halves = rows[:, :512], rows[:, 512:]
         mixed.append(sum(matmul(h, panel, ((1,), (0,))) for h, panel in zip(halves, panels)))
     mixed = mixed[0] + swap(mixed[1], "core")
     mine = iterate.astype(F32)

time: 148 us -> 144 us (0.973)
  waiting for transfers between devices: 46.5 us -> 53.4 us
  local copies, waits for them, and re-layouts: 8.92 us -> 4.04 us
  Pallas kernels: 3.29 us -> 0 us
  other arithmetic: 4.48 us -> 1.59 us
    unnamed x35 -> x27, local copies, waits for them, and re-layouts: 7.04 us -> 2.11 us
    ppermute x8, waiting for transfers between devices: 16.7 us -> 21.3 us  [swap(): return lax.ppermute(array, axis, [(0, 1), (1, 0)])]
    pallas_call x1 -> x0, Pallas kernels: 3.29 us -> none  [first_pieces(): pl.pallas_call(gram_kernel, out_shape=jax.ShapeDtypeStruct((4, 128, 768),...]
    ppermute x8, starting transfers between devices: 23.7 us -> 26.5 us  [swap(): return lax.ppermute(array, axis, [(0, 1), (1, 0)])]
    ppermute x16, starting transfers between devices: 26.6 us -> 24.1 us  [send(): lax.ppermute(array, axis, [(i, (i + k) % 4) for i in range(4)])]
    ppermute x16, waiting for transfers between devices: 29.7 us -> 32.2 us  [send(): lax.ppermute(array, axis, [(i, (i + k) % 4) for i in range(4)])]
    convert_element_type x2, other arithmetic: 2.27 us -> 0.14 us  [add(): return (got[0] + got[1] + (got[2] + got[3])).astype(BF)]
    dot_general x13 -> x14, matrix products: 13.2 us -> 13.8 us  [matmul(): return lax.dot_general(a, b, (dims, ((), ())), preferred_element_type=F32)]
  transfers between devices with their start and end apart: 25 -> 25, of which waited for: 14 -> 15; matrix products, arithmetic and copies ran while one was open for 14% -> 10% of each run, Pallas kernels for 2% -> 0%
where the time goes in v13:
time: 144 us; the launch traced here: 143 us
  starting transfers between devices  54.4 us (38%)
  waiting for transfers between devices  53.4 us (37%)
  blocking collectives  15.7 us (11%)
  matrix products  13.8 us (10%)
  local copies, waits for them, and re-layouts  4.04 us (3%)
  other arithmetic  1.59 us (1%)
    ppermute x16, waiting for transfers between devices, send(): lax.ppermute(array, axis, [(i, (i + k) % 4) for i in range(4)])  32.2 us
    ppermute x8, starting transfers between devices, swap(): return lax.ppermute(array, axis, [(0, 1), (1, 0)])  26.5 us
    ppermute x16, starting transfers between devices, send(): lax.ppermute(array, axis, [(i, (i + k) % 4) for i in range(4)])  24.1 us
    ppermute x8, waiting for transfers between devices, swap(): return lax.ppermute(array, axis, [(0, 1), (1, 0)])  21.3 us
    all_gather x1, blocking collectives, per_device(): near = lax.all_gather(part, 'zh', axis=0, tiled=True)  15.7 us
    dot_general x14, matrix products, matmul(): return lax.dot_general(a, b, (dims, ((), ())), preferred_element_type=F32)  13.8 us
    all_to_all x1, starting transfers between devices, per_device(): first = add(lax.all_to_all(pieces.reshape(4, 128, 512), 'y', 0, 0))  3.74 us
  transfers between devices with their start and end apart: 25, of which 15 were waited for; matrix products, arithmetic and copies ran while one was open for 10% of the time, Pallas kernels for 0%

profile of v13, /device:TPU:1, one launch (start us, length us, event | category | flops | bytes accessed | tf_op | source)
XLA Modules:
  0.0 143.4 jit_solution(16288838783508166140)
XLA Ops:
  0.0 3.2 %collective-permute-start = (bf16[256,512]{1,0:T(8,128)(2,1)}, bf16[256,512]{1,0:T(8,128)(2,1)S(1)}, u32[]{:S(2)}, u32[]{:S(2)}) collective-permute-start(bf16[256,512]{1,0:T(8,128)(2,1)} %param.1), channel_id=1, source_target_pairs={{0,16},{16,0},{1,17},{17,1},{2,18},{18,2},{3,19},{19,3},{4,20},{20... | collective-permute-start | bytes 786440 | tf_op jit(solution)/shard_map/ppermute | solution.py:21
  3.2 2.6 %collective-permute-start.2 = (bf16[256,512]{1,0:T(8,128)(2,1)}, bf16[256,512]{1,0:T(8,128)(2,1)S(1)}, u32[]{:S(2)}, u32[]{:S(2)}) collective-permute-start(bf16[256,512]{1,0:T(8,128)(2,1)} %param.1), channel_id=1, source_target_pairs={{0,128},{64,192},{128,0},{192,64},{1,129},{65,193},{129,1},{193,65... | collective-permute-start | bytes 786440 | tf_op jit(solution)/shard_map/ppermute | solution.py:25
  5.9 1.0 fusion.60
  6.9 1.7 %constant_dynamic-update-slice_fusion.1 = bf16[512,512]{1,0:T(8,128)(2,1)} fusion(bf16[256,512]{1,0:T(8,128)(2,1)} %param.1), kind=kLoop, calls=%fused_computation.90 | loop fusion | bytes 524288
  8.5 2.9 %collective-permute-done.1 = bf16[256,512]{1,0:T(8,128)(2,1)S(1)} collective-permute-done((bf16[256,512]{1,0:T(8,128)(2,1)}, bf16[256,512]{1,0:T(8,128)(2,1)S(1)}, u32[]{:S(2)}, u32[]{:S(2)}) %collective-permute-start.1) | collective-permute-done | bytes 262176 | tf_op jit(solution)/shard_map/ppermute | solution.py:21
  11.4 0.8 constant_dynamic-update-slice_fusion
  12.1 1.0 collective-permute-start.3
  13.2 0.5 collective-permute-start.4
  13.7 0.3 constant_dynamic-update-slice_fusion.8
  14.0 0.3 constant_dynamic-update-slice_fusion.7
  14.3 0.3 constant_dynamic-update-slice_fusion.6
  14.6 0.3 constant_dynamic-update-slice_fusion.5
  14.9 2.3 %convolution_convert_fusion.4 = bf16[512,512]{1,0:T(8,128)(2,1)} fusion(bf16[512,512]{1,0:T(8,128)(2,1)} %constant_dynamic-update-slice_fusion, bf16[128,512]{1,0:T(8,128)(2,1)S(1)} %get-tuple-element.24, bf16[128,512]{1,0:T(8,128)(2,1)S(1)} %get-tuple-element.26, bf16[128,512]{1,0:T(8,128)(2,1)S(1)} %get-tuple-element.28, ...), kind=kOutput, calls=%fused_computation.10 | convolution fusion | flops 270794752 | bytes 1572864 | tf_op jit(solution)/shard_map/dot_general | solution.py:52
  17.2 3.7 %all-to-all-start = ((bf16[4,128,512]{2,1,0:T(8,128)(2,1)}), bf16[4,128,512]{2,1,0:T(8,128)(2,1)S(1)}, u32[]{:S(2)}, u32[]{:S(2)}) async-start(bf16[4,128,512]{2,1,0:T(8,128)(2,1)} %bitcast), calls=%async_computation | async-start | bytes 1048576 | tf_op jit(solution)/shard_map/all_to_all | solution.py:77
  20.9 1.4 collective-permute-start.5
  22.4 5.1 %collective-permute-done.5 = bf16[256,512]{1,0:T(8,128)(2,1)S(1)} collective-permute-done((bf16[256,512]{1,0:T(8,128)(2,1)S(1)}, bf16[256,512]{1,0:T(8,128)(2,1)S(1)}, u32[]{:S(2)}, u32[]{:S(2)}) %collective-permute-start.5) | collective-permute-done | bytes 262176 | tf_op jit(solution)/shard_map/ppermute | solution.py:21
  27.5 0.1 pad_maximum_fusion.1
  27.6 1.6 %convolution_convert_fusion.2 = bf16[128,1536]{1,0:T(8,128)(2,1)S(1)} fusion(bf16[1536,512]{1,0:T(8,128)(2,1)S(1)} %pad_maximum_fusion.1, bf16[896,512]{1,0:T(8,128)(2,1)} %copy-done.1, s32[]{:T(128)S(6)} %add.84), kind=kOutput, calls=%fused_computation.2 | convolution fusion | flops 201523200 | bytes 2097156 | tf_op jit(solution)/shard_map/dot_general | solution.py:52
  29.2 1.3 collective-permute-start.6
  30.4 1.5 %convolution_convert_fusion.1 = bf16[128,1536]{1,0:T(8,128)(2,1)S(1)} fusion(bf16[1536,512]{1,0:T(8,128)(2,1)S(1)} %pad_maximum_fusion.1, bf16[896,512]{1,0:T(8,128)(2,1)} %copy-done.1, s32[]{:T(128)S(6)} %add.85), kind=kOutput, calls=%fused_computation.1 | convolution fusion | flops 201523200 | bytes 2097156 | tf_op jit(solution)/shard_map/dot_general | solution.py:52
  32.0 1.6 %collective-permute-start.7 = (bf16[128,1536]{1,0:T(8,128)(2,1)S(1)}, bf16[128,1536]{1,0:T(8,128)(2,1)}, u32[]{:S(2)}, u32[]{:S(2)}) collective-permute-start(bf16[128,1536]{1,0:T(8,128)(2,1)S(1)} %convolution_convert_fusion.1), channel_id=1, source_target_pairs={{0,3},{1,0},{2,1},{3,2},{4,7},{5,4},{6,5},{7,6},{8,11},{9,8},{10,9... | collective-permute-start | bytes 1179656 | tf_op jit(solution)/shard_map/ppermute | solution.py:25
  33.6 1.5 %convolution_convert_fusion = bf16[128,1536]{1,0:T(8,128)(2,1)S(1)} fusion(bf16[1536,512]{1,0:T(8,128)(2,1)S(1)} %pad_maximum_fusion.1, bf16[896,512]{1,0:T(8,128)(2,1)} %copy-done.1, s32[]{:T(128)S(6)} %add.86), kind=kOutput, calls=%fused_computation | convolution fusion | flops 201523200 | bytes 2097156 | tf_op jit(solution)/shard_map/dot_general | solution.py:52
  35.1 1.6 %collective-permute-start.8 = (bf16[128,1536]{1,0:T(8,128)(2,1)S(1)}, bf16[128,1536]{1,0:T(8,128)(2,1)}, u32[]{:S(2)}, u32[]{:S(2)}) collective-permute-start(bf16[128,1536]{1,0:T(8,128)(2,1)S(1)} %convolution_convert_fusion), channel_id=1, source_target_pairs={{0,2},{1,3},{2,0},{3,1},{4,6},{5,7},{6,4},{7,5},{8,10},{9,11},{10,... | collective-permute-start | bytes 1179656 | tf_op jit(solution)/shard_map/ppermute | solution.py:25
  36.7 0.1 fusion.33
  36.8 2.3 %collective-permute-done.6 = bf16[128,1536]{1,0:T(8,128)(2,1)} collective-permute-done((bf16[128,1536]{1,0:T(8,128)(2,1)S(1)}, bf16[128,1536]{1,0:T(8,128)(2,1)}, u32[]{:S(2)}, u32[]{:S(2)}) %collective-permute-start.6) | collective-permute-done | bytes 393248 | tf_op jit(solution)/shard_map/ppermute | solution.py:25
  39.0 1.1 collective-permute-done.7
  40.1 8.0 %collective-permute-done.8 = bf16[128,1536]{1,0:T(8,128)(2,1)} collective-permute-done((bf16[128,1536]{1,0:T(8,128)(2,1)S(1)}, bf16[128,1536]{1,0:T(8,128)(2,1)}, u32[]{:S(2)}, u32[]{:S(2)}) %collective-permute-start.8) | collective-permute-done | bytes 393248 | tf_op jit(solution)/shard_map/ppermute | solution.py:25
  48.1 1.9 %fusion.3 = bf16[128,1536]{1,0:T(8,128)(2,1)S(1)} fusion(bf16[1536,512]{1,0:T(8,128)(2,1)S(1)} %pad_maximum_fusion.1, bf16[128,1536]{1,0:T(8,128)(2,1)} %collective-permute-done.8, bf16[128,1536]{1,0:T(8,128)(2,1)} %collective-permute-done.7, bf16[128,1536]{1,0:T(8,128)(2,1)} %collective-permute-done.6, bf16[896,512]{1,0:T(8,128)(2,1)} %copy-done.1, ...), kind=kOutput, calls=%fused_computation.7 | convolution fusion | flops 203096064 | bytes 3276804 | tf_op jit(solution)/shard_map/dot_general | solution.py:52
  50.1 5.6 %collective-permute-start.10 = (bf16[32,2048]{1,0:T(8,128)(2,1)S(1)}, bf16[32,2048]{1,0:T(8,128)(2,1)S(1)}, u32[]{:S(2)}, u32[]{:S(2)}) collective-permute-start(bf16[32,2048]{1,0:T(8,128)(2,1)S(1)} %get-tuple-element.39), channel_id=1, source_target_pairs={{0,12},{4,0},{8,4},{12,8},{1,13},{5,1},{9,5},{13,9},{2,14},{6,2},{... | collective-permute-start | bytes 393224 | tf_op jit(solution)/shard_map/ppermute | solution.py:25
  55.7 1.0 collective-permute-start.11
  56.7 2.3 %collective-permute-start.9 = (bf16[32,2048]{1,0:T(8,128)(2,1)S(1)}, bf16[32,2048]{1,0:T(8,128)(2,1)S(1)}, u32[]{:S(2)}, u32[]{:S(2)}) collective-permute-start(bf16[32,2048]{1,0:T(8,128)(2,1)S(1)} %get-tuple-element.37), channel_id=1, source_target_pairs={{0,4},{4,8},{8,12},{12,0},{1,5},{5,9},{9,13},{13,1},{2,6},{6,10},{... | collective-permute-start | bytes 393224 | tf_op jit(solution)/shard_map/ppermute | solution.py:25
  59.0 5.9 %collective-permute-done.11 = bf16[32,2048]{1,0:T(8,128)(2,1)S(1)} collective-permute-done((bf16[32,2048]{1,0:T(8,128)(2,1)S(1)}, bf16[32,2048]{1,0:T(8,128)(2,1)S(1)}, u32[]{:S(2)}, u32[]{:S(2)}) %collective-permute-start.11) | collective-permute-done | bytes 131104 | tf_op jit(solution)/shard_map/ppermute | solution.py:25
  64.8 0.8 collective-permute-done.9
  65.6 0.1 add_convert_fusion
  65.7 15.7 %all_gather.3 = bf16[128,2048]{1,0:T(8,128)(2,1)S(1)} all-gather(bf16[32,2048]{1,0:T(8,128)(2,1)S(1)} %add_convert_fusion), channel_id=1, replica_groups=mesh['x'=4,'zl'=2,'core'=2,'zh'=4,'y'=4] {'zh'}, dimensions={0}, use_global_device_ids=true | all-gather | bytes 655360 | tf_op jit(solution)/shard_map/all_gather | solution.py:84
  81.4 1.1 collective-permute-start.12
  82.4 1.4 collective-permute-start.13
  83.8 0.4 fusion.51
  84.3 7.3 %collective-permute-done.13 = bf16[128,2048]{1,0:T(8,128)(2,1)S(1)} collective-permute-done((bf16[128,2048]{1,0:T(8,128)(2,1)S(1)}, bf16[128,2048]{1,0:T(8,128)(2,1)S(1)}, u32[]{:S(2)}, u32[]{:S(2)}) %collective-permute-start.13) | collective-permute-done | bytes 524320 | tf_op jit(solution)/shard_map/ppermute | solution.py:25
  91.8 0.9 collective-permute-start.15
  92.6 0.7 collective-permute-start.16
  93.3 0.4 fusion.50
  93.8 0.4 fusion.49
  94.3 12.7 %collective-permute-start.14 = (f32[192,512]{1,0:T(8,128)S(1)}, f32[192,512]{1,0:T(8,128)S(1)}, u32[]{:S(2)}, u32[]{:S(2)}) collective-permute-start(f32[192,512]{1,0:T(8,128)S(1)} %pad_maximum_fusion.3), channel_id=1, source_target_pairs={{0,16},{16,0},{1,17},{17,1},{2,18},{18,2},{3,19},{19,3},{4,20},{20... | collective-permute-start | bytes 1179656 | tf_op jit(solution)/shard_map/ppermute | solution.py:21
  107.1 0.5 fusion.48
  107.6 5.1 %collective-permute-start.17 = (f32[64,512]{1,0:T(8,128)S(1)}, f32[64,512]{1,0:T(8,128)S(1)}, u32[]{:S(2)}, u32[]{:S(2)}) collective-permute-start(f32[64,512]{1,0:T(8,128)S(1)} %fusion.48), channel_id=1, source_target_pairs={{0,16},{16,0},{1,17},{17,1},{2,18},{18,2},{3,19},{19,3},{4,20},{20... | collective-permute-start | bytes 393224 | tf_op jit(solution)/shard_map/ppermute | solution.py:21
  112.8 0.1 maximum_add_fusion
  112.9 0.8 collective-permute-done.17
  113.7 0.5 constant_dynamic-update-slice_fusion.10
  114.3 1.2 collective-permute-start.18
  115.4 0.7 collective-permute-start.19
  116.1 5.8 %collective-permute-done.18 = bf16[256,512]{1,0:T(8,128)(2,1)S(1)} collective-permute-done((bf16[256,512]{1,0:T(8,128)(2,1)S(1)}, bf16[256,512]{1,0:T(8,128)(2,1)S(1)}, u32[]{:S(2)}, u32[]{:S(2)}) %collective-permute-start.18) | collective-permute-done | bytes 262176 | tf_op jit(solution)/shard_map/ppermute | solution.py:21
  121.9 2.1 %collective-permute-start.20 = (bf16[512,512]{1,0:T(8,128)(2,1)S(1)}, bf16[512,512]{1,0:T(8,128)(2,1)S(1)}, u32[]{:S(2)}, u32[]{:S(2)}) collective-permute-start(bf16[512,512]{1,0:T(8,128)(2,1)S(1)} %pad_maximum_fusion.2), channel_id=1, source_target_pairs={{0,192},{64,0},{128,64},{192,128},{1,193},{65,1},{129,65},{193,129... | collective-permute-start | bytes 1572872 | tf_op jit(solution)/shard_map/ppermute | solution.py:25
  124.0 0.1 collective-permute-done.19
  124.1 0.5 collective-permute-start.22
  124.7 5.8 %collective-permute-done.22 = bf16[256,512]{1,0:T(8,128)(2,1)S(1)} collective-permute-done((bf16[256,512]{1,0:T(8,128)(2,1)S(1)}, bf16[256,512]{1,0:T(8,128)(2,1)S(1)}, u32[]{:S(2)}, u32[]{:S(2)}) %collective-permute-start.22) | collective-permute-done | bytes 262176 | tf_op jit(solution)/shard_map/ppermute | solution.py:21
  130.4 3.8 %collective-permute-done.20 = bf16[512,512]{1,0:T(8,128)(2,1)S(1)} collective-permute-done((bf16[512,512]{1,0:T(8,128)(2,1)S(1)}, bf16[512,512]{1,0:T(8,128)(2,1)S(1)}, u32[]{:S(2)}, u32[]{:S(2)}) %collective-permute-start.20) | collective-permute-done | bytes 524320 | tf_op jit(solution)/shard_map/ppermute | solution.py:25
  134.2 3.0 %collective-permute-done.21 = bf16[512,512]{1,0:T(8,128)(2,1)S(1)} collective-permute-done((bf16[512,512]{1,0:T(8,128)(2,1)S(1)}, bf16[512,512]{1,0:T(8,128)(2,1)S(1)}, u32[]{:S(2)}, u32[]{:S(2)}) %collective-permute-start.21) | collective-permute-done | bytes 524320 | tf_op jit(solution)/shard_map/ppermute | solution.py:25
  137.3 0.6 fusion.6
  137.9 0.3 convolution_add_fusion
  138.2 2.5 %collective-permute-start.23 = (f32[256,512]{1,0:T(8,128)S(1)}, f32[256,512]{1,0:T(8,128)S(1)}, u32[]{:S(2)}, u32[]{:S(2)}) collective-permute-start(f32[256,512]{1,0:T(8,128)S(1)} %convolution_add_fusion), channel_id=1, source_target_pairs={{0,16},{16,0},{1,17},{17,1},{2,18},{18,2},{3,19},{19,3},{4,20},{20... | collective-permute-start | bytes 1572872 | tf_op jit(solution)/shard_map/ppermute | solution.py:21
  140.7 0.6 fusion.8
  141.3 0.9 collective-permute-done.23
  142.2 1.2 add_multiply_fusion
  (53 shorter events, 0.8 us)
Async XLA Ops:
  0.0 13.6 %collective-permute-start = (bf16[256,512]{1,0:T(8,128)(2,1)}, bf16[256,512]{1,0:T(8,128)(2,1)S(1)}, u32[]{:S(2)}, u32[]{:S(2)}) collective-permute-start(bf16[256,512]{1,0:T(8,128)(2,1)} %param.1), channel_id=1, source_target_pairs={{0,16},{16,0},{1,17},{17,1},{2,18},{18,2},{3,19},{19,3},{4,20},{20... | collective-permute-start | bytes 786440 | tf_op jit(solution)/shard_map/ppermute | solution.py:21
  3.2 8.1 %collective-permute-start.1 = (bf16[256,512]{1,0:T(8,128)(2,1)}, bf16[256,512]{1,0:T(8,128)(2,1)S(1)}, u32[]{:S(2)}, u32[]{:S(2)}) collective-permute-start(bf16[256,512]{1,0:T(8,128)(2,1)} %param.1), channel_id=1, source_target_pairs={{0,32},{32,0},{1,33},{33,1},{2,34},{34,2},{3,35},{35,3},{4,36},{36... | collective-permute-start | bytes 786440 | tf_op jit(solution)/shard_map/ppermute | solution.py:21
  3.2 17.7 %collective-permute-start.2 = (bf16[256,512]{1,0:T(8,128)(2,1)}, bf16[256,512]{1,0:T(8,128)(2,1)S(1)}, u32[]{:S(2)}, u32[]{:S(2)}) collective-permute-start(bf16[256,512]{1,0:T(8,128)(2,1)} %param.1), channel_id=1, source_target_pairs={{0,128},{64,192},{128,0},{192,64},{1,129},{65,193},{129,1},{193,65... | collective-permute-start | bytes 786440 | tf_op jit(solution)/shard_map/ppermute | solution.py:25
  11.4 2.3 %copy-start.2 = (bf16[256,512]{1,0:T(8,128)(2,1)}, bf16[256,512]{1,0:T(8,128)(2,1)S(1)}, u32[]{:S(2)}) copy-start(bf16[256,512]{1,0:T(8,128)(2,1)S(1)} %collective-permute-done.1) | copy-start | bytes 786436
  12.1 15.4 %collective-permute-start.3 = (bf16[512,512]{1,0:T(8,128)(2,1)}, bf16[512,512]{1,0:T(8,128)(2,1)S(1)}, u32[]{:S(2)}, u32[]{:S(2)}) collective-permute-start(bf16[512,512]{1,0:T(8,128)(2,1)} %constant_dynamic-update-slice_fusion), channel_id=1, source_target_pairs={{0,192},{64,0},{128,64},{192,128},{1,193},{65,1},{129,65},{193,129... | collective-permute-start | bytes 1572872 | tf_op jit(solution)/shard_map/ppermute | solution.py:25
  13.2 14.3 %collective-permute-start.4 = (bf16[512,512]{1,0:T(8,128)(2,1)}, bf16[512,512]{1,0:T(8,128)(2,1)S(1)}, u32[]{:S(2)}, u32[]{:S(2)}) collective-permute-start(bf16[512,512]{1,0:T(8,128)(2,1)} %constant_dynamic-update-slice_fusion), channel_id=1, source_target_pairs={{0,64},{64,128},{128,192},{192,0},{1,65},{65,129},{129,193},{193,1... | collective-permute-start | bytes 1572872 | tf_op jit(solution)/shard_map/ppermute | solution.py:25
  17.2 19.5 %all-to-all-start = ((bf16[4,128,512]{2,1,0:T(8,128)(2,1)}), bf16[4,128,512]{2,1,0:T(8,128)(2,1)S(1)}, u32[]{:S(2)}, u32[]{:S(2)}) async-start(bf16[4,128,512]{2,1,0:T(8,128)(2,1)} %bitcast), calls=%async_computation | async-start | bytes 1048576 | tf_op jit(solution)/shard_map/all_to_all | solution.py:77
  20.9 6.6 %collective-permute-start.5 = (bf16[256,512]{1,0:T(8,128)(2,1)S(1)}, bf16[256,512]{1,0:T(8,128)(2,1)S(1)}, u32[]{:S(2)}, u32[]{:S(2)}) collective-permute-start(bf16[256,512]{1,0:T(8,128)(2,1)S(1)} %collective-permute-done.2), channel_id=1, source_target_pairs={{0,32},{32,0},{1,33},{33,1},{2,34},{34,2},{3,35},{35,3},{4,36},{36... | collective-permute-start | bytes 786440 | tf_op jit(solution)/shard_map/ppermute | solution.py:21
  22.4 5.1 %copy-start.1 = (bf16[896,512]{1,0:T(8,128)(2,1)}, bf16[896,512]{1,0:T(8,128)(2,1)S(1)}, u32[]{:S(2)}) copy-start(bf16[896,512]{1,0:T(8,128)(2,1)S(1)} %constant_dynamic-update-slice_fusion.2) | copy-start | bytes 2752516
  29.2 9.8 %collective-permute-start.6 = (bf16[128,1536]{1,0:T(8,128)(2,1)S(1)}, bf16[128,1536]{1,0:T(8,128)(2,1)}, u32[]{:S(2)}, u32[]{:S(2)}) collective-permute-start(bf16[128,1536]{1,0:T(8,128)(2,1)S(1)} %convolution_convert_fusion.2), channel_id=1, source_target_pairs={{0,1},{1,2},{2,3},{3,0},{4,5},{5,6},{6,7},{7,4},{8,9},{9,10},{10,1... | collective-permute-start | bytes 1179656 | tf_op jit(solution)/shard_map/ppermute | solution.py:25
  32.0 8.1 %collective-permute-start.7 = (bf16[128,1536]{1,0:T(8,128)(2,1)S(1)}, bf16[128,1536]{1,0:T(8,128)(2,1)}, u32[]{:S(2)}, u32[]{:S(2)}) collective-permute-start(bf16[128,1536]{1,0:T(8,128)(2,1)S(1)} %convolution_convert_fusion.1), channel_id=1, source_target_pairs={{0,3},{1,0},{2,1},{3,2},{4,7},{5,4},{6,5},{7,6},{8,11},{9,8},{10,9... | collective-permute-start | bytes 1179656 | tf_op jit(solution)/shard_map/ppermute | solution.py:25
  35.1 12.9 %collective-permute-start.8 = (bf16[128,1536]{1,0:T(8,128)(2,1)S(1)}, bf16[128,1536]{1,0:T(8,128)(2,1)}, u32[]{:S(2)}, u32[]{:S(2)}) collective-permute-start(bf16[128,1536]{1,0:T(8,128)(2,1)S(1)} %convolution_convert_fusion), channel_id=1, source_target_pairs={{0,2},{1,3},{2,0},{3,1},{4,6},{5,7},{6,4},{7,5},{8,10},{9,11},{10,... | collective-permute-start | bytes 1179656 | tf_op jit(solution)/shard_map/ppermute | solution.py:25
  50.0 33.8 %copy-start = (bf16[256,512]{1,0:T(8,128)(2,1)S(1)}, bf16[256,512]{1,0:T(8,128)(2,1)}, u32[]{:S(2)}) copy-start(bf16[256,512]{1,0:T(8,128)(2,1)} %param.1) | copy-start | bytes 786436
  50.0 33.8 %copy-start.3 = (bf16[256,512]{1,0:T(8,128)(2,1)S(1)}, bf16[256,512]{1,0:T(8,128)(2,1)}, u32[]{:S(2)}) copy-start(bf16[256,512]{1,0:T(8,128)(2,1)} %copy-done.2) | copy-start | bytes 786436
  50.1 8.9 %collective-permute-start.10 = (bf16[32,2048]{1,0:T(8,128)(2,1)S(1)}, bf16[32,2048]{1,0:T(8,128)(2,1)S(1)}, u32[]{:S(2)}, u32[]{:S(2)}) collective-permute-start(bf16[32,2048]{1,0:T(8,128)(2,1)S(1)} %get-tuple-element.39), channel_id=1, source_target_pairs={{0,12},{4,0},{8,4},{12,8},{1,13},{5,1},{9,5},{13,9},{2,14},{6,2},{... | collective-permute-start | bytes 393224 | tf_op jit(solution)/shard_map/ppermute | solution.py:25
  55.7 9.1 %collective-permute-start.11 = (bf16[32,2048]{1,0:T(8,128)(2,1)S(1)}, bf16[32,2048]{1,0:T(8,128)(2,1)S(1)}, u32[]{:S(2)}, u32[]{:S(2)}) collective-permute-start(bf16[32,2048]{1,0:T(8,128)(2,1)S(1)} %get-tuple-element.38), channel_id=1, source_target_pairs={{0,8},{4,12},{8,0},{12,4},{1,9},{5,13},{9,1},{13,5},{2,10},{6,14},... | collective-permute-start | bytes 393224 | tf_op jit(solution)/shard_map/ppermute | solution.py:25
  56.7 8.9 %collective-permute-start.9 = (bf16[32,2048]{1,0:T(8,128)(2,1)S(1)}, bf16[32,2048]{1,0:T(8,128)(2,1)S(1)}, u32[]{:S(2)}, u32[]{:S(2)}) collective-permute-start(bf16[32,2048]{1,0:T(8,128)(2,1)S(1)} %get-tuple-element.37), channel_id=1, source_target_pairs={{0,4},{4,8},{8,12},{12,0},{1,5},{5,9},{9,13},{13,1},{2,6},{6,10},{... | collective-permute-start | bytes 393224 | tf_op jit(solution)/shard_map/ppermute | solution.py:25
  81.4 10.3 %collective-permute-start.12 = (bf16[128,2048]{1,0:T(8,128)(2,1)S(1)}, bf16[128,2048]{1,0:T(8,128)(2,1)S(1)}, u32[]{:S(2)}, u32[]{:S(2)}) collective-permute-start(bf16[128,2048]{1,0:T(8,128)(2,1)S(1)} %all_gather.3), channel_id=1, source_target_pairs={{0,3},{1,0},{2,1},{3,2},{4,7},{5,4},{6,5},{7,6},{8,11},{9,8},{10,9... | collective-permute-start | bytes 1572872 | tf_op jit(solution)/shard_map/ppermute | solution.py:25
  82.4 9.2 %collective-permute-start.13 = (bf16[128,2048]{1,0:T(8,128)(2,1)S(1)}, bf16[128,2048]{1,0:T(8,128)(2,1)S(1)}, u32[]{:S(2)}, u32[]{:S(2)}) collective-permute-start(bf16[128,2048]{1,0:T(8,128)(2,1)S(1)} %all_gather.3), channel_id=1, source_target_pairs={{0,1},{1,2},{2,3},{3,0},{4,5},{5,6},{6,7},{7,4},{8,9},{9,10},{10,1... | collective-permute-start | bytes 1572872 | tf_op jit(solution)/shard_map/ppermute | solution.py:25
  91.8 15.2 %collective-permute-start.15 = (bf16[64,2048]{1,0:T(8,128)(2,1)S(1)}, bf16[64,2048]{1,0:T(8,128)(2,1)S(1)}, u32[]{:S(2)}, u32[]{:S(2)}) collective-permute-start(bf16[64,2048]{1,0:T(8,128)(2,1)S(1)} %get-tuple-element.14), channel_id=1, source_target_pairs={{0,3},{1,0},{2,1},{3,2},{4,7},{5,4},{6,5},{7,6},{8,11},{9,8},{10,9... | collective-permute-start | bytes 786440 | tf_op jit(solution)/shard_map/ppermute | solution.py:25
  92.6 14.4 %collective-permute-start.16 = (bf16[64,2048]{1,0:T(8,128)(2,1)S(1)}, bf16[64,2048]{1,0:T(8,128)(2,1)S(1)}, u32[]{:S(2)}, u32[]{:S(2)}) collective-permute-start(bf16[64,2048]{1,0:T(8,128)(2,1)S(1)} %slice.113), channel_id=1, source_target_pairs={{0,1},{1,2},{2,3},{3,0},{4,5},{5,6},{6,7},{7,4},{8,9},{9,10},{10,1... | collective-permute-start | bytes 786440 | tf_op jit(solution)/shard_map/ppermute | solution.py:25
  94.3 18.5 %collective-permute-start.14 = (f32[192,512]{1,0:T(8,128)S(1)}, f32[192,512]{1,0:T(8,128)S(1)}, u32[]{:S(2)}, u32[]{:S(2)}) collective-permute-start(f32[192,512]{1,0:T(8,128)S(1)} %pad_maximum_fusion.3), channel_id=1, source_target_pairs={{0,16},{16,0},{1,17},{17,1},{2,18},{18,2},{3,19},{19,3},{4,20},{20... | collective-permute-start | bytes 1179656 | tf_op jit(solution)/shard_map/ppermute | solution.py:21
  107.6 6.1 %collective-permute-start.17 = (f32[64,512]{1,0:T(8,128)S(1)}, f32[64,512]{1,0:T(8,128)S(1)}, u32[]{:S(2)}, u32[]{:S(2)}) collective-permute-start(f32[64,512]{1,0:T(8,128)S(1)} %fusion.48), channel_id=1, source_target_pairs={{0,16},{16,0},{1,17},{17,1},{2,18},{18,2},{3,19},{19,3},{4,20},{20... | collective-permute-start | bytes 393224 | tf_op jit(solution)/shard_map/ppermute | solution.py:21
  114.3 7.6 %collective-permute-start.18 = (bf16[256,512]{1,0:T(8,128)(2,1)S(1)}, bf16[256,512]{1,0:T(8,128)(2,1)S(1)}, u32[]{:S(2)}, u32[]{:S(2)}) collective-permute-start(bf16[256,512]{1,0:T(8,128)(2,1)S(1)} %dynamic-slice_convert_fusion), channel_id=1, source_target_pairs={{0,32},{32,0},{1,33},{33,1},{2,34},{34,2},{3,35},{35,3},{4,36},{36... | collective-permute-start | bytes 786440 | tf_op jit(solution)/shard_map/ppermute | solution.py:21
  115.4 8.7 %collective-permute-start.19 = (bf16[256,512]{1,0:T(8,128)(2,1)S(1)}, bf16[256,512]{1,0:T(8,128)(2,1)S(1)}, u32[]{:S(2)}, u32[]{:S(2)}) collective-permute-start(bf16[256,512]{1,0:T(8,128)(2,1)S(1)} %dynamic-slice_convert_fusion), channel_id=1, source_target_pairs={{0,128},{64,192},{128,0},{192,64},{1,129},{65,193},{129,1},{193,65... | collective-permute-start | bytes 786440 | tf_op jit(solution)/shard_map/ppermute | solution.py:25
  121.9 12.3 %collective-permute-start.20 = (bf16[512,512]{1,0:T(8,128)(2,1)S(1)}, bf16[512,512]{1,0:T(8,128)(2,1)S(1)}, u32[]{:S(2)}, u32[]{:S(2)}) collective-permute-start(bf16[512,512]{1,0:T(8,128)(2,1)S(1)} %pad_maximum_fusion.2), channel_id=1, source_target_pairs={{0,192},{64,0},{128,64},{192,128},{1,193},{65,1},{129,65},{193,129... | collective-permute-start | bytes 1572872 | tf_op jit(solution)/shard_map/ppermute | solution.py:25
  124.0 13.2 %collective-permute-start.21 = (bf16[512,512]{1,0:T(8,128)(2,1)S(1)}, bf16[512,512]{1,0:T(8,128)(2,1)S(1)}, u32[]{:S(2)}, u32[]{:S(2)}) collective-permute-start(bf16[512,512]{1,0:T(8,128)(2,1)S(1)} %pad_maximum_fusion.2), channel_id=1, source_target_pairs={{0,64},{64,128},{128,192},{192,0},{1,65},{65,129},{129,193},{193,1... | collective-permute-start | bytes 1572872 | tf_op jit(solution)/shard_map/ppermute | solution.py:25
  124.1 6.3 %collective-permute-start.22 = (bf16[256,512]{1,0:T(8,128)(2,1)S(1)}, bf16[256,512]{1,0:T(8,128)(2,1)S(1)}, u32[]{:S(2)}, u32[]{:S(2)}) collective-permute-start(bf16[256,512]{1,0:T(8,128)(2,1)S(1)} %collective-permute-done.19), channel_id=1, source_target_pairs={{0,32},{32,0},{1,33},{33,1},{2,34},{34,2},{3,35},{35,3},{4,36},{36... | collective-permute-start | bytes 786440 | tf_op jit(solution)/shard_map/ppermute | solution.py:21
  138.2 4.0 %collective-permute-start.23 = (f32[256,512]{1,0:T(8,128)S(1)}, f32[256,512]{1,0:T(8,128)S(1)}, u32[]{:S(2)}, u32[]{:S(2)}) collective-permute-start(f32[256,512]{1,0:T(8,128)S(1)} %convolution_add_fusion), channel_id=1, source_target_pairs={{0,16},{16,0},{1,17},{17,1},{2,18},{18,2},{3,19},{19,3},{4,20},{20... | collective-permute-start | bytes 1572872 | tf_op jit(solution)/shard_map/ppermute | solution.py:21

commit v14 on v13

--- a/solution.py
+++ b/solution.py
@@ -52,11 +52,13 @@
     return lax.dot_general(a, b, (dims, ((), ())), preferred_element_type=F32)
 
 
-def blocks_of(block):
+def pair_of(block):
     far = fetch(block, "x", 2)
-    partner = swap(block, "zl")
-    pair = jnp.concatenate([block, partner], axis=0)
-    return pair, [far, fetch(pair, "x", 1), fetch(pair, "x", 3), swap(far, "zl")]
+    return jnp.concatenate([block, swap(block, "zl")], axis=0), far
+
+
+def late_blocks(pair, far):
+    return [far, fetch(pair, "x", 1), fetch(pair, "x", 3), swap(far, "zl")]
 
 
 def core_sum(products):
@@ -69,11 +71,13 @@
     y, zh = lax.axis_index("y"), lax.axis_index("zh")
     back = lax.rem(4 - y, 4)
     other = swap(iterate, "core")
-    pair, late = blocks_of(iterate)
+    pair, far = pair_of(iterate)
 
     own = [jnp.concatenate(rows, axis=0) for rows in zip(chunks(iterate), chunks(other))]
     own = [window(chunks(rows), zh, 4) for rows in own]
     pieces = matmul(jnp.concatenate(own, axis=0), pair, ((1,), (1,))).astype(BF)
+    pieces, far = lax.optimization_barrier((pieces, far))
+    late = late_blocks(pair, far)
     first = add(lax.all_to_all(pieces.reshape(4, 128, 512), "y", 0, 0))
     panel = lax.optimization_barrier(jnp.concatenate(late, axis=0))
     pieces = [matmul(rows, panel, ((1,), (1,))).astype(BF) for rows in chunks(window(own, y, 4))]
@@ -93,8 +97,8 @@
     second = core_sum([(product(far[0]), product(far[1]))])
     inner = window([first[:64], first[64:128], second, first[128:]], back, 4)
 
-    pair, late = blocks_of(inner.astype(BF))
-    pair, *late = lax.optimization_barrier([pair, *late])
+    pair, last = pair_of(inner.astype(BF))
+    pair, *late = lax.optimization_barrier([pair, *late_blocks(pair, last)])
     panels = pair, jnp.concatenate(late, axis=0)
     gram = [(near[:64], near[64:]), (after[:64], after[64:]), far, (before[:64], before[64:])]
     mixed = []

time: 144 us -> 144 us (level)
  starting transfers between devices: 54.4 us -> 52.2 us
  waiting for transfers between devices: 53.4 us -> 55.5 us
    ppermute x16, waiting for transfers between devices: 32.2 us -> 37.2 us  [send(): lax.ppermute(array, axis, [(i, (i + k) % 4) for i in range(4)])]
    ppermute x8, waiting for transfers between devices: 21.3 us -> 18.3 us  [swap(): return lax.ppermute(array, axis, [(0, 1), (1, 0)])]
    ppermute x8, starting transfers between devices: 26.5 us -> 24.9 us  [swap(): return lax.ppermute(array, axis, [(0, 1), (1, 0)])]
  transfers between devices with their start and end apart: 25 -> 25, of which waited for: 15 -> 16; matrix products, arithmetic and copies ran while one was open for 10% -> 11% of each run, Pallas kernels for 0% -> 0%
where the time goes in v14:
time: 144 us
  waiting for transfers between devices  55.5 us (39%)
  starting transfers between devices  52.2 us (36%)
  blocking collectives  15.6 us (11%)
  matrix products  13.8 us (10%)
  local copies, waits for them, and re-layouts  4.04 us (3%)
  other arithmetic  2.54 us (2%)
    ppermute x16, waiting for transfers between devices, send(): lax.ppermute(array, axis, [(i, (i + k) % 4) for i in range(4)])  37.2 us
    ppermute x8, starting transfers between devices, swap(): return lax.ppermute(array, axis, [(0, 1), (1, 0)])  24.9 us
    ppermute x16, starting transfers between devices, send(): lax.ppermute(array, axis, [(i, (i + k) % 4) for i in range(4)])  23 us
    ppermute x8, waiting for transfers between devices, swap(): return lax.ppermute(array, axis, [(0, 1), (1, 0)])  18.3 us
    all_gather x1, blocking collectives, per_device(): near = lax.all_gather(part, 'zh', axis=0, tiled=True)  15.6 us
    dot_general x14, matrix products, matmul(): return lax.dot_general(a, b, (dims, ((), ())), preferred_element_type=F32)  13.8 us
    all_to_all x1, starting transfers between devices, per_device(): first = add(lax.all_to_all(pieces.reshape(4, 128, 512), 'y', 0, 0))  4.2 us
  transfers between devices with their start and end apart: 25, of which 16 were waited for; matrix products, arithmetic and copies ran while one was open for 11% of the time, Pallas kernels for 0%

profile of v14, /device:TPU:1, one launch (start us, length us, event | category | flops | bytes accessed | tf_op | source)
XLA Modules:
  0.0 144.1 jit_solution(9533038960894401828)
XLA Ops:
  0.0 3.2 %collective-permute-start = (bf16[256,512]{1,0:T(8,128)(2,1)}, bf16[256,512]{1,0:T(8,128)(2,1)S(1)}, u32[]{:S(2)}, u32[]{:S(2)}) collective-permute-start(bf16[256,512]{1,0:T(8,128)(2,1)} %param.1), channel_id=1, source_target_pairs={{0,16},{16,0},{1,17},{17,1},{2,18},{18,2},{3,19},{19,3},{4,20},{20... | collective-permute-start | bytes 786440 | tf_op jit(solution)/shard_map/ppermute | solution.py:21
  3.2 2.6 %collective-permute-start.2 = (bf16[256,512]{1,0:T(8,128)(2,1)}, bf16[256,512]{1,0:T(8,128)(2,1)S(1)}, u32[]{:S(2)}, u32[]{:S(2)}) collective-permute-start(bf16[256,512]{1,0:T(8,128)(2,1)} %param.1), channel_id=1, source_target_pairs={{0,128},{64,192},{128,0},{192,64},{1,129},{65,193},{129,1},{193,65... | collective-permute-start | bytes 786440 | tf_op jit(solution)/shard_map/ppermute | solution.py:25
  5.9 1.0 fusion.60
  6.9 1.7 %constant_dynamic-update-slice_fusion.1 = bf16[512,512]{1,0:T(8,128)(2,1)} fusion(bf16[256,512]{1,0:T(8,128)(2,1)} %param.1), kind=kLoop, calls=%fused_computation.90 | loop fusion | bytes 524288
  8.5 2.9 %collective-permute-done.1 = bf16[256,512]{1,0:T(8,128)(2,1)S(1)} collective-permute-done((bf16[256,512]{1,0:T(8,128)(2,1)}, bf16[256,512]{1,0:T(8,128)(2,1)S(1)}, u32[]{:S(2)}, u32[]{:S(2)}) %collective-permute-start.1) | collective-permute-done | bytes 262176 | tf_op jit(solution)/shard_map/ppermute | solution.py:21
  11.4 0.8 constant_dynamic-update-slice_fusion
  12.1 1.0 collective-permute-start.3
  13.2 0.5 collective-permute-start.4
  13.7 0.3 constant_dynamic-update-slice_fusion.8
  14.0 0.3 constant_dynamic-update-slice_fusion.7
  14.3 0.3 constant_dynamic-update-slice_fusion.6
  14.6 0.3 constant_dynamic-update-slice_fusion.5
  14.9 2.3 %convolution_convert_fusion.4 = bf16[512,512]{1,0:T(8,128)(2,1)} fusion(bf16[512,512]{1,0:T(8,128)(2,1)} %constant_dynamic-update-slice_fusion, bf16[128,512]{1,0:T(8,128)(2,1)S(1)} %get-tuple-element.28, bf16[128,512]{1,0:T(8,128)(2,1)S(1)} %get-tuple-element.30, bf16[128,512]{1,0:T(8,128)(2,1)S(1)} %get-tuple-element.32, ...), kind=kOutput, calls=%fused_computation.10 | convolution fusion | flops 270794752 | bytes 1572864 | tf_op jit(solution)/shard_map/dot_general | solution.py:52
  17.2 0.9 collective-permute-start.5
  18.1 4.2 %all-to-all-start = ((bf16[4,128,512]{2,1,0:T(8,128)(2,1)}), bf16[4,128,512]{2,1,0:T(8,128)(2,1)S(1)}, u32[]{:S(2)}, u32[]{:S(2)}) async-start(bf16[4,128,512]{2,1,0:T(8,128)(2,1)} %bitcast), calls=%async_computation | async-start | bytes 1048576 | tf_op jit(solution)/shard_map/all_to_all | solution.py:81
  22.4 1.4 collective-permute-done.5
  23.8 1.4 collective-permute-done.3
  25.1 1.9 %collective-permute-done.4 = bf16[512,512]{1,0:T(8,128)(2,1)S(1)} collective-permute-done((bf16[512,512]{1,0:T(8,128)(2,1)}, bf16[512,512]{1,0:T(8,128)(2,1)S(1)}, u32[]{:S(2)}, u32[]{:S(2)}) %collective-permute-start.4) | collective-permute-done | bytes 524320 | tf_op jit(solution)/shard_map/ppermute | solution.py:25
  27.0 1.1 pad_maximum_fusion.1
  28.1 1.5 %convolution_convert_fusion.2 = bf16[128,1536]{1,0:T(8,128)(2,1)S(1)} fusion(bf16[1536,512]{1,0:T(8,128)(2,1)S(1)} %pad_maximum_fusion.1, bf16[896,512]{1,0:T(8,128)(2,1)} %copy-done.1, s32[]{:T(128)S(6)} %add.84), kind=kOutput, calls=%fused_computation.2 | convolution fusion | flops 201523200 | bytes 2097156 | tf_op jit(solution)/shard_map/dot_general | solution.py:52
  29.7 1.4 collective-permute-start.6
  31.0 1.5 %convolution_convert_fusion.1 = bf16[128,1536]{1,0:T(8,128)(2,1)S(1)} fusion(bf16[1536,512]{1,0:T(8,128)(2,1)S(1)} %pad_maximum_fusion.1, bf16[896,512]{1,0:T(8,128)(2,1)} %copy-done.1, s32[]{:T(128)S(6)} %add.85), kind=kOutput, calls=%fused_computation.1 | convolution fusion | flops 201523200 | bytes 2097156 | tf_op jit(solution)/shard_map/dot_general | solution.py:52
  32.6 1.5 %collective-permute-start.7 = (bf16[128,1536]{1,0:T(8,128)(2,1)S(1)}, bf16[128,1536]{1,0:T(8,128)(2,1)}, u32[]{:S(2)}, u32[]{:S(2)}) collective-permute-start(bf16[128,1536]{1,0:T(8,128)(2,1)S(1)} %convolution_convert_fusion.1), channel_id=1, source_target_pairs={{0,3},{1,0},{2,1},{3,2},{4,7},{5,4},{6,5},{7,6},{8,11},{9,8},{10,9... | collective-permute-start | bytes 1179656 | tf_op jit(solution)/shard_map/ppermute | solution.py:25
  34.1 1.5 %convolution_convert_fusion = bf16[128,1536]{1,0:T(8,128)(2,1)S(1)} fusion(bf16[1536,512]{1,0:T(8,128)(2,1)S(1)} %pad_maximum_fusion.1, bf16[896,512]{1,0:T(8,128)(2,1)} %copy-done.1, s32[]{:T(128)S(6)} %add.86), kind=kOutput, calls=%fused_computation | convolution fusion | flops 201523200 | bytes 2097156 | tf_op jit(solution)/shard_map/dot_general | solution.py:52
  35.7 1.7 %collective-permute-start.8 = (bf16[128,1536]{1,0:T(8,128)(2,1)S(1)}, bf16[128,1536]{1,0:T(8,128)(2,1)}, u32[]{:S(2)}, u32[]{:S(2)}) collective-permute-start(bf16[128,1536]{1,0:T(8,128)(2,1)S(1)} %convolution_convert_fusion), channel_id=1, source_target_pairs={{0,2},{1,3},{2,0},{3,1},{4,6},{5,7},{6,4},{7,5},{8,10},{9,11},{10,... | collective-permute-start | bytes 1179656 | tf_op jit(solution)/shard_map/ppermute | solution.py:25
  37.5 2.5 %collective-permute-done.6 = bf16[128,1536]{1,0:T(8,128)(2,1)} collective-permute-done((bf16[128,1536]{1,0:T(8,128)(2,1)S(1)}, bf16[128,1536]{1,0:T(8,128)(2,1)}, u32[]{:S(2)}, u32[]{:S(2)}) %collective-permute-start.6) | collective-permute-done | bytes 393248 | tf_op jit(solution)/shard_map/ppermute | solution.py:25
  39.9 1.3 collective-permute-done.7
  41.2 8.2 %collective-permute-done.8 = bf16[128,1536]{1,0:T(8,128)(2,1)} collective-permute-done((bf16[128,1536]{1,0:T(8,128)(2,1)S(1)}, bf16[128,1536]{1,0:T(8,128)(2,1)}, u32[]{:S(2)}, u32[]{:S(2)}) %collective-permute-start.8) | collective-permute-done | bytes 393248 | tf_op jit(solution)/shard_map/ppermute | solution.py:25
  49.5 1.9 %fusion.3 = bf16[128,1536]{1,0:T(8,128)(2,1)S(1)} fusion(bf16[1536,512]{1,0:T(8,128)(2,1)S(1)} %pad_maximum_fusion.1, bf16[128,1536]{1,0:T(8,128)(2,1)} %collective-permute-done.8, bf16[128,1536]{1,0:T(8,128)(2,1)} %collective-permute-done.7, bf16[128,1536]{1,0:T(8,128)(2,1)} %collective-permute-done.6, bf16[896,512]{1,0:T(8,128)(2,1)} %copy-done.1, ...), kind=kOutput, calls=%fused_computation.7 | convolution fusion | flops 203096064 | bytes 3276804 | tf_op jit(solution)/shard_map/dot_general | solution.py:52
  51.5 5.6 %collective-permute-start.10 = (bf16[32,2048]{1,0:T(8,128)(2,1)S(1)}, bf16[32,2048]{1,0:T(8,128)(2,1)S(1)}, u32[]{:S(2)}, u32[]{:S(2)}) collective-permute-start(bf16[32,2048]{1,0:T(8,128)(2,1)S(1)} %get-tuple-element.43), channel_id=1, source_target_pairs={{0,12},{4,0},{8,4},{12,8},{1,13},{5,1},{9,5},{13,9},{2,14},{6,2},{... | collective-permute-start | bytes 393224 | tf_op jit(solution)/shard_map/ppermute | solution.py:25
  57.1 1.0 collective-permute-start.11
  58.1 2.3 %collective-permute-start.9 = (bf16[32,2048]{1,0:T(8,128)(2,1)S(1)}, bf16[32,2048]{1,0:T(8,128)(2,1)S(1)}, u32[]{:S(2)}, u32[]{:S(2)}) collective-permute-start(bf16[32,2048]{1,0:T(8,128)(2,1)S(1)} %get-tuple-element.41), channel_id=1, source_target_pairs={{0,4},{4,8},{8,12},{12,0},{1,5},{5,9},{9,13},{13,1},{2,6},{6,10},{... | collective-permute-start | bytes 393224 | tf_op jit(solution)/shard_map/ppermute | solution.py:25
  60.4 5.8 %collective-permute-done.11 = bf16[32,2048]{1,0:T(8,128)(2,1)S(1)} collective-permute-done((bf16[32,2048]{1,0:T(8,128)(2,1)S(1)}, bf16[32,2048]{1,0:T(8,128)(2,1)S(1)}, u32[]{:S(2)}, u32[]{:S(2)}) %collective-permute-start.11) | collective-permute-done | bytes 131104 | tf_op jit(solution)/shard_map/ppermute | solution.py:25
  66.2 1.5 %collective-permute-done.9 = bf16[32,2048]{1,0:T(8,128)(2,1)S(1)} collective-permute-done((bf16[32,2048]{1,0:T(8,128)(2,1)S(1)}, bf16[32,2048]{1,0:T(8,128)(2,1)S(1)}, u32[]{:S(2)}, u32[]{:S(2)}) %collective-permute-start.9) | collective-permute-done | bytes 131104 | tf_op jit(solution)/shard_map/ppermute | solution.py:25
  67.7 0.1 add_convert_fusion
  67.8 15.6 %all_gather.3 = bf16[128,2048]{1,0:T(8,128)(2,1)S(1)} all-gather(bf16[32,2048]{1,0:T(8,128)(2,1)S(1)} %add_convert_fusion), channel_id=1, replica_groups=mesh['x'=4,'zl'=2,'core'=2,'zh'=4,'y'=4] {'zh'}, dimensions={0}, use_global_device_ids=true | all-gather | bytes 655360 | tf_op jit(solution)/shard_map/all_gather | solution.py:88
  83.5 2.0 %collective-permute-start.12 = (bf16[128,2048]{1,0:T(8,128)(2,1)S(1)}, bf16[128,2048]{1,0:T(8,128)(2,1)S(1)}, u32[]{:S(2)}, u32[]{:S(2)}) collective-permute-start(bf16[128,2048]{1,0:T(8,128)(2,1)S(1)} %all_gather.3), channel_id=1, source_target_pairs={{0,3},{1,0},{2,1},{3,2},{4,7},{5,4},{6,5},{7,6},{8,11},{9,8},{10,9... | collective-permute-start | bytes 1572872 | tf_op jit(solution)/shard_map/ppermute | solution.py:25
  85.4 0.3 collective-permute-start.13
  85.7 0.4 fusion.51
  86.2 8.5 %collective-permute-done.13 = bf16[128,2048]{1,0:T(8,128)(2,1)S(1)} collective-permute-done((bf16[128,2048]{1,0:T(8,128)(2,1)S(1)}, bf16[128,2048]{1,0:T(8,128)(2,1)S(1)}, u32[]{:S(2)}, u32[]{:S(2)}) %collective-permute-start.13) | collective-permute-done | bytes 524320 | tf_op jit(solution)/shard_map/ppermute | solution.py:25
  94.8 0.1 collective-permute-start.15
  94.9 1.5 %collective-permute-start.16 = (bf16[64,2048]{1,0:T(8,128)(2,1)S(1)}, bf16[64,2048]{1,0:T(8,128)(2,1)S(1)}, u32[]{:S(2)}, u32[]{:S(2)}) collective-permute-start(bf16[64,2048]{1,0:T(8,128)(2,1)S(1)} %slice.113), channel_id=1, source_target_pairs={{0,1},{1,2},{2,3},{3,0},{4,5},{5,6},{6,7},{7,4},{8,9},{9,10},{10,1... | collective-permute-start | bytes 786440 | tf_op jit(solution)/shard_map/ppermute | solution.py:25
  96.3 0.4 fusion.50
  96.8 0.4 fusion.49
  97.3 12.8 %collective-permute-start.14 = (f32[192,512]{1,0:T(8,128)S(1)}, f32[192,512]{1,0:T(8,128)S(1)}, u32[]{:S(2)}, u32[]{:S(2)}) collective-permute-start(f32[192,512]{1,0:T(8,128)S(1)} %pad_maximum_fusion.3), channel_id=1, source_target_pairs={{0,16},{16,0},{1,17},{17,1},{2,18},{18,2},{3,19},{19,3},{4,20},{20... | collective-permute-start | bytes 1179656 | tf_op jit(solution)/shard_map/ppermute | solution.py:21
  110.2 0.5 fusion.48
  110.7 4.6 %collective-permute-start.17 = (f32[64,512]{1,0:T(8,128)S(1)}, f32[64,512]{1,0:T(8,128)S(1)}, u32[]{:S(2)}, u32[]{:S(2)}) collective-permute-start(f32[64,512]{1,0:T(8,128)S(1)} %fusion.48), channel_id=1, source_target_pairs={{0,16},{16,0},{1,17},{17,1},{2,18},{18,2},{3,19},{19,3},{4,20},{20... | collective-permute-start | bytes 393224 | tf_op jit(solution)/shard_map/ppermute | solution.py:21
  115.5 0.8 collective-permute-done.17
  116.3 0.5 constant_dynamic-update-slice_fusion.10
  116.9 0.1 collective-permute-start.18
  117.0 0.1 collective-permute-start.19
  117.1 7.4 %collective-permute-done.18 = bf16[256,512]{1,0:T(8,128)(2,1)S(1)} collective-permute-done((bf16[256,512]{1,0:T(8,128)(2,1)S(1)}, bf16[256,512]{1,0:T(8,128)(2,1)S(1)}, u32[]{:S(2)}, u32[]{:S(2)}) %collective-permute-start.18) | collective-permute-done | bytes 262176 | tf_op jit(solution)/shard_map/ppermute | solution.py:21
  124.6 0.1 collective-permute-start.20
  124.7 1.5 %collective-permute-start.21 = (bf16[512,512]{1,0:T(8,128)(2,1)S(1)}, bf16[512,512]{1,0:T(8,128)(2,1)S(1)}, u32[]{:S(2)}, u32[]{:S(2)}) collective-permute-start(bf16[512,512]{1,0:T(8,128)(2,1)S(1)} %pad_maximum_fusion.2), channel_id=1, source_target_pairs={{0,64},{64,128},{128,192},{192,0},{1,65},{65,129},{129,193},{193,1... | collective-permute-start | bytes 1572872 | tf_op jit(solution)/shard_map/ppermute | solution.py:25
  126.1 1.0 collective-permute-start.22
  127.2 4.9 %collective-permute-done.22 = bf16[256,512]{1,0:T(8,128)(2,1)S(1)} collective-permute-done((bf16[256,512]{1,0:T(8,128)(2,1)S(1)}, bf16[256,512]{1,0:T(8,128)(2,1)S(1)}, u32[]{:S(2)}, u32[]{:S(2)}) %collective-permute-start.22) | collective-permute-done | bytes 262176 | tf_op jit(solution)/shard_map/ppermute | solution.py:21
  132.2 4.7 %collective-permute-done.20 = bf16[512,512]{1,0:T(8,128)(2,1)S(1)} collective-permute-done((bf16[512,512]{1,0:T(8,128)(2,1)S(1)}, bf16[512,512]{1,0:T(8,128)(2,1)S(1)}, u32[]{:S(2)}, u32[]{:S(2)}) %collective-permute-start.20) | collective-permute-done | bytes 524320 | tf_op jit(solution)/shard_map/ppermute | solution.py:25
  136.9 1.3 collective-permute-done.21
  138.3 0.6 fusion.6
  138.9 0.3 convolution_add_fusion
  139.2 2.2 %collective-permute-start.23 = (f32[256,512]{1,0:T(8,128)S(1)}, f32[256,512]{1,0:T(8,128)S(1)}, u32[]{:S(2)}, u32[]{:S(2)}) collective-permute-start(f32[256,512]{1,0:T(8,128)S(1)} %convolution_add_fusion), channel_id=1, source_target_pairs={{0,16},{16,0},{1,17},{17,1},{2,18},{18,2},{3,19},{19,3},{4,20},{20... | collective-permute-start | bytes 1572872 | tf_op jit(solution)/shard_map/ppermute | solution.py:21
  141.4 0.6 fusion.8
  142.0 0.9 collective-permute-done.23
  142.9 1.2 add_multiply_fusion
  (53 shorter events, 0.9 us)
Async XLA Ops:
  0.0 13.6 %collective-permute-start = (bf16[256,512]{1,0:T(8,128)(2,1)}, bf16[256,512]{1,0:T(8,128)(2,1)S(1)}, u32[]{:S(2)}, u32[]{:S(2)}) collective-permute-start(bf16[256,512]{1,0:T(8,128)(2,1)} %param.1), channel_id=1, source_target_pairs={{0,16},{16,0},{1,17},{17,1},{2,18},{18,2},{3,19},{19,3},{4,20},{20... | collective-permute-start | bytes 786440 | tf_op jit(solution)/shard_map/ppermute | solution.py:21
  3.2 8.1 %collective-permute-start.1 = (bf16[256,512]{1,0:T(8,128)(2,1)}, bf16[256,512]{1,0:T(8,128)(2,1)S(1)}, u32[]{:S(2)}, u32[]{:S(2)}) collective-permute-start(bf16[256,512]{1,0:T(8,128)(2,1)} %param.1), channel_id=1, source_target_pairs={{0,32},{32,0},{1,33},{33,1},{2,34},{34,2},{3,35},{35,3},{4,36},{36... | collective-permute-start | bytes 786440 | tf_op jit(solution)/shard_map/ppermute | solution.py:21
  3.2 14.0 %collective-permute-start.2 = (bf16[256,512]{1,0:T(8,128)(2,1)}, bf16[256,512]{1,0:T(8,128)(2,1)S(1)}, u32[]{:S(2)}, u32[]{:S(2)}) collective-permute-start(bf16[256,512]{1,0:T(8,128)(2,1)} %param.1), channel_id=1, source_target_pairs={{0,128},{64,192},{128,0},{192,64},{1,129},{65,193},{129,1},{193,65... | collective-permute-start | bytes 786440 | tf_op jit(solution)/shard_map/ppermute | solution.py:25
  11.4 2.3 %copy-start.2 = (bf16[256,512]{1,0:T(8,128)(2,1)}, bf16[256,512]{1,0:T(8,128)(2,1)S(1)}, u32[]{:S(2)}) copy-start(bf16[256,512]{1,0:T(8,128)(2,1)S(1)} %collective-permute-done.1) | copy-start | bytes 786436
  12.1 13.0 %collective-permute-start.3 = (bf16[512,512]{1,0:T(8,128)(2,1)}, bf16[512,512]{1,0:T(8,128)(2,1)S(1)}, u32[]{:S(2)}, u32[]{:S(2)}) collective-permute-start(bf16[512,512]{1,0:T(8,128)(2,1)} %constant_dynamic-update-slice_fusion), channel_id=1, source_target_pairs={{0,192},{64,0},{128,64},{192,128},{1,193},{65,1},{129,65},{193,129... | collective-permute-start | bytes 1572872 | tf_op jit(solution)/shard_map/ppermute | solution.py:25
  13.2 13.9 %collective-permute-start.4 = (bf16[512,512]{1,0:T(8,128)(2,1)}, bf16[512,512]{1,0:T(8,128)(2,1)S(1)}, u32[]{:S(2)}, u32[]{:S(2)}) collective-permute-start(bf16[512,512]{1,0:T(8,128)(2,1)} %constant_dynamic-update-slice_fusion), channel_id=1, source_target_pairs={{0,64},{64,128},{128,192},{192,0},{1,65},{65,129},{129,193},{193,1... | collective-permute-start | bytes 1572872 | tf_op jit(solution)/shard_map/ppermute | solution.py:25
  17.2 6.6 %collective-permute-start.5 = (bf16[256,512]{1,0:T(8,128)(2,1)S(1)}, bf16[256,512]{1,0:T(8,128)(2,1)}, u32[]{:S(2)}, u32[]{:S(2)}) collective-permute-start(bf16[256,512]{1,0:T(8,128)(2,1)S(1)} %collective-permute-done.2), channel_id=1, source_target_pairs={{0,32},{32,0},{1,33},{33,1},{2,34},{34,2},{3,35},{35,3},{4,36},{36... | collective-permute-start | bytes 786440 | tf_op jit(solution)/shard_map/ppermute | solution.py:21
  18.1 19.3 %all-to-all-start = ((bf16[4,128,512]{2,1,0:T(8,128)(2,1)}), bf16[4,128,512]{2,1,0:T(8,128)(2,1)S(1)}, u32[]{:S(2)}, u32[]{:S(2)}) async-start(bf16[4,128,512]{2,1,0:T(8,128)(2,1)} %bitcast), calls=%async_computation | async-start | bytes 1048576 | tf_op jit(solution)/shard_map/all_to_all | solution.py:81
  22.4 2.8 %copy-start.1 = (bf16[896,512]{1,0:T(8,128)(2,1)}, bf16[896,512]{1,0:T(8,128)(2,1)S(1)}, u32[]{:S(2)}) copy-start(bf16[896,512]{1,0:T(8,128)(2,1)S(1)} %constant_dynamic-update-slice_fusion.2) | copy-start | bytes 2752516
  29.7 10.3 %collective-permute-start.6 = (bf16[128,1536]{1,0:T(8,128)(2,1)S(1)}, bf16[128,1536]{1,0:T(8,128)(2,1)}, u32[]{:S(2)}, u32[]{:S(2)}) collective-permute-start(bf16[128,1536]{1,0:T(8,128)(2,1)S(1)} %convolution_convert_fusion.2), channel_id=1, source_target_pairs={{0,1},{1,2},{2,3},{3,0},{4,5},{5,6},{6,7},{7,4},{8,9},{9,10},{10,1... | collective-permute-start | bytes 1179656 | tf_op jit(solution)/shard_map/ppermute | solution.py:25
  32.6 8.6 %collective-permute-start.7 = (bf16[128,1536]{1,0:T(8,128)(2,1)S(1)}, bf16[128,1536]{1,0:T(8,128)(2,1)}, u32[]{:S(2)}, u32[]{:S(2)}) collective-permute-start(bf16[128,1536]{1,0:T(8,128)(2,1)S(1)} %convolution_convert_fusion.1), channel_id=1, source_target_pairs={{0,3},{1,0},{2,1},{3,2},{4,7},{5,4},{6,5},{7,6},{8,11},{9,8},{10,9... | collective-permute-start | bytes 1179656 | tf_op jit(solution)/shard_map/ppermute | solution.py:25
  35.7 13.8 %collective-permute-start.8 = (bf16[128,1536]{1,0:T(8,128)(2,1)S(1)}, bf16[128,1536]{1,0:T(8,128)(2,1)}, u32[]{:S(2)}, u32[]{:S(2)}) collective-permute-start(bf16[128,1536]{1,0:T(8,128)(2,1)S(1)} %convolution_convert_fusion), channel_id=1, source_target_pairs={{0,2},{1,3},{2,0},{3,1},{4,6},{5,7},{6,4},{7,5},{8,10},{9,11},{10,... | collective-permute-start | bytes 1179656 | tf_op jit(solution)/shard_map/ppermute | solution.py:25
  51.4 34.3 %copy-start = (bf16[256,512]{1,0:T(8,128)(2,1)S(1)}, bf16[256,512]{1,0:T(8,128)(2,1)}, u32[]{:S(2)}) copy-start(bf16[256,512]{1,0:T(8,128)(2,1)} %param.1) | copy-start | bytes 786436
  51.4 34.3 %copy-start.3 = (bf16[256,512]{1,0:T(8,128)(2,1)S(1)}, bf16[256,512]{1,0:T(8,128)(2,1)}, u32[]{:S(2)}) copy-start(bf16[256,512]{1,0:T(8,128)(2,1)} %copy-done.2) | copy-start | bytes 786436
  51.5 8.9 %collective-permute-start.10 = (bf16[32,2048]{1,0:T(8,128)(2,1)S(1)}, bf16[32,2048]{1,0:T(8,128)(2,1)S(1)}, u32[]{:S(2)}, u32[]{:S(2)}) collective-permute-start(bf16[32,2048]{1,0:T(8,128)(2,1)S(1)} %get-tuple-element.43), channel_id=1, source_target_pairs={{0,12},{4,0},{8,4},{12,8},{1,13},{5,1},{9,5},{13,9},{2,14},{6,2},{... | collective-permute-start | bytes 393224 | tf_op jit(solution)/shard_map/ppermute | solution.py:25
  57.1 9.1 %collective-permute-start.11 = (bf16[32,2048]{1,0:T(8,128)(2,1)S(1)}, bf16[32,2048]{1,0:T(8,128)(2,1)S(1)}, u32[]{:S(2)}, u32[]{:S(2)}) collective-permute-start(bf16[32,2048]{1,0:T(8,128)(2,1)S(1)} %get-tuple-element.42), channel_id=1, source_target_pairs={{0,8},{4,12},{8,0},{12,4},{1,9},{5,13},{9,1},{13,5},{2,10},{6,14},... | collective-permute-start | bytes 393224 | tf_op jit(solution)/shard_map/ppermute | solution.py:25
  58.1 9.7 %collective-permute-start.9 = (bf16[32,2048]{1,0:T(8,128)(2,1)S(1)}, bf16[32,2048]{1,0:T(8,128)(2,1)S(1)}, u32[]{:S(2)}, u32[]{:S(2)}) collective-permute-start(bf16[32,2048]{1,0:T(8,128)(2,1)S(1)} %get-tuple-element.41), channel_id=1, source_target_pairs={{0,4},{4,8},{8,12},{12,0},{1,5},{5,9},{9,13},{13,1},{2,6},{6,10},{... | collective-permute-start | bytes 393224 | tf_op jit(solution)/shard_map/ppermute | solution.py:25
  83.5 11.2 %collective-permute-start.12 = (bf16[128,2048]{1,0:T(8,128)(2,1)S(1)}, bf16[128,2048]{1,0:T(8,128)(2,1)S(1)}, u32[]{:S(2)}, u32[]{:S(2)}) collective-permute-start(bf16[128,2048]{1,0:T(8,128)(2,1)S(1)} %all_gather.3), channel_id=1, source_target_pairs={{0,3},{1,0},{2,1},{3,2},{4,7},{5,4},{6,5},{7,6},{8,11},{9,8},{10,9... | collective-permute-start | bytes 1572872 | tf_op jit(solution)/shard_map/ppermute | solution.py:25
  85.4 9.2 %collective-permute-start.13 = (bf16[128,2048]{1,0:T(8,128)(2,1)S(1)}, bf16[128,2048]{1,0:T(8,128)(2,1)S(1)}, u32[]{:S(2)}, u32[]{:S(2)}) collective-permute-start(bf16[128,2048]{1,0:T(8,128)(2,1)S(1)} %all_gather.3), channel_id=1, source_target_pairs={{0,1},{1,2},{2,3},{3,0},{4,5},{5,6},{6,7},{7,4},{8,9},{9,10},{10,1... | collective-permute-start | bytes 1572872 | tf_op jit(solution)/shard_map/ppermute | solution.py:25
  94.8 15.3 %collective-permute-start.15 = (bf16[64,2048]{1,0:T(8,128)(2,1)S(1)}, bf16[64,2048]{1,0:T(8,128)(2,1)S(1)}, u32[]{:S(2)}, u32[]{:S(2)}) collective-permute-start(bf16[64,2048]{1,0:T(8,128)(2,1)S(1)} %get-tuple-element.18), channel_id=1, source_target_pairs={{0,3},{1,0},{2,1},{3,2},{4,7},{5,4},{6,5},{7,6},{8,11},{9,8},{10,9... | collective-permute-start | bytes 786440 | tf_op jit(solution)/shard_map/ppermute | solution.py:25
  94.9 15.3 %collective-permute-start.16 = (bf16[64,2048]{1,0:T(8,128)(2,1)S(1)}, bf16[64,2048]{1,0:T(8,128)(2,1)S(1)}, u32[]{:S(2)}, u32[]{:S(2)}) collective-permute-start(bf16[64,2048]{1,0:T(8,128)(2,1)S(1)} %slice.113), channel_id=1, source_target_pairs={{0,1},{1,2},{2,3},{3,0},{4,5},{5,6},{6,7},{7,4},{8,9},{9,10},{10,1... | collective-permute-start | bytes 786440 | tf_op jit(solution)/shard_map/ppermute | solution.py:25
  97.3 18.1 %collective-permute-start.14 = (f32[192,512]{1,0:T(8,128)S(1)}, f32[192,512]{1,0:T(8,128)S(1)}, u32[]{:S(2)}, u32[]{:S(2)}) collective-permute-start(f32[192,512]{1,0:T(8,128)S(1)} %pad_maximum_fusion.3), channel_id=1, source_target_pairs={{0,16},{16,0},{1,17},{17,1},{2,18},{18,2},{3,19},{19,3},{4,20},{20... | collective-permute-start | bytes 1179656 | tf_op jit(solution)/shard_map/ppermute | solution.py:21
  110.7 5.6 %collective-permute-start.17 = (f32[64,512]{1,0:T(8,128)S(1)}, f32[64,512]{1,0:T(8,128)S(1)}, u32[]{:S(2)}, u32[]{:S(2)}) collective-permute-start(f32[64,512]{1,0:T(8,128)S(1)} %fusion.48), channel_id=1, source_target_pairs={{0,16},{16,0},{1,17},{17,1},{2,18},{18,2},{3,19},{19,3},{4,20},{20... | collective-permute-start | bytes 393224 | tf_op jit(solution)/shard_map/ppermute | solution.py:21
  116.9 7.6 %collective-permute-start.18 = (bf16[256,512]{1,0:T(8,128)(2,1)S(1)}, bf16[256,512]{1,0:T(8,128)(2,1)S(1)}, u32[]{:S(2)}, u32[]{:S(2)}) collective-permute-start(bf16[256,512]{1,0:T(8,128)(2,1)S(1)} %dynamic-slice_convert_fusion), channel_id=1, source_target_pairs={{0,32},{32,0},{1,33},{33,1},{2,34},{34,2},{3,35},{35,3},{4,36},{36... | collective-permute-start | bytes 786440 | tf_op jit(solution)/shard_map/ppermute | solution.py:21
  117.0 9.1 %collective-permute-start.19 = (bf16[256,512]{1,0:T(8,128)(2,1)S(1)}, bf16[256,512]{1,0:T(8,128)(2,1)S(1)}, u32[]{:S(2)}, u32[]{:S(2)}) collective-permute-start(bf16[256,512]{1,0:T(8,128)(2,1)S(1)} %dynamic-slice_convert_fusion), channel_id=1, source_target_pairs={{0,128},{64,192},{128,0},{192,64},{1,129},{65,193},{129,1},{193,65... | collective-permute-start | bytes 786440 | tf_op jit(solution)/shard_map/ppermute | solution.py:25
  124.6 12.3 %collective-permute-start.20 = (bf16[512,512]{1,0:T(8,128)(2,1)S(1)}, bf16[512,512]{1,0:T(8,128)(2,1)S(1)}, u32[]{:S(2)}, u32[]{:S(2)}) collective-permute-start(bf16[512,512]{1,0:T(8,128)(2,1)S(1)} %pad_maximum_fusion.2), channel_id=1, source_target_pairs={{0,192},{64,0},{128,64},{192,128},{1,193},{65,1},{129,65},{193,129... | collective-permute-start | bytes 1572872 | tf_op jit(solution)/shard_map/ppermute | solution.py:25
  124.7 13.5 %collective-permute-start.21 = (bf16[512,512]{1,0:T(8,128)(2,1)S(1)}, bf16[512,512]{1,0:T(8,128)(2,1)S(1)}, u32[]{:S(2)}, u32[]{:S(2)}) collective-permute-start(bf16[512,512]{1,0:T(8,128)(2,1)S(1)} %pad_maximum_fusion.2), channel_id=1, source_target_pairs={{0,64},{64,128},{128,192},{192,0},{1,65},{65,129},{129,193},{193,1... | collective-permute-start | bytes 1572872 | tf_op jit(solution)/shard_map/ppermute | solution.py:25
  126.1 6.0 %collective-permute-start.22 = (bf16[256,512]{1,0:T(8,128)(2,1)S(1)}, bf16[256,512]{1,0:T(8,128)(2,1)S(1)}, u32[]{:S(2)}, u32[]{:S(2)}) collective-permute-start(bf16[256,512]{1,0:T(8,128)(2,1)S(1)} %collective-permute-done.19), channel_id=1, source_target_pairs={{0,32},{32,0},{1,33},{33,1},{2,34},{34,2},{3,35},{35,3},{4,36},{36... | collective-permute-start | bytes 786440 | tf_op jit(solution)/shard_map/ppermute | solution.py:21
  139.2 3.7 %collective-permute-start.23 = (f32[256,512]{1,0:T(8,128)S(1)}, f32[256,512]{1,0:T(8,128)S(1)}, u32[]{:S(2)}, u32[]{:S(2)}) collective-permute-start(f32[256,512]{1,0:T(8,128)S(1)} %convolution_add_fusion), channel_id=1, source_target_pairs={{0,16},{16,0},{1,17},{17,1},{2,18},{18,2},{3,19},{19,3},{4,20},{20... | collective-permute-start | bytes 1572872 | tf_op jit(solution)/shard_map/ppermute | solution.py:21

commit v15 on v14

--- a/solution.py
+++ b/solution.py
@@ -58,7 +58,7 @@
 
 
 def late_blocks(pair, far):
-    return [far, fetch(pair, "x", 1), fetch(pair, "x", 3), swap(far, "zl")]
+    return [fetch(pair, "x", 1), fetch(pair, "x", 3), swap(far, "zl")]
 
 
 def core_sum(products):
@@ -75,15 +75,16 @@
 
     own = [jnp.concatenate(rows, axis=0) for rows in zip(chunks(iterate), chunks(other))]
     own = [window(chunks(rows), zh, 4) for rows in own]
-    pieces = matmul(jnp.concatenate(own, axis=0), pair, ((1,), (1,))).astype(BF)
-    pieces, far = lax.optimization_barrier((pieces, far))
+    early = lax.optimization_barrier(jnp.concatenate([pair, far], axis=0))
+    pieces = matmul(jnp.concatenate(own, axis=0), early, ((1,), (1,))).astype(BF)
     late = late_blocks(pair, far)
-    first = add(lax.all_to_all(pieces.reshape(4, 128, 512), "y", 0, 0))
+    first = add(lax.all_to_all(pieces.reshape(4, 128, 768), "y", 0, 0))
     panel = lax.optimization_barrier(jnp.concatenate(late, axis=0))
     pieces = [matmul(rows, panel, ((1,), (1,))).astype(BF) for rows in chunks(window(own, y, 4))]
     second = add(scatter(pieces, "y"))
+    first, second = lax.optimization_barrier((first, second))
     part = jnp.concatenate([first, second], axis=1)
-    panel = jnp.concatenate([pair, panel], axis=0)
+    panel = jnp.concatenate([early, panel], axis=0)
     part = add(scatter(chunks(part), "zh"))
     near = lax.all_gather(part, "zh", axis=0, tiled=True)
     after, before = fetch(near, "y", 1), fetch(near, "y", 3)
@@ -98,13 +99,13 @@
     inner = window([first[:64], first[64:128], second, first[128:]], back, 4)
 
     pair, last = pair_of(inner.astype(BF))
-    pair, *late = lax.optimization_barrier([pair, *late_blocks(pair, last)])
-    panels = pair, jnp.concatenate(late, axis=0)
+    pair, *late = lax.optimization_barrier([pair, last, *late_blocks(pair, last)])
+    panels = jnp.concatenate([pair, late[0]], axis=0), jnp.concatenate(late[1:], axis=0)
     gram = [(near[:64], near[64:]), (after[:64], after[64:]), far, (before[:64], before[64:])]
     mixed = []
     for rows in zip(*gram):
         rows = window(rows, back, 4)
-        halves = rows[:, :512], rows[:, 512:]
+        halves = rows[:, :768], rows[:, 768:]
         mixed.append(sum(matmul(h, panel, ((1,), (0,))) for h, panel in zip(halves, panels)))
     mixed = mixed[0] + swap(mixed[1], "core")
     mine = iterate.astype(F32)

time: 144 us -> 144 us (level)
  waiting for transfers between devices: 55.5 us -> 50.5 us
  other arithmetic: 2.54 us -> 6.22 us
  local copies, waits for them, and re-layouts: 4.04 us -> 6.74 us
    ppermute x8, starting transfers between devices: 24.9 us -> 21.9 us  [swap(): return lax.ppermute(array, axis, [(0, 1), (1, 0)])]
    ppermute x16, waiting for transfers between devices: 37.2 us -> 34.4 us  [send(): lax.ppermute(array, axis, [(i, (i + k) % 4) for i in range(4)])]
    unnamed x4, other arithmetic: 1.21 us -> 3.72 us
    ppermute x8, waiting for transfers between devices: 18.3 us -> 16.1 us  [swap(): return lax.ppermute(array, axis, [(0, 1), (1, 0)])]
    ppermute x16, starting transfers between devices: 23 us -> 25.2 us  [send(): lax.ppermute(array, axis, [(i, (i + k) % 4) for i in range(4)])]
    unnamed x27 -> x24, local copies, waits for them, and re-layouts: 2.11 us -> 4.13 us
  transfers between devices with their start and end apart: 25 -> 25, of which waited for: 16 -> 12; matrix products, arithmetic and copies ran while one was open for 11% -> 15% of each run, Pallas kernels for 0% -> 0%
where the time goes in v15:
time: 144 us
  starting transfers between devices  51.3 us (36%)
  waiting for transfers between devices  50.5 us (35%)
  blocking collectives  14.7 us (10%)
  matrix products  14 us (10%)
  local copies, waits for them, and re-layouts  6.74 us (5%)
  other arithmetic  6.22 us (4%)
    ppermute x16, waiting for transfers between devices, send(): lax.ppermute(array, axis, [(i, (i + k) % 4) for i in range(4)])  34.4 us
    ppermute x16, starting transfers between devices, send(): lax.ppermute(array, axis, [(i, (i + k) % 4) for i in range(4)])  25.2 us
    ppermute x8, starting transfers between devices, swap(): return lax.ppermute(array, axis, [(0, 1), (1, 0)])  21.9 us
    ppermute x8, waiting for transfers between devices, swap(): return lax.ppermute(array, axis, [(0, 1), (1, 0)])  16.1 us
    all_gather x1, blocking collectives, per_device(): near = lax.all_gather(part, 'zh', axis=0, tiled=True)  14.7 us
    dot_general x14, matrix products, matmul(): return lax.dot_general(a, b, (dims, ((), ())), preferred_element_type=F32)  14 us
    all_to_all x1, starting transfers between devices, per_device(): first = add(lax.all_to_all(pieces.reshape(4, 128, 768), 'y', 0, 0))  4.18 us
    unnamed x24, local copies, waits for them, and re-layouts  4.13 us
  transfers between devices with their start and end apart: 25, of which 12 were waited for; matrix products, arithmetic and copies ran while one was open for 15% of the time, Pallas kernels for 0%

profile of v15, /device:TPU:1, one launch (start us, length us, event | category | flops | bytes accessed | tf_op | source)
XLA Modules:
  0.0 143.9 jit_solution(8973007204818866462)
XLA Ops:
  0.0 3.2 %collective-permute-start = (bf16[256,512]{1,0:T(8,128)(2,1)}, bf16[256,512]{1,0:T(8,128)(2,1)S(1)}, u32[]{:S(2)}, u32[]{:S(2)}) collective-permute-start(bf16[256,512]{1,0:T(8,128)(2,1)} %param.1), channel_id=1, source_target_pairs={{0,16},{16,0},{1,17},{17,1},{2,18},{18,2},{3,19},{19,3},{4,20},{20... | collective-permute-start | bytes 786440 | tf_op jit(solution)/shard_map/ppermute | solution.py:21
  3.2 2.6 %collective-permute-start.2 = (bf16[256,512]{1,0:T(8,128)(2,1)}, bf16[256,512]{1,0:T(8,128)(2,1)S(1)}, u32[]{:S(2)}, u32[]{:S(2)}) collective-permute-start(bf16[256,512]{1,0:T(8,128)(2,1)} %param.1), channel_id=1, source_target_pairs={{0,128},{64,192},{128,0},{192,64},{1,129},{65,193},{129,1},{193,65... | collective-permute-start | bytes 786440 | tf_op jit(solution)/shard_map/ppermute | solution.py:25
  5.9 1.0 fusion.58
  6.8 1.7 %constant_dynamic-update-slice_fusion.8 = bf16[512,512]{1,0:T(8,128)(2,1)} fusion(bf16[256,512]{1,0:T(8,128)(2,1)} %param.1), kind=kLoop, calls=%fused_computation.88 | loop fusion | bytes 524288
  8.5 2.9 %collective-permute-done.1 = bf16[256,512]{1,0:T(8,128)(2,1)S(1)} collective-permute-done((bf16[256,512]{1,0:T(8,128)(2,1)}, bf16[256,512]{1,0:T(8,128)(2,1)S(1)}, u32[]{:S(2)}, u32[]{:S(2)}) %collective-permute-start.1) | collective-permute-done | bytes 262176 | tf_op jit(solution)/shard_map/ppermute | solution.py:21
  11.4 0.7 constant_dynamic-update-slice_fusion.7
  12.1 1.0 collective-permute-start.3
  13.1 0.5 collective-permute-start.4
  13.6 1.0 pad_maximum_fusion.2
  14.6 0.9 constant_dynamic-update-slice_fusion.6
  15.6 0.9 constant_dynamic-update-slice_fusion.5
  16.5 0.9 constant_dynamic-update-slice_fusion.4
  17.4 0.9 constant_dynamic-update-slice_fusion.3
  18.4 0.9 collective-permute-start.5
  19.3 1.5 %convolution_convert_fusion.4 = bf16[512,768]{1,0:T(8,128)(2,1)} fusion(bf16[768,512]{1,0:T(8,128)(2,1)S(1)} %pad_maximum_fusion.2, bf16[128,512]{1,0:T(8,128)(2,1)S(1)} %get-tuple-element.28, bf16[128,512]{1,0:T(8,128)(2,1)S(1)} %get-tuple-element.30, bf16[128,512]{1,0:T(8,128)(2,1)S(1)} %get-tuple-element.32, bf16[128,512]{1,0:T(8,128)(2,1)S(1)} %get-tuple-element.34), kind=kOutput, calls=%fused_computation.9 | convolution fusion | flops 405143552 | bytes 2097152 | tf_op jit(solution)/shard_map/dot_general | solution.py:52
  20.8 0.6 constant_dynamic-update-slice_fusion.2
  21.4 4.2 %all-to-all-start = ((bf16[4,128,768]{2,1,0:T(8,128)(2,1)}), bf16[4,128,768]{2,1,0:T(8,128)(2,1)S(1)}, u32[]{:S(2)}, u32[]{:S(2)}) async-start(bf16[4,128,768]{2,1,0:T(8,128)(2,1)} %bitcast), calls=%async_computation | async-start | bytes 1572864 | tf_op jit(solution)/shard_map/all_to_all | solution.py:81
  25.6 0.7 constant_dynamic-update-slice_fusion.1
  26.3 0.7 constant_dynamic-update-slice_fusion
  27.0 0.7 copy-done.1
  27.7 1.2 pad_maximum_fusion.1
  28.9 1.5 %convolution_convert_fusion.2 = bf16[128,1280]{1,0:T(8,128)(2,1)S(1)} fusion(bf16[1280,512]{1,0:T(8,128)(2,1)S(1)} %pad_maximum_fusion.1, bf16[896,512]{1,0:T(8,128)(2,1)} %constant_dynamic-update-slice_fusion, s32[]{:T(128)S(6)} %add.84), kind=kOutput, calls=%fused_computation.2 | convolution fusion | flops 167936000 | bytes 1769476 | tf_op jit(solution)/shard_map/dot_general | solution.py:52
  30.4 1.5 %collective-permute-start.6 = (bf16[128,1280]{1,0:T(8,128)(2,1)S(1)}, bf16[128,1280]{1,0:T(8,128)(2,1)}, u32[]{:S(2)}, u32[]{:S(2)}) collective-permute-start(bf16[128,1280]{1,0:T(8,128)(2,1)S(1)} %convolution_convert_fusion.2), channel_id=1, source_target_pairs={{0,1},{1,2},{2,3},{3,0},{4,5},{5,6},{6,7},{7,4},{8,9},{9,10},{10,1... | collective-permute-start | bytes 983048 | tf_op jit(solution)/shard_map/ppermute | solution.py:25
  31.9 2.2 %convolution_convert_fusion.1 = bf16[128,1280]{1,0:T(8,128)(2,1)} fusion(bf16[1280,512]{1,0:T(8,128)(2,1)S(1)} %pad_maximum_fusion.1, bf16[896,512]{1,0:T(8,128)(2,1)} %constant_dynamic-update-slice_fusion, s32[]{:T(128)S(6)} %add.85), kind=kOutput, calls=%fused_computation.1 | convolution fusion | flops 167936000 | bytes 1769476 | tf_op jit(solution)/shard_map/dot_general | solution.py:52
  34.1 1.2 collective-permute-start.7
  35.3 2.2 %convolution_convert_fusion = bf16[128,1280]{1,0:T(8,128)(2,1)} fusion(bf16[1280,512]{1,0:T(8,128)(2,1)S(1)} %pad_maximum_fusion.1, bf16[896,512]{1,0:T(8,128)(2,1)} %constant_dynamic-update-slice_fusion, s32[]{:T(128)S(6)} %add.86), kind=kOutput, calls=%fused_computation | convolution fusion | flops 167936000 | bytes 1769476 | tf_op jit(solution)/shard_map/dot_general | solution.py:52
  37.5 1.7 %collective-permute-start.8 = (bf16[128,1280]{1,0:T(8,128)(2,1)}, bf16[128,1280]{1,0:T(8,128)(2,1)}, u32[]{:S(2)}, u32[]{:S(2)}) collective-permute-start(bf16[128,1280]{1,0:T(8,128)(2,1)} %convolution_convert_fusion), channel_id=1, source_target_pairs={{0,2},{1,3},{2,0},{3,1},{4,6},{5,7},{6,4},{7,5},{8,10},{9,11},{10,... | collective-permute-start | bytes 983048 | tf_op jit(solution)/shard_map/ppermute | solution.py:25
  39.2 0.1 fusion.21
  39.3 6.5 %collective-permute-done.6 = bf16[128,1280]{1,0:T(8,128)(2,1)} collective-permute-done((bf16[128,1280]{1,0:T(8,128)(2,1)S(1)}, bf16[128,1280]{1,0:T(8,128)(2,1)}, u32[]{:S(2)}, u32[]{:S(2)}) %collective-permute-start.6) | collective-permute-done | bytes 327712 | tf_op jit(solution)/shard_map/ppermute | solution.py:25
  45.8 4.7 %collective-permute-done.8 = bf16[128,1280]{1,0:T(8,128)(2,1)} collective-permute-done((bf16[128,1280]{1,0:T(8,128)(2,1)}, bf16[128,1280]{1,0:T(8,128)(2,1)}, u32[]{:S(2)}, u32[]{:S(2)}) %collective-permute-start.8) | collective-permute-done | bytes 327712 | tf_op jit(solution)/shard_map/ppermute | solution.py:25
  50.5 1.8 %fusion.3 = bf16[128,1280]{1,0:T(8,128)(2,1)S(1)} fusion(bf16[1280,512]{1,0:T(8,128)(2,1)S(1)} %pad_maximum_fusion.1, bf16[128,1280]{1,0:T(8,128)(2,1)} %collective-permute-done.8, bf16[128,1280]{1,0:T(8,128)(2,1)} %collective-permute-done.7, bf16[128,1280]{1,0:T(8,128)(2,1)} %collective-permute-done.6, ...), kind=kOutput, calls=%fused_computation.7 | convolution fusion | flops 169246720 | bytes 2752516 | tf_op jit(solution)/shard_map/dot_general | solution.py:52
  52.4 5.2 %collective-permute-start.10 = (bf16[32,2048]{1,0:T(8,128)(2,1)S(1)}, bf16[32,2048]{1,0:T(8,128)(2,1)S(1)}, u32[]{:S(2)}, u32[]{:S(2)}) collective-permute-start(bf16[32,2048]{1,0:T(8,128)(2,1)S(1)} %get-tuple-element.43), channel_id=1, source_target_pairs={{0,12},{4,0},{8,4},{12,8},{1,13},{5,1},{9,5},{13,9},{2,14},{6,2},{... | collective-permute-start | bytes 393224 | tf_op jit(solution)/shard_map/ppermute | solution.py:25
  57.5 1.2 collective-permute-start.11
  58.7 2.1 %collective-permute-start.9 = (bf16[32,2048]{1,0:T(8,128)(2,1)S(1)}, bf16[32,2048]{1,0:T(8,128)(2,1)S(1)}, u32[]{:S(2)}, u32[]{:S(2)}) collective-permute-start(bf16[32,2048]{1,0:T(8,128)(2,1)S(1)} %get-tuple-element.41), channel_id=1, source_target_pairs={{0,4},{4,8},{8,12},{12,0},{1,5},{5,9},{9,13},{13,1},{2,6},{6,10},{... | collective-permute-start | bytes 393224 | tf_op jit(solution)/shard_map/ppermute | solution.py:25
  60.8 5.9 %collective-permute-done.11 = bf16[32,2048]{1,0:T(8,128)(2,1)S(1)} collective-permute-done((bf16[32,2048]{1,0:T(8,128)(2,1)S(1)}, bf16[32,2048]{1,0:T(8,128)(2,1)S(1)}, u32[]{:S(2)}, u32[]{:S(2)}) %collective-permute-start.11) | collective-permute-done | bytes 131104 | tf_op jit(solution)/shard_map/ppermute | solution.py:25
  66.7 1.9 %collective-permute-done.9 = bf16[32,2048]{1,0:T(8,128)(2,1)S(1)} collective-permute-done((bf16[32,2048]{1,0:T(8,128)(2,1)S(1)}, bf16[32,2048]{1,0:T(8,128)(2,1)S(1)}, u32[]{:S(2)}, u32[]{:S(2)}) %collective-permute-start.9) | collective-permute-done | bytes 131104 | tf_op jit(solution)/shard_map/ppermute | solution.py:25
  68.6 0.1 add_convert_fusion.1
  68.7 14.7 %all_gather.3 = bf16[128,2048]{1,0:T(8,128)(2,1)S(1)} all-gather(bf16[32,2048]{1,0:T(8,128)(2,1)S(1)} %add_convert_fusion.1), channel_id=1, replica_groups=mesh['x'=4,'zl'=2,'core'=2,'zh'=4,'y'=4] {'zh'}, dimensions={0}, use_global_device_ids=true | all-gather | bytes 655360 | tf_op jit(solution)/shard_map/all_gather | solution.py:89
  83.4 1.5 %collective-permute-start.12 = (bf16[128,2048]{1,0:T(8,128)(2,1)S(1)}, bf16[128,2048]{1,0:T(8,128)(2,1)S(1)}, u32[]{:S(2)}, u32[]{:S(2)}) collective-permute-start(bf16[128,2048]{1,0:T(8,128)(2,1)S(1)} %all_gather.3), channel_id=1, source_target_pairs={{0,3},{1,0},{2,1},{3,2},{4,7},{5,4},{6,5},{7,6},{8,11},{9,8},{10,9... | collective-permute-start | bytes 1572872 | tf_op jit(solution)/shard_map/ppermute | solution.py:25
  84.9 0.1 collective-permute-start.13
  85.0 0.4 fusion.48
  85.5 8.6 %collective-permute-done.13 = bf16[128,2048]{1,0:T(8,128)(2,1)S(1)} collective-permute-done((bf16[128,2048]{1,0:T(8,128)(2,1)S(1)}, bf16[128,2048]{1,0:T(8,128)(2,1)S(1)}, u32[]{:S(2)}, u32[]{:S(2)}) %collective-permute-start.13) | collective-permute-done | bytes 524320 | tf_op jit(solution)/shard_map/ppermute | solution.py:25
  94.2 0.1 collective-permute-start.15
  94.3 1.5 %collective-permute-start.16 = (bf16[64,2048]{1,0:T(8,128)(2,1)S(1)}, bf16[64,2048]{1,0:T(8,128)(2,1)S(1)}, u32[]{:S(2)}, u32[]{:S(2)}) collective-permute-start(bf16[64,2048]{1,0:T(8,128)(2,1)S(1)} %slice.113), channel_id=1, source_target_pairs={{0,1},{1,2},{2,3},{3,0},{4,5},{5,6},{6,7},{7,4},{8,9},{9,10},{10,1... | collective-permute-start | bytes 786440 | tf_op jit(solution)/shard_map/ppermute | solution.py:25
  95.7 0.4 fusion.47
  96.2 0.4 fusion.46
  96.7 10.4 %collective-permute-start.14 = (f32[192,512]{1,0:T(8,128)S(1)}, f32[192,512]{1,0:T(8,128)S(1)}, u32[]{:S(2)}, u32[]{:S(2)}) collective-permute-start(f32[192,512]{1,0:T(8,128)S(1)} %pad_maximum_fusion.4), channel_id=1, source_target_pairs={{0,16},{16,0},{1,17},{17,1},{2,18},{18,2},{3,19},{19,3},{4,20},{20... | collective-permute-start | bytes 1179656 | tf_op jit(solution)/shard_map/ppermute | solution.py:21
  107.2 0.5 fusion.45
  107.7 4.6 %collective-permute-start.17 = (f32[64,512]{1,0:T(8,128)S(1)}, f32[64,512]{1,0:T(8,128)S(1)}, u32[]{:S(2)}, u32[]{:S(2)}) collective-permute-start(f32[64,512]{1,0:T(8,128)S(1)} %fusion.45), channel_id=1, source_target_pairs={{0,16},{16,0},{1,17},{17,1},{2,18},{18,2},{3,19},{19,3},{4,20},{20... | collective-permute-start | bytes 393224 | tf_op jit(solution)/shard_map/ppermute | solution.py:21
  112.5 0.8 collective-permute-done.17
  113.3 0.5 constant_dynamic-update-slice_fusion.12
  113.9 0.2 collective-permute-start.18
  114.1 2.1 %collective-permute-start.19 = (bf16[256,512]{1,0:T(8,128)(2,1)S(1)}, bf16[256,512]{1,0:T(8,128)(2,1)S(1)}, u32[]{:S(2)}, u32[]{:S(2)}) collective-permute-start(bf16[256,512]{1,0:T(8,128)(2,1)S(1)} %dynamic-slice_convert_fusion), channel_id=1, source_target_pairs={{0,128},{64,192},{128,0},{192,64},{1,129},{65,193},{129,1},{193,65... | collective-permute-start | bytes 786440 | tf_op jit(solution)/shard_map/ppermute | solution.py:25
  116.3 5.3 %collective-permute-done.18 = bf16[256,512]{1,0:T(8,128)(2,1)S(1)} collective-permute-done((bf16[256,512]{1,0:T(8,128)(2,1)S(1)}, bf16[256,512]{1,0:T(8,128)(2,1)S(1)}, u32[]{:S(2)}, u32[]{:S(2)}) %collective-permute-start.18) | collective-permute-done | bytes 262176 | tf_op jit(solution)/shard_map/ppermute | solution.py:21
  121.6 2.8 %collective-permute-start.20 = (bf16[512,512]{1,0:T(8,128)(2,1)S(1)}, bf16[512,512]{1,0:T(8,128)(2,1)S(1)}, u32[]{:S(2)}, u32[]{:S(2)}) collective-permute-start(bf16[512,512]{1,0:T(8,128)(2,1)S(1)} %pad_maximum_fusion.3), channel_id=1, source_target_pairs={{0,192},{64,0},{128,64},{192,128},{1,193},{65,1},{129,65},{193,129... | collective-permute-start | bytes 1572872 | tf_op jit(solution)/shard_map/ppermute | solution.py:25
  124.5 6.2 %collective-permute-done.22 = bf16[256,512]{1,0:T(8,128)(2,1)S(1)} collective-permute-done((bf16[256,512]{1,0:T(8,128)(2,1)S(1)}, bf16[256,512]{1,0:T(8,128)(2,1)S(1)}, u32[]{:S(2)}, u32[]{:S(2)}) %collective-permute-start.22) | collective-permute-done | bytes 262176 | tf_op jit(solution)/shard_map/ppermute | solution.py:21
  130.8 3.7 %collective-permute-done.20 = bf16[512,512]{1,0:T(8,128)(2,1)S(1)} collective-permute-done((bf16[512,512]{1,0:T(8,128)(2,1)S(1)}, bf16[512,512]{1,0:T(8,128)(2,1)S(1)}, u32[]{:S(2)}, u32[]{:S(2)}) %collective-permute-start.20) | collective-permute-done | bytes 524320 | tf_op jit(solution)/shard_map/ppermute | solution.py:25
  134.4 3.1 %collective-permute-done.21 = bf16[512,512]{1,0:T(8,128)(2,1)S(1)} collective-permute-done((bf16[512,512]{1,0:T(8,128)(2,1)S(1)}, bf16[512,512]{1,0:T(8,128)(2,1)S(1)}, u32[]{:S(2)}, u32[]{:S(2)}) %collective-permute-start.21) | collective-permute-done | bytes 524320 | tf_op jit(solution)/shard_map/ppermute | solution.py:25
  137.7 0.5 fusion.6
  138.3 0.4 convolution_add_fusion
  138.7 2.5 %collective-permute-start.23 = (f32[256,512]{1,0:T(8,128)S(1)}, f32[256,512]{1,0:T(8,128)S(1)}, u32[]{:S(2)}, u32[]{:S(2)}) collective-permute-start(f32[256,512]{1,0:T(8,128)S(1)} %convolution_add_fusion), channel_id=1, source_target_pairs={{0,16},{16,0},{1,17},{17,1},{2,18},{18,2},{3,19},{19,3},{4,20},{20... | collective-permute-start | bytes 1572872 | tf_op jit(solution)/shard_map/ppermute | solution.py:21
  141.2 0.5 fusion.8
  141.7 1.0 collective-permute-done.23
  142.7 1.2 add_multiply_fusion
  (52 shorter events, 0.9 us)
Async XLA Ops:
  0.0 14.6 %collective-permute-start = (bf16[256,512]{1,0:T(8,128)(2,1)}, bf16[256,512]{1,0:T(8,128)(2,1)S(1)}, u32[]{:S(2)}, u32[]{:S(2)}) collective-permute-start(bf16[256,512]{1,0:T(8,128)(2,1)} %param.1), channel_id=1, source_target_pairs={{0,16},{16,0},{1,17},{17,1},{2,18},{18,2},{3,19},{19,3},{4,20},{20... | collective-permute-start | bytes 786440 | tf_op jit(solution)/shard_map/ppermute | solution.py:21
  3.2 8.1 %collective-permute-start.1 = (bf16[256,512]{1,0:T(8,128)(2,1)}, bf16[256,512]{1,0:T(8,128)(2,1)S(1)}, u32[]{:S(2)}, u32[]{:S(2)}) collective-permute-start(bf16[256,512]{1,0:T(8,128)(2,1)} %param.1), channel_id=1, source_target_pairs={{0,32},{32,0},{1,33},{33,1},{2,34},{34,2},{3,35},{35,3},{4,36},{36... | collective-permute-start | bytes 786440 | tf_op jit(solution)/shard_map/ppermute | solution.py:21
  3.2 10.3 %collective-permute-start.2 = (bf16[256,512]{1,0:T(8,128)(2,1)}, bf16[256,512]{1,0:T(8,128)(2,1)S(1)}, u32[]{:S(2)}, u32[]{:S(2)}) collective-permute-start(bf16[256,512]{1,0:T(8,128)(2,1)} %param.1), channel_id=1, source_target_pairs={{0,128},{64,192},{128,0},{192,64},{1,129},{65,193},{129,1},{193,65... | collective-permute-start | bytes 786440 | tf_op jit(solution)/shard_map/ppermute | solution.py:25
  12.1 14.8 %collective-permute-start.3 = (bf16[512,512]{1,0:T(8,128)(2,1)}, bf16[512,512]{1,0:T(8,128)(2,1)S(1)}, u32[]{:S(2)}, u32[]{:S(2)}) collective-permute-start(bf16[512,512]{1,0:T(8,128)(2,1)} %constant_dynamic-update-slice_fusion.7), channel_id=1, source_target_pairs={{0,192},{64,0},{128,64},{192,128},{1,193},{65,1},{129,65},{193,129... | collective-permute-start | bytes 1572872 | tf_op jit(solution)/shard_map/ppermute | solution.py:25
  13.1 14.6 %collective-permute-start.4 = (bf16[512,512]{1,0:T(8,128)(2,1)}, bf16[512,512]{1,0:T(8,128)(2,1)}, u32[]{:S(2)}, u32[]{:S(2)}) collective-permute-start(bf16[512,512]{1,0:T(8,128)(2,1)} %constant_dynamic-update-slice_fusion.7), channel_id=1, source_target_pairs={{0,64},{64,128},{128,192},{192,0},{1,65},{65,129},{129,193},{193,1... | collective-permute-start | bytes 1572872 | tf_op jit(solution)/shard_map/ppermute | solution.py:25
  18.4 8.6 %collective-permute-start.5 = (bf16[256,512]{1,0:T(8,128)(2,1)S(1)}, bf16[256,512]{1,0:T(8,128)(2,1)S(1)}, u32[]{:S(2)}, u32[]{:S(2)}) collective-permute-start(bf16[256,512]{1,0:T(8,128)(2,1)S(1)} %collective-permute-done.2), channel_id=1, source_target_pairs={{0,32},{32,0},{1,33},{33,1},{2,34},{34,2},{3,35},{35,3},{4,36},{36... | collective-permute-start | bytes 786440 | tf_op jit(solution)/shard_map/ppermute | solution.py:21
  21.4 17.8 %all-to-all-start = ((bf16[4,128,768]{2,1,0:T(8,128)(2,1)}), bf16[4,128,768]{2,1,0:T(8,128)(2,1)S(1)}, u32[]{:S(2)}, u32[]{:S(2)}) async-start(bf16[4,128,768]{2,1,0:T(8,128)(2,1)} %bitcast), calls=%async_computation | async-start | bytes 1572864 | tf_op jit(solution)/shard_map/all_to_all | solution.py:81
  26.9 0.7 copy-start.1
  30.4 15.5 %collective-permute-start.6 = (bf16[128,1280]{1,0:T(8,128)(2,1)S(1)}, bf16[128,1280]{1,0:T(8,128)(2,1)}, u32[]{:S(2)}, u32[]{:S(2)}) collective-permute-start(bf16[128,1280]{1,0:T(8,128)(2,1)S(1)} %convolution_convert_fusion.2), channel_id=1, source_target_pairs={{0,1},{1,2},{2,3},{3,0},{4,5},{5,6},{6,7},{7,4},{8,9},{9,10},{10,1... | collective-permute-start | bytes 983048 | tf_op jit(solution)/shard_map/ppermute | solution.py:25
  34.1 11.7 %collective-permute-start.7 = (bf16[128,1280]{1,0:T(8,128)(2,1)}, bf16[128,1280]{1,0:T(8,128)(2,1)}, u32[]{:S(2)}, u32[]{:S(2)}) collective-permute-start(bf16[128,1280]{1,0:T(8,128)(2,1)} %convolution_convert_fusion.1), channel_id=1, source_target_pairs={{0,3},{1,0},{2,1},{3,2},{4,7},{5,4},{6,5},{7,6},{8,11},{9,8},{10,9... | collective-permute-start | bytes 983048 | tf_op jit(solution)/shard_map/ppermute | solution.py:25
  37.5 13.0 %collective-permute-start.8 = (bf16[128,1280]{1,0:T(8,128)(2,1)}, bf16[128,1280]{1,0:T(8,128)(2,1)}, u32[]{:S(2)}, u32[]{:S(2)}) collective-permute-start(bf16[128,1280]{1,0:T(8,128)(2,1)} %convolution_convert_fusion), channel_id=1, source_target_pairs={{0,2},{1,3},{2,0},{3,1},{4,6},{5,7},{6,4},{7,5},{8,10},{9,11},{10,... | collective-permute-start | bytes 983048 | tf_op jit(solution)/shard_map/ppermute | solution.py:25
  52.4 8.4 %collective-permute-start.10 = (bf16[32,2048]{1,0:T(8,128)(2,1)S(1)}, bf16[32,2048]{1,0:T(8,128)(2,1)S(1)}, u32[]{:S(2)}, u32[]{:S(2)}) collective-permute-start(bf16[32,2048]{1,0:T(8,128)(2,1)S(1)} %get-tuple-element.43), channel_id=1, source_target_pairs={{0,12},{4,0},{8,4},{12,8},{1,13},{5,1},{9,5},{13,9},{2,14},{6,2},{... | collective-permute-start | bytes 393224 | tf_op jit(solution)/shard_map/ppermute | solution.py:25
  57.5 9.2 %collective-permute-start.11 = (bf16[32,2048]{1,0:T(8,128)(2,1)S(1)}, bf16[32,2048]{1,0:T(8,128)(2,1)S(1)}, u32[]{:S(2)}, u32[]{:S(2)}) collective-permute-start(bf16[32,2048]{1,0:T(8,128)(2,1)S(1)} %get-tuple-element.42), channel_id=1, source_target_pairs={{0,8},{4,12},{8,0},{12,4},{1,9},{5,13},{9,1},{13,5},{2,10},{6,14},... | collective-permute-start | bytes 393224 | tf_op jit(solution)/shard_map/ppermute | solution.py:25
  58.7 9.9 %collective-permute-start.9 = (bf16[32,2048]{1,0:T(8,128)(2,1)S(1)}, bf16[32,2048]{1,0:T(8,128)(2,1)S(1)}, u32[]{:S(2)}, u32[]{:S(2)}) collective-permute-start(bf16[32,2048]{1,0:T(8,128)(2,1)S(1)} %get-tuple-element.41), channel_id=1, source_target_pairs={{0,4},{4,8},{8,12},{12,0},{1,5},{5,9},{9,13},{13,1},{2,6},{6,10},{... | collective-permute-start | bytes 393224 | tf_op jit(solution)/shard_map/ppermute | solution.py:25
  83.4 10.7 %collective-permute-start.12 = (bf16[128,2048]{1,0:T(8,128)(2,1)S(1)}, bf16[128,2048]{1,0:T(8,128)(2,1)S(1)}, u32[]{:S(2)}, u32[]{:S(2)}) collective-permute-start(bf16[128,2048]{1,0:T(8,128)(2,1)S(1)} %all_gather.3), channel_id=1, source_target_pairs={{0,3},{1,0},{2,1},{3,2},{4,7},{5,4},{6,5},{7,6},{8,11},{9,8},{10,9... | collective-permute-start | bytes 1572872 | tf_op jit(solution)/shard_map/ppermute | solution.py:25
  84.9 9.2 %collective-permute-start.13 = (bf16[128,2048]{1,0:T(8,128)(2,1)S(1)}, bf16[128,2048]{1,0:T(8,128)(2,1)S(1)}, u32[]{:S(2)}, u32[]{:S(2)}) collective-permute-start(bf16[128,2048]{1,0:T(8,128)(2,1)S(1)} %all_gather.3), channel_id=1, source_target_pairs={{0,1},{1,2},{2,3},{3,0},{4,5},{5,6},{6,7},{7,4},{8,9},{9,10},{10,1... | collective-permute-start | bytes 1572872 | tf_op jit(solution)/shard_map/ppermute | solution.py:25
  94.2 12.9 %collective-permute-start.15 = (bf16[64,2048]{1,0:T(8,128)(2,1)S(1)}, bf16[64,2048]{1,0:T(8,128)(2,1)S(1)}, u32[]{:S(2)}, u32[]{:S(2)}) collective-permute-start(bf16[64,2048]{1,0:T(8,128)(2,1)S(1)} %get-tuple-element.18), channel_id=1, source_target_pairs={{0,3},{1,0},{2,1},{3,2},{4,7},{5,4},{6,5},{7,6},{8,11},{9,8},{10,9... | collective-permute-start | bytes 786440 | tf_op jit(solution)/shard_map/ppermute | solution.py:25
  94.3 12.8 %collective-permute-start.16 = (bf16[64,2048]{1,0:T(8,128)(2,1)S(1)}, bf16[64,2048]{1,0:T(8,128)(2,1)S(1)}, u32[]{:S(2)}, u32[]{:S(2)}) collective-permute-start(bf16[64,2048]{1,0:T(8,128)(2,1)S(1)} %slice.113), channel_id=1, source_target_pairs={{0,1},{1,2},{2,3},{3,0},{4,5},{5,6},{6,7},{7,4},{8,9},{9,10},{10,1... | collective-permute-start | bytes 786440 | tf_op jit(solution)/shard_map/ppermute | solution.py:25
  96.7 15.7 %collective-permute-start.14 = (f32[192,512]{1,0:T(8,128)S(1)}, f32[192,512]{1,0:T(8,128)S(1)}, u32[]{:S(2)}, u32[]{:S(2)}) collective-permute-start(f32[192,512]{1,0:T(8,128)S(1)} %pad_maximum_fusion.4), channel_id=1, source_target_pairs={{0,16},{16,0},{1,17},{17,1},{2,18},{18,2},{3,19},{19,3},{4,20},{20... | collective-permute-start | bytes 1179656 | tf_op jit(solution)/shard_map/ppermute | solution.py:21
  107.7 5.6 %collective-permute-start.17 = (f32[64,512]{1,0:T(8,128)S(1)}, f32[64,512]{1,0:T(8,128)S(1)}, u32[]{:S(2)}, u32[]{:S(2)}) collective-permute-start(f32[64,512]{1,0:T(8,128)S(1)} %fusion.45), channel_id=1, source_target_pairs={{0,16},{16,0},{1,17},{17,1},{2,18},{18,2},{3,19},{19,3},{4,20},{20... | collective-permute-start | bytes 393224 | tf_op jit(solution)/shard_map/ppermute | solution.py:21
  113.9 7.6 %collective-permute-start.18 = (bf16[256,512]{1,0:T(8,128)(2,1)S(1)}, bf16[256,512]{1,0:T(8,128)(2,1)S(1)}, u32[]{:S(2)}, u32[]{:S(2)}) collective-permute-start(bf16[256,512]{1,0:T(8,128)(2,1)S(1)} %dynamic-slice_convert_fusion), channel_id=1, source_target_pairs={{0,32},{32,0},{1,33},{33,1},{2,34},{34,2},{3,35},{35,3},{4,36},{36... | collective-permute-start | bytes 786440 | tf_op jit(solution)/shard_map/ppermute | solution.py:21
  114.1 10.3 %collective-permute-start.19 = (bf16[256,512]{1,0:T(8,128)(2,1)S(1)}, bf16[256,512]{1,0:T(8,128)(2,1)S(1)}, u32[]{:S(2)}, u32[]{:S(2)}) collective-permute-start(bf16[256,512]{1,0:T(8,128)(2,1)S(1)} %dynamic-slice_convert_fusion), channel_id=1, source_target_pairs={{0,128},{64,192},{128,0},{192,64},{1,129},{65,193},{129,1},{193,65... | collective-permute-start | bytes 786440 | tf_op jit(solution)/shard_map/ppermute | solution.py:25
  121.6 12.9 %collective-permute-start.20 = (bf16[512,512]{1,0:T(8,128)(2,1)S(1)}, bf16[512,512]{1,0:T(8,128)(2,1)S(1)}, u32[]{:S(2)}, u32[]{:S(2)}) collective-permute-start(bf16[512,512]{1,0:T(8,128)(2,1)S(1)} %pad_maximum_fusion.3), channel_id=1, source_target_pairs={{0,192},{64,0},{128,64},{192,128},{1,193},{65,1},{129,65},{193,129... | collective-permute-start | bytes 1572872 | tf_op jit(solution)/shard_map/ppermute | solution.py:25
  124.4 13.2 %collective-permute-start.21 = (bf16[512,512]{1,0:T(8,128)(2,1)S(1)}, bf16[512,512]{1,0:T(8,128)(2,1)S(1)}, u32[]{:S(2)}, u32[]{:S(2)}) collective-permute-start(bf16[512,512]{1,0:T(8,128)(2,1)S(1)} %pad_maximum_fusion.3), channel_id=1, source_target_pairs={{0,64},{64,128},{128,192},{192,0},{1,65},{65,129},{129,193},{193,1... | collective-permute-start | bytes 1572872 | tf_op jit(solution)/shard_map/ppermute | solution.py:25
  124.4 6.3 %collective-permute-start.22 = (bf16[256,512]{1,0:T(8,128)(2,1)S(1)}, bf16[256,512]{1,0:T(8,128)(2,1)S(1)}, u32[]{:S(2)}, u32[]{:S(2)}) collective-permute-start(bf16[256,512]{1,0:T(8,128)(2,1)S(1)} %collective-permute-done.19), channel_id=1, source_target_pairs={{0,32},{32,0},{1,33},{33,1},{2,34},{34,2},{3,35},{35,3},{4,36},{36... | collective-permute-start | bytes 786440 | tf_op jit(solution)/shard_map/ppermute | solution.py:21
  138.7 4.0 %copy-start = (bf16[256,512]{1,0:T(8,128)(2,1)S(1)}, bf16[256,512]{1,0:T(8,128)(2,1)}, u32[]{:S(2)}) copy-start(bf16[256,512]{1,0:T(8,128)(2,1)} %param.1) | copy-start | bytes 786436
  138.7 4.0 %collective-permute-start.23 = (f32[256,512]{1,0:T(8,128)S(1)}, f32[256,512]{1,0:T(8,128)S(1)}, u32[]{:S(2)}, u32[]{:S(2)}) collective-permute-start(f32[256,512]{1,0:T(8,128)S(1)} %convolution_add_fusion), channel_id=1, source_target_pairs={{0,16},{16,0},{1,17},{17,1},{2,18},{18,2},{3,19},{19,3},{4,20},{20... | collective-permute-start | bytes 1572872 | tf_op jit(solution)/shard_map/ppermute | solution.py:21

commit v16 on v15

--- a/solution.py
+++ b/solution.py
@@ -75,14 +75,16 @@
 
     own = [jnp.concatenate(rows, axis=0) for rows in zip(chunks(iterate), chunks(other))]
     own = [window(chunks(rows), zh, 4) for rows in own]
+    own, turned = jnp.concatenate(own, axis=0), window(own, y, 4)
+    pair, own, turned = lax.optimization_barrier((pair, own, turned))
     early = lax.optimization_barrier(jnp.concatenate([pair, far], axis=0))
-    pieces = matmul(jnp.concatenate(own, axis=0), early, ((1,), (1,))).astype(BF)
+    pieces = matmul(own, early, ((1,), (1,))).astype(BF)
     late = late_blocks(pair, far)
     first = add(lax.all_to_all(pieces.reshape(4, 128, 768), "y", 0, 0))
     panel = lax.optimization_barrier(jnp.concatenate(late, axis=0))
-    pieces = [matmul(rows, panel, ((1,), (1,))).astype(BF) for rows in chunks(window(own, y, 4))]
+    pieces = [matmul(rows, panel, ((1,), (1,))).astype(BF) for rows in chunks(turned)]
+    pieces[0] = lax.optimization_barrier(pieces[0])
     second = add(scatter(pieces, "y"))
-    first, second = lax.optimization_barrier((first, second))
     part = jnp.concatenate([first, second], axis=1)
     panel = jnp.concatenate([early, panel], axis=0)
     part = add(scatter(chunks(part), "zh"))

time: 144 us -> 141 us (0.979)
  waiting for transfers between devices: 50.5 us -> 56.2 us
  local copies, waits for them, and re-layouts: 6.74 us -> 1.64 us
  matrix products: 14 us -> 10.1 us
    ppermute x16, waiting for transfers between devices: 34.4 us -> 39.4 us  [send(): lax.ppermute(array, axis, [(i, (i + k) % 4) for i in range(4)])]
    dot_general x14, matrix products: 14 us -> 10.1 us  [matmul(): return lax.dot_general(a, b, (dims, ((), ())), preferred_element_type=F32)]
    unnamed x24, local copies, waits for them, and re-layouts: 4.13 us -> 0.44 us
    unnamed x4, other arithmetic: 3.72 us -> 1.21 us
    ppermute x8, starting transfers between devices: 21.9 us -> 24.2 us  [swap(): return lax.ppermute(array, axis, [(0, 1), (1, 0)])]
    convert_element_type x2 -> x3, other arithmetic: 0.17 us -> 2.4 us  [add(): return (got[0] + got[1] + (got[2] + got[3])).astype(BF)]
    ppermute x16, starting transfers between devices: 25.2 us -> 23.1 us  [send(): lax.ppermute(array, axis, [(i, (i + k) % 4) for i in range(4)])]
  transfers between devices with their start and end apart: 25 -> 25, of which waited for: 12 -> 15; matrix products, arithmetic and copies ran while one was open for 15% -> 9% of each run, Pallas kernels for 0% -> 0%
where the time goes in v16:
time: 141 us
  waiting for transfers between devices  56.2 us (40%)
  starting transfers between devices  51.5 us (37%)
  blocking collectives  15.1 us (11%)
  matrix products  10.1 us (7%)
  other arithmetic  6.08 us (4%)
  local copies, waits for them, and re-layouts  1.64 us (1%)
    ppermute x16, waiting for transfers between devices, send(): lax.ppermute(array, axis, [(i, (i + k) % 4) for i in range(4)])  39.4 us
    ppermute x8, starting transfers between devices, swap(): return lax.ppermute(array, axis, [(0, 1), (1, 0)])  24.2 us
    ppermute x16, starting transfers between devices, send(): lax.ppermute(array, axis, [(i, (i + k) % 4) for i in range(4)])  23.1 us
    ppermute x8, waiting for transfers between devices, swap(): return lax.ppermute(array, axis, [(0, 1), (1, 0)])  16.8 us
    all_gather x1, blocking collectives, per_device(): near = lax.all_gather(part, 'zh', axis=0, tiled=True)  15.1 us
    dot_general x14, matrix products, matmul(): return lax.dot_general(a, b, (dims, ((), ())), preferred_element_type=F32)  10.1 us
    all_to_all x1, starting transfers between devices, per_device(): first = add(lax.all_to_all(pieces.reshape(4, 128, 768), 'y', 0, 0))  4.08 us
  transfers between devices with their start and end apart: 25, of which 15 were waited for; matrix products, arithmetic and copies ran while one was open for 9% of the time, Pallas kernels for 0%

profile of v16, /device:TPU:1, one launch (start us, length us, event | category | flops | bytes accessed | tf_op | source)
XLA Modules:
  0.0 141.0 jit_solution(10382773080745163592)
XLA Ops:
  0.0 3.2 %collective-permute-start.1 = (bf16[256,512]{1,0:T(8,128)(2,1)}, bf16[256,512]{1,0:T(8,128)(2,1)S(1)}, u32[]{:S(2)}, u32[]{:S(2)}) collective-permute-start(bf16[256,512]{1,0:T(8,128)(2,1)} %param.1), channel_id=1, source_target_pairs={{0,16},{16,0},{1,17},{17,1},{2,18},{18,2},{3,19},{19,3},{4,20},{20... | collective-permute-start | bytes 786440 | tf_op jit(solution)/shard_map/ppermute | solution.py:21
  3.2 2.7 %collective-permute-start.2 = (bf16[256,512]{1,0:T(8,128)(2,1)}, bf16[256,512]{1,0:T(8,128)(2,1)}, u32[]{:S(2)}, u32[]{:S(2)}) collective-permute-start(bf16[256,512]{1,0:T(8,128)(2,1)} %param.1), channel_id=1, source_target_pairs={{0,128},{64,192},{128,0},{192,64},{1,129},{65,193},{129,1},{193,65... | collective-permute-start | bytes 786440 | tf_op jit(solution)/shard_map/ppermute | solution.py:25
  5.9 1.0 fusion.44
  6.9 0.3 constant_dynamic-update-slice_fusion.6
  7.2 0.3 constant_dynamic-update-slice_fusion.5
  7.5 0.3 constant_dynamic-update-slice_fusion.4
  7.8 0.3 constant_dynamic-update-slice_fusion.3
  8.2 3.3 %collective-permute-done = bf16[256,512]{1,0:T(8,128)(2,1)S(1)} collective-permute-done((bf16[256,512]{1,0:T(8,128)(2,1)}, bf16[256,512]{1,0:T(8,128)(2,1)S(1)}, u32[]{:S(2)}, u32[]{:S(2)}) %collective-permute-start) | collective-permute-done | bytes 262176 | tf_op jit(solution)/shard_map/ppermute | solution.py:21
  11.6 0.1 pad_maximum_fusion.4
  11.6 1.1 collective-permute-start.3
  12.7 0.4 collective-permute-start.4
  13.2 1.0 pad_maximum_fusion.2
  14.2 1.0 collective-permute-start.5
  15.3 1.5 %convolution_convert_fusion.4 = bf16[512,768]{1,0:T(8,128)(2,1)} fusion(bf16[512,512]{1,0:T(8,128)(2,1)S(1)} %get-tuple-element.17, bf16[768,512]{1,0:T(8,128)(2,1)S(1)} %pad_maximum_fusion.2), kind=kOutput, calls=%fused_computation.5 | convolution fusion | flops 403046400 | bytes 2097152 | tf_op jit(solution)/shard_map/dot_general | solution.py:52
  16.8 4.1 %all-to-all-start = ((bf16[4,128,768]{2,1,0:T(8,128)(2,1)}), bf16[4,128,768]{2,1,0:T(8,128)(2,1)S(1)}, u32[]{:S(2)}, u32[]{:S(2)}) async-start(bf16[4,128,768]{2,1,0:T(8,128)(2,1)} %bitcast.18), calls=%async_computation | async-start | bytes 1572864 | tf_op jit(solution)/shard_map/all_to_all | solution.py:83
  20.8 0.3 collective-permute-done.5
  21.2 3.4 %collective-permute-done.3 = bf16[512,512]{1,0:T(8,128)(2,1)S(1)} collective-permute-done((bf16[512,512]{1,0:T(8,128)(2,1)S(1)}, bf16[512,512]{1,0:T(8,128)(2,1)S(1)}, u32[]{:S(2)}, u32[]{:S(2)}) %collective-permute-start.3) | collective-permute-done | bytes 524320 | tf_op jit(solution)/shard_map/ppermute | solution.py:25
  24.6 2.0 %collective-permute-done.4 = bf16[512,512]{1,0:T(8,128)(2,1)} collective-permute-done((bf16[512,512]{1,0:T(8,128)(2,1)S(1)}, bf16[512,512]{1,0:T(8,128)(2,1)}, u32[]{:S(2)}, u32[]{:S(2)}) %collective-permute-start.4) | collective-permute-done | bytes 524320 | tf_op jit(solution)/shard_map/ppermute | solution.py:25
  26.6 1.2 pad_maximum_fusion.1
  27.9 1.3 convolution_convert_fusion.2
  29.1 0.5 convolution_convert_fusion.1
  29.7 1.4 collective-permute-start.6
  31.1 1.5 %collective-permute-start.7 = (bf16[128,1280]{1,0:T(8,128)(2,1)S(1)}, bf16[128,1280]{1,0:T(8,128)(2,1)}, u32[]{:S(2)}, u32[]{:S(2)}) collective-permute-start(bf16[128,1280]{1,0:T(8,128)(2,1)S(1)} %convolution_convert_fusion.1), channel_id=1, source_target_pairs={{0,3},{1,0},{2,1},{3,2},{4,7},{5,4},{6,5},{7,6},{8,11},{9,8},{10,9... | collective-permute-start | bytes 983048 | tf_op jit(solution)/shard_map/ppermute | solution.py:25
  32.6 1.3 convolution_convert_fusion
  33.9 1.5 %collective-permute-start.8 = (bf16[128,1280]{1,0:T(8,128)(2,1)}, bf16[128,1280]{1,0:T(8,128)(2,1)}, u32[]{:S(2)}, u32[]{:S(2)}) collective-permute-start(bf16[128,1280]{1,0:T(8,128)(2,1)} %convolution_convert_fusion), channel_id=1, source_target_pairs={{0,2},{1,3},{2,0},{3,1},{4,6},{5,7},{6,4},{7,5},{8,10},{9,11},{10,... | collective-permute-start | bytes 983048 | tf_op jit(solution)/shard_map/ppermute | solution.py:25
  35.4 0.5 convolution_convert_fusion.3
  36.0 0.1 fusion.10
  36.1 2.8 %collective-permute-done.6 = bf16[128,1280]{1,0:T(8,128)(2,1)} collective-permute-done((bf16[128,1280]{1,0:T(8,128)(2,1)}, bf16[128,1280]{1,0:T(8,128)(2,1)}, u32[]{:S(2)}, u32[]{:S(2)}) %collective-permute-start.6) | collective-permute-done | bytes 327712 | tf_op jit(solution)/shard_map/ppermute | solution.py:25
  38.9 8.1 %collective-permute-done.8 = bf16[128,1280]{1,0:T(8,128)(2,1)} collective-permute-done((bf16[128,1280]{1,0:T(8,128)(2,1)}, bf16[128,1280]{1,0:T(8,128)(2,1)}, u32[]{:S(2)}, u32[]{:S(2)}) %collective-permute-start.8) | collective-permute-done | bytes 327712 | tf_op jit(solution)/shard_map/ppermute | solution.py:25
  47.0 1.3 add_convert_fusion
  48.4 5.3 %collective-permute-start.10 = (bf16[32,2048]{1,0:T(8,128)(2,1)S(1)}, bf16[32,2048]{1,0:T(8,128)(2,1)S(1)}, u32[]{:S(2)}, u32[]{:S(2)}) collective-permute-start(bf16[32,2048]{1,0:T(8,128)(2,1)S(1)} %get-tuple-element.45), channel_id=1, source_target_pairs={{0,12},{4,0},{8,4},{12,8},{1,13},{5,1},{9,5},{13,9},{2,14},{6,2},{... | collective-permute-start | bytes 393224 | tf_op jit(solution)/shard_map/ppermute | solution.py:25
  53.7 1.0 collective-permute-start.11
  54.7 2.3 %collective-permute-start.9 = (bf16[32,2048]{1,0:T(8,128)(2,1)S(1)}, bf16[32,2048]{1,0:T(8,128)(2,1)}, u32[]{:S(2)}, u32[]{:S(2)}) collective-permute-start(bf16[32,2048]{1,0:T(8,128)(2,1)S(1)} %get-tuple-element.43), channel_id=1, source_target_pairs={{0,4},{4,8},{8,12},{12,0},{1,5},{5,9},{9,13},{13,1},{2,6},{6,10},{... | collective-permute-start | bytes 393224 | tf_op jit(solution)/shard_map/ppermute | solution.py:25
  57.0 5.8 %collective-permute-done.11 = bf16[32,2048]{1,0:T(8,128)(2,1)S(1)} collective-permute-done((bf16[32,2048]{1,0:T(8,128)(2,1)S(1)}, bf16[32,2048]{1,0:T(8,128)(2,1)S(1)}, u32[]{:S(2)}, u32[]{:S(2)}) %collective-permute-start.11) | collective-permute-done | bytes 131104 | tf_op jit(solution)/shard_map/ppermute | solution.py:25
  62.8 1.6 %collective-permute-done.9 = bf16[32,2048]{1,0:T(8,128)(2,1)} collective-permute-done((bf16[32,2048]{1,0:T(8,128)(2,1)S(1)}, bf16[32,2048]{1,0:T(8,128)(2,1)}, u32[]{:S(2)}, u32[]{:S(2)}) %collective-permute-start.9) | collective-permute-done | bytes 131104 | tf_op jit(solution)/shard_map/ppermute | solution.py:25
  64.5 1.0 add_convert_fusion.2
  65.4 15.1 %all_gather.3 = bf16[128,2048]{1,0:T(8,128)(2,1)S(1)} all-gather(bf16[32,2048]{1,0:T(8,128)(2,1)S(1)} %add_convert_fusion.2), channel_id=1, replica_groups=mesh['x'=4,'zl'=2,'core'=2,'zh'=4,'y'=4] {'zh'}, dimensions={0}, use_global_device_ids=true | all-gather | bytes 655360 | tf_op jit(solution)/shard_map/all_gather | solution.py:91
  80.5 1.0 collective-permute-start.12
  81.5 0.5 collective-permute-start.13
  82.0 0.4 fusion.35
  82.5 8.3 %collective-permute-done.13 = bf16[128,2048]{1,0:T(8,128)(2,1)S(1)} collective-permute-done((bf16[128,2048]{1,0:T(8,128)(2,1)S(1)}, bf16[128,2048]{1,0:T(8,128)(2,1)S(1)}, u32[]{:S(2)}, u32[]{:S(2)}) %collective-permute-start.13) | collective-permute-done | bytes 524320 | tf_op jit(solution)/shard_map/ppermute | solution.py:25
  90.8 0.1 collective-permute-start.15
  90.9 1.5 %collective-permute-start.16 = (bf16[64,2048]{1,0:T(8,128)(2,1)S(1)}, bf16[64,2048]{1,0:T(8,128)(2,1)S(1)}, u32[]{:S(2)}, u32[]{:S(2)}) collective-permute-start(bf16[64,2048]{1,0:T(8,128)(2,1)S(1)} %slice.113), channel_id=1, source_target_pairs={{0,1},{1,2},{2,3},{3,0},{4,5},{5,6},{6,7},{7,4},{8,9},{9,10},{10,1... | collective-permute-start | bytes 786440 | tf_op jit(solution)/shard_map/ppermute | solution.py:25
  92.4 0.4 fusion.34
  92.8 0.4 fusion.33
  93.4 11.9 %collective-permute-start.14 = (f32[192,512]{1,0:T(8,128)S(1)}, f32[192,512]{1,0:T(8,128)S(1)}, u32[]{:S(2)}, u32[]{:S(2)}) collective-permute-start(f32[192,512]{1,0:T(8,128)S(1)} %pad_maximum_fusion.6), channel_id=1, source_target_pairs={{0,16},{16,0},{1,17},{17,1},{2,18},{18,2},{3,19},{19,3},{4,20},{20... | collective-permute-start | bytes 1179656 | tf_op jit(solution)/shard_map/ppermute | solution.py:21
  105.4 0.5 fusion.32
  105.9 4.6 %collective-permute-start.17 = (f32[64,512]{1,0:T(8,128)S(1)}, f32[64,512]{1,0:T(8,128)S(1)}, u32[]{:S(2)}, u32[]{:S(2)}) collective-permute-start(f32[64,512]{1,0:T(8,128)S(1)} %fusion.32), channel_id=1, source_target_pairs={{0,16},{16,0},{1,17},{17,1},{2,18},{18,2},{3,19},{19,3},{4,20},{20... | collective-permute-start | bytes 393224 | tf_op jit(solution)/shard_map/ppermute | solution.py:21
  110.7 0.8 collective-permute-done.17
  111.5 0.5 constant_dynamic-update-slice_fusion.8
  112.1 0.1 collective-permute-start.18
  112.2 1.1 collective-permute-start.19
  113.4 6.3 %collective-permute-done.18 = bf16[256,512]{1,0:T(8,128)(2,1)S(1)} collective-permute-done((bf16[256,512]{1,0:T(8,128)(2,1)S(1)}, bf16[256,512]{1,0:T(8,128)(2,1)S(1)}, u32[]{:S(2)}, u32[]{:S(2)}) %collective-permute-start.18) | collective-permute-done | bytes 262176 | tf_op jit(solution)/shard_map/ppermute | solution.py:21
  119.7 1.7 %collective-permute-start.20 = (bf16[512,512]{1,0:T(8,128)(2,1)S(1)}, bf16[512,512]{1,0:T(8,128)(2,1)S(1)}, u32[]{:S(2)}, u32[]{:S(2)}) collective-permute-start(bf16[512,512]{1,0:T(8,128)(2,1)S(1)} %pad_maximum_fusion.5), channel_id=1, source_target_pairs={{0,192},{64,0},{128,64},{192,128},{1,193},{65,1},{129,65},{193,129... | collective-permute-start | bytes 1572872 | tf_op jit(solution)/shard_map/ppermute | solution.py:25
  121.5 1.1 collective-permute-start.22
  122.7 5.0 %collective-permute-done.22 = bf16[256,512]{1,0:T(8,128)(2,1)S(1)} collective-permute-done((bf16[256,512]{1,0:T(8,128)(2,1)S(1)}, bf16[256,512]{1,0:T(8,128)(2,1)S(1)}, u32[]{:S(2)}, u32[]{:S(2)}) %collective-permute-start.22) | collective-permute-done | bytes 262176 | tf_op jit(solution)/shard_map/ppermute | solution.py:21
  127.7 4.4 %collective-permute-done.20 = bf16[512,512]{1,0:T(8,128)(2,1)S(1)} collective-permute-done((bf16[512,512]{1,0:T(8,128)(2,1)S(1)}, bf16[512,512]{1,0:T(8,128)(2,1)S(1)}, u32[]{:S(2)}, u32[]{:S(2)}) %collective-permute-start.20) | collective-permute-done | bytes 524320 | tf_op jit(solution)/shard_map/ppermute | solution.py:25
  132.0 2.9 %collective-permute-done.21 = bf16[512,512]{1,0:T(8,128)(2,1)S(1)} collective-permute-done((bf16[512,512]{1,0:T(8,128)(2,1)S(1)}, bf16[512,512]{1,0:T(8,128)(2,1)S(1)}, u32[]{:S(2)}, u32[]{:S(2)}) %collective-permute-start.21) | collective-permute-done | bytes 524320 | tf_op jit(solution)/shard_map/ppermute | solution.py:25
  135.1 0.5 fusion.2
  135.6 0.4 convolution_add_fusion
  136.0 2.2 %collective-permute-start.23 = (f32[256,512]{1,0:T(8,128)S(1)}, f32[256,512]{1,0:T(8,128)S(1)}, u32[]{:S(2)}, u32[]{:S(2)}) collective-permute-start(f32[256,512]{1,0:T(8,128)S(1)} %convolution_add_fusion), channel_id=1, source_target_pairs={{0,16},{16,0},{1,17},{17,1},{2,18},{18,2},{3,19},{19,3},{4,20},{20... | collective-permute-start | bytes 1572872 | tf_op jit(solution)/shard_map/ppermute | solution.py:21
  138.2 0.5 fusion.4
  138.7 1.0 collective-permute-done.23
  139.7 1.2 add_multiply_fusion
  (54 shorter events, 0.9 us)
Async XLA Ops:
  0.0 11.5 %copy-start = (bf16[256,512]{1,0:T(8,128)(2,1)S(1)}, bf16[256,512]{1,0:T(8,128)(2,1)}, u32[]{:S(2)}) copy-start(bf16[256,512]{1,0:T(8,128)(2,1)} %param.1) | copy-start | bytes 786436
  0.0 6.9 %collective-permute-start.1 = (bf16[256,512]{1,0:T(8,128)(2,1)}, bf16[256,512]{1,0:T(8,128)(2,1)S(1)}, u32[]{:S(2)}, u32[]{:S(2)}) collective-permute-start(bf16[256,512]{1,0:T(8,128)(2,1)} %param.1), channel_id=1, source_target_pairs={{0,16},{16,0},{1,17},{17,1},{2,18},{18,2},{3,19},{19,3},{4,20},{20... | collective-permute-start | bytes 786440 | tf_op jit(solution)/shard_map/ppermute | solution.py:21
  3.2 8.3 %collective-permute-start = (bf16[256,512]{1,0:T(8,128)(2,1)}, bf16[256,512]{1,0:T(8,128)(2,1)S(1)}, u32[]{:S(2)}, u32[]{:S(2)}) collective-permute-start(bf16[256,512]{1,0:T(8,128)(2,1)} %param.1), channel_id=1, source_target_pairs={{0,32},{32,0},{1,33},{33,1},{2,34},{34,2},{3,35},{35,3},{4,36},{36... | collective-permute-start | bytes 786440 | tf_op jit(solution)/shard_map/ppermute | solution.py:21
  3.2 9.9 %collective-permute-start.2 = (bf16[256,512]{1,0:T(8,128)(2,1)}, bf16[256,512]{1,0:T(8,128)(2,1)}, u32[]{:S(2)}, u32[]{:S(2)}) collective-permute-start(bf16[256,512]{1,0:T(8,128)(2,1)} %param.1), channel_id=1, source_target_pairs={{0,128},{64,192},{128,0},{192,64},{1,129},{65,193},{129,1},{193,65... | collective-permute-start | bytes 786440 | tf_op jit(solution)/shard_map/ppermute | solution.py:25
  11.6 13.0 %collective-permute-start.3 = (bf16[512,512]{1,0:T(8,128)(2,1)S(1)}, bf16[512,512]{1,0:T(8,128)(2,1)S(1)}, u32[]{:S(2)}, u32[]{:S(2)}) collective-permute-start(bf16[512,512]{1,0:T(8,128)(2,1)S(1)} %pad_maximum_fusion.3), channel_id=1, source_target_pairs={{0,192},{64,0},{128,64},{192,128},{1,193},{65,1},{129,65},{193,129... | collective-permute-start | bytes 1572872 | tf_op jit(solution)/shard_map/ppermute | solution.py:25
  12.7 13.9 %collective-permute-start.4 = (bf16[512,512]{1,0:T(8,128)(2,1)S(1)}, bf16[512,512]{1,0:T(8,128)(2,1)}, u32[]{:S(2)}, u32[]{:S(2)}) collective-permute-start(bf16[512,512]{1,0:T(8,128)(2,1)S(1)} %pad_maximum_fusion.3), channel_id=1, source_target_pairs={{0,64},{64,128},{128,192},{192,0},{1,65},{65,129},{129,193},{193,1... | collective-permute-start | bytes 1572872 | tf_op jit(solution)/shard_map/ppermute | solution.py:25
  14.2 2.6 %copy-start.1 = (bf16[768,512]{1,0:T(8,128)(2,1)}, bf16[768,512]{1,0:T(8,128)(2,1)S(1)}, u32[]{:S(2)}) copy-start(bf16[768,512]{1,0:T(8,128)(2,1)S(1)} %pad_maximum_fusion.2) | copy-start | bytes 2359300
  14.2 7.0 %collective-permute-start.5 = (bf16[256,512]{1,0:T(8,128)(2,1)}, bf16[256,512]{1,0:T(8,128)(2,1)}, u32[]{:S(2)}, u32[]{:S(2)}) collective-permute-start(bf16[256,512]{1,0:T(8,128)(2,1)} %collective-permute-done.2), channel_id=1, source_target_pairs={{0,32},{32,0},{1,33},{33,1},{2,34},{34,2},{3,35},{35,3},{4,36},{36... | collective-permute-start | bytes 786440 | tf_op jit(solution)/shard_map/ppermute | solution.py:21
  16.8 19.2 %all-to-all-start = ((bf16[4,128,768]{2,1,0:T(8,128)(2,1)}), bf16[4,128,768]{2,1,0:T(8,128)(2,1)S(1)}, u32[]{:S(2)}, u32[]{:S(2)}) async-start(bf16[4,128,768]{2,1,0:T(8,128)(2,1)} %bitcast.18), calls=%async_computation | async-start | bytes 1572864 | tf_op jit(solution)/shard_map/all_to_all | solution.py:83
  29.7 9.2 %collective-permute-start.6 = (bf16[128,1280]{1,0:T(8,128)(2,1)}, bf16[128,1280]{1,0:T(8,128)(2,1)}, u32[]{:S(2)}, u32[]{:S(2)}) collective-permute-start(bf16[128,1280]{1,0:T(8,128)(2,1)} %convolution_convert_fusion.2), channel_id=1, source_target_pairs={{0,1},{1,2},{2,3},{3,0},{4,5},{5,6},{6,7},{7,4},{8,9},{9,10},{10,1... | collective-permute-start | bytes 983048 | tf_op jit(solution)/shard_map/ppermute | solution.py:25
  31.1 7.8 %collective-permute-start.7 = (bf16[128,1280]{1,0:T(8,128)(2,1)S(1)}, bf16[128,1280]{1,0:T(8,128)(2,1)}, u32[]{:S(2)}, u32[]{:S(2)}) collective-permute-start(bf16[128,1280]{1,0:T(8,128)(2,1)S(1)} %convolution_convert_fusion.1), channel_id=1, source_target_pairs={{0,3},{1,0},{2,1},{3,2},{4,7},{5,4},{6,5},{7,6},{8,11},{9,8},{10,9... | collective-permute-start | bytes 983048 | tf_op jit(solution)/shard_map/ppermute | solution.py:25
  33.9 13.1 %collective-permute-start.8 = (bf16[128,1280]{1,0:T(8,128)(2,1)}, bf16[128,1280]{1,0:T(8,128)(2,1)}, u32[]{:S(2)}, u32[]{:S(2)}) collective-permute-start(bf16[128,1280]{1,0:T(8,128)(2,1)} %convolution_convert_fusion), channel_id=1, source_target_pairs={{0,2},{1,3},{2,0},{3,1},{4,6},{5,7},{6,4},{7,5},{8,10},{9,11},{10,... | collective-permute-start | bytes 983048 | tf_op jit(solution)/shard_map/ppermute | solution.py:25
  36.1 45.9 %copy-start.2 = (bf16[768,512]{1,0:T(8,128)(2,1)S(1)}, bf16[768,512]{1,0:T(8,128)(2,1)}, u32[]{:S(2)}) copy-start(bf16[768,512]{1,0:T(8,128)(2,1)} %copy-done.1) | copy-start | bytes 2359300
  48.4 8.6 %collective-permute-start.10 = (bf16[32,2048]{1,0:T(8,128)(2,1)S(1)}, bf16[32,2048]{1,0:T(8,128)(2,1)S(1)}, u32[]{:S(2)}, u32[]{:S(2)}) collective-permute-start(bf16[32,2048]{1,0:T(8,128)(2,1)S(1)} %get-tuple-element.45), channel_id=1, source_target_pairs={{0,12},{4,0},{8,4},{12,8},{1,13},{5,1},{9,5},{13,9},{2,14},{6,2},{... | collective-permute-start | bytes 393224 | tf_op jit(solution)/shard_map/ppermute | solution.py:25
  53.7 9.1 %collective-permute-start.11 = (bf16[32,2048]{1,0:T(8,128)(2,1)S(1)}, bf16[32,2048]{1,0:T(8,128)(2,1)S(1)}, u32[]{:S(2)}, u32[]{:S(2)}) collective-permute-start(bf16[32,2048]{1,0:T(8,128)(2,1)S(1)} %get-tuple-element.44), channel_id=1, source_target_pairs={{0,8},{4,12},{8,0},{12,4},{1,9},{5,13},{9,1},{13,5},{2,10},{6,14},... | collective-permute-start | bytes 393224 | tf_op jit(solution)/shard_map/ppermute | solution.py:25
  54.7 9.7 %collective-permute-start.9 = (bf16[32,2048]{1,0:T(8,128)(2,1)S(1)}, bf16[32,2048]{1,0:T(8,128)(2,1)}, u32[]{:S(2)}, u32[]{:S(2)}) collective-permute-start(bf16[32,2048]{1,0:T(8,128)(2,1)S(1)} %get-tuple-element.43), channel_id=1, source_target_pairs={{0,4},{4,8},{8,12},{12,0},{1,5},{5,9},{9,13},{13,1},{2,6},{6,10},{... | collective-permute-start | bytes 393224 | tf_op jit(solution)/shard_map/ppermute | solution.py:25
  80.5 10.3 %collective-permute-start.12 = (bf16[128,2048]{1,0:T(8,128)(2,1)S(1)}, bf16[128,2048]{1,0:T(8,128)(2,1)S(1)}, u32[]{:S(2)}, u32[]{:S(2)}) collective-permute-start(bf16[128,2048]{1,0:T(8,128)(2,1)S(1)} %all_gather.3), channel_id=1, source_target_pairs={{0,3},{1,0},{2,1},{3,2},{4,7},{5,4},{6,5},{7,6},{8,11},{9,8},{10,9... | collective-permute-start | bytes 1572872 | tf_op jit(solution)/shard_map/ppermute | solution.py:25
  81.5 9.2 %collective-permute-start.13 = (bf16[128,2048]{1,0:T(8,128)(2,1)S(1)}, bf16[128,2048]{1,0:T(8,128)(2,1)S(1)}, u32[]{:S(2)}, u32[]{:S(2)}) collective-permute-start(bf16[128,2048]{1,0:T(8,128)(2,1)S(1)} %all_gather.3), channel_id=1, source_target_pairs={{0,1},{1,2},{2,3},{3,0},{4,5},{5,6},{6,7},{7,4},{8,9},{9,10},{10,1... | collective-permute-start | bytes 1572872 | tf_op jit(solution)/shard_map/ppermute | solution.py:25
  90.8 14.5 %collective-permute-start.15 = (bf16[64,2048]{1,0:T(8,128)(2,1)S(1)}, bf16[64,2048]{1,0:T(8,128)(2,1)S(1)}, u32[]{:S(2)}, u32[]{:S(2)}) collective-permute-start(bf16[64,2048]{1,0:T(8,128)(2,1)S(1)} %get-tuple-element.20), channel_id=1, source_target_pairs={{0,3},{1,0},{2,1},{3,2},{4,7},{5,4},{6,5},{7,6},{8,11},{9,8},{10,9... | collective-permute-start | bytes 786440 | tf_op jit(solution)/shard_map/ppermute | solution.py:25
  90.9 14.4 %collective-permute-start.16 = (bf16[64,2048]{1,0:T(8,128)(2,1)S(1)}, bf16[64,2048]{1,0:T(8,128)(2,1)S(1)}, u32[]{:S(2)}, u32[]{:S(2)}) collective-permute-start(bf16[64,2048]{1,0:T(8,128)(2,1)S(1)} %slice.113), channel_id=1, source_target_pairs={{0,1},{1,2},{2,3},{3,0},{4,5},{5,6},{6,7},{7,4},{8,9},{9,10},{10,1... | collective-permute-start | bytes 786440 | tf_op jit(solution)/shard_map/ppermute | solution.py:25
  93.4 17.2 %collective-permute-start.14 = (f32[192,512]{1,0:T(8,128)S(1)}, f32[192,512]{1,0:T(8,128)S(1)}, u32[]{:S(2)}, u32[]{:S(2)}) collective-permute-start(f32[192,512]{1,0:T(8,128)S(1)} %pad_maximum_fusion.6), channel_id=1, source_target_pairs={{0,16},{16,0},{1,17},{17,1},{2,18},{18,2},{3,19},{19,3},{4,20},{20... | collective-permute-start | bytes 1179656 | tf_op jit(solution)/shard_map/ppermute | solution.py:21
  105.9 5.6 %collective-permute-start.17 = (f32[64,512]{1,0:T(8,128)S(1)}, f32[64,512]{1,0:T(8,128)S(1)}, u32[]{:S(2)}, u32[]{:S(2)}) collective-permute-start(f32[64,512]{1,0:T(8,128)S(1)} %fusion.32), channel_id=1, source_target_pairs={{0,16},{16,0},{1,17},{17,1},{2,18},{18,2},{3,19},{19,3},{4,20},{20... | collective-permute-start | bytes 393224 | tf_op jit(solution)/shard_map/ppermute | solution.py:21
  112.1 7.6 %collective-permute-start.18 = (bf16[256,512]{1,0:T(8,128)(2,1)S(1)}, bf16[256,512]{1,0:T(8,128)(2,1)S(1)}, u32[]{:S(2)}, u32[]{:S(2)}) collective-permute-start(bf16[256,512]{1,0:T(8,128)(2,1)S(1)} %dynamic-slice_convert_fusion), channel_id=1, source_target_pairs={{0,32},{32,0},{1,33},{33,1},{2,34},{34,2},{3,35},{35,3},{4,36},{36... | collective-permute-start | bytes 786440 | tf_op jit(solution)/shard_map/ppermute | solution.py:21
  112.2 9.3 %collective-permute-start.19 = (bf16[256,512]{1,0:T(8,128)(2,1)S(1)}, bf16[256,512]{1,0:T(8,128)(2,1)S(1)}, u32[]{:S(2)}, u32[]{:S(2)}) collective-permute-start(bf16[256,512]{1,0:T(8,128)(2,1)S(1)} %dynamic-slice_convert_fusion), channel_id=1, source_target_pairs={{0,128},{64,192},{128,0},{192,64},{1,129},{65,193},{129,1},{193,65... | collective-permute-start | bytes 786440 | tf_op jit(solution)/shard_map/ppermute | solution.py:25
  119.7 12.3 %collective-permute-start.20 = (bf16[512,512]{1,0:T(8,128)(2,1)S(1)}, bf16[512,512]{1,0:T(8,128)(2,1)S(1)}, u32[]{:S(2)}, u32[]{:S(2)}) collective-permute-start(bf16[512,512]{1,0:T(8,128)(2,1)S(1)} %pad_maximum_fusion.5), channel_id=1, source_target_pairs={{0,192},{64,0},{128,64},{192,128},{1,193},{65,1},{129,65},{193,129... | collective-permute-start | bytes 1572872 | tf_op jit(solution)/shard_map/ppermute | solution.py:25
  121.5 13.5 %collective-permute-start.21 = (bf16[512,512]{1,0:T(8,128)(2,1)S(1)}, bf16[512,512]{1,0:T(8,128)(2,1)S(1)}, u32[]{:S(2)}, u32[]{:S(2)}) collective-permute-start(bf16[512,512]{1,0:T(8,128)(2,1)S(1)} %pad_maximum_fusion.5), channel_id=1, source_target_pairs={{0,64},{64,128},{128,192},{192,0},{1,65},{65,129},{129,193},{193,1... | collective-permute-start | bytes 1572872 | tf_op jit(solution)/shard_map/ppermute | solution.py:25
  121.5 6.2 %collective-permute-start.22 = (bf16[256,512]{1,0:T(8,128)(2,1)S(1)}, bf16[256,512]{1,0:T(8,128)(2,1)S(1)}, u32[]{:S(2)}, u32[]{:S(2)}) collective-permute-start(bf16[256,512]{1,0:T(8,128)(2,1)S(1)} %collective-permute-done.19), channel_id=1, source_target_pairs={{0,32},{32,0},{1,33},{33,1},{2,34},{34,2},{3,35},{35,3},{4,36},{36... | collective-permute-start | bytes 786440 | tf_op jit(solution)/shard_map/ppermute | solution.py:21
  136.0 3.7 %collective-permute-start.23 = (f32[256,512]{1,0:T(8,128)S(1)}, f32[256,512]{1,0:T(8,128)S(1)}, u32[]{:S(2)}, u32[]{:S(2)}) collective-permute-start(f32[256,512]{1,0:T(8,128)S(1)} %convolution_add_fusion), channel_id=1, source_target_pairs={{0,16},{16,0},{1,17},{17,1},{2,18},{18,2},{3,19},{19,3},{4,20},{20... | collective-permute-start | bytes 1572872 | tf_op jit(solution)/shard_map/ppermute | solution.py:21

commit v17 on v16

--- a/solution.py
+++ b/solution.py
@@ -68,13 +68,12 @@
 
 
 def per_device(iterate):
-    y, zh = lax.axis_index("y"), lax.axis_index("zh")
+    y = lax.axis_index("y")
     back = lax.rem(4 - y, 4)
     other = swap(iterate, "core")
     pair, far = pair_of(iterate)
 
     own = [jnp.concatenate(rows, axis=0) for rows in zip(chunks(iterate), chunks(other))]
-    own = [window(chunks(rows), zh, 4) for rows in own]
     own, turned = jnp.concatenate(own, axis=0), window(own, y, 4)
     pair, own, turned = lax.optimization_barrier((pair, own, turned))
     early = lax.optimization_barrier(jnp.concatenate([pair, far], axis=0))
@@ -87,7 +86,7 @@
     second = add(scatter(pieces, "y"))
     part = jnp.concatenate([first, second], axis=1)
     panel = jnp.concatenate([early, panel], axis=0)
-    part = add(scatter(chunks(part), "zh"))
+    part = add(lax.all_to_all(part.reshape(4, 32, 2048), "zh", 0, 0))
     near = lax.all_gather(part, "zh", axis=0, tiled=True)
     after, before = fetch(near, "y", 1), fetch(near, "y", 3)
     sent = lax.optimization_barrier((after[:64], before[64:]))

time: 141 us -> 144 us (1.021)
  local copies, waits for them, and re-layouts: 1.64 us -> 5.88 us
    all_to_all x0 -> x1, waiting for transfers between devices: none -> 9.88 us  [per_device(): part = add(lax.all_to_all(part.reshape(4, 32, 2048), 'zh', 0, 0))]
    ppermute x16 -> x13, starting transfers between devices: 23.1 us -> 14.2 us  [send(): lax.ppermute(array, axis, [(i, (i + k) % 4) for i in range(4)])]
    ppermute x16 -> x13, waiting for transfers between devices: 39.4 us -> 31.6 us  [send(): lax.ppermute(array, axis, [(i, (i + k) % 4) for i in range(4)])]
    all_to_all x0 -> x1, starting transfers between devices: none -> 7.41 us  [per_device(): part = add(lax.all_to_all(part.reshape(4, 32, 2048), 'zh', 0, 0))]
    unnamed x24 -> x37, local copies, waits for them, and re-layouts: 0.44 us -> 5.62 us
    ppermute x8, waiting for transfers between devices: 16.8 us -> 14.1 us  [swap(): return lax.ppermute(array, axis, [(0, 1), (1, 0)])]
    ppermute x8, starting transfers between devices: 24.2 us -> 26.5 us  [swap(): return lax.ppermute(array, axis, [(0, 1), (1, 0)])]
  transfers between devices with their start and end apart: 25 -> 23, of which waited for: 15 -> 14; matrix products, arithmetic and copies ran while one was open for 9% -> 11% of each run, Pallas kernels for 0% -> 0%
where the time goes in v17:
time: 144 us; the launch traced here: 143 us
  waiting for transfers between devices  55.6 us (39%)
  starting transfers between devices  52.1 us (36%)
  blocking collectives  14.2 us (10%)
  matrix products  10.1 us (7%)
  local copies, waits for them, and re-layouts  5.88 us (4%)
  other arithmetic  4.71 us (3%)
    ppermute x13, waiting for transfers between devices, send(): lax.ppermute(array, axis, [(i, (i + k) % 4) for i in range(4)])  31.6 us
    ppermute x8, starting transfers between devices, swap(): return lax.ppermute(array, axis, [(0, 1), (1, 0)])  26.5 us
    ppermute x13, starting transfers between devices, send(): lax.ppermute(array, axis, [(i, (i + k) % 4) for i in range(4)])  14.2 us
    all_gather x1, blocking collectives, per_device(): near = lax.all_gather(part, 'zh', axis=0, tiled=True)  14.2 us
    ppermute x8, waiting for transfers between devices, swap(): return lax.ppermute(array, axis, [(0, 1), (1, 0)])  14.1 us
    dot_general x14, matrix products, matmul(): return lax.dot_general(a, b, (dims, ((), ())), preferred_element_type=F32)  10.1 us
    all_to_all x1, waiting for transfers between devices, per_device(): part = add(lax.all_to_all(part.reshape(4, 32, 2048), 'zh', 0, 0))  9.88 us
    all_to_all x1, starting transfers between devices, per_device(): part = add(lax.all_to_all(part.reshape(4, 32, 2048), 'zh', 0, 0))  7.41 us
  transfers between devices with their start and end apart: 23, of which 14 were waited for; matrix products, arithmetic and copies ran while one was open for 11% of the time, Pallas kernels for 0%

profile of v17, /device:TPU:1, one launch (start us, length us, event | category | flops | bytes accessed | tf_op | source)
XLA Modules:
  0.0 143.1 jit_solution(10675992490098108735)
XLA Ops:
  0.0 3.2 %collective-permute-start.1 = (bf16[256,512]{1,0:T(8,128)(2,1)}, bf16[256,512]{1,0:T(8,128)(2,1)S(1)}, u32[]{:S(2)}, u32[]{:S(2)}) collective-permute-start(bf16[256,512]{1,0:T(8,128)(2,1)} %param.1), channel_id=1, source_target_pairs={{0,16},{16,0},{1,17},{17,1},{2,18},{18,2},{3,19},{19,3},{4,20},{20... | collective-permute-start | bytes 786440 | tf_op jit(solution)/shard_map/ppermute | solution.py:21
  3.2 2.7 %collective-permute-start.2 = (bf16[256,512]{1,0:T(8,128)(2,1)}, bf16[256,512]{1,0:T(8,128)(2,1)}, u32[]{:S(2)}, u32[]{:S(2)}) collective-permute-start(bf16[256,512]{1,0:T(8,128)(2,1)} %param.1), channel_id=1, source_target_pairs={{0,128},{64,192},{128,0},{192,64},{1,129},{65,193},{129,1},{193,65... | collective-permute-start | bytes 786440 | tf_op jit(solution)/shard_map/ppermute | solution.py:25
  5.9 0.9 constant_dynamic-update-slice_fusion.21
  6.8 0.8 constant_dynamic-update-slice_fusion.19
  7.7 0.8 constant_dynamic-update-slice_fusion.17
  8.5 0.8 constant_dynamic-update-slice_fusion.15
  9.4 0.9 constant_dynamic-update-slice_fusion.13
  10.2 0.9 constant_dynamic-update-slice_fusion.11
  11.2 0.3 collective-permute-done
  11.5 1.1 collective-permute-start.3
  12.6 0.4 collective-permute-start.4
  13.1 0.0 collective-permute-done.2
  13.1 1.0 pad_maximum_fusion.2
  14.1 1.2 collective-permute-start.5
  15.3 1.5 %convolution_convert_fusion.4 = bf16[512,768]{1,0:T(8,128)(2,1)} fusion(bf16[512,512]{1,0:T(8,128)(2,1)S(1)} %get-tuple-element.17, bf16[768,512]{1,0:T(8,128)(2,1)S(1)} %pad_maximum_fusion.2), kind=kOutput, calls=%fused_computation.5 | convolution fusion | flops 403046400 | bytes 2097152 | tf_op jit(solution)/shard_map/dot_general | solution.py:52
  16.8 4.0 %all-to-all-start = ((bf16[4,128,768]{2,1,0:T(8,128)(2,1)}), bf16[4,128,768]{2,1,0:T(8,128)(2,1)S(1)}, u32[]{:S(2)}, u32[]{:S(2)}) async-start(bf16[4,128,768]{2,1,0:T(8,128)(2,1)} %bitcast.35), calls=%async_computation | async-start | bytes 1572864 | tf_op jit(solution)/shard_map/all_to_all | solution.py:82
  20.7 0.3 collective-permute-done.5
  21.1 3.4 %collective-permute-done.3 = bf16[512,512]{1,0:T(8,128)(2,1)S(1)} collective-permute-done((bf16[512,512]{1,0:T(8,128)(2,1)S(1)}, bf16[512,512]{1,0:T(8,128)(2,1)S(1)}, u32[]{:S(2)}, u32[]{:S(2)}) %collective-permute-start.3) | collective-permute-done | bytes 524320 | tf_op jit(solution)/shard_map/ppermute | solution.py:25
  24.5 2.0 %collective-permute-done.4 = bf16[512,512]{1,0:T(8,128)(2,1)} collective-permute-done((bf16[512,512]{1,0:T(8,128)(2,1)S(1)}, bf16[512,512]{1,0:T(8,128)(2,1)}, u32[]{:S(2)}, u32[]{:S(2)}) %collective-permute-start.4) | collective-permute-done | bytes 524320 | tf_op jit(solution)/shard_map/ppermute | solution.py:25
  26.5 1.2 pad_maximum_fusion.1
  27.7 1.3 convolution_convert_fusion.2
  29.0 0.5 convolution_convert_fusion.1
  29.6 1.4 collective-permute-start.6
  31.0 1.5 %collective-permute-start.7 = (bf16[128,1280]{1,0:T(8,128)(2,1)S(1)}, bf16[128,1280]{1,0:T(8,128)(2,1)}, u32[]{:S(2)}, u32[]{:S(2)}) collective-permute-start(bf16[128,1280]{1,0:T(8,128)(2,1)S(1)} %convolution_convert_fusion.1), channel_id=1, source_target_pairs={{0,3},{1,0},{2,1},{3,2},{4,7},{5,4},{6,5},{7,6},{8,11},{9,8},{10,9... | collective-permute-start | bytes 983048 | tf_op jit(solution)/shard_map/ppermute | solution.py:25
  32.5 1.3 convolution_convert_fusion
  33.8 1.5 %collective-permute-start.8 = (bf16[128,1280]{1,0:T(8,128)(2,1)}, bf16[128,1280]{1,0:T(8,128)(2,1)}, u32[]{:S(2)}, u32[]{:S(2)}) collective-permute-start(bf16[128,1280]{1,0:T(8,128)(2,1)} %convolution_convert_fusion), channel_id=1, source_target_pairs={{0,2},{1,3},{2,0},{3,1},{4,6},{5,7},{6,4},{7,5},{8,10},{9,11},{10,... | collective-permute-start | bytes 983048 | tf_op jit(solution)/shard_map/ppermute | solution.py:25
  35.3 0.5 convolution_convert_fusion.3
  35.9 0.1 fusion.14
  36.0 2.8 %collective-permute-done.6 = bf16[128,1280]{1,0:T(8,128)(2,1)} collective-permute-done((bf16[128,1280]{1,0:T(8,128)(2,1)}, bf16[128,1280]{1,0:T(8,128)(2,1)}, u32[]{:S(2)}, u32[]{:S(2)}) %collective-permute-start.6) | collective-permute-done | bytes 327712 | tf_op jit(solution)/shard_map/ppermute | solution.py:25
  38.8 8.1 %collective-permute-done.8 = bf16[128,1280]{1,0:T(8,128)(2,1)} collective-permute-done((bf16[128,1280]{1,0:T(8,128)(2,1)}, bf16[128,1280]{1,0:T(8,128)(2,1)}, u32[]{:S(2)}, u32[]{:S(2)}) %collective-permute-start.8) | collective-permute-done | bytes 327712 | tf_op jit(solution)/shard_map/ppermute | solution.py:25
  46.9 1.3 add_convert_fusion
  48.3 0.8 pad_maximum_fusion.4
  49.1 7.4 %all-to-all-start.1 = ((bf16[4,32,2048]{2,1,0:T(8,128)(2,1)}), bf16[4,32,2048]{2,1,0:T(8,128)(2,1)S(1)}, u32[]{:S(2)}, u32[]{:S(2)}) async-start(bf16[4,32,2048]{2,1,0:T(8,128)(2,1)} %bitcast.2), calls=%async_computation.1 | async-start | bytes 1048576 | tf_op jit(solution)/shard_map/all_to_all | solution.py:89
  56.5 9.9 %all-to-all-done.1 = bf16[4,32,2048]{2,1,0:T(8,128)(2,1)S(1)} async-done(((bf16[4,32,2048]{2,1,0:T(8,128)(2,1)}), bf16[4,32,2048]{2,1,0:T(8,128)(2,1)S(1)}, u32[]{:S(2)}, u32[]{:S(2)}) %all-to-all-start.1) | async-done | bytes 524320 | tf_op jit(solution)/shard_map/all_to_all | solution.py:89
  66.4 0.1 add_convert_fusion.2
  66.5 14.2 %all-gather = bf16[1,128,2048]{2,1,0:T(8,128)(2,1)S(1)} all-gather(bf16[1,32,2048]{2,1,0:T(8,128)(2,1)S(1)} %add_convert_fusion.2), channel_id=2, replica_groups=mesh['x'=4,'zl'=2,'core'=2,'zh'=4,'y'=4] {'zh'}, dimensions={1}, use_global_device_ids=true | all-gather | bytes 655360 | tf_op jit(solution)/shard_map/all_gather | solution.py:90
  80.7 1.1 collective-permute-start.9
  81.8 0.4 collective-permute-start.10
  82.1 0.4 fusion.21
  82.6 8.4 %collective-permute-done.10 = bf16[128,2048]{1,0:T(8,128)(2,1)S(1)} collective-permute-done((bf16[128,2048]{1,0:T(8,128)(2,1)S(1)}, bf16[128,2048]{1,0:T(8,128)(2,1)S(1)}, u32[]{:S(2)}, u32[]{:S(2)}) %collective-permute-start.10) | collective-permute-done | bytes 524320 | tf_op jit(solution)/shard_map/ppermute | solution.py:25
  91.1 0.1 collective-permute-start.12
  91.2 1.5 %collective-permute-start.13 = (bf16[64,2048]{1,0:T(8,128)(2,1)S(1)}, bf16[64,2048]{1,0:T(8,128)(2,1)S(1)}, u32[]{:S(2)}, u32[]{:S(2)}) collective-permute-start(bf16[64,2048]{1,0:T(8,128)(2,1)S(1)} %slice.87), channel_id=1, source_target_pairs={{0,1},{1,2},{2,3},{3,0},{4,5},{5,6},{6,7},{7,4},{8,9},{9,10},{10,1... | collective-permute-start | bytes 786440 | tf_op jit(solution)/shard_map/ppermute | solution.py:25
  92.6 0.4 fusion.25
  93.1 0.4 fusion.24
  93.6 13.4 %collective-permute-start.11 = (f32[192,512]{1,0:T(8,128)S(1)}, f32[192,512]{1,0:T(8,128)S(1)}, u32[]{:S(2)}, u32[]{:S(2)}) collective-permute-start(f32[192,512]{1,0:T(8,128)S(1)} %pad_maximum_fusion.6), channel_id=1, source_target_pairs={{0,16},{16,0},{1,17},{17,1},{2,18},{18,2},{3,19},{19,3},{4,20},{20... | collective-permute-start | bytes 1179656 | tf_op jit(solution)/shard_map/ppermute | solution.py:21
  107.2 0.5 fusion.23
  107.6 4.8 %collective-permute-start.14 = (f32[64,512]{1,0:T(8,128)S(1)}, f32[64,512]{1,0:T(8,128)S(1)}, u32[]{:S(2)}, u32[]{:S(2)}) collective-permute-start(f32[64,512]{1,0:T(8,128)S(1)} %fusion.23), channel_id=1, source_target_pairs={{0,16},{16,0},{1,17},{17,1},{2,18},{18,2},{3,19},{19,3},{4,20},{20... | collective-permute-start | bytes 393224 | tf_op jit(solution)/shard_map/ppermute | solution.py:21
  112.6 0.1 maximum_add_fusion
  112.7 0.8 collective-permute-done.14
  113.4 0.5 constant_dynamic-update-slice_fusion.23
  114.0 0.7 collective-permute-start.15
  114.7 0.7 collective-permute-start.16
  115.4 6.2 %collective-permute-done.15 = bf16[256,512]{1,0:T(8,128)(2,1)S(1)} collective-permute-done((bf16[256,512]{1,0:T(8,128)(2,1)S(1)}, bf16[256,512]{1,0:T(8,128)(2,1)S(1)}, u32[]{:S(2)}, u32[]{:S(2)}) %collective-permute-start.15) | collective-permute-done | bytes 262176 | tf_op jit(solution)/shard_map/ppermute | solution.py:21
  121.7 1.9 %collective-permute-start.17 = (bf16[512,512]{1,0:T(8,128)(2,1)S(1)}, bf16[512,512]{1,0:T(8,128)(2,1)S(1)}, u32[]{:S(2)}, u32[]{:S(2)}) collective-permute-start(bf16[512,512]{1,0:T(8,128)(2,1)S(1)} %pad_maximum_fusion.5), channel_id=1, source_target_pairs={{0,192},{64,0},{128,64},{192,128},{1,193},{65,1},{129,65},{193,129... | collective-permute-start | bytes 1572872 | tf_op jit(solution)/shard_map/ppermute | solution.py:25
  123.6 0.7 collective-permute-start.19
  124.4 5.6 %collective-permute-done.19 = bf16[256,512]{1,0:T(8,128)(2,1)S(1)} collective-permute-done((bf16[256,512]{1,0:T(8,128)(2,1)S(1)}, bf16[256,512]{1,0:T(8,128)(2,1)S(1)}, u32[]{:S(2)}, u32[]{:S(2)}) %collective-permute-start.19) | collective-permute-done | bytes 262176 | tf_op jit(solution)/shard_map/ppermute | solution.py:21
  129.9 4.1 %collective-permute-done.17 = bf16[512,512]{1,0:T(8,128)(2,1)S(1)} collective-permute-done((bf16[512,512]{1,0:T(8,128)(2,1)S(1)}, bf16[512,512]{1,0:T(8,128)(2,1)S(1)}, u32[]{:S(2)}, u32[]{:S(2)}) %collective-permute-start.17) | collective-permute-done | bytes 524320 | tf_op jit(solution)/shard_map/ppermute | solution.py:25
  134.0 2.7 %collective-permute-done.18 = bf16[512,512]{1,0:T(8,128)(2,1)S(1)} collective-permute-done((bf16[512,512]{1,0:T(8,128)(2,1)S(1)}, bf16[512,512]{1,0:T(8,128)(2,1)S(1)}, u32[]{:S(2)}, u32[]{:S(2)}) %collective-permute-start.18) | collective-permute-done | bytes 524320 | tf_op jit(solution)/shard_map/ppermute | solution.py:25
  136.9 0.5 fusion.2
  137.4 0.4 convolution_add_fusion
  137.8 2.5 %collective-permute-start.20 = (f32[256,512]{1,0:T(8,128)S(1)}, f32[256,512]{1,0:T(8,128)S(1)}, u32[]{:S(2)}, u32[]{:S(2)}) collective-permute-start(f32[256,512]{1,0:T(8,128)S(1)} %convolution_add_fusion), channel_id=1, source_target_pairs={{0,16},{16,0},{1,17},{17,1},{2,18},{18,2},{3,19},{19,3},{4,20},{20... | collective-permute-start | bytes 1572872 | tf_op jit(solution)/shard_map/ppermute | solution.py:21
  140.3 0.5 fusion.4
  140.8 1.0 collective-permute-done.20
  141.8 1.2 add_multiply_fusion
  (55 shorter events, 0.9 us)
Async XLA Ops:
  0.0 11.1 %copy-start = (bf16[256,512]{1,0:T(8,128)(2,1)S(1)}, bf16[256,512]{1,0:T(8,128)(2,1)}, u32[]{:S(2)}) copy-start(bf16[256,512]{1,0:T(8,128)(2,1)} %param.1) | copy-start | bytes 786436
  0.0 6.8 %collective-permute-start.1 = (bf16[256,512]{1,0:T(8,128)(2,1)}, bf16[256,512]{1,0:T(8,128)(2,1)S(1)}, u32[]{:S(2)}, u32[]{:S(2)}) collective-permute-start(bf16[256,512]{1,0:T(8,128)(2,1)} %param.1), channel_id=1, source_target_pairs={{0,16},{16,0},{1,17},{17,1},{2,18},{18,2},{3,19},{19,3},{4,20},{20... | collective-permute-start | bytes 786440 | tf_op jit(solution)/shard_map/ppermute | solution.py:21
  3.2 8.3 %collective-permute-start = (bf16[256,512]{1,0:T(8,128)(2,1)}, bf16[256,512]{1,0:T(8,128)(2,1)S(1)}, u32[]{:S(2)}, u32[]{:S(2)}) collective-permute-start(bf16[256,512]{1,0:T(8,128)(2,1)} %param.1), channel_id=1, source_target_pairs={{0,32},{32,0},{1,33},{33,1},{2,34},{34,2},{3,35},{35,3},{4,36},{36... | collective-permute-start | bytes 786440 | tf_op jit(solution)/shard_map/ppermute | solution.py:21
  3.2 9.8 %collective-permute-start.2 = (bf16[256,512]{1,0:T(8,128)(2,1)}, bf16[256,512]{1,0:T(8,128)(2,1)}, u32[]{:S(2)}, u32[]{:S(2)}) collective-permute-start(bf16[256,512]{1,0:T(8,128)(2,1)} %param.1), channel_id=1, source_target_pairs={{0,128},{64,192},{128,0},{192,64},{1,129},{65,193},{129,1},{193,65... | collective-permute-start | bytes 786440 | tf_op jit(solution)/shard_map/ppermute | solution.py:25
  11.5 13.0 %collective-permute-start.3 = (bf16[512,512]{1,0:T(8,128)(2,1)S(1)}, bf16[512,512]{1,0:T(8,128)(2,1)S(1)}, u32[]{:S(2)}, u32[]{:S(2)}) collective-permute-start(bf16[512,512]{1,0:T(8,128)(2,1)S(1)} %pad_maximum_fusion.3), channel_id=1, source_target_pairs={{0,192},{64,0},{128,64},{192,128},{1,193},{65,1},{129,65},{193,129... | collective-permute-start | bytes 1572872 | tf_op jit(solution)/shard_map/ppermute | solution.py:25
  12.6 13.9 %collective-permute-start.4 = (bf16[512,512]{1,0:T(8,128)(2,1)S(1)}, bf16[512,512]{1,0:T(8,128)(2,1)}, u32[]{:S(2)}, u32[]{:S(2)}) collective-permute-start(bf16[512,512]{1,0:T(8,128)(2,1)S(1)} %pad_maximum_fusion.3), channel_id=1, source_target_pairs={{0,64},{64,128},{128,192},{192,0},{1,65},{65,129},{129,193},{193,1... | collective-permute-start | bytes 1572872 | tf_op jit(solution)/shard_map/ppermute | solution.py:25
  14.1 2.7 %copy-start.1 = (bf16[768,512]{1,0:T(8,128)(2,1)}, bf16[768,512]{1,0:T(8,128)(2,1)S(1)}, u32[]{:S(2)}) copy-start(bf16[768,512]{1,0:T(8,128)(2,1)S(1)} %pad_maximum_fusion.2) | copy-start | bytes 2359300
  14.1 7.0 %collective-permute-start.5 = (bf16[256,512]{1,0:T(8,128)(2,1)}, bf16[256,512]{1,0:T(8,128)(2,1)}, u32[]{:S(2)}, u32[]{:S(2)}) collective-permute-start(bf16[256,512]{1,0:T(8,128)(2,1)} %collective-permute-done.2), channel_id=1, source_target_pairs={{0,32},{32,0},{1,33},{33,1},{2,34},{34,2},{3,35},{35,3},{4,36},{36... | collective-permute-start | bytes 786440 | tf_op jit(solution)/shard_map/ppermute | solution.py:21
  16.8 19.1 %all-to-all-start = ((bf16[4,128,768]{2,1,0:T(8,128)(2,1)}), bf16[4,128,768]{2,1,0:T(8,128)(2,1)S(1)}, u32[]{:S(2)}, u32[]{:S(2)}) async-start(bf16[4,128,768]{2,1,0:T(8,128)(2,1)} %bitcast.35), calls=%async_computation | async-start | bytes 1572864 | tf_op jit(solution)/shard_map/all_to_all | solution.py:82
  29.6 9.2 %collective-permute-start.6 = (bf16[128,1280]{1,0:T(8,128)(2,1)}, bf16[128,1280]{1,0:T(8,128)(2,1)}, u32[]{:S(2)}, u32[]{:S(2)}) collective-permute-start(bf16[128,1280]{1,0:T(8,128)(2,1)} %convolution_convert_fusion.2), channel_id=1, source_target_pairs={{0,1},{1,2},{2,3},{3,0},{4,5},{5,6},{6,7},{7,4},{8,9},{9,10},{10,1... | collective-permute-start | bytes 983048 | tf_op jit(solution)/shard_map/ppermute | solution.py:25
  31.0 7.8 %collective-permute-start.7 = (bf16[128,1280]{1,0:T(8,128)(2,1)S(1)}, bf16[128,1280]{1,0:T(8,128)(2,1)}, u32[]{:S(2)}, u32[]{:S(2)}) collective-permute-start(bf16[128,1280]{1,0:T(8,128)(2,1)S(1)} %convolution_convert_fusion.1), channel_id=1, source_target_pairs={{0,3},{1,0},{2,1},{3,2},{4,7},{5,4},{6,5},{7,6},{8,11},{9,8},{10,9... | collective-permute-start | bytes 983048 | tf_op jit(solution)/shard_map/ppermute | solution.py:25
  33.8 13.1 %collective-permute-start.8 = (bf16[128,1280]{1,0:T(8,128)(2,1)}, bf16[128,1280]{1,0:T(8,128)(2,1)}, u32[]{:S(2)}, u32[]{:S(2)}) collective-permute-start(bf16[128,1280]{1,0:T(8,128)(2,1)} %convolution_convert_fusion), channel_id=1, source_target_pairs={{0,2},{1,3},{2,0},{3,1},{4,6},{5,7},{6,4},{7,5},{8,10},{9,11},{10,... | collective-permute-start | bytes 983048 | tf_op jit(solution)/shard_map/ppermute | solution.py:25
  48.3 33.9 %copy-start.2 = (bf16[768,512]{1,0:T(8,128)(2,1)S(1)}, bf16[768,512]{1,0:T(8,128)(2,1)}, u32[]{:S(2)}) copy-start(bf16[768,512]{1,0:T(8,128)(2,1)} %copy-done.1) | copy-start | bytes 2359300
  49.1 17.3 %all-to-all-start.1 = ((bf16[4,32,2048]{2,1,0:T(8,128)(2,1)}), bf16[4,32,2048]{2,1,0:T(8,128)(2,1)S(1)}, u32[]{:S(2)}, u32[]{:S(2)}) async-start(bf16[4,32,2048]{2,1,0:T(8,128)(2,1)} %bitcast.2), calls=%async_computation.1 | async-start | bytes 1048576 | tf_op jit(solution)/shard_map/all_to_all | solution.py:89
  80.7 10.4 %collective-permute-start.9 = (bf16[128,2048]{1,0:T(8,128)(2,1)S(1)}, bf16[128,2048]{1,0:T(8,128)(2,1)S(1)}, u32[]{:S(2)}, u32[]{:S(2)}) collective-permute-start(bf16[128,2048]{1,0:T(8,128)(2,1)S(1)} %bitcast.33), channel_id=1, source_target_pairs={{0,3},{1,0},{2,1},{3,2},{4,7},{5,4},{6,5},{7,6},{8,11},{9,8},{10,9... | collective-permute-start | bytes 1572872 | tf_op jit(solution)/shard_map/ppermute | solution.py:25
  81.8 9.2 %collective-permute-start.10 = (bf16[128,2048]{1,0:T(8,128)(2,1)S(1)}, bf16[128,2048]{1,0:T(8,128)(2,1)S(1)}, u32[]{:S(2)}, u32[]{:S(2)}) collective-permute-start(bf16[128,2048]{1,0:T(8,128)(2,1)S(1)} %bitcast.34), channel_id=1, source_target_pairs={{0,1},{1,2},{2,3},{3,0},{4,5},{5,6},{6,7},{7,4},{8,9},{9,10},{10,1... | collective-permute-start | bytes 1572872 | tf_op jit(solution)/shard_map/ppermute | solution.py:25
  91.1 16.0 %collective-permute-start.12 = (bf16[64,2048]{1,0:T(8,128)(2,1)S(1)}, bf16[64,2048]{1,0:T(8,128)(2,1)S(1)}, u32[]{:S(2)}, u32[]{:S(2)}) collective-permute-start(bf16[64,2048]{1,0:T(8,128)(2,1)S(1)} %get-tuple-element.20), channel_id=1, source_target_pairs={{0,3},{1,0},{2,1},{3,2},{4,7},{5,4},{6,5},{7,6},{8,11},{9,8},{10,9... | collective-permute-start | bytes 786440 | tf_op jit(solution)/shard_map/ppermute | solution.py:25
  91.2 15.9 %collective-permute-start.13 = (bf16[64,2048]{1,0:T(8,128)(2,1)S(1)}, bf16[64,2048]{1,0:T(8,128)(2,1)S(1)}, u32[]{:S(2)}, u32[]{:S(2)}) collective-permute-start(bf16[64,2048]{1,0:T(8,128)(2,1)S(1)} %slice.87), channel_id=1, source_target_pairs={{0,1},{1,2},{2,3},{3,0},{4,5},{5,6},{6,7},{7,4},{8,9},{9,10},{10,1... | collective-permute-start | bytes 786440 | tf_op jit(solution)/shard_map/ppermute | solution.py:25
  93.6 18.9 %collective-permute-start.11 = (f32[192,512]{1,0:T(8,128)S(1)}, f32[192,512]{1,0:T(8,128)S(1)}, u32[]{:S(2)}, u32[]{:S(2)}) collective-permute-start(f32[192,512]{1,0:T(8,128)S(1)} %pad_maximum_fusion.6), channel_id=1, source_target_pairs={{0,16},{16,0},{1,17},{17,1},{2,18},{18,2},{3,19},{19,3},{4,20},{20... | collective-permute-start | bytes 1179656 | tf_op jit(solution)/shard_map/ppermute | solution.py:21
  107.6 5.8 %collective-permute-start.14 = (f32[64,512]{1,0:T(8,128)S(1)}, f32[64,512]{1,0:T(8,128)S(1)}, u32[]{:S(2)}, u32[]{:S(2)}) collective-permute-start(f32[64,512]{1,0:T(8,128)S(1)} %fusion.23), channel_id=1, source_target_pairs={{0,16},{16,0},{1,17},{17,1},{2,18},{18,2},{3,19},{19,3},{4,20},{20... | collective-permute-start | bytes 393224 | tf_op jit(solution)/shard_map/ppermute | solution.py:21
  114.0 7.6 %collective-permute-start.15 = (bf16[256,512]{1,0:T(8,128)(2,1)S(1)}, bf16[256,512]{1,0:T(8,128)(2,1)S(1)}, u32[]{:S(2)}, u32[]{:S(2)}) collective-permute-start(bf16[256,512]{1,0:T(8,128)(2,1)S(1)} %dynamic-slice_convert_fusion), channel_id=1, source_target_pairs={{0,32},{32,0},{1,33},{33,1},{2,34},{34,2},{3,35},{35,3},{4,36},{36... | collective-permute-start | bytes 786440 | tf_op jit(solution)/shard_map/ppermute | solution.py:21
  114.7 8.9 %collective-permute-start.16 = (bf16[256,512]{1,0:T(8,128)(2,1)S(1)}, bf16[256,512]{1,0:T(8,128)(2,1)S(1)}, u32[]{:S(2)}, u32[]{:S(2)}) collective-permute-start(bf16[256,512]{1,0:T(8,128)(2,1)S(1)} %dynamic-slice_convert_fusion), channel_id=1, source_target_pairs={{0,128},{64,192},{128,0},{192,64},{1,129},{65,193},{129,1},{193,65... | collective-permute-start | bytes 786440 | tf_op jit(solution)/shard_map/ppermute | solution.py:25
  121.7 12.3 %collective-permute-start.17 = (bf16[512,512]{1,0:T(8,128)(2,1)S(1)}, bf16[512,512]{1,0:T(8,128)(2,1)S(1)}, u32[]{:S(2)}, u32[]{:S(2)}) collective-permute-start(bf16[512,512]{1,0:T(8,128)(2,1)S(1)} %pad_maximum_fusion.5), channel_id=1, source_target_pairs={{0,192},{64,0},{128,64},{192,128},{1,193},{65,1},{129,65},{193,129... | collective-permute-start | bytes 1572872 | tf_op jit(solution)/shard_map/ppermute | solution.py:25
  123.6 13.2 %collective-permute-start.18 = (bf16[512,512]{1,0:T(8,128)(2,1)S(1)}, bf16[512,512]{1,0:T(8,128)(2,1)S(1)}, u32[]{:S(2)}, u32[]{:S(2)}) collective-permute-start(bf16[512,512]{1,0:T(8,128)(2,1)S(1)} %pad_maximum_fusion.5), channel_id=1, source_target_pairs={{0,64},{64,128},{128,192},{192,0},{1,65},{65,129},{129,193},{193,1... | collective-permute-start | bytes 1572872 | tf_op jit(solution)/shard_map/ppermute | solution.py:25
  123.6 6.3 %collective-permute-start.19 = (bf16[256,512]{1,0:T(8,128)(2,1)S(1)}, bf16[256,512]{1,0:T(8,128)(2,1)S(1)}, u32[]{:S(2)}, u32[]{:S(2)}) collective-permute-start(bf16[256,512]{1,0:T(8,128)(2,1)S(1)} %collective-permute-done.16), channel_id=1, source_target_pairs={{0,32},{32,0},{1,33},{33,1},{2,34},{34,2},{3,35},{35,3},{4,36},{36... | collective-permute-start | bytes 786440 | tf_op jit(solution)/shard_map/ppermute | solution.py:21
  137.8 4.0 %collective-permute-start.20 = (f32[256,512]{1,0:T(8,128)S(1)}, f32[256,512]{1,0:T(8,128)S(1)}, u32[]{:S(2)}, u32[]{:S(2)}) collective-permute-start(f32[256,512]{1,0:T(8,128)S(1)} %convolution_add_fusion), channel_id=1, source_target_pairs={{0,16},{16,0},{1,17},{17,1},{2,18},{18,2},{3,19},{19,3},{4,20},{20... | collective-permute-start | bytes 1572872 | tf_op jit(solution)/shard_map/ppermute | solution.py:21

commit v18 on v16

--- a/solution.py
+++ b/solution.py
@@ -100,15 +100,21 @@
     second = core_sum([(product(far[0]), product(far[1]))])
     inner = window([first[:64], first[64:128], second, first[128:]], back, 4)
 
-    pair, last = pair_of(inner.astype(BF))
-    pair, *late = lax.optimization_barrier([pair, last, *late_blocks(pair, last)])
-    panels = jnp.concatenate([pair, late[0]], axis=0), jnp.concatenate(late[1:], axis=0)
+    pair, last = lax.optimization_barrier(pair_of(inner.astype(BF)))
+    *late, zl_far = late_blocks(pair, last)
     gram = [(near[:64], near[64:]), (after[:64], after[64:]), far, (before[:64], before[64:])]
-    mixed = []
-    for rows in zip(*gram):
-        rows = window(rows, back, 4)
-        halves = rows[:, :768], rows[:, 768:]
-        mixed.append(sum(matmul(h, panel, ((1,), (0,))) for h, panel in zip(halves, panels)))
+    gram = [window(rows, back, 4) for rows in zip(*gram)]
+    early = jnp.concatenate([pair, last, zl_far], axis=0)
+    mixed = [
+        matmul(jnp.concatenate([rows[:, :768], rows[:, 1792:]], axis=1), early, ((1,), (0,)))
+        for rows in gram
+    ]
+    *late, mixed_0, mixed_1 = lax.optimization_barrier((*late, *mixed))
+    late = jnp.concatenate(late, axis=0)
+    mixed = [
+        product + matmul(rows[:, 768:1792], late, ((1,), (0,)))
+        for product, rows in zip((mixed_0, mixed_1), gram)
+    ]
     mixed = mixed[0] + swap(mixed[1], "core")
     mine = iterate.astype(F32)
     return math.sqrt(COLS) * (coef_a * mine + (coef_b * inner + coef_c * mixed))

time: 141 us -> 146 us (1.035)
  waiting for transfers between devices: 56.2 us -> 65.9 us
  starting transfers between devices: 51.5 us -> 45.9 us
    ppermute x16, waiting for transfers between devices: 39.4 us -> 49.3 us  [send(): lax.ppermute(array, axis, [(i, (i + k) % 4) for i in range(4)])]
    ppermute x8, starting transfers between devices: 24.2 us -> 19.3 us  [swap(): return lax.ppermute(array, axis, [(0, 1), (1, 0)])]
  transfers between devices with their start and end apart: 25 -> 25, of which waited for: 15 -> 16; matrix products, arithmetic and copies ran while one was open for 9% -> 9% of each run, Pallas kernels for 0% -> 0%
where the time goes in v18:
time: 146 us; the launch traced here: 145 us
  waiting for transfers between devices  65.9 us (45%)
  starting transfers between devices  45.9 us (31%)
  blocking collectives  15 us (10%)
  matrix products  9.13 us (6%)
  other arithmetic  7.28 us (5%)
  local copies, waits for them, and re-layouts  1.78 us (1%)
    ppermute x16, waiting for transfers between devices, send(): lax.ppermute(array, axis, [(i, (i + k) % 4) for i in range(4)])  49.3 us
    ppermute x16, starting transfers between devices, send(): lax.ppermute(array, axis, [(i, (i + k) % 4) for i in range(4)])  22.3 us
    ppermute x8, starting transfers between devices, swap(): return lax.ppermute(array, axis, [(0, 1), (1, 0)])  19.3 us
    ppermute x8, waiting for transfers between devices, swap(): return lax.ppermute(array, axis, [(0, 1), (1, 0)])  16.6 us
    all_gather x1, blocking collectives, per_device(): near = lax.all_gather(part, 'zh', axis=0, tiled=True)  15 us
    dot_general x14, matrix products, matmul(): return lax.dot_general(a, b, (dims, ((), ())), preferred_element_type=F32)  9.13 us
    all_to_all x1, starting transfers between devices, per_device(): first = add(lax.all_to_all(pieces.reshape(4, 128, 768), 'y', 0, 0))  4.19 us
  transfers between devices with their start and end apart: 25, of which 16 were waited for; matrix products, arithmetic and copies ran while one was open for 9% of the time, Pallas kernels for 0%

profile of v18, /device:TPU:1, one launch (start us, length us, event | category | flops | bytes accessed | tf_op | source)
XLA Modules:
  0.0 145.4 jit_solution(2575300107965850062)
XLA Ops:
  0.0 3.2 %collective-permute-start.1 = (bf16[256,512]{1,0:T(8,128)(2,1)}, bf16[256,512]{1,0:T(8,128)(2,1)S(1)}, u32[]{:S(2)}, u32[]{:S(2)}) collective-permute-start(bf16[256,512]{1,0:T(8,128)(2,1)} %param.1), channel_id=1, source_target_pairs={{0,16},{16,0},{1,17},{17,1},{2,18},{18,2},{3,19},{19,3},{4,20},{20... | collective-permute-start | bytes 786440 | tf_op jit(solution)/shard_map/ppermute | solution.py:21
  3.2 1.0 collective-permute-start.2
  4.3 1.6 %collective-permute-start = (bf16[256,512]{1,0:T(8,128)(2,1)}, bf16[256,512]{1,0:T(8,128)(2,1)S(1)}, u32[]{:S(2)}, u32[]{:S(2)}) collective-permute-start(bf16[256,512]{1,0:T(8,128)(2,1)} %param.1), channel_id=1, source_target_pairs={{0,32},{32,0},{1,33},{33,1},{2,34},{34,2},{3,35},{35,3},{4,36},{36... | collective-permute-start | bytes 786440 | tf_op jit(solution)/shard_map/ppermute | solution.py:21
  5.9 1.0 fusion.46
  6.9 0.3 constant_dynamic-update-slice_fusion.6
  7.2 0.3 constant_dynamic-update-slice_fusion.5
  7.5 0.3 constant_dynamic-update-slice_fusion.4
  7.8 0.3 constant_dynamic-update-slice_fusion.3
  8.2 4.4 %collective-permute-done = bf16[256,512]{1,0:T(8,128)(2,1)S(1)} collective-permute-done((bf16[256,512]{1,0:T(8,128)(2,1)}, bf16[256,512]{1,0:T(8,128)(2,1)S(1)}, u32[]{:S(2)}, u32[]{:S(2)}) %collective-permute-start) | collective-permute-done | bytes 262176 | tf_op jit(solution)/shard_map/ppermute | solution.py:21
  12.7 0.4 collective-permute-start.4
  13.1 2.4 %collective-permute-start.3 = (bf16[512,512]{1,0:T(8,128)(2,1)S(1)}, bf16[512,512]{1,0:T(8,128)(2,1)}, u32[]{:S(2)}, u32[]{:S(2)}) collective-permute-start(bf16[512,512]{1,0:T(8,128)(2,1)S(1)} %pad_maximum_fusion.3), channel_id=1, source_target_pairs={{0,192},{64,0},{128,64},{192,128},{1,193},{65,1},{129,65},{193,129... | collective-permute-start | bytes 1572872 | tf_op jit(solution)/shard_map/ppermute | solution.py:25
  15.5 1.0 pad_maximum_fusion.2
  16.5 1.2 collective-permute-start.5
  17.7 1.5 %convolution_convert_fusion.4 = bf16[512,768]{1,0:T(8,128)(2,1)} fusion(bf16[512,512]{1,0:T(8,128)(2,1)S(1)} %get-tuple-element.18, bf16[768,512]{1,0:T(8,128)(2,1)S(1)} %pad_maximum_fusion.2), kind=kOutput, calls=%fused_computation.5 | convolution fusion | flops 403046400 | bytes 2097152 | tf_op jit(solution)/shard_map/dot_general | solution.py:52
  19.2 4.2 %all-to-all-start = ((bf16[4,128,768]{2,1,0:T(8,128)(2,1)}), bf16[4,128,768]{2,1,0:T(8,128)(2,1)S(1)}, u32[]{:S(2)}, u32[]{:S(2)}) async-start(bf16[4,128,768]{2,1,0:T(8,128)(2,1)} %bitcast.18), calls=%async_computation | async-start | bytes 1572864 | tf_op jit(solution)/shard_map/all_to_all | solution.py:83
  23.3 3.3 %collective-permute-done.4 = bf16[512,512]{1,0:T(8,128)(2,1)S(1)} collective-permute-done((bf16[512,512]{1,0:T(8,128)(2,1)S(1)}, bf16[512,512]{1,0:T(8,128)(2,1)S(1)}, u32[]{:S(2)}, u32[]{:S(2)}) %collective-permute-start.4) | collective-permute-done | bytes 524320 | tf_op jit(solution)/shard_map/ppermute | solution.py:25
  26.6 1.2 pad_maximum_fusion.1
  27.8 1.3 convolution_convert_fusion
  29.1 0.5 convolution_convert_fusion.1
  29.6 2.8 %collective-permute-start.8 = (bf16[128,1280]{1,0:T(8,128)(2,1)}, bf16[128,1280]{1,0:T(8,128)(2,1)}, u32[]{:S(2)}, u32[]{:S(2)}) collective-permute-start(bf16[128,1280]{1,0:T(8,128)(2,1)} %convolution_convert_fusion), channel_id=1, source_target_pairs={{0,2},{1,3},{2,0},{3,1},{4,6},{5,7},{6,4},{7,5},{8,10},{9,11},{10,... | collective-permute-start | bytes 983048 | tf_op jit(solution)/shard_map/ppermute | solution.py:25
  32.4 0.8 collective-permute-start.7
  33.2 1.3 convolution_convert_fusion.2
  34.5 0.7 collective-permute-start.6
  35.2 0.5 convolution_convert_fusion.3
  35.7 0.1 fusion.12
  35.8 5.5 %collective-permute-done.8 = bf16[128,1280]{1,0:T(8,128)(2,1)} collective-permute-done((bf16[128,1280]{1,0:T(8,128)(2,1)}, bf16[128,1280]{1,0:T(8,128)(2,1)}, u32[]{:S(2)}, u32[]{:S(2)}) %collective-permute-start.8) | collective-permute-done | bytes 327712 | tf_op jit(solution)/shard_map/ppermute | solution.py:25
  41.4 6.3 %collective-permute-done.7 = bf16[128,1280]{1,0:T(8,128)(2,1)} collective-permute-done((bf16[128,1280]{1,0:T(8,128)(2,1)S(1)}, bf16[128,1280]{1,0:T(8,128)(2,1)}, u32[]{:S(2)}, u32[]{:S(2)}) %collective-permute-start.7) | collective-permute-done | bytes 327712 | tf_op jit(solution)/shard_map/ppermute | solution.py:25
  47.7 2.6 %collective-permute-done.6 = bf16[128,1280]{1,0:T(8,128)(2,1)} collective-permute-done((bf16[128,1280]{1,0:T(8,128)(2,1)}, bf16[128,1280]{1,0:T(8,128)(2,1)}, u32[]{:S(2)}, u32[]{:S(2)}) %collective-permute-start.6) | collective-permute-done | bytes 327712 | tf_op jit(solution)/shard_map/ppermute | solution.py:25
  50.2 1.3 add_convert_fusion
  51.6 5.8 %collective-permute-start.11 = (bf16[32,2048]{1,0:T(8,128)(2,1)S(1)}, bf16[32,2048]{1,0:T(8,128)(2,1)S(1)}, u32[]{:S(2)}, u32[]{:S(2)}) collective-permute-start(bf16[32,2048]{1,0:T(8,128)(2,1)S(1)} %get-tuple-element.46), channel_id=1, source_target_pairs={{0,8},{4,12},{8,0},{12,4},{1,9},{5,13},{9,1},{13,5},{2,10},{6,14},... | collective-permute-start | bytes 393224 | tf_op jit(solution)/shard_map/ppermute | solution.py:25
  57.4 0.5 collective-permute-start.10
  57.9 1.9 %collective-permute-start.9 = (bf16[32,2048]{1,0:T(8,128)(2,1)S(1)}, bf16[32,2048]{1,0:T(8,128)(2,1)}, u32[]{:S(2)}, u32[]{:S(2)}) collective-permute-start(bf16[32,2048]{1,0:T(8,128)(2,1)S(1)} %get-tuple-element.45), channel_id=1, source_target_pairs={{0,4},{4,8},{8,12},{12,0},{1,5},{5,9},{9,13},{13,1},{2,6},{6,10},{... | collective-permute-start | bytes 393224 | tf_op jit(solution)/shard_map/ppermute | solution.py:25
  59.8 0.7 collective-permute-done.11
  60.5 10.0 %collective-permute-done.10 = bf16[32,2048]{1,0:T(8,128)(2,1)} collective-permute-done((bf16[32,2048]{1,0:T(8,128)(2,1)S(1)}, bf16[32,2048]{1,0:T(8,128)(2,1)}, u32[]{:S(2)}, u32[]{:S(2)}) %collective-permute-start.10) | collective-permute-done | bytes 131104 | tf_op jit(solution)/shard_map/ppermute | solution.py:25
  70.5 1.0 add_convert_fusion.2
  71.5 15.0 %all_gather.3 = bf16[128,2048]{1,0:T(8,128)(2,1)S(1)} all-gather(bf16[32,2048]{1,0:T(8,128)(2,1)S(1)} %add_convert_fusion.2), channel_id=1, replica_groups=mesh['x'=4,'zl'=2,'core'=2,'zh'=4,'y'=4] {'zh'}, dimensions={0}, use_global_device_ids=true | all-gather | bytes 655360 | tf_op jit(solution)/shard_map/all_gather | solution.py:91
  86.5 0.2 collective-permute-start.13
  86.6 2.5 %collective-permute-start.12 = (bf16[128,2048]{1,0:T(8,128)(2,1)S(1)}, bf16[128,2048]{1,0:T(8,128)(2,1)S(1)}, u32[]{:S(2)}, u32[]{:S(2)}) collective-permute-start(bf16[128,2048]{1,0:T(8,128)(2,1)S(1)} %all_gather.3), channel_id=1, source_target_pairs={{0,3},{1,0},{2,1},{3,2},{4,7},{5,4},{6,5},{7,6},{8,11},{9,8},{10,9... | collective-permute-start | bytes 1572872 | tf_op jit(solution)/shard_map/ppermute | solution.py:25
  89.2 0.4 fusion.37
  89.6 9.6 %collective-permute-done.13 = bf16[128,2048]{1,0:T(8,128)(2,1)S(1)} collective-permute-done((bf16[128,2048]{1,0:T(8,128)(2,1)S(1)}, bf16[128,2048]{1,0:T(8,128)(2,1)S(1)}, u32[]{:S(2)}, u32[]{:S(2)}) %collective-permute-start.13) | collective-permute-done | bytes 524320 | tf_op jit(solution)/shard_map/ppermute | solution.py:25
  99.2 0.4 fusion.35
  99.8 2.0 %collective-permute-start.15 = (bf16[64,2048]{1,0:T(8,128)(2,1)S(1)}, bf16[64,2048]{1,0:T(8,128)(2,1)S(1)}, u32[]{:S(2)}, u32[]{:S(2)}) collective-permute-start(bf16[64,2048]{1,0:T(8,128)(2,1)S(1)} %get-tuple-element.21), channel_id=1, source_target_pairs={{0,3},{1,0},{2,1},{3,2},{4,7},{5,4},{6,5},{7,6},{8,11},{9,8},{10,9... | collective-permute-start | bytes 786440 | tf_op jit(solution)/shard_map/ppermute | solution.py:25
  101.7 0.4 fusion.36
  102.2 3.4 %collective-permute-start.14 = (f32[192,512]{1,0:T(8,128)S(1)}, f32[192,512]{1,0:T(8,128)S(1)}, u32[]{:S(2)}, u32[]{:S(2)}) collective-permute-start(f32[192,512]{1,0:T(8,128)S(1)} %pad_maximum_fusion.6), channel_id=1, source_target_pairs={{0,16},{16,0},{1,17},{17,1},{2,18},{18,2},{3,19},{19,3},{4,20},{20... | collective-permute-start | bytes 1179656 | tf_op jit(solution)/shard_map/ppermute | solution.py:21
  105.7 2.5 %collective-permute-done.16 = bf16[64,2048]{1,0:T(8,128)(2,1)S(1)} collective-permute-done((bf16[64,2048]{1,0:T(8,128)(2,1)S(1)}, bf16[64,2048]{1,0:T(8,128)(2,1)S(1)}, u32[]{:S(2)}, u32[]{:S(2)}) %collective-permute-start.16) | collective-permute-done | bytes 262176 | tf_op jit(solution)/shard_map/ppermute | solution.py:25
  108.2 0.5 fusion.34
  108.6 4.6 %collective-permute-start.17 = (f32[64,512]{1,0:T(8,128)S(1)}, f32[64,512]{1,0:T(8,128)S(1)}, u32[]{:S(2)}, u32[]{:S(2)}) collective-permute-start(f32[64,512]{1,0:T(8,128)S(1)} %fusion.34), channel_id=1, source_target_pairs={{0,16},{16,0},{1,17},{17,1},{2,18},{18,2},{3,19},{19,3},{4,20},{20... | collective-permute-start | bytes 393224 | tf_op jit(solution)/shard_map/ppermute | solution.py:21
  113.6 0.6 collective-permute-done.17
  114.2 0.5 constant_dynamic-update-slice_fusion.8
  114.8 2.3 %collective-permute-start.18 = (bf16[256,512]{1,0:T(8,128)(2,1)S(1)}, bf16[256,512]{1,0:T(8,128)(2,1)S(1)}, u32[]{:S(2)}, u32[]{:S(2)}) collective-permute-start(bf16[256,512]{1,0:T(8,128)(2,1)S(1)} %dynamic-slice_convert_fusion), channel_id=1, source_target_pairs={{0,32},{32,0},{1,33},{33,1},{2,34},{34,2},{3,35},{35,3},{4,36},{36... | collective-permute-start | bytes 786440 | tf_op jit(solution)/shard_map/ppermute | solution.py:21
  117.2 6.3 %collective-permute-done.18 = bf16[256,512]{1,0:T(8,128)(2,1)S(1)} collective-permute-done((bf16[256,512]{1,0:T(8,128)(2,1)S(1)}, bf16[256,512]{1,0:T(8,128)(2,1)S(1)}, u32[]{:S(2)}, u32[]{:S(2)}) %collective-permute-start.18) | collective-permute-done | bytes 262176 | tf_op jit(solution)/shard_map/ppermute | solution.py:21
  123.6 2.3 %collective-permute-done.19 = bf16[256,512]{1,0:T(8,128)(2,1)S(1)} collective-permute-done((bf16[256,512]{1,0:T(8,128)(2,1)S(1)}, bf16[256,512]{1,0:T(8,128)(2,1)S(1)}, u32[]{:S(2)}, u32[]{:S(2)}) %collective-permute-start.19) | collective-permute-done | bytes 262176 | tf_op jit(solution)/shard_map/ppermute | solution.py:25
  125.9 0.4 collective-permute-start.22
  126.5 1.5 collective-permute-start.21
  128.0 4.2 %collective-permute-done.22 = bf16[256,512]{1,0:T(8,128)(2,1)S(1)} collective-permute-done((bf16[256,512]{1,0:T(8,128)(2,1)S(1)}, bf16[256,512]{1,0:T(8,128)(2,1)S(1)}, u32[]{:S(2)}, u32[]{:S(2)}) %collective-permute-start.22) | collective-permute-done | bytes 262176 | tf_op jit(solution)/shard_map/ppermute | solution.py:21
  132.2 0.4 fusion.4
  132.6 0.4 fusion.8
  133.1 5.4 %collective-permute-done.20 = bf16[512,512]{1,0:T(8,128)(2,1)S(1)} collective-permute-done((bf16[512,512]{1,0:T(8,128)(2,1)S(1)}, bf16[512,512]{1,0:T(8,128)(2,1)S(1)}, u32[]{:S(2)}, u32[]{:S(2)}) %collective-permute-start.20) | collective-permute-done | bytes 524320 | tf_op jit(solution)/shard_map/ppermute | solution.py:25
  138.4 1.3 collective-permute-done.21
  139.8 0.4 fusion
  140.3 2.5 %collective-permute-start.23 = (f32[256,512]{1,0:T(8,128)S(1)}, f32[256,512]{1,0:T(8,128)S(1)}, u32[]{:S(2)}, u32[]{:S(2)}) collective-permute-start(f32[256,512]{1,0:T(8,128)S(1)} %add.80), channel_id=1, source_target_pairs={{0,16},{16,0},{1,17},{17,1},{2,18},{18,2},{3,19},{19,3},{4,20},{20... | collective-permute-start | bytes 1572872 | tf_op jit(solution)/shard_map/ppermute | solution.py:21
  142.8 0.4 fusion.2
  143.3 1.1 collective-permute-done.23
  144.4 1.1 add_multiply_fusion
  (60 shorter events, 1.3 us)
Async XLA Ops:
  0.0 12.6 %copy-start = (bf16[256,512]{1,0:T(8,128)(2,1)S(1)}, bf16[256,512]{1,0:T(8,128)(2,1)}, u32[]{:S(2)}) copy-start(bf16[256,512]{1,0:T(8,128)(2,1)} %param.1) | copy-start | bytes 786436
  0.0 6.9 %collective-permute-start.1 = (bf16[256,512]{1,0:T(8,128)(2,1)}, bf16[256,512]{1,0:T(8,128)(2,1)S(1)}, u32[]{:S(2)}, u32[]{:S(2)}) collective-permute-start(bf16[256,512]{1,0:T(8,128)(2,1)} %param.1), channel_id=1, source_target_pairs={{0,16},{16,0},{1,17},{17,1},{2,18},{18,2},{3,19},{19,3},{4,20},{20... | collective-permute-start | bytes 786440 | tf_op jit(solution)/shard_map/ppermute | solution.py:21
  3.2 12.2 %collective-permute-start.2 = (bf16[256,512]{1,0:T(8,128)(2,1)}, bf16[256,512]{1,0:T(8,128)(2,1)}, u32[]{:S(2)}, u32[]{:S(2)}) collective-permute-start(bf16[256,512]{1,0:T(8,128)(2,1)} %param.1), channel_id=1, source_target_pairs={{0,128},{64,192},{128,0},{192,64},{1,129},{65,193},{129,1},{193,65... | collective-permute-start | bytes 786440 | tf_op jit(solution)/shard_map/ppermute | solution.py:25
  4.3 8.3 %collective-permute-start = (bf16[256,512]{1,0:T(8,128)(2,1)}, bf16[256,512]{1,0:T(8,128)(2,1)S(1)}, u32[]{:S(2)}, u32[]{:S(2)}) collective-permute-start(bf16[256,512]{1,0:T(8,128)(2,1)} %param.1), channel_id=1, source_target_pairs={{0,32},{32,0},{1,33},{33,1},{2,34},{34,2},{3,35},{35,3},{4,36},{36... | collective-permute-start | bytes 786440 | tf_op jit(solution)/shard_map/ppermute | solution.py:21
  12.7 13.9 %collective-permute-start.4 = (bf16[512,512]{1,0:T(8,128)(2,1)S(1)}, bf16[512,512]{1,0:T(8,128)(2,1)S(1)}, u32[]{:S(2)}, u32[]{:S(2)}) collective-permute-start(bf16[512,512]{1,0:T(8,128)(2,1)S(1)} %pad_maximum_fusion.3), channel_id=1, source_target_pairs={{0,64},{64,128},{128,192},{192,0},{1,65},{65,129},{129,193},{193,1... | collective-permute-start | bytes 1572872 | tf_op jit(solution)/shard_map/ppermute | solution.py:25
  13.1 13.5 %collective-permute-start.3 = (bf16[512,512]{1,0:T(8,128)(2,1)S(1)}, bf16[512,512]{1,0:T(8,128)(2,1)}, u32[]{:S(2)}, u32[]{:S(2)}) collective-permute-start(bf16[512,512]{1,0:T(8,128)(2,1)S(1)} %pad_maximum_fusion.3), channel_id=1, source_target_pairs={{0,192},{64,0},{128,64},{192,128},{1,193},{65,1},{129,65},{193,129... | collective-permute-start | bytes 1572872 | tf_op jit(solution)/shard_map/ppermute | solution.py:25
  16.5 2.7 %copy-start.1 = (bf16[768,512]{1,0:T(8,128)(2,1)}, bf16[768,512]{1,0:T(8,128)(2,1)S(1)}, u32[]{:S(2)}) copy-start(bf16[768,512]{1,0:T(8,128)(2,1)S(1)} %pad_maximum_fusion.2) | copy-start | bytes 2359300
  16.5 6.9 %collective-permute-start.5 = (bf16[256,512]{1,0:T(8,128)(2,1)}, bf16[256,512]{1,0:T(8,128)(2,1)}, u32[]{:S(2)}, u32[]{:S(2)}) collective-permute-start(bf16[256,512]{1,0:T(8,128)(2,1)} %collective-permute-done.2), channel_id=1, source_target_pairs={{0,32},{32,0},{1,33},{33,1},{2,34},{34,2},{3,35},{35,3},{4,36},{36... | collective-permute-start | bytes 786440 | tf_op jit(solution)/shard_map/ppermute | solution.py:21
  19.2 16.6 %all-to-all-start = ((bf16[4,128,768]{2,1,0:T(8,128)(2,1)}), bf16[4,128,768]{2,1,0:T(8,128)(2,1)S(1)}, u32[]{:S(2)}, u32[]{:S(2)}) async-start(bf16[4,128,768]{2,1,0:T(8,128)(2,1)} %bitcast.18), calls=%async_computation | async-start | bytes 1572864 | tf_op jit(solution)/shard_map/all_to_all | solution.py:83
  29.6 11.7 %collective-permute-start.8 = (bf16[128,1280]{1,0:T(8,128)(2,1)}, bf16[128,1280]{1,0:T(8,128)(2,1)}, u32[]{:S(2)}, u32[]{:S(2)}) collective-permute-start(bf16[128,1280]{1,0:T(8,128)(2,1)} %convolution_convert_fusion), channel_id=1, source_target_pairs={{0,2},{1,3},{2,0},{3,1},{4,6},{5,7},{6,4},{7,5},{8,10},{9,11},{10,... | collective-permute-start | bytes 983048 | tf_op jit(solution)/shard_map/ppermute | solution.py:25
  32.4 15.2 %collective-permute-start.7 = (bf16[128,1280]{1,0:T(8,128)(2,1)S(1)}, bf16[128,1280]{1,0:T(8,128)(2,1)}, u32[]{:S(2)}, u32[]{:S(2)}) collective-permute-start(bf16[128,1280]{1,0:T(8,128)(2,1)S(1)} %convolution_convert_fusion.1), channel_id=1, source_target_pairs={{0,3},{1,0},{2,1},{3,2},{4,7},{5,4},{6,5},{7,6},{8,11},{9,8},{10,9... | collective-permute-start | bytes 983048 | tf_op jit(solution)/shard_map/ppermute | solution.py:25
  34.5 15.7 %collective-permute-start.6 = (bf16[128,1280]{1,0:T(8,128)(2,1)}, bf16[128,1280]{1,0:T(8,128)(2,1)}, u32[]{:S(2)}, u32[]{:S(2)}) collective-permute-start(bf16[128,1280]{1,0:T(8,128)(2,1)} %convolution_convert_fusion.2), channel_id=1, source_target_pairs={{0,1},{1,2},{2,3},{3,0},{4,5},{5,6},{6,7},{7,4},{8,9},{9,10},{10,1... | collective-permute-start | bytes 983048 | tf_op jit(solution)/shard_map/ppermute | solution.py:25
  51.6 37.6 %copy-start.2 = (bf16[768,512]{1,0:T(8,128)(2,1)S(1)}, bf16[768,512]{1,0:T(8,128)(2,1)}, u32[]{:S(2)}) copy-start(bf16[768,512]{1,0:T(8,128)(2,1)} %copy-done.1) | copy-start | bytes 2359300
  51.6 8.9 %collective-permute-start.11 = (bf16[32,2048]{1,0:T(8,128)(2,1)S(1)}, bf16[32,2048]{1,0:T(8,128)(2,1)S(1)}, u32[]{:S(2)}, u32[]{:S(2)}) collective-permute-start(bf16[32,2048]{1,0:T(8,128)(2,1)S(1)} %get-tuple-element.46), channel_id=1, source_target_pairs={{0,8},{4,12},{8,0},{12,4},{1,9},{5,13},{9,1},{13,5},{2,10},{6,14},... | collective-permute-start | bytes 393224 | tf_op jit(solution)/shard_map/ppermute | solution.py:25
  57.4 13.1 %collective-permute-start.10 = (bf16[32,2048]{1,0:T(8,128)(2,1)S(1)}, bf16[32,2048]{1,0:T(8,128)(2,1)}, u32[]{:S(2)}, u32[]{:S(2)}) collective-permute-start(bf16[32,2048]{1,0:T(8,128)(2,1)S(1)} %get-tuple-element.47), channel_id=1, source_target_pairs={{0,12},{4,0},{8,4},{12,8},{1,13},{5,1},{9,5},{13,9},{2,14},{6,2},{... | collective-permute-start | bytes 393224 | tf_op jit(solution)/shard_map/ppermute | solution.py:25
  57.9 12.6 %collective-permute-start.9 = (bf16[32,2048]{1,0:T(8,128)(2,1)S(1)}, bf16[32,2048]{1,0:T(8,128)(2,1)}, u32[]{:S(2)}, u32[]{:S(2)}) collective-permute-start(bf16[32,2048]{1,0:T(8,128)(2,1)S(1)} %get-tuple-element.45), channel_id=1, source_target_pairs={{0,4},{4,8},{8,12},{12,0},{1,5},{5,9},{9,13},{13,1},{2,6},{6,10},{... | collective-permute-start | bytes 393224 | tf_op jit(solution)/shard_map/ppermute | solution.py:25
  86.5 12.8 %collective-permute-start.13 = (bf16[128,2048]{1,0:T(8,128)(2,1)S(1)}, bf16[128,2048]{1,0:T(8,128)(2,1)S(1)}, u32[]{:S(2)}, u32[]{:S(2)}) collective-permute-start(bf16[128,2048]{1,0:T(8,128)(2,1)S(1)} %all_gather.3), channel_id=1, source_target_pairs={{0,1},{1,2},{2,3},{3,0},{4,5},{5,6},{6,7},{7,4},{8,9},{9,10},{10,1... | collective-permute-start | bytes 1572872 | tf_op jit(solution)/shard_map/ppermute | solution.py:25
  86.6 13.1 %collective-permute-start.12 = (bf16[128,2048]{1,0:T(8,128)(2,1)S(1)}, bf16[128,2048]{1,0:T(8,128)(2,1)S(1)}, u32[]{:S(2)}, u32[]{:S(2)}) collective-permute-start(bf16[128,2048]{1,0:T(8,128)(2,1)S(1)} %all_gather.3), channel_id=1, source_target_pairs={{0,3},{1,0},{2,1},{3,2},{4,7},{5,4},{6,5},{7,6},{8,11},{9,8},{10,9... | collective-permute-start | bytes 1572872 | tf_op jit(solution)/shard_map/ppermute | solution.py:25
  99.8 5.9 %collective-permute-start.15 = (bf16[64,2048]{1,0:T(8,128)(2,1)S(1)}, bf16[64,2048]{1,0:T(8,128)(2,1)S(1)}, u32[]{:S(2)}, u32[]{:S(2)}) collective-permute-start(bf16[64,2048]{1,0:T(8,128)(2,1)S(1)} %get-tuple-element.21), channel_id=1, source_target_pairs={{0,3},{1,0},{2,1},{3,2},{4,7},{5,4},{6,5},{7,6},{8,11},{9,8},{10,9... | collective-permute-start | bytes 786440 | tf_op jit(solution)/shard_map/ppermute | solution.py:25
  101.7 6.4 %collective-permute-start.16 = (bf16[64,2048]{1,0:T(8,128)(2,1)S(1)}, bf16[64,2048]{1,0:T(8,128)(2,1)S(1)}, u32[]{:S(2)}, u32[]{:S(2)}) collective-permute-start(bf16[64,2048]{1,0:T(8,128)(2,1)S(1)} %slice.121), channel_id=1, source_target_pairs={{0,1},{1,2},{2,3},{3,0},{4,5},{5,6},{6,7},{7,4},{8,9},{9,10},{10,1... | collective-permute-start | bytes 786440 | tf_op jit(solution)/shard_map/ppermute | solution.py:25
  102.2 11.3 %collective-permute-start.14 = (f32[192,512]{1,0:T(8,128)S(1)}, f32[192,512]{1,0:T(8,128)S(1)}, u32[]{:S(2)}, u32[]{:S(2)}) collective-permute-start(f32[192,512]{1,0:T(8,128)S(1)} %pad_maximum_fusion.6), channel_id=1, source_target_pairs={{0,16},{16,0},{1,17},{17,1},{2,18},{18,2},{3,19},{19,3},{4,20},{20... | collective-permute-start | bytes 1179656 | tf_op jit(solution)/shard_map/ppermute | solution.py:21
  108.6 5.6 %collective-permute-start.17 = (f32[64,512]{1,0:T(8,128)S(1)}, f32[64,512]{1,0:T(8,128)S(1)}, u32[]{:S(2)}, u32[]{:S(2)}) collective-permute-start(f32[64,512]{1,0:T(8,128)S(1)} %fusion.34), channel_id=1, source_target_pairs={{0,16},{16,0},{1,17},{17,1},{2,18},{18,2},{3,19},{19,3},{4,20},{20... | collective-permute-start | bytes 393224 | tf_op jit(solution)/shard_map/ppermute | solution.py:21
  114.8 8.7 %collective-permute-start.18 = (bf16[256,512]{1,0:T(8,128)(2,1)S(1)}, bf16[256,512]{1,0:T(8,128)(2,1)S(1)}, u32[]{:S(2)}, u32[]{:S(2)}) collective-permute-start(bf16[256,512]{1,0:T(8,128)(2,1)S(1)} %dynamic-slice_convert_fusion), channel_id=1, source_target_pairs={{0,32},{32,0},{1,33},{33,1},{2,34},{34,2},{3,35},{35,3},{4,36},{36... | collective-permute-start | bytes 786440 | tf_op jit(solution)/shard_map/ppermute | solution.py:21
  117.2 8.7 %collective-permute-start.19 = (bf16[256,512]{1,0:T(8,128)(2,1)S(1)}, bf16[256,512]{1,0:T(8,128)(2,1)S(1)}, u32[]{:S(2)}, u32[]{:S(2)}) collective-permute-start(bf16[256,512]{1,0:T(8,128)(2,1)S(1)} %dynamic-slice_convert_fusion), channel_id=1, source_target_pairs={{0,128},{64,192},{128,0},{192,64},{1,129},{65,193},{129,1},{193,65... | collective-permute-start | bytes 786440 | tf_op jit(solution)/shard_map/ppermute | solution.py:25
  125.9 6.3 %collective-permute-start.22 = (bf16[256,512]{1,0:T(8,128)(2,1)S(1)}, bf16[256,512]{1,0:T(8,128)(2,1)S(1)}, u32[]{:S(2)}, u32[]{:S(2)}) collective-permute-start(bf16[256,512]{1,0:T(8,128)(2,1)S(1)} %collective-permute-done.19), channel_id=1, source_target_pairs={{0,32},{32,0},{1,33},{33,1},{2,34},{34,2},{3,35},{35,3},{4,36},{36... | collective-permute-start | bytes 786440 | tf_op jit(solution)/shard_map/ppermute | solution.py:21
  126.4 12.0 %collective-permute-start.20 = (bf16[512,512]{1,0:T(8,128)(2,1)S(1)}, bf16[512,512]{1,0:T(8,128)(2,1)S(1)}, u32[]{:S(2)}, u32[]{:S(2)}) collective-permute-start(bf16[512,512]{1,0:T(8,128)(2,1)S(1)} %pad_maximum_fusion.5), channel_id=1, source_target_pairs={{0,192},{64,0},{128,64},{192,128},{1,193},{65,1},{129,65},{193,129... | collective-permute-start | bytes 1572872 | tf_op jit(solution)/shard_map/ppermute | solution.py:25
  126.5 13.2 %collective-permute-start.21 = (bf16[512,512]{1,0:T(8,128)(2,1)S(1)}, bf16[512,512]{1,0:T(8,128)(2,1)S(1)}, u32[]{:S(2)}, u32[]{:S(2)}) collective-permute-start(bf16[512,512]{1,0:T(8,128)(2,1)S(1)} %pad_maximum_fusion.5), channel_id=1, source_target_pairs={{0,64},{64,128},{128,192},{192,0},{1,65},{65,129},{129,193},{193,1... | collective-permute-start | bytes 1572872 | tf_op jit(solution)/shard_map/ppermute | solution.py:25
  140.3 4.0 %collective-permute-start.23 = (f32[256,512]{1,0:T(8,128)S(1)}, f32[256,512]{1,0:T(8,128)S(1)}, u32[]{:S(2)}, u32[]{:S(2)}) collective-permute-start(f32[256,512]{1,0:T(8,128)S(1)} %add.80), channel_id=1, source_target_pairs={{0,16},{16,0},{1,17},{17,1},{2,18},{18,2},{3,19},{19,3},{4,20},{20... | collective-permute-start | bytes 1572872 | tf_op jit(solution)/shard_map/ppermute | solution.py:21

commit v19 on v16

--- a/solution.py
+++ b/solution.py
@@ -38,6 +38,10 @@
     return [send(pieces[k], axis, k) for k in (0, 1, 3, 2)]
 
 
+def scatter_pairs(pieces, axis):
+    return [pieces[0]] + [lax.ppermute(pieces[k], axis, [(i, i ^ k) for i in range(4)]) for k in (1, 3, 2)]
+
+
 def chunks(array):
     return jnp.split(array, 4, axis=0)
 
@@ -74,8 +78,10 @@
     pair, far = pair_of(iterate)
 
     own = [jnp.concatenate(rows, axis=0) for rows in zip(chunks(iterate), chunks(other))]
-    own = [window(chunks(rows), zh, 4) for rows in own]
-    own, turned = jnp.concatenate(own, axis=0), window(own, y, 4)
+    own = jnp.stack(own).reshape(4, 4, 32, 512)
+    own = [lax.dynamic_slice_in_dim(own, zh ^ k, 1, 1) for k in range(4)]
+    own = jnp.concatenate(own, axis=1).reshape(512, 512)
+    turned = window(chunks(own), y, 4)
     pair, own, turned = lax.optimization_barrier((pair, own, turned))
     early = lax.optimization_barrier(jnp.concatenate([pair, far], axis=0))
     pieces = matmul(own, early, ((1,), (1,))).astype(BF)
@@ -87,7 +93,7 @@
     second = add(scatter(pieces, "y"))
     part = jnp.concatenate([first, second], axis=1)
     panel = jnp.concatenate([early, panel], axis=0)
-    part = add(scatter(chunks(part), "zh"))
+    part = add(scatter_pairs(chunks(part), "zh"))
     near = lax.all_gather(part, "zh", axis=0, tiled=True)
     after, before = fetch(near, "y", 1), fetch(near, "y", 3)
     sent = lax.optimization_barrier((after[:64], before[64:]))

time: 141 us -> 141 us (level)
    ppermute x16 -> x13, waiting for transfers between devices: 39.4 us -> 30.7 us  [send(): lax.ppermute(array, axis, [(i, (i + k) % 4) for i in range(4)])]
    ppermute x16 -> x13, starting transfers between devices: 23.1 us -> 14.8 us  [send(): lax.ppermute(array, axis, [(i, (i + k) % 4) for i in range(4)])]
    ppermute x0 -> x3, starting transfers between devices: none -> 7.79 us  [scatter_pairs(): lax.ppermute(pieces[k], axis, [(i, i ^ k) for i in range(4)])]
    ppermute x0 -> x3, waiting for transfers between devices: none -> 7.35 us  [scatter_pairs(): lax.ppermute(pieces[k], axis, [(i, i ^ k) for i in range(4)])]
    ppermute x8, starting transfers between devices: 24.2 us -> 26.2 us  [swap(): return lax.ppermute(array, axis, [(0, 1), (1, 0)])]
  transfers between devices with their start and end apart: 25 -> 25, of which waited for: 15 -> 15; matrix products, arithmetic and copies ran while one was open for 9% -> 8% of each run, Pallas kernels for 0% -> 0%
where the time goes in v19:
time: 141 us; the launch traced here: 140 us
  waiting for transfers between devices  55.1 us (39%)
  starting transfers between devices  52.8 us (37%)
  blocking collectives  15.1 us (11%)
  matrix products  10.1 us (7%)
  other arithmetic  4.98 us (4%)
  local copies, waits for them, and re-layouts  1.81 us (1%)
    ppermute x13, waiting for transfers between devices, send(): lax.ppermute(array, axis, [(i, (i + k) % 4) for i in range(4)])  30.7 us
    ppermute x8, starting transfers between devices, swap(): return lax.ppermute(array, axis, [(0, 1), (1, 0)])  26.2 us
    ppermute x8, waiting for transfers between devices, swap(): return lax.ppermute(array, axis, [(0, 1), (1, 0)])  17 us
    all_gather x1, blocking collectives, per_device(): near = lax.all_gather(part, 'zh', axis=0, tiled=True)  15.1 us
    ppermute x13, starting transfers between devices, send(): lax.ppermute(array, axis, [(i, (i + k) % 4) for i in range(4)])  14.8 us
    dot_general x14, matrix products, matmul(): return lax.dot_general(a, b, (dims, ((), ())), preferred_element_type=F32)  10.1 us
    ppermute x3, starting transfers between devices, scatter_pairs(): lax.ppermute(pieces[k], axis, [(i, i ^ k) for i in range(4)])  7.79 us
    ppermute x3, waiting for transfers between devices, scatter_pairs(): lax.ppermute(pieces[k], axis, [(i, i ^ k) for i in range(4)])  7.35 us
  transfers between devices with their start and end apart: 25, of which 15 were waited for; matrix products, arithmetic and copies ran while one was open for 8% of the time, Pallas kernels for 0%

profile of v19, /device:TPU:1, one launch (start us, length us, event | category | flops | bytes accessed | tf_op | source)
XLA Modules:
  0.0 140.4 jit_solution(2959960828946976199)
XLA Ops:
  0.0 3.2 %collective-permute-start.1 = (bf16[256,512]{1,0:T(8,128)(2,1)}, bf16[256,512]{1,0:T(8,128)(2,1)S(1)}, u32[]{:S(2)}, u32[]{:S(2)}) collective-permute-start(bf16[256,512]{1,0:T(8,128)(2,1)} %param.1), channel_id=1, source_target_pairs={{0,16},{16,0},{1,17},{17,1},{2,18},{18,2},{3,19},{19,3},{4,20},{20... | collective-permute-start | bytes 786440 | tf_op jit(solution)/shard_map/ppermute | solution.py:21
  3.2 2.6 %collective-permute-start.2 = (bf16[256,512]{1,0:T(8,128)(2,1)}, bf16[256,512]{1,0:T(8,128)(2,1)}, u32[]{:S(2)}, u32[]{:S(2)}) collective-permute-start(bf16[256,512]{1,0:T(8,128)(2,1)} %param.1), channel_id=1, source_target_pairs={{0,128},{64,192},{128,0},{192,64},{1,129},{65,193},{129,1},{193,65... | collective-permute-start | bytes 786440 | tf_op jit(solution)/shard_map/ppermute | solution.py:25
  5.9 1.0 fusion.28
  6.9 0.1 pad_maximum_fusion.4
  7.1 0.1 pad_maximum_fusion.5
  7.4 4.1 %collective-permute-done = bf16[256,512]{1,0:T(8,128)(2,1)S(1)} collective-permute-done((bf16[256,512]{1,0:T(8,128)(2,1)}, bf16[256,512]{1,0:T(8,128)(2,1)S(1)}, u32[]{:S(2)}, u32[]{:S(2)}) %collective-permute-start) | collective-permute-done | bytes 262176 | tf_op jit(solution)/shard_map/ppermute | solution.py:21
  11.5 1.1 collective-permute-start.3
  12.6 0.5 collective-permute-start.4
  13.1 1.0 pad_maximum_fusion.2
  14.1 1.1 collective-permute-start.5
  15.2 1.5 %convolution_convert_fusion.4 = bf16[512,768]{1,0:T(8,128)(2,1)} fusion(bf16[512,512]{1,0:T(8,128)(2,1)S(1)} %bitcast.27, bf16[768,512]{1,0:T(8,128)(2,1)S(1)} %pad_maximum_fusion.2), kind=kOutput, calls=%fused_computation.5 | convolution fusion | flops 403046400 | bytes 2097152 | tf_op jit(solution)/shard_map/dot_general | solution.py:56
  16.8 4.0 %all-to-all-start = ((bf16[4,128,768]{2,1,0:T(8,128)(2,1)}), bf16[4,128,768]{2,1,0:T(8,128)(2,1)S(1)}, u32[]{:S(2)}, u32[]{:S(2)}) async-start(bf16[4,128,768]{2,1,0:T(8,128)(2,1)} %bitcast.34), calls=%async_computation | async-start | bytes 1572864 | tf_op jit(solution)/shard_map/all_to_all | solution.py:89
  20.8 0.3 collective-permute-done.5
  21.1 3.4 %collective-permute-done.3 = bf16[512,512]{1,0:T(8,128)(2,1)S(1)} collective-permute-done((bf16[512,512]{1,0:T(8,128)(2,1)S(1)}, bf16[512,512]{1,0:T(8,128)(2,1)S(1)}, u32[]{:S(2)}, u32[]{:S(2)}) %collective-permute-start.3) | collective-permute-done | bytes 524320 | tf_op jit(solution)/shard_map/ppermute | solution.py:25
  24.5 2.0 %collective-permute-done.4 = bf16[512,512]{1,0:T(8,128)(2,1)} collective-permute-done((bf16[512,512]{1,0:T(8,128)(2,1)S(1)}, bf16[512,512]{1,0:T(8,128)(2,1)}, u32[]{:S(2)}, u32[]{:S(2)}) %collective-permute-start.4) | collective-permute-done | bytes 524320 | tf_op jit(solution)/shard_map/ppermute | solution.py:25
  26.5 1.2 pad_maximum_fusion.1
  27.7 1.3 convolution_convert_fusion.2
  29.0 0.5 convolution_convert_fusion.1
  29.6 1.4 collective-permute-start.6
  31.0 1.5 %collective-permute-start.7 = (bf16[128,1280]{1,0:T(8,128)(2,1)S(1)}, bf16[128,1280]{1,0:T(8,128)(2,1)}, u32[]{:S(2)}, u32[]{:S(2)}) collective-permute-start(bf16[128,1280]{1,0:T(8,128)(2,1)S(1)} %convolution_convert_fusion.1), channel_id=1, source_target_pairs={{0,3},{1,0},{2,1},{3,2},{4,7},{5,4},{6,5},{7,6},{8,11},{9,8},{10,9... | collective-permute-start | bytes 983048 | tf_op jit(solution)/shard_map/ppermute | solution.py:25
  32.5 1.3 convolution_convert_fusion
  33.8 1.5 %collective-permute-start.8 = (bf16[128,1280]{1,0:T(8,128)(2,1)}, bf16[128,1280]{1,0:T(8,128)(2,1)}, u32[]{:S(2)}, u32[]{:S(2)}) collective-permute-start(bf16[128,1280]{1,0:T(8,128)(2,1)} %convolution_convert_fusion), channel_id=1, source_target_pairs={{0,2},{1,3},{2,0},{3,1},{4,6},{5,7},{6,4},{7,5},{8,10},{9,11},{10,... | collective-permute-start | bytes 983048 | tf_op jit(solution)/shard_map/ppermute | solution.py:25
  35.3 0.5 convolution_convert_fusion.3
  35.9 0.1 fusion.10
  36.0 2.8 %collective-permute-done.6 = bf16[128,1280]{1,0:T(8,128)(2,1)} collective-permute-done((bf16[128,1280]{1,0:T(8,128)(2,1)}, bf16[128,1280]{1,0:T(8,128)(2,1)}, u32[]{:S(2)}, u32[]{:S(2)}) %collective-permute-start.6) | collective-permute-done | bytes 327712 | tf_op jit(solution)/shard_map/ppermute | solution.py:25
  38.8 8.1 %collective-permute-done.8 = bf16[128,1280]{1,0:T(8,128)(2,1)} collective-permute-done((bf16[128,1280]{1,0:T(8,128)(2,1)}, bf16[128,1280]{1,0:T(8,128)(2,1)}, u32[]{:S(2)}, u32[]{:S(2)}) %collective-permute-start.8) | collective-permute-done | bytes 327712 | tf_op jit(solution)/shard_map/ppermute | solution.py:25
  46.9 1.3 add_convert_fusion
  48.3 5.6 %collective-permute-start.10 = (bf16[32,2048]{1,0:T(8,128)(2,1)S(1)}, bf16[32,2048]{1,0:T(8,128)(2,1)S(1)}, u32[]{:S(2)}, u32[]{:S(2)}) collective-permute-start(bf16[32,2048]{1,0:T(8,128)(2,1)S(1)} %get-tuple-element.37), channel_id=1, source_target_pairs={{0,12},{4,8},{8,4},{12,0},{1,13},{5,9},{9,5},{13,1},{2,14},{6,10},... | collective-permute-start | bytes 393224 | tf_op jit(solution)/shard_map/ppermute | solution.py:42
  53.9 1.0 collective-permute-start.11
  54.8 1.2 collective-permute-start.9
  56.1 2.9 %collective-permute-done.10 = bf16[32,2048]{1,0:T(8,128)(2,1)S(1)} collective-permute-done((bf16[32,2048]{1,0:T(8,128)(2,1)S(1)}, bf16[32,2048]{1,0:T(8,128)(2,1)S(1)}, u32[]{:S(2)}, u32[]{:S(2)}) %collective-permute-start.10) | collective-permute-done | bytes 131104 | tf_op jit(solution)/shard_map/ppermute | solution.py:42
  59.0 4.4 %collective-permute-done.11 = bf16[32,2048]{1,0:T(8,128)(2,1)S(1)} collective-permute-done((bf16[32,2048]{1,0:T(8,128)(2,1)S(1)}, bf16[32,2048]{1,0:T(8,128)(2,1)S(1)}, u32[]{:S(2)}, u32[]{:S(2)}) %collective-permute-start.11) | collective-permute-done | bytes 131104 | tf_op jit(solution)/shard_map/ppermute | solution.py:42
  63.4 1.0 add_convert_fusion.2
  64.4 15.1 %all_gather.3 = bf16[128,2048]{1,0:T(8,128)(2,1)S(1)} all-gather(bf16[32,2048]{1,0:T(8,128)(2,1)S(1)} %add_convert_fusion.2), channel_id=1, replica_groups=mesh['x'=4,'zl'=2,'core'=2,'zh'=4,'y'=4] {'zh'}, dimensions={0}, use_global_device_ids=true | all-gather | bytes 655360 | tf_op jit(solution)/shard_map/all_gather | solution.py:97
  79.5 0.8 collective-permute-start.12
  80.2 0.7 collective-permute-start.13
  80.9 0.4 fusion.23
  81.4 8.0 %collective-permute-done.13 = bf16[128,2048]{1,0:T(8,128)(2,1)S(1)} collective-permute-done((bf16[128,2048]{1,0:T(8,128)(2,1)S(1)}, bf16[128,2048]{1,0:T(8,128)(2,1)S(1)}, u32[]{:S(2)}, u32[]{:S(2)}) %collective-permute-start.13) | collective-permute-done | bytes 524320 | tf_op jit(solution)/shard_map/ppermute | solution.py:25
  89.6 0.1 collective-permute-start.15
  89.7 1.5 %collective-permute-start.16 = (bf16[64,2048]{1,0:T(8,128)(2,1)S(1)}, bf16[64,2048]{1,0:T(8,128)(2,1)S(1)}, u32[]{:S(2)}, u32[]{:S(2)}) collective-permute-start(bf16[64,2048]{1,0:T(8,128)(2,1)S(1)} %slice.89), channel_id=1, source_target_pairs={{0,1},{1,2},{2,3},{3,0},{4,5},{5,6},{6,7},{7,4},{8,9},{9,10},{10,1... | collective-permute-start | bytes 786440 | tf_op jit(solution)/shard_map/ppermute | solution.py:25
  91.1 0.4 fusion.22
  91.6 0.4 fusion.21
  92.1 13.6 %collective-permute-start.14 = (f32[192,512]{1,0:T(8,128)S(1)}, f32[192,512]{1,0:T(8,128)S(1)}, u32[]{:S(2)}, u32[]{:S(2)}) collective-permute-start(f32[192,512]{1,0:T(8,128)S(1)} %pad_maximum_fusion.7), channel_id=1, source_target_pairs={{0,16},{16,0},{1,17},{17,1},{2,18},{18,2},{3,19},{19,3},{4,20},{20... | collective-permute-start | bytes 1179656 | tf_op jit(solution)/shard_map/ppermute | solution.py:21
  105.8 0.5 fusion.20
  106.3 4.6 %collective-permute-start.17 = (f32[64,512]{1,0:T(8,128)S(1)}, f32[64,512]{1,0:T(8,128)S(1)}, u32[]{:S(2)}, u32[]{:S(2)}) collective-permute-start(f32[64,512]{1,0:T(8,128)S(1)} %fusion.20), channel_id=1, source_target_pairs={{0,16},{16,0},{1,17},{17,1},{2,18},{18,2},{3,19},{19,3},{4,20},{20... | collective-permute-start | bytes 393224 | tf_op jit(solution)/shard_map/ppermute | solution.py:21
  111.0 0.1 maximum_add_fusion
  111.1 0.8 collective-permute-done.17
  111.9 0.5 constant_dynamic-update-slice_fusion.8
  112.5 0.1 collective-permute-start.18
  112.6 1.6 %collective-permute-start.19 = (bf16[256,512]{1,0:T(8,128)(2,1)S(1)}, bf16[256,512]{1,0:T(8,128)(2,1)S(1)}, u32[]{:S(2)}, u32[]{:S(2)}) collective-permute-start(bf16[256,512]{1,0:T(8,128)(2,1)S(1)} %dynamic-slice_convert_fusion), channel_id=1, source_target_pairs={{0,128},{64,192},{128,0},{192,64},{1,129},{65,193},{129,1},{193,65... | collective-permute-start | bytes 786440 | tf_op jit(solution)/shard_map/ppermute | solution.py:25
  114.2 5.9 %collective-permute-done.18 = bf16[256,512]{1,0:T(8,128)(2,1)S(1)} collective-permute-done((bf16[256,512]{1,0:T(8,128)(2,1)S(1)}, bf16[256,512]{1,0:T(8,128)(2,1)S(1)}, u32[]{:S(2)}, u32[]{:S(2)}) %collective-permute-start.18) | collective-permute-done | bytes 262176 | tf_op jit(solution)/shard_map/ppermute | solution.py:21
  120.2 0.7 collective-permute-start.20
  120.9 0.8 collective-permute-start.21
  121.7 0.0 collective-permute-done.19
  121.7 1.0 collective-permute-start.22
  122.8 5.0 %collective-permute-done.22 = bf16[256,512]{1,0:T(8,128)(2,1)S(1)} collective-permute-done((bf16[256,512]{1,0:T(8,128)(2,1)S(1)}, bf16[256,512]{1,0:T(8,128)(2,1)S(1)}, u32[]{:S(2)}, u32[]{:S(2)}) %collective-permute-start.22) | collective-permute-done | bytes 262176 | tf_op jit(solution)/shard_map/ppermute | solution.py:21
  127.8 4.7 %collective-permute-done.20 = bf16[512,512]{1,0:T(8,128)(2,1)S(1)} collective-permute-done((bf16[512,512]{1,0:T(8,128)(2,1)S(1)}, bf16[512,512]{1,0:T(8,128)(2,1)S(1)}, u32[]{:S(2)}, u32[]{:S(2)}) %collective-permute-start.20) | collective-permute-done | bytes 524320 | tf_op jit(solution)/shard_map/ppermute | solution.py:25
  132.5 1.6 %collective-permute-done.21 = bf16[512,512]{1,0:T(8,128)(2,1)S(1)} collective-permute-done((bf16[512,512]{1,0:T(8,128)(2,1)S(1)}, bf16[512,512]{1,0:T(8,128)(2,1)S(1)}, u32[]{:S(2)}, u32[]{:S(2)}) %collective-permute-start.21) | collective-permute-done | bytes 524320 | tf_op jit(solution)/shard_map/ppermute | solution.py:25
  134.2 0.5 fusion.2
  134.8 0.4 convolution_add_fusion
  135.1 2.5 %collective-permute-start.23 = (f32[256,512]{1,0:T(8,128)S(1)}, f32[256,512]{1,0:T(8,128)S(1)}, u32[]{:S(2)}, u32[]{:S(2)}) collective-permute-start(f32[256,512]{1,0:T(8,128)S(1)} %convolution_add_fusion), channel_id=1, source_target_pairs={{0,16},{16,0},{1,17},{17,1},{2,18},{18,2},{3,19},{19,3},{4,20},{20... | collective-permute-start | bytes 1572872 | tf_op jit(solution)/shard_map/ppermute | solution.py:21
  137.6 0.5 fusion.4
  138.2 1.0 collective-permute-done.23
  139.1 1.2 add_multiply_fusion
  (59 shorter events, 1.1 us)
Async XLA Ops:
  0.0 6.8 %collective-permute-start.1 = (bf16[256,512]{1,0:T(8,128)(2,1)}, bf16[256,512]{1,0:T(8,128)(2,1)S(1)}, u32[]{:S(2)}, u32[]{:S(2)}) collective-permute-start(bf16[256,512]{1,0:T(8,128)(2,1)} %param.1), channel_id=1, source_target_pairs={{0,16},{16,0},{1,17},{17,1},{2,18},{18,2},{3,19},{19,3},{4,20},{20... | collective-permute-start | bytes 786440 | tf_op jit(solution)/shard_map/ppermute | solution.py:21
  3.2 8.3 %collective-permute-start = (bf16[256,512]{1,0:T(8,128)(2,1)}, bf16[256,512]{1,0:T(8,128)(2,1)S(1)}, u32[]{:S(2)}, u32[]{:S(2)}) collective-permute-start(bf16[256,512]{1,0:T(8,128)(2,1)} %param.1), channel_id=1, source_target_pairs={{0,32},{32,0},{1,33},{33,1},{2,34},{34,2},{3,35},{35,3},{4,36},{36... | collective-permute-start | bytes 786440 | tf_op jit(solution)/shard_map/ppermute | solution.py:21
  3.2 9.8 %collective-permute-start.2 = (bf16[256,512]{1,0:T(8,128)(2,1)}, bf16[256,512]{1,0:T(8,128)(2,1)}, u32[]{:S(2)}, u32[]{:S(2)}) collective-permute-start(bf16[256,512]{1,0:T(8,128)(2,1)} %param.1), channel_id=1, source_target_pairs={{0,128},{64,192},{128,0},{192,64},{1,129},{65,193},{129,1},{193,65... | collective-permute-start | bytes 786440 | tf_op jit(solution)/shard_map/ppermute | solution.py:25
  7.1 4.4 %copy-start = (bf16[256,512]{1,0:T(8,128)(2,1)S(1)}, bf16[256,512]{1,0:T(8,128)(2,1)}, u32[]{:S(2)}) copy-start(bf16[256,512]{1,0:T(8,128)(2,1)} %param.1) | copy-start | bytes 786436
  11.5 13.0 %collective-permute-start.3 = (bf16[512,512]{1,0:T(8,128)(2,1)S(1)}, bf16[512,512]{1,0:T(8,128)(2,1)S(1)}, u32[]{:S(2)}, u32[]{:S(2)}) collective-permute-start(bf16[512,512]{1,0:T(8,128)(2,1)S(1)} %pad_maximum_fusion.3), channel_id=1, source_target_pairs={{0,192},{64,0},{128,64},{192,128},{1,193},{65,1},{129,65},{193,129... | collective-permute-start | bytes 1572872 | tf_op jit(solution)/shard_map/ppermute | solution.py:25
  12.6 13.9 %collective-permute-start.4 = (bf16[512,512]{1,0:T(8,128)(2,1)S(1)}, bf16[512,512]{1,0:T(8,128)(2,1)}, u32[]{:S(2)}, u32[]{:S(2)}) collective-permute-start(bf16[512,512]{1,0:T(8,128)(2,1)S(1)} %pad_maximum_fusion.3), channel_id=1, source_target_pairs={{0,64},{64,128},{128,192},{192,0},{1,65},{65,129},{129,193},{193,1... | collective-permute-start | bytes 1572872 | tf_op jit(solution)/shard_map/ppermute | solution.py:25
  14.1 2.7 %copy-start.1 = (bf16[768,512]{1,0:T(8,128)(2,1)}, bf16[768,512]{1,0:T(8,128)(2,1)S(1)}, u32[]{:S(2)}) copy-start(bf16[768,512]{1,0:T(8,128)(2,1)S(1)} %pad_maximum_fusion.2) | copy-start | bytes 2359300
  14.1 7.0 %collective-permute-start.5 = (bf16[256,512]{1,0:T(8,128)(2,1)}, bf16[256,512]{1,0:T(8,128)(2,1)}, u32[]{:S(2)}, u32[]{:S(2)}) collective-permute-start(bf16[256,512]{1,0:T(8,128)(2,1)} %collective-permute-done.2), channel_id=1, source_target_pairs={{0,32},{32,0},{1,33},{33,1},{2,34},{34,2},{3,35},{35,3},{4,36},{36... | collective-permute-start | bytes 786440 | tf_op jit(solution)/shard_map/ppermute | solution.py:21
  16.8 19.1 %all-to-all-start = ((bf16[4,128,768]{2,1,0:T(8,128)(2,1)}), bf16[4,128,768]{2,1,0:T(8,128)(2,1)S(1)}, u32[]{:S(2)}, u32[]{:S(2)}) async-start(bf16[4,128,768]{2,1,0:T(8,128)(2,1)} %bitcast.34), calls=%async_computation | async-start | bytes 1572864 | tf_op jit(solution)/shard_map/all_to_all | solution.py:89
  29.6 9.2 %collective-permute-start.6 = (bf16[128,1280]{1,0:T(8,128)(2,1)}, bf16[128,1280]{1,0:T(8,128)(2,1)}, u32[]{:S(2)}, u32[]{:S(2)}) collective-permute-start(bf16[128,1280]{1,0:T(8,128)(2,1)} %convolution_convert_fusion.2), channel_id=1, source_target_pairs={{0,1},{1,2},{2,3},{3,0},{4,5},{5,6},{6,7},{7,4},{8,9},{9,10},{10,1... | collective-permute-start | bytes 983048 | tf_op jit(solution)/shard_map/ppermute | solution.py:25
  31.0 7.8 %collective-permute-start.7 = (bf16[128,1280]{1,0:T(8,128)(2,1)S(1)}, bf16[128,1280]{1,0:T(8,128)(2,1)}, u32[]{:S(2)}, u32[]{:S(2)}) collective-permute-start(bf16[128,1280]{1,0:T(8,128)(2,1)S(1)} %convolution_convert_fusion.1), channel_id=1, source_target_pairs={{0,3},{1,0},{2,1},{3,2},{4,7},{5,4},{6,5},{7,6},{8,11},{9,8},{10,9... | collective-permute-start | bytes 983048 | tf_op jit(solution)/shard_map/ppermute | solution.py:25
  33.8 13.1 %collective-permute-start.8 = (bf16[128,1280]{1,0:T(8,128)(2,1)}, bf16[128,1280]{1,0:T(8,128)(2,1)}, u32[]{:S(2)}, u32[]{:S(2)}) collective-permute-start(bf16[128,1280]{1,0:T(8,128)(2,1)} %convolution_convert_fusion), channel_id=1, source_target_pairs={{0,2},{1,3},{2,0},{3,1},{4,6},{5,7},{6,4},{7,5},{8,10},{9,11},{10,... | collective-permute-start | bytes 983048 | tf_op jit(solution)/shard_map/ppermute | solution.py:25
  36.0 45.0 %copy-start.2 = (bf16[768,512]{1,0:T(8,128)(2,1)S(1)}, bf16[768,512]{1,0:T(8,128)(2,1)}, u32[]{:S(2)}) copy-start(bf16[768,512]{1,0:T(8,128)(2,1)} %copy-done.1) | copy-start | bytes 2359300
  48.3 10.7 %collective-permute-start.10 = (bf16[32,2048]{1,0:T(8,128)(2,1)S(1)}, bf16[32,2048]{1,0:T(8,128)(2,1)S(1)}, u32[]{:S(2)}, u32[]{:S(2)}) collective-permute-start(bf16[32,2048]{1,0:T(8,128)(2,1)S(1)} %get-tuple-element.37), channel_id=1, source_target_pairs={{0,12},{4,8},{8,4},{12,0},{1,13},{5,9},{9,5},{13,1},{2,14},{6,10},... | collective-permute-start | bytes 393224 | tf_op jit(solution)/shard_map/ppermute | solution.py:42
  53.9 9.5 %collective-permute-start.11 = (bf16[32,2048]{1,0:T(8,128)(2,1)S(1)}, bf16[32,2048]{1,0:T(8,128)(2,1)S(1)}, u32[]{:S(2)}, u32[]{:S(2)}) collective-permute-start(bf16[32,2048]{1,0:T(8,128)(2,1)S(1)} %get-tuple-element.36), channel_id=1, source_target_pairs={{0,8},{4,12},{8,0},{12,4},{1,9},{5,13},{9,1},{13,5},{2,10},{6,14},... | collective-permute-start | bytes 393224 | tf_op jit(solution)/shard_map/ppermute | solution.py:42
  54.8 8.6 %collective-permute-start.9 = (bf16[32,2048]{1,0:T(8,128)(2,1)S(1)}, bf16[32,2048]{1,0:T(8,128)(2,1)}, u32[]{:S(2)}, u32[]{:S(2)}) collective-permute-start(bf16[32,2048]{1,0:T(8,128)(2,1)S(1)} %get-tuple-element.35), channel_id=1, source_target_pairs={{0,4},{4,0},{8,12},{12,8},{1,5},{5,1},{9,13},{13,9},{2,6},{6,2},{1... | collective-permute-start | bytes 393224 | tf_op jit(solution)/shard_map/ppermute | solution.py:42
  79.5 10.0 %collective-permute-start.12 = (bf16[128,2048]{1,0:T(8,128)(2,1)S(1)}, bf16[128,2048]{1,0:T(8,128)(2,1)S(1)}, u32[]{:S(2)}, u32[]{:S(2)}) collective-permute-start(bf16[128,2048]{1,0:T(8,128)(2,1)S(1)} %all_gather.3), channel_id=1, source_target_pairs={{0,3},{1,0},{2,1},{3,2},{4,7},{5,4},{6,5},{7,6},{8,11},{9,8},{10,9... | collective-permute-start | bytes 1572872 | tf_op jit(solution)/shard_map/ppermute | solution.py:25
  80.2 9.2 %collective-permute-start.13 = (bf16[128,2048]{1,0:T(8,128)(2,1)S(1)}, bf16[128,2048]{1,0:T(8,128)(2,1)S(1)}, u32[]{:S(2)}, u32[]{:S(2)}) collective-permute-start(bf16[128,2048]{1,0:T(8,128)(2,1)S(1)} %all_gather.3), channel_id=1, source_target_pairs={{0,1},{1,2},{2,3},{3,0},{4,5},{5,6},{6,7},{7,4},{8,9},{9,10},{10,1... | collective-permute-start | bytes 1572872 | tf_op jit(solution)/shard_map/ppermute | solution.py:25
  89.6 16.1 %collective-permute-start.15 = (bf16[64,2048]{1,0:T(8,128)(2,1)S(1)}, bf16[64,2048]{1,0:T(8,128)(2,1)S(1)}, u32[]{:S(2)}, u32[]{:S(2)}) collective-permute-start(bf16[64,2048]{1,0:T(8,128)(2,1)S(1)} %get-tuple-element.20), channel_id=1, source_target_pairs={{0,3},{1,0},{2,1},{3,2},{4,7},{5,4},{6,5},{7,6},{8,11},{9,8},{10,9... | collective-permute-start | bytes 786440 | tf_op jit(solution)/shard_map/ppermute | solution.py:25
  89.7 16.0 %collective-permute-start.16 = (bf16[64,2048]{1,0:T(8,128)(2,1)S(1)}, bf16[64,2048]{1,0:T(8,128)(2,1)S(1)}, u32[]{:S(2)}, u32[]{:S(2)}) collective-permute-start(bf16[64,2048]{1,0:T(8,128)(2,1)S(1)} %slice.89), channel_id=1, source_target_pairs={{0,1},{1,2},{2,3},{3,0},{4,5},{5,6},{6,7},{7,4},{8,9},{9,10},{10,1... | collective-permute-start | bytes 786440 | tf_op jit(solution)/shard_map/ppermute | solution.py:25
  92.1 18.9 %collective-permute-start.14 = (f32[192,512]{1,0:T(8,128)S(1)}, f32[192,512]{1,0:T(8,128)S(1)}, u32[]{:S(2)}, u32[]{:S(2)}) collective-permute-start(f32[192,512]{1,0:T(8,128)S(1)} %pad_maximum_fusion.7), channel_id=1, source_target_pairs={{0,16},{16,0},{1,17},{17,1},{2,18},{18,2},{3,19},{19,3},{4,20},{20... | collective-permute-start | bytes 1179656 | tf_op jit(solution)/shard_map/ppermute | solution.py:21
  106.3 5.6 %collective-permute-start.17 = (f32[64,512]{1,0:T(8,128)S(1)}, f32[64,512]{1,0:T(8,128)S(1)}, u32[]{:S(2)}, u32[]{:S(2)}) collective-permute-start(f32[64,512]{1,0:T(8,128)S(1)} %fusion.20), channel_id=1, source_target_pairs={{0,16},{16,0},{1,17},{17,1},{2,18},{18,2},{3,19},{19,3},{4,20},{20... | collective-permute-start | bytes 393224 | tf_op jit(solution)/shard_map/ppermute | solution.py:21
  112.5 7.6 %collective-permute-start.18 = (bf16[256,512]{1,0:T(8,128)(2,1)S(1)}, bf16[256,512]{1,0:T(8,128)(2,1)S(1)}, u32[]{:S(2)}, u32[]{:S(2)}) collective-permute-start(bf16[256,512]{1,0:T(8,128)(2,1)S(1)} %dynamic-slice_convert_fusion), channel_id=1, source_target_pairs={{0,32},{32,0},{1,33},{33,1},{2,34},{34,2},{3,35},{35,3},{4,36},{36... | collective-permute-start | bytes 786440 | tf_op jit(solution)/shard_map/ppermute | solution.py:21
  112.6 9.1 %collective-permute-start.19 = (bf16[256,512]{1,0:T(8,128)(2,1)S(1)}, bf16[256,512]{1,0:T(8,128)(2,1)S(1)}, u32[]{:S(2)}, u32[]{:S(2)}) collective-permute-start(bf16[256,512]{1,0:T(8,128)(2,1)S(1)} %dynamic-slice_convert_fusion), channel_id=1, source_target_pairs={{0,128},{64,192},{128,0},{192,64},{1,129},{65,193},{129,1},{193,65... | collective-permute-start | bytes 786440 | tf_op jit(solution)/shard_map/ppermute | solution.py:25
  120.2 12.3 %collective-permute-start.20 = (bf16[512,512]{1,0:T(8,128)(2,1)S(1)}, bf16[512,512]{1,0:T(8,128)(2,1)S(1)}, u32[]{:S(2)}, u32[]{:S(2)}) collective-permute-start(bf16[512,512]{1,0:T(8,128)(2,1)S(1)} %pad_maximum_fusion.6), channel_id=1, source_target_pairs={{0,192},{64,0},{128,64},{192,128},{1,193},{65,1},{129,65},{193,129... | collective-permute-start | bytes 1572872 | tf_op jit(solution)/shard_map/ppermute | solution.py:25
  120.9 13.2 %collective-permute-start.21 = (bf16[512,512]{1,0:T(8,128)(2,1)S(1)}, bf16[512,512]{1,0:T(8,128)(2,1)S(1)}, u32[]{:S(2)}, u32[]{:S(2)}) collective-permute-start(bf16[512,512]{1,0:T(8,128)(2,1)S(1)} %pad_maximum_fusion.6), channel_id=1, source_target_pairs={{0,64},{64,128},{128,192},{192,0},{1,65},{65,129},{129,193},{193,1... | collective-permute-start | bytes 1572872 | tf_op jit(solution)/shard_map/ppermute | solution.py:25
  121.7 6.1 %collective-permute-start.22 = (bf16[256,512]{1,0:T(8,128)(2,1)S(1)}, bf16[256,512]{1,0:T(8,128)(2,1)S(1)}, u32[]{:S(2)}, u32[]{:S(2)}) collective-permute-start(bf16[256,512]{1,0:T(8,128)(2,1)S(1)} %collective-permute-done.19), channel_id=1, source_target_pairs={{0,32},{32,0},{1,33},{33,1},{2,34},{34,2},{3,35},{35,3},{4,36},{36... | collective-permute-start | bytes 786440 | tf_op jit(solution)/shard_map/ppermute | solution.py:21
  135.1 4.0 %collective-permute-start.23 = (f32[256,512]{1,0:T(8,128)S(1)}, f32[256,512]{1,0:T(8,128)S(1)}, u32[]{:S(2)}, u32[]{:S(2)}) collective-permute-start(f32[256,512]{1,0:T(8,128)S(1)} %convolution_add_fusion), channel_id=1, source_target_pairs={{0,16},{16,0},{1,17},{17,1},{2,18},{18,2},{3,19},{19,3},{4,20},{20... | collective-permute-start | bytes 1572872 | tf_op jit(solution)/shard_map/ppermute | solution.py:21

commit v20 on v19

--- a/solution.py
+++ b/solution.py
@@ -32,10 +32,6 @@
 def add(got):
     got = [g.astype(F32) for g in got]
     return ((got[0] + got[1]) + (got[2] + got[3])).astype(BF)
-
-
-def scatter(pieces, axis):
-    return [send(pieces[k], axis, k) for k in (0, 1, 3, 2)]
 
 
 def scatter_pairs(pieces, axis):
@@ -81,7 +77,8 @@
     own = jnp.stack(own).reshape(4, 4, 32, 512)
     own = [lax.dynamic_slice_in_dim(own, zh ^ k, 1, 1) for k in range(4)]
     own = jnp.concatenate(own, axis=1).reshape(512, 512)
-    turned = window(chunks(own), y, 4)
+    turned = [lax.dynamic_slice_in_dim(own, (y ^ k) * 128, 128) for k in range(4)]
+    turned = jnp.concatenate(turned, axis=0)
     pair, own, turned = lax.optimization_barrier((pair, own, turned))
     early = lax.optimization_barrier(jnp.concatenate([pair, far], axis=0))
     pieces = matmul(own, early, ((1,), (1,))).astype(BF)
@@ -90,7 +87,7 @@
     panel = lax.optimization_barrier(jnp.concatenate(late, axis=0))
     pieces = [matmul(rows, panel, ((1,), (1,))).astype(BF) for rows in chunks(turned)]
     pieces[0] = lax.optimization_barrier(pieces[0])
-    second = add(scatter(pieces, "y"))
+    second = add(scatter_pairs(pieces, "y"))
     part = jnp.concatenate([first, second], axis=1)
     panel = jnp.concatenate([early, panel], axis=0)
     part = add(scatter_pairs(chunks(part), "zh"))

time: 141 us -> 140 us (level)
  starting transfers between devices: 52.8 us -> 50 us
  waiting for transfers between devices: 55.1 us -> 57.7 us
    ppermute x3 -> x6, waiting for transfers between devices: 7.35 us -> 18.7 us  [scatter_pairs(): lax.ppermute(pieces[k], axis, [(i, i ^ k) for i in range(4)])]
    ppermute x13 -> x10, waiting for transfers between devices: 30.7 us -> 20.3 us  [send(): lax.ppermute(array, axis, [(i, (i + k) % 4) for i in range(4)])]
    ppermute x13 -> x10, starting transfers between devices: 14.8 us -> 9 us  [send(): lax.ppermute(array, axis, [(i, (i + k) % 4) for i in range(4)])]
    ppermute x3 -> x6, starting transfers between devices: 7.79 us -> 11.8 us  [scatter_pairs(): lax.ppermute(pieces[k], axis, [(i, i ^ k) for i in range(4)])]
    ppermute x8, waiting for transfers between devices: 17 us -> 18.6 us  [swap(): return lax.ppermute(array, axis, [(0, 1), (1, 0)])]
  transfers between devices with their start and end apart: 25 -> 25, of which waited for: 15 -> 16; matrix products, arithmetic and copies ran while one was open for 8% -> 8% of each run, Pallas kernels for 0% -> 0%
where the time goes in v20:
time: 140 us
  waiting for transfers between devices  57.7 us (41%)
  starting transfers between devices  50 us (36%)
  blocking collectives  15.1 us (11%)
  matrix products  10.1 us (7%)
  other arithmetic  5.01 us (4%)
  local copies, waits for them, and re-layouts  1.71 us (1%)
    ppermute x8, starting transfers between devices, swap(): return lax.ppermute(array, axis, [(0, 1), (1, 0)])  25.2 us
    ppermute x10, waiting for transfers between devices, send(): lax.ppermute(array, axis, [(i, (i + k) % 4) for i in range(4)])  20.3 us
    ppermute x6, waiting for transfers between devices, scatter_pairs(): lax.ppermute(pieces[k], axis, [(i, i ^ k) for i in range(4)])  18.7 us
    ppermute x8, waiting for transfers between devices, swap(): return lax.ppermute(array, axis, [(0, 1), (1, 0)])  18.6 us
    all_gather x1, blocking collectives, per_device(): near = lax.all_gather(part, 'zh', axis=0, tiled=True)  15.1 us
    ppermute x6, starting transfers between devices, scatter_pairs(): lax.ppermute(pieces[k], axis, [(i, i ^ k) for i in range(4)])  11.8 us
    dot_general x14, matrix products, matmul(): return lax.dot_general(a, b, (dims, ((), ())), preferred_element_type=F32)  10.1 us
    ppermute x10, starting transfers between devices, send(): lax.ppermute(array, axis, [(i, (i + k) % 4) for i in range(4)])  9 us
  transfers between devices with their start and end apart: 25, of which 16 were waited for; matrix products, arithmetic and copies ran while one was open for 8% of the time, Pallas kernels for 0%

profile of v20, /device:TPU:1, one launch (start us, length us, event | category | flops | bytes accessed | tf_op | source)
XLA Modules:
  0.0 140.1 jit_solution(11338318831113698781)
XLA Ops:
  0.0 3.2 %collective-permute-start.1 = (bf16[256,512]{1,0:T(8,128)(2,1)}, bf16[256,512]{1,0:T(8,128)(2,1)S(1)}, u32[]{:S(2)}, u32[]{:S(2)}) collective-permute-start(bf16[256,512]{1,0:T(8,128)(2,1)} %param.1), channel_id=1, source_target_pairs={{0,16},{16,0},{1,17},{17,1},{2,18},{18,2},{3,19},{19,3},{4,20},{20... | collective-permute-start | bytes 786440 | tf_op jit(solution)/shard_map/ppermute | solution.py:21
  3.2 2.6 %collective-permute-start.2 = (bf16[256,512]{1,0:T(8,128)(2,1)}, bf16[256,512]{1,0:T(8,128)(2,1)}, u32[]{:S(2)}, u32[]{:S(2)}) collective-permute-start(bf16[256,512]{1,0:T(8,128)(2,1)} %param.1), channel_id=1, source_target_pairs={{0,128},{64,192},{128,0},{192,64},{1,129},{65,193},{129,1},{193,65... | collective-permute-start | bytes 786440 | tf_op jit(solution)/shard_map/ppermute | solution.py:25
  5.9 1.0 fusion.27
  6.9 0.1 pad_maximum_fusion.4
  7.1 0.1 pad_maximum_fusion.5
  7.3 4.2 %collective-permute-done = bf16[256,512]{1,0:T(8,128)(2,1)S(1)} collective-permute-done((bf16[256,512]{1,0:T(8,128)(2,1)}, bf16[256,512]{1,0:T(8,128)(2,1)S(1)}, u32[]{:S(2)}, u32[]{:S(2)}) %collective-permute-start) | collective-permute-done | bytes 262176 | tf_op jit(solution)/shard_map/ppermute | solution.py:21
  11.5 1.1 collective-permute-start.3
  12.6 0.5 collective-permute-start.4
  13.1 1.0 pad_maximum_fusion.2
  14.1 1.1 collective-permute-start.5
  15.2 1.5 %convolution_convert_fusion.4 = bf16[512,768]{1,0:T(8,128)(2,1)} fusion(bf16[512,512]{1,0:T(8,128)(2,1)S(1)} %bitcast.24, bf16[768,512]{1,0:T(8,128)(2,1)S(1)} %pad_maximum_fusion.2), kind=kOutput, calls=%fused_computation.5 | convolution fusion | flops 403046400 | bytes 2097152 | tf_op jit(solution)/shard_map/dot_general | solution.py:52
  16.8 4.0 %all-to-all-start = ((bf16[4,128,768]{2,1,0:T(8,128)(2,1)}), bf16[4,128,768]{2,1,0:T(8,128)(2,1)S(1)}, u32[]{:S(2)}, u32[]{:S(2)}) async-start(bf16[4,128,768]{2,1,0:T(8,128)(2,1)} %bitcast.25), calls=%async_computation | async-start | bytes 1572864 | tf_op jit(solution)/shard_map/all_to_all | solution.py:86
  20.8 0.3 collective-permute-done.5
  21.1 3.4 %collective-permute-done.3 = bf16[512,512]{1,0:T(8,128)(2,1)S(1)} collective-permute-done((bf16[512,512]{1,0:T(8,128)(2,1)S(1)}, bf16[512,512]{1,0:T(8,128)(2,1)S(1)}, u32[]{:S(2)}, u32[]{:S(2)}) %collective-permute-start.3) | collective-permute-done | bytes 524320 | tf_op jit(solution)/shard_map/ppermute | solution.py:25
  24.5 2.0 %collective-permute-done.4 = bf16[512,512]{1,0:T(8,128)(2,1)} collective-permute-done((bf16[512,512]{1,0:T(8,128)(2,1)S(1)}, bf16[512,512]{1,0:T(8,128)(2,1)}, u32[]{:S(2)}, u32[]{:S(2)}) %collective-permute-start.4) | collective-permute-done | bytes 524320 | tf_op jit(solution)/shard_map/ppermute | solution.py:25
  26.5 1.2 pad_maximum_fusion.1
  27.7 1.3 convolution_convert_fusion.2
  29.0 0.5 convolution_convert_fusion.1
  29.6 1.4 collective-permute-start.6
  31.0 1.9 %collective-permute-start.7 = (bf16[128,1280]{1,0:T(8,128)(2,1)S(1)}, bf16[128,1280]{1,0:T(8,128)(2,1)}, u32[]{:S(2)}, u32[]{:S(2)}) collective-permute-start(bf16[128,1280]{1,0:T(8,128)(2,1)S(1)} %convolution_convert_fusion.1), channel_id=1, source_target_pairs={{0,3},{1,2},{2,1},{3,0},{4,7},{5,6},{6,5},{7,4},{8,11},{9,10},{10,... | collective-permute-start | bytes 983048 | tf_op jit(solution)/shard_map/ppermute | solution.py:38
  32.9 1.3 convolution_convert_fusion
  34.1 0.7 collective-permute-start.8
  34.9 0.5 convolution_convert_fusion.3
  35.4 0.1 fusion.10
  35.5 1.9 %collective-permute-done.6 = bf16[128,1280]{1,0:T(8,128)(2,1)} collective-permute-done((bf16[128,1280]{1,0:T(8,128)(2,1)}, bf16[128,1280]{1,0:T(8,128)(2,1)}, u32[]{:S(2)}, u32[]{:S(2)}) %collective-permute-start.6) | collective-permute-done | bytes 327712 | tf_op jit(solution)/shard_map/ppermute | solution.py:38
  37.4 2.0 %collective-permute-done.7 = bf16[128,1280]{1,0:T(8,128)(2,1)} collective-permute-done((bf16[128,1280]{1,0:T(8,128)(2,1)S(1)}, bf16[128,1280]{1,0:T(8,128)(2,1)}, u32[]{:S(2)}, u32[]{:S(2)}) %collective-permute-start.7) | collective-permute-done | bytes 327712 | tf_op jit(solution)/shard_map/ppermute | solution.py:38
  39.4 7.5 %collective-permute-done.8 = bf16[128,1280]{1,0:T(8,128)(2,1)} collective-permute-done((bf16[128,1280]{1,0:T(8,128)(2,1)}, bf16[128,1280]{1,0:T(8,128)(2,1)}, u32[]{:S(2)}, u32[]{:S(2)}) %collective-permute-start.8) | collective-permute-done | bytes 327712 | tf_op jit(solution)/shard_map/ppermute | solution.py:38
  46.9 1.3 add_convert_fusion
  48.3 5.6 %collective-permute-start.10 = (bf16[32,2048]{1,0:T(8,128)(2,1)S(1)}, bf16[32,2048]{1,0:T(8,128)(2,1)S(1)}, u32[]{:S(2)}, u32[]{:S(2)}) collective-permute-start(bf16[32,2048]{1,0:T(8,128)(2,1)S(1)} %get-tuple-element.37), channel_id=1, source_target_pairs={{0,12},{4,8},{8,4},{12,0},{1,13},{5,9},{9,5},{13,1},{2,14},{6,10},... | collective-permute-start | bytes 393224 | tf_op jit(solution)/shard_map/ppermute | solution.py:38
  53.9 1.0 collective-permute-start.11
  54.9 1.2 collective-permute-start.9
  56.1 2.9 %collective-permute-done.10 = bf16[32,2048]{1,0:T(8,128)(2,1)S(1)} collective-permute-done((bf16[32,2048]{1,0:T(8,128)(2,1)S(1)}, bf16[32,2048]{1,0:T(8,128)(2,1)S(1)}, u32[]{:S(2)}, u32[]{:S(2)}) %collective-permute-start.10) | collective-permute-done | bytes 131104 | tf_op jit(solution)/shard_map/ppermute | solution.py:38
  59.0 4.4 %collective-permute-done.11 = bf16[32,2048]{1,0:T(8,128)(2,1)S(1)} collective-permute-done((bf16[32,2048]{1,0:T(8,128)(2,1)S(1)}, bf16[32,2048]{1,0:T(8,128)(2,1)S(1)}, u32[]{:S(2)}, u32[]{:S(2)}) %collective-permute-start.11) | collective-permute-done | bytes 131104 | tf_op jit(solution)/shard_map/ppermute | solution.py:38
  63.4 1.0 add_convert_fusion.2
  64.4 15.1 %all_gather.3 = bf16[128,2048]{1,0:T(8,128)(2,1)S(1)} all-gather(bf16[32,2048]{1,0:T(8,128)(2,1)S(1)} %add_convert_fusion.2), channel_id=1, replica_groups=mesh['x'=4,'zl'=2,'core'=2,'zh'=4,'y'=4] {'zh'}, dimensions={0}, use_global_device_ids=true | all-gather | bytes 655360 | tf_op jit(solution)/shard_map/all_gather | solution.py:94
  79.5 1.3 collective-permute-start.12
  80.8 0.2 collective-permute-start.13
  80.9 0.4 fusion.23
  81.5 8.6 %collective-permute-done.13 = bf16[128,2048]{1,0:T(8,128)(2,1)S(1)} collective-permute-done((bf16[128,2048]{1,0:T(8,128)(2,1)S(1)}, bf16[128,2048]{1,0:T(8,128)(2,1)S(1)}, u32[]{:S(2)}, u32[]{:S(2)}) %collective-permute-start.13) | collective-permute-done | bytes 524320 | tf_op jit(solution)/shard_map/ppermute | solution.py:25
  90.1 0.3 collective-permute-start.15
  90.4 1.5 %collective-permute-start.16 = (bf16[64,2048]{1,0:T(8,128)(2,1)S(1)}, bf16[64,2048]{1,0:T(8,128)(2,1)S(1)}, u32[]{:S(2)}, u32[]{:S(2)}) collective-permute-start(bf16[64,2048]{1,0:T(8,128)(2,1)S(1)} %slice.85), channel_id=1, source_target_pairs={{0,1},{1,2},{2,3},{3,0},{4,5},{5,6},{6,7},{7,4},{8,9},{9,10},{10,1... | collective-permute-start | bytes 786440 | tf_op jit(solution)/shard_map/ppermute | solution.py:25
  91.8 0.4 fusion.22
  92.3 0.4 fusion.21
  92.8 12.8 %collective-permute-start.14 = (f32[192,512]{1,0:T(8,128)S(1)}, f32[192,512]{1,0:T(8,128)S(1)}, u32[]{:S(2)}, u32[]{:S(2)}) collective-permute-start(f32[192,512]{1,0:T(8,128)S(1)} %pad_maximum_fusion.8), channel_id=1, source_target_pairs={{0,16},{16,0},{1,17},{17,1},{2,18},{18,2},{3,19},{19,3},{4,20},{20... | collective-permute-start | bytes 1179656 | tf_op jit(solution)/shard_map/ppermute | solution.py:21
  105.8 0.5 fusion.20
  106.3 4.6 %collective-permute-start.17 = (f32[64,512]{1,0:T(8,128)S(1)}, f32[64,512]{1,0:T(8,128)S(1)}, u32[]{:S(2)}, u32[]{:S(2)}) collective-permute-start(f32[64,512]{1,0:T(8,128)S(1)} %fusion.20), channel_id=1, source_target_pairs={{0,16},{16,0},{1,17},{17,1},{2,18},{18,2},{3,19},{19,3},{4,20},{20... | collective-permute-start | bytes 393224 | tf_op jit(solution)/shard_map/ppermute | solution.py:21
  111.0 0.1 maximum_add_fusion
  111.1 0.8 collective-permute-done.17
  111.9 0.5 constant_dynamic-update-slice_fusion.1
  112.5 0.1 collective-permute-start.18
  112.6 0.1 collective-permute-start.19
  112.7 7.4 %collective-permute-done.18 = bf16[256,512]{1,0:T(8,128)(2,1)S(1)} collective-permute-done((bf16[256,512]{1,0:T(8,128)(2,1)S(1)}, bf16[256,512]{1,0:T(8,128)(2,1)S(1)}, u32[]{:S(2)}, u32[]{:S(2)}) %collective-permute-start.18) | collective-permute-done | bytes 262176 | tf_op jit(solution)/shard_map/ppermute | solution.py:21
  120.1 0.4 collective-permute-start.20
  120.6 1.1 collective-permute-start.21
  121.7 1.0 collective-permute-start.22
  122.8 5.0 %collective-permute-done.22 = bf16[256,512]{1,0:T(8,128)(2,1)S(1)} collective-permute-done((bf16[256,512]{1,0:T(8,128)(2,1)S(1)}, bf16[256,512]{1,0:T(8,128)(2,1)S(1)}, u32[]{:S(2)}, u32[]{:S(2)}) %collective-permute-start.22) | collective-permute-done | bytes 262176 | tf_op jit(solution)/shard_map/ppermute | solution.py:21
  127.8 4.7 %collective-permute-done.20 = bf16[512,512]{1,0:T(8,128)(2,1)S(1)} collective-permute-done((bf16[512,512]{1,0:T(8,128)(2,1)S(1)}, bf16[512,512]{1,0:T(8,128)(2,1)S(1)}, u32[]{:S(2)}, u32[]{:S(2)}) %collective-permute-start.20) | collective-permute-done | bytes 524320 | tf_op jit(solution)/shard_map/ppermute | solution.py:25
  132.5 1.6 %collective-permute-done.21 = bf16[512,512]{1,0:T(8,128)(2,1)S(1)} collective-permute-done((bf16[512,512]{1,0:T(8,128)(2,1)S(1)}, bf16[512,512]{1,0:T(8,128)(2,1)S(1)}, u32[]{:S(2)}, u32[]{:S(2)}) %collective-permute-start.21) | collective-permute-done | bytes 524320 | tf_op jit(solution)/shard_map/ppermute | solution.py:25
  134.2 0.5 fusion.2
  134.7 0.4 convolution_add_fusion
  135.1 2.2 %collective-permute-start.23 = (f32[256,512]{1,0:T(8,128)S(1)}, f32[256,512]{1,0:T(8,128)S(1)}, u32[]{:S(2)}, u32[]{:S(2)}) collective-permute-start(f32[256,512]{1,0:T(8,128)S(1)} %convolution_add_fusion), channel_id=1, source_target_pairs={{0,16},{16,0},{1,17},{17,1},{2,18},{18,2},{3,19},{19,3},{4,20},{20... | collective-permute-start | bytes 1572872 | tf_op jit(solution)/shard_map/ppermute | solution.py:21
  137.3 0.5 fusion.4
  137.8 1.0 collective-permute-done.23
  138.8 1.2 add_multiply_fusion
  (52 shorter events, 1.0 us)
Async XLA Ops:
  0.0 6.8 %collective-permute-start.1 = (bf16[256,512]{1,0:T(8,128)(2,1)}, bf16[256,512]{1,0:T(8,128)(2,1)S(1)}, u32[]{:S(2)}, u32[]{:S(2)}) collective-permute-start(bf16[256,512]{1,0:T(8,128)(2,1)} %param.1), channel_id=1, source_target_pairs={{0,16},{16,0},{1,17},{17,1},{2,18},{18,2},{3,19},{19,3},{4,20},{20... | collective-permute-start | bytes 786440 | tf_op jit(solution)/shard_map/ppermute | solution.py:21
  3.2 8.3 %collective-permute-start = (bf16[256,512]{1,0:T(8,128)(2,1)}, bf16[256,512]{1,0:T(8,128)(2,1)S(1)}, u32[]{:S(2)}, u32[]{:S(2)}) collective-permute-start(bf16[256,512]{1,0:T(8,128)(2,1)} %param.1), channel_id=1, source_target_pairs={{0,32},{32,0},{1,33},{33,1},{2,34},{34,2},{3,35},{35,3},{4,36},{36... | collective-permute-start | bytes 786440 | tf_op jit(solution)/shard_map/ppermute | solution.py:21
  3.2 9.8 %collective-permute-start.2 = (bf16[256,512]{1,0:T(8,128)(2,1)}, bf16[256,512]{1,0:T(8,128)(2,1)}, u32[]{:S(2)}, u32[]{:S(2)}) collective-permute-start(bf16[256,512]{1,0:T(8,128)(2,1)} %param.1), channel_id=1, source_target_pairs={{0,128},{64,192},{128,0},{192,64},{1,129},{65,193},{129,1},{193,65... | collective-permute-start | bytes 786440 | tf_op jit(solution)/shard_map/ppermute | solution.py:25
  7.1 4.4 %copy-start = (bf16[256,512]{1,0:T(8,128)(2,1)S(1)}, bf16[256,512]{1,0:T(8,128)(2,1)}, u32[]{:S(2)}) copy-start(bf16[256,512]{1,0:T(8,128)(2,1)} %param.1) | copy-start | bytes 786436
  11.5 13.0 %collective-permute-start.3 = (bf16[512,512]{1,0:T(8,128)(2,1)S(1)}, bf16[512,512]{1,0:T(8,128)(2,1)S(1)}, u32[]{:S(2)}, u32[]{:S(2)}) collective-permute-start(bf16[512,512]{1,0:T(8,128)(2,1)S(1)} %pad_maximum_fusion.3), channel_id=1, source_target_pairs={{0,192},{64,0},{128,64},{192,128},{1,193},{65,1},{129,65},{193,129... | collective-permute-start | bytes 1572872 | tf_op jit(solution)/shard_map/ppermute | solution.py:25
  12.6 13.9 %collective-permute-start.4 = (bf16[512,512]{1,0:T(8,128)(2,1)S(1)}, bf16[512,512]{1,0:T(8,128)(2,1)}, u32[]{:S(2)}, u32[]{:S(2)}) collective-permute-start(bf16[512,512]{1,0:T(8,128)(2,1)S(1)} %pad_maximum_fusion.3), channel_id=1, source_target_pairs={{0,64},{64,128},{128,192},{192,0},{1,65},{65,129},{129,193},{193,1... | collective-permute-start | bytes 1572872 | tf_op jit(solution)/shard_map/ppermute | solution.py:25
  14.1 2.7 %copy-start.1 = (bf16[768,512]{1,0:T(8,128)(2,1)}, bf16[768,512]{1,0:T(8,128)(2,1)S(1)}, u32[]{:S(2)}) copy-start(bf16[768,512]{1,0:T(8,128)(2,1)S(1)} %pad_maximum_fusion.2) | copy-start | bytes 2359300
  14.1 7.0 %collective-permute-start.5 = (bf16[256,512]{1,0:T(8,128)(2,1)}, bf16[256,512]{1,0:T(8,128)(2,1)}, u32[]{:S(2)}, u32[]{:S(2)}) collective-permute-start(bf16[256,512]{1,0:T(8,128)(2,1)} %collective-permute-done.2), channel_id=1, source_target_pairs={{0,32},{32,0},{1,33},{33,1},{2,34},{34,2},{3,35},{35,3},{4,36},{36... | collective-permute-start | bytes 786440 | tf_op jit(solution)/shard_map/ppermute | solution.py:21
  16.8 18.7 %all-to-all-start = ((bf16[4,128,768]{2,1,0:T(8,128)(2,1)}), bf16[4,128,768]{2,1,0:T(8,128)(2,1)S(1)}, u32[]{:S(2)}, u32[]{:S(2)}) async-start(bf16[4,128,768]{2,1,0:T(8,128)(2,1)} %bitcast.25), calls=%async_computation | async-start | bytes 1572864 | tf_op jit(solution)/shard_map/all_to_all | solution.py:86
  29.6 7.9 %collective-permute-start.6 = (bf16[128,1280]{1,0:T(8,128)(2,1)}, bf16[128,1280]{1,0:T(8,128)(2,1)}, u32[]{:S(2)}, u32[]{:S(2)}) collective-permute-start(bf16[128,1280]{1,0:T(8,128)(2,1)} %convolution_convert_fusion.2), channel_id=1, source_target_pairs={{0,1},{1,0},{2,3},{3,2},{4,5},{5,4},{6,7},{7,6},{8,9},{9,8},{10,11... | collective-permute-start | bytes 983048 | tf_op jit(solution)/shard_map/ppermute | solution.py:38
  31.0 8.5 %collective-permute-start.7 = (bf16[128,1280]{1,0:T(8,128)(2,1)S(1)}, bf16[128,1280]{1,0:T(8,128)(2,1)}, u32[]{:S(2)}, u32[]{:S(2)}) collective-permute-start(bf16[128,1280]{1,0:T(8,128)(2,1)S(1)} %convolution_convert_fusion.1), channel_id=1, source_target_pairs={{0,3},{1,2},{2,1},{3,0},{4,7},{5,6},{6,5},{7,4},{8,11},{9,10},{10,... | collective-permute-start | bytes 983048 | tf_op jit(solution)/shard_map/ppermute | solution.py:38
  34.1 12.8 %collective-permute-start.8 = (bf16[128,1280]{1,0:T(8,128)(2,1)}, bf16[128,1280]{1,0:T(8,128)(2,1)}, u32[]{:S(2)}, u32[]{:S(2)}) collective-permute-start(bf16[128,1280]{1,0:T(8,128)(2,1)} %convolution_convert_fusion), channel_id=1, source_target_pairs={{0,2},{1,3},{2,0},{3,1},{4,6},{5,7},{6,4},{7,5},{8,10},{9,11},{10,... | collective-permute-start | bytes 983048 | tf_op jit(solution)/shard_map/ppermute | solution.py:38
  35.5 45.4 %copy-start.2 = (bf16[768,512]{1,0:T(8,128)(2,1)S(1)}, bf16[768,512]{1,0:T(8,128)(2,1)}, u32[]{:S(2)}) copy-start(bf16[768,512]{1,0:T(8,128)(2,1)} %copy-done.1) | copy-start | bytes 2359300
  48.3 10.7 %collective-permute-start.10 = (bf16[32,2048]{1,0:T(8,128)(2,1)S(1)}, bf16[32,2048]{1,0:T(8,128)(2,1)S(1)}, u32[]{:S(2)}, u32[]{:S(2)}) collective-permute-start(bf16[32,2048]{1,0:T(8,128)(2,1)S(1)} %get-tuple-element.37), channel_id=1, source_target_pairs={{0,12},{4,8},{8,4},{12,0},{1,13},{5,9},{9,5},{13,1},{2,14},{6,10},... | collective-permute-start | bytes 393224 | tf_op jit(solution)/shard_map/ppermute | solution.py:38
  53.9 9.5 %collective-permute-start.11 = (bf16[32,2048]{1,0:T(8,128)(2,1)S(1)}, bf16[32,2048]{1,0:T(8,128)(2,1)S(1)}, u32[]{:S(2)}, u32[]{:S(2)}) collective-permute-start(bf16[32,2048]{1,0:T(8,128)(2,1)S(1)} %get-tuple-element.36), channel_id=1, source_target_pairs={{0,8},{4,12},{8,0},{12,4},{1,9},{5,13},{9,1},{13,5},{2,10},{6,14},... | collective-permute-start | bytes 393224 | tf_op jit(solution)/shard_map/ppermute | solution.py:38
  54.9 8.6 %collective-permute-start.9 = (bf16[32,2048]{1,0:T(8,128)(2,1)S(1)}, bf16[32,2048]{1,0:T(8,128)(2,1)}, u32[]{:S(2)}, u32[]{:S(2)}) collective-permute-start(bf16[32,2048]{1,0:T(8,128)(2,1)S(1)} %get-tuple-element.35), channel_id=1, source_target_pairs={{0,4},{4,0},{8,12},{12,8},{1,5},{5,1},{9,13},{13,9},{2,6},{6,2},{1... | collective-permute-start | bytes 393224 | tf_op jit(solution)/shard_map/ppermute | solution.py:38
  79.5 10.6 %collective-permute-start.12 = (bf16[128,2048]{1,0:T(8,128)(2,1)S(1)}, bf16[128,2048]{1,0:T(8,128)(2,1)S(1)}, u32[]{:S(2)}, u32[]{:S(2)}) collective-permute-start(bf16[128,2048]{1,0:T(8,128)(2,1)S(1)} %all_gather.3), channel_id=1, source_target_pairs={{0,3},{1,0},{2,1},{3,2},{4,7},{5,4},{6,5},{7,6},{8,11},{9,8},{10,9... | collective-permute-start | bytes 1572872 | tf_op jit(solution)/shard_map/ppermute | solution.py:25
  80.8 9.2 %collective-permute-start.13 = (bf16[128,2048]{1,0:T(8,128)(2,1)S(1)}, bf16[128,2048]{1,0:T(8,128)(2,1)S(1)}, u32[]{:S(2)}, u32[]{:S(2)}) collective-permute-start(bf16[128,2048]{1,0:T(8,128)(2,1)S(1)} %all_gather.3), channel_id=1, source_target_pairs={{0,1},{1,2},{2,3},{3,0},{4,5},{5,6},{6,7},{7,4},{8,9},{9,10},{10,1... | collective-permute-start | bytes 1572872 | tf_op jit(solution)/shard_map/ppermute | solution.py:25
  90.1 15.6 %collective-permute-start.15 = (bf16[64,2048]{1,0:T(8,128)(2,1)S(1)}, bf16[64,2048]{1,0:T(8,128)(2,1)S(1)}, u32[]{:S(2)}, u32[]{:S(2)}) collective-permute-start(bf16[64,2048]{1,0:T(8,128)(2,1)S(1)} %get-tuple-element.20), channel_id=1, source_target_pairs={{0,3},{1,0},{2,1},{3,2},{4,7},{5,4},{6,5},{7,6},{8,11},{9,8},{10,9... | collective-permute-start | bytes 786440 | tf_op jit(solution)/shard_map/ppermute | solution.py:25
  90.4 15.3 %collective-permute-start.16 = (bf16[64,2048]{1,0:T(8,128)(2,1)S(1)}, bf16[64,2048]{1,0:T(8,128)(2,1)S(1)}, u32[]{:S(2)}, u32[]{:S(2)}) collective-permute-start(bf16[64,2048]{1,0:T(8,128)(2,1)S(1)} %slice.85), channel_id=1, source_target_pairs={{0,1},{1,2},{2,3},{3,0},{4,5},{5,6},{6,7},{7,4},{8,9},{9,10},{10,1... | collective-permute-start | bytes 786440 | tf_op jit(solution)/shard_map/ppermute | solution.py:25
  92.8 18.2 %collective-permute-start.14 = (f32[192,512]{1,0:T(8,128)S(1)}, f32[192,512]{1,0:T(8,128)S(1)}, u32[]{:S(2)}, u32[]{:S(2)}) collective-permute-start(f32[192,512]{1,0:T(8,128)S(1)} %pad_maximum_fusion.8), channel_id=1, source_target_pairs={{0,16},{16,0},{1,17},{17,1},{2,18},{18,2},{3,19},{19,3},{4,20},{20... | collective-permute-start | bytes 1179656 | tf_op jit(solution)/shard_map/ppermute | solution.py:21
  106.3 5.6 %collective-permute-start.17 = (f32[64,512]{1,0:T(8,128)S(1)}, f32[64,512]{1,0:T(8,128)S(1)}, u32[]{:S(2)}, u32[]{:S(2)}) collective-permute-start(f32[64,512]{1,0:T(8,128)S(1)} %fusion.20), channel_id=1, source_target_pairs={{0,16},{16,0},{1,17},{17,1},{2,18},{18,2},{3,19},{19,3},{4,20},{20... | collective-permute-start | bytes 393224 | tf_op jit(solution)/shard_map/ppermute | solution.py:21
  112.5 7.6 %collective-permute-start.18 = (bf16[256,512]{1,0:T(8,128)(2,1)S(1)}, bf16[256,512]{1,0:T(8,128)(2,1)S(1)}, u32[]{:S(2)}, u32[]{:S(2)}) collective-permute-start(bf16[256,512]{1,0:T(8,128)(2,1)S(1)} %dynamic-slice_convert_fusion), channel_id=1, source_target_pairs={{0,32},{32,0},{1,33},{33,1},{2,34},{34,2},{3,35},{35,3},{4,36},{36... | collective-permute-start | bytes 786440 | tf_op jit(solution)/shard_map/ppermute | solution.py:21
  112.6 9.1 %collective-permute-start.19 = (bf16[256,512]{1,0:T(8,128)(2,1)S(1)}, bf16[256,512]{1,0:T(8,128)(2,1)S(1)}, u32[]{:S(2)}, u32[]{:S(2)}) collective-permute-start(bf16[256,512]{1,0:T(8,128)(2,1)S(1)} %dynamic-slice_convert_fusion), channel_id=1, source_target_pairs={{0,128},{64,192},{128,0},{192,64},{1,129},{65,193},{129,1},{193,65... | collective-permute-start | bytes 786440 | tf_op jit(solution)/shard_map/ppermute | solution.py:25
  120.1 12.3 %collective-permute-start.20 = (bf16[512,512]{1,0:T(8,128)(2,1)S(1)}, bf16[512,512]{1,0:T(8,128)(2,1)S(1)}, u32[]{:S(2)}, u32[]{:S(2)}) collective-permute-start(bf16[512,512]{1,0:T(8,128)(2,1)S(1)} %pad_maximum_fusion.7), channel_id=1, source_target_pairs={{0,192},{64,0},{128,64},{192,128},{1,193},{65,1},{129,65},{193,129... | collective-permute-start | bytes 1572872 | tf_op jit(solution)/shard_map/ppermute | solution.py:25
  120.6 13.5 %collective-permute-start.21 = (bf16[512,512]{1,0:T(8,128)(2,1)S(1)}, bf16[512,512]{1,0:T(8,128)(2,1)S(1)}, u32[]{:S(2)}, u32[]{:S(2)}) collective-permute-start(bf16[512,512]{1,0:T(8,128)(2,1)S(1)} %pad_maximum_fusion.7), channel_id=1, source_target_pairs={{0,64},{64,128},{128,192},{192,0},{1,65},{65,129},{129,193},{193,1... | collective-permute-start | bytes 1572872 | tf_op jit(solution)/shard_map/ppermute | solution.py:25
  121.7 6.1 %collective-permute-start.22 = (bf16[256,512]{1,0:T(8,128)(2,1)S(1)}, bf16[256,512]{1,0:T(8,128)(2,1)S(1)}, u32[]{:S(2)}, u32[]{:S(2)}) collective-permute-start(bf16[256,512]{1,0:T(8,128)(2,1)S(1)} %collective-permute-done.19), channel_id=1, source_target_pairs={{0,32},{32,0},{1,33},{33,1},{2,34},{34,2},{3,35},{35,3},{4,36},{36... | collective-permute-start | bytes 786440 | tf_op jit(solution)/shard_map/ppermute | solution.py:21
  135.1 3.7 %collective-permute-start.23 = (f32[256,512]{1,0:T(8,128)S(1)}, f32[256,512]{1,0:T(8,128)S(1)}, u32[]{:S(2)}, u32[]{:S(2)}) collective-permute-start(f32[256,512]{1,0:T(8,128)S(1)} %convolution_add_fusion), channel_id=1, source_target_pairs={{0,16},{16,0},{1,17},{17,1},{2,18},{18,2},{3,19},{19,3},{4,20},{20... | collective-permute-start | bytes 1572872 | tf_op jit(solution)/shard_map/ppermute | solution.py:21

commit v21 on v20

--- a/solution.py
+++ b/solution.py
@@ -34,8 +34,12 @@
     return ((got[0] + got[1]) + (got[2] + got[3])).astype(BF)
 
 
+def trade(array, axis, k):
+    return lax.ppermute(array, axis, [(i, i ^ k) for i in range(4)])
+
+
 def scatter_pairs(pieces, axis):
-    return [pieces[0]] + [lax.ppermute(pieces[k], axis, [(i, i ^ k) for i in range(4)]) for k in (1, 3, 2)]
+    return [pieces[0]] + [trade(pieces[k], axis, k) for k in (1, 3, 2)]
 
 
 def chunks(array):
@@ -58,7 +62,7 @@
 
 
 def late_blocks(pair, far):
-    return [fetch(pair, "x", 1), fetch(pair, "x", 3), swap(far, "zl")]
+    return [trade(pair, "x", 1), trade(pair, "x", 3), swap(far, "zl")]
 
 
 def core_sum(products):

time: 140 us -> 140 us (level)
  waiting for transfers between devices: 57.7 us -> 53.2 us
  starting transfers between devices: 50 us -> 53.1 us
    ppermute x10 -> x6, waiting for transfers between devices: 20.3 us -> 8.59 us  [send(): lax.ppermute(array, axis, [(i, (i + k) % 4) for i in range(4)])]
    ppermute x6 -> x10, waiting for transfers between devices: 18.7 us -> 29.8 us  [trade(): return lax.ppermute(array, axis, [(i, i ^ k) for i in range(4)])]
    ppermute x8, starting transfers between devices: 25.2 us -> 18.6 us  [swap(): return lax.ppermute(array, axis, [(0, 1), (1, 0)])]
    ppermute x6 -> x10, starting transfers between devices: 11.8 us -> 16.8 us  [trade(): return lax.ppermute(array, axis, [(i, i ^ k) for i in range(4)])]
    ppermute x10 -> x6, starting transfers between devices: 9 us -> 13.6 us  [send(): lax.ppermute(array, axis, [(i, (i + k) % 4) for i in range(4)])]
    ppermute x8, waiting for transfers between devices: 18.6 us -> 14.8 us  [swap(): return lax.ppermute(array, axis, [(0, 1), (1, 0)])]
  transfers between devices with their start and end apart: 25 -> 25, of which waited for: 16 -> 18; matrix products, arithmetic and copies ran while one was open for 8% -> 8% of each run, Pallas kernels for 0% -> 0%
where the time goes in v21:
time: 140 us; the launch traced here: 139 us
  waiting for transfers between devices  53.2 us (38%)
  starting transfers between devices  53.1 us (38%)
  blocking collectives  15.8 us (11%)
  matrix products  10.1 us (7%)
  other arithmetic  5.01 us (4%)
  local copies, waits for them, and re-layouts  1.71 us (1%)
    ppermute x10, waiting for transfers between devices, trade(): return lax.ppermute(array, axis, [(i, i ^ k) for i in range(4)])  29.8 us
    ppermute x8, starting transfers between devices, swap(): return lax.ppermute(array, axis, [(0, 1), (1, 0)])  18.6 us
    ppermute x10, starting transfers between devices, trade(): return lax.ppermute(array, axis, [(i, i ^ k) for i in range(4)])  16.8 us
    all_gather x1, blocking collectives, per_device(): near = lax.all_gather(part, 'zh', axis=0, tiled=True)  15.8 us
    ppermute x8, waiting for transfers between devices, swap(): return lax.ppermute(array, axis, [(0, 1), (1, 0)])  14.8 us
    ppermute x6, starting transfers between devices, send(): lax.ppermute(array, axis, [(i, (i + k) % 4) for i in range(4)])  13.6 us
    dot_general x14, matrix products, matmul(): return lax.dot_general(a, b, (dims, ((), ())), preferred_element_type=F32)  10.1 us
    ppermute x6, waiting for transfers between devices, send(): lax.ppermute(array, axis, [(i, (i + k) % 4) for i in range(4)])  8.59 us
  transfers between devices with their start and end apart: 25, of which 18 were waited for; matrix products, arithmetic and copies ran while one was open for 8% of the time, Pallas kernels for 0%

profile of v21, /device:TPU:1, one launch (start us, length us, event | category | flops | bytes accessed | tf_op | source)
XLA Modules:
  0.0 139.4 jit_solution(9716099758347293773)
XLA Ops:
  0.0 3.2 %collective-permute-start.1 = (bf16[256,512]{1,0:T(8,128)(2,1)}, bf16[256,512]{1,0:T(8,128)(2,1)S(1)}, u32[]{:S(2)}, u32[]{:S(2)}) collective-permute-start(bf16[256,512]{1,0:T(8,128)(2,1)} %param.1), channel_id=1, source_target_pairs={{0,16},{16,0},{1,17},{17,1},{2,18},{18,2},{3,19},{19,3},{4,20},{20... | collective-permute-start | bytes 786440 | tf_op jit(solution)/shard_map/ppermute | solution.py:21
  3.2 2.6 %collective-permute-start.2 = (bf16[256,512]{1,0:T(8,128)(2,1)}, bf16[256,512]{1,0:T(8,128)(2,1)}, u32[]{:S(2)}, u32[]{:S(2)}) collective-permute-start(bf16[256,512]{1,0:T(8,128)(2,1)} %param.1), channel_id=1, source_target_pairs={{0,128},{64,192},{128,0},{192,64},{1,129},{65,193},{129,1},{193,65... | collective-permute-start | bytes 786440 | tf_op jit(solution)/shard_map/ppermute | solution.py:25
  5.9 1.0 fusion.27
  6.9 0.1 pad_maximum_fusion.4
  7.1 0.1 pad_maximum_fusion.5
  7.3 4.2 %collective-permute-done = bf16[256,512]{1,0:T(8,128)(2,1)S(1)} collective-permute-done((bf16[256,512]{1,0:T(8,128)(2,1)}, bf16[256,512]{1,0:T(8,128)(2,1)S(1)}, u32[]{:S(2)}, u32[]{:S(2)}) %collective-permute-start) | collective-permute-done | bytes 262176 | tf_op jit(solution)/shard_map/ppermute | solution.py:21
  11.5 0.1 collective-permute-start.3
  11.6 1.6 %collective-permute-start.4 = (bf16[512,512]{1,0:T(8,128)(2,1)S(1)}, bf16[512,512]{1,0:T(8,128)(2,1)}, u32[]{:S(2)}, u32[]{:S(2)}) collective-permute-start(bf16[512,512]{1,0:T(8,128)(2,1)S(1)} %pad_maximum_fusion.3), channel_id=1, source_target_pairs={{0,192},{64,128},{128,64},{192,0},{1,193},{65,129},{129,65},{193,1... | collective-permute-start | bytes 1572872 | tf_op jit(solution)/shard_map/ppermute | solution.py:38
  13.2 1.0 pad_maximum_fusion.2
  14.2 1.5 %collective-permute-start.5 = (bf16[256,512]{1,0:T(8,128)(2,1)}, bf16[256,512]{1,0:T(8,128)(2,1)}, u32[]{:S(2)}, u32[]{:S(2)}) collective-permute-start(bf16[256,512]{1,0:T(8,128)(2,1)} %collective-permute-done.2), channel_id=1, source_target_pairs={{0,32},{32,0},{1,33},{33,1},{2,34},{34,2},{3,35},{35,3},{4,36},{36... | collective-permute-start | bytes 786440 | tf_op jit(solution)/shard_map/ppermute | solution.py:21
  15.7 1.5 %convolution_convert_fusion.4 = bf16[512,768]{1,0:T(8,128)(2,1)} fusion(bf16[512,512]{1,0:T(8,128)(2,1)S(1)} %bitcast.24, bf16[768,512]{1,0:T(8,128)(2,1)S(1)} %pad_maximum_fusion.2), kind=kOutput, calls=%fused_computation.5 | convolution fusion | flops 403046400 | bytes 2097152 | tf_op jit(solution)/shard_map/dot_general | solution.py:56
  17.2 4.2 %all-to-all-start = ((bf16[4,128,768]{2,1,0:T(8,128)(2,1)}), bf16[4,128,768]{2,1,0:T(8,128)(2,1)S(1)}, u32[]{:S(2)}, u32[]{:S(2)}) async-start(bf16[4,128,768]{2,1,0:T(8,128)(2,1)} %bitcast.25), calls=%async_computation | async-start | bytes 1572864 | tf_op jit(solution)/shard_map/all_to_all | solution.py:90
  21.3 3.2 %collective-permute-done.3 = bf16[512,512]{1,0:T(8,128)(2,1)S(1)} collective-permute-done((bf16[512,512]{1,0:T(8,128)(2,1)S(1)}, bf16[512,512]{1,0:T(8,128)(2,1)S(1)}, u32[]{:S(2)}, u32[]{:S(2)}) %collective-permute-start.3) | collective-permute-done | bytes 524320 | tf_op jit(solution)/shard_map/ppermute | solution.py:38
  24.5 1.3 collective-permute-done.4
  25.8 1.2 pad_maximum_fusion.1
  27.0 1.3 convolution_convert_fusion.2
  28.3 0.5 convolution_convert_fusion.1
  28.9 0.8 collective-permute-start.6
  29.7 1.9 %collective-permute-start.7 = (bf16[128,1280]{1,0:T(8,128)(2,1)S(1)}, bf16[128,1280]{1,0:T(8,128)(2,1)}, u32[]{:S(2)}, u32[]{:S(2)}) collective-permute-start(bf16[128,1280]{1,0:T(8,128)(2,1)S(1)} %convolution_convert_fusion.1), channel_id=1, source_target_pairs={{0,3},{1,2},{2,1},{3,0},{4,7},{5,6},{6,5},{7,4},{8,11},{9,10},{10,... | collective-permute-start | bytes 983048 | tf_op jit(solution)/shard_map/ppermute | solution.py:38
  31.6 1.3 convolution_convert_fusion
  32.9 0.7 collective-permute-start.8
  33.6 0.5 convolution_convert_fusion.3
  34.2 0.1 fusion.10
  34.3 4.2 %collective-permute-done.6 = bf16[128,1280]{1,0:T(8,128)(2,1)} collective-permute-done((bf16[128,1280]{1,0:T(8,128)(2,1)}, bf16[128,1280]{1,0:T(8,128)(2,1)}, u32[]{:S(2)}, u32[]{:S(2)}) %collective-permute-start.6) | collective-permute-done | bytes 327712 | tf_op jit(solution)/shard_map/ppermute | solution.py:38
  38.5 0.8 collective-permute-done.7
  39.3 7.1 %collective-permute-done.8 = bf16[128,1280]{1,0:T(8,128)(2,1)} collective-permute-done((bf16[128,1280]{1,0:T(8,128)(2,1)}, bf16[128,1280]{1,0:T(8,128)(2,1)}, u32[]{:S(2)}, u32[]{:S(2)}) %collective-permute-start.8) | collective-permute-done | bytes 327712 | tf_op jit(solution)/shard_map/ppermute | solution.py:38
  46.4 1.3 add_convert_fusion
  47.8 4.8 %collective-permute-start.10 = (bf16[32,2048]{1,0:T(8,128)(2,1)S(1)}, bf16[32,2048]{1,0:T(8,128)(2,1)S(1)}, u32[]{:S(2)}, u32[]{:S(2)}) collective-permute-start(bf16[32,2048]{1,0:T(8,128)(2,1)S(1)} %get-tuple-element.37), channel_id=1, source_target_pairs={{0,12},{4,8},{8,4},{12,0},{1,13},{5,9},{9,5},{13,1},{2,14},{6,10},... | collective-permute-start | bytes 393224 | tf_op jit(solution)/shard_map/ppermute | solution.py:38
  52.6 1.6 %collective-permute-start.11 = (bf16[32,2048]{1,0:T(8,128)(2,1)S(1)}, bf16[32,2048]{1,0:T(8,128)(2,1)S(1)}, u32[]{:S(2)}, u32[]{:S(2)}) collective-permute-start(bf16[32,2048]{1,0:T(8,128)(2,1)S(1)} %get-tuple-element.36), channel_id=1, source_target_pairs={{0,8},{4,12},{8,0},{12,4},{1,9},{5,13},{9,1},{13,5},{2,10},{6,14},... | collective-permute-start | bytes 393224 | tf_op jit(solution)/shard_map/ppermute | solution.py:38
  54.2 0.6 collective-permute-start.9
  54.8 7.4 %collective-permute-done.10 = bf16[32,2048]{1,0:T(8,128)(2,1)S(1)} collective-permute-done((bf16[32,2048]{1,0:T(8,128)(2,1)S(1)}, bf16[32,2048]{1,0:T(8,128)(2,1)S(1)}, u32[]{:S(2)}, u32[]{:S(2)}) %collective-permute-start.10) | collective-permute-done | bytes 131104 | tf_op jit(solution)/shard_map/ppermute | solution.py:38
  62.2 0.3 collective-permute-done.11
  62.4 0.8 collective-permute-done.9
  63.3 1.0 add_convert_fusion.2
  64.2 15.8 %all_gather.3 = bf16[128,2048]{1,0:T(8,128)(2,1)S(1)} all-gather(bf16[32,2048]{1,0:T(8,128)(2,1)S(1)} %add_convert_fusion.2), channel_id=1, replica_groups=mesh['x'=4,'zl'=2,'core'=2,'zh'=4,'y'=4] {'zh'}, dimensions={0}, use_global_device_ids=true | all-gather | bytes 655360 | tf_op jit(solution)/shard_map/all_gather | solution.py:98
  80.0 1.5 %collective-permute-start.12 = (bf16[128,2048]{1,0:T(8,128)(2,1)S(1)}, bf16[128,2048]{1,0:T(8,128)(2,1)S(1)}, u32[]{:S(2)}, u32[]{:S(2)}) collective-permute-start(bf16[128,2048]{1,0:T(8,128)(2,1)S(1)} %all_gather.3), channel_id=1, source_target_pairs={{0,3},{1,0},{2,1},{3,2},{4,7},{5,4},{6,5},{7,6},{8,11},{9,8},{10,9... | collective-permute-start | bytes 1572872 | tf_op jit(solution)/shard_map/ppermute | solution.py:25
  81.5 3.4 %collective-permute-start.13 = (bf16[128,2048]{1,0:T(8,128)(2,1)S(1)}, bf16[128,2048]{1,0:T(8,128)(2,1)S(1)}, u32[]{:S(2)}, u32[]{:S(2)}) collective-permute-start(bf16[128,2048]{1,0:T(8,128)(2,1)S(1)} %all_gather.3), channel_id=1, source_target_pairs={{0,1},{1,2},{2,3},{3,0},{4,5},{5,6},{6,7},{7,4},{8,9},{9,10},{10,1... | collective-permute-start | bytes 1572872 | tf_op jit(solution)/shard_map/ppermute | solution.py:25
  85.0 0.4 fusion.23
  85.5 7.4 %collective-permute-done.13 = bf16[128,2048]{1,0:T(8,128)(2,1)S(1)} collective-permute-done((bf16[128,2048]{1,0:T(8,128)(2,1)S(1)}, bf16[128,2048]{1,0:T(8,128)(2,1)S(1)}, u32[]{:S(2)}, u32[]{:S(2)}) %collective-permute-start.13) | collective-permute-done | bytes 524320 | tf_op jit(solution)/shard_map/ppermute | solution.py:25
  92.9 1.0 collective-permute-done.12
  94.0 1.9 %collective-permute-start.15 = (bf16[64,2048]{1,0:T(8,128)(2,1)S(1)}, bf16[64,2048]{1,0:T(8,128)(2,1)S(1)}, u32[]{:S(2)}, u32[]{:S(2)}) collective-permute-start(bf16[64,2048]{1,0:T(8,128)(2,1)S(1)} %get-tuple-element.20), channel_id=1, source_target_pairs={{0,3},{1,0},{2,1},{3,2},{4,7},{5,4},{6,5},{7,6},{8,11},{9,8},{10,9... | collective-permute-start | bytes 786440 | tf_op jit(solution)/shard_map/ppermute | solution.py:25
  95.9 0.5 fusion.22
  96.4 0.4 fusion.21
  96.9 5.3 %collective-permute-start.14 = (f32[192,512]{1,0:T(8,128)S(1)}, f32[192,512]{1,0:T(8,128)S(1)}, u32[]{:S(2)}, u32[]{:S(2)}) collective-permute-start(f32[192,512]{1,0:T(8,128)S(1)} %pad_maximum_fusion.8), channel_id=1, source_target_pairs={{0,16},{16,0},{1,17},{17,1},{2,18},{18,2},{3,19},{19,3},{4,20},{20... | collective-permute-start | bytes 1179656 | tf_op jit(solution)/shard_map/ppermute | solution.py:21
  102.1 0.2 collective-permute-done.16
  102.4 0.5 fusion.20
  102.9 5.7 %collective-permute-start.17 = (f32[64,512]{1,0:T(8,128)S(1)}, f32[64,512]{1,0:T(8,128)S(1)}, u32[]{:S(2)}, u32[]{:S(2)}) collective-permute-start(f32[64,512]{1,0:T(8,128)S(1)} %fusion.20), channel_id=1, source_target_pairs={{0,16},{16,0},{1,17},{17,1},{2,18},{18,2},{3,19},{19,3},{4,20},{20... | collective-permute-start | bytes 393224 | tf_op jit(solution)/shard_map/ppermute | solution.py:21
  108.8 0.8 collective-permute-done.17
  109.6 0.5 constant_dynamic-update-slice_fusion.1
  110.2 0.4 collective-permute-start.18
  110.6 4.1 %collective-permute-start.19 = (bf16[256,512]{1,0:T(8,128)(2,1)S(1)}, bf16[256,512]{1,0:T(8,128)(2,1)S(1)}, u32[]{:S(2)}, u32[]{:S(2)}) collective-permute-start(bf16[256,512]{1,0:T(8,128)(2,1)S(1)} %dynamic-slice_convert_fusion), channel_id=1, source_target_pairs={{0,128},{64,192},{128,0},{192,64},{1,129},{65,193},{129,1},{193,65... | collective-permute-start | bytes 786440 | tf_op jit(solution)/shard_map/ppermute | solution.py:25
  114.7 3.1 %collective-permute-done.18 = bf16[256,512]{1,0:T(8,128)(2,1)S(1)} collective-permute-done((bf16[256,512]{1,0:T(8,128)(2,1)S(1)}, bf16[256,512]{1,0:T(8,128)(2,1)S(1)}, u32[]{:S(2)}, u32[]{:S(2)}) %collective-permute-start.18) | collective-permute-done | bytes 262176 | tf_op jit(solution)/shard_map/ppermute | solution.py:21
  117.9 1.2 collective-permute-start.20
  119.0 3.5 %collective-permute-start.21 = (bf16[512,512]{1,0:T(8,128)(2,1)S(1)}, bf16[512,512]{1,0:T(8,128)(2,1)S(1)}, u32[]{:S(2)}, u32[]{:S(2)}) collective-permute-start(bf16[512,512]{1,0:T(8,128)(2,1)S(1)} %pad_maximum_fusion.7), channel_id=1, source_target_pairs={{0,192},{64,128},{128,64},{192,0},{1,193},{65,129},{129,65},{193,1... | collective-permute-start | bytes 1572872 | tf_op jit(solution)/shard_map/ppermute | solution.py:38
  122.6 0.3 collective-permute-start.22
  122.9 5.7 %collective-permute-done.22 = bf16[256,512]{1,0:T(8,128)(2,1)S(1)} collective-permute-done((bf16[256,512]{1,0:T(8,128)(2,1)S(1)}, bf16[256,512]{1,0:T(8,128)(2,1)S(1)}, u32[]{:S(2)}, u32[]{:S(2)}) %collective-permute-start.22) | collective-permute-done | bytes 262176 | tf_op jit(solution)/shard_map/ppermute | solution.py:21
  128.6 2.7 %collective-permute-done.20 = bf16[512,512]{1,0:T(8,128)(2,1)S(1)} collective-permute-done((bf16[512,512]{1,0:T(8,128)(2,1)S(1)}, bf16[512,512]{1,0:T(8,128)(2,1)S(1)}, u32[]{:S(2)}, u32[]{:S(2)}) %collective-permute-start.20) | collective-permute-done | bytes 524320 | tf_op jit(solution)/shard_map/ppermute | solution.py:38
  131.3 2.0 %collective-permute-done.21 = bf16[512,512]{1,0:T(8,128)(2,1)S(1)} collective-permute-done((bf16[512,512]{1,0:T(8,128)(2,1)S(1)}, bf16[512,512]{1,0:T(8,128)(2,1)S(1)}, u32[]{:S(2)}, u32[]{:S(2)}) %collective-permute-start.21) | collective-permute-done | bytes 524320 | tf_op jit(solution)/shard_map/ppermute | solution.py:38
  133.5 0.5 fusion.2
  134.0 0.4 convolution_add_fusion
  134.4 2.2 %collective-permute-start.23 = (f32[256,512]{1,0:T(8,128)S(1)}, f32[256,512]{1,0:T(8,128)S(1)}, u32[]{:S(2)}, u32[]{:S(2)}) collective-permute-start(f32[256,512]{1,0:T(8,128)S(1)} %convolution_add_fusion), channel_id=1, source_target_pairs={{0,16},{16,0},{1,17},{17,1},{2,18},{18,2},{3,19},{19,3},{4,20},{20... | collective-permute-start | bytes 1572872 | tf_op jit(solution)/shard_map/ppermute | solution.py:21
  136.6 0.5 fusion.4
  137.1 1.0 collective-permute-done.23
  138.1 1.2 add_multiply_fusion
  (52 shorter events, 1.0 us)
Async XLA Ops:
  0.0 6.8 %collective-permute-start.1 = (bf16[256,512]{1,0:T(8,128)(2,1)}, bf16[256,512]{1,0:T(8,128)(2,1)S(1)}, u32[]{:S(2)}, u32[]{:S(2)}) collective-permute-start(bf16[256,512]{1,0:T(8,128)(2,1)} %param.1), channel_id=1, source_target_pairs={{0,16},{16,0},{1,17},{17,1},{2,18},{18,2},{3,19},{19,3},{4,20},{20... | collective-permute-start | bytes 786440 | tf_op jit(solution)/shard_map/ppermute | solution.py:21
  3.2 8.3 %collective-permute-start = (bf16[256,512]{1,0:T(8,128)(2,1)}, bf16[256,512]{1,0:T(8,128)(2,1)S(1)}, u32[]{:S(2)}, u32[]{:S(2)}) collective-permute-start(bf16[256,512]{1,0:T(8,128)(2,1)} %param.1), channel_id=1, source_target_pairs={{0,32},{32,0},{1,33},{33,1},{2,34},{34,2},{3,35},{35,3},{4,36},{36... | collective-permute-start | bytes 786440 | tf_op jit(solution)/shard_map/ppermute | solution.py:21
  3.2 9.9 %collective-permute-start.2 = (bf16[256,512]{1,0:T(8,128)(2,1)}, bf16[256,512]{1,0:T(8,128)(2,1)}, u32[]{:S(2)}, u32[]{:S(2)}) collective-permute-start(bf16[256,512]{1,0:T(8,128)(2,1)} %param.1), channel_id=1, source_target_pairs={{0,128},{64,192},{128,0},{192,64},{1,129},{65,193},{129,1},{193,65... | collective-permute-start | bytes 786440 | tf_op jit(solution)/shard_map/ppermute | solution.py:25
  7.1 4.4 %copy-start = (bf16[256,512]{1,0:T(8,128)(2,1)S(1)}, bf16[256,512]{1,0:T(8,128)(2,1)}, u32[]{:S(2)}) copy-start(bf16[256,512]{1,0:T(8,128)(2,1)} %param.1) | copy-start | bytes 786436
  11.5 13.0 %collective-permute-start.3 = (bf16[512,512]{1,0:T(8,128)(2,1)S(1)}, bf16[512,512]{1,0:T(8,128)(2,1)S(1)}, u32[]{:S(2)}, u32[]{:S(2)}) collective-permute-start(bf16[512,512]{1,0:T(8,128)(2,1)S(1)} %pad_maximum_fusion.3), channel_id=1, source_target_pairs={{0,64},{64,0},{128,192},{192,128},{1,65},{65,1},{129,193},{193,129... | collective-permute-start | bytes 1572872 | tf_op jit(solution)/shard_map/ppermute | solution.py:38
  11.6 14.2 %collective-permute-start.4 = (bf16[512,512]{1,0:T(8,128)(2,1)S(1)}, bf16[512,512]{1,0:T(8,128)(2,1)}, u32[]{:S(2)}, u32[]{:S(2)}) collective-permute-start(bf16[512,512]{1,0:T(8,128)(2,1)S(1)} %pad_maximum_fusion.3), channel_id=1, source_target_pairs={{0,192},{64,128},{128,64},{192,0},{1,193},{65,129},{129,65},{193,1... | collective-permute-start | bytes 1572872 | tf_op jit(solution)/shard_map/ppermute | solution.py:38
  14.2 3.0 %copy-start.1 = (bf16[768,512]{1,0:T(8,128)(2,1)}, bf16[768,512]{1,0:T(8,128)(2,1)S(1)}, u32[]{:S(2)}) copy-start(bf16[768,512]{1,0:T(8,128)(2,1)S(1)} %pad_maximum_fusion.2) | copy-start | bytes 2359300
  14.2 7.1 %collective-permute-start.5 = (bf16[256,512]{1,0:T(8,128)(2,1)}, bf16[256,512]{1,0:T(8,128)(2,1)}, u32[]{:S(2)}, u32[]{:S(2)}) collective-permute-start(bf16[256,512]{1,0:T(8,128)(2,1)} %collective-permute-done.2), channel_id=1, source_target_pairs={{0,32},{32,0},{1,33},{33,1},{2,34},{34,2},{3,35},{35,3},{4,36},{36... | collective-permute-start | bytes 786440 | tf_op jit(solution)/shard_map/ppermute | solution.py:21
  17.2 17.0 %all-to-all-start = ((bf16[4,128,768]{2,1,0:T(8,128)(2,1)}), bf16[4,128,768]{2,1,0:T(8,128)(2,1)S(1)}, u32[]{:S(2)}, u32[]{:S(2)}) async-start(bf16[4,128,768]{2,1,0:T(8,128)(2,1)} %bitcast.25), calls=%async_computation | async-start | bytes 1572864 | tf_op jit(solution)/shard_map/all_to_all | solution.py:90
  28.9 9.6 %collective-permute-start.6 = (bf16[128,1280]{1,0:T(8,128)(2,1)}, bf16[128,1280]{1,0:T(8,128)(2,1)}, u32[]{:S(2)}, u32[]{:S(2)}) collective-permute-start(bf16[128,1280]{1,0:T(8,128)(2,1)} %convolution_convert_fusion.2), channel_id=1, source_target_pairs={{0,1},{1,0},{2,3},{3,2},{4,5},{5,4},{6,7},{7,6},{8,9},{9,8},{10,11... | collective-permute-start | bytes 983048 | tf_op jit(solution)/shard_map/ppermute | solution.py:38
  29.7 9.6 %collective-permute-start.7 = (bf16[128,1280]{1,0:T(8,128)(2,1)S(1)}, bf16[128,1280]{1,0:T(8,128)(2,1)}, u32[]{:S(2)}, u32[]{:S(2)}) collective-permute-start(bf16[128,1280]{1,0:T(8,128)(2,1)S(1)} %convolution_convert_fusion.1), channel_id=1, source_target_pairs={{0,3},{1,2},{2,1},{3,0},{4,7},{5,6},{6,5},{7,4},{8,11},{9,10},{10,... | collective-permute-start | bytes 983048 | tf_op jit(solution)/shard_map/ppermute | solution.py:38
  32.9 13.6 %collective-permute-start.8 = (bf16[128,1280]{1,0:T(8,128)(2,1)}, bf16[128,1280]{1,0:T(8,128)(2,1)}, u32[]{:S(2)}, u32[]{:S(2)}) collective-permute-start(bf16[128,1280]{1,0:T(8,128)(2,1)} %convolution_convert_fusion), channel_id=1, source_target_pairs={{0,2},{1,3},{2,0},{3,1},{4,6},{5,7},{6,4},{7,5},{8,10},{9,11},{10,... | collective-permute-start | bytes 983048 | tf_op jit(solution)/shard_map/ppermute | solution.py:38
  34.3 50.7 %copy-start.2 = (bf16[768,512]{1,0:T(8,128)(2,1)S(1)}, bf16[768,512]{1,0:T(8,128)(2,1)}, u32[]{:S(2)}) copy-start(bf16[768,512]{1,0:T(8,128)(2,1)} %copy-done.1) | copy-start | bytes 2359300
  47.8 14.3 %collective-permute-start.10 = (bf16[32,2048]{1,0:T(8,128)(2,1)S(1)}, bf16[32,2048]{1,0:T(8,128)(2,1)S(1)}, u32[]{:S(2)}, u32[]{:S(2)}) collective-permute-start(bf16[32,2048]{1,0:T(8,128)(2,1)S(1)} %get-tuple-element.37), channel_id=1, source_target_pairs={{0,12},{4,8},{8,4},{12,0},{1,13},{5,9},{9,5},{13,1},{2,14},{6,10},... | collective-permute-start | bytes 393224 | tf_op jit(solution)/shard_map/ppermute | solution.py:38
  52.6 9.8 %collective-permute-start.11 = (bf16[32,2048]{1,0:T(8,128)(2,1)S(1)}, bf16[32,2048]{1,0:T(8,128)(2,1)S(1)}, u32[]{:S(2)}, u32[]{:S(2)}) collective-permute-start(bf16[32,2048]{1,0:T(8,128)(2,1)S(1)} %get-tuple-element.36), channel_id=1, source_target_pairs={{0,8},{4,12},{8,0},{12,4},{1,9},{5,13},{9,1},{13,5},{2,10},{6,14},... | collective-permute-start | bytes 393224 | tf_op jit(solution)/shard_map/ppermute | solution.py:38
  54.2 9.1 %collective-permute-start.9 = (bf16[32,2048]{1,0:T(8,128)(2,1)S(1)}, bf16[32,2048]{1,0:T(8,128)(2,1)}, u32[]{:S(2)}, u32[]{:S(2)}) collective-permute-start(bf16[32,2048]{1,0:T(8,128)(2,1)S(1)} %get-tuple-element.35), channel_id=1, source_target_pairs={{0,4},{4,0},{8,12},{12,8},{1,5},{5,1},{9,13},{13,9},{2,6},{6,2},{1... | collective-permute-start | bytes 393224 | tf_op jit(solution)/shard_map/ppermute | solution.py:38
  80.0 13.9 %collective-permute-start.12 = (bf16[128,2048]{1,0:T(8,128)(2,1)S(1)}, bf16[128,2048]{1,0:T(8,128)(2,1)S(1)}, u32[]{:S(2)}, u32[]{:S(2)}) collective-permute-start(bf16[128,2048]{1,0:T(8,128)(2,1)S(1)} %all_gather.3), channel_id=1, source_target_pairs={{0,3},{1,0},{2,1},{3,2},{4,7},{5,4},{6,5},{7,6},{8,11},{9,8},{10,9... | collective-permute-start | bytes 1572872 | tf_op jit(solution)/shard_map/ppermute | solution.py:25
  81.5 11.4 %collective-permute-start.13 = (bf16[128,2048]{1,0:T(8,128)(2,1)S(1)}, bf16[128,2048]{1,0:T(8,128)(2,1)S(1)}, u32[]{:S(2)}, u32[]{:S(2)}) collective-permute-start(bf16[128,2048]{1,0:T(8,128)(2,1)S(1)} %all_gather.3), channel_id=1, source_target_pairs={{0,1},{1,2},{2,3},{3,0},{4,5},{5,6},{6,7},{7,4},{8,9},{9,10},{10,1... | collective-permute-start | bytes 1572872 | tf_op jit(solution)/shard_map/ppermute | solution.py:25
  94.0 8.2 %collective-permute-start.15 = (bf16[64,2048]{1,0:T(8,128)(2,1)S(1)}, bf16[64,2048]{1,0:T(8,128)(2,1)S(1)}, u32[]{:S(2)}, u32[]{:S(2)}) collective-permute-start(bf16[64,2048]{1,0:T(8,128)(2,1)S(1)} %get-tuple-element.20), channel_id=1, source_target_pairs={{0,3},{1,0},{2,1},{3,2},{4,7},{5,4},{6,5},{7,6},{8,11},{9,8},{10,9... | collective-permute-start | bytes 786440 | tf_op jit(solution)/shard_map/ppermute | solution.py:25
  95.9 6.4 %collective-permute-start.16 = (bf16[64,2048]{1,0:T(8,128)(2,1)S(1)}, bf16[64,2048]{1,0:T(8,128)(2,1)S(1)}, u32[]{:S(2)}, u32[]{:S(2)}) collective-permute-start(bf16[64,2048]{1,0:T(8,128)(2,1)S(1)} %slice.85), channel_id=1, source_target_pairs={{0,1},{1,2},{2,3},{3,0},{4,5},{5,6},{6,7},{7,4},{8,9},{9,10},{10,1... | collective-permute-start | bytes 786440 | tf_op jit(solution)/shard_map/ppermute | solution.py:25
  96.9 11.8 %collective-permute-start.14 = (f32[192,512]{1,0:T(8,128)S(1)}, f32[192,512]{1,0:T(8,128)S(1)}, u32[]{:S(2)}, u32[]{:S(2)}) collective-permute-start(f32[192,512]{1,0:T(8,128)S(1)} %pad_maximum_fusion.8), channel_id=1, source_target_pairs={{0,16},{16,0},{1,17},{17,1},{2,18},{18,2},{3,19},{19,3},{4,20},{20... | collective-permute-start | bytes 1179656 | tf_op jit(solution)/shard_map/ppermute | solution.py:21
  102.9 6.7 %collective-permute-start.17 = (f32[64,512]{1,0:T(8,128)S(1)}, f32[64,512]{1,0:T(8,128)S(1)}, u32[]{:S(2)}, u32[]{:S(2)}) collective-permute-start(f32[64,512]{1,0:T(8,128)S(1)} %fusion.20), channel_id=1, source_target_pairs={{0,16},{16,0},{1,17},{17,1},{2,18},{18,2},{3,19},{19,3},{4,20},{20... | collective-permute-start | bytes 393224 | tf_op jit(solution)/shard_map/ppermute | solution.py:21
  110.2 7.6 %collective-permute-start.18 = (bf16[256,512]{1,0:T(8,128)(2,1)S(1)}, bf16[256,512]{1,0:T(8,128)(2,1)S(1)}, u32[]{:S(2)}, u32[]{:S(2)}) collective-permute-start(bf16[256,512]{1,0:T(8,128)(2,1)S(1)} %dynamic-slice_convert_fusion), channel_id=1, source_target_pairs={{0,32},{32,0},{1,33},{33,1},{2,34},{34,2},{3,35},{35,3},{4,36},{36... | collective-permute-start | bytes 786440 | tf_op jit(solution)/shard_map/ppermute | solution.py:21
  110.6 11.9 %collective-permute-start.19 = (bf16[256,512]{1,0:T(8,128)(2,1)S(1)}, bf16[256,512]{1,0:T(8,128)(2,1)S(1)}, u32[]{:S(2)}, u32[]{:S(2)}) collective-permute-start(bf16[256,512]{1,0:T(8,128)(2,1)S(1)} %dynamic-slice_convert_fusion), channel_id=1, source_target_pairs={{0,128},{64,192},{128,0},{192,64},{1,129},{65,193},{129,1},{193,65... | collective-permute-start | bytes 786440 | tf_op jit(solution)/shard_map/ppermute | solution.py:25
  117.9 13.4 %collective-permute-start.20 = (bf16[512,512]{1,0:T(8,128)(2,1)S(1)}, bf16[512,512]{1,0:T(8,128)(2,1)S(1)}, u32[]{:S(2)}, u32[]{:S(2)}) collective-permute-start(bf16[512,512]{1,0:T(8,128)(2,1)S(1)} %pad_maximum_fusion.7), channel_id=1, source_target_pairs={{0,64},{64,0},{128,192},{192,128},{1,65},{65,1},{129,193},{193,129... | collective-permute-start | bytes 1572872 | tf_op jit(solution)/shard_map/ppermute | solution.py:38
  119.0 14.3 %collective-permute-start.21 = (bf16[512,512]{1,0:T(8,128)(2,1)S(1)}, bf16[512,512]{1,0:T(8,128)(2,1)S(1)}, u32[]{:S(2)}, u32[]{:S(2)}) collective-permute-start(bf16[512,512]{1,0:T(8,128)(2,1)S(1)} %pad_maximum_fusion.7), channel_id=1, source_target_pairs={{0,192},{64,128},{128,64},{192,0},{1,193},{65,129},{129,65},{193,1... | collective-permute-start | bytes 1572872 | tf_op jit(solution)/shard_map/ppermute | solution.py:38
  122.6 6.0 %collective-permute-start.22 = (bf16[256,512]{1,0:T(8,128)(2,1)S(1)}, bf16[256,512]{1,0:T(8,128)(2,1)S(1)}, u32[]{:S(2)}, u32[]{:S(2)}) collective-permute-start(bf16[256,512]{1,0:T(8,128)(2,1)S(1)} %collective-permute-done.19), channel_id=1, source_target_pairs={{0,32},{32,0},{1,33},{33,1},{2,34},{34,2},{3,35},{35,3},{4,36},{36... | collective-permute-start | bytes 786440 | tf_op jit(solution)/shard_map/ppermute | solution.py:21
  134.4 3.7 %collective-permute-start.23 = (f32[256,512]{1,0:T(8,128)S(1)}, f32[256,512]{1,0:T(8,128)S(1)}, u32[]{:S(2)}, u32[]{:S(2)}) collective-permute-start(f32[256,512]{1,0:T(8,128)S(1)} %convolution_add_fusion), channel_id=1, source_target_pairs={{0,16},{16,0},{1,17},{17,1},{2,18},{18,2},{3,19},{19,3},{4,20},{20... | collective-permute-start | bytes 1572872 | tf_op jit(solution)/shard_map/ppermute | solution.py:21
